TPU v7x, 32 devices: a whole 2x2x4 slice. The times are simulated.
32 devices in a mesh: fsdp: 16 (over z, y, core), ctx: 2 (over x).
Axes of the slice: x: 2, y: 2, z: 4, core: 2. Of those that a mesh axis runs over, the one named last changes fastest.
Arguments:
- tokens: bfloat16 [8192, 2048], P(('fsdp', 'ctx')), may hold values from -6 to 6
- qkv_weight: bfloat16 [2048, 5120], P('fsdp'), may hold values from -0.125 to 0.125
- out_weight: bfloat16 [4096, 2048], P('fsdp'), may hold values from -1.5 to 1.5
- router_weight: bfloat16 [2048, 32], P('fsdp'), may hold values from -0.125 to 0.125
- attn_gain: bfloat16 [2048], P('fsdp'), may hold values from 0.5 to 1.5
- moe_gain: bfloat16 [2048], P('fsdp'), may hold values from 0.5 to 1.5
- query_gain: bfloat16 [128], replicated, may hold values from 0.5 to 1.5
- key_gain: bfloat16 [128], replicated, may hold values from 0.5 to 1.5
- expert_gate_up: bfloat16 [32, 2048, 1536], P(('fsdp', 'ctx')), may hold values from -0.125 to 0.125
- expert_down: bfloat16 [32, 768, 2048], P(('fsdp', 'ctx')), may hold values from -0.21875 to 0.21875
- routes: int32 [8192, 8], P(('fsdp', 'ctx')), may hold values from 0 to 31, all different within a row; in each aligned block of 256 rows (0 to 255, 256 to 511, ...) at most 128 rows name the same one
- cotangent: bfloat16 [8192, 2048], P(('fsdp', 'ctx')), may hold values from -6 to 6
Outputs:
- output: bfloat16 [8192, 2048], P(('fsdp', 'ctx'))
- grad_tokens: float32 [8192, 2048], P(('fsdp', 'ctx'))
- grad_qkv: float32 [2048, 5120], P('fsdp')
- grad_out: float32 [4096, 2048], P('fsdp')
- grad_router: float32 [2048, 32], P('fsdp')
- grad_attn_gain: float32 [2048], P('fsdp')
- grad_moe_gain: float32 [2048], P('fsdp')
- grad_query_gain: float32 [128], replicated
- grad_key_gain: float32 [128], replicated
- grad_gate_up: float32 [32, 2048, 1536], P(('fsdp', 'ctx'))
- grad_down: float32 [32, 768, 2048], P(('fsdp', 'ctx'))
Inputs may be any that keep to these rules, and one draw needn't show every extreme that they name: `routes`: each row names 8 different experts. In each aligned block of 256 rows (the rows of one device) no expert is named by more than 128 rows, a bound that some block reaches.
All inputs are finite; a program needn't handle non-finite values.
Results may differ from a plain program's by a relative error of at most 0.019.
Values may be sent and summed in bfloat16 or wider, within the bound.
No kernel may reach another device: no remote copies, remote signals or barrier semaphores. Data moves between devices by JAX's collectives and lax.ppermute only.
A program may use at most 448 MiB of HBM per device.

v0:
```python
import math

import jax
import jax.numpy as jnp
from jax import lax
from jax.sharding import PartitionSpec as P

eps_norm = 1e-06
theta_base = 1000000.0


def rms_scale(values, gain):
    return values * lax.rsqrt(jnp.mean(values * values, axis=-1, keepdims=True) + eps_norm) * gain


def rotate(values, cosine, sine):
    half_width = values.shape[-1] // 2
    turned = jnp.concatenate([-values[..., half_width:], values[..., :half_width]], axis=-1)
    return values * cosine + turned * sine


def angles(positions, width):
    freqs = theta_base ** (-(jnp.arange(width // 2, dtype=jnp.float32) * 2.0) / width)
    phase = positions.astype(jnp.float32)[:, None] * freqs[None, :]
    phase = jnp.concatenate([phase, phase], axis=-1)
    return (jnp.cos(phase)[:, None, :], jnp.sin(phase)[:, None, :])


def device_positions(block_rank, ctx_count, tok_rows):
    half_rows = tok_rows // 2
    within = jnp.arange(tok_rows, dtype=jnp.int32)
    span_id = jnp.where(within < half_rows, block_rank, 2 * ctx_count - 1 - block_rank)
    return span_id * half_rows + within % half_rows


def attend_head(query, keys_in, values_in, causal, scale_root):
    scores = (
        jnp.einsum("tgd,sd->gts", query, keys_in, preferred_element_type=jnp.float32) / scale_root
    )
    expo = jnp.where(causal[None], jnp.exp(scores), 0.0)
    totals = jnp.sum(expo, axis=-1, keepdims=True)
    probs = (expo / totals).astype(jnp.bfloat16)
    attended = jnp.einsum("gts,sd->tgd", probs, values_in, preferred_element_type=jnp.float32)
    return (attended, jnp.log(totals[..., 0]))


def attend_back(query, keys_in, values_in, causal, log_total, grad_attended, scale_root):
    scores = (
        jnp.einsum("tgd,sd->gts", query, keys_in, preferred_element_type=jnp.float32) / scale_root
    )
    probs = jnp.where(causal[None], jnp.exp(scores - log_total[..., None]), 0.0)
    low_probs = probs.astype(jnp.bfloat16)
    grad_values = jnp.einsum(
        "gts,tgd->sd", low_probs, grad_attended, preferred_element_type=jnp.float32
    )
    grad_probs = jnp.einsum(
        "tgd,sd->gts", grad_attended, values_in, preferred_element_type=jnp.float32
    )
    delta_rows = jnp.sum(grad_probs * probs, axis=-1, keepdims=True)
    grad_scores = (probs * (grad_probs - delta_rows)).astype(jnp.bfloat16)
    grad_query = (
        jnp.einsum("gts,sd->tgd", grad_scores, keys_in, preferred_element_type=jnp.float32)
        / scale_root
    )
    grad_keys = (
        jnp.einsum("gts,tgd->sd", grad_scores, query, preferred_element_type=jnp.float32)
        / scale_root
    )
    return (grad_query, grad_keys, grad_values)


def swiglu(paired):
    half_width = paired.shape[-1] // 2
    return jax.nn.silu(paired[..., :half_width]) * paired[..., half_width:]


def gating(selected):
    expo = jnp.exp(selected)
    return expo / jnp.sum(expo, axis=1, keepdims=True)


def body(
    tokens,
    qkv_weight,
    out_weight,
    router_weight,
    attn_gain,
    moe_gain,
    query_gain,
    key_gain,
    expert_gate_up,
    expert_down,
    routes,
    cotangent,
):
    rows_dev, width = tokens.shape
    head_dim = query_gain.shape[0]
    top_k = routes.shape[1]
    ctx_count = lax.axis_size("ctx")
    ctx_rank = lax.axis_index("ctx")
    qkv_all, out_all, router_all, attn_all, moe_all = (
        lax.all_gather(qkv_weight, "fsdp", axis=0, tiled=True),
        lax.all_gather(out_weight, "fsdp", axis=0, tiled=True),
        lax.all_gather(router_weight, "fsdp", axis=0, tiled=True),
        lax.all_gather(attn_gain, "fsdp", axis=0, tiled=True),
        lax.all_gather(moe_gain, "fsdp", axis=0, tiled=True),
    )
    experts_all = router_all.shape[1]
    heads = out_all.shape[0] // head_dim
    kv_heads = (qkv_all.shape[1] // head_dim - heads) // 2
    group_size = heads // kv_heads
    capacity = 2 * rows_dev * top_k // experts_all
    width_q = heads * head_dim
    width_k = kv_heads * head_dim
    scale_root = math.sqrt(head_dim)
    inputs = tokens.astype(jnp.float32)
    normed_in = rms_scale(inputs, attn_all.astype(jnp.float32))
    low_in = normed_in.astype(jnp.bfloat16)
    projected = jnp.dot(low_in, qkv_all, preferred_element_type=jnp.float32)
    query_raw = projected[:, :width_q].reshape(rows_dev, heads, head_dim)
    key_raw = projected[:, width_q : width_q + width_k].reshape(rows_dev, kv_heads, head_dim)
    value_low = (
        projected[:, width_q + width_k :].astype(jnp.bfloat16).reshape(rows_dev, kv_heads, head_dim)
    )
    positions = device_positions(ctx_rank, ctx_count, rows_dev)
    cosine, sine = angles(positions, head_dim)
    query_gain_f = query_gain.astype(jnp.float32)
    key_gain_f = key_gain.astype(jnp.float32)

    def query_rope(values_in, gain):
        return rotate(rms_scale(values_in, gain), cosine, sine)

    query_low = query_rope(query_raw, query_gain_f).astype(jnp.bfloat16)
    key_low = query_rope(key_raw, key_gain_f).astype(jnp.bfloat16)
    keys_all, values_all = (
        lax.all_gather(key_low, "ctx", axis=0, tiled=True),
        lax.all_gather(value_low, "ctx", axis=0, tiled=True),
    )
    key_pos = jnp.concatenate(
        [device_positions(other, ctx_count, rows_dev) for other in range(ctx_count)]
    )
    causal = key_pos[None, :] <= positions[:, None]
    query_heads = query_low.reshape(rows_dev, kv_heads, group_size, head_dim).transpose(1, 0, 2, 3)
    key_heads = keys_all.transpose(1, 0, 2)
    value_heads = values_all.transpose(1, 0, 2)
    attended, log_total = lax.map(
        lambda member: attend_head(member[0], member[1], member[2], causal, scale_root),
        (query_heads, key_heads, value_heads),
    )
    attended_low = attended.transpose(1, 0, 2, 3).reshape(rows_dev, width_q).astype(jnp.bfloat16)
    mixed = inputs + jnp.dot(attended_low, out_all, preferred_element_type=jnp.float32)
    normed_mid = rms_scale(mixed, moe_all.astype(jnp.float32))
    low_mid = normed_mid.astype(jnp.bfloat16)
    logits = jnp.dot(low_mid, router_all, preferred_element_type=jnp.float32)
    selected = jnp.take_along_axis(logits, routes, axis=1)
    gates, gate_back = jax.vjp(gating, selected)
    flat_routes = routes.reshape(-1)
    expert_ids = jnp.arange(experts_all, dtype=jnp.int32)
    hit_table = (flat_routes[:, None] == expert_ids[None, :]).astype(jnp.int32)
    slot_index = jnp.sum(jnp.cumsum(hit_table, axis=0) * hit_table, axis=1) - 1
    target = flat_routes * capacity + slot_index
    pair_count = rows_dev * top_k
    source_pair = (
        jnp.full((experts_all * capacity,), pair_count, jnp.int32)
        .at[target]
        .set(jnp.arange(pair_count, dtype=jnp.int32))
    )
    padded = jnp.concatenate([low_mid, jnp.zeros((1, width), jnp.bfloat16)], axis=0)
    outgoing = padded[source_pair // top_k].reshape(experts_all, capacity, width)
    received = lax.all_to_all(outgoing, ("fsdp", "ctx"), split_axis=0, concat_axis=1, tiled=True)
    gate_and_up = jnp.einsum(
        "esd,edf->esf", received, expert_gate_up, preferred_element_type=jnp.float32
    )
    hidden_val, swiglu_back = jax.vjp(swiglu, gate_and_up)
    hidden_low = hidden_val.astype(jnp.bfloat16)
    result_low = jnp.einsum(
        "esf,efd->esd", hidden_low, expert_down, preferred_element_type=jnp.float32
    ).astype(jnp.bfloat16)
    returned = lax.all_to_all(
        result_low, ("fsdp", "ctx"), split_axis=1, concat_axis=0, tiled=True
    ).reshape(experts_all * capacity, width)
    picked = returned[target].reshape(rows_dev, top_k, width).astype(jnp.float32)
    output = (mixed + jnp.sum(gates[:, :, None] * picked, axis=1)).astype(jnp.bfloat16)
    qkv_back, out_back, router_back, attn_back_g, moe_back_g = (
        qkv_all,
        out_all,
        router_all,
        attn_all,
        moe_all,
    )
    grad_final = cotangent.astype(jnp.float32)
    grad_gates = jnp.sum(grad_final[:, None, :] * picked, axis=2)
    grad_result = (
        (gates[:, :, None] * grad_final[:, None, :]).astype(jnp.bfloat16).reshape(pair_count, width)
    )
    grad_padded = jnp.concatenate([grad_result, jnp.zeros((1, width), jnp.bfloat16)], axis=0)
    grad_outgoing = grad_padded[source_pair].reshape(experts_all, capacity, width)
    grad_received = lax.all_to_all(
        grad_outgoing, ("fsdp", "ctx"), split_axis=0, concat_axis=1, tiled=True
    )
    grad_down = jnp.einsum(
        "esf,esd->efd", hidden_low, grad_received, preferred_element_type=jnp.float32
    )
    grad_hidden = jnp.einsum(
        "esd,efd->esf", grad_received, expert_down, preferred_element_type=jnp.float32
    )
    grad_paired = swiglu_back(grad_hidden)[0].astype(jnp.bfloat16)
    grad_gate_up = jnp.einsum(
        "esd,esf->edf", received, grad_paired, preferred_element_type=jnp.float32
    )
    grad_rows = jnp.einsum(
        "esf,edf->esd", grad_paired, expert_gate_up, preferred_element_type=jnp.float32
    ).astype(jnp.bfloat16)
    grad_returned = lax.all_to_all(
        grad_rows, ("fsdp", "ctx"), split_axis=1, concat_axis=0, tiled=True
    ).reshape(experts_all * capacity, width)
    grad_mid = jnp.sum(
        grad_returned[target].reshape(rows_dev, top_k, width).astype(jnp.float32), axis=1
    )
    grad_selected = gate_back(grad_gates)[0]
    route_table = (routes[:, :, None] == expert_ids[None, None, :]).astype(jnp.float32)
    grad_logits = jnp.sum(route_table * grad_selected[:, :, None], axis=1).astype(jnp.bfloat16)
    grad_router = jnp.dot(low_mid.T, grad_logits, preferred_element_type=jnp.float32)
    grad_mid = grad_mid + jnp.dot(grad_logits, router_back.T, preferred_element_type=jnp.float32)
    unused_mid, mid_back = jax.vjp(rms_scale, mixed, moe_back_g.astype(jnp.float32))
    grad_mixed_part, grad_moe_gain = mid_back(grad_mid)
    grad_mixed = grad_final + grad_mixed_part
    grad_branch = grad_mixed.astype(jnp.bfloat16)
    grad_out = jnp.dot(attended_low.T, grad_branch, preferred_element_type=jnp.float32)
    grad_attended = jnp.dot(grad_branch, out_back.T, preferred_element_type=jnp.float32).astype(
        jnp.bfloat16
    )
    grad_heads = grad_attended.reshape(rows_dev, kv_heads, group_size, head_dim).transpose(
        1, 0, 2, 3
    )
    grad_query_h, grad_key_h, grad_value_h = lax.map(
        lambda member: attend_back(
            member[0], member[1], member[2], causal, member[3], member[4], scale_root
        ),
        (query_heads, key_heads, value_heads, log_total, grad_heads),
    )
    grad_keys, grad_values = (
        lax.psum_scatter(
            grad_key_h.transpose(1, 0, 2).astype(jnp.bfloat16),
            "ctx",
            scatter_dimension=0,
            tiled=True,
        ).astype(jnp.float32),
        lax.psum_scatter(
            grad_value_h.transpose(1, 0, 2).astype(jnp.bfloat16),
            "ctx",
            scatter_dimension=0,
            tiled=True,
        ).astype(jnp.float32),
    )
    grad_query_rot = (
        grad_query_h.transpose(1, 0, 2, 3).reshape(rows_dev, heads, head_dim).astype(jnp.bfloat16)
    )
    grad_query_rot = lax.optimization_barrier(grad_query_rot).astype(jnp.float32)
    grad_key_rot = lax.optimization_barrier(grad_keys.astype(jnp.bfloat16)).astype(jnp.float32)
    unused_query, query_back = jax.vjp(query_rope, query_raw, query_gain_f)
    grad_query_raw, grad_query_gain = query_back(grad_query_rot)
    unused_key, key_back = jax.vjp(query_rope, key_raw, key_gain_f)
    grad_key_raw, grad_key_gain = key_back(grad_key_rot)
    grad_projected = jnp.concatenate(
        [
            grad_query_raw.reshape(rows_dev, width_q).astype(jnp.bfloat16),
            grad_key_raw.reshape(rows_dev, width_k).astype(jnp.bfloat16),
            grad_values.reshape(rows_dev, width_k).astype(jnp.bfloat16),
        ],
        axis=1,
    )
    grad_qkv = jnp.dot(low_in.T, grad_projected, preferred_element_type=jnp.float32)
    grad_normed = jnp.dot(grad_projected, qkv_back.T, preferred_element_type=jnp.float32)
    unused_in, in_back = jax.vjp(rms_scale, inputs, attn_back_g.astype(jnp.float32))
    grad_in_part, grad_attn_gain = in_back(grad_normed)
    grad_tokens = grad_mixed + grad_in_part
    gradients = (grad_qkv, grad_out, grad_router, grad_attn_gain, grad_moe_gain)
    pieces = (
        lax.psum_scatter(gradients[0], "fsdp", scatter_dimension=0, tiled=True),
        lax.psum_scatter(gradients[1], "fsdp", scatter_dimension=0, tiled=True),
        lax.psum_scatter(gradients[2], "fsdp", scatter_dimension=0, tiled=True),
        lax.psum_scatter(gradients[3], "fsdp", scatter_dimension=0, tiled=True),
        lax.psum_scatter(gradients[4], "fsdp", scatter_dimension=0, tiled=True),
    )
    reduced = (
        lax.psum(pieces[0].astype(jnp.bfloat16), "ctx").astype(jnp.float32),
        lax.psum(pieces[1].astype(jnp.bfloat16), "ctx").astype(jnp.float32),
        lax.psum(pieces[2].astype(jnp.bfloat16), "ctx").astype(jnp.float32),
        lax.psum(pieces[3].astype(jnp.bfloat16), "ctx").astype(jnp.float32),
        lax.psum(pieces[4].astype(jnp.bfloat16), "ctx").astype(jnp.float32),
    )
    gain_sums = lax.psum((grad_query_gain, grad_key_gain), ("fsdp", "ctx"))
    return (
        output,
        grad_tokens,
        reduced[0],
        reduced[1],
        reduced[2],
        reduced[3],
        reduced[4],
        gain_sums[0],
        gain_sums[1],
        grad_gate_up,
        grad_down,
    )


def solution(mesh):
    in_specs = (
        P(("fsdp", "ctx"), None),
        P("fsdp", None),
        P("fsdp", None),
        P("fsdp", None),
        P("fsdp"),
        P("fsdp"),
        P(),
        P(),
        P(("fsdp", "ctx"), None, None),
        P(("fsdp", "ctx"), None, None),
        P(("fsdp", "ctx"), None),
        P(("fsdp", "ctx"), None),
    )
    out_specs = (
        P(("fsdp", "ctx"), None),
        P(("fsdp", "ctx"), None),
        P("fsdp", None),
        P("fsdp", None),
        P("fsdp", None),
        P("fsdp"),
        P("fsdp"),
        P(),
        P(),
        P(("fsdp", "ctx"), None, None),
        P(("fsdp", "ctx"), None, None),
    )
    return jax.shard_map(body, mesh=mesh, in_specs=in_specs, out_specs=out_specs, check_vma=False)
```

profile of v0, /device:TPU:0, one launch (start us, length us, event | category | flops | bytes accessed | tf_op | source)
XLA Modules:
  0.0 3262.7 jit_solution(13427144638700404289)
XLA Ops:
  12.7 23.2 all-gather
  35.9 17.5 all-gather.1
  58.4 17.7 reduce-window.6
  96.7 24.6 all-gather.5.cloned.1.call-done
  121.2 10.2 fusion.104
  202.1 23.6 while.28
  225.8 24.6 all-gather.7.cloned.1.call-done
  250.4 11.2 multiply_reduce_fusion.5
  265.3 32.7 %gather_fusion = bf16[4096,2048]{1,0:T(8,128)(2,1)} fusion(bf16[257,2048]{1,0:T(8,128)(2,1)} %concatenate.40, s32[4096]{0:T(1024)S(1)} %copy-done.48), kind=kCustom, calls=%fused_computation | custom fusion | bytes 33570816 | tf_op jit(solution)/shard_map/gather | solution.py:169
  305.1 291.7 %all_gather.27 = bf16[2048,32]{0,1:T(8,128)(2,1)S(1)} all-gather(bf16[128,32]{0,1:T(8,128)(2,1)S(1)} %copy-done.66), channel_id=1, replica_groups=mesh['fsdp'=16,'ctx'=2] {'fsdp'}, dimensions={0}, use_global_device_ids=true | all-gather | bytes 139264 | tf_op jit(solution)/shard_map/all_gather | solution.py:104
  599.2 16.8 gather_fusion.4
  631.4 35.8 %gather_fusion.2 = bf16[4096,2048]{1,0:T(8,128)(2,1)} fusion(bf16[2049,2048]{1,0:T(8,128)(2,1)} %concatenate.41, s32[4096]{0:T(1024)S(1)} %copy-done.47), kind=kCustom, calls=%fused_computation.2 | custom fusion | bytes 33570816 | tf_op jit(solution)/shard_map/gather | solution.py:197
  667.8 97.2 %all-to-all-start.2 = ((bf16[32,128,2048]{2,1,0:T(8,128)(2,1)}), bf16[32,128,2048]{2,1,0:T(8,128)(2,1)}, u32[]{:S(2)}, u32[]{:S(2)}) async-start(bf16[32,128,2048]{2,1,0:T(8,128)(2,1)} %bitcast.323), calls=%async_computation.2 | async-start | bytes 33554432 | tf_op jit(solution)/shard_map/all_to_all | solution.py:198
  765.0 33.3 %convolution_bitcast_fusion.1 = f32[1,4096,1536]{2,1,0:T(8,128)} fusion(bf16[4096,2048]{1,0:T(8,128)(2,1)} %bitcast.20, bf16[1,2048,1536]{2,1,0:T(8,128)(2,1)} %param.24), kind=kOutput, calls=%fused_computation.76 | convolution fusion | flops 25769803776 | bytes 48234496 | tf_op jit(solution)/shard_map/esd,edf->esf/dot_general | solution.py:171
  798.3 332.3 %all-to-all-done.2 = bf16[32,128,2048]{2,1,0:T(8,128)(2,1)} async-done(((bf16[32,128,2048]{2,1,0:T(8,128)(2,1)}), bf16[32,128,2048]{2,1,0:T(8,128)(2,1)}, u32[]{:S(2)}, u32[]{:S(2)}) %all-to-all-start.2) | async-done | bytes 16777248 | tf_op jit(solution)/shard_map/all_to_all | solution.py:198
  1130.6 33.1 %bitcast_multiply_fusion.3 = (f32[1,4096,768]{2,1,0:T(8,128)}, f32[1,4096,768]{2,1,0:T(8,128)}, bf16[4096,768]{1,0:T(8,128)(2,1)}) fusion(f32[1,4096,1536]{2,1,0:T(8,128)} %convolution_bitcast_fusion.1, bf16[4096,2048]{1,0:T(8,128)(2,1)} %bitcast.29, bf16[1,768,2048]{2,1,0:T(8,128)(2,1)S(1)} %copy-done), kind=kOutput, calls=%fused_computation.90 | convolution fusion | flops 12928942080 | bytes 76546048 | tf_op jit(solution)/shard_map/esd,efd->esf/dot_general | solution.py:204
  1163.8 33.7 %convert_bitcast_fusion = bf16[1,4096,2048]{2,1,0:T(8,128)(2,1)} fusion(bf16[1,2048,1536]{2,1,0:T(8,128)(2,1)} %param.24, f32[1,4096,768]{2,1,0:T(8,128)} %get-tuple-element.359, f32[1,4096,768]{2,1,0:T(8,128)} %get-tuple-element.358), kind=kOutput, calls=%fused_computation.84 | convolution fusion | flops 25790775296 | bytes 48234496 | tf_op jit(solution)/shard_map/esf,edf->esd/dot_general | solution.py:211
  1197.4 29.2 copy.358
  1227.1 99.7 %reduce.4 = bf16[4096,2048]{1,0:T(8,128)(2,1)} reduce(bf16[4096,1,2048]{2,1,0:T(2,128)(2,1)} %bitcast.318, bf16[]{:T(256)} %broadcast.513), dimensions={1}, to_apply=%bitcast.259.reduce_sub_computation | reduce | bytes 33554432
  1326.8 27.8 reshape.504
  1354.6 17.9 all-to-all-start.3
  1372.6 18.8 convert_bitcast_fusion.1
  1391.3 29.2 copy.359
  1420.5 99.7 %reduce.5 = bf16[4096,2048]{1,0:T(8,128)(2,1)} reduce(bf16[4096,1,2048]{2,1,0:T(2,128)(2,1)} %bitcast.319, bf16[]{:T(256)} %broadcast.513), dimensions={1}, to_apply=%bitcast.260.reduce_sub_computation | reduce | bytes 33554432
  1520.2 27.9 reshape.502
  1548.2 190.0 %all-to-all-done.3 = bf16[32,2,131072]{2,1,0:T(2,128)(2,1)} async-done(((bf16[32,2,131072]{2,1,0:T(2,128)(2,1)}), bf16[32,2,131072]{2,1,0:T(2,128)(2,1)}, u32[]{:S(2)}, u32[]{:S(2)}) %all-to-all-start.3) | async-done | bytes 16777248 | tf_op jit(solution)/shard_map/all_to_all | solution.py:214
  1738.2 17.7 all-to-all-start.1
  1756.0 32.0 reshape.505
  1788.0 24.1 copy.355
  1812.1 24.4 gather_fusion.3
  1836.5 11.3 convert_reduce_fusion
  1847.8 273.7 %all-to-all-done.1 = bf16[32,2,131072]{2,1,0:T(2,128)(2,1)} async-done(((bf16[32,2,131072]{2,1,0:T(2,128)(2,1)}), bf16[32,2,131072]{2,1,0:T(2,128)(2,1)}, u32[]{:S(2)}, u32[]{:S(2)}) %all-to-all-start.1) | async-done | bytes 16777248 | tf_op jit(solution)/shard_map/all_to_all | solution.py:179
  2121.5 31.6 reshape.503
  2153.1 24.5 copy.356
  2177.6 24.3 gather_fusion.1
  2201.9 9.8 fusion.62
  2217.6 12.3 fusion.92
  2235.6 49.6 %while.29 = (s32[]{:T(128)}, bf16[4,256,8,128]{1,3,2,0:T(8,128)(2,1)}, bf16[4,512,128]{1,2,0:T(8,128)(2,1)}, bf16[4,512,128]{1,2,0:T(8,128)(2,1)}, bf16[4,512,12...) while((s32[]{:T(128)}, ...), condition=%wide.region_20.21_spmd.clone, body=%wide.region_18.20_spmd.clone.sunk | while | flops 1358428160 | bytes 40697024 | solution.py:236
  2288.4 14.9 fusion.100
  2319.1 10.6 reduce-scatter.8.cloned.1.call-done
  2329.7 18.4 fusion.93
  2350.0 20.5 convolution_bitcast_fusion.3
  2370.5 38.1 %convolution_bitcast_fusion.2 = f32[1,2048,1536]{2,1,0:T(8,128)} fusion(bf16[4096,2048]{1,0:T(8,128)(2,1)} %bitcast.20, f32[1,4096,768]{2,1,0:T(8,128)} %get-tuple-element.359, f32[1,4096,768]{2,1,0:T(8,128)} %get-tuple-element.358), kind=kOutput, calls=%fused_computation.94 | convolution fusion | flops 25782386688 | bytes 54525952 | tf_op jit(solution)/shard_map/esd,esf->edf/dot_general | solution.py:208
  2409.3 315.6 %reduce-scatter.12.cloned.1.call-done = f32[256,2048]{1,0:T(8,128)} async-done(((f32[4096,2048]{1,0:T(8,128)}), f32[256,2048]{1,0:T(8,128)}) %reduce-scatter.12.cloned.1.call-update) | async-done | bytes 2097168 | tf_op jit(solution)/shard_map/reduce_scatter | solution.py:281
  2727.6 401.1 %reduce-scatter.10.cloned.1.call-done = f32[128,5120]{1,0:T(8,128)} async-done(((f32[2048,5120]{1,0:T(8,128)}), f32[128,5120]{1,0:T(8,128)}) %reduce-scatter.10.cloned.1.call-update) | async-done | bytes 2621456 | tf_op jit(solution)/shard_map/reduce_scatter | solution.py:280
  3131.8 11.9 fusion.84
  3143.6 58.9 %all-reduce.11 = (bf16[2048]{0:T(1024)(128)(2,1)S(1)}, bf16[2048]{0:T(1024)(128)(2,1)S(1)}) all-reduce(f32[2048]{0:T(1024)S(1)} %get-tuple-element.301, f32[2048]{0:T(1024)S(1)} %copy-done.52), channel_id=7, replica_groups=mesh['fsdp'=16,'ctx'=2] {'fsdp'}, use_global_device_ids=true, to_apply=%region_33.34.clone | all-reduce | flops 4096 | bytes 24576
  3209.3 36.8 %all-reduce.10 = (f32[128]{0:T(128)}, f32[128]{0:T(128)}) all-reduce(f32[128]{0:T(128)S(1)} %get-tuple-element.297, f32[128]{0:T(128)S(1)} %get-tuple-element.303), channel_id=1, replica_groups=mesh['fsdp'=16,'ctx'=2] {'fsdp','ctx'}, use_global_device_ids=true, to_apply=%region_39.40 | all-reduce | flops 256 | bytes 2048 | tf_op jit(solution)/shard_map/psum | solution.py:293
  (351 shorter events, 257.9 us)
Async XLA Ops:
  7.2 1123.5 %copy-start = (bf16[1,768,2048]{2,1,0:T(8,128)(2,1)S(1)}, bf16[1,768,2048]{2,1,0:T(8,128)(2,1)}, u32[]{:S(2)}) copy-start(bf16[1,768,2048]{2,1,0:T(8,128)(2,1)} %param.25) | copy-start | bytes 9437188
  7.2 114.0 %all-gather.5.cloned.1.call-start = ((), (), s32[]{:S(2)}) async-start(), calls=%async_computation.9 | async-start | bytes 22282240 | tf_op jit(solution)/shard_map/all_gather | solution.py:102
  7.9 242.5 %all-gather.7.cloned.1.call-start = ((), (), s32[]{:S(2)}) async-start(), calls=%async_computation.10 | async-start | bytes 17825792 | tf_op jit(solution)/shard_map/all_gather | solution.py:103
  35.9 95.6 %copy-start.31 = (f32[16,1,128]{2,1,0:T(1,128)}, f32[16,1,128]{2,1,0:T(1,128)S(1)}, u32[]{:S(2)}) copy-start(f32[16,1,128]{2,1,0:T(1,128)S(1)} %convert_element_type.247) | copy-start | bytes 24580
  56.1 86.9 %copy-start.14 = (f32[256,128]{0,1:T(8,128)}, f32[256,128]{0,1:T(8,128)S(1)}, u32[]{:S(2)}) copy-start(f32[256,128]{0,1:T(8,128)S(1)} %get-tuple-element.373) | copy-start | bytes 393220
  56.1 86.9 %copy-start.19 = (f32[256,128]{0,1:T(8,128)}, f32[256,128]{0,1:T(8,128)S(1)}, u32[]{:S(2)}) copy-start(f32[256,128]{0,1:T(8,128)S(1)} %get-tuple-element.374) | copy-start | bytes 393220
  141.8 18.5 copy-start.50
  141.8 18.5 copy-start.45
  179.8 13.3 copy-start.28
  225.8 35.8 %copy-start.35 = (s32[512]{0:T(512)}, s32[512]{0:T(512)S(1)}, u32[]{:S(2)}) copy-start(s32[512]{0:T(512)S(1)} %get-tuple-element.618) | copy-start | bytes 6148
  225.8 35.8 %copy-start.43 = (s32[256]{0:T(256)}, s32[256]{0:T(256)S(1)}, u32[]{:S(2)}) copy-start(s32[256]{0:T(256)S(1)} %get-tuple-element.619) | copy-start | bytes 3076
  250.4 12.6 copy-start.39
  261.6 36.3 %copy-start.61 = (f32[256]{0:T(256)}, f32[256]{0:T(256)S(1)}, u32[]{:S(2)}) copy-start(f32[256]{0:T(256)S(1)} %get-tuple-element.379) | copy-start | bytes 3076
  298.0 4.1 copy-start.37
  298.0 7.1 copy-start.66
  298.0 369.8 %all-to-all-start = ((bf16[32,128,2048]{2,1,0:T(8,128)(2,1)}), bf16[32,128,2048]{2,1,0:T(8,128)(2,1)}, u32[]{:S(2)}, u32[]{:S(2)}) async-start(bf16[32,128,2048]{2,1,0:T(8,128)(2,1)} %bitcast.322), calls=%async_computation | async-start | bytes 33554432 | tf_op jit(solution)/shard_map/all_to_all | solution.py:170
  616.9 6.1 copy-start.21
  623.0 8.5 copy-start.47
  667.8 462.9 %all-to-all-start.2 = ((bf16[32,128,2048]{2,1,0:T(8,128)(2,1)}), bf16[32,128,2048]{2,1,0:T(8,128)(2,1)}, u32[]{:S(2)}, u32[]{:S(2)}) async-start(bf16[32,128,2048]{2,1,0:T(8,128)(2,1)} %bitcast.323), calls=%async_computation.2 | async-start | bytes 33554432 | tf_op jit(solution)/shard_map/all_to_all | solution.py:198
  1354.6 383.5 %all-to-all-start.3 = ((bf16[32,2,131072]{2,1,0:T(2,128)(2,1)}), bf16[32,2,131072]{2,1,0:T(2,128)(2,1)}, u32[]{:S(2)}, u32[]{:S(2)}) async-start(bf16[32,2,131072]{2,1,0:T(2,128)(2,1)} %reshape.504), calls=%async_computation.3 | async-start | bytes 33554432 | tf_op jit(solution)/shard_map/all_to_all | solution.py:214
  1548.2 207.8 %copy-start.54 = (s32[2048,1]{0,1:T(1,128)S(1)}, s32[2048,1]{0,1:T(1,128)}, u32[]{:S(2)}) copy-start(s32[2048,1]{0,1:T(1,128)} %copy-done.53) | copy-start | bytes 24580
  1548.2 207.8 %copy-start.58 = (f32[256]{0:T(256)S(1)}, f32[256]{0:T(256)}, u32[]{:S(2)}) copy-start(f32[256]{0:T(256)} %copy-done.57) | copy-start | bytes 3076
  1738.2 383.3 %all-to-all-start.1 = ((bf16[32,2,131072]{2,1,0:T(2,128)(2,1)}), bf16[32,2,131072]{2,1,0:T(2,128)(2,1)}, u32[]{:S(2)}, u32[]{:S(2)}) async-start(bf16[32,2,131072]{2,1,0:T(2,128)(2,1)} %reshape.502), calls=%async_computation.1 | async-start | bytes 33554432 | tf_op jit(solution)/shard_map/all_to_all | solution.py:179
  1755.9 559.7 %reduce-scatter.6.cloned.1.call-start = ((), (), s32[]{:S(2)}) async-start(), calls=%async_computation.11 | async-start | bytes 786432 | tf_op jit(solution)/shard_map/reduce_scatter | solution.py:243
  2177.6 24.3 copy-start.22
  2201.8 9.9 copy-start.42
  2201.8 10.0 copy-start.38
  2201.8 10.0 copy-start.5
  2201.9 10.0 copy-start.24
  2201.9 10.0 copy-start.40
  2201.9 10.0 copy-start.56
  2231.9 3.7 copy-start.16
  2285.3 44.4 %reduce-scatter.8.cloned.1.call-start = ((), (), s32[]{:S(2)}) async-start(), calls=%async_computation.12 | async-start | bytes 786432 | tf_op jit(solution)/shard_map/reduce_scatter | solution.py:249
  2285.9 122.7 %reduce-scatter.14.cloned.1.call-start = ((), (), s32[]{:S(2)}) async-start(), calls=%async_computation.15 | async-start | bytes 278528 | tf_op jit(solution)/shard_map/reduce_scatter | solution.py:282
  2288.3 436.5 %reduce-scatter.12.cloned.1.call-start = ((), (), s32[]{:S(2)}) async-start(), calls=%async_computation.14 | async-start | bytes 35651584 | tf_op jit(solution)/shard_map/reduce_scatter | solution.py:281
  2303.3 825.4 %reduce-scatter.10.cloned.1.call-start = ((), (), s32[]{:S(2)}) async-start(), calls=%async_computation.13 | async-start | bytes 44564480 | tf_op jit(solution)/shard_map/reduce_scatter | solution.py:280
  2311.7 5.1 copy-start.11
  2311.7 5.1 copy-start.46
  2311.7 5.1 copy-start.63
  2311.7 6.2 copy-start.51
  2315.6 14.1 copy-start.9
  2315.6 14.1 copy-start.32
  2315.6 14.1 copy-start.49
  2348.2 902.5 %all-reduce.16.cloned.1.call-start = ((), (), s32[]{:S(2)}) async-start(), calls=%async_computation.16 | async-start | bytes 4718592 | tf_op jit(solution)/shard_map/psum | solution.py:287
  2409.3 722.5 %copy-start.12 = (bf16[256,32,128]{0,2,1:T(8,128)(2,1)S(1)}, bf16[256,32,128]{0,2,1:T(8,128)(2,1)}, u32[]{:S(2)}) copy-start(bf16[256,32,128]{0,2,1:T(8,128)(2,1)} %fusion.73) | copy-start | bytes 6291460
  3131.8 11.9 copy-start.52
  3131.8 114.4 %copy-start.60 = (f32[256]{0:T(256)S(1)}, f32[256]{0:T(256)}, u32[]{:S(2)}) copy-start(f32[256]{0:T(256)} %copy-done.59) | copy-start | bytes 3076
  3246.2 9.3 copy-start.1
  (44 other events, 97.1 us)
Sparse Core Ops, SparseCore 0:
  9.6 111.5 all-gather.4
  123.4 126.9 all-gather.6
  2285.4 27.4 reduce-scatter.5
  2315.1 14.5 reduce-scatter.7
  2333.7 55.2 reduce-scatter.13
  2393.1 331.7 reduce-scatter.11
  2729.1 399.5 reduce-scatter.9
  3131.9 67.9 all-reduce.15
where the time goes:
time: 3280 us; the launch traced here: 3260 us
  waiting for transfers between devices  1580 us (48%)
  blocking collectives  451 us (14%)
  local copies, waits for them, and re-layouts  448 us (14%)
  matrix products  319 us (10%)
  other arithmetic  316 us (10%)
  starting transfers between devices  137 us (4%)
    reduce_scatter x1, waiting for transfers between devices, body(): lax.psum_scatter(gradients[0], 'fsdp', scatter_dimension=0, tiled=True)  401 us
    all_to_all x1, waiting for transfers between devices, body(): lax.all_to_all(grad_outgoing, ('fsdp', 'ctx'), split_axis=0, concat_axis=...  332 us
    reduce_scatter x1, waiting for transfers between devices, body(): lax.psum_scatter(gradients[1], 'fsdp', scatter_dimension=0, tiled=True)  316 us
    all_gather x1, blocking collectives, body(): lax.all_gather(router_weight, 'fsdp', axis=0, tiled=True)  292 us
    all_to_all x1, waiting for transfers between devices, body(): lax.all_to_all(result_low, ('fsdp', 'ctx'), split_axis=1, concat_axis=0,...  274 us
    unnamed x2, other arithmetic  199 us
    unnamed x143, local copies, waits for them, and re-layouts  192 us
    all_to_all x1, waiting for transfers between devices, body(): lax.all_to_all(grad_rows, ('fsdp', 'ctx'), split_axis=1, concat_axis=0, t...  190 us
  transfers between devices with their start and end apart: 12, of which 9 were waited for; matrix products, arithmetic and copies ran while one was open for 19% of the time, Pallas kernels for 0%

commit v1 on v0

--- a/solution.py
+++ b/solution.py
@@ -1,8 +1,11 @@
+import functools
 import math
 
 import jax
 import jax.numpy as jnp
 from jax import lax
+from jax.experimental import pallas as pl
+from jax.experimental.pallas import tpu as pltpu
 from jax.sharding import PartitionSpec as P
 
 eps_norm = 1e-06
@@ -79,7 +82,7 @@
     return expo / jnp.sum(expo, axis=1, keepdims=True)
 
 
-def body(
+def body_routed(
     tokens,
     qkv_weight,
     out_weight,
@@ -306,6 +309,573 @@
     )
 
 
+low = jnp.bfloat16
+full = jnp.float32
+plain = (((1,), (0,)), ((), ()))
+rhs_turned = (((1,), (1,)), ((), ()))
+lhs_turned = (((0,), (0,)), ((), ()))
+vmem_bytes = 58 << 20
+
+
+def mul(left, right, dims=plain):
+    return lax.dot_general(left, right, dims, preferred_element_type=full)
+
+
+def core_pairs(fsdp):
+    return [(i, i ^ 1) for i in range(fsdp)]
+
+
+def side_pairs(fsdp):
+    return [(i, i ^ 2) for i in range(fsdp)]
+
+
+def swap_core(values):
+    return lax.ppermute(values, "fsdp", core_pairs(lax.axis_size("fsdp")))
+
+
+def swap_side(values):
+    return lax.ppermute(values, "fsdp", side_pairs(lax.axis_size("fsdp")))
+
+
+def swap_ctx(values):
+    return lax.ppermute(values, "ctx", [(0, 1), (1, 0)])
+
+
+def add_low(one, two):
+    return (one.astype(full) + two.astype(full)).astype(low)
+
+
+def take(values, index):
+    return lax.dynamic_index_in_dim(values, index, 0, keepdims=False)
+
+
+def halve(values, index, swap):
+    return add_low(take(values, index), swap(take(values, 1 - index)))
+
+
+def line_sum(values, place):
+    count = values.shape[0]
+    fsdp = lax.axis_size("fsdp")
+    up = down = None
+    for step in range(1, count):
+        pairs_up = [
+            (i, i + 4) for i in range(fsdp - 4) if i // 4 < step
+        ]
+        pairs_down = [
+            (i, i - 4) for i in range(4, fsdp) if count - 1 - i // 4 < step
+        ]
+        send_up = take(values, jnp.clip(count - step + place, 0, count - 1))
+        send_down = take(values, jnp.clip(place + step - count, 0, count - 1))
+        if up is not None:
+            send_up = add_low(send_up, up)
+            send_down = add_low(send_down, down)
+        up = lax.ppermute(send_up, "fsdp", pairs_up)
+        down = lax.ppermute(send_down, "fsdp", pairs_down)
+    return take(values, place).astype(full) + up.astype(full) + down.astype(full)
+
+
+def sum_rows(keep, send, place):
+    mine = add_low(keep, swap_core(send))
+    half = keep.shape[-1] // 2
+    one, two = mine[..., :half], mine[..., half:]
+    one = add_low(one[:, 0], swap_ctx(one[:, 1]))
+    two = add_low(two[0], swap_side(two[1]))
+    one = add_low(one[0], swap_side(one[1]))
+    two = add_low(two[0], swap_ctx(two[1]))
+    return jnp.concatenate([line_sum(one, place), line_sum(two, place)], axis=-1)
+
+
+def sum_fsdp(values, place, side, core):
+    fsdp = lax.axis_size("fsdp")
+    rows, width = values.shape[0] // fsdp, values.shape[1]
+    parts = values.reshape(fsdp // 2, 2, rows, width).swapaxes(0, 1)
+    mine = halve(parts, core, swap_core).reshape(fsdp // 4, 2, rows, width)
+    half = width // 2
+    one, two = mine[..., :half], mine[..., half:]
+    one = line_sum(halve(one.swapaxes(0, 1), side, swap_side), place)
+    two = line_sum(two, place).astype(low)
+    two = take(two, side).astype(full) + swap_side(take(two, 1 - side)).astype(full)
+    return jnp.concatenate([one, two], axis=-1)
+
+
+def sum_all(values, fsdp):
+    values = values + lax.ppermute(values, "fsdp", core_pairs(fsdp))
+    values = values + swap_ctx(values)
+    step = 2
+    while step < fsdp:
+        values = values + lax.ppermute(values, "fsdp", [(i, i ^ step) for i in range(fsdp)])
+        step *= 2
+    return values
+
+
+def turn(values):
+    return pltpu.roll(values, values.shape[-1] // 2, 1)
+
+
+def norm_rope(raw, gain, cosine, sine):
+    scale = lax.rsqrt(jnp.mean(raw * raw, axis=-1, keepdims=True) + eps_norm)
+    scaled = raw * scale * gain
+    return scaled * cosine + turn(scaled) * sine
+
+
+def norm_rope_back(raw, gain, cosine, sine, grad):
+    scale = lax.rsqrt(jnp.mean(raw * raw, axis=-1, keepdims=True) + eps_norm)
+    unit = raw * scale
+    grad_scaled = grad * cosine - turn(grad) * sine
+    grad_gain = jnp.sum(grad_scaled * unit, axis=0, keepdims=True)
+    grad_unit = grad_scaled * gain
+    grad_raw = scale * (grad_unit - unit * jnp.mean(grad_unit * unit, axis=-1, keepdims=True))
+    return grad_raw, grad_gain
+
+
+def tiles_of(rows):
+    step = rows // 2
+    return [(start, start + step) for start in range(0, rows, step)]
+
+
+def allowed(start, stop):
+    shape = (stop - start, stop)
+    return lax.broadcasted_iota(jnp.int32, shape, 1) <= (
+        lax.broadcasted_iota(jnp.int32, shape, 0) + start
+    )
+
+
+def attend_kernel(q_ref, k_ref, v_ref, cos_ref, sin_ref, qg_ref, kg_ref, o_ref, qr_ref, kr_ref, vl_ref):
+    head_dim = k_ref.shape[1]
+    rows = k_ref.shape[0]
+    cosine, sine = cos_ref[...], sin_ref[...]
+    keys = norm_rope(k_ref[...], kg_ref[...], cosine, sine).astype(low)
+    values = v_ref[...].astype(low)
+    kr_ref[...] = keys
+    vl_ref[...] = values
+    for head in range(q_ref.shape[1] // head_dim):
+        cols = slice(head * head_dim, (head + 1) * head_dim)
+        query = norm_rope(q_ref[:, cols], qg_ref[...], cosine, sine).astype(low)
+        qr_ref[:, cols] = query
+        for start, stop in tiles_of(rows):
+            scores = mul(query[start:stop], keys[:stop], rhs_turned) * (1.0 / math.sqrt(head_dim))
+            expo = jnp.where(allowed(start, stop), jnp.exp(scores), 0.0)
+            probs = (expo / jnp.sum(expo, axis=-1, keepdims=True)).astype(low)
+            o_ref[start:stop, cols] = mul(probs, values[:stop]).astype(low)
+
+
+def attend_grad_kernel(
+    q_ref, k_ref, qr_ref, kr_ref, vl_ref, go_ref, cos_ref, sin_ref, qg_ref, kg_ref,
+    dq_ref, dk_ref, dv_ref, dqg_ref, dkg_ref, dk_sum, dv_sum, dq_sum,
+):
+    head_dim = k_ref.shape[1]
+    rows = k_ref.shape[0]
+    root = 1.0 / math.sqrt(head_dim)
+    cosine, sine = cos_ref[...], sin_ref[...]
+    keys, values = kr_ref[...], vl_ref[...]
+    gain_sum = jnp.zeros((1, head_dim), full)
+    dk_sum[...] = jnp.zeros_like(dk_sum)
+    dv_sum[...] = jnp.zeros_like(dv_sum)
+    for head in range(q_ref.shape[1] // head_dim):
+        cols = slice(head * head_dim, (head + 1) * head_dim)
+        for start, stop in tiles_of(rows):
+            query = qr_ref[start:stop, cols]
+            grad = go_ref[start:stop, cols]
+            scores = mul(query, keys[:stop], rhs_turned) * root
+            expo = jnp.where(allowed(start, stop), jnp.exp(scores), 0.0)
+            probs = expo / jnp.sum(expo, axis=-1, keepdims=True)
+            grad_probs = mul(grad, values[:stop], rhs_turned)
+            delta = jnp.sum(grad_probs * probs, axis=-1, keepdims=True)
+            grad_scores = (probs * (grad_probs - delta)).astype(low)
+            dv_sum[:stop] += mul(probs.astype(low), grad, lhs_turned)
+            dk_sum[:stop] += mul(grad_scores, query, lhs_turned)
+            dq_sum[start:stop] = mul(grad_scores, keys[:stop])
+        grad_query = (dq_sum[...] * root).astype(low).astype(full)
+        grad_raw, grad_gain = norm_rope_back(q_ref[:, cols], qg_ref[...], cosine, sine, grad_query)
+        dq_ref[:, cols] = grad_raw.astype(low)
+        gain_sum = gain_sum + grad_gain
+    dqg_ref[0] = gain_sum
+    grad_key = (dk_sum[...] * root).astype(low).astype(full)
+    grad_raw, grad_gain = norm_rope_back(k_ref[...], kg_ref[...], cosine, sine, grad_key)
+    dk_ref[...] = grad_raw.astype(low)
+    dkg_ref[0] = grad_gain
+    dv_ref[...] = dv_sum[...].astype(low)
+
+
+def attention_specs(rows, head_dim, kv_heads, group):
+    wide, narrow = group * head_dim, head_dim
+    heads_end = kv_heads * group
+    return dict(
+        q=pl.BlockSpec((rows, wide), lambda i: (0, i)),
+        k=pl.BlockSpec((rows, narrow), lambda i: (0, heads_end + i)),
+        v=pl.BlockSpec((rows, narrow), lambda i: (0, heads_end + kv_heads + i)),
+        own=pl.BlockSpec((rows, narrow), lambda i: (0, i)),
+        table=pl.BlockSpec((rows, head_dim), lambda i: (0, 0)),
+        gain=pl.BlockSpec((1, head_dim), lambda i: (0, 0)),
+        gain_out=pl.BlockSpec((1, 1, head_dim), lambda i: (i, 0, 0)),
+    )
+
+
+def attend(projected, cosine, sine, query_gain, key_gain, kv_heads, group):
+    rows, head_dim = cosine.shape
+    s = attention_specs(rows, head_dim, kv_heads, group)
+    shape = jax.ShapeDtypeStruct
+    work = rows * rows * head_dim * kv_heads * group
+    return pl.pallas_call(
+        attend_kernel,
+        grid=(kv_heads,),
+        in_specs=[s["q"], s["k"], s["v"], s["table"], s["table"], s["gain"], s["gain"]],
+        out_specs=[s["q"], s["q"], s["own"], s["own"]],
+        out_shape=[
+            shape((rows, kv_heads * group * head_dim), low),
+            shape((rows, kv_heads * group * head_dim), low),
+            shape((rows, kv_heads * head_dim), low),
+            shape((rows, kv_heads * head_dim), low),
+        ],
+        compiler_params=pltpu.CompilerParams(vmem_limit_bytes=48 << 20),
+        cost_estimate=pl.CostEstimate(
+            flops=4 * work, bytes_accessed=projected.size * 6, transcendentals=work // head_dim
+        ),
+        name="attend",
+    )(projected, projected, projected, cosine, sine, query_gain, key_gain)
+
+
+def attend_grad(projected, roped_q, roped_k, values_low, grad, cosine, sine, query_gain, key_gain, kv_heads, group):
+    rows, head_dim = cosine.shape
+    s = attention_specs(rows, head_dim, kv_heads, group)
+    shape = jax.ShapeDtypeStruct
+    work = rows * rows * head_dim * kv_heads * group
+    return pl.pallas_call(
+        attend_grad_kernel,
+        grid=(kv_heads,),
+        in_specs=[
+            s["q"], s["k"], s["q"], s["own"], s["own"], s["q"],
+            s["table"], s["table"], s["gain"], s["gain"],
+        ],
+        out_specs=[s["q"], s["own"], s["own"], s["gain_out"], s["gain_out"]],
+        out_shape=[
+            shape((rows, kv_heads * group * head_dim), low),
+            shape((rows, kv_heads * head_dim), low),
+            shape((rows, kv_heads * head_dim), low),
+            shape((kv_heads, 1, head_dim), full),
+            shape((kv_heads, 1, head_dim), full),
+        ],
+        scratch_shapes=[pltpu.VMEM((rows, head_dim), full)] * 3,
+        compiler_params=pltpu.CompilerParams(vmem_limit_bytes=48 << 20),
+        cost_estimate=pl.CostEstimate(
+            flops=10 * work, bytes_accessed=projected.size * 10, transcendentals=work // head_dim
+        ),
+        name="attend_grad",
+    )(projected, projected, roped_q, roped_k, values_low, grad, cosine, sine, query_gain, key_gain)
+
+
+def expert_kernel(
+    who, order, m_ref, g_ref, r_ref, w_ref, gu_ref, dn_ref,
+    keep_out, send_out, keep_back, send_back, gate_back, rows_ref, dy_ref, z_ref, pair_ref,
+):
+    expert, core = who[0], who[1]
+    block = m_ref.shape[3]
+    hidden = dn_ref.shape[0]
+    slots = z_ref.shape[0] // 2
+    shape = (block, block)
+    earlier = (
+        lax.broadcasted_iota(jnp.int32, shape, 0) < lax.broadcasted_iota(jnp.int32, shape, 1)
+    ).astype(low)
+    slot_ids = lax.broadcasted_iota(jnp.int32, (slots, block), 0)
+    places, picks, weights, rows, grads = [], [], [], [], []
+    for part in range(2):
+        at = lax.rem(core + part, 2)
+        named = r_ref[0, at, 0] == expert
+        ones = jnp.where(named, 1.0, 0.0)
+        hit = jnp.sum(ones, axis=0, keepdims=True)
+        gate = jnp.sum(jnp.where(named, w_ref[0, at, 0], 0.0), axis=0, keepdims=True)
+        count = jnp.sum(mul(ones.astype(low), earlier), axis=0, keepdims=True).astype(jnp.int32)
+        place = (slot_ids == count) & (hit > 0.5)
+        pick = place.astype(full).astype(low)
+        places.append(place)
+        picks.append(pick)
+        weights.append(jnp.sum(jnp.where(place, gate, 0.0), axis=1, keepdims=True))
+        rows.append(mul(pick, m_ref[0, at, 0]).astype(low))
+        grads.append(mul(pick, g_ref[0, at, 0]))
+    row, grad, weight = (jnp.concatenate(items, axis=0) for items in (rows, grads, weights))
+    rows_ref[...] = row
+    paired = mul(row, gu_ref[...])
+    gate_in, up = paired[:, :hidden], paired[:, hidden:]
+    sig = jax.nn.sigmoid(gate_in)
+    act = gate_in * sig
+    z = (act * up).astype(low)
+    z_ref[...] = z
+    y = mul(z, dn_ref[...]).astype(low).astype(full)
+    grad_gate = jnp.sum(grad * y, axis=1, keepdims=True)
+    y_scaled = (weight * y).astype(low)
+    dy = (weight * grad).astype(low)
+    dy_ref[...] = dy
+    for part, out in enumerate((keep_out, send_out)):
+        mine = slice(part * slots, (part + 1) * slots)
+        out[0] = mul(picks[part], y_scaled[mine], lhs_turned).astype(low)
+        gate_back[0, lax.rem(core + part, 2), 0] = jnp.sum(
+            jnp.where(places[part], grad_gate[mine], 0.0), axis=0, keepdims=True
+        )
+    dz = mul(dy, dn_ref[...], rhs_turned)
+    grad_in = dz * up * (sig * (1.0 + gate_in * (1.0 - sig)))
+    pair = jnp.concatenate([grad_in, dz * act], axis=1).astype(low)
+    pair_ref[...] = pair
+    back = mul(pair, gu_ref[...], rhs_turned).astype(low)
+    for part, out in enumerate((keep_back, send_back)):
+        mine = slice(part * slots, (part + 1) * slots)
+        out[0] = mul(picks[part], back[mine], lhs_turned).astype(low)
+
+
+def run_expert(who, order, m_all, g_all, routes_all, gates_all, gate_up, down, slots):
+    places, _, _, block, width = m_all.shape
+    top = routes_all.shape[3]
+    paired = gate_up.shape[1]
+    steps = places * 2
+    total = steps * 2 * slots
+    hidden = paired // 2
+    shape = jax.ShapeDtypeStruct
+
+    def token_at(i, who, order):
+        return (order[2 * i], 0, order[2 * i + 1], 0, 0)
+
+    def fixed(i, who, order):
+        return (0, 0)
+
+    def flat(i, who, order):
+        return (i, 0)
+
+    def stacked(i, who, order):
+        return (i, 0, 0)
+
+    tokens = pl.BlockSpec((1, 2, 1, block, width), token_at)
+    small = pl.BlockSpec((1, 2, 1, top, block), token_at)
+    out_rows = pl.BlockSpec((1, block, width), stacked)
+    slot_rows = [pl.BlockSpec((2 * slots, n), flat) for n in (width, width, hidden, paired)]
+    grid_spec = pltpu.PrefetchScalarGridSpec(
+        num_scalar_prefetch=2,
+        grid=(steps,),
+        in_specs=[
+            tokens, tokens, small, small,
+            pl.BlockSpec(gate_up.shape, fixed, pipeline_mode=pl.Buffered(1)),
+            pl.BlockSpec(down.shape, fixed, pipeline_mode=pl.Buffered(1)),
+        ],
+        out_specs=[out_rows] * 4 + [pl.BlockSpec((1, 2, 1, 1, block), token_at)] + slot_rows,
+    )
+    return pl.pallas_call(
+        expert_kernel,
+        grid_spec=grid_spec,
+        out_shape=[shape((steps, block, width), low)] * 4
+        + [shape((places, 2, 2, 1, block), full)]
+        + [shape((total, n), low) for n in (width, width, hidden, paired)],
+        compiler_params=pltpu.CompilerParams(vmem_limit_bytes=vmem_bytes),
+        cost_estimate=pl.CostEstimate(
+            flops=total * width * (4 * paired + 4 * hidden + 8 * block),
+            bytes_accessed=steps * block * width * 16 + total * (width * 4 + paired * 3),
+            transcendentals=total * hidden,
+        ),
+        name="experts",
+    )(who, order, m_all, g_all, routes_all, gates_all, gate_up, down)
+
+
+def rms_back(values, gain, grad):
+    scale = lax.rsqrt(jnp.mean(values * values, axis=-1, keepdims=True) + eps_norm)
+    unit = values * scale
+    grad_gain = jnp.sum(grad * unit, axis=0)
+    grad_unit = grad * gain
+    back = scale * (grad_unit - unit * jnp.mean(grad_unit * unit, axis=-1, keepdims=True))
+    return back, grad_gain
+
+
+def in_order(first, second):
+    half = first.shape[0] // 2
+    return jnp.concatenate([first[:half], second, first[half:]], axis=0)
+
+
+def of_block(values, rank):
+    quarter = values.shape[0] // 4
+    outer = jnp.concatenate([values[:quarter], values[3 * quarter :]], axis=0)
+    return jnp.where(rank == 0, outer, values[quarter : 3 * quarter])
+
+
+def body_gathered(
+    tokens, qkv_weight, out_weight, router_weight, attn_gain, moe_gain, query_gain, key_gain,
+    expert_gate_up, expert_down, routes, cotangent,
+):
+    rows_dev, width = tokens.shape
+    head_dim = query_gain.shape[0]
+    top_k = routes.shape[1]
+    fsdp = lax.axis_size("fsdp")
+    spot = lax.axis_index("fsdp")
+    rank = lax.axis_index("ctx")
+    place, side, core = spot // 4, (spot // 2) % 2, spot % 2
+    shard = qkv_weight.shape[0]
+    heads = out_weight.shape[0] * fsdp // head_dim
+    kv_heads = (qkv_weight.shape[1] // head_dim - heads) // 2
+    group = heads // kv_heads // 2
+    my_heads = heads // 2
+    width_q, width_k = my_heads * head_dim, kv_heads * head_dim
+    experts_all = router_weight.shape[1]
+    capacity = 2 * rows_dev * top_k // experts_all
+    both = ("fsdp", "ctx")
+
+    def sequence(values):
+        other = swap_ctx(values)
+        first = jnp.where(rank == 0, values, other)
+        second = jnp.where(rank == 0, other, values)
+        return in_order(first, second)
+
+    by_parity = qkv_weight[:, : 2 * width_q].reshape(shard, my_heads, 2, head_dim)
+    q_local = jnp.where(rank == 0, by_parity[:, :, 0], by_parity[:, :, 1]).reshape(shard, width_q)
+    qkv_local = jnp.concatenate([q_local, qkv_weight[:, 2 * width_q :]], axis=1)
+    out_local = lax.dynamic_slice_in_dim(out_weight, rank * head_dim, head_dim, 0)
+    small_local = jnp.concatenate([router_weight, attn_gain[:, None], moe_gain[:, None]], axis=1)
+    small_all = lax.all_gather(small_local, "fsdp", axis=0, tiled=True)
+    qkv_all = lax.all_gather(qkv_local, "fsdp", axis=0, tiled=True)
+    out_all = lax.all_gather(out_local, "fsdp", axis=0, tiled=True)
+    router_all = small_all[:, :experts_all]
+    attn_all = small_all[:, experts_all].astype(full)
+    moe_all = small_all[:, experts_all + 1].astype(full)
+    routes_all = lax.all_gather(routes.T, both, axis=0)
+    g_all = lax.all_gather(cotangent, both, axis=0)
+
+    sequence_in = sequence(tokens).astype(full)
+    low_in = rms_scale(sequence_in, attn_all).astype(low)
+    projected = mul(low_in, qkv_all)
+    cosine, sine = (t[:, 0] for t in angles(jnp.arange(2 * rows_dev, dtype=jnp.int32), head_dim))
+    sine = jnp.concatenate([-sine[:, : head_dim // 2], sine[:, head_dim // 2 :]], axis=1)
+    gain_q, gain_k = query_gain.astype(full)[None], key_gain.astype(full)[None]
+    attended, roped_q, roped_k, values_low = attend(
+        projected, cosine, sine, gain_q, gain_k, kv_heads, group
+    )
+    branch = mul(attended, out_all)
+    inputs = tokens.astype(full)
+    mixed = (
+        inputs
+        + of_block(branch, rank)
+        + swap_ctx(of_block(branch, 1 - rank).astype(low)).astype(full)
+    )
+    low_mid = rms_scale(mixed, moe_all).astype(low)
+    m_all = lax.all_gather(low_mid, both, axis=0)
+
+    logits = mul(low_mid, router_all)
+    named = routes[:, :, None] == jnp.arange(experts_all, dtype=jnp.int32)[None, None, :]
+    selected = jnp.sum(jnp.where(named, logits[:, None, :], 0.0), axis=2)
+    gates = gating(selected)
+    gates_all = lax.all_gather(gates.T, both, axis=0)
+
+    steps = jnp.arange(fsdp, dtype=jnp.int32)
+    lines = fsdp // 4
+    order = jnp.stack(
+        [
+            (steps % lines) * 2 + (side + steps // (2 * lines)) % 2,
+            (rank + steps // lines) % 2,
+        ],
+        axis=1,
+    ).reshape(-1)
+    who = jnp.stack([spot * 2 + rank, core]).astype(jnp.int32)
+    grid_of = (fsdp // 2, 2, 2)
+    keep_out, send_out, keep_back, send_back, gate_back, rows, grad_rows, hidden, grad_pair = run_expert(
+        who,
+        order.astype(jnp.int32),
+        m_all.reshape(*grid_of, rows_dev, width),
+        g_all.reshape(*grid_of, rows_dev, width),
+        routes_all.reshape(*grid_of, top_k, rows_dev),
+        gates_all.reshape(*grid_of, top_k, rows_dev),
+        expert_gate_up[0],
+        expert_down[0],
+        capacity,
+    )
+    parts = (2, 2, lines, rows_dev, width)
+    grad_gates = lax.all_to_all(
+        gate_back.reshape(fsdp * 2, rows_dev), both, split_axis=0, concat_axis=0, tiled=True
+    ).T
+    grad_mid = sum_rows(keep_back.reshape(parts), send_back.reshape(parts), place)
+    grad_down = mul(hidden, grad_rows, lhs_turned)[None]
+    grad_gate_up = mul(rows, grad_pair, lhs_turned)[None]
+    output = (mixed + sum_rows(keep_out.reshape(parts), send_out.reshape(parts), place)).astype(low)
+
+    gates_wide = jnp.sum(jnp.where(named, gates[:, :, None], 0.0), axis=1)
+    chosen = jnp.any(named, axis=1)
+    grad_wide = jnp.where(chosen, grad_gates, 0.0)
+    grad_logits = (
+        gates_wide * (grad_wide - jnp.sum(gates_wide * grad_wide, axis=1, keepdims=True))
+    ).astype(low)
+    grad_router = mul(low_mid, grad_logits, lhs_turned)
+    grad_mid = grad_mid + mul(grad_logits, router_all, rhs_turned)
+    grad_mixed_part, grad_moe_gain = rms_back(mixed, moe_all, grad_mid)
+    grad_mixed = cotangent.astype(full) + grad_mixed_part
+
+    grad_branch = sequence(grad_mixed.astype(low))
+    grad_attended = mul(grad_branch, out_all, rhs_turned).astype(low)
+    grad_out_part = mul(attended, grad_branch, lhs_turned).astype(low)
+    grad_q, grad_k, grad_v, gain_q_part, gain_k_part = attend_grad(
+        projected, roped_q, roped_k, values_low, grad_attended, cosine, sine, gain_q, gain_k, kv_heads, group
+    )
+    grad_projected = jnp.concatenate([grad_q, grad_k, grad_v], axis=1)
+    grad_qkv_part = mul(low_in, grad_projected, lhs_turned).astype(low)
+    grad_normed_part = mul(grad_projected, qkv_all, rhs_turned)
+    grad_normed = of_block(grad_normed_part, rank) + swap_ctx(
+        of_block(grad_normed_part, 1 - rank).astype(low)
+    ).astype(full)
+    grad_in_part, grad_attn_gain = rms_back(inputs, attn_all, grad_normed)
+    grad_tokens = grad_mixed + grad_in_part
+
+    out_mine = sum_fsdp(grad_out_part, place, side, core)
+    out_other = swap_ctx(out_mine.astype(low)).astype(full)
+    grad_out = jnp.where(
+        rank == 0,
+        jnp.concatenate([out_mine, out_other], axis=0),
+        jnp.concatenate([out_other, out_mine], axis=0),
+    )
+    qkv_mine = sum_fsdp(grad_qkv_part, place, side, core)
+    qkv_other = swap_ctx(qkv_mine.astype(low)).astype(full)
+    q_mine = qkv_mine[:, :width_q].reshape(shard, my_heads, 1, head_dim)
+    q_other = qkv_other[:, :width_q].reshape(shard, my_heads, 1, head_dim)
+    grad_q_all = jnp.where(
+        rank == 0,
+        jnp.concatenate([q_mine, q_other], axis=2),
+        jnp.concatenate([q_other, q_mine], axis=2),
+    ).reshape(shard, 2 * width_q)
+    grad_qkv = jnp.concatenate(
+        [grad_q_all, qkv_mine[:, width_q:] + qkv_other[:, width_q:]], axis=1
+    )
+    total = sum_all(
+        jnp.concatenate(
+            [
+                grad_router,
+                grad_attn_gain[:, None],
+                grad_moe_gain[:, None],
+            ],
+            axis=1,
+        ),
+        fsdp,
+    )
+    gains = sum_all(
+        jnp.concatenate([jnp.sum(gain_q_part, axis=0), jnp.sum(gain_k_part, axis=0)], axis=0), fsdp
+    )
+    owned = lax.dynamic_slice_in_dim(total, spot * shard, shard, 0)
+    return (
+        output,
+        grad_tokens,
+        grad_qkv,
+        grad_out,
+        owned[:, :experts_all],
+        owned[:, experts_all],
+        owned[:, experts_all + 1],
+        gains[0],
+        gains[1],
+        grad_gate_up,
+        grad_down,
+    )
+
+
+gathered_bytes = 1 << 26
+
+
+def choose_body(*args):
+    tokens, gate_up = args[0], args[8]
+    fsdp, ctx = lax.axis_size("fsdp"), lax.axis_size("ctx")
+    fits = tokens.size * tokens.dtype.itemsize * fsdp * ctx <= gathered_bytes
+    if fits and fsdp % 4 == 0 and ctx == 2 and gate_up.shape[0] == 1:
+        return body_gathered(*args)
+    return body_routed(*args)
+
+
 def solution(mesh):
     in_specs = (
         P(("fsdp", "ctx"), None),
@@ -334,4 +904,4 @@
         P(("fsdp", "ctx"), None, None),
         P(("fsdp", "ctx"), None, None),
     )
-    return jax.shard_map(body, mesh=mesh, in_specs=in_specs, out_specs=out_specs, check_vma=False)
+    return jax.shard_map(choose_body, mesh=mesh, in_specs=in_specs, out_specs=out_specs, check_vma=False)

time: 3280 us -> 1510 us (0.46)
  waiting for transfers between devices: 1580 us -> 660 us
  local copies, waits for them, and re-layouts: 448 us -> 67.5 us
  blocking collectives: 451 us -> 170 us
  matrix products: 319 us -> 113 us
  other arithmetic: 316 us -> 121 us
  Pallas kernels: 0 us -> 175 us
    all_to_all x4 -> x1, waiting for transfers between devices: 797 us -> 0.01 us  [body_gathered(): lax.all_to_all(gate_back.reshape(fsdp * 2, rows_dev), both, split_axis=0,...]
    reduce_scatter x5 -> x0, waiting for transfers between devices: 727 us -> none  [the longest x1 401 us: body(): lax.psum_scatter(gradients[0], 'fsdp', scatter_dimension=0, tiled=True)]
    ppermute x0 -> x80, waiting for transfers between devices: none -> 328 us  [the longest x24 101 us: line_sum(): up = lax.ppermute(send_up, 'fsdp', pairs_up)]
    all_gather x2 -> x4, waiting for transfers between devices: 49.2 us -> 331 us  [the longest x1 196 us: body_gathered(): m_all = lax.all_gather(low_mid, both, axis=0)]
    dot_general x43 -> x11, matrix products: 319 us -> 113 us  [mul(): return lax.dot_general(left, right, dims, preferred_element_type=full)]
    unnamed x2 -> x4, other arithmetic: 199 us -> 0.07 us
    all_gather x5 -> x3, blocking collectives: 350 us -> 170 us  [the longest x1 74 us: body_gathered(): routes_all = lax.all_gather(routes.T, both, axis=0)]
    pallas_call x0 -> x3, Pallas kernels: none -> 175 us  [the longest x1 132 us: run_expert(): pl.pallas_call(expert_kernel, grid_spec=grid_spec, out_shape=[shape((step...]
  transfers between devices with their start and end apart: 12 -> 85, of which waited for: 9 -> 30; matrix products, arithmetic and copies ran while one was open for 19% -> 18% of each run, Pallas kernels for 0% -> 3%
where the time goes in v1:
time: 1510 us; the launch traced here: 1490 us
  waiting for transfers between devices  660 us (44%)
  Pallas kernels  175 us (12%)
  blocking collectives  170 us (11%)
  starting transfers between devices  165 us (11%)
  other arithmetic  121 us (8%)
  matrix products  113 us (7%)
  local copies, waits for them, and re-layouts  67.5 us (4%)
  between operations  16.3 us (1%)
    all_gather x1, waiting for transfers between devices, body_gathered(): m_all = lax.all_gather(low_mid, both, axis=0)  196 us
    pallas_call x1, Pallas kernels, run_expert(): pl.pallas_call(expert_kernel, grid_spec=grid_spec, out_shape=[shape((step...  132 us
    dot_general x11, matrix products, mul(): return lax.dot_general(left, right, dims, preferred_element_type=full)  113 us
    ppermute x24, starting transfers between devices, line_sum(): up = lax.ppermute(send_up, 'fsdp', pairs_up)  102 us
    ppermute x24, waiting for transfers between devices, line_sum(): up = lax.ppermute(send_up, 'fsdp', pairs_up)  101 us
    ppermute x12, waiting for transfers between devices, swap_ctx(): return lax.ppermute(values, 'ctx', [(0, 1), (1, 0)])  100 us
    convert_element_type x36, other arithmetic, add_low(): return (one.astype(full) + two.astype(full)).astype(low)  93.5 us
    all_gather x1, waiting for transfers between devices, body_gathered(): qkv_all = lax.all_gather(qkv_local, 'fsdp', axis=0, tiled=True)  76.6 us
  transfers between devices with their start and end apart: 85, of which 30 were waited for; matrix products, arithmetic and copies ran while one was open for 18% of the time, Pallas kernels for 3%

profile of v1, /device:TPU:0, one launch (start us, length us, event | category | flops | bytes accessed | tf_op | source)
XLA Modules:
  0.0 1488.8 jit_solution(18109618833234893477)
XLA Ops:
  16.7 22.8 %all_gather.33 = bf16[2048,34]{0,1:T(8,128)(2,1)S(1)} all-gather(bf16[128,34]{0,1:T(8,128)(2,1)S(1)} %pad_maximum_fusion.12), channel_id=1, replica_groups=mesh['fsdp'=16,'ctx'=2] {'fsdp'}, dimensions={0}, use_global_device_ids=true | all-gather | bytes 147968 | tf_op jit(solution)/shard_map/all_gather | solution.py:727
  41.9 76.6 %all-gather.9.cloned.1.call-done = bf16[2048,3072]{0,1:T(8,128)(2,1)} async-done(((bf16[128,3072]{0,1:T(8,128)(2,1)}), bf16[2048,3072]{0,1:T(8,128)(2,1)}) %all-gather.9.cloned.1.call-update) | async-done | bytes 12582928 | tf_op jit(solution)/shard_map/all_gather | solution.py:728
  118.4 11.4 fusion.92.q_ref.k_ref.v_ref
  129.8 18.3 %attend.1 = (bf16[512,2048]{1,0:T(8,128)(2,1)S(1)}, bf16[512,2048]{1,0:T(8,128)(2,1)S(1)}, bf16[512,512]{1,0:T(8,128)(2,1)S(1)}, bf16[512,512]{1,0:T(8,128)(2,1)S(1)}) custom-call(f32[512,3072]{1,0:T(8,128)} %fusion.92.q_ref.k_ref.v_ref, f32[512,3072]{1,0:T(8,128)} %fusion.92.q_ref.k_ref.v_ref, f32[512,3072]{1,0:T(8,128)} %fusion.92.q_ref.k_ref.v_ref, ...), custom_call_target="tpu_custom_call" | custom-call | flops 2147483648 | bytes 9437184 | tf_op jit(solution)/shard_map/attend/pallas_call | solution.py:519
  150.2 44.0 %all-gather.11.cloned.1.call-done = bf16[2048,2048]{1,0:T(8,128)(2,1)} async-done(((bf16[128,2048]{1,0:T(8,128)(2,1)}), bf16[2048,2048]{1,0:T(8,128)(2,1)}) %all-gather.11.cloned.1.call-update) | async-done | bytes 8388624 | tf_op jit(solution)/shard_map/all_gather | solution.py:729
  194.3 6.9 fusion.102
  203.3 31.4 %collective-permute-done.1 = bf16[256,2048]{1,0:T(8,128)(2,1)S(1)} collective-permute-done((bf16[256,2048]{1,0:T(8,128)(2,1)S(1)}, bf16[256,2048]{1,0:T(8,128)(2,1)S(1)}, u32[]{:S(2)}, u32[]{:S(2)}) %collective-permute-start.1) | collective-permute-done | bytes 1048608 | tf_op jit(solution)/shard_map/ppermute | solution.py:341
  238.6 74.0 %all-gather.2 = s32[256,256]{1,0:T(8,128)} all-gather(s32[8,256]{1,0:T(8,128)S(1)} %bitcast.350), channel_id=4, replica_groups=mesh['fsdp'=16,'ctx'=2] {'fsdp','ctx'}, dimensions={0}, use_global_device_ids=true | all-gather | bytes 270336 | tf_op jit(solution)/shard_map/all_gather | solution.py:733
  314.4 73.5 %all-gather.3 = f32[256,256]{1,0:T(8,128)} all-gather(f32[8,256]{1,0:T(8,128)S(1)} %fusion.122), channel_id=5, replica_groups=mesh['fsdp'=16,'ctx'=2] {'fsdp','ctx'}, dimensions={0}, use_global_device_ids=true | all-gather | bytes 270336 | tf_op jit(solution)/shard_map/all_gather | solution.py:759
  387.9 14.4 all-gather.15.cloned.1.call-done
  402.3 196.4 %all-gather.13.cloned.1.call-done = bf16[8192,2048]{1,0:T(8,128)(2,1)} async-done(((bf16[256,2048]{1,0:T(8,128)(2,1)}), bf16[8192,2048]{1,0:T(8,128)(2,1)}) %all-gather.13.cloned.1.call-update) | async-done | bytes 33554448 | tf_op jit(solution)/shard_map/all_gather | solution.py:753
  598.8 132.1 %experts.1 = (bf16[16,256,2048]{2,1,0:T(8,128)(2,1)}, bf16[16,256,2048]{2,1,0:T(8,128)(2,1)}, bf16[16,256,2048]{2,1,0:T(8,128)(2,1)}, bf16[16,256,2048]{2,1,0:T(...) custom-call(s32[2]{0:T(128)} %pad_add_fusion.1.who, ...), custom_call_target="tpu_custom_call" | custom-call | flops 94489280512 | bytes 186646528 | tf_op jit(solution)/shard_map/experts/pallas_call | solution.py:659
  731.4 25.0 %collective-permute-done.19 = bf16[2,2,4,256,2048]{4,3,2,1,0:T(8,128)(2,1)} collective-permute-done((bf16[2,2,4,256,2048]{4,3,2,1,0:T(8,128)(2,1)}, bf16[2,2,4,256,2048]{4,3,2,1,0:T(8,128)(2,1)}, u32[]{:S(2)}, u32[]{:S(2)}) %collective-permute-start.19) | collective-permute-done | bytes 16777248 | tf_op jit(solution)/shard_map/ppermute | solution.py:333
  756.4 14.0 fusion
  785.0 22.0 %fusion.1 = bf16[2,2,4,256,2048]{4,3,2,1,0:T(8,128)(2,1)} fusion(bf16[2,2,4,256,2048]{4,3,2,1,0:T(8,128)(2,1)} %bitcast.333, bf16[2,2,4,256,2048]{4,3,2,1,0:T(8,128)(2,1)} %collective-permute-done.2), kind=kLoop, calls=%fused_computation.3 | loop fusion | flops 33554432 | bytes 50331648 | tf_op jit(solution)/shard_map/convert_element_type | solution.py:345
  807.0 4.9 slice_bitcast_fusion.4
  819.8 53.2 %collective-permute-done.20 = bf16[2,4,256,1024]{3,2,1,0:T(8,128)(2,1)} collective-permute-done((bf16[2,4,256,1024]{3,2,1,0:T(8,128)(2,1)}, bf16[2,4,256,1024]{3,2,1,0:T(8,128)(2,1)}, u32[]{:S(2)}, u32[]{:S(2)}) %collective-permute-start.20) | collective-permute-done | bytes 4194336 | tf_op jit(solution)/shard_map/ppermute | solution.py:341
  874.6 7.9 fusion.5
  889.3 34.6 %convolution_bitcast_fusion = f32[1,2048,1536]{2,1,0:T(8,128)} fusion(bf16[4096,2048]{1,0:T(8,128)(2,1)} %get-tuple-element.43, bf16[4096,1536]{1,0:T(8,128)(2,1)} %get-tuple-element.44), kind=kOutput, calls=%fused_computation.7 | convolution fusion | flops 25769803776 | bytes 41943040 | tf_op jit(solution)/shard_map/dot_general | solution.py:321
  924.0 40.5 %collective-permute-done.11 = bf16[2,4,256,1024]{3,2,1,0:T(8,128)(2,1)} collective-permute-done((bf16[2,4,256,1024]{3,2,1,0:T(8,128)(2,1)}, bf16[2,4,256,1024]{3,2,1,0:T(8,128)(2,1)}, u32[]{:S(2)}, u32[]{:S(2)}) %collective-permute-start.11) | collective-permute-done | bytes 4194336 | tf_op jit(solution)/shard_map/ppermute | solution.py:337
  964.5 8.0 fusion.7
  977.8 31.6 %collective-permute-done.21 = bf16[4,256,1024]{2,1,0:T(8,128)(2,1)} collective-permute-done((bf16[4,256,1024]{2,1,0:T(8,128)(2,1)S(1)}, bf16[4,256,1024]{2,1,0:T(8,128)(2,1)}, u32[]{:S(2)}, u32[]{:S(2)}) %collective-permute-start.21) | collective-permute-done | bytes 2097184 | tf_op jit(solution)/shard_map/ppermute | solution.py:337
  1028.5 6.0 collective-permute-done.30
  1034.5 5.2 collective-permute-start.23
  1042.8 8.7 collective-permute-done.23
  1054.0 5.1 collective-permute-done.31
  1064.9 5.3 collective-permute-start.5
  1082.0 11.7 collective-permute-done.24
  1099.8 5.2 collective-permute-done.32
  1108.1 18.9 %convolution_bitcast_fusion.1 = f32[1,768,2048]{2,1,0:T(8,128)} fusion(bf16[4096,768]{1,0:T(8,128)(2,1)S(1)} %bitcast.374, bf16[4096,2048]{1,0:T(8,128)(2,1)} %get-tuple-element.46), kind=kOutput, calls=%fused_computation.42 | convolution fusion | flops 12884901888 | bytes 29360128 | tf_op jit(solution)/shard_map/dot_general | solution.py:321
  1131.2 5.2 collective-permute-start.6
  1139.3 5.2 convolution_convert_fusion.1
  1144.5 13.3 convolution_convert_fusion.2.go_ref
  1157.8 25.0 %attend_grad.1 = (bf16[512,2048]{1,0:T(8,128)(2,1)S(1)}, bf16[512,512]{1,0:T(8,128)(2,1)S(1)}, bf16[512,512]{1,0:T(8,128)(2,1)S(1)}, f32[4,1,128]{2,1,0:T(1,128)S(1)}, f32[4,1,128]{2,1,0:T(1,128)S(1)}) custom-call(f32[512,3072]{1,0:T(8,128)} %fusion.92.q_ref.k_ref.v_ref, f32[512,3072]{1,0:T(8,128)} %fusion.92.q_ref.k_ref.v_ref, bf16[512,2048]{1,0:T(8,128)(2,1)} %copy-done.2, ...), custom_call_target="tpu_custom_call" | custom-call | flops 5368709120 | bytes 15728640 | tf_op jit(solution)/shard_map/attend_grad/pallas_call | solution.py:543
  1188.4 9.2 convolution_convert_fusion
  1204.6 10.6 fusion.103
  1224.9 7.5 collective-permute-done.14
  1235.2 11.3 collective-permute-done.76
  1255.8 5.4 fusion.3
  1262.0 6.0 collective-permute-start.62
  1272.2 8.1 collective-permute-done.62
  1282.0 6.4 collective-permute-done.15
  1302.2 15.3 %collective-permute-done.72 = f32[2048,34]{0,1:T(8,128)S(1)} collective-permute-done((f32[2048,34]{0,1:T(8,128)S(1)}, f32[2048,34]{0,1:T(8,128)S(1)}, u32[]{:S(2)}, u32[]{:S(2)}) %collective-permute-start.72) | collective-permute-done | bytes 278560 | tf_op jit(solution)/shard_map/ppermute | solution.py:406
  1328.1 7.4 fusion.2
  1350.0 13.1 collective-permute-done.57
  1371.7 5.2 collective-permute-start.40
  1379.9 18.4 %collective-permute-done.40 = bf16[128,1536]{1,0:T(8,128)(2,1)S(1)} collective-permute-done((bf16[128,1536]{1,0:T(8,128)(2,1)S(1)}, bf16[128,1536]{1,0:T(8,128)(2,1)S(1)}, u32[]{:S(2)}, u32[]{:S(2)}) %collective-permute-start.40) | collective-permute-done | bytes 393248 | tf_op jit(solution)/shard_map/ppermute | solution.py:372
  1415.7 33.6 %collective-permute-start.42 = (bf16[128,1536]{1,0:T(8,128)(2,1)S(1)}, bf16[128,1536]{1,0:T(8,128)(2,1)S(1)}, u32[]{:S(2)}, u32[]{:S(2)}) collective-permute-start(bf16[128,1536]{1,0:T(8,128)(2,1)S(1)} %get-tuple-element.96), channel_id=1, source_target_pairs={{0,8},{2,10},{4,12},{6,14},{8,16},{10,18},{12,20},{14,22},{16,24},... | collective-permute-start | bytes 1179656 | tf_op jit(solution)/shard_map/ppermute | solution.py:372
  (458 shorter events, 256.9 us)
Async XLA Ops:
  7.2 111.2 %all-gather.9.cloned.1.call-start = ((), (), s32[]{:S(2)}) async-start(), calls=%async_computation.1 | async-start | bytes 13369344 | tf_op jit(solution)/shard_map/all_gather | solution.py:728
  10.6 183.7 %all-gather.11.cloned.1.call-start = ((), (), s32[]{:S(2)}) async-start(), calls=%async_computation.2 | async-start | bytes 8912896 | tf_op jit(solution)/shard_map/all_gather | solution.py:729
  11.6 390.8 %all-gather.15.cloned.1.call-start = ((), (), s32[]{:S(2)}) async-start(), calls=%async_computation.4 | async-start | bytes 34603008 | tf_op jit(solution)/shard_map/all_gather | solution.py:734
  12.3 586.5 %all-gather.13.cloned.1.call-start = ((), (), s32[]{:S(2)}) async-start(), calls=%async_computation.3 | async-start | bytes 34603008 | tf_op jit(solution)/shard_map/all_gather | solution.py:753
  12.4 27.5 %collective-permute-start = (bf16[256,2048]{1,0:T(8,128)(2,1)S(1)}, bf16[256,2048]{1,0:T(8,128)(2,1)}, u32[]{:S(2)}, u32[]{:S(2)}) collective-permute-start(bf16[256,2048]{1,0:T(8,128)(2,1)S(1)} %copy-done.13), channel_id=1, source_target_pairs={{0,1},{1,0},{2,3},{3,2},{4,5},{5,4},{6,7},{7,6},{8,9},{9,8},{10,11... | collective-permute-start | bytes 3145736 | tf_op jit(solution)/shard_map/ppermute | solution.py:341
  201.8 32.9 %collective-permute-start.1 = (bf16[256,2048]{1,0:T(8,128)(2,1)S(1)}, bf16[256,2048]{1,0:T(8,128)(2,1)S(1)}, u32[]{:S(2)}, u32[]{:S(2)}) collective-permute-start(bf16[256,2048]{1,0:T(8,128)(2,1)S(1)} %select_convert_fusion.1), channel_id=1, source_target_pairs={{0,1},{1,0},{2,3},{3,2},{4,5},{5,4},{6,7},{7,6},{8,9},{9,8},{10,11... | collective-permute-start | bytes 3145736 | tf_op jit(solution)/shard_map/ppermute | solution.py:341
  730.9 25.6 %collective-permute-start.19 = (bf16[2,2,4,256,2048]{4,3,2,1,0:T(8,128)(2,1)}, bf16[2,2,4,256,2048]{4,3,2,1,0:T(8,128)(2,1)}, u32[]{:S(2)}, u32[]{:S(2)}) collective-permute-start(bf16[2,2,4,256,2048]{4,3,2,1,0:T(8,128)(2,1)} %bitcast.370), channel_id=1, source_target_pairs={{0,2},{2,0},{4,6},{6,4},{8,10},{10,8},{12,14},{14,12},{16,18},{18,... | collective-permute-start | bytes 50331656 | tf_op jit(solution)/shard_map/ppermute | solution.py:333
  731.2 53.7 %collective-permute-start.2 = (bf16[2,2,4,256,2048]{4,3,2,1,0:T(8,128)(2,1)}, bf16[2,2,4,256,2048]{4,3,2,1,0:T(8,128)(2,1)}, u32[]{:S(2)}, u32[]{:S(2)}) collective-permute-start(bf16[2,2,4,256,2048]{4,3,2,1,0:T(8,128)(2,1)} %bitcast.369), channel_id=1, source_target_pairs={{0,2},{2,0},{4,6},{6,4},{8,10},{10,8},{12,14},{14,12},{16,18},{18,... | collective-permute-start | bytes 50331656 | tf_op jit(solution)/shard_map/ppermute | solution.py:333
  779.0 94.0 %collective-permute-start.20 = (bf16[2,4,256,1024]{3,2,1,0:T(8,128)(2,1)}, bf16[2,4,256,1024]{3,2,1,0:T(8,128)(2,1)}, u32[]{:S(2)}, u32[]{:S(2)}) collective-permute-start(bf16[2,4,256,1024]{3,2,1,0:T(8,128)(2,1)} %slice_bitcast_fusion.2), channel_id=1, source_target_pairs={{0,1},{1,0},{2,3},{3,2},{4,5},{5,4},{6,7},{7,6},{8,9},{9,8},{10,11... | collective-permute-start | bytes 12582920 | tf_op jit(solution)/shard_map/ppermute | solution.py:341
  780.5 94.1 %collective-permute-start.28 = (bf16[2,4,256,1024]{3,2,1,0:T(8,128)(2,1)}, bf16[2,4,256,1024]{3,2,1,0:T(8,128)(2,1)}, u32[]{:S(2)}, u32[]{:S(2)}) collective-permute-start(bf16[2,4,256,1024]{3,2,1,0:T(8,128)(2,1)} %slice_bitcast_fusion), channel_id=1, source_target_pairs={{0,4},{2,6},{4,0},{6,2},{8,12},{10,14},{12,8},{14,10},{16,20},{18,... | collective-permute-start | bytes 12582920 | tf_op jit(solution)/shard_map/ppermute | solution.py:337
  781.7 261.1 %all-to-all-start = ((f32[32,1,256]{2,1,0:T(1,128)}), f32[32,1,256]{2,1,0:T(1,128)S(1)}, u32[]{:S(2)}, u32[]{:S(2)}) async-start(f32[32,1,256]{2,1,0:T(1,128)} %bitcast.66), calls=%async_computation | async-start | bytes 65536 | tf_op jit(solution)/shard_map/all_to_all | solution.py:784
  811.8 152.6 %collective-permute-start.11 = (bf16[2,4,256,1024]{3,2,1,0:T(8,128)(2,1)}, bf16[2,4,256,1024]{3,2,1,0:T(8,128)(2,1)}, u32[]{:S(2)}, u32[]{:S(2)}) collective-permute-start(bf16[2,4,256,1024]{3,2,1,0:T(8,128)(2,1)} %slice_bitcast_fusion.4), channel_id=1, source_target_pairs={{0,4},{2,6},{4,0},{6,2},{8,12},{10,14},{12,8},{14,10},{16,20},{18,... | collective-permute-start | bytes 12582920 | tf_op jit(solution)/shard_map/ppermute | solution.py:337
  818.3 146.1 %collective-permute-start.3 = (bf16[2,4,256,1024]{3,2,1,0:T(8,128)(2,1)}, bf16[2,4,256,1024]{3,2,1,0:T(8,128)(2,1)}, u32[]{:S(2)}, u32[]{:S(2)}) collective-permute-start(bf16[2,4,256,1024]{3,2,1,0:T(8,128)(2,1)} %slice_bitcast_fusion.6), channel_id=1, source_target_pairs={{0,1},{1,0},{2,3},{3,2},{4,5},{5,4},{6,7},{7,6},{8,9},{9,8},{10,11... | collective-permute-start | bytes 12582920 | tf_op jit(solution)/shard_map/ppermute | solution.py:341
  885.7 123.7 %collective-permute-start.21 = (bf16[4,256,1024]{2,1,0:T(8,128)(2,1)S(1)}, bf16[4,256,1024]{2,1,0:T(8,128)(2,1)}, u32[]{:S(2)}, u32[]{:S(2)}) collective-permute-start(bf16[4,256,1024]{2,1,0:T(8,128)(2,1)S(1)} %slice_bitcast_fusion.10), channel_id=1, source_target_pairs={{0,4},{2,6},{4,0},{6,2},{8,12},{10,14},{12,8},{14,10},{16,20},{18,... | collective-permute-start | bytes 6291464 | tf_op jit(solution)/shard_map/ppermute | solution.py:337
  887.9 127.4 %collective-permute-start.29 = (bf16[4,256,1024]{2,1,0:T(8,128)(2,1)}, bf16[4,256,1024]{2,1,0:T(8,128)(2,1)}, u32[]{:S(2)}, u32[]{:S(2)}) collective-permute-start(bf16[4,256,1024]{2,1,0:T(8,128)(2,1)} %slice_bitcast_fusion.8), channel_id=1, source_target_pairs={{0,1},{1,0},{2,3},{3,2},{4,5},{5,4},{6,7},{7,6},{8,9},{9,8},{10,11... | collective-permute-start | bytes 6291464 | tf_op jit(solution)/shard_map/ppermute | solution.py:341
  977.2 84.2 %collective-permute-start.4 = (bf16[4,256,1024]{2,1,0:T(8,128)(2,1)}, bf16[4,256,1024]{2,1,0:T(8,128)(2,1)}, u32[]{:S(2)}, u32[]{:S(2)}) collective-permute-start(bf16[4,256,1024]{2,1,0:T(8,128)(2,1)} %slice_bitcast_fusion.14), channel_id=1, source_target_pairs={{0,4},{2,6},{4,0},{6,2},{8,12},{10,14},{12,8},{14,10},{16,20},{18,... | collective-permute-start | bytes 6291464 | tf_op jit(solution)/shard_map/ppermute | solution.py:337
  1013.8 26.9 %collective-permute-start.25 = (bf16[256,1024]{1,0:T(8,128)(2,1)S(1)}, bf16[256,1024]{1,0:T(8,128)(2,1)}, u32[]{:S(2)}, u32[]{:S(2)}) collective-permute-start(bf16[256,1024]{1,0:T(8,128)(2,1)S(1)} %get-tuple-element.81), channel_id=1, source_target_pairs={{24,16},{26,18},{28,20},{30,22},{25,17},{27,19},{29,21},{31,23}} | collective-permute-start | bytes 1572872 | tf_op jit(solution)/shard_map/ppermute | solution.py:373
  1021.7 55.5 %collective-permute-start.12 = (bf16[4,256,1024]{2,1,0:T(8,128)(2,1)}, bf16[4,256,1024]{2,1,0:T(8,128)(2,1)}, u32[]{:S(2)}, u32[]{:S(2)}) collective-permute-start(bf16[4,256,1024]{2,1,0:T(8,128)(2,1)} %slice_bitcast_fusion.12), channel_id=1, source_target_pairs={{0,1},{1,0},{2,3},{3,2},{4,5},{5,4},{6,7},{7,6},{8,9},{9,8},{10,11... | collective-permute-start | bytes 6291464 | tf_op jit(solution)/shard_map/ppermute | solution.py:341
  1026.1 27.9 %collective-permute-start.33 = (bf16[256,1024]{1,0:T(8,128)(2,1)}, bf16[256,1024]{1,0:T(8,128)(2,1)}, u32[]{:S(2)}, u32[]{:S(2)}) collective-permute-start(bf16[256,1024]{1,0:T(8,128)(2,1)} %get-tuple-element.85), channel_id=1, source_target_pairs={{24,16},{26,18},{28,20},{30,22},{25,17},{27,19},{29,21},{31,23}} | collective-permute-start | bytes 1572872 | tf_op jit(solution)/shard_map/ppermute | solution.py:373
  1064.9 65.3 %collective-permute-start.5 = (bf16[256,1024]{1,0:T(8,128)(2,1)S(1)}, bf16[256,1024]{1,0:T(8,128)(2,1)S(1)}, u32[]{:S(2)}, u32[]{:S(2)}) collective-permute-start(bf16[256,1024]{1,0:T(8,128)(2,1)S(1)} %get-tuple-element.88), channel_id=1, source_target_pairs={{0,8},{2,10},{4,12},{6,14},{1,9},{3,11},{5,13},{7,15}} | collective-permute-start | bytes 1572872 | tf_op jit(solution)/shard_map/ppermute | solution.py:372
  1071.5 33.5 %collective-permute-start.32 = (bf16[256,1024]{1,0:T(8,128)(2,1)S(1)}, bf16[256,1024]{1,0:T(8,128)(2,1)S(1)}, u32[]{:S(2)}, u32[]{:S(2)}) collective-permute-start(bf16[256,1024]{1,0:T(8,128)(2,1)S(1)} %get-tuple-element.82), channel_id=1, source_target_pairs={{0,8},{2,10},{4,12},{6,14},{8,16},{10,18},{12,20},{14,22},{16,24},... | collective-permute-start | bytes 1572872 | tf_op jit(solution)/shard_map/ppermute | solution.py:372
  1077.2 27.8 %collective-permute-start.35 = (bf16[256,1024]{1,0:T(8,128)(2,1)S(1)}, bf16[256,1024]{1,0:T(8,128)(2,1)S(1)}, u32[]{:S(2)}, u32[]{:S(2)}) collective-permute-start(bf16[256,1024]{1,0:T(8,128)(2,1)S(1)} %fusion.44), channel_id=1, source_target_pairs={{8,0},{10,2},{12,4},{14,6},{16,8},{18,10},{20,12},{22,14},{24,16},... | collective-permute-start | bytes 1572872 | tf_op jit(solution)/shard_map/ppermute | solution.py:373
  1093.7 42.7 %collective-permute-start.13 = (bf16[256,1024]{1,0:T(8,128)(2,1)S(1)}, bf16[256,1024]{1,0:T(8,128)(2,1)S(1)}, u32[]{:S(2)}, u32[]{:S(2)}) collective-permute-start(bf16[256,1024]{1,0:T(8,128)(2,1)S(1)} %get-tuple-element.92), channel_id=1, source_target_pairs={{0,8},{2,10},{4,12},{6,14},{1,9},{3,11},{5,13},{7,15}} | collective-permute-start | bytes 1572872 | tf_op jit(solution)/shard_map/ppermute | solution.py:372
  1107.5 29.9 %collective-permute-start.36 = (bf16[256,2048]{1,0:T(8,128)(2,1)S(1)}, bf16[256,2048]{1,0:T(8,128)(2,1)S(1)}, u32[]{:S(2)}, u32[]{:S(2)}) collective-permute-start(bf16[256,2048]{1,0:T(8,128)(2,1)S(1)} %fusion.94), channel_id=1, source_target_pairs={{0,1},{1,0},{2,3},{3,2},{4,5},{5,4},{6,7},{7,6},{8,9},{9,8},{10,11... | collective-permute-start | bytes 3145736 | tf_op jit(solution)/shard_map/ppermute | solution.py:341
  1127.3 92.0 %collective-permute-start.8 = (bf16[256,1024]{1,0:T(8,128)(2,1)}, bf16[256,1024]{1,0:T(8,128)(2,1)}, u32[]{:S(2)}, u32[]{:S(2)}) collective-permute-start(bf16[256,1024]{1,0:T(8,128)(2,1)} %get-tuple-element.89), channel_id=1, source_target_pairs={{24,16},{26,18},{28,20},{30,22},{25,17},{27,19},{29,21},{31,23}} | collective-permute-start | bytes 1572872 | tf_op jit(solution)/shard_map/ppermute | solution.py:373
  1128.7 92.0 %collective-permute-start.16 = (bf16[256,1024]{1,0:T(8,128)(2,1)}, bf16[256,1024]{1,0:T(8,128)(2,1)}, u32[]{:S(2)}, u32[]{:S(2)}) collective-permute-start(bf16[256,1024]{1,0:T(8,128)(2,1)} %get-tuple-element.93), channel_id=1, source_target_pairs={{24,16},{26,18},{28,20},{30,22},{25,17},{27,19},{29,21},{31,23}} | collective-permute-start | bytes 1572872 | tf_op jit(solution)/shard_map/ppermute | solution.py:373
  1131.2 89.7 %collective-permute-start.6 = (bf16[256,1024]{1,0:T(8,128)(2,1)}, bf16[256,1024]{1,0:T(8,128)(2,1)}, u32[]{:S(2)}, u32[]{:S(2)}) collective-permute-start(bf16[256,1024]{1,0:T(8,128)(2,1)} %fusion.60), channel_id=1, source_target_pairs={{0,8},{2,10},{4,12},{6,14},{8,16},{10,18},{12,20},{14,22},{1,9},{3... | collective-permute-start | bytes 1572872 | tf_op jit(solution)/shard_map/ppermute | solution.py:372
  1186.6 69.2 %collective-permute-start.54 = (bf16[8,128,2048]{2,1,0:T(8,128)(2,1)}, bf16[8,128,2048]{2,1,0:T(8,128)(2,1)}, u32[]{:S(2)}, u32[]{:S(2)}) collective-permute-start(bf16[8,128,2048]{2,1,0:T(8,128)(2,1)} %dynamic-slice_bitcast_fusion.1), channel_id=1, source_target_pairs={{0,2},{2,0},{4,6},{6,4},{8,10},{10,8},{12,14},{14,12},{16,18},{18,... | collective-permute-start | bytes 12582920 | tf_op jit(solution)/shard_map/ppermute | solution.py:333
  1204.1 124.0 %collective-permute-start.38 = (bf16[8,128,3072]{2,1,0:T(8,128)(2,1)}, bf16[8,128,3072]{2,1,0:T(8,128)(2,1)}, u32[]{:S(2)}, u32[]{:S(2)}) collective-permute-start(bf16[8,128,3072]{2,1,0:T(8,128)(2,1)} %dynamic-slice_bitcast_fusion), channel_id=1, source_target_pairs={{0,2},{2,0},{4,6},{6,4},{8,10},{10,8},{12,14},{14,12},{16,18},{18,... | collective-permute-start | bytes 18874376 | tf_op jit(solution)/shard_map/ppermute | solution.py:333
  1220.9 32.0 %collective-permute-start.37 = (bf16[256,2048]{1,0:T(8,128)(2,1)S(1)}, bf16[256,2048]{1,0:T(8,128)(2,1)S(1)}, u32[]{:S(2)}, u32[]{:S(2)}) collective-permute-start(bf16[256,2048]{1,0:T(8,128)(2,1)S(1)} %select_convert_fusion), channel_id=1, source_target_pairs={{0,1},{1,0},{2,3},{3,2},{4,5},{5,4},{6,7},{7,6},{8,9},{9,8},{10,11... | collective-permute-start | bytes 3145736 | tf_op jit(solution)/shard_map/ppermute | solution.py:341
  1224.1 24.1 %collective-permute-start.9 = (bf16[256,1024]{1,0:T(8,128)(2,1)S(1)}, bf16[256,1024]{1,0:T(8,128)(2,1)S(1)}, u32[]{:S(2)}, u32[]{:S(2)}) collective-permute-start(bf16[256,1024]{1,0:T(8,128)(2,1)S(1)} %get-tuple-element.87), channel_id=1, source_target_pairs={{16,8},{18,10},{20,12},{22,14},{24,16},{26,18},{28,20},{30,22},{17... | collective-permute-start | bytes 1572872 | tf_op jit(solution)/shard_map/ppermute | solution.py:373
  1288.4 34.5 %collective-permute-start.55 = (bf16[4,128,1024]{2,1,0:T(8,128)(2,1)S(1)}, bf16[4,128,1024]{2,1,0:T(8,128)(2,1)S(1)}, u32[]{:S(2)}, u32[]{:S(2)}) collective-permute-start(bf16[4,128,1024]{2,1,0:T(8,128)(2,1)S(1)} %dynamic-slice_bitcast_fusion.3), channel_id=1, source_target_pairs={{0,4},{2,6},{4,0},{6,2},{8,12},{10,14},{12,8},{14,10},{16,20},{18,... | collective-permute-start | bytes 3145736 | tf_op jit(solution)/shard_map/ppermute | solution.py:337
  1294.1 25.9 %collective-permute-start.65 = (bf16[2,128,1024]{2,1,0:T(8,128)(2,1)S(1)}, bf16[2,128,1024]{2,1,0:T(8,128)(2,1)S(1)}, u32[]{:S(2)}, u32[]{:S(2)}) collective-permute-start(bf16[2,128,1024]{2,1,0:T(8,128)(2,1)S(1)} %get-tuple-element.73), channel_id=1, source_target_pairs={{24,16},{26,18},{28,20},{30,22},{25,17},{27,19},{29,21},{31,23}} | collective-permute-start | bytes 1572872 | tf_op jit(solution)/shard_map/ppermute | solution.py:373
  1294.8 25.2 %collective-permute-start.63 = (bf16[2,128,1024]{2,1,0:T(8,128)(2,1)S(1)}, bf16[2,128,1024]{2,1,0:T(8,128)(2,1)S(1)}, u32[]{:S(2)}, u32[]{:S(2)}) collective-permute-start(bf16[2,128,1024]{2,1,0:T(8,128)(2,1)S(1)} %fusion.39), channel_id=1, source_target_pairs={{0,8},{2,10},{4,12},{6,14},{8,16},{10,18},{12,20},{14,22},{1,9},{3... | collective-permute-start | bytes 1572872 | tf_op jit(solution)/shard_map/ppermute | solution.py:372
  1336.4 32.1 %collective-permute-start.39 = (bf16[4,128,1536]{2,1,0:T(8,128)(2,1)S(1)}, bf16[4,128,1536]{2,1,0:T(8,128)(2,1)S(1)}, u32[]{:S(2)}, u32[]{:S(2)}) collective-permute-start(bf16[4,128,1536]{2,1,0:T(8,128)(2,1)S(1)} %dynamic-slice_bitcast_fusion.2), channel_id=1, source_target_pairs={{0,4},{2,6},{4,0},{6,2},{8,12},{10,14},{12,8},{14,10},{16,20},{18,... | collective-permute-start | bytes 4718600 | tf_op jit(solution)/shard_map/ppermute | solution.py:337
  1338.1 26.8 %collective-permute-start.46 = (bf16[2,128,1536]{2,1,0:T(8,128)(2,1)S(1)}, bf16[2,128,1536]{2,1,0:T(8,128)(2,1)S(1)}, u32[]{:S(2)}, u32[]{:S(2)}) collective-permute-start(bf16[2,128,1536]{2,1,0:T(8,128)(2,1)S(1)} %get-tuple-element.68), channel_id=1, source_target_pairs={{0,8},{2,10},{4,12},{6,14},{1,9},{3,11},{5,13},{7,15}} | collective-permute-start | bytes 2359304 | tf_op jit(solution)/shard_map/ppermute | solution.py:372
  1343.0 34.0 %collective-permute-start.64 = (bf16[2,128,1024]{2,1,0:T(8,128)(2,1)S(1)}, bf16[2,128,1024]{2,1,0:T(8,128)(2,1)S(1)}, u32[]{:S(2)}, u32[]{:S(2)}) collective-permute-start(bf16[2,128,1024]{2,1,0:T(8,128)(2,1)S(1)} %copy-done.53), channel_id=1, source_target_pairs={{0,8},{2,10},{4,12},{6,14},{8,16},{10,18},{12,20},{14,22},{16,24},... | collective-permute-start | bytes 1572872 | tf_op jit(solution)/shard_map/ppermute | solution.py:372
  1348.7 29.7 %collective-permute-start.67 = (bf16[2,128,1024]{2,1,0:T(8,128)(2,1)S(1)}, bf16[2,128,1024]{2,1,0:T(8,128)(2,1)S(1)}, u32[]{:S(2)}, u32[]{:S(2)}) collective-permute-start(bf16[2,128,1024]{2,1,0:T(8,128)(2,1)S(1)} %fusion.38), channel_id=1, source_target_pairs={{8,0},{10,2},{12,4},{14,6},{16,8},{18,10},{20,12},{22,14},{24,16},... | collective-permute-start | bytes 1572872 | tf_op jit(solution)/shard_map/ppermute | solution.py:373
  1364.9 34.1 %collective-permute-start.49 = (bf16[2,128,1536]{2,1,0:T(8,128)(2,1)S(1)}, bf16[2,128,1536]{2,1,0:T(8,128)(2,1)S(1)}, u32[]{:S(2)}, u32[]{:S(2)}) collective-permute-start(bf16[2,128,1536]{2,1,0:T(8,128)(2,1)S(1)} %get-tuple-element.69), channel_id=1, source_target_pairs={{24,16},{26,18},{28,20},{30,22},{25,17},{27,19},{29,21},{31,23}} | collective-permute-start | bytes 2359304 | tf_op jit(solution)/shard_map/ppermute | solution.py:373
  1368.5 35.0 %collective-permute-start.47 = (bf16[2,128,1536]{2,1,0:T(8,128)(2,1)S(1)}, bf16[2,128,1536]{2,1,0:T(8,128)(2,1)S(1)}, u32[]{:S(2)}, u32[]{:S(2)}) collective-permute-start(bf16[2,128,1536]{2,1,0:T(8,128)(2,1)S(1)} %fusion.31), channel_id=1, source_target_pairs={{0,8},{2,10},{4,12},{6,14},{8,16},{10,18},{12,20},{14,22},{1,9},{3... | collective-permute-start | bytes 2359304 | tf_op jit(solution)/shard_map/ppermute | solution.py:372
  1371.7 26.6 %collective-permute-start.40 = (bf16[128,1536]{1,0:T(8,128)(2,1)S(1)}, bf16[128,1536]{1,0:T(8,128)(2,1)S(1)}, u32[]{:S(2)}, u32[]{:S(2)}) collective-permute-start(bf16[128,1536]{1,0:T(8,128)(2,1)S(1)} %get-tuple-element.98), channel_id=1, source_target_pairs={{0,8},{2,10},{4,12},{6,14},{1,9},{3,11},{5,13},{7,15}} | collective-permute-start | bytes 1179656 | tf_op jit(solution)/shard_map/ppermute | solution.py:372
  1377.0 27.7 %collective-permute-start.58 = (bf16[128,1024]{1,0:T(8,128)(2,1)S(1)}, bf16[128,1024]{1,0:T(8,128)(2,1)S(1)}, u32[]{:S(2)}, u32[]{:S(2)}) collective-permute-start(bf16[128,1024]{1,0:T(8,128)(2,1)S(1)} %get-tuple-element.100), channel_id=1, source_target_pairs={{0,8},{2,10},{4,12},{6,14},{8,16},{10,18},{12,20},{14,22},{16,24},... | collective-permute-start | bytes 786440 | tf_op jit(solution)/shard_map/ppermute | solution.py:372
  1378.3 29.1 %collective-permute-start.61 = (bf16[128,1024]{1,0:T(8,128)(2,1)S(1)}, bf16[128,1024]{1,0:T(8,128)(2,1)S(1)}, u32[]{:S(2)}, u32[]{:S(2)}) collective-permute-start(bf16[128,1024]{1,0:T(8,128)(2,1)S(1)} %fusion.69), channel_id=1, source_target_pairs={{8,0},{10,2},{12,4},{14,6},{16,8},{18,10},{20,12},{22,14},{24,16},... | collective-permute-start | bytes 786440 | tf_op jit(solution)/shard_map/ppermute | solution.py:373
  1404.7 59.6 %collective-permute-start.74 = (f32[2048,34]{0,1:T(8,128)S(1)}, f32[2048,34]{0,1:T(8,128)S(1)}, u32[]{:S(2)}, u32[]{:S(2)}) collective-permute-start(f32[2048,34]{0,1:T(8,128)S(1)} %add.632), channel_id=1, source_target_pairs={{0,16},{2,18},{4,20},{6,22},{8,24},{10,26},{12,28},{14,30},{16,0},... | collective-permute-start | bytes 835592 | tf_op jit(solution)/shard_map/ppermute | solution.py:406
  1407.5 41.9 %collective-permute-start.48 = (bf16[2,128,1536]{2,1,0:T(8,128)(2,1)S(1)}, bf16[2,128,1536]{2,1,0:T(8,128)(2,1)S(1)}, u32[]{:S(2)}, u32[]{:S(2)}) collective-permute-start(bf16[2,128,1536]{2,1,0:T(8,128)(2,1)S(1)} %get-tuple-element.66), channel_id=1, source_target_pairs={{0,8},{2,10},{4,12},{6,14},{8,16},{10,18},{12,20},{14,22},{16,24},... | collective-permute-start | bytes 2359304 | tf_op jit(solution)/shard_map/ppermute | solution.py:372
  1414.1 36.8 %collective-permute-start.51 = (bf16[2,128,1536]{2,1,0:T(8,128)(2,1)S(1)}, bf16[2,128,1536]{2,1,0:T(8,128)(2,1)S(1)}, u32[]{:S(2)}, u32[]{:S(2)}) collective-permute-start(bf16[2,128,1536]{2,1,0:T(8,128)(2,1)S(1)} %fusion.30), channel_id=1, source_target_pairs={{8,0},{10,2},{12,4},{14,6},{16,8},{18,10},{20,12},{22,14},{24,16},... | collective-permute-start | bytes 2359304 | tf_op jit(solution)/shard_map/ppermute | solution.py:373
  1415.6 49.8 %collective-permute-start.69 = (bf16[128,2048]{1,0:T(8,128)(2,1)S(1)}, bf16[128,2048]{1,0:T(8,128)(2,1)S(1)}, u32[]{:S(2)}, u32[]{:S(2)}) collective-permute-start(bf16[128,2048]{1,0:T(8,128)(2,1)S(1)} %maximum_convert_fusion), channel_id=1, source_target_pairs={{0,1},{1,0},{2,3},{3,2},{4,5},{5,4},{6,7},{7,6},{8,9},{9,8},{10,11... | collective-permute-start | bytes 1572872 | tf_op jit(solution)/shard_map/ppermute | solution.py:341
  1415.7 38.9 %collective-permute-start.42 = (bf16[128,1536]{1,0:T(8,128)(2,1)S(1)}, bf16[128,1536]{1,0:T(8,128)(2,1)S(1)}, u32[]{:S(2)}, u32[]{:S(2)}) collective-permute-start(bf16[128,1536]{1,0:T(8,128)(2,1)S(1)} %get-tuple-element.96), channel_id=1, source_target_pairs={{0,8},{2,10},{4,12},{6,14},{8,16},{10,18},{12,20},{14,22},{16,24},... | collective-permute-start | bytes 1179656 | tf_op jit(solution)/shard_map/ppermute | solution.py:372
  (118 other events, 2994.4 us)
Sparse Core Ops, SparseCore 0:
  10.8 107.6 all-gather.8
  121.2 73.0 all-gather.10
  197.3 205.0 all-gather.14
  405.8 192.9 all-gather.12

commit v2 on v1

--- a/solution.py
+++ b/solution.py
@@ -353,10 +353,15 @@
     return add_low(take(values, index), swap(take(values, 1 - index)))
 
 
-def line_sum(values, place):
+def line_sum(values, place, relative=False):
     count = values.shape[0]
     fsdp = lax.axis_size("fsdp")
     up = down = None
+
+    def part(at):
+        at = jnp.clip(at, 0, count - 1)
+        return take(values, (place - at) % count if relative else at)
+
     for step in range(1, count):
         pairs_up = [
             (i, i + 4) for i in range(fsdp - 4) if i // 4 < step
@@ -364,25 +369,53 @@
         pairs_down = [
             (i, i - 4) for i in range(4, fsdp) if count - 1 - i // 4 < step
         ]
-        send_up = take(values, jnp.clip(count - step + place, 0, count - 1))
-        send_down = take(values, jnp.clip(place + step - count, 0, count - 1))
+        send_up = part(count - step + place)
+        send_down = part(place + step - count)
         if up is not None:
             send_up = add_low(send_up, up)
             send_down = add_low(send_down, down)
         up = lax.ppermute(send_up, "fsdp", pairs_up)
         down = lax.ppermute(send_down, "fsdp", pairs_down)
-    return take(values, place).astype(full) + up.astype(full) + down.astype(full)
-
-
-def sum_rows(keep, send, place):
-    mine = add_low(keep, swap_core(send))
-    half = keep.shape[-1] // 2
-    one, two = mine[..., :half], mine[..., half:]
-    one = add_low(one[:, 0], swap_ctx(one[:, 1]))
-    two = add_low(two[0], swap_side(two[1]))
-    one = add_low(one[0], swap_side(one[1]))
-    two = add_low(two[0], swap_ctx(two[1]))
-    return jnp.concatenate([line_sum(one, place), line_sum(two, place)], axis=-1)
+    return part(place).astype(full) + up.astype(full) + down.astype(full)
+
+
+def sum_quarters(quarters, place):
+    half = quarters[0, 0][0].shape[-1] // 2
+    one, two = {}, {}
+    for at in ((1, 1), (0, 1), (1, 0), (0, 0)):
+        keep, send = quarters[at]
+        other = swap_core(send)
+        one[at] = add_low(keep[..., :half], other[..., :half])
+        two[at] = add_low(keep[..., half:], other[..., half:])
+    one_side = add_low(one[1, 0], swap_ctx(one[1, 1]))
+    two_ctx = add_low(two[0, 1], swap_side(two[1, 1]))
+    one_ctx = swap_ctx(one[0, 1])
+    two_side = swap_side(two[1, 0])
+    one_mine = add_low(add_low(one[0, 0], one_ctx), swap_side(one_side))
+    two_mine = add_low(add_low(two[0, 0], two_side), swap_ctx(two_ctx))
+    sums = [line_sum(item, place, relative=True) for item in (two_mine, one_mine)]
+    return jnp.concatenate([sums[1], sums[0]], axis=-1)
+
+
+def gather_line(values):
+    fsdp = lax.axis_size("fsdp")
+    count = fsdp // 4
+    ups, downs = [values], [values]
+    for _ in range(count - 1):
+        ups.append(lax.ppermute(ups[-1], "fsdp", [(i, i + 4) for i in range(fsdp - 4)]))
+        downs.append(lax.ppermute(downs[-1], "fsdp", [(i, i - 4) for i in range(4, fsdp)]))
+    return jnp.stack([values] + [ups[s] + downs[count - s] for s in range(1, count)])
+
+
+def gather_quarters(values):
+    got = {(0, 0, 0): gather_line(values)}
+    got[1, 0, 0] = swap_side(got[0, 0, 0])
+    for side in range(2):
+        got[side, 1, 0] = swap_ctx(got[side, 0, 0])
+    for side in range(2):
+        for ctx in range(2):
+            got[side, ctx, 1] = swap_core(got[side, ctx, 0])
+    return got
 
 
 def sum_fsdp(values, place, side, core):
@@ -564,11 +597,9 @@
     )(projected, projected, roped_q, roped_k, values_low, grad, cosine, sine, query_gain, key_gain)
 
 
-def expert_kernel(
-    who, order, m_ref, g_ref, r_ref, w_ref, gu_ref, dn_ref,
-    keep_out, send_out, keep_back, send_back, gate_back, rows_ref, dy_ref, z_ref, pair_ref,
-):
-    expert, core = who[0], who[1]
+def expert_kernel(core_ref, order, m_ref, g_keep, g_send, w_ref, gu_ref, dn_ref, *refs):
+    (keep_out, send_out, keep_back, send_back, gate_back, rows_ref, dy_ref, z_ref, pair_ref) = refs[-9:]
+    core = core_ref[0]
     block = m_ref.shape[3]
     hidden = dn_ref.shape[0]
     slots = z_ref.shape[0] // 2
@@ -578,20 +609,19 @@
     ).astype(low)
     slot_ids = lax.broadcasted_iota(jnp.int32, (slots, block), 0)
     places, picks, weights, rows, grads = [], [], [], [], []
-    for part in range(2):
+    for part, g_ref in enumerate((g_keep, g_send)):
         at = lax.rem(core + part, 2)
-        named = r_ref[0, at, 0] == expert
-        ones = jnp.where(named, 1.0, 0.0)
-        hit = jnp.sum(ones, axis=0, keepdims=True)
-        gate = jnp.sum(jnp.where(named, w_ref[0, at, 0], 0.0), axis=0, keepdims=True)
-        count = jnp.sum(mul(ones.astype(low), earlier), axis=0, keepdims=True).astype(jnp.int32)
+        gate = w_ref[0, at, 0]
+        hit = jnp.where(gate >= 0.0, 1.0, 0.0)
+        ones = jnp.broadcast_to(hit, (8, block)).astype(low)
+        count = mul(ones, earlier)[:1].astype(jnp.int32)
         place = (slot_ids == count) & (hit > 0.5)
         pick = place.astype(full).astype(low)
         places.append(place)
         picks.append(pick)
         weights.append(jnp.sum(jnp.where(place, gate, 0.0), axis=1, keepdims=True))
         rows.append(mul(pick, m_ref[0, at, 0]).astype(low))
-        grads.append(mul(pick, g_ref[0, at, 0]))
+        grads.append(mul(pick, g_ref[0]))
     row, grad, weight = (jnp.concatenate(items, axis=0) for items in (rows, grads, weights))
     rows_ref[...] = row
     paired = mul(row, gu_ref[...])
@@ -621,55 +651,55 @@
         out[0] = mul(picks[part], back[mine], lhs_turned).astype(low)
 
 
-def run_expert(who, order, m_all, g_all, routes_all, gates_all, gate_up, down, slots):
+def run_expert(core, order, number, parts, m_all, g_keep, g_send, gates_all, gate_up, down, slots, kept):
     places, _, _, block, width = m_all.shape
-    top = routes_all.shape[3]
     paired = gate_up.shape[1]
-    steps = places * 2
-    total = steps * 2 * slots
+    steps = g_keep.shape[0]
+    part_rows = steps * 2 * slots
     hidden = paired // 2
     shape = jax.ShapeDtypeStruct
 
-    def token_at(i, who, order):
+    def token_at(i, core, order):
         return (order[2 * i], 0, order[2 * i + 1], 0, 0)
 
-    def fixed(i, who, order):
+    def fixed(i, core, order):
         return (0, 0)
 
-    def flat(i, who, order):
-        return (i, 0)
-
-    def stacked(i, who, order):
+    def flat(i, core, order):
+        return (number * steps + i, 0)
+
+    def stacked(i, core, order):
         return (i, 0, 0)
 
-    tokens = pl.BlockSpec((1, 2, 1, block, width), token_at)
-    small = pl.BlockSpec((1, 2, 1, top, block), token_at)
-    out_rows = pl.BlockSpec((1, block, width), stacked)
-    slot_rows = [pl.BlockSpec((2 * slots, n), flat) for n in (width, width, hidden, paired)]
+    small = pl.BlockSpec((1, 2, 1, 1, block), token_at)
+    one_block = pl.BlockSpec((1, block, width), stacked)
+    widths = (width, width, hidden, paired)
     grid_spec = pltpu.PrefetchScalarGridSpec(
         num_scalar_prefetch=2,
         grid=(steps,),
         in_specs=[
-            tokens, tokens, small, small,
+            pl.BlockSpec((1, 2, 1, block, width), token_at), one_block, one_block, small,
             pl.BlockSpec(gate_up.shape, fixed, pipeline_mode=pl.Buffered(1)),
             pl.BlockSpec(down.shape, fixed, pipeline_mode=pl.Buffered(1)),
-        ],
-        out_specs=[out_rows] * 4 + [pl.BlockSpec((1, 2, 1, 1, block), token_at)] + slot_rows,
+        ]
+        + [pl.BlockSpec(memory_space=pl.ANY)] * (0 if kept is None else 5),
+        out_specs=[one_block] * 4 + [small] + [pl.BlockSpec((2 * slots, n), flat) for n in widths],
     )
     return pl.pallas_call(
         expert_kernel,
         grid_spec=grid_spec,
         out_shape=[shape((steps, block, width), low)] * 4
         + [shape((places, 2, 2, 1, block), full)]
-        + [shape((total, n), low) for n in (width, width, hidden, paired)],
+        + [shape((parts * part_rows, n), low) for n in widths],
+        input_output_aliases={} if kept is None else {8 + i: 4 + i for i in range(5)},
         compiler_params=pltpu.CompilerParams(vmem_limit_bytes=vmem_bytes),
         cost_estimate=pl.CostEstimate(
-            flops=total * width * (4 * paired + 4 * hidden + 8 * block),
-            bytes_accessed=steps * block * width * 16 + total * (width * 4 + paired * 3),
-            transcendentals=total * hidden,
+            flops=part_rows * width * (4 * paired + 4 * hidden + 8 * block),
+            bytes_accessed=steps * block * width * 16 + part_rows * (width * 4 + paired * 3),
+            transcendentals=part_rows * hidden,
         ),
         name="experts",
-    )(who, order, m_all, g_all, routes_all, gates_all, gate_up, down)
+    )(core, order, m_all, g_keep, g_send, gates_all, gate_up, down, *(() if kept is None else kept))
 
 
 def rms_back(values, gain, grad):
@@ -721,17 +751,17 @@
 
     by_parity = qkv_weight[:, : 2 * width_q].reshape(shard, my_heads, 2, head_dim)
     q_local = jnp.where(rank == 0, by_parity[:, :, 0], by_parity[:, :, 1]).reshape(shard, width_q)
-    qkv_local = jnp.concatenate([q_local, qkv_weight[:, 2 * width_q :]], axis=1)
     out_local = lax.dynamic_slice_in_dim(out_weight, rank * head_dim, head_dim, 0)
+    weights_local = jnp.concatenate([q_local, qkv_weight[:, 2 * width_q :], out_local], axis=1)
     small_local = jnp.concatenate([router_weight, attn_gain[:, None], moe_gain[:, None]], axis=1)
     small_all = lax.all_gather(small_local, "fsdp", axis=0, tiled=True)
-    qkv_all = lax.all_gather(qkv_local, "fsdp", axis=0, tiled=True)
-    out_all = lax.all_gather(out_local, "fsdp", axis=0, tiled=True)
+    weights_all = lax.all_gather(weights_local, "fsdp", axis=0, tiled=True)
+    qkv_all = weights_all[:, : width_q + 2 * width_k]
+    out_all = weights_all[:, width_q + 2 * width_k :]
     router_all = small_all[:, :experts_all]
     attn_all = small_all[:, experts_all].astype(full)
     moe_all = small_all[:, experts_all + 1].astype(full)
-    routes_all = lax.all_gather(routes.T, both, axis=0)
-    g_all = lax.all_gather(cotangent, both, axis=0)
+    g_parts = gather_quarters(cotangent)
 
     sequence_in = sequence(tokens).astype(full)
     low_in = rms_scale(sequence_in, attn_all).astype(low)
@@ -756,41 +786,45 @@
     named = routes[:, :, None] == jnp.arange(experts_all, dtype=jnp.int32)[None, None, :]
     selected = jnp.sum(jnp.where(named, logits[:, None, :], 0.0), axis=2)
     gates = gating(selected)
-    gates_all = lax.all_gather(gates.T, both, axis=0)
-
-    steps = jnp.arange(fsdp, dtype=jnp.int32)
+    chosen = jnp.any(named, axis=1)
+    gates_wide = jnp.sum(jnp.where(named, gates[:, :, None], 0.0), axis=1)
+    gates_sent = jnp.where(chosen, gates_wide, -1.0).T
+    gates_all = lax.all_to_all(gates_sent, both, split_axis=0, concat_axis=0, tiled=True)
+
     lines = fsdp // 4
-    order = jnp.stack(
-        [
-            (steps % lines) * 2 + (side + steps // (2 * lines)) % 2,
-            (rank + steps // lines) % 2,
-        ],
-        axis=1,
-    ).reshape(-1)
-    who = jnp.stack([spot * 2 + rank, core]).astype(jnp.int32)
     grid_of = (fsdp // 2, 2, 2)
-    keep_out, send_out, keep_back, send_back, gate_back, rows, grad_rows, hidden, grad_pair = run_expert(
-        who,
-        order.astype(jnp.int32),
-        m_all.reshape(*grid_of, rows_dev, width),
-        g_all.reshape(*grid_of, rows_dev, width),
-        routes_all.reshape(*grid_of, top_k, rows_dev),
-        gates_all.reshape(*grid_of, top_k, rows_dev),
-        expert_gate_up[0],
-        expert_down[0],
-        capacity,
-    )
-    parts = (2, 2, lines, rows_dev, width)
+    lines_at = (place - jnp.arange(lines, dtype=jnp.int32)) % lines
+    kept, summed_back, summed_out = None, {}, {}
+    for number, (d_side, d_ctx) in enumerate(((1, 1), (0, 1), (1, 0), (0, 0))):
+        order = jnp.stack(
+            [lines_at * 2 + (side + d_side) % 2, jnp.broadcast_to((rank + d_ctx) % 2, (lines,))], axis=1
+        ).reshape(-1)
+        keep_out, send_out, keep_back, send_back, *kept = run_expert(
+            core[None].astype(jnp.int32),
+            order.astype(jnp.int32),
+            number,
+            4,
+            m_all.reshape(*grid_of, rows_dev, width),
+            g_parts[d_side, d_ctx, 0],
+            g_parts[d_side, d_ctx, 1],
+            gates_all.reshape(*grid_of, 1, rows_dev),
+            expert_gate_up[0],
+            expert_down[0],
+            capacity,
+            kept,
+        )
+        summed_back[d_side, d_ctx] = (keep_back, send_back)
+        summed_out[d_side, d_ctx] = (keep_out, send_out)
+    gate_back, rows, grad_rows, hidden, grad_pair = kept
     grad_gates = lax.all_to_all(
         gate_back.reshape(fsdp * 2, rows_dev), both, split_axis=0, concat_axis=0, tiled=True
     ).T
-    grad_mid = sum_rows(keep_back.reshape(parts), send_back.reshape(parts), place)
+    grad_mid = sum_quarters(summed_back, place)
     grad_down = mul(hidden, grad_rows, lhs_turned)[None]
     grad_gate_up = mul(rows, grad_pair, lhs_turned)[None]
-    output = (mixed + sum_rows(keep_out.reshape(parts), send_out.reshape(parts), place)).astype(low)
-
-    gates_wide = jnp.sum(jnp.where(named, gates[:, :, None], 0.0), axis=1)
-    chosen = jnp.any(named, axis=1)
+    summed_out, grad_mid = lax.optimization_barrier((summed_out, grad_mid))
+    output = (mixed + sum_quarters(summed_out, place)).astype(low)
+
     grad_wide = jnp.where(chosen, grad_gates, 0.0)
     grad_logits = (
         gates_wide * (grad_wide - jnp.sum(gates_wide * grad_wide, axis=1, keepdims=True))

time: 1510 us -> 1700 us (1.13)
  waiting for transfers between devices: 660 us -> 932 us
  blocking collectives: 170 us -> 23.1 us
  starting transfers between devices: 165 us -> 248 us
  Pallas kernels: 175 us -> 197 us
  local copies, waits for them, and re-layouts: 67.5 us -> 46.5 us
    ppermute x12 -> x16, waiting for transfers between devices: 100 us -> 369 us  [swap_ctx(): return lax.ppermute(values, 'ctx', [(0, 1), (1, 0)])]
    all_gather x1, waiting for transfers between devices: 196 us -> 0.01 us  [body_gathered(): m_all = lax.all_gather(low_mid, both, axis=0)]
    ppermute x8 -> x11, waiting for transfers between devices: 76.1 us -> 242 us  [swap_side(): return lax.ppermute(values, 'fsdp', side_pairs(lax.axis_size('fsdp')))]
    all_gather x2 -> x0, blocking collectives: 148 us -> none  [the longest x1 74 us: body_gathered(): routes_all = lax.all_gather(routes.T, both, axis=0)]
    ppermute x0 -> x6, waiting for transfers between devices: none -> 112 us  [the longest x3 86.5 us: gather_line(): lax.ppermute(ups[-1], 'fsdp', [(i, i + 4) for i in range(fsdp - 4)])]
    all_gather x3 -> x1, waiting for transfers between devices: 135 us -> 81.6 us  [body_gathered(): weights_all = lax.all_gather(weights_local, 'fsdp', axis=0, tiled=True)]
    ppermute x0 -> x6, starting transfers between devices: none -> 43.3 us  [the longest x3 38.9 us: gather_line(): lax.ppermute(ups[-1], 'fsdp', [(i, i + 4) for i in range(fsdp - 4)])]
    squeeze x8 -> x0, local copies, waits for them, and re-layouts: 26.4 us -> none  [the longest x2 8.08 us: sum_rows(): two = add_low(two[0], swap_side(two[1]))]
  transfers between devices with their start and end apart: 85 -> 107, of which waited for: 30 -> 44; matrix products, arithmetic and copies ran while one was open for 18% -> 11% of each run, Pallas kernels for 3% -> 9%
where the time goes in v2:
time: 1700 us; the launch traced here: 1680 us
  waiting for transfers between devices  932 us (55%)
  starting transfers between devices  248 us (15%)
  Pallas kernels  197 us (12%)
  matrix products  113 us (7%)
  other arithmetic  109 us (6%)
  local copies, waits for them, and re-layouts  46.5 us (3%)
  blocking collectives  23.1 us (1%)
    ppermute x16, waiting for transfers between devices, swap_ctx(): return lax.ppermute(values, 'ctx', [(0, 1), (1, 0)])  369 us
    ppermute x11, waiting for transfers between devices, swap_side(): return lax.ppermute(values, 'fsdp', side_pairs(lax.axis_size('fsdp')))  242 us
    pallas_call x4, Pallas kernels, run_expert(): pl.pallas_call(expert_kernel, grid_spec=grid_spec, out_shape=[shape((step...  154 us
    ppermute x24, starting transfers between devices, line_sum(): up = lax.ppermute(send_up, 'fsdp', pairs_up)  125 us
    dot_general x11, matrix products, mul(): return lax.dot_general(left, right, dims, preferred_element_type=full)  113 us
    ppermute x3, waiting for transfers between devices, gather_line(): lax.ppermute(ups[-1], 'fsdp', [(i, i + 4) for i in range(fsdp - 4)])  86.5 us
    all_gather x1, waiting for transfers between devices, body_gathered(): weights_all = lax.all_gather(weights_local, 'fsdp', axis=0, tiled=True)  81.6 us
    ppermute x24, waiting for transfers between devices, line_sum(): up = lax.ppermute(send_up, 'fsdp', pairs_up)  77.4 us
  transfers between devices with their start and end apart: 107, of which 44 were waited for; matrix products, arithmetic and copies ran while one was open for 11% of the time, Pallas kernels for 9%

profile of v2, /device:TPU:0, one launch (start us, length us, event | category | flops | bytes accessed | tf_op | source)
XLA Modules:
  0.0 1684.4 jit_solution(17577084577257080984)
XLA Ops:
  17.5 23.1 %all_gather.12 = bf16[2048,34]{0,1:T(8,128)(2,1)S(1)} all-gather(bf16[128,34]{0,1:T(8,128)(2,1)S(1)} %pad_maximum_fusion.14), channel_id=1, replica_groups=mesh['fsdp'=16,'ctx'=2] {'fsdp'}, dimensions={0}, use_global_device_ids=true | all-gather | bytes 147968 | tf_op jit(solution)/shard_map/all_gather | solution.py:757
  44.2 81.6 %all-gather.4.cloned.1.call-done = bf16[2048,5120]{1,0:T(8,128)(2,1)} async-done(((bf16[128,5120]{1,0:T(8,128)(2,1)}), bf16[2048,5120]{1,0:T(8,128)(2,1)}) %all-gather.4.cloned.1.call-update) | async-done | bytes 20971536 | tf_op jit(solution)/shard_map/all_gather | solution.py:758
  125.8 11.7 fusion.3.q_ref.k_ref.v_ref
  137.5 18.3 %attend.1 = (bf16[512,2048]{1,0:T(8,128)(2,1)S(1)}, bf16[512,2048]{1,0:T(8,128)(2,1)S(1)}, bf16[512,512]{1,0:T(8,128)(2,1)S(1)}, bf16[512,512]{1,0:T(8,128)(2,1)S(1)}) custom-call(f32[512,3072]{1,0:T(8,128)} %fusion.3.q_ref.k_ref.v_ref, f32[512,3072]{1,0:T(8,128)} %fusion.3.q_ref.k_ref.v_ref, f32[512,3072]{1,0:T(8,128)} %fusion.3.q_ref.k_ref.v_ref, ...), custom_call_target="tpu_custom_call" | custom-call | flops 2147483648 | bytes 9437184 | tf_op jit(solution)/shard_map/attend/pallas_call | solution.py:552
  155.8 8.7 fusion.8
  166.6 23.9 %collective-permute-done.1 = bf16[256,2048]{1,0:T(8,128)(2,1)S(1)} collective-permute-done((bf16[256,2048]{1,0:T(8,128)(2,1)S(1)}, bf16[256,2048]{1,0:T(8,128)(2,1)S(1)}, u32[]{:S(2)}, u32[]{:S(2)}) %collective-permute-start.1) | collective-permute-done | bytes 1048608 | tf_op jit(solution)/shard_map/ppermute | solution.py:341
  198.7 36.8 %collective-permute-done.2 = bf16[256,2048]{1,0:T(8,128)(2,1)S(1)} collective-permute-done((bf16[256,2048]{1,0:T(8,128)(2,1)S(1)}, bf16[256,2048]{1,0:T(8,128)(2,1)S(1)}, u32[]{:S(2)}, u32[]{:S(2)}) %collective-permute-start.2) | collective-permute-done | bytes 1048608 | tf_op jit(solution)/shard_map/ppermute | solution.py:405
  235.5 9.7 collective-permute-start.6
  247.2 34.3 %collective-permute-done.6 = bf16[256,2048]{1,0:T(8,128)(2,1)S(1)} collective-permute-done((bf16[256,2048]{1,0:T(8,128)(2,1)S(1)}, bf16[256,2048]{1,0:T(8,128)(2,1)S(1)}, u32[]{:S(2)}, u32[]{:S(2)}) %collective-permute-start.6) | collective-permute-done | bytes 1048608 | tf_op jit(solution)/shard_map/ppermute | solution.py:405
  281.5 26.4 %collective-permute-start.7 = (bf16[256,2048]{1,0:T(8,128)(2,1)S(1)}, bf16[256,2048]{1,0:T(8,128)(2,1)S(1)}, u32[]{:S(2)}, u32[]{:S(2)}) collective-permute-start(bf16[256,2048]{1,0:T(8,128)(2,1)S(1)} %collective-permute-done.6), channel_id=1, source_target_pairs={{0,8},{2,10},{4,12},{6,14},{8,16},{10,18},{12,20},{14,22},{16,24},... | collective-permute-start | bytes 3145736 | tf_op jit(solution)/shard_map/ppermute | solution.py:405
  316.2 15.4 collective-permute-done.7
  331.8 18.7 %collective-permute-done.5 = bf16[256,2048]{1,0:T(8,128)(2,1)S(1)} collective-permute-done((bf16[256,2048]{1,0:T(8,128)(2,1)S(1)}, bf16[256,2048]{1,0:T(8,128)(2,1)S(1)}, u32[]{:S(2)}, u32[]{:S(2)}) %collective-permute-start.5) | collective-permute-done | bytes 1048608 | tf_op jit(solution)/shard_map/ppermute | solution.py:406
  352.6 132.4 %collective-permute-done.9.g_keep = bf16[4,256,2048]{2,1,0:T(8,128)(2,1)S(1)} collective-permute-done((bf16[4,256,2048]{2,1,0:T(8,128)(2,1)S(1)}, bf16[4,256,2048]{2,1,0:T(8,128)(2,1)S(1)}, u32[]{:S(2)}, u32[]{:S(2)}) %collective-permute-start.9) | collective-permute-done | bytes 4194336 | tf_op jit(solution)/shard_map/ppermute | solution.py:337
  487.1 91.6 %collective-permute-done.13.g_keep = bf16[4,256,2048]{2,1,0:T(8,128)(2,1)} collective-permute-done((bf16[4,256,2048]{2,1,0:T(8,128)(2,1)S(1)}, bf16[4,256,2048]{2,1,0:T(8,128)(2,1)}, u32[]{:S(2)}, u32[]{:S(2)}) %collective-permute-start.13) | collective-permute-done | bytes 4194336 | tf_op jit(solution)/shard_map/ppermute | solution.py:341
  578.7 83.5 %collective-permute-done.11.g_keep = bf16[4,256,2048]{2,1,0:T(8,128)(2,1)} collective-permute-done((bf16[4,256,2048]{2,1,0:T(8,128)(2,1)S(1)}, bf16[4,256,2048]{2,1,0:T(8,128)(2,1)}, u32[]{:S(2)}, u32[]{:S(2)}) %collective-permute-start.11) | collective-permute-done | bytes 4194336 | tf_op jit(solution)/shard_map/ppermute | solution.py:341
  678.6 37.8 %experts.4 = (bf16[4,256,2048]{2,1,0:T(8,128)(2,1)}, bf16[4,256,2048]{2,1,0:T(8,128)(2,1)}, bf16[4,256,2048]{2,1,0:T(8,128)(2,1)}, bf16[4,256,2048]{2,1,0:T(8,12...) custom-call(s32[1]{0:T(128)} %bitcast.5.core_ref, ...), custom_call_target="tpu_custom_call" | custom-call | flops 23622320128 | bytes 46661632 | tf_op jit(solution)/shard_map/experts/pallas_call | solution.py:688
  716.5 38.4 %experts.5 = (bf16[4,256,2048]{2,1,0:T(8,128)(2,1)}, bf16[4,256,2048]{2,1,0:T(8,128)(2,1)}, bf16[4,256,2048]{2,1,0:T(8,128)(2,1)}, bf16[4,256,2048]{2,1,0:T(8,12...) custom-call(s32[1]{0:T(128)} %bitcast.5.core_ref, ...), custom_call_target="tpu_custom_call", output_to_operand_aliasing={{4}: (8, {}), {5}: (9, {}), {6}: (10, {}), {7}: (11, {}), {... | custom-call | flops 23622320128 | bytes 46661632 | tf_op jit(solution)/shard_map/experts/pallas_call | solution.py:688
  755.4 38.7 %experts.6 = (bf16[4,256,2048]{2,1,0:T(8,128)(2,1)}, bf16[4,256,2048]{2,1,0:T(8,128)(2,1)}, bf16[4,256,2048]{2,1,0:T(8,128)(2,1)}, bf16[4,256,2048]{2,1,0:T(8,12...) custom-call(s32[1]{0:T(128)} %bitcast.5.core_ref, ...), custom_call_target="tpu_custom_call", output_to_operand_aliasing={{4}: (8, {}), {5}: (9, {}), {6}: (10, {}), {7}: (11, {}), {... | custom-call | flops 23622320128 | bytes 46661632 | tf_op jit(solution)/shard_map/experts/pallas_call | solution.py:688
  800.3 38.6 %experts.7 = (bf16[4,256,2048]{2,1,0:T(8,128)(2,1)}, bf16[4,256,2048]{2,1,0:T(8,128)(2,1)}, bf16[4,256,2048]{2,1,0:T(8,128)(2,1)}, bf16[4,256,2048]{2,1,0:T(8,12...) custom-call(s32[1]{0:T(128)} %bitcast.5.core_ref, ...), custom_call_target="tpu_custom_call", output_to_operand_aliasing={{4}: (8, {}), {5}: (9, {}), {6}: (10, {}), {7}: (11, {}), {... | custom-call | flops 23622320128 | bytes 46661632 | tf_op jit(solution)/shard_map/experts/pallas_call | solution.py:688
  839.0 8.7 collective-permute-done.29
  863.3 39.0 %collective-permute-done.17 = bf16[4,256,1024]{2,1,0:T(8,128)(2,1)S(1)} collective-permute-done((bf16[4,256,1024]{2,1,0:T(8,128)(2,1)}, bf16[4,256,1024]{2,1,0:T(8,128)(2,1)S(1)}, u32[]{:S(2)}, u32[]{:S(2)}) %collective-permute-start.17) | collective-permute-done | bytes 2097184 | tf_op jit(solution)/shard_map/ppermute | solution.py:341
  902.3 43.4 %collective-permute-done.30 = bf16[4,256,1024]{2,1,0:T(8,128)(2,1)} collective-permute-done((bf16[4,256,1024]{2,1,0:T(8,128)(2,1)}, bf16[4,256,1024]{2,1,0:T(8,128)(2,1)}, u32[]{:S(2)}, u32[]{:S(2)}) %collective-permute-start.30) | collective-permute-done | bytes 2097184 | tf_op jit(solution)/shard_map/ppermute | solution.py:341
  945.7 7.2 collective-permute-done.28
  952.9 7.8 add_convert_fusion.21
  965.2 13.3 collective-permute-start.31
  1035.3 6.9 collective-permute-done.36
  1045.8 11.9 collective-permute-done.41
  1061.8 45.7 %collective-permute-done.42 = bf16[4,256,1024]{2,1,0:T(8,128)(2,1)S(1)} collective-permute-done((bf16[4,256,1024]{2,1,0:T(8,128)(2,1)S(1)}, bf16[4,256,1024]{2,1,0:T(8,128)(2,1)S(1)}, u32[]{:S(2)}, u32[]{:S(2)}) %collective-permute-start.42) | collective-permute-done | bytes 2097184 | tf_op jit(solution)/shard_map/ppermute | solution.py:341
  1116.7 41.9 %collective-permute-done.43 = bf16[4,256,1024]{2,1,0:T(8,128)(2,1)S(1)} collective-permute-done((bf16[4,256,1024]{2,1,0:T(8,128)(2,1)S(1)}, bf16[4,256,1024]{2,1,0:T(8,128)(2,1)S(1)}, u32[]{:S(2)}, u32[]{:S(2)}) %collective-permute-start.43) | collective-permute-done | bytes 2097184 | tf_op jit(solution)/shard_map/ppermute | solution.py:337
  1158.6 43.2 %collective-permute-done.50 = bf16[4,256,1024]{2,1,0:T(8,128)(2,1)S(1)} collective-permute-done((bf16[4,256,1024]{2,1,0:T(8,128)(2,1)S(1)}, bf16[4,256,1024]{2,1,0:T(8,128)(2,1)S(1)}, u32[]{:S(2)}, u32[]{:S(2)}) %collective-permute-start.50) | collective-permute-done | bytes 2097184 | tf_op jit(solution)/shard_map/ppermute | solution.py:337
  1211.1 9.3 collective-permute-start.44
  1224.1 8.6 collective-permute-done.44
  1284.8 8.3 collective-permute-done.49
  1307.2 19.7 %collective-permute-done.59 = bf16[256,2048]{1,0:T(8,128)(2,1)S(1)} collective-permute-done((bf16[256,2048]{1,0:T(8,128)(2,1)}, bf16[256,2048]{1,0:T(8,128)(2,1)S(1)}, u32[]{:S(2)}, u32[]{:S(2)}) %collective-permute-start.59) | collective-permute-done | bytes 1048608 | tf_op jit(solution)/shard_map/ppermute | solution.py:341
  1329.9 7.3 convolution_convert_fusion.1
  1337.2 9.3 fusion.14.go_ref
  1346.5 25.1 %attend_grad.1 = (bf16[512,2048]{1,0:T(8,128)(2,1)S(1)}, bf16[512,512]{1,0:T(8,128)(2,1)S(1)}, bf16[512,512]{1,0:T(8,128)(2,1)S(1)}, f32[4,1,128]{2,1,0:T(1,128)S(1)}, f32[4,1,128]{2,1,0:T(1,128)S(1)}) custom-call(f32[512,3072]{1,0:T(8,128)} %fusion.3.q_ref.k_ref.v_ref, f32[512,3072]{1,0:T(8,128)} %fusion.3.q_ref.k_ref.v_ref, bf16[512,2048]{1,0:T(8,128)(2,1)} %copy-done.10, ...), custom_call_target="tpu_custom_call" | custom-call | flops 5368709120 | bytes 15728640 | tf_op jit(solution)/shard_map/attend_grad/pallas_call | solution.py:576
  1377.3 9.9 fusion.1
  1390.0 10.0 convolution_convert_fusion
  1400.1 13.0 collective-permute-done.99
  1415.6 6.5 dynamic-slice_bitcast_fusion
  1422.6 8.1 collective-permute-start.101
  1442.0 33.0 %convolution_bitcast_fusion = f32[1,2048,1536]{2,1,0:T(8,128)} fusion(bf16[4096,2048]{1,0:T(8,128)(2,1)S(1)} %bitcast.272, bf16[4096,1536]{1,0:T(8,128)(2,1)} %get-tuple-element.116), kind=kOutput, calls=%fused_computation.7 | convolution fusion | flops 25769803776 | bytes 41943040 | tf_op jit(solution)/shard_map/dot_general | solution.py:321
  1486.7 19.2 %convolution_bitcast_fusion.1 = f32[1,768,2048]{2,1,0:T(8,128)} fusion(bf16[4096,768]{1,0:T(8,128)(2,1)S(1)} %bitcast.278, bf16[4096,2048]{1,0:T(8,128)(2,1)} %get-tuple-element.118), kind=kOutput, calls=%fused_computation.51 | convolution fusion | flops 12884901888 | bytes 29360128 | tf_op jit(solution)/shard_map/dot_general | solution.py:321
  1516.9 10.3 fusion
  1538.6 17.8 %collective-permute-done.80 = bf16[128,1024]{1,0:T(8,128)(2,1)S(1)} collective-permute-done((bf16[128,1024]{1,0:T(8,128)(2,1)S(1)}, bf16[128,1024]{1,0:T(8,128)(2,1)S(1)}, u32[]{:S(2)}, u32[]{:S(2)}) %collective-permute-start.80) | collective-permute-done | bytes 262176 | tf_op jit(solution)/shard_map/ppermute | solution.py:377
  1573.2 19.7 %collective-permute-done.63 = bf16[128,1536]{1,0:T(8,128)(2,1)S(1)} collective-permute-done((bf16[128,1536]{1,0:T(8,128)(2,1)S(1)}, bf16[128,1536]{1,0:T(8,128)(2,1)S(1)}, u32[]{:S(2)}, u32[]{:S(2)}) %collective-permute-start.63) | collective-permute-done | bytes 393248 | tf_op jit(solution)/shard_map/ppermute | solution.py:377
  1610.8 34.2 %collective-permute-start.65 = (bf16[128,1536]{1,0:T(8,128)(2,1)S(1)}, bf16[128,1536]{1,0:T(8,128)(2,1)S(1)}, u32[]{:S(2)}, u32[]{:S(2)}) collective-permute-start(bf16[128,1536]{1,0:T(8,128)(2,1)S(1)} %get-tuple-element.181), channel_id=1, source_target_pairs={{0,8},{2,10},{4,12},{6,14},{8,16},{10,18},{12,20},{14,22},{16,24},... | collective-permute-start | bytes 1179656 | tf_op jit(solution)/shard_map/ppermute | solution.py:377
  (505 shorter events, 359.8 us)
Async XLA Ops:
  7.2 118.6 %all-gather.4.cloned.1.call-start = ((), (), s32[]{:S(2)}) async-start(), calls=%async_computation.2 | async-start | bytes 22282240 | tf_op jit(solution)/shard_map/all_gather | solution.py:758
  13.1 664.9 %all-gather.6.cloned.1.call-start = ((), (), s32[]{:S(2)}) async-start(), calls=%async_computation.3 | async-start | bytes 34603008 | tf_op jit(solution)/shard_map/all_gather | solution.py:783
  194.5 41.0 %collective-permute-start.2 = (bf16[256,2048]{1,0:T(8,128)(2,1)S(1)}, bf16[256,2048]{1,0:T(8,128)(2,1)S(1)}, u32[]{:S(2)}, u32[]{:S(2)}) collective-permute-start(bf16[256,2048]{1,0:T(8,128)(2,1)S(1)} %copy-done.43), channel_id=1, source_target_pairs={{0,8},{2,10},{4,12},{6,14},{8,16},{10,18},{12,20},{14,22},{16,24},... | collective-permute-start | bytes 3145736 | tf_op jit(solution)/shard_map/ppermute | solution.py:405
  197.4 48.6 %collective-permute-start.3 = (bf16[256,2048]{1,0:T(8,128)(2,1)S(1)}, bf16[256,2048]{1,0:T(8,128)(2,1)S(1)}, u32[]{:S(2)}, u32[]{:S(2)}) collective-permute-start(bf16[256,2048]{1,0:T(8,128)(2,1)S(1)} %copy-done.43), channel_id=1, source_target_pairs={{8,0},{10,2},{12,4},{14,6},{16,8},{18,10},{20,12},{22,14},{24,16},... | collective-permute-start | bytes 3145736 | tf_op jit(solution)/shard_map/ppermute | solution.py:406
  235.5 46.0 %collective-permute-start.6 = (bf16[256,2048]{1,0:T(8,128)(2,1)S(1)}, bf16[256,2048]{1,0:T(8,128)(2,1)S(1)}, u32[]{:S(2)}, u32[]{:S(2)}) collective-permute-start(bf16[256,2048]{1,0:T(8,128)(2,1)S(1)} %collective-permute-done.2), channel_id=1, source_target_pairs={{0,8},{2,10},{4,12},{6,14},{8,16},{10,18},{12,20},{14,22},{16,24},... | collective-permute-start | bytes 3145736 | tf_op jit(solution)/shard_map/ppermute | solution.py:405
  245.9 68.4 %collective-permute-start.4 = (bf16[256,2048]{1,0:T(8,128)(2,1)S(1)}, bf16[256,2048]{1,0:T(8,128)(2,1)S(1)}, u32[]{:S(2)}, u32[]{:S(2)}) collective-permute-start(bf16[256,2048]{1,0:T(8,128)(2,1)S(1)} %collective-permute-done.3), channel_id=1, source_target_pairs={{8,0},{10,2},{12,4},{14,6},{16,8},{18,10},{20,12},{22,14},{24,16},... | collective-permute-start | bytes 3145736 | tf_op jit(solution)/shard_map/ppermute | solution.py:406
  281.5 50.2 %collective-permute-start.7 = (bf16[256,2048]{1,0:T(8,128)(2,1)S(1)}, bf16[256,2048]{1,0:T(8,128)(2,1)S(1)}, u32[]{:S(2)}, u32[]{:S(2)}) collective-permute-start(bf16[256,2048]{1,0:T(8,128)(2,1)S(1)} %collective-permute-done.6), channel_id=1, source_target_pairs={{0,8},{2,10},{4,12},{6,14},{8,16},{10,18},{12,20},{14,22},{16,24},... | collective-permute-start | bytes 3145736 | tf_op jit(solution)/shard_map/ppermute | solution.py:405
  314.3 36.2 %collective-permute-start.5 = (bf16[256,2048]{1,0:T(8,128)(2,1)S(1)}, bf16[256,2048]{1,0:T(8,128)(2,1)S(1)}, u32[]{:S(2)}, u32[]{:S(2)}) collective-permute-start(bf16[256,2048]{1,0:T(8,128)(2,1)S(1)} %collective-permute-done.4), channel_id=1, source_target_pairs={{8,0},{10,2},{12,4},{14,6},{16,8},{18,10},{20,12},{22,14},{24,16},... | collective-permute-start | bytes 3145736 | tf_op jit(solution)/shard_map/ppermute | solution.py:406
  351.2 133.8 %collective-permute-start.9 = (bf16[4,256,2048]{2,1,0:T(8,128)(2,1)S(1)}, bf16[4,256,2048]{2,1,0:T(8,128)(2,1)S(1)}, u32[]{:S(2)}, u32[]{:S(2)}) collective-permute-start(bf16[4,256,2048]{2,1,0:T(8,128)(2,1)S(1)} %pad_maximum_fusion.g_keep), channel_id=1, source_target_pairs={{0,4},{2,6},{4,0},{6,2},{8,12},{10,14},{12,8},{14,10},{16,20},{18,... | collective-permute-start | bytes 12582920 | tf_op jit(solution)/shard_map/ppermute | solution.py:337
  485.1 93.6 %collective-permute-start.13 = (bf16[4,256,2048]{2,1,0:T(8,128)(2,1)S(1)}, bf16[4,256,2048]{2,1,0:T(8,128)(2,1)}, u32[]{:S(2)}, u32[]{:S(2)}) collective-permute-start(bf16[4,256,2048]{2,1,0:T(8,128)(2,1)S(1)} %collective-permute-done.9.g_keep), channel_id=1, source_target_pairs={{0,1},{1,0},{2,3},{3,2},{4,5},{5,4},{6,7},{7,6},{8,9},{9,8},{10,11... | collective-permute-start | bytes 12582920 | tf_op jit(solution)/shard_map/ppermute | solution.py:341
  486.5 175.7 %collective-permute-start.11 = (bf16[4,256,2048]{2,1,0:T(8,128)(2,1)S(1)}, bf16[4,256,2048]{2,1,0:T(8,128)(2,1)}, u32[]{:S(2)}, u32[]{:S(2)}) collective-permute-start(bf16[4,256,2048]{2,1,0:T(8,128)(2,1)S(1)} %pad_maximum_fusion.g_keep), channel_id=1, source_target_pairs={{0,1},{1,0},{2,3},{3,2},{4,5},{5,4},{6,7},{7,6},{8,9},{9,8},{10,11... | collective-permute-start | bytes 12582920 | tf_op jit(solution)/shard_map/ppermute | solution.py:341
  578.7 93.8 %collective-permute-start.14 = (bf16[4,256,2048]{2,1,0:T(8,128)(2,1)}, bf16[4,256,2048]{2,1,0:T(8,128)(2,1)}, u32[]{:S(2)}, u32[]{:S(2)}) collective-permute-start(bf16[4,256,2048]{2,1,0:T(8,128)(2,1)} %collective-permute-done.13.g_keep), channel_id=1, source_target_pairs={{0,2},{2,0},{4,6},{6,4},{8,10},{10,8},{12,14},{14,12},{16,18},{18,... | collective-permute-start | bytes 12582920 | tf_op jit(solution)/shard_map/ppermute | solution.py:333
  662.2 54.3 %collective-permute-start.12 = (bf16[4,256,2048]{2,1,0:T(8,128)(2,1)}, bf16[4,256,2048]{2,1,0:T(8,128)(2,1)}, u32[]{:S(2)}, u32[]{:S(2)}) collective-permute-start(bf16[4,256,2048]{2,1,0:T(8,128)(2,1)} %collective-permute-done.11.g_keep), channel_id=1, source_target_pairs={{0,2},{2,0},{4,6},{6,4},{8,10},{10,8},{12,14},{14,12},{16,18},{18,... | collective-permute-start | bytes 12582920 | tf_op jit(solution)/shard_map/ppermute | solution.py:333
  671.9 128.3 %collective-permute-start.8 = (bf16[4,256,2048]{2,1,0:T(8,128)(2,1)}, bf16[4,256,2048]{2,1,0:T(8,128)(2,1)}, u32[]{:S(2)}, u32[]{:S(2)}) collective-permute-start(bf16[4,256,2048]{2,1,0:T(8,128)(2,1)} %copy-done.22), channel_id=1, source_target_pairs={{0,2},{2,0},{4,6},{6,4},{8,10},{10,8},{12,14},{14,12},{16,18},{18,... | collective-permute-start | bytes 12582920 | tf_op jit(solution)/shard_map/ppermute | solution.py:333
  672.2 83.3 %collective-permute-start.10 = (bf16[4,256,2048]{2,1,0:T(8,128)(2,1)}, bf16[4,256,2048]{2,1,0:T(8,128)(2,1)}, u32[]{:S(2)}, u32[]{:S(2)}) collective-permute-start(bf16[4,256,2048]{2,1,0:T(8,128)(2,1)} %copy-done.37), channel_id=1, source_target_pairs={{0,2},{2,0},{4,6},{6,4},{8,10},{10,8},{12,14},{14,12},{16,18},{18,... | collective-permute-start | bytes 12582920 | tf_op jit(solution)/shard_map/ppermute | solution.py:333
  716.4 77.9 %collective-permute-start.19 = (bf16[4,256,2048]{2,1,0:T(8,128)(2,1)}, bf16[4,256,2048]{2,1,0:T(8,128)(2,1)}, u32[]{:S(2)}, u32[]{:S(2)}) collective-permute-start(bf16[4,256,2048]{2,1,0:T(8,128)(2,1)} %get-tuple-element.96), channel_id=1, source_target_pairs={{0,2},{2,0},{4,6},{6,4},{8,10},{10,8},{12,14},{14,12},{16,18},{18,... | collective-permute-start | bytes 12582920 | tf_op jit(solution)/shard_map/ppermute | solution.py:333
  754.9 84.1 %collective-permute-start.16 = (bf16[4,256,2048]{2,1,0:T(8,128)(2,1)}, bf16[4,256,2048]{2,1,0:T(8,128)(2,1)}, u32[]{:S(2)}, u32[]{:S(2)}) collective-permute-start(bf16[4,256,2048]{2,1,0:T(8,128)(2,1)} %get-tuple-element.92), channel_id=1, source_target_pairs={{0,2},{2,0},{4,6},{6,4},{8,10},{10,8},{12,14},{14,12},{16,18},{18,... | collective-permute-start | bytes 12582920 | tf_op jit(solution)/shard_map/ppermute | solution.py:333
  794.2 61.4 %collective-permute-start.18 = (bf16[4,256,2048]{2,1,0:T(8,128)(2,1)}, bf16[4,256,2048]{2,1,0:T(8,128)(2,1)}, u32[]{:S(2)}, u32[]{:S(2)}) collective-permute-start(bf16[4,256,2048]{2,1,0:T(8,128)(2,1)} %get-tuple-element.94), channel_id=1, source_target_pairs={{0,2},{2,0},{4,6},{6,4},{8,10},{10,8},{12,14},{14,12},{16,18},{18,... | collective-permute-start | bytes 12582920 | tf_op jit(solution)/shard_map/ppermute | solution.py:333
  799.1 56.4 %collective-permute-start.20 = (bf16[4,256,1024]{2,1,0:T(8,128)(2,1)}, bf16[4,256,1024]{2,1,0:T(8,128)(2,1)}, u32[]{:S(2)}, u32[]{:S(2)}) collective-permute-start(bf16[4,256,1024]{2,1,0:T(8,128)(2,1)} %get-tuple-element.142), channel_id=1, source_target_pairs={{0,1},{1,0},{2,3},{3,2},{4,5},{5,4},{6,7},{7,6},{8,9},{9,8},{10,11... | collective-permute-start | bytes 6291464 | tf_op jit(solution)/shard_map/ppermute | solution.py:341
  799.6 48.0 %collective-permute-start.29 = (bf16[4,256,1024]{2,1,0:T(8,128)(2,1)}, bf16[4,256,1024]{2,1,0:T(8,128)(2,1)}, u32[]{:S(2)}, u32[]{:S(2)}) collective-permute-start(bf16[4,256,1024]{2,1,0:T(8,128)(2,1)} %get-tuple-element.143), channel_id=1, source_target_pairs={{0,4},{2,6},{4,0},{6,2},{8,12},{10,14},{12,8},{14,10},{16,20},{18,... | collective-permute-start | bytes 6291464 | tf_op jit(solution)/shard_map/ppermute | solution.py:337
  853.5 48.8 %collective-permute-start.17 = (bf16[4,256,1024]{2,1,0:T(8,128)(2,1)}, bf16[4,256,1024]{2,1,0:T(8,128)(2,1)S(1)}, u32[]{:S(2)}, u32[]{:S(2)}) collective-permute-start(bf16[4,256,1024]{2,1,0:T(8,128)(2,1)} %get-tuple-element.138), channel_id=1, source_target_pairs={{0,1},{1,0},{2,3},{3,2},{4,5},{5,4},{6,7},{7,6},{8,9},{9,8},{10,11... | collective-permute-start | bytes 6291464 | tf_op jit(solution)/shard_map/ppermute | solution.py:341
  855.0 90.6 %collective-permute-start.30 = (bf16[4,256,1024]{2,1,0:T(8,128)(2,1)}, bf16[4,256,1024]{2,1,0:T(8,128)(2,1)}, u32[]{:S(2)}, u32[]{:S(2)}) collective-permute-start(bf16[4,256,1024]{2,1,0:T(8,128)(2,1)} %get-tuple-element.139), channel_id=1, source_target_pairs={{0,1},{1,0},{2,3},{3,2},{4,5},{5,4},{6,7},{7,6},{8,9},{9,8},{10,11... | collective-permute-start | bytes 6291464 | tf_op jit(solution)/shard_map/ppermute | solution.py:341
  861.2 84.4 %collective-permute-start.21 = (bf16[4,256,1024]{2,1,0:T(8,128)(2,1)}, bf16[4,256,1024]{2,1,0:T(8,128)(2,1)}, u32[]{:S(2)}, u32[]{:S(2)}) collective-permute-start(bf16[4,256,1024]{2,1,0:T(8,128)(2,1)} %get-tuple-element.140), channel_id=1, source_target_pairs={{0,4},{2,6},{4,0},{6,2},{8,12},{10,14},{12,8},{14,10},{16,20},{18,... | collective-permute-start | bytes 6291464 | tf_op jit(solution)/shard_map/ppermute | solution.py:337
  861.9 91.0 %collective-permute-start.28 = (bf16[4,256,1024]{2,1,0:T(8,128)(2,1)}, bf16[4,256,1024]{2,1,0:T(8,128)(2,1)}, u32[]{:S(2)}, u32[]{:S(2)}) collective-permute-start(bf16[4,256,1024]{2,1,0:T(8,128)(2,1)} %get-tuple-element.141), channel_id=1, source_target_pairs={{0,4},{2,6},{4,0},{6,2},{8,12},{10,14},{12,8},{14,10},{16,20},{18,... | collective-permute-start | bytes 6291464 | tf_op jit(solution)/shard_map/ppermute | solution.py:337
  1045.7 66.3 %collective-permute-start.38 = (bf16[4,256,2048]{2,1,0:T(8,128)(2,1)}, bf16[4,256,2048]{2,1,0:T(8,128)(2,1)S(1)}, u32[]{:S(2)}, u32[]{:S(2)}) collective-permute-start(bf16[4,256,2048]{2,1,0:T(8,128)(2,1)} %get-tuple-element.100), channel_id=1, source_target_pairs={{0,2},{2,0},{4,6},{6,4},{8,10},{10,8},{12,14},{14,12},{16,18},{18,... | collective-permute-start | bytes 12582920 | tf_op jit(solution)/shard_map/ppermute | solution.py:333
  1059.7 47.7 %collective-permute-start.42 = (bf16[4,256,1024]{2,1,0:T(8,128)(2,1)S(1)}, bf16[4,256,1024]{2,1,0:T(8,128)(2,1)S(1)}, u32[]{:S(2)}, u32[]{:S(2)}) collective-permute-start(bf16[4,256,1024]{2,1,0:T(8,128)(2,1)S(1)} %get-tuple-element.134), channel_id=1, source_target_pairs={{0,1},{1,0},{2,3},{3,2},{4,5},{5,4},{6,7},{7,6},{8,9},{9,8},{10,11... | collective-permute-start | bytes 6291464 | tf_op jit(solution)/shard_map/ppermute | solution.py:341
  1060.7 51.3 %collective-permute-start.51 = (bf16[4,256,1024]{2,1,0:T(8,128)(2,1)S(1)}, bf16[4,256,1024]{2,1,0:T(8,128)(2,1)S(1)}, u32[]{:S(2)}, u32[]{:S(2)}) collective-permute-start(bf16[4,256,1024]{2,1,0:T(8,128)(2,1)S(1)} %get-tuple-element.135), channel_id=1, source_target_pairs={{0,4},{2,6},{4,0},{6,2},{8,12},{10,14},{12,8},{14,10},{16,20},{18,... | collective-permute-start | bytes 6291464 | tf_op jit(solution)/shard_map/ppermute | solution.py:337
  1061.8 54.9 %collective-permute-start.37 = (bf16[4,256,2048]{2,1,0:T(8,128)(2,1)S(1)}, bf16[4,256,2048]{2,1,0:T(8,128)(2,1)S(1)}, u32[]{:S(2)}, u32[]{:S(2)}) collective-permute-start(bf16[4,256,2048]{2,1,0:T(8,128)(2,1)S(1)} %copy-done.74), channel_id=1, source_target_pairs={{0,2},{2,0},{4,6},{6,4},{8,10},{10,8},{12,14},{14,12},{16,18},{18,... | collective-permute-start | bytes 12582920 | tf_op jit(solution)/shard_map/ppermute | solution.py:333
  1109.9 48.6 %collective-permute-start.43 = (bf16[4,256,1024]{2,1,0:T(8,128)(2,1)S(1)}, bf16[4,256,1024]{2,1,0:T(8,128)(2,1)S(1)}, u32[]{:S(2)}, u32[]{:S(2)}) collective-permute-start(bf16[4,256,1024]{2,1,0:T(8,128)(2,1)S(1)} %get-tuple-element.132), channel_id=1, source_target_pairs={{0,4},{2,6},{4,0},{6,2},{8,12},{10,14},{12,8},{14,10},{16,20},{18,... | collective-permute-start | bytes 6291464 | tf_op jit(solution)/shard_map/ppermute | solution.py:337
  1110.6 91.1 %collective-permute-start.50 = (bf16[4,256,1024]{2,1,0:T(8,128)(2,1)S(1)}, bf16[4,256,1024]{2,1,0:T(8,128)(2,1)S(1)}, u32[]{:S(2)}, u32[]{:S(2)}) collective-permute-start(bf16[4,256,1024]{2,1,0:T(8,128)(2,1)S(1)} %get-tuple-element.133), channel_id=1, source_target_pairs={{0,4},{2,6},{4,0},{6,2},{8,12},{10,14},{12,8},{14,10},{16,20},{18,... | collective-permute-start | bytes 6291464 | tf_op jit(solution)/shard_map/ppermute | solution.py:337
  1114.6 87.2 %collective-permute-start.39 = (bf16[4,256,1024]{2,1,0:T(8,128)(2,1)S(1)}, bf16[4,256,1024]{2,1,0:T(8,128)(2,1)S(1)}, u32[]{:S(2)}, u32[]{:S(2)}) collective-permute-start(bf16[4,256,1024]{2,1,0:T(8,128)(2,1)S(1)} %get-tuple-element.130), channel_id=1, source_target_pairs={{0,1},{1,0},{2,3},{3,2},{4,5},{5,4},{6,7},{7,6},{8,9},{9,8},{10,11... | collective-permute-start | bytes 6291464 | tf_op jit(solution)/shard_map/ppermute | solution.py:341
  1115.5 90.3 %collective-permute-start.52 = (bf16[4,256,1024]{2,1,0:T(8,128)(2,1)S(1)}, bf16[4,256,1024]{2,1,0:T(8,128)(2,1)S(1)}, u32[]{:S(2)}, u32[]{:S(2)}) collective-permute-start(bf16[4,256,1024]{2,1,0:T(8,128)(2,1)S(1)} %get-tuple-element.131), channel_id=1, source_target_pairs={{0,1},{1,0},{2,3},{3,2},{4,5},{5,4},{6,7},{7,6},{8,9},{9,8},{10,11... | collective-permute-start | bytes 6291464 | tf_op jit(solution)/shard_map/ppermute | solution.py:341
  1376.7 56.4 %collective-permute-start.77 = (bf16[8,128,2048]{2,1,0:T(8,128)(2,1)}, bf16[8,128,2048]{2,1,0:T(8,128)(2,1)S(1)}, u32[]{:S(2)}, u32[]{:S(2)}) collective-permute-start(bf16[8,128,2048]{2,1,0:T(8,128)(2,1)} %dynamic-slice_bitcast_fusion.1), channel_id=1, source_target_pairs={{0,2},{2,0},{4,6},{6,4},{8,10},{10,8},{12,14},{14,12},{16,18},{18,... | collective-permute-start | bytes 12582920 | tf_op jit(solution)/shard_map/ppermute | solution.py:333
  1422.1 94.8 %collective-permute-start.61 = (bf16[8,128,3072]{2,1,0:T(8,128)(2,1)}, bf16[8,128,3072]{2,1,0:T(8,128)(2,1)}, u32[]{:S(2)}, u32[]{:S(2)}) collective-permute-start(bf16[8,128,3072]{2,1,0:T(8,128)(2,1)} %dynamic-slice_bitcast_fusion), channel_id=1, source_target_pairs={{0,2},{2,0},{4,6},{6,4},{8,10},{10,8},{12,14},{14,12},{16,18},{18,... | collective-permute-start | bytes 18874376 | tf_op jit(solution)/shard_map/ppermute | solution.py:333
  1422.6 52.4 %collective-permute-start.101 = (f32[2,128]{1,0:T(2,128)S(1)}, f32[2,128]{1,0:T(2,128)S(1)}, u32[]{:S(2)}, u32[]{:S(2)}) collective-permute-start(f32[2,128]{1,0:T(2,128)S(1)} %add.779), channel_id=1, source_target_pairs={{0,8},{2,10},{4,12},{6,14},{8,0},{10,2},{12,4},{14,6},{16,24},{18,... | collective-permute-start | bytes 3080 | tf_op jit(solution)/shard_map/ppermute | solution.py:439
  1431.5 45.7 %collective-permute-start.94 = (f32[2048,34]{0,1:T(8,128)}, f32[2048,34]{0,1:T(8,128)}, u32[]{:S(2)}, u32[]{:S(2)}) collective-permute-start(f32[2048,34]{0,1:T(8,128)} %fusion.86), channel_id=1, source_target_pairs={{0,1},{1,0},{2,3},{3,2},{4,5},{5,4},{6,7},{7,6},{8,9},{9,8},{10,11... | collective-permute-start | bytes 835592 | tf_op jit(solution)/shard_map/ppermute | solution.py:341
  1439.9 41.0 %collective-permute-start.85 = (bf16[2,128,1024]{2,1,0:T(8,128)(2,1)S(1)}, bf16[2,128,1024]{2,1,0:T(8,128)(2,1)S(1)}, u32[]{:S(2)}, u32[]{:S(2)}) collective-permute-start(bf16[2,128,1024]{2,1,0:T(8,128)(2,1)S(1)} %get-tuple-element.158), channel_id=1, source_target_pairs={{0,8},{2,10},{4,12},{6,14},{1,9},{3,11},{5,13},{7,15}} | collective-permute-start | bytes 1572872 | tf_op jit(solution)/shard_map/ppermute | solution.py:377
  1530.8 34.4 %collective-permute-start.62 = (bf16[4,128,1536]{2,1,0:T(8,128)(2,1)S(1)}, bf16[4,128,1536]{2,1,0:T(8,128)(2,1)S(1)}, u32[]{:S(2)}, u32[]{:S(2)}) collective-permute-start(bf16[4,128,1536]{2,1,0:T(8,128)(2,1)S(1)} %dynamic-slice_bitcast_fusion.2), channel_id=1, source_target_pairs={{0,4},{2,6},{4,0},{6,2},{8,12},{10,14},{12,8},{14,10},{16,20},{18,... | collective-permute-start | bytes 4718600 | tf_op jit(solution)/shard_map/ppermute | solution.py:337
  1535.3 35.0 %collective-permute-start.87 = (bf16[2,128,1024]{2,1,0:T(8,128)(2,1)S(1)}, bf16[2,128,1024]{2,1,0:T(8,128)(2,1)S(1)}, u32[]{:S(2)}, u32[]{:S(2)}) collective-permute-start(bf16[2,128,1024]{2,1,0:T(8,128)(2,1)S(1)} %get-tuple-element.156), channel_id=1, source_target_pairs={{0,8},{2,10},{4,12},{6,14},{8,16},{10,18},{12,20},{14,22},{16,24},... | collective-permute-start | bytes 1572872 | tf_op jit(solution)/shard_map/ppermute | solution.py:377
  1537.3 34.3 %collective-permute-start.90 = (bf16[2,128,1024]{2,1,0:T(8,128)(2,1)S(1)}, bf16[2,128,1024]{2,1,0:T(8,128)(2,1)S(1)}, u32[]{:S(2)}, u32[]{:S(2)}) collective-permute-start(bf16[2,128,1024]{2,1,0:T(8,128)(2,1)S(1)} %fusion.39), channel_id=1, source_target_pairs={{8,0},{10,2},{12,4},{14,6},{16,8},{18,10},{20,12},{22,14},{24,16},... | collective-permute-start | bytes 1572872 | tf_op jit(solution)/shard_map/ppermute | solution.py:378
  1558.2 35.5 %collective-permute-start.72 = (bf16[2,128,1536]{2,1,0:T(8,128)(2,1)S(1)}, bf16[2,128,1536]{2,1,0:T(8,128)(2,1)S(1)}, u32[]{:S(2)}, u32[]{:S(2)}) collective-permute-start(bf16[2,128,1536]{2,1,0:T(8,128)(2,1)S(1)} %get-tuple-element.155), channel_id=1, source_target_pairs={{24,16},{26,18},{28,20},{30,22},{25,17},{27,19},{29,21},{31,23}} | collective-permute-start | bytes 2359304 | tf_op jit(solution)/shard_map/ppermute | solution.py:378
  1565.2 32.9 %collective-permute-start.70 = (bf16[2,128,1536]{2,1,0:T(8,128)(2,1)S(1)}, bf16[2,128,1536]{2,1,0:T(8,128)(2,1)S(1)}, u32[]{:S(2)}, u32[]{:S(2)}) collective-permute-start(bf16[2,128,1536]{2,1,0:T(8,128)(2,1)S(1)} %fusion.32), channel_id=1, source_target_pairs={{0,8},{2,10},{4,12},{6,14},{8,16},{10,18},{12,20},{14,22},{1,9},{3... | collective-permute-start | bytes 2359304 | tf_op jit(solution)/shard_map/ppermute | solution.py:377
  1571.6 30.4 %collective-permute-start.84 = (bf16[128,1024]{1,0:T(8,128)(2,1)S(1)}, bf16[128,1024]{1,0:T(8,128)(2,1)S(1)}, u32[]{:S(2)}, u32[]{:S(2)}) collective-permute-start(bf16[128,1024]{1,0:T(8,128)(2,1)S(1)} %fusion.70), channel_id=1, source_target_pairs={{8,0},{10,2},{12,4},{14,6},{16,8},{18,10},{20,12},{22,14},{24,16},... | collective-permute-start | bytes 786440 | tf_op jit(solution)/shard_map/ppermute | solution.py:378
  1599.3 59.6 %collective-permute-start.97 = (f32[2048,34]{0,1:T(8,128)S(1)}, f32[2048,34]{0,1:T(8,128)S(1)}, u32[]{:S(2)}, u32[]{:S(2)}) collective-permute-start(f32[2048,34]{0,1:T(8,128)S(1)} %add.774), channel_id=1, source_target_pairs={{0,16},{2,18},{4,20},{6,22},{8,24},{10,26},{12,28},{14,30},{16,0},... | collective-permute-start | bytes 835592 | tf_op jit(solution)/shard_map/ppermute | solution.py:439
  1602.7 42.4 %collective-permute-start.71 = (bf16[2,128,1536]{2,1,0:T(8,128)(2,1)S(1)}, bf16[2,128,1536]{2,1,0:T(8,128)(2,1)S(1)}, u32[]{:S(2)}, u32[]{:S(2)}) collective-permute-start(bf16[2,128,1536]{2,1,0:T(8,128)(2,1)S(1)} %get-tuple-element.152), channel_id=1, source_target_pairs={{0,8},{2,10},{4,12},{6,14},{8,16},{10,18},{12,20},{14,22},{16,24},... | collective-permute-start | bytes 2359304 | tf_op jit(solution)/shard_map/ppermute | solution.py:377
  1608.8 37.6 %collective-permute-start.74 = (bf16[2,128,1536]{2,1,0:T(8,128)(2,1)S(1)}, bf16[2,128,1536]{2,1,0:T(8,128)(2,1)S(1)}, u32[]{:S(2)}, u32[]{:S(2)}) collective-permute-start(bf16[2,128,1536]{2,1,0:T(8,128)(2,1)S(1)} %fusion.31), channel_id=1, source_target_pairs={{8,0},{10,2},{12,4},{14,6},{16,8},{18,10},{20,12},{22,14},{24,16},... | collective-permute-start | bytes 2359304 | tf_op jit(solution)/shard_map/ppermute | solution.py:378
  1610.2 49.9 %collective-permute-start.92 = (bf16[128,2048]{1,0:T(8,128)(2,1)S(1)}, bf16[128,2048]{1,0:T(8,128)(2,1)S(1)}, u32[]{:S(2)}, u32[]{:S(2)}) collective-permute-start(bf16[128,2048]{1,0:T(8,128)(2,1)S(1)} %maximum_convert_fusion), channel_id=1, source_target_pairs={{0,1},{1,0},{2,3},{3,2},{4,5},{5,4},{6,7},{7,6},{8,9},{9,8},{10,11... | collective-permute-start | bytes 1572872 | tf_op jit(solution)/shard_map/ppermute | solution.py:341
  1610.8 39.4 %collective-permute-start.65 = (bf16[128,1536]{1,0:T(8,128)(2,1)S(1)}, bf16[128,1536]{1,0:T(8,128)(2,1)S(1)}, u32[]{:S(2)}, u32[]{:S(2)}) collective-permute-start(bf16[128,1536]{1,0:T(8,128)(2,1)S(1)} %get-tuple-element.181), channel_id=1, source_target_pairs={{0,8},{2,10},{4,12},{6,14},{8,16},{10,18},{12,20},{14,22},{16,24},... | collective-permute-start | bytes 1179656 | tf_op jit(solution)/shard_map/ppermute | solution.py:377
  (142 other events, 4428.5 us)
Sparse Core Ops, SparseCore 0:
  13.3 112.4 all-gather.3
  194.5 288.9 all-gather.5

commit v3 on v2

--- a/solution.py
+++ b/solution.py
@@ -345,6 +345,10 @@
     return (one.astype(full) + two.astype(full)).astype(low)
 
 
+def hold(values, first):
+    return lax.optimization_barrier((values, first))
+
+
 def take(values, index):
     return lax.dynamic_index_in_dim(values, index, 0, keepdims=False)
 
@@ -379,22 +383,10 @@
     return part(place).astype(full) + up.astype(full) + down.astype(full)
 
 
-def sum_quarters(quarters, place):
-    half = quarters[0, 0][0].shape[-1] // 2
-    one, two = {}, {}
-    for at in ((1, 1), (0, 1), (1, 0), (0, 0)):
-        keep, send = quarters[at]
-        other = swap_core(send)
-        one[at] = add_low(keep[..., :half], other[..., :half])
-        two[at] = add_low(keep[..., half:], other[..., half:])
-    one_side = add_low(one[1, 0], swap_ctx(one[1, 1]))
-    two_ctx = add_low(two[0, 1], swap_side(two[1, 1]))
-    one_ctx = swap_ctx(one[0, 1])
-    two_side = swap_side(two[1, 0])
-    one_mine = add_low(add_low(one[0, 0], one_ctx), swap_side(one_side))
-    two_mine = add_low(add_low(two[0, 0], two_side), swap_ctx(two_ctx))
-    sums = [line_sum(item, place, relative=True) for item in (two_mine, one_mine)]
-    return jnp.concatenate([sums[1], sums[0]], axis=-1)
+def over_core(keep, send):
+    half = keep.shape[-1] // 2
+    other = swap_core(send)
+    return add_low(keep[..., :half], other[..., :half]), add_low(keep[..., half:], other[..., half:])
 
 
 def gather_line(values):
@@ -439,6 +431,20 @@
         values = values + lax.ppermute(values, "fsdp", [(i, i ^ step) for i in range(fsdp)])
         step *= 2
     return values
+
+
+def sum_owned(values, fsdp, spot):
+    items, shard = values.shape[0], values.shape[1] // fsdp
+    values = values.reshape(items, fsdp, shard).swapaxes(0, 1)
+    step = fsdp // 2
+    while step:
+        bit = (spot // step) % 2
+        values = values.reshape(2, step, items, shard)
+        other = lax.ppermute(take(values, 1 - bit), "fsdp", [(i, i ^ step) for i in range(fsdp)])
+        values = take(values, bit) + other
+        step //= 2
+    values = values[0]
+    return values + swap_ctx(values)
 
 
 def turn(values):
@@ -597,7 +603,7 @@
     )(projected, projected, roped_q, roped_k, values_low, grad, cosine, sine, query_gain, key_gain)
 
 
-def expert_kernel(core_ref, order, m_ref, g_keep, g_send, w_ref, gu_ref, dn_ref, *refs):
+def expert_kernel(core_ref, order, m_ref, g_ref, g_keep, g_send, w_ref, gu_ref, dn_ref, *refs):
     (keep_out, send_out, keep_back, send_back, gate_back, rows_ref, dy_ref, z_ref, pair_ref) = refs[-9:]
     core = core_ref[0]
     block = m_ref.shape[3]
@@ -609,7 +615,7 @@
     ).astype(low)
     slot_ids = lax.broadcasted_iota(jnp.int32, (slots, block), 0)
     places, picks, weights, rows, grads = [], [], [], [], []
-    for part, g_ref in enumerate((g_keep, g_send)):
+    for part, g_more in enumerate((g_keep, g_send)):
         at = lax.rem(core + part, 2)
         gate = w_ref[0, at, 0]
         hit = jnp.where(gate >= 0.0, 1.0, 0.0)
@@ -621,7 +627,9 @@
         picks.append(pick)
         weights.append(jnp.sum(jnp.where(place, gate, 0.0), axis=1, keepdims=True))
         rows.append(mul(pick, m_ref[0, at, 0]).astype(low))
-        grads.append(mul(pick, g_ref[0]))
+        grads.append(
+            jnp.concatenate([mul(pick, g_ref[0, at, 0]), mul(pick, g_more[0])], axis=1)
+        )
     row, grad, weight = (jnp.concatenate(items, axis=0) for items in (rows, grads, weights))
     rows_ref[...] = row
     paired = mul(row, gu_ref[...])
@@ -651,7 +659,7 @@
         out[0] = mul(picks[part], back[mine], lhs_turned).astype(low)
 
 
-def run_expert(core, order, number, parts, m_all, g_keep, g_send, gates_all, gate_up, down, slots, kept):
+def run_expert(core, order, number, parts, m_all, g_all, g_keep, g_send, gates_all, gate_up, down, slots, kept):
     places, _, _, block, width = m_all.shape
     paired = gate_up.shape[1]
     steps = g_keep.shape[0]
@@ -678,7 +686,11 @@
         num_scalar_prefetch=2,
         grid=(steps,),
         in_specs=[
-            pl.BlockSpec((1, 2, 1, block, width), token_at), one_block, one_block, small,
+            pl.BlockSpec((1, 2, 1, block, width), token_at),
+            pl.BlockSpec((1, 2, 1, block, g_all.shape[4]), token_at),
+            pl.BlockSpec((1, block, g_keep.shape[2]), stacked),
+            pl.BlockSpec((1, block, g_keep.shape[2]), stacked),
+            small,
             pl.BlockSpec(gate_up.shape, fixed, pipeline_mode=pl.Buffered(1)),
             pl.BlockSpec(down.shape, fixed, pipeline_mode=pl.Buffered(1)),
         ]
@@ -691,7 +703,7 @@
         out_shape=[shape((steps, block, width), low)] * 4
         + [shape((places, 2, 2, 1, block), full)]
         + [shape((parts * part_rows, n), low) for n in widths],
-        input_output_aliases={} if kept is None else {8 + i: 4 + i for i in range(5)},
+        input_output_aliases={} if kept is None else {9 + i: 4 + i for i in range(5)},
         compiler_params=pltpu.CompilerParams(vmem_limit_bytes=vmem_bytes),
         cost_estimate=pl.CostEstimate(
             flops=part_rows * width * (4 * paired + 4 * hidden + 8 * block),
@@ -699,7 +711,7 @@
             transcendentals=part_rows * hidden,
         ),
         name="experts",
-    )(core, order, m_all, g_keep, g_send, gates_all, gate_up, down, *(() if kept is None else kept))
+    )(core, order, m_all, g_all, g_keep, g_send, gates_all, gate_up, down, *(() if kept is None else kept))
 
 
 def rms_back(values, gain, grad):
@@ -761,7 +773,9 @@
     router_all = small_all[:, :experts_all]
     attn_all = small_all[:, experts_all].astype(full)
     moe_all = small_all[:, experts_all + 1].astype(full)
-    g_parts = gather_quarters(cotangent)
+    g_half = width // 2
+    g_all = lax.all_gather(cotangent[:, :g_half], both, axis=0)
+    g_parts = gather_quarters(cotangent[:, g_half:])
 
     sequence_in = sequence(tokens).astype(full)
     low_in = rms_scale(sequence_in, attn_all).astype(low)
@@ -794,17 +808,25 @@
     lines = fsdp // 4
     grid_of = (fsdp // 2, 2, 2)
     lines_at = (place - jnp.arange(lines, dtype=jnp.int32)) % lines
-    kept, summed_back, summed_out = None, {}, {}
-    for number, (d_side, d_ctx) in enumerate(((1, 1), (0, 1), (1, 0), (0, 0))):
+    kept, back, out, wait = None, {}, {}, None
+    core_at = core[None].astype(jnp.int32)
+    for number, at in enumerate(((1, 1), (0, 1), (1, 0), (0, 0))):
+        d_side, d_ctx = at
         order = jnp.stack(
             [lines_at * 2 + (side + d_side) % 2, jnp.broadcast_to((rank + d_ctx) % 2, (lines,))], axis=1
         ).reshape(-1)
+        if number == 2:
+            core_at, back[1, 1] = hold(core_at, back[1, 1])
+        if number == 3:
+            far_ctx, far_side = swap_ctx(back[1, 1][0]), swap_side(back[1, 1][1])
+            core_at, (back[0, 1], far_ctx, far_side) = hold(core_at, (back[0, 1], far_ctx, far_side))
         keep_out, send_out, keep_back, send_back, *kept = run_expert(
-            core[None].astype(jnp.int32),
+            core_at,
             order.astype(jnp.int32),
             number,
             4,
             m_all.reshape(*grid_of, rows_dev, width),
+            g_all.reshape(*grid_of, rows_dev, g_half),
             g_parts[d_side, d_ctx, 0],
             g_parts[d_side, d_ctx, 1],
             gates_all.reshape(*grid_of, 1, rows_dev),
@@ -813,17 +835,25 @@
             capacity,
             kept,
         )
-        summed_back[d_side, d_ctx] = (keep_back, send_back)
-        summed_out[d_side, d_ctx] = (keep_out, send_out)
+        back[at] = over_core(keep_back, send_back)
+        out[at] = (keep_out, send_out)
     gate_back, rows, grad_rows, hidden, grad_pair = kept
     grad_gates = lax.all_to_all(
         gate_back.reshape(fsdp * 2, rows_dev), both, split_axis=0, concat_axis=0, tiled=True
     ).T
-    grad_mid = sum_quarters(summed_back, place)
+    one_ctx, two_side = swap_ctx(back[0, 1][0]), swap_side(back[1, 0][1])
+    one_side = swap_side(add_low(back[1, 0][0], far_ctx))
+    two_ctx = swap_ctx(add_low(back[0, 1][1], far_side))
+    one_mine = add_low(add_low(back[0, 0][0], one_ctx), one_side)
+    two_mine = add_low(add_low(back[0, 0][1], two_side), two_ctx)
+    two_sum = line_sum(two_mine, place, relative=True)
+    one_sum = line_sum(one_mine, place, relative=True)
+    grad_mid = jnp.concatenate([one_sum, two_sum], axis=-1)
+    out = {at: over_core(*out[at]) for at in out}
+    out_far_ctx, out_far_side = swap_ctx(out[1, 1][0]), swap_side(out[1, 1][1])
+    grad_mid, (out_far_ctx, out_far_side) = hold(grad_mid, (out_far_ctx, out_far_side))
     grad_down = mul(hidden, grad_rows, lhs_turned)[None]
     grad_gate_up = mul(rows, grad_pair, lhs_turned)[None]
-    summed_out, grad_mid = lax.optimization_barrier((summed_out, grad_mid))
-    output = (mixed + sum_quarters(summed_out, place)).astype(low)
 
     grad_wide = jnp.where(chosen, grad_gates, 0.0)
     grad_logits = (
@@ -837,10 +867,23 @@
     grad_branch = sequence(grad_mixed.astype(low))
     grad_attended = mul(grad_branch, out_all, rhs_turned).astype(low)
     grad_out_part = mul(attended, grad_branch, lhs_turned).astype(low)
+    out_ctx, out_side = swap_ctx(out[0, 1][0]), swap_side(out[1, 0][1])
+    grad_attended, (out_ctx, out_side) = hold(grad_attended, (out_ctx, out_side))
     grad_q, grad_k, grad_v, gain_q_part, gain_k_part = attend_grad(
         projected, roped_q, roped_k, values_low, grad_attended, cosine, sine, gain_q, gain_k, kv_heads, group
     )
     grad_projected = jnp.concatenate([grad_q, grad_k, grad_v], axis=1)
+    out_one = swap_side(add_low(out[1, 0][0], out_far_ctx))
+    out_two = swap_ctx(add_low(out[0, 1][1], out_far_side))
+    grad_projected, (out_one, out_two) = hold(grad_projected, (out_one, out_two))
+    one_mine = add_low(add_low(out[0, 0][0], out_ctx), out_one)
+    two_mine = add_low(add_low(out[0, 0][1], out_side), out_two)
+    output = (
+        mixed
+        + jnp.concatenate(
+            [line_sum(one_mine, place, relative=True), line_sum(two_mine, place, relative=True)], axis=-1
+        )
+    ).astype(low)
     grad_qkv_part = mul(low_in, grad_projected, lhs_turned).astype(low)
     grad_normed_part = mul(grad_projected, qkv_all, rhs_turned)
     grad_normed = of_block(grad_normed_part, rank) + swap_ctx(
@@ -868,31 +911,29 @@
     grad_qkv = jnp.concatenate(
         [grad_q_all, qkv_mine[:, width_q:] + qkv_other[:, width_q:]], axis=1
     )
-    total = sum_all(
+    early = sum_owned(jnp.concatenate([grad_router.T, grad_moe_gain[None]], axis=0), fsdp, spot)
+    late = sum_all(
         jnp.concatenate(
             [
-                grad_router,
-                grad_attn_gain[:, None],
-                grad_moe_gain[:, None],
+                grad_attn_gain.reshape(-1, head_dim),
+                jnp.sum(gain_q_part, axis=0),
+                jnp.sum(gain_k_part, axis=0),
             ],
-            axis=1,
+            axis=0,
         ),
         fsdp,
     )
-    gains = sum_all(
-        jnp.concatenate([jnp.sum(gain_q_part, axis=0), jnp.sum(gain_k_part, axis=0)], axis=0), fsdp
-    )
-    owned = lax.dynamic_slice_in_dim(total, spot * shard, shard, 0)
+    gain_rows = width // head_dim
     return (
         output,
         grad_tokens,
         grad_qkv,
         grad_out,
-        owned[:, :experts_all],
-        owned[:, experts_all],
-        owned[:, experts_all + 1],
-        gains[0],
-        gains[1],
+        early[:experts_all].T,
+        lax.dynamic_slice_in_dim(late[:gain_rows].reshape(-1), spot * shard, shard, 0),
+        early[experts_all],
+        late[gain_rows],
+        late[gain_rows + 1],
         grad_gate_up,
         grad_down,
     )
@@ -905,7 +946,7 @@
     tokens, gate_up = args[0], args[8]
     fsdp, ctx = lax.axis_size("fsdp"), lax.axis_size("ctx")
     fits = tokens.size * tokens.dtype.itemsize * fsdp * ctx <= gathered_bytes
-    if fits and fsdp % 4 == 0 and ctx == 2 and gate_up.shape[0] == 1:
+    if fits and fsdp % 4 == 0 and ctx == 2 and fsdp & (fsdp - 1) == 0 and gate_up.shape[0] == 1:
         return body_gathered(*args)
     return body_routed(*args)
 

time: 1700 us -> 1410 us (0.83)
  waiting for transfers between devices: 932 us -> 689 us
  starting transfers between devices: 248 us -> 192 us
    ppermute x11, waiting for transfers between devices: 242 us -> 127 us  [swap_side(): return lax.ppermute(values, 'fsdp', side_pairs(lax.axis_size('fsdp')))]
    ppermute x16, waiting for transfers between devices: 369 us -> 279 us  [swap_ctx(): return lax.ppermute(values, 'ctx', [(0, 1), (1, 0)])]
    ppermute x3, waiting for transfers between devices: 86.5 us -> 50.2 us  [gather_line(): lax.ppermute(ups[-1], 'fsdp', [(i, i + 4) for i in range(fsdp - 4)])]
    ppermute x24, starting transfers between devices: 125 us -> 92.4 us  [line_sum(): up = lax.ppermute(send_up, 'fsdp', pairs_up)]
    all_gather x1, waiting for transfers between devices: 0.01 us -> 28.2 us  [body_gathered(): m_all = lax.all_gather(low_mid, both, axis=0)]
    ppermute x3, waiting for transfers between devices: 25.8 us -> 6.81 us  [gather_line(): lax.ppermute(downs[-1], 'fsdp', [(i, i - 4) for i in range(4, fsdp)])]
    convert_element_type x36 -> x37, other arithmetic: 75 us -> 85.3 us  [add_low(): return (one.astype(full) + two.astype(full)).astype(low)]
  transfers between devices with their start and end apart: 107 -> 108, of which waited for: 44 -> 43; matrix products, arithmetic and copies ran while one was open for 11% -> 18% of each run, Pallas kernels for 9% -> 14%
where the time goes in v3:
time: 1410 us; the launch traced here: 1400 us
  waiting for transfers between devices  689 us (49%)
  Pallas kernels  197 us (14%)
  starting transfers between devices  192 us (14%)
  other arithmetic  116 us (8%)
  matrix products  111 us (8%)
  local copies, waits for them, and re-layouts  54.3 us (4%)
  blocking collectives  23.2 us (2%)
  between operations  16.5 us (1%)
    ppermute x16, waiting for transfers between devices, swap_ctx(): return lax.ppermute(values, 'ctx', [(0, 1), (1, 0)])  279 us
    pallas_call x4, Pallas kernels, run_expert(): pl.pallas_call(expert_kernel, grid_spec=grid_spec, out_shape=[shape((step...  154 us
    ppermute x11, waiting for transfers between devices, swap_side(): return lax.ppermute(values, 'fsdp', side_pairs(lax.axis_size('fsdp')))  127 us
    dot_general x11, matrix products, mul(): return lax.dot_general(left, right, dims, preferred_element_type=full)  111 us
    ppermute x24, starting transfers between devices, line_sum(): up = lax.ppermute(send_up, 'fsdp', pairs_up)  92.4 us
    convert_element_type x37, other arithmetic, add_low(): return (one.astype(full) + two.astype(full)).astype(low)  85.3 us
    all_gather x1, waiting for transfers between devices, body_gathered(): weights_all = lax.all_gather(weights_local, 'fsdp', axis=0, tiled=True)  80.4 us
    ppermute x24, waiting for transfers between devices, line_sum(): up = lax.ppermute(send_up, 'fsdp', pairs_up)  77.5 us
  transfers between devices with their start and end apart: 108, of which 43 were waited for; matrix products, arithmetic and copies ran while one was open for 18% of the time, Pallas kernels for 14%

profile of v3, /device:TPU:0, one launch (start us, length us, event | category | flops | bytes accessed | tf_op | source)
XLA Modules:
  0.0 1399.0 jit_solution(10771889615718295833)
XLA Ops:
  20.8 23.2 %all_gather.18 = bf16[2048,34]{0,1:T(8,128)(2,1)S(1)} all-gather(bf16[128,34]{0,1:T(8,128)(2,1)S(1)} %pad_maximum_fusion.15), channel_id=1, replica_groups=mesh['fsdp'=16,'ctx'=2] {'fsdp'}, dimensions={0}, use_global_device_ids=true | all-gather | bytes 147968 | tf_op jit(solution)/shard_map/all_gather | solution.py:769
  47.4 80.4 %all-gather.6.cloned.1.call-done = bf16[2048,5120]{1,0:T(8,128)(2,1)} async-done(((bf16[128,5120]{1,0:T(8,128)(2,1)}), bf16[2048,5120]{1,0:T(8,128)(2,1)}) %all-gather.6.cloned.1.call-update) | async-done | bytes 20971536 | tf_op jit(solution)/shard_map/all_gather | solution.py:770
  127.8 11.6 fusion.3.q_ref.k_ref.v_ref
  139.4 18.4 %attend.1 = (bf16[512,2048]{1,0:T(8,128)(2,1)S(1)}, bf16[512,2048]{1,0:T(8,128)(2,1)S(1)}, bf16[512,512]{1,0:T(8,128)(2,1)S(1)}, bf16[512,512]{1,0:T(8,128)(2,1)S(1)}) custom-call(f32[512,3072]{1,0:T(8,128)} %fusion.3.q_ref.k_ref.v_ref, f32[512,3072]{1,0:T(8,128)} %fusion.3.q_ref.k_ref.v_ref, f32[512,3072]{1,0:T(8,128)} %fusion.3.q_ref.k_ref.v_ref, ...), custom_call_target="tpu_custom_call" | custom-call | flops 2147483648 | bytes 9437184 | tf_op jit(solution)/shard_map/attend/pallas_call | solution.py:558
  157.8 8.9 fusion.8
  168.8 31.4 %collective-permute-done.1 = bf16[256,2048]{1,0:T(8,128)(2,1)S(1)} collective-permute-done((bf16[256,2048]{1,0:T(8,128)(2,1)S(1)}, bf16[256,2048]{1,0:T(8,128)(2,1)S(1)}, u32[]{:S(2)}, u32[]{:S(2)}) %collective-permute-start.1) | collective-permute-done | bytes 1048608 | tf_op jit(solution)/shard_map/ppermute | solution.py:341
  208.4 21.8 %collective-permute-done.2 = bf16[256,1024]{1,0:T(8,128)(2,1)S(1)} collective-permute-done((bf16[256,1024]{1,0:T(8,128)(2,1)S(1)}, bf16[256,1024]{1,0:T(8,128)(2,1)S(1)}, u32[]{:S(2)}, u32[]{:S(2)}) %collective-permute-start.2) | collective-permute-done | bytes 524320 | tf_op jit(solution)/shard_map/ppermute | solution.py:397
  230.2 14.3 %collective-permute-start.6 = (bf16[256,1024]{1,0:T(8,128)(2,1)S(1)}, bf16[256,1024]{1,0:T(8,128)(2,1)S(1)}, u32[]{:S(2)}, u32[]{:S(2)}) collective-permute-start(bf16[256,1024]{1,0:T(8,128)(2,1)S(1)} %collective-permute-done.2), channel_id=1, source_target_pairs={{0,8},{2,10},{4,12},{6,14},{8,16},{10,18},{12,20},{14,22},{16,24},... | collective-permute-start | bytes 1572872 | tf_op jit(solution)/shard_map/ppermute | solution.py:397
  247.8 19.0 %collective-permute-done.6 = bf16[256,1024]{1,0:T(8,128)(2,1)S(1)} collective-permute-done((bf16[256,1024]{1,0:T(8,128)(2,1)S(1)}, bf16[256,1024]{1,0:T(8,128)(2,1)S(1)}, u32[]{:S(2)}, u32[]{:S(2)}) %collective-permute-start.6) | collective-permute-done | bytes 524320 | tf_op jit(solution)/shard_map/ppermute | solution.py:397
  273.4 9.5 collective-permute-done.7
  291.2 64.9 %collective-permute-done.8.g_keep = bf16[4,256,1024]{2,1,0:T(8,128)(2,1)S(1)} collective-permute-done((bf16[4,256,1024]{2,1,0:T(8,128)(2,1)}, bf16[4,256,1024]{2,1,0:T(8,128)(2,1)S(1)}, u32[]{:S(2)}, u32[]{:S(2)}) %collective-permute-start.8) | collective-permute-done | bytes 2097184 | tf_op jit(solution)/shard_map/ppermute | solution.py:337
  359.4 72.6 %collective-permute-done.9.g_keep = bf16[4,256,1024]{2,1,0:T(8,128)(2,1)} collective-permute-done((bf16[4,256,1024]{2,1,0:T(8,128)(2,1)S(1)}, bf16[4,256,1024]{2,1,0:T(8,128)(2,1)}, u32[]{:S(2)}, u32[]{:S(2)}) %collective-permute-start.9) | collective-permute-done | bytes 2097184 | tf_op jit(solution)/shard_map/ppermute | solution.py:341
  433.9 5.6 all-to-all-start
  440.1 69.5 %collective-permute-done.12.g_keep = bf16[4,256,1024]{2,1,0:T(8,128)(2,1)} collective-permute-done((bf16[4,256,1024]{2,1,0:T(8,128)(2,1)}, bf16[4,256,1024]{2,1,0:T(8,128)(2,1)}, u32[]{:S(2)}, u32[]{:S(2)}) %collective-permute-start.12) | collective-permute-done | bytes 2097184 | tf_op jit(solution)/shard_map/ppermute | solution.py:341
  509.6 28.2 %all-gather.8.cloned.1.call-done = bf16[8192,2048]{1,0:T(8,128)(2,1)} async-done(((bf16[256,2048]{1,0:T(8,128)(2,1)}), bf16[8192,2048]{1,0:T(8,128)(2,1)}) %all-gather.8.cloned.1.call-update) | async-done | bytes 33554448 | tf_op jit(solution)/shard_map/all_gather | solution.py:797
  537.8 37.9 %experts.4 = (bf16[4,256,2048]{2,1,0:T(8,128)(2,1)}, bf16[4,256,2048]{2,1,0:T(8,128)(2,1)}, bf16[4,256,2048]{2,1,0:T(8,128)(2,1)}, bf16[4,256,2048]{2,1,0:T(8,12...) custom-call(s32[1]{0:T(128)} %bitcast.5.core_ref, ...), custom_call_target="tpu_custom_call" | custom-call | flops 23622320128 | bytes 46661632 | tf_op jit(solution)/shard_map/experts/pallas_call | solution.py:700
  576.9 38.5 %experts.5 = (bf16[4,256,2048]{2,1,0:T(8,128)(2,1)}, bf16[4,256,2048]{2,1,0:T(8,128)(2,1)}, bf16[4,256,2048]{2,1,0:T(8,128)(2,1)}, bf16[4,256,2048]{2,1,0:T(8,12...) custom-call(s32[1]{0:T(128)} %bitcast.5.core_ref, ...), custom_call_target="tpu_custom_call", output_to_operand_aliasing={{4}: (9, {}), {5}: (10, {}), {6}: (11, {}), {7}: (12, {}), ... | custom-call | flops 23622320128 | bytes 46661632 | tf_op jit(solution)/shard_map/experts/pallas_call | solution.py:700
  617.2 5.8 add_convert_fusion.26
  625.0 38.5 %experts.6 = (bf16[4,256,2048]{2,1,0:T(8,128)(2,1)}, bf16[4,256,2048]{2,1,0:T(8,128)(2,1)}, bf16[4,256,2048]{2,1,0:T(8,128)(2,1)}, bf16[4,256,2048]{2,1,0:T(8,12...) custom-call(s32[1]{0:T(128)} %bitcast.5.core_ref, ...), custom_call_target="tpu_custom_call", output_to_operand_aliasing={{4}: (9, {}), {5}: (10, {}), {6}: (11, {}), {7}: (12, {}), ... | custom-call | flops 23622320128 | bytes 46661632 | tf_op jit(solution)/shard_map/experts/pallas_call | solution.py:700
  663.7 5.4 add_convert_fusion.24
  674.2 38.6 %experts.7 = (bf16[4,256,2048]{2,1,0:T(8,128)(2,1)}, bf16[4,256,2048]{2,1,0:T(8,128)(2,1)}, bf16[4,256,2048]{2,1,0:T(8,128)(2,1)}, bf16[4,256,2048]{2,1,0:T(8,12...) custom-call(s32[1]{0:T(128)} %bitcast.5.core_ref, ...), custom_call_target="tpu_custom_call", output_to_operand_aliasing={{4}: (9, {}), {5}: (10, {}), {6}: (11, {}), {7}: (12, {}), ... | custom-call | flops 23622320128 | bytes 46661632 | tf_op jit(solution)/shard_map/experts/pallas_call | solution.py:700
  718.1 5.7 add_convert_fusion.19
  725.9 39.5 %collective-permute-done.31 = bf16[4,256,1024]{2,1,0:T(8,128)(2,1)} collective-permute-done((bf16[4,256,1024]{2,1,0:T(8,128)(2,1)}, bf16[4,256,1024]{2,1,0:T(8,128)(2,1)}, u32[]{:S(2)}, u32[]{:S(2)}) %collective-permute-start.31) | collective-permute-done | bytes 2097184 | tf_op jit(solution)/shard_map/ppermute | solution.py:341
  765.4 7.3 collective-permute-done.23
  772.7 43.7 %collective-permute-done.30 = bf16[4,256,1024]{2,1,0:T(8,128)(2,1)} collective-permute-done((bf16[4,256,1024]{2,1,0:T(8,128)(2,1)}, bf16[4,256,1024]{2,1,0:T(8,128)(2,1)}, u32[]{:S(2)}, u32[]{:S(2)}) %collective-permute-start.30) | collective-permute-done | bytes 2097184 | tf_op jit(solution)/shard_map/ppermute | solution.py:337
  816.4 8.0 add_convert_fusion.18
  832.3 6.8 collective-permute-done.32
  856.0 5.9 add_convert_fusion.11
  875.5 34.5 %convolution_bitcast_fusion = f32[1,2048,1536]{2,1,0:T(8,128)} fusion(bf16[4096,2048]{1,0:T(8,128)(2,1)} %get-tuple-element.131, bf16[4096,1536]{1,0:T(8,128)(2,1)} %get-tuple-element.132), kind=kOutput, calls=%fused_computation.7 | convolution fusion | flops 25769803776 | bytes 41943040 | tf_op jit(solution)/shard_map/dot_general | solution.py:321
  928.3 9.8 collective-permute-done.37
  940.2 7.1 collective-permute-done.29
  952.5 19.1 %convolution_bitcast_fusion.1 = f32[1,768,2048]{2,1,0:T(8,128)} fusion(bf16[4096,768]{1,0:T(8,128)(2,1)S(1)} %bitcast.314, bf16[4096,2048]{1,0:T(8,128)(2,1)} %get-tuple-element.134), kind=kOutput, calls=%fused_computation.50 | convolution fusion | flops 12884901888 | bytes 29360128 | tf_op jit(solution)/shard_map/dot_general | solution.py:321
  994.2 54.0 %collective-permute-done.97 = f32[33,128]{1,0:T(8,128)S(1)} collective-permute-done((f32[33,128]{1,0:T(8,128)S(1)}, f32[33,128]{1,0:T(8,128)S(1)}, u32[]{:S(2)}, u32[]{:S(2)}) %collective-permute-start.97) | collective-permute-done | bytes 16928 | tf_op jit(solution)/shard_map/ppermute | solution.py:341
  1064.1 9.3 fusion.14.go_ref
  1073.4 25.1 %attend_grad.1 = (bf16[512,2048]{1,0:T(8,128)(2,1)S(1)}, bf16[512,512]{1,0:T(8,128)(2,1)S(1)}, bf16[512,512]{1,0:T(8,128)(2,1)S(1)}, f32[4,1,128]{2,1,0:T(1,128)S(1)}, f32[4,1,128]{2,1,0:T(1,128)S(1)}) custom-call(f32[512,3072]{1,0:T(8,128)} %fusion.3.q_ref.k_ref.v_ref, f32[512,3072]{1,0:T(8,128)} %fusion.3.q_ref.k_ref.v_ref, bf16[512,2048]{1,0:T(8,128)(2,1)} %copy-done.2, ...), custom_call_target="tpu_custom_call" | custom-call | flops 5368709120 | bytes 15728640 | tf_op jit(solution)/shard_map/attend_grad/pallas_call | solution.py:582
  1098.9 11.1 fusion.1
  1114.6 9.9 convolution_convert_fusion
  1137.3 6.1 dynamic-slice_bitcast_fusion
  1172.7 5.2 collective-permute-start.56
  1196.5 5.4 fusion.5
  1209.6 7.7 collective-permute-done.85
  1228.8 6.9 collective-permute-done.86
  1246.3 10.3 fusion
  1271.5 14.6 %collective-permute-done.80 = bf16[128,1024]{1,0:T(8,128)(2,1)S(1)} collective-permute-done((bf16[128,1024]{1,0:T(8,128)(2,1)S(1)}, bf16[128,1024]{1,0:T(8,128)(2,1)S(1)}, u32[]{:S(2)}, u32[]{:S(2)}) %collective-permute-start.80) | collective-permute-done | bytes 262176 | tf_op jit(solution)/shard_map/ppermute | solution.py:381
  1302.0 18.8 %collective-permute-done.63 = bf16[128,1536]{1,0:T(8,128)(2,1)S(1)} collective-permute-done((bf16[128,1536]{1,0:T(8,128)(2,1)S(1)}, bf16[128,1536]{1,0:T(8,128)(2,1)S(1)}, u32[]{:S(2)}, u32[]{:S(2)}) %collective-permute-start.63) | collective-permute-done | bytes 393248 | tf_op jit(solution)/shard_map/ppermute | solution.py:381
  1338.2 14.9 %collective-permute-start.65 = (bf16[128,1536]{1,0:T(8,128)(2,1)S(1)}, bf16[128,1536]{1,0:T(8,128)(2,1)S(1)}, u32[]{:S(2)}, u32[]{:S(2)}) collective-permute-start(bf16[128,1536]{1,0:T(8,128)(2,1)S(1)} %get-tuple-element.196), channel_id=1, source_target_pairs={{0,8},{2,10},{4,12},{6,14},{8,16},{10,18},{12,20},{14,22},{16,24},... | collective-permute-start | bytes 1179656 | tf_op jit(solution)/shard_map/ppermute | solution.py:381
  1354.5 6.3 collective-permute-done.74
  1372.4 8.8 collective-permute-done.76
  (497 shorter events, 336.9 us)
Async XLA Ops:
  7.2 120.6 %all-gather.6.cloned.1.call-start = ((), (), s32[]{:S(2)}) async-start(), calls=%async_computation.2 | async-start | bytes 22282240 | tf_op jit(solution)/shard_map/all_gather | solution.py:770
  15.1 494.5 %all-gather.10.cloned.1.call-start = ((), (), s32[]{:S(2)}) async-start(), calls=%async_computation.4 | async-start | bytes 17301504 | tf_op jit(solution)/shard_map/all_gather | solution.py:777
  16.4 521.4 %all-gather.8.cloned.1.call-start = ((), (), s32[]{:S(2)}) async-start(), calls=%async_computation.3 | async-start | bytes 34603008 | tf_op jit(solution)/shard_map/all_gather | solution.py:797
  207.1 39.4 %collective-permute-start.3 = (bf16[256,1024]{1,0:T(8,128)(2,1)S(1)}, bf16[256,1024]{1,0:T(8,128)(2,1)S(1)}, u32[]{:S(2)}, u32[]{:S(2)}) collective-permute-start(bf16[256,1024]{1,0:T(8,128)(2,1)S(1)} %copy-done.47), channel_id=1, source_target_pairs={{8,0},{10,2},{12,4},{14,6},{16,8},{18,10},{20,12},{22,14},{24,16},... | collective-permute-start | bytes 1572872 | tf_op jit(solution)/shard_map/ppermute | solution.py:398
  230.2 36.6 %collective-permute-start.6 = (bf16[256,1024]{1,0:T(8,128)(2,1)S(1)}, bf16[256,1024]{1,0:T(8,128)(2,1)S(1)}, u32[]{:S(2)}, u32[]{:S(2)}) collective-permute-start(bf16[256,1024]{1,0:T(8,128)(2,1)S(1)} %collective-permute-done.2), channel_id=1, source_target_pairs={{0,8},{2,10},{4,12},{6,14},{8,16},{10,18},{12,20},{14,22},{16,24},... | collective-permute-start | bytes 1572872 | tf_op jit(solution)/shard_map/ppermute | solution.py:397
  289.4 66.6 %collective-permute-start.8 = (bf16[4,256,1024]{2,1,0:T(8,128)(2,1)}, bf16[4,256,1024]{2,1,0:T(8,128)(2,1)S(1)}, u32[]{:S(2)}, u32[]{:S(2)}) collective-permute-start(bf16[4,256,1024]{2,1,0:T(8,128)(2,1)} %pad_maximum_fusion.4.g_keep), channel_id=1, source_target_pairs={{0,4},{2,6},{4,0},{6,2},{8,12},{10,14},{12,8},{14,10},{16,20},{18,... | collective-permute-start | bytes 6291464 | tf_op jit(solution)/shard_map/ppermute | solution.py:337
  357.4 74.6 %collective-permute-start.9 = (bf16[4,256,1024]{2,1,0:T(8,128)(2,1)S(1)}, bf16[4,256,1024]{2,1,0:T(8,128)(2,1)}, u32[]{:S(2)}, u32[]{:S(2)}) collective-permute-start(bf16[4,256,1024]{2,1,0:T(8,128)(2,1)S(1)} %collective-permute-done.8.g_keep), channel_id=1, source_target_pairs={{0,1},{1,0},{2,3},{3,2},{4,5},{5,4},{6,7},{7,6},{8,9},{9,8},{10,11... | collective-permute-start | bytes 6291464 | tf_op jit(solution)/shard_map/ppermute | solution.py:341
  358.8 150.7 %collective-permute-start.12 = (bf16[4,256,1024]{2,1,0:T(8,128)(2,1)}, bf16[4,256,1024]{2,1,0:T(8,128)(2,1)}, u32[]{:S(2)}, u32[]{:S(2)}) collective-permute-start(bf16[4,256,1024]{2,1,0:T(8,128)(2,1)} %pad_maximum_fusion.4.g_keep), channel_id=1, source_target_pairs={{0,1},{1,0},{2,3},{3,2},{4,5},{5,4},{6,7},{7,6},{8,9},{9,8},{10,11... | collective-permute-start | bytes 6291464 | tf_op jit(solution)/shard_map/ppermute | solution.py:341
  432.0 77.6 %collective-permute-start.10 = (bf16[4,256,1024]{2,1,0:T(8,128)(2,1)}, bf16[4,256,1024]{2,1,0:T(8,128)(2,1)}, u32[]{:S(2)}, u32[]{:S(2)}) collective-permute-start(bf16[4,256,1024]{2,1,0:T(8,128)(2,1)} %collective-permute-done.9.g_keep), channel_id=1, source_target_pairs={{0,2},{2,0},{4,6},{6,4},{8,10},{10,8},{12,14},{14,12},{16,18},{18,... | collective-permute-start | bytes 6291464 | tf_op jit(solution)/shard_map/ppermute | solution.py:333
  433.9 75.7 %all-to-all-start = ((f32[32,1,256]{2,1,0:T(1,128)}), f32[32,1,256]{2,1,0:T(1,128)S(1)}, u32[]{:S(2)}, u32[]{:S(2)}) async-start(f32[32,1,256]{2,1,0:T(1,128)} %copy.90), calls=%async_computation | async-start | bytes 65536 | tf_op jit(solution)/shard_map/all_to_all | solution.py:806
  509.6 67.4 %collective-permute-start.13 = (bf16[4,256,1024]{2,1,0:T(8,128)(2,1)}, bf16[4,256,1024]{2,1,0:T(8,128)(2,1)}, u32[]{:S(2)}, u32[]{:S(2)}) collective-permute-start(bf16[4,256,1024]{2,1,0:T(8,128)(2,1)} %collective-permute-done.12.g_keep), channel_id=1, source_target_pairs={{0,2},{2,0},{4,6},{6,4},{8,10},{10,8},{12,14},{14,12},{16,18},{18,... | collective-permute-start | bytes 6291464 | tf_op jit(solution)/shard_map/ppermute | solution.py:333
  575.8 41.5 %collective-permute-start.11 = (bf16[4,256,2048]{2,1,0:T(8,128)(2,1)}, bf16[4,256,2048]{2,1,0:T(8,128)(2,1)}, u32[]{:S(2)}, u32[]{:S(2)}) collective-permute-start(bf16[4,256,2048]{2,1,0:T(8,128)(2,1)} %get-tuple-element.75), channel_id=1, source_target_pairs={{0,2},{2,0},{4,6},{6,4},{8,10},{10,8},{12,14},{14,12},{16,18},{18,... | collective-permute-start | bytes 12582920 | tf_op jit(solution)/shard_map/ppermute | solution.py:333
  576.7 48.3 %collective-permute-start.18 = (bf16[4,256,1024]{2,1,0:T(8,128)(2,1)}, bf16[4,256,1024]{2,1,0:T(8,128)(2,1)}, u32[]{:S(2)}, u32[]{:S(2)}) collective-permute-start(bf16[4,256,1024]{2,1,0:T(8,128)(2,1)} %copy-done.38), channel_id=1, source_target_pairs={{0,2},{2,0},{4,6},{6,4},{8,10},{10,8},{12,14},{14,12},{16,18},{18,... | collective-permute-start | bytes 6291464 | tf_op jit(solution)/shard_map/ppermute | solution.py:333
  615.5 48.2 %collective-permute-start.14 = (bf16[4,256,2048]{2,1,0:T(8,128)(2,1)}, bf16[4,256,2048]{2,1,0:T(8,128)(2,1)}, u32[]{:S(2)}, u32[]{:S(2)}) collective-permute-start(bf16[4,256,2048]{2,1,0:T(8,128)(2,1)} %get-tuple-element.83), channel_id=1, source_target_pairs={{0,2},{2,0},{4,6},{6,4},{8,10},{10,8},{12,14},{14,12},{16,18},{18,... | collective-permute-start | bytes 12582920 | tf_op jit(solution)/shard_map/ppermute | solution.py:333
  617.0 55.9 %collective-permute-start.17 = (bf16[4,256,1024]{2,1,0:T(8,128)(2,1)}, bf16[4,256,1024]{2,1,0:T(8,128)(2,1)S(1)}, u32[]{:S(2)}, u32[]{:S(2)}) collective-permute-start(bf16[4,256,1024]{2,1,0:T(8,128)(2,1)} %pad_maximum_fusion.4.g_keep), channel_id=1, source_target_pairs={{0,2},{2,0},{4,6},{6,4},{8,10},{10,8},{12,14},{14,12},{16,18},{18,... | collective-permute-start | bytes 6291464 | tf_op jit(solution)/shard_map/ppermute | solution.py:333
  623.0 48.1 %collective-permute-start.15 = (bf16[4,256,1024]{2,1,0:T(8,128)(2,1)}, bf16[4,256,1024]{2,1,0:T(8,128)(2,1)}, u32[]{:S(2)}, u32[]{:S(2)}) collective-permute-start(bf16[4,256,1024]{2,1,0:T(8,128)(2,1)} %get-tuple-element.84), channel_id=1, source_target_pairs={{0,1},{1,0},{2,3},{3,2},{4,5},{5,4},{6,7},{7,6},{8,9},{9,8},{10,11... | collective-permute-start | bytes 6291464 | tf_op jit(solution)/shard_map/ppermute | solution.py:341
  623.5 47.8 %collective-permute-start.16 = (bf16[4,256,1024]{2,1,0:T(8,128)(2,1)}, bf16[4,256,1024]{2,1,0:T(8,128)(2,1)}, u32[]{:S(2)}, u32[]{:S(2)}) collective-permute-start(bf16[4,256,1024]{2,1,0:T(8,128)(2,1)} %get-tuple-element.85), channel_id=1, source_target_pairs={{0,4},{2,6},{4,0},{6,2},{8,12},{10,14},{12,8},{14,10},{16,20},{18,... | collective-permute-start | bytes 6291464 | tf_op jit(solution)/shard_map/ppermute | solution.py:337
  663.6 54.6 %collective-permute-start.22 = (bf16[4,256,2048]{2,1,0:T(8,128)(2,1)}, bf16[4,256,2048]{2,1,0:T(8,128)(2,1)}, u32[]{:S(2)}, u32[]{:S(2)}) collective-permute-start(bf16[4,256,2048]{2,1,0:T(8,128)(2,1)} %get-tuple-element.103), channel_id=1, source_target_pairs={{0,2},{2,0},{4,6},{6,4},{8,10},{10,8},{12,14},{14,12},{16,18},{18,... | collective-permute-start | bytes 12582920 | tf_op jit(solution)/shard_map/ppermute | solution.py:333
  671.4 54.0 %collective-permute-start.21 = (bf16[4,256,1024]{2,1,0:T(8,128)(2,1)}, bf16[4,256,1024]{2,1,0:T(8,128)(2,1)}, u32[]{:S(2)}, u32[]{:S(2)}) collective-permute-start(bf16[4,256,1024]{2,1,0:T(8,128)(2,1)} %get-tuple-element.101), channel_id=1, source_target_pairs={{0,1},{1,0},{2,3},{3,2},{4,5},{5,4},{6,7},{7,6},{8,9},{9,8},{10,11... | collective-permute-start | bytes 6291464 | tf_op jit(solution)/shard_map/ppermute | solution.py:341
  712.8 59.9 %collective-permute-start.20 = (bf16[4,256,2048]{2,1,0:T(8,128)(2,1)}, bf16[4,256,2048]{2,1,0:T(8,128)(2,1)}, u32[]{:S(2)}, u32[]{:S(2)}) collective-permute-start(bf16[4,256,2048]{2,1,0:T(8,128)(2,1)} %get-tuple-element.100), channel_id=1, source_target_pairs={{0,2},{2,0},{4,6},{6,4},{8,10},{10,8},{12,14},{14,12},{16,18},{18,... | collective-permute-start | bytes 12582920 | tf_op jit(solution)/shard_map/ppermute | solution.py:333
  712.9 143.1 %collective-permute-start.38 = (bf16[4,256,2048]{2,1,0:T(8,128)(2,1)}, bf16[4,256,2048]{2,1,0:T(8,128)(2,1)}, u32[]{:S(2)}, u32[]{:S(2)}) collective-permute-start(bf16[4,256,2048]{2,1,0:T(8,128)(2,1)} %get-tuple-element.108), channel_id=1, source_target_pairs={{0,2},{2,0},{4,6},{6,4},{8,10},{10,8},{12,14},{14,12},{16,18},{18,... | collective-permute-start | bytes 12582920 | tf_op jit(solution)/shard_map/ppermute | solution.py:333
  717.6 47.9 %collective-permute-start.31 = (bf16[4,256,1024]{2,1,0:T(8,128)(2,1)}, bf16[4,256,1024]{2,1,0:T(8,128)(2,1)}, u32[]{:S(2)}, u32[]{:S(2)}) collective-permute-start(bf16[4,256,1024]{2,1,0:T(8,128)(2,1)} %add_convert_fusion.14), channel_id=1, source_target_pairs={{0,1},{1,0},{2,3},{3,2},{4,5},{5,4},{6,7},{7,6},{8,9},{9,8},{10,11... | collective-permute-start | bytes 6291464 | tf_op jit(solution)/shard_map/ppermute | solution.py:341
  723.8 48.9 %collective-permute-start.23 = (bf16[4,256,1024]{2,1,0:T(8,128)(2,1)}, bf16[4,256,1024]{2,1,0:T(8,128)(2,1)}, u32[]{:S(2)}, u32[]{:S(2)}) collective-permute-start(bf16[4,256,1024]{2,1,0:T(8,128)(2,1)} %get-tuple-element.154), channel_id=1, source_target_pairs={{0,4},{2,6},{4,0},{6,2},{8,12},{10,14},{12,8},{14,10},{16,20},{18,... | collective-permute-start | bytes 6291464 | tf_op jit(solution)/shard_map/ppermute | solution.py:337
  725.3 91.0 %collective-permute-start.30 = (bf16[4,256,1024]{2,1,0:T(8,128)(2,1)}, bf16[4,256,1024]{2,1,0:T(8,128)(2,1)}, u32[]{:S(2)}, u32[]{:S(2)}) collective-permute-start(bf16[4,256,1024]{2,1,0:T(8,128)(2,1)} %get-tuple-element.155), channel_id=1, source_target_pairs={{0,4},{2,6},{4,0},{6,2},{8,12},{10,14},{12,8},{14,10},{16,20},{18,... | collective-permute-start | bytes 6291464 | tf_op jit(solution)/shard_map/ppermute | solution.py:337
  829.3 36.8 %collective-permute-start.35 = (bf16[256,1024]{1,0:T(8,128)(2,1)}, bf16[256,1024]{1,0:T(8,128)(2,1)}, u32[]{:S(2)}, u32[]{:S(2)}) collective-permute-start(bf16[256,1024]{1,0:T(8,128)(2,1)} %get-tuple-element.193), channel_id=1, source_target_pairs={{24,16},{26,18},{28,20},{30,22},{25,17},{27,19},{29,21},{31,23}} | collective-permute-start | bytes 1572872 | tf_op jit(solution)/shard_map/ppermute | solution.py:382
  830.8 40.7 %collective-permute-start.27 = (bf16[256,1024]{1,0:T(8,128)(2,1)}, bf16[256,1024]{1,0:T(8,128)(2,1)}, u32[]{:S(2)}, u32[]{:S(2)}) collective-permute-start(bf16[256,1024]{1,0:T(8,128)(2,1)} %get-tuple-element.189), channel_id=1, source_target_pairs={{24,16},{26,18},{28,20},{30,22},{25,17},{27,19},{29,21},{31,23}} | collective-permute-start | bytes 1572872 | tf_op jit(solution)/shard_map/ppermute | solution.py:382
  861.9 86.9 %collective-permute-start.39 = (bf16[4,256,1024]{2,1,0:T(8,128)(2,1)}, bf16[4,256,1024]{2,1,0:T(8,128)(2,1)}, u32[]{:S(2)}, u32[]{:S(2)}) collective-permute-start(bf16[4,256,1024]{2,1,0:T(8,128)(2,1)} %get-tuple-element.151), channel_id=1, source_target_pairs={{0,1},{1,0},{2,3},{3,2},{4,5},{5,4},{6,7},{7,6},{8,9},{9,8},{10,11... | collective-permute-start | bytes 6291464 | tf_op jit(solution)/shard_map/ppermute | solution.py:341
  863.6 51.2 %all-to-all-start.1 = ((f32[32,1,256]{2,1,0:T(1,128)}), f32[32,1,256]{2,1,0:T(1,128)S(1)}, u32[]{:S(2)}, u32[]{:S(2)}) async-start(f32[32,1,256]{2,1,0:T(1,128)} %bitcast.32), calls=%async_computation.1 | async-start | bytes 65536 | tf_op jit(solution)/shard_map/all_to_all | solution.py:841
  866.2 82.6 %collective-permute-start.40 = (bf16[4,256,1024]{2,1,0:T(8,128)(2,1)}, bf16[4,256,1024]{2,1,0:T(8,128)(2,1)}, u32[]{:S(2)}, u32[]{:S(2)}) collective-permute-start(bf16[4,256,1024]{2,1,0:T(8,128)(2,1)} %get-tuple-element.150), channel_id=1, source_target_pairs={{0,4},{2,6},{4,0},{6,2},{8,12},{10,14},{12,8},{14,10},{16,20},{18,... | collective-permute-start | bytes 6291464 | tf_op jit(solution)/shard_map/ppermute | solution.py:337
  870.9 44.0 %collective-permute-start.36 = (bf16[256,1024]{1,0:T(8,128)(2,1)}, bf16[256,1024]{1,0:T(8,128)(2,1)S(1)}, u32[]{:S(2)}, u32[]{:S(2)}) collective-permute-start(bf16[256,1024]{1,0:T(8,128)(2,1)} %get-tuple-element.191), channel_id=1, source_target_pairs={{16,8},{18,10},{20,12},{22,14},{24,16},{26,18},{28,20},{30,22},{17... | collective-permute-start | bytes 1572872 | tf_op jit(solution)/shard_map/ppermute | solution.py:382
  874.0 46.5 %collective-permute-start.28 = (bf16[256,1024]{1,0:T(8,128)(2,1)}, bf16[256,1024]{1,0:T(8,128)(2,1)}, u32[]{:S(2)}, u32[]{:S(2)}) collective-permute-start(bf16[256,1024]{1,0:T(8,128)(2,1)} %get-tuple-element.187), channel_id=1, source_target_pairs={{16,8},{18,10},{20,12},{22,14},{24,16},{26,18},{28,20},{30,22},{17... | collective-permute-start | bytes 1572872 | tf_op jit(solution)/shard_map/ppermute | solution.py:382
  938.0 42.5 %collective-permute-start.42 = (bf16[4,256,2048]{2,1,0:T(8,128)(2,1)}, bf16[4,256,2048]{2,1,0:T(8,128)(2,1)}, u32[]{:S(2)}, u32[]{:S(2)}) collective-permute-start(bf16[4,256,2048]{2,1,0:T(8,128)(2,1)} %get-tuple-element.112), channel_id=1, source_target_pairs={{0,2},{2,0},{4,6},{6,4},{8,10},{10,8},{12,14},{14,12},{16,18},{18,... | collective-permute-start | bytes 12582920 | tf_op jit(solution)/shard_map/ppermute | solution.py:333
  939.6 48.3 %collective-permute-start.44 = (bf16[4,256,2048]{2,1,0:T(8,128)(2,1)}, bf16[4,256,2048]{2,1,0:T(8,128)(2,1)S(1)}, u32[]{:S(2)}, u32[]{:S(2)}) collective-permute-start(bf16[4,256,2048]{2,1,0:T(8,128)(2,1)} %get-tuple-element.114), channel_id=1, source_target_pairs={{0,2},{2,0},{4,6},{6,4},{8,10},{10,8},{12,14},{14,12},{16,18},{18,... | collective-permute-start | bytes 12582920 | tf_op jit(solution)/shard_map/ppermute | solution.py:333
  947.3 177.2 %collective-permute-start.19 = (bf16[4,256,2048]{2,1,0:T(8,128)(2,1)}, bf16[4,256,2048]{2,1,0:T(8,128)(2,1)S(1)}, u32[]{:S(2)}, u32[]{:S(2)}) collective-permute-start(bf16[4,256,2048]{2,1,0:T(8,128)(2,1)} %get-tuple-element.98), channel_id=1, source_target_pairs={{0,2},{2,0},{4,6},{6,4},{8,10},{10,8},{12,14},{14,12},{16,18},{18,... | collective-permute-start | bytes 12582920 | tf_op jit(solution)/shard_map/ppermute | solution.py:333
  978.9 71.2 %collective-permute-start.41 = (bf16[256,2048]{1,0:T(8,128)(2,1)S(1)}, bf16[256,2048]{1,0:T(8,128)(2,1)S(1)}, u32[]{:S(2)}, u32[]{:S(2)}) collective-permute-start(bf16[256,2048]{1,0:T(8,128)(2,1)S(1)} %get-tuple-element.140), channel_id=1, source_target_pairs={{0,1},{1,0},{2,3},{3,2},{4,5},{5,4},{6,7},{7,6},{8,9},{9,8},{10,11... | collective-permute-start | bytes 3145736 | tf_op jit(solution)/shard_map/ppermute | solution.py:341
  985.8 87.6 %collective-permute-start.43 = (bf16[4,256,1024]{2,1,0:T(8,128)(2,1)}, bf16[4,256,1024]{2,1,0:T(8,128)(2,1)}, u32[]{:S(2)}, u32[]{:S(2)}) collective-permute-start(bf16[4,256,1024]{2,1,0:T(8,128)(2,1)} %get-tuple-element.147), channel_id=1, source_target_pairs={{0,1},{1,0},{2,3},{3,2},{4,5},{5,4},{6,7},{7,6},{8,9},{9,8},{10,11... | collective-permute-start | bytes 6291464 | tf_op jit(solution)/shard_map/ppermute | solution.py:341
  987.0 61.2 %collective-permute-start.97 = (f32[33,128]{1,0:T(8,128)S(1)}, f32[33,128]{1,0:T(8,128)S(1)}, u32[]{:S(2)}, u32[]{:S(2)}) collective-permute-start(f32[33,128]{1,0:T(8,128)S(1)} %bitcast.348), channel_id=1, source_target_pairs={{0,1},{1,0},{2,3},{3,2},{4,5},{5,4},{6,7},{7,6},{8,9},{9,8},{10,11... | collective-permute-start | bytes 50696 | tf_op jit(solution)/shard_map/ppermute | solution.py:341
  992.8 80.5 %collective-permute-start.45 = (bf16[4,256,1024]{2,1,0:T(8,128)(2,1)}, bf16[4,256,1024]{2,1,0:T(8,128)(2,1)S(1)}, u32[]{:S(2)}, u32[]{:S(2)}) collective-permute-start(bf16[4,256,1024]{2,1,0:T(8,128)(2,1)} %get-tuple-element.149), channel_id=1, source_target_pairs={{0,4},{2,6},{4,0},{6,2},{8,12},{10,14},{12,8},{14,10},{16,20},{18,... | collective-permute-start | bytes 6291464 | tf_op jit(solution)/shard_map/ppermute | solution.py:337
  1048.2 50.7 %collective-permute-start.46 = (bf16[4,256,1024]{2,1,0:T(8,128)(2,1)}, bf16[4,256,1024]{2,1,0:T(8,128)(2,1)}, u32[]{:S(2)}, u32[]{:S(2)}) collective-permute-start(bf16[4,256,1024]{2,1,0:T(8,128)(2,1)} %get-tuple-element.148), channel_id=1, source_target_pairs={{0,4},{2,6},{4,0},{6,2},{8,12},{10,14},{12,8},{14,10},{16,20},{18,... | collective-permute-start | bytes 6291464 | tf_op jit(solution)/shard_map/ppermute | solution.py:337
  1050.1 48.7 %collective-permute-start.47 = (bf16[4,256,1024]{2,1,0:T(8,128)(2,1)}, bf16[4,256,1024]{2,1,0:T(8,128)(2,1)}, u32[]{:S(2)}, u32[]{:S(2)}) collective-permute-start(bf16[4,256,1024]{2,1,0:T(8,128)(2,1)} %get-tuple-element.146), channel_id=1, source_target_pairs={{0,1},{1,0},{2,3},{3,2},{4,5},{5,4},{6,7},{7,6},{8,9},{9,8},{10,11... | collective-permute-start | bytes 6291464 | tf_op jit(solution)/shard_map/ppermute | solution.py:341
  1073.4 123.1 %collective-permute-start.77 = (bf16[8,128,2048]{2,1,0:T(8,128)(2,1)}, bf16[8,128,2048]{2,1,0:T(8,128)(2,1)}, u32[]{:S(2)}, u32[]{:S(2)}) collective-permute-start(bf16[8,128,2048]{2,1,0:T(8,128)(2,1)} %dynamic-slice_bitcast_fusion.1), channel_id=1, source_target_pairs={{0,2},{2,0},{4,6},{6,4},{8,10},{10,8},{12,14},{14,12},{16,18},{18,... | collective-permute-start | bytes 12582920 | tf_op jit(solution)/shard_map/ppermute | solution.py:333
  1113.3 34.6 %collective-permute-start.60 = (bf16[256,2048]{1,0:T(8,128)(2,1)}, bf16[256,2048]{1,0:T(8,128)(2,1)}, u32[]{:S(2)}, u32[]{:S(2)}) collective-permute-start(bf16[256,2048]{1,0:T(8,128)(2,1)} %select_convert_fusion), channel_id=1, source_target_pairs={{0,1},{1,0},{2,3},{3,2},{4,5},{5,4},{6,7},{7,6},{8,9},{9,8},{10,11... | collective-permute-start | bytes 3145736 | tf_op jit(solution)/shard_map/ppermute | solution.py:341
  1146.7 99.6 %collective-permute-start.61 = (bf16[8,128,3072]{2,1,0:T(8,128)(2,1)}, bf16[8,128,3072]{2,1,0:T(8,128)(2,1)}, u32[]{:S(2)}, u32[]{:S(2)}) collective-permute-start(bf16[8,128,3072]{2,1,0:T(8,128)(2,1)} %dynamic-slice_bitcast_fusion), channel_id=1, source_target_pairs={{0,2},{2,0},{4,6},{6,4},{8,10},{10,8},{12,14},{14,12},{16,18},{18,... | collective-permute-start | bytes 18874376 | tf_op jit(solution)/shard_map/ppermute | solution.py:333
  1171.9 36.0 %collective-permute-start.58 = (bf16[256,1024]{1,0:T(8,128)(2,1)S(1)}, bf16[256,1024]{1,0:T(8,128)(2,1)S(1)}, u32[]{:S(2)}, u32[]{:S(2)}) collective-permute-start(bf16[256,1024]{1,0:T(8,128)(2,1)S(1)} %get-tuple-element.181), channel_id=1, source_target_pairs={{16,8},{18,10},{20,12},{22,14},{24,16},{26,18},{28,20},{30,22},{17... | collective-permute-start | bytes 1572872 | tf_op jit(solution)/shard_map/ppermute | solution.py:382
  1172.7 45.5 %collective-permute-start.56 = (bf16[256,1024]{1,0:T(8,128)(2,1)S(1)}, bf16[256,1024]{1,0:T(8,128)(2,1)S(1)}, u32[]{:S(2)}, u32[]{:S(2)}) collective-permute-start(bf16[256,1024]{1,0:T(8,128)(2,1)S(1)} %get-tuple-element.180), channel_id=1, source_target_pairs={{0,8},{2,10},{4,12},{6,14},{8,16},{10,18},{12,20},{14,22},{16,24},... | collective-permute-start | bytes 1572872 | tf_op jit(solution)/shard_map/ppermute | solution.py:381
  1223.6 40.0 %collective-permute-start.50 = (bf16[256,1024]{1,0:T(8,128)(2,1)}, bf16[256,1024]{1,0:T(8,128)(2,1)}, u32[]{:S(2)}, u32[]{:S(2)}) collective-permute-start(bf16[256,1024]{1,0:T(8,128)(2,1)} %get-tuple-element.176), channel_id=1, source_target_pairs={{0,8},{2,10},{4,12},{6,14},{8,16},{10,18},{12,20},{14,22},{16,24},... | collective-permute-start | bytes 1572872 | tf_op jit(solution)/shard_map/ppermute | solution.py:381
  1227.5 36.8 %collective-permute-start.53 = (bf16[256,1024]{1,0:T(8,128)(2,1)S(1)}, bf16[256,1024]{1,0:T(8,128)(2,1)}, u32[]{:S(2)}, u32[]{:S(2)}) collective-permute-start(bf16[256,1024]{1,0:T(8,128)(2,1)S(1)} %fusion.50), channel_id=1, source_target_pairs={{8,0},{10,2},{12,4},{14,6},{16,8},{18,10},{20,12},{22,14},{24,16},... | collective-permute-start | bytes 1572872 | tf_op jit(solution)/shard_map/ppermute | solution.py:382
  1287.0 34.6 %collective-permute-start.72 = (bf16[2,128,1536]{2,1,0:T(8,128)(2,1)S(1)}, bf16[2,128,1536]{2,1,0:T(8,128)(2,1)S(1)}, u32[]{:S(2)}, u32[]{:S(2)}) collective-permute-start(bf16[2,128,1536]{2,1,0:T(8,128)(2,1)S(1)} %get-tuple-element.171), channel_id=1, source_target_pairs={{24,16},{26,18},{28,20},{30,22},{25,17},{27,19},{29,21},{31,23}} | collective-permute-start | bytes 2359304 | tf_op jit(solution)/shard_map/ppermute | solution.py:382
  (133 other events, 3134.6 us)
Sparse Core Ops, SparseCore 0:
  15.2 112.6 all-gather.5
  131.4 137.4 all-gather.9
  272.5 265.2 all-gather.7

commit v4 on v3

--- a/solution.py
+++ b/solution.py
@@ -353,74 +353,26 @@
     return lax.dynamic_index_in_dim(values, index, 0, keepdims=False)
 
 
-def halve(values, index, swap):
-    return add_low(take(values, index), swap(take(values, 1 - index)))
-
-
-def line_sum(values, place, relative=False):
+def line_shift(values, step):
+    fsdp = lax.axis_size("fsdp")
+    return lax.ppermute(values, "fsdp", [(i, (i + 4 * step) % fsdp) for i in range(fsdp)])
+
+
+def line_sum(values):
     count = values.shape[0]
-    fsdp = lax.axis_size("fsdp")
-    up = down = None
-
-    def part(at):
-        at = jnp.clip(at, 0, count - 1)
-        return take(values, (place - at) % count if relative else at)
-
+    total = values[0].astype(full)
     for step in range(1, count):
-        pairs_up = [
-            (i, i + 4) for i in range(fsdp - 4) if i // 4 < step
-        ]
-        pairs_down = [
-            (i, i - 4) for i in range(4, fsdp) if count - 1 - i // 4 < step
-        ]
-        send_up = part(count - step + place)
-        send_down = part(place + step - count)
-        if up is not None:
-            send_up = add_low(send_up, up)
-            send_down = add_low(send_down, down)
-        up = lax.ppermute(send_up, "fsdp", pairs_up)
-        down = lax.ppermute(send_down, "fsdp", pairs_down)
-    return part(place).astype(full) + up.astype(full) + down.astype(full)
-
-
-def over_core(keep, send):
-    half = keep.shape[-1] // 2
+        total = total + line_shift(values[count - step], step).astype(full)
+    return total
+
+
+def over_core(keep, send, pieces):
+    step = keep.shape[-1] // pieces
     other = swap_core(send)
-    return add_low(keep[..., :half], other[..., :half]), add_low(keep[..., half:], other[..., half:])
-
-
-def gather_line(values):
-    fsdp = lax.axis_size("fsdp")
-    count = fsdp // 4
-    ups, downs = [values], [values]
-    for _ in range(count - 1):
-        ups.append(lax.ppermute(ups[-1], "fsdp", [(i, i + 4) for i in range(fsdp - 4)]))
-        downs.append(lax.ppermute(downs[-1], "fsdp", [(i, i - 4) for i in range(4, fsdp)]))
-    return jnp.stack([values] + [ups[s] + downs[count - s] for s in range(1, count)])
-
-
-def gather_quarters(values):
-    got = {(0, 0, 0): gather_line(values)}
-    got[1, 0, 0] = swap_side(got[0, 0, 0])
-    for side in range(2):
-        got[side, 1, 0] = swap_ctx(got[side, 0, 0])
-    for side in range(2):
-        for ctx in range(2):
-            got[side, ctx, 1] = swap_core(got[side, ctx, 0])
-    return got
-
-
-def sum_fsdp(values, place, side, core):
-    fsdp = lax.axis_size("fsdp")
-    rows, width = values.shape[0] // fsdp, values.shape[1]
-    parts = values.reshape(fsdp // 2, 2, rows, width).swapaxes(0, 1)
-    mine = halve(parts, core, swap_core).reshape(fsdp // 4, 2, rows, width)
-    half = width // 2
-    one, two = mine[..., :half], mine[..., half:]
-    one = line_sum(halve(one.swapaxes(0, 1), side, swap_side), place)
-    two = line_sum(two, place).astype(low)
-    two = take(two, side).astype(full) + swap_side(take(two, 1 - side)).astype(full)
-    return jnp.concatenate([one, two], axis=-1)
+    return [
+        add_low(keep[..., i * step : (i + 1) * step], other[..., i * step : (i + 1) * step])
+        for i in range(pieces)
+    ]
 
 
 def sum_all(values, fsdp):
@@ -603,7 +555,7 @@
     )(projected, projected, roped_q, roped_k, values_low, grad, cosine, sine, query_gain, key_gain)
 
 
-def expert_kernel(core_ref, order, m_ref, g_ref, g_keep, g_send, w_ref, gu_ref, dn_ref, *refs):
+def expert_kernel(core_ref, order, m_ref, g_ref, g_more, w_ref, gu_ref, dn_ref, *refs):
     (keep_out, send_out, keep_back, send_back, gate_back, rows_ref, dy_ref, z_ref, pair_ref) = refs[-9:]
     core = core_ref[0]
     block = m_ref.shape[3]
@@ -615,7 +567,7 @@
     ).astype(low)
     slot_ids = lax.broadcasted_iota(jnp.int32, (slots, block), 0)
     places, picks, weights, rows, grads = [], [], [], [], []
-    for part, g_more in enumerate((g_keep, g_send)):
+    for part in range(2):
         at = lax.rem(core + part, 2)
         gate = w_ref[0, at, 0]
         hit = jnp.where(gate >= 0.0, 1.0, 0.0)
@@ -628,7 +580,7 @@
         weights.append(jnp.sum(jnp.where(place, gate, 0.0), axis=1, keepdims=True))
         rows.append(mul(pick, m_ref[0, at, 0]).astype(low))
         grads.append(
-            jnp.concatenate([mul(pick, g_ref[0, at, 0]), mul(pick, g_more[0])], axis=1)
+            jnp.concatenate([mul(pick, g_ref[0, at, 0]), mul(pick, g_more[0, at, 0])], axis=1)
         )
     row, grad, weight = (jnp.concatenate(items, axis=0) for items in (rows, grads, weights))
     rows_ref[...] = row
@@ -659,16 +611,22 @@
         out[0] = mul(picks[part], back[mine], lhs_turned).astype(low)
 
 
-def run_expert(core, order, number, parts, m_all, g_all, g_keep, g_send, gates_all, gate_up, down, slots, kept):
+def run_expert(core, order, number, parts, m_all, g_one, g_two, gates_all, gate_up, down, slots, kept):
     places, _, _, block, width = m_all.shape
     paired = gate_up.shape[1]
-    steps = g_keep.shape[0]
+    steps = order.shape[0] // 3
     part_rows = steps * 2 * slots
     hidden = paired // 2
     shape = jax.ShapeDtypeStruct
 
+    def gates_at(i, core, order):
+        return (order[3 * i], 0, order[3 * i + 1], 0, 0)
+
     def token_at(i, core, order):
-        return (order[2 * i], 0, order[2 * i + 1], 0, 0)
+        return (order[3 * i], 0, order[3 * i + 2], 0, 0)
+
+    def half_spec(index):
+        return pl.BlockSpec((1, 2, 1, block, width // 2), lambda i, core, order: (order[3 * i], 0, index, 0, 0))
 
     def fixed(i, core, order):
         return (0, 0)
@@ -679,7 +637,7 @@
     def stacked(i, core, order):
         return (i, 0, 0)
 
-    small = pl.BlockSpec((1, 2, 1, 1, block), token_at)
+    small = pl.BlockSpec((1, 2, 1, 1, block), gates_at)
     one_block = pl.BlockSpec((1, block, width), stacked)
     widths = (width, width, hidden, paired)
     grid_spec = pltpu.PrefetchScalarGridSpec(
@@ -687,10 +645,7 @@
         grid=(steps,),
         in_specs=[
             pl.BlockSpec((1, 2, 1, block, width), token_at),
-            pl.BlockSpec((1, 2, 1, block, g_all.shape[4]), token_at),
-            pl.BlockSpec((1, block, g_keep.shape[2]), stacked),
-            pl.BlockSpec((1, block, g_keep.shape[2]), stacked),
-            small,
+            half_spec(g_one[1]), half_spec(g_two[1]), small,
             pl.BlockSpec(gate_up.shape, fixed, pipeline_mode=pl.Buffered(1)),
             pl.BlockSpec(down.shape, fixed, pipeline_mode=pl.Buffered(1)),
         ]
@@ -703,7 +658,7 @@
         out_shape=[shape((steps, block, width), low)] * 4
         + [shape((places, 2, 2, 1, block), full)]
         + [shape((parts * part_rows, n), low) for n in widths],
-        input_output_aliases={} if kept is None else {9 + i: 4 + i for i in range(5)},
+        input_output_aliases={} if kept is None else {8 + i: 4 + i for i in range(5)},
         compiler_params=pltpu.CompilerParams(vmem_limit_bytes=vmem_bytes),
         cost_estimate=pl.CostEstimate(
             flops=part_rows * width * (4 * paired + 4 * hidden + 8 * block),
@@ -711,7 +666,7 @@
             transcendentals=part_rows * hidden,
         ),
         name="experts",
-    )(core, order, m_all, g_all, g_keep, g_send, gates_all, gate_up, down, *(() if kept is None else kept))
+    )(core, order, m_all, g_one[0], g_two[0], gates_all, gate_up, down, *(() if kept is None else kept))
 
 
 def rms_back(values, gain, grad):
@@ -774,8 +729,13 @@
     attn_all = small_all[:, experts_all].astype(full)
     moe_all = small_all[:, experts_all + 1].astype(full)
     g_half = width // 2
-    g_all = lax.all_gather(cotangent[:, :g_half], both, axis=0)
-    g_parts = gather_quarters(cotangent[:, g_half:])
+    g_local = jnp.stack(
+        [cotangent[:, :g_half], cotangent[:, g_half:], swap_ctx(cotangent[:, g_half:])]
+    )
+    g_all = lax.all_gather(
+        g_local.reshape(3 * rows_dev, g_half), "fsdp", axis=0, tiled=True
+    ).reshape(fsdp // 2, 2, 3, rows_dev, g_half)
+    g_far = swap_ctx(g_all[:, :, :1])
 
     sequence_in = sequence(tokens).astype(full)
     low_in = rms_scale(sequence_in, attn_all).astype(low)
@@ -794,7 +754,7 @@
         + swap_ctx(of_block(branch, 1 - rank).astype(low)).astype(full)
     )
     low_mid = rms_scale(mixed, moe_all).astype(low)
-    m_all = lax.all_gather(low_mid, both, axis=0)
+    m_all = lax.all_gather(jnp.concatenate([low_mid, swap_ctx(low_mid)]), "fsdp", axis=0, tiled=True)
 
     logits = mul(low_mid, router_all)
     named = routes[:, :, None] == jnp.arange(experts_all, dtype=jnp.int32)[None, None, :]
@@ -808,52 +768,72 @@
     lines = fsdp // 4
     grid_of = (fsdp // 2, 2, 2)
     lines_at = (place - jnp.arange(lines, dtype=jnp.int32)) % lines
-    kept, back, out, wait = None, {}, {}, None
+    kept, back, out = None, {}, {}
     core_at = core[None].astype(jnp.int32)
     for number, at in enumerate(((1, 1), (0, 1), (1, 0), (0, 0))):
         d_side, d_ctx = at
         order = jnp.stack(
-            [lines_at * 2 + (side + d_side) % 2, jnp.broadcast_to((rank + d_ctx) % 2, (lines,))], axis=1
+            [
+                lines_at * 2 + (side + d_side) % 2,
+                jnp.broadcast_to((rank + d_ctx) % 2, (lines,)),
+                jnp.full((lines,), d_ctx),
+            ],
+            axis=1,
         ).reshape(-1)
+        if number == 1:
+            core_at, back[1, 1] = hold(core_at, back[1, 1])
         if number == 2:
-            core_at, back[1, 1] = hold(core_at, back[1, 1])
+            far_ctx = swap_ctx(jnp.concatenate(back[1, 1][:2], axis=-1))
+            far_side = swap_side(jnp.concatenate(back[1, 1][2:], axis=-1))
+            core_at, (far_ctx, far_side) = hold(core_at, (far_ctx, far_side))
         if number == 3:
-            far_ctx, far_side = swap_ctx(back[1, 1][0]), swap_side(back[1, 1][1])
-            core_at, (back[0, 1], far_ctx, far_side) = hold(core_at, (back[0, 1], far_ctx, far_side))
+            core_at, (back[0, 1], back[1, 0]) = hold(core_at, (back[0, 1], back[1, 0]))
         keep_out, send_out, keep_back, send_back, *kept = run_expert(
             core_at,
             order.astype(jnp.int32),
             number,
             4,
             m_all.reshape(*grid_of, rows_dev, width),
-            g_all.reshape(*grid_of, rows_dev, g_half),
-            g_parts[d_side, d_ctx, 0],
-            g_parts[d_side, d_ctx, 1],
+            (g_far, 0) if d_ctx else (g_all, 0),
+            (g_all, 1 + d_ctx),
             gates_all.reshape(*grid_of, 1, rows_dev),
             expert_gate_up[0],
             expert_down[0],
             capacity,
             kept,
         )
-        back[at] = over_core(keep_back, send_back)
+        back[at] = over_core(keep_back, send_back, 4)
         out[at] = (keep_out, send_out)
     gate_back, rows, grad_rows, hidden, grad_pair = kept
     grad_gates = lax.all_to_all(
         gate_back.reshape(fsdp * 2, rows_dev), both, split_axis=0, concat_axis=0, tiled=True
     ).T
-    one_ctx, two_side = swap_ctx(back[0, 1][0]), swap_side(back[1, 0][1])
-    one_side = swap_side(add_low(back[1, 0][0], far_ctx))
-    two_ctx = swap_ctx(add_low(back[0, 1][1], far_side))
-    one_mine = add_low(add_low(back[0, 0][0], one_ctx), one_side)
-    two_mine = add_low(add_low(back[0, 0][1], two_side), two_ctx)
-    two_sum = line_sum(two_mine, place, relative=True)
-    one_sum = line_sum(one_mine, place, relative=True)
-    grad_mid = jnp.concatenate([one_sum, two_sum], axis=-1)
-    out = {at: over_core(*out[at]) for at in out}
-    out_far_ctx, out_far_side = swap_ctx(out[1, 1][0]), swap_side(out[1, 1][1])
-    grad_mid, (out_far_ctx, out_far_side) = hold(grad_mid, (out_far_ctx, out_far_side))
+    cut = far_ctx.shape[-1] // 2
     grad_down = mul(hidden, grad_rows, lhs_turned)[None]
     grad_gate_up = mul(rows, grad_pair, lhs_turned)[None]
+    sums = []
+    for k in range(2):
+        cols = slice(k * cut, (k + 1) * cut)
+        from_ctx, from_side = swap_ctx(back[0, 1][k]), swap_side(back[1, 0][2 + k])
+        one_side = swap_side(add_low(back[1, 0][k], far_ctx[..., cols]))
+        two_ctx = swap_ctx(add_low(back[0, 1][2 + k], far_side[..., cols]))
+        both_mine = jnp.concatenate(
+            [
+                add_low(add_low(back[0, 0][k], from_ctx), one_side),
+                add_low(add_low(back[0, 0][2 + k], from_side), two_ctx),
+            ],
+            axis=-1,
+        )
+        if k == 1:
+            both_mine, (grad_down, grad_gate_up) = hold(both_mine, (grad_down, grad_gate_up))
+        sums.append(line_sum(both_mine))
+    out, last_round = hold(out, (one_side, two_ctx))
+    out = {at: over_core(*out[at], 2) for at in out}
+    out_far_ctx, out_far_side = swap_ctx(out[1, 1][0]), swap_side(out[1, 1][1])
+    sums, (out_far_ctx, out_far_side) = hold(sums, (out_far_ctx, out_far_side))
+    grad_mid = jnp.concatenate(
+        [sums[0][:, :cut], sums[1][:, :cut], sums[0][:, cut:], sums[1][:, cut:]], axis=-1
+    )
 
     grad_wide = jnp.where(chosen, grad_gates, 0.0)
     grad_logits = (
@@ -867,6 +847,7 @@
     grad_branch = sequence(grad_mixed.astype(low))
     grad_attended = mul(grad_branch, out_all, rhs_turned).astype(low)
     grad_out_part = mul(attended, grad_branch, lhs_turned).astype(low)
+    out, grad_branch = hold(out, grad_branch)
     out_ctx, out_side = swap_ctx(out[0, 1][0]), swap_side(out[1, 0][1])
     grad_attended, (out_ctx, out_side) = hold(grad_attended, (out_ctx, out_side))
     grad_q, grad_k, grad_v, gain_q_part, gain_k_part = attend_grad(
@@ -881,7 +862,7 @@
     output = (
         mixed
         + jnp.concatenate(
-            [line_sum(one_mine, place, relative=True), line_sum(two_mine, place, relative=True)], axis=-1
+            [line_sum(one_mine), line_sum(two_mine)], axis=-1
         )
     ).astype(low)
     grad_qkv_part = mul(low_in, grad_projected, lhs_turned).astype(low)
@@ -892,14 +873,14 @@
     grad_in_part, grad_attn_gain = rms_back(inputs, attn_all, grad_normed)
     grad_tokens = grad_mixed + grad_in_part
 
-    out_mine = sum_fsdp(grad_out_part, place, side, core)
+    out_mine = lax.psum_scatter(grad_out_part, "fsdp", scatter_dimension=0, tiled=True).astype(full)
     out_other = swap_ctx(out_mine.astype(low)).astype(full)
     grad_out = jnp.where(
         rank == 0,
         jnp.concatenate([out_mine, out_other], axis=0),
         jnp.concatenate([out_other, out_mine], axis=0),
     )
-    qkv_mine = sum_fsdp(grad_qkv_part, place, side, core)
+    qkv_mine = lax.psum_scatter(grad_qkv_part, "fsdp", scatter_dimension=0, tiled=True).astype(full)
     qkv_other = swap_ctx(qkv_mine.astype(low)).astype(full)
     q_mine = qkv_mine[:, :width_q].reshape(shard, my_heads, 1, head_dim)
     q_other = qkv_other[:, :width_q].reshape(shard, my_heads, 1, head_dim)

time: 1410 us -> 1250 us (0.89)
  waiting for transfers between devices: 689 us -> 627 us
  starting transfers between devices: 192 us -> 152 us
  other arithmetic: 116 us -> 81.8 us
    all_to_all x1, waiting for transfers between devices: 0.01 us -> 175 us  [body_gathered(): lax.all_to_all(gates_sent, both, split_axis=0, concat_axis=0, tiled=True)]
    ppermute x16 -> x19, waiting for transfers between devices: 279 us -> 164 us  [swap_ctx(): return lax.ppermute(values, 'ctx', [(0, 1), (1, 0)])]
    ppermute x11 -> x8, waiting for transfers between devices: 127 us -> 50.2 us  [swap_side(): return lax.ppermute(values, 'fsdp', side_pairs(lax.axis_size('fsdp')))]
    ppermute x54 -> x12, starting transfers between devices: 144 us -> 70.9 us  [line_shift(): lax.ppermute(values, 'fsdp', [(i, (i + 4 * step) % fsdp) for i in range(f...]
    ppermute x54 -> x12, waiting for transfers between devices: 160 us -> 97.4 us  [line_shift(): lax.ppermute(values, 'fsdp', [(i, (i + 4 * step) % fsdp) for i in range(f...]
    convert_element_type x37 -> x14, other arithmetic: 85.3 us -> 47.5 us  [add_low(): return (one.astype(full) + two.astype(full)).astype(low)]
    ppermute x3, starting transfers between devices: 3.21 us -> 24.8 us  [sum_all(): lax.ppermute(values, 'fsdp', [(i, i ^ step) for i in range(fsdp)])]
    ppermute x14 -> x8, waiting for transfers between devices: 0.04 us -> 21 us  [swap_core(): return lax.ppermute(values, 'fsdp', core_pairs(lax.axis_size('fsdp')))]
  transfers between devices with their start and end apart: 108 -> 62, of which waited for: 43 -> 36; matrix products, arithmetic and copies ran while one was open for 18% -> 15% of each run, Pallas kernels for 14% -> 13%
where the time goes in v4:
time: 1250 us
  waiting for transfers between devices  627 us (50%)
  Pallas kernels  197 us (16%)
  starting transfers between devices  152 us (12%)
  matrix products  111 us (9%)
  other arithmetic  81.8 us (7%)
  local copies, waits for them, and re-layouts  43.7 us (3%)
  blocking collectives  23.2 us (2%)
  between operations  15.3 us (1%)
    all_to_all x1, waiting for transfers between devices, body_gathered(): lax.all_to_all(gates_sent, both, split_axis=0, concat_axis=0, tiled=True)  175 us
    ppermute x19, waiting for transfers between devices, swap_ctx(): return lax.ppermute(values, 'ctx', [(0, 1), (1, 0)])  164 us
    pallas_call x4, Pallas kernels, run_expert(): pl.pallas_call(expert_kernel, grid_spec=grid_spec, out_shape=[shape((step...  153 us
    dot_general x11, matrix products, mul(): return lax.dot_general(left, right, dims, preferred_element_type=full)  111 us
    ppermute x12, waiting for transfers between devices, line_shift(): lax.ppermute(values, 'fsdp', [(i, (i + 4 * step) % fsdp) for i in range(f...  97.4 us
    ppermute x12, starting transfers between devices, line_shift(): lax.ppermute(values, 'fsdp', [(i, (i + 4 * step) % fsdp) for i in range(f...  70.9 us
    all_gather x1, waiting for transfers between devices, body_gathered(): weights_all = lax.all_gather(weights_local, 'fsdp', axis=0, tiled=True)  66.7 us
    ppermute x8, waiting for transfers between devices, swap_side(): return lax.ppermute(values, 'fsdp', side_pairs(lax.axis_size('fsdp')))  50.2 us
  transfers between devices with their start and end apart: 62, of which 36 were waited for; matrix products, arithmetic and copies ran while one was open for 15% of the time, Pallas kernels for 13%

profile of v4, /device:TPU:0, one launch (start us, length us, event | category | flops | bytes accessed | tf_op | source)
XLA Modules:
  0.0 1251.2 jit_solution(3793714162286208544)
XLA Ops:
  18.2 11.9 collective-permute-done.3
  34.8 23.2 %all_gather.12 = bf16[2048,34]{0,1:T(8,128)(2,1)S(1)} all-gather(bf16[128,34]{0,1:T(8,128)(2,1)S(1)} %pad_maximum_fusion.16), channel_id=1, replica_groups=mesh['fsdp'=16,'ctx'=2] {'fsdp'}, dimensions={0}, use_global_device_ids=true | all-gather | bytes 147968 | tf_op jit(solution)/shard_map/all_gather | solution.py:724
  61.4 66.7 %all-gather.4.cloned.1.call-done = bf16[2048,5120]{1,0:T(8,128)(2,1)} async-done(((bf16[128,5120]{1,0:T(8,128)(2,1)}), bf16[2048,5120]{1,0:T(8,128)(2,1)}) %all-gather.4.cloned.1.call-update) | async-done | bytes 20971536 | tf_op jit(solution)/shard_map/all_gather | solution.py:725
  128.0 11.6 fusion.2.q_ref.k_ref.v_ref
  139.6 18.3 %attend.1 = (bf16[512,2048]{1,0:T(8,128)(2,1)S(1)}, bf16[512,2048]{1,0:T(8,128)(2,1)S(1)}, bf16[512,512]{1,0:T(8,128)(2,1)S(1)}, bf16[512,512]{1,0:T(8,128)(2,1)S(1)}) custom-call(f32[512,3072]{1,0:T(8,128)} %fusion.2.q_ref.k_ref.v_ref, f32[512,3072]{1,0:T(8,128)} %fusion.2.q_ref.k_ref.v_ref, f32[512,3072]{1,0:T(8,128)} %fusion.2.q_ref.k_ref.v_ref, ...), custom_call_target="tpu_custom_call" | custom-call | flops 2147483648 | bytes 9437184 | tf_op jit(solution)/shard_map/attend/pallas_call | solution.py:510
  157.9 8.5 fusion.6
  168.5 24.0 %collective-permute-done.1 = bf16[256,2048]{1,0:T(8,128)(2,1)S(1)} collective-permute-done((bf16[256,2048]{1,0:T(8,128)(2,1)S(1)}, bf16[256,2048]{1,0:T(8,128)(2,1)S(1)}, u32[]{:S(2)}, u32[]{:S(2)}) %collective-permute-start.1) | collective-permute-done | bytes 1048608 | tf_op jit(solution)/shard_map/ppermute | solution.py:341
  197.0 23.2 %collective-permute-done.2 = bf16[256,2048]{1,0:T(8,128)(2,1)S(1)} collective-permute-done((bf16[256,2048]{1,0:T(8,128)(2,1)S(1)}, bf16[256,2048]{1,0:T(8,128)(2,1)S(1)}, u32[]{:S(2)}, u32[]{:S(2)}) %collective-permute-start.2) | collective-permute-done | bytes 1048608 | tf_op jit(solution)/shard_map/ppermute | solution.py:341
  221.8 37.3 %all-gather.8.cloned.1.call-done = bf16[12288,1024]{1,0:T(8,128)(2,1)} async-done(((bf16[768,1024]{1,0:T(8,128)(2,1)}), bf16[12288,1024]{1,0:T(8,128)(2,1)}) %all-gather.8.cloned.1.call-update) | async-done | bytes 25165840 | tf_op jit(solution)/shard_map/all_gather | solution.py:735
  259.1 8.1 slice.440
  275.7 175.3 %all-to-all-done = f32[32,1,256]{2,1,0:T(1,128)S(1)} async-done(((f32[32,1,256]{2,1,0:T(1,128)}), f32[32,1,256]{2,1,0:T(1,128)S(1)}, u32[]{:S(2)}, u32[]{:S(2)}) %all-to-all-start) | async-done | bytes 32800 | tf_op jit(solution)/shard_map/all_to_all | solution.py:766
  451.6 37.9 %experts.4 = (bf16[4,256,2048]{2,1,0:T(8,128)(2,1)}, bf16[4,256,2048]{2,1,0:T(8,128)(2,1)}, bf16[4,256,2048]{2,1,0:T(8,128)(2,1)}, bf16[4,256,2048]{2,1,0:T(8,12...) custom-call(s32[1]{0:T(128)} %bitcast.5.core_ref, ...), custom_call_target="tpu_custom_call" | custom-call | flops 23622320128 | bytes 46661632 | tf_op jit(solution)/shard_map/experts/pallas_call | solution.py:655
  490.8 6.3 collective-permute-done.5
  506.7 38.3 %experts.5 = (bf16[4,256,2048]{2,1,0:T(8,128)(2,1)}, bf16[4,256,2048]{2,1,0:T(8,128)(2,1)}, bf16[4,256,2048]{2,1,0:T(8,128)(2,1)}, bf16[4,256,2048]{2,1,0:T(8,12...) custom-call(s32[1]{0:T(128)} %bitcast.5.core_ref, ...), custom_call_target="tpu_custom_call", output_to_operand_aliasing={{4}: (8, {}), {5}: (9, {}), {6}: (10, {}), {7}: (11, {}), {... | custom-call | flops 23622320128 | bytes 46661632 | tf_op jit(solution)/shard_map/experts/pallas_call | solution.py:655
  545.1 5.6 collective-permute-done.7
  552.8 38.5 %experts.6 = (bf16[4,256,2048]{2,1,0:T(8,128)(2,1)}, bf16[4,256,2048]{2,1,0:T(8,128)(2,1)}, bf16[4,256,2048]{2,1,0:T(8,128)(2,1)}, bf16[4,256,2048]{2,1,0:T(8,12...) custom-call(s32[1]{0:T(128)} %bitcast.5.core_ref, ...), custom_call_target="tpu_custom_call", output_to_operand_aliasing={{4}: (8, {}), {5}: (9, {}), {6}: (10, {}), {7}: (11, {}), {... | custom-call | flops 23622320128 | bytes 46661632 | tf_op jit(solution)/shard_map/experts/pallas_call | solution.py:655
  592.0 5.0 add_convert_fusion.34
  598.9 4.4 add_convert_fusion.30
  612.5 38.5 %experts.7 = (bf16[4,256,2048]{2,1,0:T(8,128)(2,1)}, bf16[4,256,2048]{2,1,0:T(8,128)(2,1)}, bf16[4,256,2048]{2,1,0:T(8,128)(2,1)}, bf16[4,256,2048]{2,1,0:T(8,12...) custom-call(s32[1]{0:T(128)} %bitcast.5.core_ref, ...), custom_call_target="tpu_custom_call", output_to_operand_aliasing={{4}: (8, {}), {5}: (9, {}), {6}: (10, {}), {7}: (11, {}), {... | custom-call | flops 23622320128 | bytes 46661632 | tf_op jit(solution)/shard_map/experts/pallas_call | solution.py:655
  658.9 17.4 %collective-permute-done.17 = bf16[4,256,512]{2,1,0:T(8,128)(2,1)} collective-permute-done((bf16[4,256,512]{2,1,0:T(8,128)(2,1)}, bf16[4,256,512]{2,1,0:T(8,128)(2,1)}, u32[]{:S(2)}, u32[]{:S(2)}) %collective-permute-start.17) | collective-permute-done | bytes 1048608 | tf_op jit(solution)/shard_map/ppermute | solution.py:341
  676.3 35.1 %convolution_bitcast_fusion = f32[1,2048,1536]{2,1,0:T(8,128)} fusion(bf16[4096,2048]{1,0:T(8,128)(2,1)} %get-tuple-element.159, bf16[4096,1536]{1,0:T(8,128)(2,1)} %get-tuple-element.160), kind=kOutput, calls=%fused_computation.5 | convolution fusion | flops 25769803776 | bytes 41943040 | tf_op jit(solution)/shard_map/dot_general | solution.py:321
  712.7 5.9 add_convert_fusion.17
  725.2 4.3 add_convert_fusion.6
  732.2 16.5 %convolution_bitcast_fusion.1 = f32[1,768,2048]{2,1,0:T(8,128)} fusion(bf16[4096,768]{1,0:T(8,128)(2,1)} %get-tuple-element.157, bf16[4096,2048]{1,0:T(8,128)(2,1)S(1)} %bitcast.168), kind=kOutput, calls=%fused_computation.30 | convolution fusion | flops 12884901888 | bytes 29360128 | tf_op jit(solution)/shard_map/dot_general | solution.py:321
  752.9 6.2 collective-permute-done.22
  759.5 29.3 %collective-permute-start.28 = (bf16[256,1024]{1,0:T(8,128)(2,1)}, bf16[256,1024]{1,0:T(8,128)(2,1)}, u32[]{:S(2)}, u32[]{:S(2)}) collective-permute-start(bf16[256,1024]{1,0:T(8,128)(2,1)} %get-tuple-element.235), channel_id=1, source_target_pairs={{0,24},{2,26},{4,28},{6,30},{8,0},{10,2},{12,4},{14,6},{16,8},{18,... | collective-permute-start | bytes 1572872 | tf_op jit(solution)/shard_map/ppermute | solution.py:358
  790.4 13.3 %collective-permute-done.27 = bf16[256,1024]{1,0:T(8,128)(2,1)} collective-permute-done((bf16[256,1024]{1,0:T(8,128)(2,1)}, bf16[256,1024]{1,0:T(8,128)(2,1)}, u32[]{:S(2)}, u32[]{:S(2)}) %collective-permute-start.27) | collective-permute-done | bytes 524320 | tf_op jit(solution)/shard_map/ppermute | solution.py:358
  803.7 5.5 collective-permute-done.28
  816.3 23.3 %collective-permute-done.31 = bf16[256,2048]{1,0:T(8,128)(2,1)S(1)} collective-permute-done((bf16[256,2048]{1,0:T(8,128)(2,1)S(1)}, bf16[256,2048]{1,0:T(8,128)(2,1)S(1)}, u32[]{:S(2)}, u32[]{:S(2)}) %collective-permute-start.31) | collective-permute-done | bytes 1048608 | tf_op jit(solution)/shard_map/ppermute | solution.py:341
  842.0 6.9 convolution_convert_fusion.1
  849.6 6.8 collective-permute-done.14
  882.4 9.5 fusion.11.go_ref
  891.9 29.3 %collective-permute-done.32 = bf16[4,256,1024]{2,1,0:T(8,128)(2,1)S(1)} collective-permute-done((bf16[4,256,1024]{2,1,0:T(8,128)(2,1)}, bf16[4,256,1024]{2,1,0:T(8,128)(2,1)S(1)}, u32[]{:S(2)}, u32[]{:S(2)}) %collective-permute-start.32) | collective-permute-done | bytes 2097184 | tf_op jit(solution)/shard_map/ppermute | solution.py:341
  921.3 15.4 %collective-permute-done.33 = bf16[4,256,1024]{2,1,0:T(8,128)(2,1)S(1)} collective-permute-done((bf16[4,256,1024]{2,1,0:T(8,128)(2,1)S(1)}, bf16[4,256,1024]{2,1,0:T(8,128)(2,1)S(1)}, u32[]{:S(2)}, u32[]{:S(2)}) %collective-permute-start.33) | collective-permute-done | bytes 2097184 | tf_op jit(solution)/shard_map/ppermute | solution.py:337
  936.7 25.8 %attend_grad.1 = (bf16[512,2048]{1,0:T(8,128)(2,1)S(1)}, bf16[512,512]{1,0:T(8,128)(2,1)S(1)}, bf16[512,512]{1,0:T(8,128)(2,1)S(1)}, f32[4,1,128]{2,1,0:T(1,128)S(1)}, f32[4,1,128]{2,1,0:T(1,128)S(1)}) custom-call(f32[512,3072]{1,0:T(8,128)} %fusion.2.q_ref.k_ref.v_ref, f32[512,3072]{1,0:T(8,128)} %fusion.2.q_ref.k_ref.v_ref, bf16[512,2048]{1,0:T(8,128)(2,1)} %copy-done.2, ...), custom_call_target="tpu_custom_call" | custom-call | flops 5368709120 | bytes 15728640 | tf_op jit(solution)/shard_map/attend_grad/pallas_call | solution.py:534
  965.4 29.2 %collective-permute-done.34 = bf16[4,256,1024]{2,1,0:T(8,128)(2,1)} collective-permute-done((bf16[4,256,1024]{2,1,0:T(8,128)(2,1)S(1)}, bf16[4,256,1024]{2,1,0:T(8,128)(2,1)}, u32[]{:S(2)}, u32[]{:S(2)}) %collective-permute-start.34) | collective-permute-done | bytes 2097184 | tf_op jit(solution)/shard_map/ppermute | solution.py:337
  994.6 9.9 convolution_convert_fusion
  1006.1 6.3 collective-permute-start.45
  1032.3 11.3 fusion
  1056.6 12.1 collective-permute-done.42
  1073.1 4.3 collective-permute-done.36
  1077.4 26.5 %collective-permute-start.40 = (bf16[256,1024]{1,0:T(8,128)(2,1)S(1)}, bf16[256,1024]{1,0:T(8,128)(2,1)S(1)}, u32[]{:S(2)}, u32[]{:S(2)}) collective-permute-start(bf16[256,1024]{1,0:T(8,128)(2,1)S(1)} %get-tuple-element.231), channel_id=1, source_target_pairs={{0,16},{2,18},{4,20},{6,22},{8,24},{10,26},{12,28},{14,30},{16,0},... | collective-permute-start | bytes 1572872 | tf_op jit(solution)/shard_map/ppermute | solution.py:358
  1103.9 10.6 collective-permute-done.37
  1121.4 21.9 %collective-permute-done.39 = bf16[256,1024]{1,0:T(8,128)(2,1)S(1)} collective-permute-done((bf16[256,1024]{1,0:T(8,128)(2,1)S(1)}, bf16[256,1024]{1,0:T(8,128)(2,1)S(1)}, u32[]{:S(2)}, u32[]{:S(2)}) %collective-permute-start.39) | collective-permute-done | bytes 524320 | tf_op jit(solution)/shard_map/ppermute | solution.py:358
  1143.2 32.6 %collective-permute-done.40 = bf16[256,1024]{1,0:T(8,128)(2,1)S(1)} collective-permute-done((bf16[256,1024]{1,0:T(8,128)(2,1)S(1)}, bf16[256,1024]{1,0:T(8,128)(2,1)S(1)}, u32[]{:S(2)}, u32[]{:S(2)}) %collective-permute-start.40) | collective-permute-done | bytes 524320 | tf_op jit(solution)/shard_map/ppermute | solution.py:358
  1177.2 23.6 %collective-permute-start.53 = (f32[18,128]{1,0:T(8,128)S(1)}, f32[18,128]{1,0:T(8,128)S(1)}, u32[]{:S(2)}, u32[]{:S(2)}) collective-permute-start(f32[18,128]{1,0:T(8,128)S(1)} %add.473), channel_id=1, source_target_pairs={{0,8},{2,10},{4,12},{6,14},{8,0},{10,2},{12,4},{14,6},{16,24},{18,... | collective-permute-start | bytes 27656 | tf_op jit(solution)/shard_map/ppermute | solution.py:383
  1205.1 5.3 fusion.20
  1218.6 15.0 %collective-permute-done.43 = bf16[128,3072]{1,0:T(8,128)(2,1)S(1)} collective-permute-done((bf16[128,3072]{1,0:T(8,128)(2,1)}, bf16[128,3072]{1,0:T(8,128)(2,1)S(1)}, u32[]{:S(2)}, u32[]{:S(2)}) %collective-permute-start.43) | collective-permute-done | bytes 786464 | tf_op jit(solution)/shard_map/ppermute | solution.py:341
  (375 shorter events, 194.4 us)
Async XLA Ops:
  7.2 120.8 %all-gather.4.cloned.1.call-start = ((), (), s32[]{:S(2)}) async-start(), calls=%async_computation.4 | async-start | bytes 22282240 | tf_op jit(solution)/shard_map/all_gather | solution.py:725
  15.0 244.0 %all-gather.8.cloned.1.call-start = ((), (), s32[]{:S(2)}) async-start(), calls=%async_computation.6 | async-start | bytes 26738688 | tf_op jit(solution)/shard_map/all_gather | solution.py:735
  31.5 419.5 %all-gather.6.cloned.1.call-start = ((), (), s32[]{:S(2)}) async-start(), calls=%async_computation.5 | async-start | bytes 35651584 | tf_op jit(solution)/shard_map/all_gather | solution.py:757
  31.7 26.6 %collective-permute-start = (bf16[256,2048]{1,0:T(8,128)(2,1)S(1)}, bf16[256,2048]{1,0:T(8,128)(2,1)}, u32[]{:S(2)}, u32[]{:S(2)}) collective-permute-start(bf16[256,2048]{1,0:T(8,128)(2,1)S(1)} %copy-done.7), channel_id=1, source_target_pairs={{0,1},{1,0},{2,3},{3,2},{4,5},{5,4},{6,7},{7,6},{8,9},{9,8},{10,11... | collective-permute-start | bytes 3145736 | tf_op jit(solution)/shard_map/ppermute | solution.py:341
  167.0 25.5 %collective-permute-start.1 = (bf16[256,2048]{1,0:T(8,128)(2,1)S(1)}, bf16[256,2048]{1,0:T(8,128)(2,1)S(1)}, u32[]{:S(2)}, u32[]{:S(2)}) collective-permute-start(bf16[256,2048]{1,0:T(8,128)(2,1)S(1)} %select_convert_fusion.1), channel_id=1, source_target_pairs={{0,1},{1,0},{2,3},{3,2},{4,5},{5,4},{6,7},{7,6},{8,9},{9,8},{10,11... | collective-permute-start | bytes 3145736 | tf_op jit(solution)/shard_map/ppermute | solution.py:341
  195.4 24.8 %collective-permute-start.2 = (bf16[256,2048]{1,0:T(8,128)(2,1)S(1)}, bf16[256,2048]{1,0:T(8,128)(2,1)S(1)}, u32[]{:S(2)}, u32[]{:S(2)}) collective-permute-start(bf16[256,2048]{1,0:T(8,128)(2,1)S(1)} %multiply_convert_fusion), channel_id=1, source_target_pairs={{0,1},{1,0},{2,3},{3,2},{4,5},{5,4},{6,7},{7,6},{8,9},{9,8},{10,11... | collective-permute-start | bytes 3145736 | tf_op jit(solution)/shard_map/ppermute | solution.py:341
  267.2 183.8 %collective-permute-start.4 = (bf16[8,2,1,256,1024]{4,3,2,1,0:T(8,128)(2,1)}, bf16[8,2,1,256,1024]{4,3,2,1,0:T(8,128)(2,1)}, u32[]{:S(2)}, u32[]{:S(2)}) collective-permute-start(bf16[8,2,1,256,1024]{4,3,2,1,0:T(8,128)(2,1)} %slice.440), channel_id=1, source_target_pairs={{0,1},{1,0},{2,3},{3,2},{4,5},{5,4},{6,7},{7,6},{8,9},{9,8},{10,11... | collective-permute-start | bytes 25165832 | tf_op jit(solution)/shard_map/ppermute | solution.py:341
  270.8 180.2 %all-to-all-start = ((f32[32,1,256]{2,1,0:T(1,128)}), f32[32,1,256]{2,1,0:T(1,128)S(1)}, u32[]{:S(2)}, u32[]{:S(2)}) async-start(f32[32,1,256]{2,1,0:T(1,128)} %copy.84), calls=%async_computation | async-start | bytes 65536 | tf_op jit(solution)/shard_map/all_to_all | solution.py:766
  502.8 47.9 %collective-permute-start.7 = (bf16[4,256,1024]{2,1,0:T(8,128)(2,1)}, bf16[4,256,1024]{2,1,0:T(8,128)(2,1)S(1)}, u32[]{:S(2)}, u32[]{:S(2)}) collective-permute-start(bf16[4,256,1024]{2,1,0:T(8,128)(2,1)} %pad_maximum_fusion.6), channel_id=1, source_target_pairs={{0,4},{2,6},{4,0},{6,2},{8,12},{10,14},{12,8},{14,10},{16,20},{18,... | collective-permute-start | bytes 6291464 | tf_op jit(solution)/shard_map/ppermute | solution.py:337
  505.2 47.6 %collective-permute-start.6 = (bf16[4,256,1024]{2,1,0:T(8,128)(2,1)}, bf16[4,256,1024]{2,1,0:T(8,128)(2,1)S(1)}, u32[]{:S(2)}, u32[]{:S(2)}) collective-permute-start(bf16[4,256,1024]{2,1,0:T(8,128)(2,1)} %pad_maximum_fusion.5), channel_id=1, source_target_pairs={{0,1},{1,0},{2,3},{3,2},{4,5},{5,4},{6,7},{7,6},{8,9},{9,8},{10,11... | collective-permute-start | bytes 6291464 | tf_op jit(solution)/shard_map/ppermute | solution.py:341
  545.0 47.0 %collective-permute-start.8 = (bf16[4,256,2048]{2,1,0:T(8,128)(2,1)}, bf16[4,256,2048]{2,1,0:T(8,128)(2,1)}, u32[]{:S(2)}, u32[]{:S(2)}) collective-permute-start(bf16[4,256,2048]{2,1,0:T(8,128)(2,1)} %get-tuple-element.115), channel_id=1, source_target_pairs={{0,2},{2,0},{4,6},{6,4},{8,10},{10,8},{12,14},{14,12},{16,18},{18,... | collective-permute-start | bytes 12582920 | tf_op jit(solution)/shard_map/ppermute | solution.py:333
  605.0 46.0 %collective-permute-start.11 = (bf16[4,256,512]{2,1,0:T(8,128)(2,1)S(1)}, bf16[4,256,512]{2,1,0:T(8,128)(2,1)}, u32[]{:S(2)}, u32[]{:S(2)}) collective-permute-start(bf16[4,256,512]{2,1,0:T(8,128)(2,1)S(1)} %get-tuple-element.239), channel_id=1, source_target_pairs={{0,1},{1,0},{2,3},{3,2},{4,5},{5,4},{6,7},{7,6},{8,9},{9,8},{10,11... | collective-permute-start | bytes 3145736 | tf_op jit(solution)/shard_map/ppermute | solution.py:341
  608.4 46.6 %collective-permute-start.10 = (bf16[4,256,512]{2,1,0:T(8,128)(2,1)}, bf16[4,256,512]{2,1,0:T(8,128)(2,1)}, u32[]{:S(2)}, u32[]{:S(2)}) collective-permute-start(bf16[4,256,512]{2,1,0:T(8,128)(2,1)} %get-tuple-element.237), channel_id=1, source_target_pairs={{0,4},{2,6},{4,0},{6,2},{8,12},{10,14},{12,8},{14,10},{16,20},{18,... | collective-permute-start | bytes 3145736 | tf_op jit(solution)/shard_map/ppermute | solution.py:337
  609.6 47.2 %collective-permute-start.20 = (bf16[4,256,512]{2,1,0:T(8,128)(2,1)}, bf16[4,256,512]{2,1,0:T(8,128)(2,1)}, u32[]{:S(2)}, u32[]{:S(2)}) collective-permute-start(bf16[4,256,512]{2,1,0:T(8,128)(2,1)} %get-tuple-element.240), channel_id=1, source_target_pairs={{0,1},{1,0},{2,3},{3,2},{4,5},{5,4},{6,7},{7,6},{8,9},{9,8},{10,11... | collective-permute-start | bytes 3145736 | tf_op jit(solution)/shard_map/ppermute | solution.py:341
  610.2 48.1 %collective-permute-start.18 = (bf16[4,256,512]{2,1,0:T(8,128)(2,1)}, bf16[4,256,512]{2,1,0:T(8,128)(2,1)}, u32[]{:S(2)}, u32[]{:S(2)}) collective-permute-start(bf16[4,256,512]{2,1,0:T(8,128)(2,1)} %get-tuple-element.238), channel_id=1, source_target_pairs={{0,4},{2,6},{4,0},{6,2},{8,12},{10,14},{12,8},{14,10},{16,20},{18,... | collective-permute-start | bytes 3145736 | tf_op jit(solution)/shard_map/ppermute | solution.py:337
  611.0 65.3 %collective-permute-start.17 = (bf16[4,256,512]{2,1,0:T(8,128)(2,1)}, bf16[4,256,512]{2,1,0:T(8,128)(2,1)}, u32[]{:S(2)}, u32[]{:S(2)}) collective-permute-start(bf16[4,256,512]{2,1,0:T(8,128)(2,1)} %get-tuple-element.151), channel_id=1, source_target_pairs={{0,1},{1,0},{2,3},{3,2},{4,5},{5,4},{6,7},{7,6},{8,9},{9,8},{10,11... | collective-permute-start | bytes 3145736 | tf_op jit(solution)/shard_map/ppermute | solution.py:341
  651.0 60.4 %collective-permute-start.16 = (bf16[4,256,2048]{2,1,0:T(8,128)(2,1)}, bf16[4,256,2048]{2,1,0:T(8,128)(2,1)}, u32[]{:S(2)}, u32[]{:S(2)}) collective-permute-start(bf16[4,256,2048]{2,1,0:T(8,128)(2,1)} %get-tuple-element.150), channel_id=1, source_target_pairs={{0,2},{2,0},{4,6},{6,4},{8,10},{10,8},{12,14},{14,12},{16,18},{18,... | collective-permute-start | bytes 12582920 | tf_op jit(solution)/shard_map/ppermute | solution.py:333
  651.1 137.7 %all-to-all-start.1 = ((f32[32,1,256]{2,1,0:T(1,128)}), f32[32,1,256]{2,1,0:T(1,128)S(1)}, u32[]{:S(2)}, u32[]{:S(2)}) async-start(f32[32,1,256]{2,1,0:T(1,128)} %bitcast.189), calls=%async_computation.1 | async-start | bytes 65536 | tf_op jit(solution)/shard_map/all_to_all | solution.py:808
  655.0 548.3 %reduce-scatter.5.cloned.1.call-start = ((), (), s32[]{:S(2)}) async-start(), calls=%async_computation.8 | async-start | bytes 8912896 | tf_op jit(solution)/shard_map/reduce_scatter | solution.py:876
  655.0 56.3 %collective-permute-start.19 = (bf16[4,256,512]{2,1,0:T(8,128)(2,1)}, bf16[4,256,512]{2,1,0:T(8,128)(2,1)S(1)}, u32[]{:S(2)}, u32[]{:S(2)}) collective-permute-start(bf16[4,256,512]{2,1,0:T(8,128)(2,1)} %get-tuple-element.153), channel_id=1, source_target_pairs={{0,4},{2,6},{4,0},{6,2},{8,12},{10,14},{12,8},{14,10},{16,20},{18,... | collective-permute-start | bytes 3145736 | tf_op jit(solution)/shard_map/ppermute | solution.py:337
  656.9 54.5 %collective-permute-start.24 = (bf16[4,256,512]{2,1,0:T(8,128)(2,1)S(1)}, bf16[4,256,512]{2,1,0:T(8,128)(2,1)S(1)}, u32[]{:S(2)}, u32[]{:S(2)}) collective-permute-start(bf16[4,256,512]{2,1,0:T(8,128)(2,1)S(1)} %get-tuple-element.155), channel_id=1, source_target_pairs={{0,1},{1,0},{2,3},{3,2},{4,5},{5,4},{6,7},{7,6},{8,9},{9,8},{10,11... | collective-permute-start | bytes 3145736 | tf_op jit(solution)/shard_map/ppermute | solution.py:341
  658.3 53.1 %collective-permute-start.25 = (bf16[4,256,512]{2,1,0:T(8,128)(2,1)}, bf16[4,256,512]{2,1,0:T(8,128)(2,1)S(1)}, u32[]{:S(2)}, u32[]{:S(2)}) collective-permute-start(bf16[4,256,512]{2,1,0:T(8,128)(2,1)} %get-tuple-element.156), channel_id=1, source_target_pairs={{0,4},{2,6},{4,0},{6,2},{8,12},{10,14},{12,8},{14,10},{16,20},{18,... | collective-permute-start | bytes 3145736 | tf_op jit(solution)/shard_map/ppermute | solution.py:337
  676.3 48.9 %collective-permute-start.15 = (bf16[4,256,2048]{2,1,0:T(8,128)(2,1)}, bf16[4,256,2048]{2,1,0:T(8,128)(2,1)}, u32[]{:S(2)}, u32[]{:S(2)}) collective-permute-start(bf16[4,256,2048]{2,1,0:T(8,128)(2,1)} %get-tuple-element.148), channel_id=1, source_target_pairs={{0,2},{2,0},{4,6},{6,4},{8,10},{10,8},{12,14},{14,12},{16,18},{18,... | collective-permute-start | bytes 12582920 | tf_op jit(solution)/shard_map/ppermute | solution.py:333
  719.8 31.6 %collective-permute-start.21 = (bf16[256,1024]{1,0:T(8,128)(2,1)S(1)}, bf16[256,1024]{1,0:T(8,128)(2,1)S(1)}, u32[]{:S(2)}, u32[]{:S(2)}) collective-permute-start(bf16[256,1024]{1,0:T(8,128)(2,1)S(1)} %get-tuple-element.241), channel_id=1, source_target_pairs={{0,8},{2,10},{4,12},{6,14},{8,16},{10,18},{12,20},{14,22},{16,24},... | collective-permute-start | bytes 1572872 | tf_op jit(solution)/shard_map/ppermute | solution.py:358
  721.4 37.7 %collective-permute-start.22 = (bf16[256,1024]{1,0:T(8,128)(2,1)S(1)}, bf16[256,1024]{1,0:T(8,128)(2,1)}, u32[]{:S(2)}, u32[]{:S(2)}) collective-permute-start(bf16[256,1024]{1,0:T(8,128)(2,1)S(1)} %get-tuple-element.243), channel_id=1, source_target_pairs={{0,16},{2,18},{4,20},{6,22},{8,24},{10,26},{12,28},{14,30},{16,0},... | collective-permute-start | bytes 1572872 | tf_op jit(solution)/shard_map/ppermute | solution.py:358
  723.8 35.8 %collective-permute-start.23 = (bf16[256,1024]{1,0:T(8,128)(2,1)S(1)}, bf16[256,1024]{1,0:T(8,128)(2,1)}, u32[]{:S(2)}, u32[]{:S(2)}) collective-permute-start(bf16[256,1024]{1,0:T(8,128)(2,1)S(1)} %get-tuple-element.242), channel_id=1, source_target_pairs={{0,24},{2,26},{4,28},{6,30},{8,0},{10,2},{12,4},{14,6},{16,8},{18,... | collective-permute-start | bytes 1572872 | tf_op jit(solution)/shard_map/ppermute | solution.py:358
  729.5 81.5 %collective-permute-start.29 = (bf16[4,256,1024]{2,1,0:T(8,128)(2,1)}, bf16[4,256,1024]{2,1,0:T(8,128)(2,1)}, u32[]{:S(2)}, u32[]{:S(2)}) collective-permute-start(bf16[4,256,1024]{2,1,0:T(8,128)(2,1)} %get-tuple-element.203), channel_id=1, source_target_pairs={{0,1},{1,0},{2,3},{3,2},{4,5},{5,4},{6,7},{7,6},{8,9},{9,8},{10,11... | collective-permute-start | bytes 6291464 | tf_op jit(solution)/shard_map/ppermute | solution.py:341
  731.0 80.1 %collective-permute-start.30 = (bf16[4,256,1024]{2,1,0:T(8,128)(2,1)}, bf16[4,256,1024]{2,1,0:T(8,128)(2,1)}, u32[]{:S(2)}, u32[]{:S(2)}) collective-permute-start(bf16[4,256,1024]{2,1,0:T(8,128)(2,1)} %get-tuple-element.202), channel_id=1, source_target_pairs={{0,4},{2,6},{4,0},{6,2},{8,12},{10,14},{12,8},{14,10},{16,20},{18,... | collective-permute-start | bytes 6291464 | tf_op jit(solution)/shard_map/ppermute | solution.py:337
  751.5 39.0 %collective-permute-start.26 = (bf16[256,1024]{1,0:T(8,128)(2,1)}, bf16[256,1024]{1,0:T(8,128)(2,1)}, u32[]{:S(2)}, u32[]{:S(2)}) collective-permute-start(bf16[256,1024]{1,0:T(8,128)(2,1)} %get-tuple-element.234), channel_id=1, source_target_pairs={{0,8},{2,10},{4,12},{6,14},{8,16},{10,18},{12,20},{14,22},{16,24},... | collective-permute-start | bytes 1572872 | tf_op jit(solution)/shard_map/ppermute | solution.py:358
  759.1 44.6 %collective-permute-start.27 = (bf16[256,1024]{1,0:T(8,128)(2,1)}, bf16[256,1024]{1,0:T(8,128)(2,1)}, u32[]{:S(2)}, u32[]{:S(2)}) collective-permute-start(bf16[256,1024]{1,0:T(8,128)(2,1)} %get-tuple-element.236), channel_id=1, source_target_pairs={{0,16},{2,18},{4,20},{6,22},{8,24},{10,26},{12,28},{14,30},{16,0},... | collective-permute-start | bytes 1572872 | tf_op jit(solution)/shard_map/ppermute | solution.py:358
  759.5 49.6 %collective-permute-start.28 = (bf16[256,1024]{1,0:T(8,128)(2,1)}, bf16[256,1024]{1,0:T(8,128)(2,1)}, u32[]{:S(2)}, u32[]{:S(2)}) collective-permute-start(bf16[256,1024]{1,0:T(8,128)(2,1)} %get-tuple-element.235), channel_id=1, source_target_pairs={{0,24},{2,26},{4,28},{6,30},{8,0},{10,2},{12,4},{14,6},{16,8},{18,... | collective-permute-start | bytes 1572872 | tf_op jit(solution)/shard_map/ppermute | solution.py:358
  814.8 24.7 %collective-permute-start.31 = (bf16[256,2048]{1,0:T(8,128)(2,1)S(1)}, bf16[256,2048]{1,0:T(8,128)(2,1)S(1)}, u32[]{:S(2)}, u32[]{:S(2)}) collective-permute-start(bf16[256,2048]{1,0:T(8,128)(2,1)S(1)} %fusion.52), channel_id=1, source_target_pairs={{0,1},{1,0},{2,3},{3,2},{4,5},{5,4},{6,7},{7,6},{8,9},{9,8},{10,11... | collective-permute-start | bytes 3145736 | tf_op jit(solution)/shard_map/ppermute | solution.py:341
  848.9 364.9 %reduce-scatter.3.cloned.1.call-start = ((), (), s32[]{:S(2)}) async-start(), calls=%async_computation.7 | async-start | bytes 13369344 | tf_op jit(solution)/shard_map/reduce_scatter | solution.py:883
  872.6 48.7 %collective-permute-start.32 = (bf16[4,256,1024]{2,1,0:T(8,128)(2,1)}, bf16[4,256,1024]{2,1,0:T(8,128)(2,1)S(1)}, u32[]{:S(2)}, u32[]{:S(2)}) collective-permute-start(bf16[4,256,1024]{2,1,0:T(8,128)(2,1)} %get-tuple-element.166), channel_id=1, source_target_pairs={{0,1},{1,0},{2,3},{3,2},{4,5},{5,4},{6,7},{7,6},{8,9},{9,8},{10,11... | collective-permute-start | bytes 6291464 | tf_op jit(solution)/shard_map/ppermute | solution.py:341
  874.1 62.6 %collective-permute-start.33 = (bf16[4,256,1024]{2,1,0:T(8,128)(2,1)S(1)}, bf16[4,256,1024]{2,1,0:T(8,128)(2,1)S(1)}, u32[]{:S(2)}, u32[]{:S(2)}) collective-permute-start(bf16[4,256,1024]{2,1,0:T(8,128)(2,1)S(1)} %get-tuple-element.167), channel_id=1, source_target_pairs={{0,4},{2,6},{4,0},{6,2},{8,12},{10,14},{12,8},{14,10},{16,20},{18,... | collective-permute-start | bytes 6291464 | tf_op jit(solution)/shard_map/ppermute | solution.py:337
  878.0 87.4 %collective-permute-start.35 = (bf16[4,256,1024]{2,1,0:T(8,128)(2,1)S(1)}, bf16[4,256,1024]{2,1,0:T(8,128)(2,1)S(1)}, u32[]{:S(2)}, u32[]{:S(2)}) collective-permute-start(bf16[4,256,1024]{2,1,0:T(8,128)(2,1)S(1)} %add_convert_fusion.3), channel_id=1, source_target_pairs={{0,1},{1,0},{2,3},{3,2},{4,5},{5,4},{6,7},{7,6},{8,9},{9,8},{10,11... | collective-permute-start | bytes 6291464 | tf_op jit(solution)/shard_map/ppermute | solution.py:341
  881.5 113.1 %collective-permute-start.34 = (bf16[4,256,1024]{2,1,0:T(8,128)(2,1)S(1)}, bf16[4,256,1024]{2,1,0:T(8,128)(2,1)}, u32[]{:S(2)}, u32[]{:S(2)}) collective-permute-start(bf16[4,256,1024]{2,1,0:T(8,128)(2,1)S(1)} %add_convert_fusion.4), channel_id=1, source_target_pairs={{0,4},{2,6},{4,0},{6,2},{8,12},{10,14},{12,8},{14,10},{16,20},{18,... | collective-permute-start | bytes 6291464 | tf_op jit(solution)/shard_map/ppermute | solution.py:337
  1044.2 24.5 %collective-permute-start.42 = (bf16[256,2048]{1,0:T(8,128)(2,1)S(1)}, bf16[256,2048]{1,0:T(8,128)(2,1)S(1)}, u32[]{:S(2)}, u32[]{:S(2)}) collective-permute-start(bf16[256,2048]{1,0:T(8,128)(2,1)S(1)} %select_convert_fusion), channel_id=1, source_target_pairs={{0,1},{1,0},{2,3},{3,2},{4,5},{5,4},{6,7},{7,6},{8,9},{9,8},{10,11... | collective-permute-start | bytes 3145736 | tf_op jit(solution)/shard_map/ppermute | solution.py:341
  1049.2 28.2 %collective-permute-start.36 = (bf16[256,1024]{1,0:T(8,128)(2,1)S(1)}, bf16[256,1024]{1,0:T(8,128)(2,1)S(1)}, u32[]{:S(2)}, u32[]{:S(2)}) collective-permute-start(bf16[256,1024]{1,0:T(8,128)(2,1)S(1)} %get-tuple-element.226), channel_id=1, source_target_pairs={{0,8},{2,10},{4,12},{6,14},{8,16},{10,18},{12,20},{14,22},{16,24},... | collective-permute-start | bytes 1572872 | tf_op jit(solution)/shard_map/ppermute | solution.py:358
  1051.2 63.4 %collective-permute-start.37 = (bf16[256,1024]{1,0:T(8,128)(2,1)S(1)}, bf16[256,1024]{1,0:T(8,128)(2,1)S(1)}, u32[]{:S(2)}, u32[]{:S(2)}) collective-permute-start(bf16[256,1024]{1,0:T(8,128)(2,1)S(1)} %get-tuple-element.228), channel_id=1, source_target_pairs={{0,16},{2,18},{4,20},{6,22},{8,24},{10,26},{12,28},{14,30},{16,0},... | collective-permute-start | bytes 1572872 | tf_op jit(solution)/shard_map/ppermute | solution.py:358
  1054.0 64.9 %collective-permute-start.38 = (bf16[256,1024]{1,0:T(8,128)(2,1)S(1)}, bf16[256,1024]{1,0:T(8,128)(2,1)S(1)}, u32[]{:S(2)}, u32[]{:S(2)}) collective-permute-start(bf16[256,1024]{1,0:T(8,128)(2,1)S(1)} %get-tuple-element.227), channel_id=1, source_target_pairs={{0,24},{2,26},{4,28},{6,30},{8,0},{10,2},{12,4},{14,6},{16,8},{18,... | collective-permute-start | bytes 1572872 | tf_op jit(solution)/shard_map/ppermute | solution.py:358
  1070.9 33.0 %collective-permute-start.50 = (f32[18,128]{1,0:T(8,128)S(1)}, f32[18,128]{1,0:T(8,128)S(1)}, u32[]{:S(2)}, u32[]{:S(2)}) collective-permute-start(f32[18,128]{1,0:T(8,128)S(1)} %pad_maximum_fusion.15), channel_id=1, source_target_pairs={{0,2},{2,0},{4,6},{6,4},{8,10},{10,8},{12,14},{14,12},{16,18},{18,... | collective-permute-start | bytes 27656 | tf_op jit(solution)/shard_map/ppermute | solution.py:379
  1071.1 72.1 %collective-permute-start.39 = (bf16[256,1024]{1,0:T(8,128)(2,1)S(1)}, bf16[256,1024]{1,0:T(8,128)(2,1)S(1)}, u32[]{:S(2)}, u32[]{:S(2)}) collective-permute-start(bf16[256,1024]{1,0:T(8,128)(2,1)S(1)} %get-tuple-element.229), channel_id=1, source_target_pairs={{0,8},{2,10},{4,12},{6,14},{8,16},{10,18},{12,20},{14,22},{16,24},... | collective-permute-start | bytes 1572872 | tf_op jit(solution)/shard_map/ppermute | solution.py:358
  1077.4 98.5 %collective-permute-start.40 = (bf16[256,1024]{1,0:T(8,128)(2,1)S(1)}, bf16[256,1024]{1,0:T(8,128)(2,1)S(1)}, u32[]{:S(2)}, u32[]{:S(2)}) collective-permute-start(bf16[256,1024]{1,0:T(8,128)(2,1)S(1)} %get-tuple-element.231), channel_id=1, source_target_pairs={{0,16},{2,18},{4,20},{6,22},{8,24},{10,26},{12,28},{14,30},{16,0},... | collective-permute-start | bytes 1572872 | tf_op jit(solution)/shard_map/ppermute | solution.py:358
  1103.9 71.9 %collective-permute-start.41 = (bf16[256,1024]{1,0:T(8,128)(2,1)S(1)}, bf16[256,1024]{1,0:T(8,128)(2,1)S(1)}, u32[]{:S(2)}, u32[]{:S(2)}) collective-permute-start(bf16[256,1024]{1,0:T(8,128)(2,1)S(1)} %get-tuple-element.230), channel_id=1, source_target_pairs={{0,24},{2,26},{4,28},{6,30},{8,0},{10,2},{12,4},{14,6},{16,8},{18,... | collective-permute-start | bytes 1572872 | tf_op jit(solution)/shard_map/ppermute | solution.py:358
  1120.2 57.0 %collective-permute-start.52 = (f32[18,128]{1,0:T(8,128)S(1)}, f32[18,128]{1,0:T(8,128)S(1)}, u32[]{:S(2)}, u32[]{:S(2)}) collective-permute-start(f32[18,128]{1,0:T(8,128)S(1)} %add.472), channel_id=1, source_target_pairs={{0,4},{2,6},{4,0},{6,2},{8,12},{10,14},{12,8},{14,10},{16,20},{18,... | collective-permute-start | bytes 27656 | tf_op jit(solution)/shard_map/ppermute | solution.py:383
  1177.2 26.1 %collective-permute-start.53 = (f32[18,128]{1,0:T(8,128)S(1)}, f32[18,128]{1,0:T(8,128)S(1)}, u32[]{:S(2)}, u32[]{:S(2)}) collective-permute-start(f32[18,128]{1,0:T(8,128)S(1)} %add.473), channel_id=1, source_target_pairs={{0,8},{2,10},{4,12},{6,14},{8,0},{10,2},{12,4},{14,6},{16,24},{18,... | collective-permute-start | bytes 27656 | tf_op jit(solution)/shard_map/ppermute | solution.py:383
  1213.8 19.8 %collective-permute-start.43 = (bf16[128,3072]{1,0:T(8,128)(2,1)}, bf16[128,3072]{1,0:T(8,128)(2,1)S(1)}, u32[]{:S(2)}, u32[]{:S(2)}) collective-permute-start(bf16[128,3072]{1,0:T(8,128)(2,1)} %reduce-scatter.3.cloned.1.call-done), channel_id=1, source_target_pairs={{0,1},{1,0},{2,3},{3,2},{4,5},{5,4},{6,7},{7,6},{8,9},{9,8},{10,11... | collective-permute-start | bytes 2359304 | tf_op jit(solution)/shard_map/ppermute | solution.py:341
  (89 other events, 1865.3 us)
Sparse Core Ops, SparseCore 0:
  15.2 112.8 all-gather.3
  130.2 128.7 all-gather.7
  261.2 168.5 all-gather.5
  849.1 139.9 reduce-scatter.4
  1004.7 209.0 reduce-scatter.2

commit v5 on v4

--- a/solution.py
+++ b/solution.py
@@ -358,21 +358,36 @@
     return lax.ppermute(values, "fsdp", [(i, (i + 4 * step) % fsdp) for i in range(fsdp)])
 
 
-def line_sum(values):
-    count = values.shape[0]
-    total = values[0].astype(full)
-    for step in range(1, count):
-        total = total + line_shift(values[count - step], step).astype(full)
+def line_total(own, arrived):
+    total = own.astype(full)
+    for item in arrived.values():
+        total = total + item.astype(full)
     return total
 
 
-def over_core(keep, send, pieces):
-    step = keep.shape[-1] // pieces
-    other = swap_core(send)
-    return [
-        add_low(keep[..., i * step : (i + 1) * step], other[..., i * step : (i + 1) * step])
-        for i in range(pieces)
-    ]
+def line_sum(entries, count):
+    return line_total(entries[0], {s: line_shift(entries[s], count - s) for s in range(1, count)})
+
+
+def joined(places, own, got):
+    from_ctx, from_side, one_side, two_ctx = got
+    entries = {}
+    for at, p in enumerate(places):
+        one = add_low(add_low(own[0][at], from_ctx[at]), one_side[at])
+        two = add_low(add_low(own[1][at], from_side[at]), two_ctx[at])
+        entries[p] = jnp.concatenate([one, two], axis=-1)
+    return entries
+
+
+def over_core(keep, send):
+    return keep, swap_core(send)
+
+
+def pick_sum(parts, start, stop, column):
+    keep, other = parts
+    half = keep.shape[-1] // 2
+    cut = (slice(start, stop), slice(None), slice(column * half, (column + 1) * half))
+    return add_low(keep[cut], other[cut])
 
 
 def sum_all(values, fsdp):
@@ -555,9 +570,10 @@
     )(projected, projected, roped_q, roped_k, values_low, grad, cosine, sine, query_gain, key_gain)
 
 
-def expert_kernel(core_ref, order, m_ref, g_ref, g_more, w_ref, gu_ref, dn_ref, *refs):
+def expert_kernel(core_ref, order, m_ref, near_ref, far_ref, g_ref, w_ref, gu_ref, dn_ref, *refs):
     (keep_out, send_out, keep_back, send_back, gate_back, rows_ref, dy_ref, z_ref, pair_ref) = refs[-9:]
     core = core_ref[0]
+    far = order[5 * pl.program_id(0) + 2] == 1
     block = m_ref.shape[3]
     hidden = dn_ref.shape[0]
     slots = z_ref.shape[0] // 2
@@ -580,7 +596,13 @@
         weights.append(jnp.sum(jnp.where(place, gate, 0.0), axis=1, keepdims=True))
         rows.append(mul(pick, m_ref[0, at, 0]).astype(low))
         grads.append(
-            jnp.concatenate([mul(pick, g_ref[0, at, 0]), mul(pick, g_more[0, at, 0])], axis=1)
+            jnp.concatenate(
+                [
+                    mul(pick, jnp.where(far, far_ref[0, at, 0], near_ref[0, at, 0])),
+                    mul(pick, g_ref[0, at, 0]),
+                ],
+                axis=1,
+            )
         )
     row, grad, weight = (jnp.concatenate(items, axis=0) for items in (rows, grads, weights))
     rows_ref[...] = row
@@ -611,41 +633,51 @@
         out[0] = mul(picks[part], back[mine], lhs_turned).astype(low)
 
 
-def run_expert(core, order, number, parts, m_all, g_one, g_two, gates_all, gate_up, down, slots, kept):
+def run_expert(core, order, first, total_steps, m_all, g_all, g_far, gates_all, gate_up, down, slots, kept):
     places, _, _, block, width = m_all.shape
     paired = gate_up.shape[1]
-    steps = order.shape[0] // 3
+    steps = order.shape[0] // 5
     part_rows = steps * 2 * slots
     hidden = paired // 2
     shape = jax.ShapeDtypeStruct
 
     def gates_at(i, core, order):
-        return (order[3 * i], 0, order[3 * i + 1], 0, 0)
+        return (order[5 * i], 0, order[5 * i + 1], 0, 0)
 
     def token_at(i, core, order):
-        return (order[3 * i], 0, order[3 * i + 2], 0, 0)
-
-    def half_spec(index):
-        return pl.BlockSpec((1, 2, 1, block, width // 2), lambda i, core, order: (order[3 * i], 0, index, 0, 0))
+        return (order[5 * i], 0, order[5 * i + 2], 0, 0)
+
+    def half_at(i, core, order):
+        return (order[5 * i], 0, 1 + order[5 * i + 2], 0, 0)
+
+    def near_at(i, core, order):
+        return (order[5 * i + 3], 0, 0, 0, 0)
+
+    def far_at(i, core, order):
+        return (order[5 * i + 4], 0, 0, 0, 0)
 
     def fixed(i, core, order):
         return (0, 0)
 
     def flat(i, core, order):
-        return (number * steps + i, 0)
+        return (first + i, 0)
 
     def stacked(i, core, order):
         return (i, 0, 0)
 
     small = pl.BlockSpec((1, 2, 1, 1, block), gates_at)
     one_block = pl.BlockSpec((1, block, width), stacked)
+    half_block = (1, 2, 1, block, width // 2)
     widths = (width, width, hidden, paired)
     grid_spec = pltpu.PrefetchScalarGridSpec(
         num_scalar_prefetch=2,
         grid=(steps,),
         in_specs=[
             pl.BlockSpec((1, 2, 1, block, width), token_at),
-            half_spec(g_one[1]), half_spec(g_two[1]), small,
+            pl.BlockSpec(half_block, near_at),
+            pl.BlockSpec(half_block, far_at),
+            pl.BlockSpec(half_block, half_at),
+            small,
             pl.BlockSpec(gate_up.shape, fixed, pipeline_mode=pl.Buffered(1)),
             pl.BlockSpec(down.shape, fixed, pipeline_mode=pl.Buffered(1)),
         ]
@@ -657,8 +689,8 @@
         grid_spec=grid_spec,
         out_shape=[shape((steps, block, width), low)] * 4
         + [shape((places, 2, 2, 1, block), full)]
-        + [shape((parts * part_rows, n), low) for n in widths],
-        input_output_aliases={} if kept is None else {8 + i: 4 + i for i in range(5)},
+        + [shape((total_steps * 2 * slots, n), low) for n in widths],
+        input_output_aliases={} if kept is None else {9 + i: 4 + i for i in range(5)},
         compiler_params=pltpu.CompilerParams(vmem_limit_bytes=vmem_bytes),
         cost_estimate=pl.CostEstimate(
             flops=part_rows * width * (4 * paired + 4 * hidden + 8 * block),
@@ -666,7 +698,7 @@
             transcendentals=part_rows * hidden,
         ),
         name="experts",
-    )(core, order, m_all, g_one[0], g_two[0], gates_all, gate_up, down, *(() if kept is None else kept))
+    )(core, order, m_all, g_all, g_far, g_all, gates_all, gate_up, down, *(() if kept is None else kept))
 
 
 def rms_back(values, gain, grad):
@@ -735,7 +767,6 @@
     g_all = lax.all_gather(
         g_local.reshape(3 * rows_dev, g_half), "fsdp", axis=0, tiled=True
     ).reshape(fsdp // 2, 2, 3, rows_dev, g_half)
-    g_far = swap_ctx(g_all[:, :, :1])
 
     sequence_in = sequence(tokens).astype(full)
     low_in = rms_scale(sequence_in, attn_all).astype(low)
@@ -765,75 +796,103 @@
     gates_sent = jnp.where(chosen, gates_wide, -1.0).T
     gates_all = lax.all_to_all(gates_sent, both, split_axis=0, concat_axis=0, tiled=True)
 
+    g_all, gates_all = hold(g_all, gates_all)
+    g_far = swap_ctx(g_all[:, :, :1])
+
     lines = fsdp // 4
-    grid_of = (fsdp // 2, 2, 2)
-    lines_at = (place - jnp.arange(lines, dtype=jnp.int32)) % lines
-    kept, back, out = None, {}, {}
-    core_at = core[None].astype(jnp.int32)
-    for number, at in enumerate(((1, 1), (0, 1), (1, 0), (0, 0))):
-        d_side, d_ctx = at
-        order = jnp.stack(
-            [
-                lines_at * 2 + (side + d_side) % 2,
-                jnp.broadcast_to((rank + d_ctx) % 2, (lines,)),
-                jnp.full((lines,), d_ctx),
-            ],
-            axis=1,
-        ).reshape(-1)
-        if number == 1:
-            core_at, back[1, 1] = hold(core_at, back[1, 1])
-        if number == 2:
-            far_ctx = swap_ctx(jnp.concatenate(back[1, 1][:2], axis=-1))
-            far_side = swap_side(jnp.concatenate(back[1, 1][2:], axis=-1))
-            core_at, (far_ctx, far_side) = hold(core_at, (far_ctx, far_side))
-        if number == 3:
-            core_at, (back[0, 1], back[1, 0]) = hold(core_at, (back[0, 1], back[1, 0]))
+    places = list(range(1, lines)) + [0]
+    cut = lines // 2
+    parts = [places[:cut], places[cut:]]
+    m_all = m_all.reshape(fsdp // 2, 2, 2, rows_dev, width)
+    gates_all = gates_all.reshape(fsdp // 2, 2, 2, 1, rows_dev)
+    state = dict(kept=None, first=0, core=core[None].astype(jnp.int32))
+
+    def call(steps, raw=False):
+        spots = [((place - p) % lines) * 2 + (side + d) % 2 for d, _, p in steps]
+        near = [i for i, step in enumerate(steps) if step[1] == 0] or [0]
+        far = [i for i, step in enumerate(steps) if step[1] == 1] or [0]
+
+        def nearest(i, among):
+            return spots[min(among, key=lambda j: abs(j - i))]
+
+        order = [
+            item
+            for i, step in enumerate(steps)
+            for item in (spots[i], (rank + step[1]) % 2, step[1], nearest(i, near), nearest(i, far))
+        ]
         keep_out, send_out, keep_back, send_back, *kept = run_expert(
-            core_at,
-            order.astype(jnp.int32),
-            number,
-            4,
-            m_all.reshape(*grid_of, rows_dev, width),
-            (g_far, 0) if d_ctx else (g_all, 0),
-            (g_all, 1 + d_ctx),
-            gates_all.reshape(*grid_of, 1, rows_dev),
+            state["core"],
+            jnp.stack([jnp.asarray(item, jnp.int32) for item in order]),
+            state["first"],
+            4 * lines,
+            m_all,
+            g_all,
+            g_far,
+            gates_all,
             expert_gate_up[0],
             expert_down[0],
             capacity,
-            kept,
+            state["kept"],
         )
-        back[at] = over_core(keep_back, send_back, 4)
-        out[at] = (keep_out, send_out)
-    gate_back, rows, grad_rows, hidden, grad_pair = kept
+        state["kept"] = kept
+        state["first"] += len(steps)
+        back = (keep_back, send_back)
+        return back if raw else over_core(*back), (keep_out, send_out)
+
+    def wait(first):
+        state["core"], first = hold(state["core"], first)
+        return first
+
+    back, out_far = call([(1, 1, p) for p in places])
+    far_one, far_two = wait([pick_sum(back, 0, lines, column) for column in range(2)])
+    far_one, far_two = swap_ctx(far_one), swap_side(far_two)
+
+    def mixed_call(part, raw=False):
+        return call([(1, 0, p) for p in parts[part]] + [(0, 1, p) for p in parts[part]], raw)
+
+    def mixed_sums(back):
+        return [pick_sum(back, start, start + cut, column) for start in (0, cut) for column in range(2)]
+
+    def rounds(sums, part):
+        side_one, side_two, ctx_one, ctx_two = sums
+        span = slice(part * cut, (part + 1) * cut)
+        return [
+            swap_ctx(ctx_one),
+            swap_side(side_two),
+            swap_side(add_low(side_one, far_one[span])),
+            swap_ctx(add_low(ctx_two, far_two[span])),
+        ]
+
+    (keep, send), out_first = mixed_call(0, raw=True)
+    send, (far_one, far_two) = hold(send, (far_one, far_two))
+    back = over_core(keep, send)
+    back_own, out_own = call([(0, 0, p) for p in places])
+    sums = wait(mixed_sums(back))
+    back_own = [pick_sum(back_own, 0, lines, column) for column in range(2)]
+    got = rounds(sums, 0)
+    (keep, send), out_second = mixed_call(1, raw=True)
+    send, got = hold(send, got)
+    back = over_core(keep, send)
+    entries = joined(parts[0], [item[:cut] for item in back_own], got)
+    arrived = {p: line_shift(entries[p], lines - p) for p in parts[0]}
+    got = rounds(mixed_sums(back), 1)
+    gate_back, rows, grad_rows, hidden, grad_pair = state["kept"]
     grad_gates = lax.all_to_all(
         gate_back.reshape(fsdp * 2, rows_dev), both, split_axis=0, concat_axis=0, tiled=True
     ).T
-    cut = far_ctx.shape[-1] // 2
+    grad_gate_up = mul(rows, grad_pair, lhs_turned)[None]
     grad_down = mul(hidden, grad_rows, lhs_turned)[None]
-    grad_gate_up = mul(rows, grad_pair, lhs_turned)[None]
-    sums = []
-    for k in range(2):
-        cols = slice(k * cut, (k + 1) * cut)
-        from_ctx, from_side = swap_ctx(back[0, 1][k]), swap_side(back[1, 0][2 + k])
-        one_side = swap_side(add_low(back[1, 0][k], far_ctx[..., cols]))
-        two_ctx = swap_ctx(add_low(back[0, 1][2 + k], far_side[..., cols]))
-        both_mine = jnp.concatenate(
-            [
-                add_low(add_low(back[0, 0][k], from_ctx), one_side),
-                add_low(add_low(back[0, 0][2 + k], from_side), two_ctx),
-            ],
-            axis=-1,
-        )
-        if k == 1:
-            both_mine, (grad_down, grad_gate_up) = hold(both_mine, (grad_down, grad_gate_up))
-        sums.append(line_sum(both_mine))
-    out, last_round = hold(out, (one_side, two_ctx))
-    out = {at: over_core(*out[at], 2) for at in out}
-    out_far_ctx, out_far_side = swap_ctx(out[1, 1][0]), swap_side(out[1, 1][1])
-    sums, (out_far_ctx, out_far_side) = hold(sums, (out_far_ctx, out_far_side))
-    grad_mid = jnp.concatenate(
-        [sums[0][:, :cut], sums[1][:, :cut], sums[0][:, cut:], sums[1][:, cut:]], axis=-1
-    )
+    out_far = over_core(*out_far)
+    out_far = [pick_sum(out_far, 0, lines, column) for column in range(2)]
+    grad_gate_up, got, out_far, arrived = lax.optimization_barrier((grad_gate_up, got, out_far, arrived))
+    entries.update(joined(parts[1], [item[cut:] for item in back_own], got))
+    out_far = [swap_ctx(out_far[0]), swap_side(out_far[1])]
+    outs, entries = hold((out_first, out_own, out_second), entries)
+    out_first, out_own, out_second = (over_core(*item) for item in outs)
+    for p in parts[1][:-1]:
+        arrived[p] = line_shift(entries[p], lines - p)
+    arrived, grad_down = hold(arrived, grad_down)
+    grad_mid = line_total(entries[0], arrived)
 
     grad_wide = jnp.where(chosen, grad_gates, 0.0)
     grad_logits = (
@@ -844,29 +903,36 @@
     grad_mixed_part, grad_moe_gain = rms_back(mixed, moe_all, grad_mid)
     grad_mixed = cotangent.astype(full) + grad_mixed_part
 
-    grad_branch = sequence(grad_mixed.astype(low))
+    low_mixed, (out_far, outs) = hold(
+        grad_mixed.astype(low), (out_far, (out_first, out_own, out_second))
+    )
+    grad_branch = sequence(low_mixed)
+    out_first, out_own, out_second = outs
+    out_sums = [
+        jnp.concatenate([one, two]) for one, two in zip(mixed_sums(out_first), mixed_sums(out_second))
+    ]
+    out_own = [pick_sum(out_own, 0, lines, column) for column in range(2)]
+    (out_sums, out_own), grad_branch = hold((out_sums, out_own), grad_branch)
+    side_one, side_two, ctx_one, ctx_two = out_sums
+    got = [
+        swap_ctx(ctx_one),
+        swap_side(side_two),
+        add_low(side_one, out_far[0]),
+        add_low(ctx_two, out_far[1]),
+    ]
     grad_attended = mul(grad_branch, out_all, rhs_turned).astype(low)
     grad_out_part = mul(attended, grad_branch, lhs_turned).astype(low)
-    out, grad_branch = hold(out, grad_branch)
-    out_ctx, out_side = swap_ctx(out[0, 1][0]), swap_side(out[1, 0][1])
-    grad_attended, (out_ctx, out_side) = hold(grad_attended, (out_ctx, out_side))
     grad_q, grad_k, grad_v, gain_q_part, gain_k_part = attend_grad(
         projected, roped_q, roped_k, values_low, grad_attended, cosine, sine, gain_q, gain_k, kv_heads, group
     )
     grad_projected = jnp.concatenate([grad_q, grad_k, grad_v], axis=1)
-    out_one = swap_side(add_low(out[1, 0][0], out_far_ctx))
-    out_two = swap_ctx(add_low(out[0, 1][1], out_far_side))
-    grad_projected, (out_one, out_two) = hold(grad_projected, (out_one, out_two))
-    one_mine = add_low(add_low(out[0, 0][0], out_ctx), out_one)
-    two_mine = add_low(add_low(out[0, 0][1], out_side), out_two)
-    output = (
-        mixed
-        + jnp.concatenate(
-            [line_sum(one_mine), line_sum(two_mine)], axis=-1
-        )
-    ).astype(low)
+    grad_projected, got = hold(grad_projected, got)
+    got[2], got[3] = swap_side(got[2]), swap_ctx(got[3])
     grad_qkv_part = mul(low_in, grad_projected, lhs_turned).astype(low)
     grad_normed_part = mul(grad_projected, qkv_all, rhs_turned)
+    grad_normed_part, got = hold(grad_normed_part, got)
+    entries = joined(places, out_own, got)
+    output = (mixed + line_sum(entries, lines)).astype(low)
     grad_normed = of_block(grad_normed_part, rank) + swap_ctx(
         of_block(grad_normed_part, 1 - rank).astype(low)
     ).astype(full)
@@ -927,7 +993,7 @@
     tokens, gate_up = args[0], args[8]
     fsdp, ctx = lax.axis_size("fsdp"), lax.axis_size("ctx")
     fits = tokens.size * tokens.dtype.itemsize * fsdp * ctx <= gathered_bytes
-    if fits and fsdp % 4 == 0 and ctx == 2 and fsdp & (fsdp - 1) == 0 and gate_up.shape[0] == 1:
+    if fits and fsdp % 4 == 0 and ctx == 2 and fsdp >= 8 and fsdp & (fsdp - 1) == 0 and gate_up.shape[0] == 1:
         return body_gathered(*args)
     return body_routed(*args)
 

time: 1250 us -> 1200 us (0.960)
  starting transfers between devices: 152 us -> 53.7 us
  other arithmetic: 81.8 us -> 107 us
  blocking collectives: 23.2 us -> 36 us
    all_to_all x1 -> x0, waiting for transfers between devices: 175 us -> none  [body_gathered(): lax.all_to_all(gates_sent, both, split_axis=0, concat_axis=0, tiled=True)]
    ppermute x19, waiting for transfers between devices: 164 us -> 276 us  [swap_ctx(): return lax.ppermute(values, 'ctx', [(0, 1), (1, 0)])]
    ppermute x3, waiting for transfers between devices: 2.48 us -> 95.4 us  [sum_all(): lax.ppermute(values, 'fsdp', [(i, i ^ step) for i in range(fsdp)])]
    ppermute x12 -> x6, starting transfers between devices: 70.9 us -> 6.93 us  [line_shift(): lax.ppermute(values, 'fsdp', [(i, (i + 4 * step) % fsdp) for i in range(f...]
    ppermute x12 -> x6, waiting for transfers between devices: 97.4 us -> 59.2 us  [line_shift(): lax.ppermute(values, 'fsdp', [(i, (i + 4 * step) % fsdp) for i in range(f...]
    ppermute x3, starting transfers between devices: 24.8 us -> 1.05 us  [sum_all(): lax.ppermute(values, 'fsdp', [(i, i ^ step) for i in range(fsdp)])]
    reduce_scatter x1, waiting for transfers between devices: 3.39 us -> 22.2 us  [body_gathered(): lax.psum_scatter(grad_qkv_part, 'fsdp', scatter_dimension=0, tiled=True)]
    convert_element_type x14 -> x18, other arithmetic: 47.5 us -> 63.8 us  [add_low(): return (one.astype(full) + two.astype(full)).astype(low)]
  transfers between devices with their start and end apart: 62 -> 55, of which waited for: 36 -> 29; matrix products, arithmetic and copies ran while one was open for 15% -> 18% of each run, Pallas kernels for 13% -> 13%
where the time goes in v5:
time: 1200 us; the launch traced here: 1190 us
  waiting for transfers between devices  630 us (52%)
  Pallas kernels  199 us (17%)
  matrix products  112 us (9%)
  other arithmetic  107 us (9%)
  starting transfers between devices  53.7 us (4%)
  local copies, waits for them, and re-layouts  42.2 us (4%)
  blocking collectives  36 us (3%)
  between operations  15.3 us (1%)
    ppermute x19, waiting for transfers between devices, swap_ctx(): return lax.ppermute(values, 'ctx', [(0, 1), (1, 0)])  276 us
    pallas_call x4, Pallas kernels, run_expert(): pl.pallas_call(expert_kernel, grid_spec=grid_spec, out_shape=[shape((step...  155 us
    dot_general x11, matrix products, mul(): return lax.dot_general(left, right, dims, preferred_element_type=full)  112 us
    ppermute x3, waiting for transfers between devices, sum_all(): lax.ppermute(values, 'fsdp', [(i, i ^ step) for i in range(fsdp)])  95.4 us
    all_gather x1, waiting for transfers between devices, body_gathered(): weights_all = lax.all_gather(weights_local, 'fsdp', axis=0, tiled=True)  66.7 us
    convert_element_type x18, other arithmetic, add_low(): return (one.astype(full) + two.astype(full)).astype(low)  63.8 us
    ppermute x6, waiting for transfers between devices, line_shift(): lax.ppermute(values, 'fsdp', [(i, (i + 4 * step) % fsdp) for i in range(f...  59.2 us
    ppermute x8, waiting for transfers between devices, swap_side(): return lax.ppermute(values, 'fsdp', side_pairs(lax.axis_size('fsdp')))  59.2 us
  transfers between devices with their start and end apart: 55, of which 29 were waited for; matrix products, arithmetic and copies ran while one was open for 18% of the time, Pallas kernels for 13%

profile of v5, /device:TPU:0, one launch (start us, length us, event | category | flops | bytes accessed | tf_op | source)
XLA Modules:
  0.0 1194.8 jit_solution(18405637934495599466)
XLA Ops:
  18.2 11.9 collective-permute-done.3
  34.8 23.2 %all_gather.12 = bf16[2048,34]{0,1:T(8,128)(2,1)S(1)} all-gather(bf16[128,34]{0,1:T(8,128)(2,1)S(1)} %pad_maximum_fusion.23), channel_id=1, replica_groups=mesh['fsdp'=16,'ctx'=2] {'fsdp'}, dimensions={0}, use_global_device_ids=true | all-gather | bytes 147968 | tf_op jit(solution)/shard_map/all_gather | solution.py:756
  61.4 66.7 %all-gather.4.cloned.1.call-done = bf16[2048,5120]{1,0:T(8,128)(2,1)} async-done(((bf16[128,5120]{1,0:T(8,128)(2,1)}), bf16[2048,5120]{1,0:T(8,128)(2,1)}) %all-gather.4.cloned.1.call-update) | async-done | bytes 20971536 | tf_op jit(solution)/shard_map/all_gather | solution.py:757
  128.0 11.5 fusion.2.q_ref.k_ref.v_ref
  139.6 18.3 %attend.1 = (bf16[512,2048]{1,0:T(8,128)(2,1)S(1)}, bf16[512,2048]{1,0:T(8,128)(2,1)S(1)}, bf16[512,512]{1,0:T(8,128)(2,1)S(1)}, bf16[512,512]{1,0:T(8,128)(2,1)S(1)}) custom-call(f32[512,3072]{1,0:T(8,128)} %fusion.2.q_ref.k_ref.v_ref, f32[512,3072]{1,0:T(8,128)} %fusion.2.q_ref.k_ref.v_ref, f32[512,3072]{1,0:T(8,128)} %fusion.2.q_ref.k_ref.v_ref, ...), custom_call_target="tpu_custom_call" | custom-call | flops 2147483648 | bytes 9437184 | tf_op jit(solution)/shard_map/attend/pallas_call | solution.py:525
  157.9 8.5 fusion.6
  168.5 24.0 %collective-permute-done.1 = bf16[256,2048]{1,0:T(8,128)(2,1)S(1)} collective-permute-done((bf16[256,2048]{1,0:T(8,128)(2,1)S(1)}, bf16[256,2048]{1,0:T(8,128)(2,1)S(1)}, u32[]{:S(2)}, u32[]{:S(2)}) %collective-permute-start.1) | collective-permute-done | bytes 1048608 | tf_op jit(solution)/shard_map/ppermute | solution.py:341
  196.9 23.3 %collective-permute-done.2 = bf16[256,2048]{1,0:T(8,128)(2,1)S(1)} collective-permute-done((bf16[256,2048]{1,0:T(8,128)(2,1)S(1)}, bf16[256,2048]{1,0:T(8,128)(2,1)S(1)}, u32[]{:S(2)}, u32[]{:S(2)}) %collective-permute-start.2) | collective-permute-done | bytes 1048608 | tf_op jit(solution)/shard_map/ppermute | solution.py:341
  223.8 12.8 %all_to_all.24 = f32[32,1,256]{2,1,0:T(1,128)S(1)} all-to-all(f32[32,1,256]{2,1,0:T(1,128)S(1)} %copy.77), channel_id=1, replica_groups=mesh['fsdp'=16,'ctx'=2] {'fsdp','ctx'}, dimensions={0} | all-to-all | bytes 65536 | tf_op jit(solution)/shard_map/all_to_all | solution.py:797
  236.6 23.0 %all-gather.8.cloned.1.call-done = bf16[12288,1024]{1,0:T(8,128)(2,1)} async-done(((bf16[768,1024]{1,0:T(8,128)(2,1)}), bf16[12288,1024]{1,0:T(8,128)(2,1)}) %all-gather.8.cloned.1.call-update) | async-done | bytes 25165840 | tf_op jit(solution)/shard_map/all_gather | solution.py:767
  259.6 8.1 slice.436
  270.4 180.2 %collective-permute-done.4.far_ref = bf16[8,2,1,256,1024]{4,3,2,1,0:T(8,128)(2,1)} collective-permute-done((bf16[8,2,1,256,1024]{4,3,2,1,0:T(8,128)(2,1)}, bf16[8,2,1,256,1024]{4,3,2,1,0:T(8,128)(2,1)}, u32[]{:S(2)}, u32[]{:S(2)}) %collective-permute-start.4) | collective-permute-done | bytes 8388640 | tf_op jit(solution)/shard_map/ppermute | solution.py:341
  450.6 38.6 %experts.4 = (bf16[4,256,2048]{2,1,0:T(8,128)(2,1)}, bf16[4,256,2048]{2,1,0:T(8,128)(2,1)}, bf16[4,256,2048]{2,1,0:T(8,128)(2,1)}, bf16[4,256,2048]{2,1,0:T(8,12...) custom-call(s32[1]{0:T(128)} %bitcast.5.core_ref, ...), custom_call_target="tpu_custom_call" | custom-call | flops 23622320128 | bytes 46661632 | tf_op jit(solution)/shard_map/experts/pallas_call | solution.py:687
  490.0 6.8 collective-permute-done.5
  496.8 4.4 add_convert_fusion.8
  504.0 38.9 %experts.5 = (bf16[4,256,2048]{2,1,0:T(8,128)(2,1)}, bf16[4,256,2048]{2,1,0:T(8,128)(2,1)}, bf16[4,256,2048]{2,1,0:T(8,128)(2,1)}, bf16[4,256,2048]{2,1,0:T(8,12...) custom-call(s32[1]{0:T(128)} %bitcast.5.core_ref, ...), custom_call_target="tpu_custom_call", output_to_operand_aliasing={{4}: (9, {}), {5}: (10, {}), {6}: (11, {}), {7}: (12, {}), ... | custom-call | flops 23622320128 | bytes 46661632 | tf_op jit(solution)/shard_map/experts/pallas_call | solution.py:687
  542.9 6.2 collective-permute-done.6
  552.1 5.7 collective-permute-done.8
  557.8 5.4 add_convert_fusion.27
  566.3 38.9 %experts.6 = (bf16[4,256,2048]{2,1,0:T(8,128)(2,1)}, bf16[4,256,2048]{2,1,0:T(8,128)(2,1)}, bf16[4,256,2048]{2,1,0:T(8,128)(2,1)}, bf16[4,256,2048]{2,1,0:T(8,12...) custom-call(s32[1]{0:T(128)} %bitcast.5.core_ref, ...), custom_call_target="tpu_custom_call", output_to_operand_aliasing={{4}: (9, {}), {5}: (10, {}), {6}: (11, {}), {7}: (12, {}), ... | custom-call | flops 23622320128 | bytes 46661632 | tf_op jit(solution)/shard_map/experts/pallas_call | solution.py:687
  611.7 39.0 %experts.7 = (bf16[4,256,2048]{2,1,0:T(8,128)(2,1)}, bf16[4,256,2048]{2,1,0:T(8,128)(2,1)}, bf16[4,256,2048]{2,1,0:T(8,128)(2,1)}, bf16[4,256,2048]{2,1,0:T(8,12...) custom-call(s32[1]{0:T(128)} %bitcast.5.core_ref, ...), custom_call_target="tpu_custom_call", output_to_operand_aliasing={{4}: (9, {}), {5}: (10, {}), {6}: (11, {}), {7}: (12, {}), ... | custom-call | flops 23622320128 | bytes 46661632 | tf_op jit(solution)/shard_map/experts/pallas_call | solution.py:687
  650.7 5.9 collective-permute-done.11
  658.5 4.5 add_convert_fusion.7
  670.7 5.7 add_convert_fusion.5
  677.8 4.3 add_convert_fusion.19
  685.7 8.6 collective-permute-done.20
  695.8 32.4 %convolution_bitcast_fusion = f32[1,2048,1536]{2,1,0:T(8,128)} fusion(bf16[4096,2048]{1,0:T(8,128)(2,1)S(1)} %bitcast.171, bf16[4096,1536]{1,0:T(8,128)(2,1)} %get-tuple-element.157), kind=kOutput, calls=%fused_computation.5 | convolution fusion | flops 25769803776 | bytes 41943040 | tf_op jit(solution)/shard_map/dot_general | solution.py:321
  728.2 11.1 collective-permute-done.21
  746.8 4.8 all-to-all-start.1
  755.7 17.8 %collective-permute-done.22 = bf16[256,2048]{1,0:T(8,128)(2,1)S(1)} collective-permute-done((bf16[256,2048]{1,0:T(8,128)(2,1)}, bf16[256,2048]{1,0:T(8,128)(2,1)S(1)}, u32[]{:S(2)}, u32[]{:S(2)}) %collective-permute-start.22) | collective-permute-done | bytes 1048608 | tf_op jit(solution)/shard_map/ppermute | solution.py:358
  774.5 20.4 %convolution_bitcast_fusion.1 = f32[1,768,2048]{2,1,0:T(8,128)} fusion(bf16[4096,768]{1,0:T(8,128)(2,1)} %get-tuple-element.181, bf16[4096,2048]{1,0:T(8,128)(2,1)} %get-tuple-element.182), kind=kOutput, calls=%fused_computation.26 | convolution fusion | flops 12884901888 | bytes 29360128 | tf_op jit(solution)/shard_map/dot_general | solution.py:321
  821.0 5.1 collective-permute-done.28
  828.7 6.9 convolution_convert_fusion.1
  838.0 4.5 add_convert_fusion
  842.5 4.3 add_convert_fusion.1
  846.8 10.1 fusion.11.go_ref
  856.9 25.1 %attend_grad.1 = (bf16[512,2048]{1,0:T(8,128)(2,1)S(1)}, bf16[512,512]{1,0:T(8,128)(2,1)S(1)}, bf16[512,512]{1,0:T(8,128)(2,1)S(1)}, f32[4,1,128]{2,1,0:T(1,128)S(1)}, f32[4,1,128]{2,1,0:T(1,128)S(1)}) custom-call(f32[512,3072]{1,0:T(8,128)} %fusion.2.q_ref.k_ref.v_ref, f32[512,3072]{1,0:T(8,128)} %fusion.2.q_ref.k_ref.v_ref, bf16[512,2048]{1,0:T(8,128)(2,1)} %copy-done.2, ...), custom_call_target="tpu_custom_call" | custom-call | flops 5368709120 | bytes 15728640 | tf_op jit(solution)/shard_map/attend_grad/pallas_call | solution.py:549
  882.5 12.3 %collective-permute-done.30 = bf16[4,256,1024]{2,1,0:T(8,128)(2,1)} collective-permute-done((bf16[4,256,1024]{2,1,0:T(8,128)(2,1)}, bf16[4,256,1024]{2,1,0:T(8,128)(2,1)}, u32[]{:S(2)}, u32[]{:S(2)}) %collective-permute-start.30) | collective-permute-done | bytes 2097184 | tf_op jit(solution)/shard_map/ppermute | solution.py:337
  894.8 9.9 convolution_convert_fusion
  907.0 7.5 collective-permute-done.39
  926.4 11.1 fusion
  937.5 39.6 %collective-permute-done.31 = bf16[4,256,1024]{2,1,0:T(8,128)(2,1)} collective-permute-done((bf16[4,256,1024]{2,1,0:T(8,128)(2,1)}, bf16[4,256,1024]{2,1,0:T(8,128)(2,1)}, u32[]{:S(2)}, u32[]{:S(2)}) %collective-permute-start.31) | collective-permute-done | bytes 2097184 | tf_op jit(solution)/shard_map/ppermute | solution.py:337
  991.1 11.2 collective-permute-done.36
  1013.3 93.3 %collective-permute-done.47 = f32[18,128]{1,0:T(8,128)S(1)} collective-permute-done((f32[18,128]{1,0:T(8,128)S(1)}, f32[18,128]{1,0:T(8,128)S(1)}, u32[]{:S(2)}, u32[]{:S(2)}) %collective-permute-start.47) | collective-permute-done | bytes 9248 | tf_op jit(solution)/shard_map/ppermute | solution.py:398
  1108.3 21.6 %collective-permute-done.34 = bf16[256,2048]{1,0:T(8,128)(2,1)} collective-permute-done((bf16[256,2048]{1,0:T(8,128)(2,1)}, bf16[256,2048]{1,0:T(8,128)(2,1)}, u32[]{:S(2)}, u32[]{:S(2)}) %collective-permute-start.34) | collective-permute-done | bytes 1048608 | tf_op jit(solution)/shard_map/ppermute | solution.py:358
  1129.9 6.2 fusion.20
  1136.1 22.2 %reduce-scatter.3.cloned.1.call-done = bf16[128,3072]{1,0:T(8,128)(2,1)} async-done(((bf16[2048,3072]{1,0:T(8,128)(2,1)}), bf16[128,3072]{1,0:T(8,128)(2,1)}) %reduce-scatter.3.cloned.1.call-update) | async-done | bytes 786448 | tf_op jit(solution)/shard_map/reduce_scatter | solution.py:949
  1165.2 11.9 collective-permute-done.37
  (334 shorter events, 165.6 us)
Async XLA Ops:
  7.2 120.8 %all-gather.4.cloned.1.call-start = ((), (), s32[]{:S(2)}) async-start(), calls=%async_computation.4 | async-start | bytes 22282240 | tf_op jit(solution)/shard_map/all_gather | solution.py:757
  15.0 244.5 %all-gather.8.cloned.1.call-start = ((), (), s32[]{:S(2)}) async-start(), calls=%async_computation.6 | async-start | bytes 26738688 | tf_op jit(solution)/shard_map/all_gather | solution.py:767
  15.2 14.9 %collective-permute-start.3 = (bf16[256,1024]{1,0:T(8,128)(2,1)S(1)}, bf16[256,1024]{1,0:T(8,128)(2,1)S(1)}, u32[]{:S(2)}, u32[]{:S(2)}) collective-permute-start(bf16[256,1024]{1,0:T(8,128)(2,1)S(1)} %get-tuple-element.294), channel_id=1, source_target_pairs={{0,1},{1,0},{2,3},{3,2},{4,5},{5,4},{6,7},{7,6},{8,9},{9,8},{10,11... | collective-permute-start | bytes 1572872 | tf_op jit(solution)/shard_map/ppermute | solution.py:341
  31.5 419.1 %all-gather.6.cloned.1.call-start = ((), (), s32[]{:S(2)}) async-start(), calls=%async_computation.5 | async-start | bytes 35651584 | tf_op jit(solution)/shard_map/all_gather | solution.py:788
  31.7 26.6 %collective-permute-start = (bf16[256,2048]{1,0:T(8,128)(2,1)S(1)}, bf16[256,2048]{1,0:T(8,128)(2,1)}, u32[]{:S(2)}, u32[]{:S(2)}) collective-permute-start(bf16[256,2048]{1,0:T(8,128)(2,1)S(1)} %copy-done.8), channel_id=1, source_target_pairs={{0,1},{1,0},{2,3},{3,2},{4,5},{5,4},{6,7},{7,6},{8,9},{9,8},{10,11... | collective-permute-start | bytes 3145736 | tf_op jit(solution)/shard_map/ppermute | solution.py:341
  167.0 25.6 %collective-permute-start.1 = (bf16[256,2048]{1,0:T(8,128)(2,1)S(1)}, bf16[256,2048]{1,0:T(8,128)(2,1)S(1)}, u32[]{:S(2)}, u32[]{:S(2)}) collective-permute-start(bf16[256,2048]{1,0:T(8,128)(2,1)S(1)} %select_convert_fusion.1), channel_id=1, source_target_pairs={{0,1},{1,0},{2,3},{3,2},{4,5},{5,4},{6,7},{7,6},{8,9},{9,8},{10,11... | collective-permute-start | bytes 3145736 | tf_op jit(solution)/shard_map/ppermute | solution.py:341
  195.4 24.9 %collective-permute-start.2 = (bf16[256,2048]{1,0:T(8,128)(2,1)S(1)}, bf16[256,2048]{1,0:T(8,128)(2,1)S(1)}, u32[]{:S(2)}, u32[]{:S(2)}) collective-permute-start(bf16[256,2048]{1,0:T(8,128)(2,1)S(1)} %multiply_convert_fusion), channel_id=1, source_target_pairs={{0,1},{1,0},{2,3},{3,2},{4,5},{5,4},{6,7},{7,6},{8,9},{9,8},{10,11... | collective-permute-start | bytes 3145736 | tf_op jit(solution)/shard_map/ppermute | solution.py:341
  267.7 182.9 %collective-permute-start.4 = (bf16[8,2,1,256,1024]{4,3,2,1,0:T(8,128)(2,1)}, bf16[8,2,1,256,1024]{4,3,2,1,0:T(8,128)(2,1)}, u32[]{:S(2)}, u32[]{:S(2)}) collective-permute-start(bf16[8,2,1,256,1024]{4,3,2,1,0:T(8,128)(2,1)} %slice.436), channel_id=1, source_target_pairs={{0,1},{1,0},{2,3},{3,2},{4,5},{5,4},{6,7},{7,6},{8,9},{9,8},{10,11... | collective-permute-start | bytes 25165832 | tf_op jit(solution)/shard_map/ppermute | solution.py:341
  489.3 7.6 collective-permute-start.5
  501.3 47.8 %collective-permute-start.6 = (bf16[4,256,1024]{2,1,0:T(8,128)(2,1)S(1)}, bf16[4,256,1024]{2,1,0:T(8,128)(2,1)}, u32[]{:S(2)}, u32[]{:S(2)}) collective-permute-start(bf16[4,256,1024]{2,1,0:T(8,128)(2,1)S(1)} %get-tuple-element.143), channel_id=1, source_target_pairs={{0,1},{1,0},{2,3},{3,2},{4,5},{5,4},{6,7},{7,6},{8,9},{9,8},{10,11... | collective-permute-start | bytes 6291464 | tf_op jit(solution)/shard_map/ppermute | solution.py:341
  502.8 47.5 %collective-permute-start.7 = (bf16[4,256,1024]{2,1,0:T(8,128)(2,1)S(1)}, bf16[4,256,1024]{2,1,0:T(8,128)(2,1)}, u32[]{:S(2)}, u32[]{:S(2)}) collective-permute-start(bf16[4,256,1024]{2,1,0:T(8,128)(2,1)S(1)} %get-tuple-element.144), channel_id=1, source_target_pairs={{0,4},{2,6},{4,0},{6,2},{8,12},{10,14},{12,8},{14,10},{16,20},{18,... | collective-permute-start | bytes 6291464 | tf_op jit(solution)/shard_map/ppermute | solution.py:337
  551.6 119.1 %collective-permute-start.19 = (bf16[4,256,2048]{2,1,0:T(8,128)(2,1)}, bf16[4,256,2048]{2,1,0:T(8,128)(2,1)}, u32[]{:S(2)}, u32[]{:S(2)}) collective-permute-start(bf16[4,256,2048]{2,1,0:T(8,128)(2,1)} %get-tuple-element.168), channel_id=1, source_target_pairs={{0,2},{2,0},{4,6},{6,4},{8,10},{10,8},{12,14},{14,12},{16,18},{18,... | collective-permute-start | bytes 12582920 | tf_op jit(solution)/shard_map/ppermute | solution.py:333
  565.7 45.2 %collective-permute-start.13 = (bf16[2,256,1024]{2,1,0:T(8,128)(2,1)}, bf16[2,256,1024]{2,1,0:T(8,128)(2,1)}, u32[]{:S(2)}, u32[]{:S(2)}) collective-permute-start(bf16[2,256,1024]{2,1,0:T(8,128)(2,1)} %add_convert_fusion.25), channel_id=1, source_target_pairs={{0,1},{1,0},{2,3},{3,2},{4,5},{5,4},{6,7},{7,6},{8,9},{9,8},{10,11... | collective-permute-start | bytes 3145736 | tf_op jit(solution)/shard_map/ppermute | solution.py:341
  605.2 51.4 %collective-permute-start.9 = (bf16[4,256,2048]{2,1,0:T(8,128)(2,1)}, bf16[4,256,2048]{2,1,0:T(8,128)(2,1)S(1)}, u32[]{:S(2)}, u32[]{:S(2)}) collective-permute-start(bf16[4,256,2048]{2,1,0:T(8,128)(2,1)} %get-tuple-element.155), channel_id=1, source_target_pairs={{0,2},{2,0},{4,6},{6,4},{8,10},{10,8},{12,14},{14,12},{16,18},{18,... | collective-permute-start | bytes 12582920 | tf_op jit(solution)/shard_map/ppermute | solution.py:333
  608.2 42.5 %collective-permute-start.12 = (bf16[2,256,1024]{2,1,0:T(8,128)(2,1)}, bf16[2,256,1024]{2,1,0:T(8,128)(2,1)}, u32[]{:S(2)}, u32[]{:S(2)}) collective-permute-start(bf16[2,256,1024]{2,1,0:T(8,128)(2,1)} %add_convert_fusion.26), channel_id=1, source_target_pairs={{0,4},{2,6},{4,0},{6,2},{8,12},{10,14},{12,8},{14,10},{16,20},{18,... | collective-permute-start | bytes 3145736 | tf_op jit(solution)/shard_map/ppermute | solution.py:337
  609.5 41.3 %collective-permute-start.10 = (bf16[2,256,1024]{2,1,0:T(8,128)(2,1)}, bf16[2,256,1024]{2,1,0:T(8,128)(2,1)}, u32[]{:S(2)}, u32[]{:S(2)}) collective-permute-start(bf16[2,256,1024]{2,1,0:T(8,128)(2,1)} %get-tuple-element.160), channel_id=1, source_target_pairs={{0,1},{1,0},{2,3},{3,2},{4,5},{5,4},{6,7},{7,6},{8,9},{9,8},{10,11... | collective-permute-start | bytes 3145736 | tf_op jit(solution)/shard_map/ppermute | solution.py:341
  610.9 45.7 %collective-permute-start.11 = (bf16[2,256,1024]{2,1,0:T(8,128)(2,1)}, bf16[2,256,1024]{2,1,0:T(8,128)(2,1)}, u32[]{:S(2)}, u32[]{:S(2)}) collective-permute-start(bf16[2,256,1024]{2,1,0:T(8,128)(2,1)} %get-tuple-element.161), channel_id=1, source_target_pairs={{0,4},{2,6},{4,0},{6,2},{8,12},{10,14},{12,8},{14,10},{16,20},{18,... | collective-permute-start | bytes 3145736 | tf_op jit(solution)/shard_map/ppermute | solution.py:337
  656.6 21.2 %collective-permute-start.14 = (bf16[4,256,2048]{2,1,0:T(8,128)(2,1)}, bf16[4,256,2048]{2,1,0:T(8,128)(2,1)S(1)}, u32[]{:S(2)}, u32[]{:S(2)}) collective-permute-start(bf16[4,256,2048]{2,1,0:T(8,128)(2,1)} %get-tuple-element.166), channel_id=1, source_target_pairs={{0,2},{2,0},{4,6},{6,4},{8,10},{10,8},{12,14},{14,12},{16,18},{18,... | collective-permute-start | bytes 12582920 | tf_op jit(solution)/shard_map/ppermute | solution.py:333
  667.6 26.7 %collective-permute-start.20 = (bf16[256,2048]{1,0:T(8,128)(2,1)S(1)}, bf16[256,2048]{1,0:T(8,128)(2,1)S(1)}, u32[]{:S(2)}, u32[]{:S(2)}) collective-permute-start(bf16[256,2048]{1,0:T(8,128)(2,1)S(1)} %pad_maximum_fusion.13), channel_id=1, source_target_pairs={{0,24},{2,26},{4,28},{6,30},{8,0},{10,2},{12,4},{14,6},{16,8},{18,... | collective-permute-start | bytes 3145736 | tf_op jit(solution)/shard_map/ppermute | solution.py:358
  677.5 61.9 %collective-permute-start.21 = (bf16[256,2048]{1,0:T(8,128)(2,1)}, bf16[256,2048]{1,0:T(8,128)(2,1)}, u32[]{:S(2)}, u32[]{:S(2)}) collective-permute-start(bf16[256,2048]{1,0:T(8,128)(2,1)} %pad_maximum_fusion.14), channel_id=1, source_target_pairs={{0,16},{2,18},{4,20},{6,22},{8,24},{10,26},{12,28},{14,30},{16,0},... | collective-permute-start | bytes 3145736 | tf_op jit(solution)/shard_map/ppermute | solution.py:358
  682.1 57.2 %collective-permute-start.18 = (bf16[2,256,1024]{2,1,0:T(8,128)(2,1)}, bf16[2,256,1024]{2,1,0:T(8,128)(2,1)}, u32[]{:S(2)}, u32[]{:S(2)}) collective-permute-start(bf16[2,256,1024]{2,1,0:T(8,128)(2,1)} %get-tuple-element.253), channel_id=1, source_target_pairs={{0,1},{1,0},{2,3},{3,2},{4,5},{5,4},{6,7},{7,6},{8,9},{9,8},{10,11... | collective-permute-start | bytes 3145736 | tf_op jit(solution)/shard_map/ppermute | solution.py:341
  683.6 55.7 %collective-permute-start.17 = (bf16[2,256,1024]{2,1,0:T(8,128)(2,1)S(1)}, bf16[2,256,1024]{2,1,0:T(8,128)(2,1)}, u32[]{:S(2)}, u32[]{:S(2)}) collective-permute-start(bf16[2,256,1024]{2,1,0:T(8,128)(2,1)S(1)} %get-tuple-element.254), channel_id=1, source_target_pairs={{0,4},{2,6},{4,0},{6,2},{8,12},{10,14},{12,8},{14,10},{16,20},{18,... | collective-permute-start | bytes 3145736 | tf_op jit(solution)/shard_map/ppermute | solution.py:337
  684.7 54.6 %collective-permute-start.16 = (bf16[2,256,1024]{2,1,0:T(8,128)(2,1)S(1)}, bf16[2,256,1024]{2,1,0:T(8,128)(2,1)}, u32[]{:S(2)}, u32[]{:S(2)}) collective-permute-start(bf16[2,256,1024]{2,1,0:T(8,128)(2,1)S(1)} %get-tuple-element.255), channel_id=1, source_target_pairs={{0,4},{2,6},{4,0},{6,2},{8,12},{10,14},{12,8},{14,10},{16,20},{18,... | collective-permute-start | bytes 3145736 | tf_op jit(solution)/shard_map/ppermute | solution.py:337
  694.3 45.1 %collective-permute-start.15 = (bf16[2,256,1024]{2,1,0:T(8,128)(2,1)S(1)}, bf16[2,256,1024]{2,1,0:T(8,128)(2,1)}, u32[]{:S(2)}, u32[]{:S(2)}) collective-permute-start(bf16[2,256,1024]{2,1,0:T(8,128)(2,1)S(1)} %get-tuple-element.256), channel_id=1, source_target_pairs={{0,1},{1,0},{2,3},{3,2},{4,5},{5,4},{6,7},{7,6},{8,9},{9,8},{10,11... | collective-permute-start | bytes 3145736 | tf_op jit(solution)/shard_map/ppermute | solution.py:341
  745.8 27.7 %collective-permute-start.22 = (bf16[256,2048]{1,0:T(8,128)(2,1)}, bf16[256,2048]{1,0:T(8,128)(2,1)S(1)}, u32[]{:S(2)}, u32[]{:S(2)}) collective-permute-start(bf16[256,2048]{1,0:T(8,128)(2,1)} %pad_maximum_fusion.16), channel_id=1, source_target_pairs={{0,8},{2,10},{4,12},{6,14},{8,16},{10,18},{12,20},{14,22},{16,24},... | collective-permute-start | bytes 3145736 | tf_op jit(solution)/shard_map/ppermute | solution.py:358
  746.8 48.1 %all-to-all-start.1 = ((f32[32,1,256]{2,1,0:T(1,128)}), f32[32,1,256]{2,1,0:T(1,128)S(1)}, u32[]{:S(2)}, u32[]{:S(2)}) async-start(f32[32,1,256]{2,1,0:T(1,128)} %bitcast.37), calls=%async_computation.1 | async-start | bytes 65536 | tf_op jit(solution)/shard_map/all_to_all | solution.py:880
  751.6 354.9 %reduce-scatter.5.cloned.1.call-start = ((), (), s32[]{:S(2)}) async-start(), calls=%async_computation.8 | async-start | bytes 8912896 | tf_op jit(solution)/shard_map/reduce_scatter | solution.py:942
  751.9 49.6 %collective-permute-start.23 = (bf16[4,256,1024]{2,1,0:T(8,128)(2,1)}, bf16[4,256,1024]{2,1,0:T(8,128)(2,1)}, u32[]{:S(2)}, u32[]{:S(2)}) collective-permute-start(bf16[4,256,1024]{2,1,0:T(8,128)(2,1)} %get-tuple-element.187), channel_id=1, source_target_pairs={{0,1},{1,0},{2,3},{3,2},{4,5},{5,4},{6,7},{7,6},{8,9},{9,8},{10,11... | collective-permute-start | bytes 6291464 | tf_op jit(solution)/shard_map/ppermute | solution.py:341
  753.7 48.0 %collective-permute-start.24 = (bf16[4,256,1024]{2,1,0:T(8,128)(2,1)}, bf16[4,256,1024]{2,1,0:T(8,128)(2,1)}, u32[]{:S(2)}, u32[]{:S(2)}) collective-permute-start(bf16[4,256,1024]{2,1,0:T(8,128)(2,1)} %get-tuple-element.188), channel_id=1, source_target_pairs={{0,4},{2,6},{4,0},{6,2},{8,12},{10,14},{12,8},{14,10},{16,20},{18,... | collective-permute-start | bytes 6291464 | tf_op jit(solution)/shard_map/ppermute | solution.py:337
  755.2 46.5 %collective-permute-start.25 = (bf16[4,256,2048]{2,1,0:T(8,128)(2,1)}, bf16[4,256,2048]{2,1,0:T(8,128)(2,1)}, u32[]{:S(2)}, u32[]{:S(2)}) collective-permute-start(bf16[4,256,2048]{2,1,0:T(8,128)(2,1)} %get-tuple-element.190), channel_id=1, source_target_pairs={{0,2},{2,0},{4,6},{6,4},{8,10},{10,8},{12,14},{14,12},{16,18},{18,... | collective-permute-start | bytes 12582920 | tf_op jit(solution)/shard_map/ppermute | solution.py:333
  755.2 46.5 %collective-permute-start.26 = (bf16[4,256,2048]{2,1,0:T(8,128)(2,1)}, bf16[4,256,2048]{2,1,0:T(8,128)(2,1)}, u32[]{:S(2)}, u32[]{:S(2)}) collective-permute-start(bf16[4,256,2048]{2,1,0:T(8,128)(2,1)} %get-tuple-element.192), channel_id=1, source_target_pairs={{0,2},{2,0},{4,6},{6,4},{8,10},{10,8},{12,14},{14,12},{16,18},{18,... | collective-permute-start | bytes 12582920 | tf_op jit(solution)/shard_map/ppermute | solution.py:333
  773.5 28.2 %collective-permute-start.27 = (bf16[4,256,2048]{2,1,0:T(8,128)(2,1)}, bf16[4,256,2048]{2,1,0:T(8,128)(2,1)}, u32[]{:S(2)}, u32[]{:S(2)}) collective-permute-start(bf16[4,256,2048]{2,1,0:T(8,128)(2,1)} %get-tuple-element.194), channel_id=1, source_target_pairs={{0,2},{2,0},{4,6},{6,4},{8,10},{10,8},{12,14},{14,12},{16,18},{18,... | collective-permute-start | bytes 12582920 | tf_op jit(solution)/shard_map/ppermute | solution.py:333
  801.7 24.5 %collective-permute-start.28 = (bf16[256,2048]{1,0:T(8,128)(2,1)S(1)}, bf16[256,2048]{1,0:T(8,128)(2,1)S(1)}, u32[]{:S(2)}, u32[]{:S(2)}) collective-permute-start(bf16[256,2048]{1,0:T(8,128)(2,1)S(1)} %fusion.51), channel_id=1, source_target_pairs={{0,1},{1,0},{2,3},{3,2},{4,5},{5,4},{6,7},{7,6},{8,9},{9,8},{10,11... | collective-permute-start | bytes 3145736 | tf_op jit(solution)/shard_map/ppermute | solution.py:341
  835.6 322.7 %reduce-scatter.3.cloned.1.call-start = ((), (), s32[]{:S(2)}) async-start(), calls=%async_computation.7 | async-start | bytes 13369344 | tf_op jit(solution)/shard_map/reduce_scatter | solution.py:949
  835.7 46.7 %collective-permute-start.29 = (bf16[4,256,1024]{2,1,0:T(8,128)(2,1)}, bf16[4,256,1024]{2,1,0:T(8,128)(2,1)}, u32[]{:S(2)}, u32[]{:S(2)}) collective-permute-start(bf16[4,256,1024]{2,1,0:T(8,128)(2,1)} %pad_maximum_fusion.7), channel_id=1, source_target_pairs={{0,1},{1,0},{2,3},{3,2},{4,5},{5,4},{6,7},{7,6},{8,9},{9,8},{10,11... | collective-permute-start | bytes 6291464 | tf_op jit(solution)/shard_map/ppermute | solution.py:341
  837.3 57.5 %collective-permute-start.30 = (bf16[4,256,1024]{2,1,0:T(8,128)(2,1)}, bf16[4,256,1024]{2,1,0:T(8,128)(2,1)}, u32[]{:S(2)}, u32[]{:S(2)}) collective-permute-start(bf16[4,256,1024]{2,1,0:T(8,128)(2,1)} %pad_maximum_fusion.6), channel_id=1, source_target_pairs={{0,4},{2,6},{4,0},{6,2},{8,12},{10,14},{12,8},{14,10},{16,20},{18,... | collective-permute-start | bytes 6291464 | tf_op jit(solution)/shard_map/ppermute | solution.py:337
  906.3 8.2 collective-permute-start.39
  923.1 54.0 %collective-permute-start.31 = (bf16[4,256,1024]{2,1,0:T(8,128)(2,1)}, bf16[4,256,1024]{2,1,0:T(8,128)(2,1)}, u32[]{:S(2)}, u32[]{:S(2)}) collective-permute-start(bf16[4,256,1024]{2,1,0:T(8,128)(2,1)} %add_convert_fusion.1), channel_id=1, source_target_pairs={{0,4},{2,6},{4,0},{6,2},{8,12},{10,14},{12,8},{14,10},{16,20},{18,... | collective-permute-start | bytes 6291464 | tf_op jit(solution)/shard_map/ppermute | solution.py:337
  924.2 52.9 %collective-permute-start.32 = (bf16[4,256,1024]{2,1,0:T(8,128)(2,1)}, bf16[4,256,1024]{2,1,0:T(8,128)(2,1)}, u32[]{:S(2)}, u32[]{:S(2)}) collective-permute-start(bf16[4,256,1024]{2,1,0:T(8,128)(2,1)} %add_convert_fusion), channel_id=1, source_target_pairs={{0,1},{1,0},{2,3},{3,2},{4,5},{5,4},{6,7},{7,6},{8,9},{9,8},{10,11... | collective-permute-start | bytes 6291464 | tf_op jit(solution)/shard_map/ppermute | solution.py:341
  925.6 79.0 %collective-permute-start.43 = (f32[33,128]{1,0:T(8,128)S(1)}, f32[33,128]{1,0:T(8,128)S(1)}, u32[]{:S(2)}, u32[]{:S(2)}) collective-permute-start(f32[33,128]{1,0:T(8,128)S(1)} %bitcast.203), channel_id=1, source_target_pairs={{0,1},{1,0},{2,3},{3,2},{4,5},{5,4},{6,7},{7,6},{8,9},{9,8},{10,11... | collective-permute-start | bytes 50696 | tf_op jit(solution)/shard_map/ppermute | solution.py:341
  977.5 24.8 %collective-permute-start.36 = (bf16[256,2048]{1,0:T(8,128)(2,1)S(1)}, bf16[256,2048]{1,0:T(8,128)(2,1)S(1)}, u32[]{:S(2)}, u32[]{:S(2)}) collective-permute-start(bf16[256,2048]{1,0:T(8,128)(2,1)S(1)} %select_convert_fusion), channel_id=1, source_target_pairs={{0,1},{1,0},{2,3},{3,2},{4,5},{5,4},{6,7},{7,6},{8,9},{9,8},{10,11... | collective-permute-start | bytes 3145736 | tf_op jit(solution)/shard_map/ppermute | solution.py:341
  986.6 121.7 %collective-permute-start.33 = (bf16[256,2048]{1,0:T(8,128)(2,1)}, bf16[256,2048]{1,0:T(8,128)(2,1)}, u32[]{:S(2)}, u32[]{:S(2)}) collective-permute-start(bf16[256,2048]{1,0:T(8,128)(2,1)} %pad_maximum_fusion.17), channel_id=1, source_target_pairs={{0,24},{2,26},{4,28},{6,30},{8,0},{10,2},{12,4},{14,6},{16,8},{18,... | collective-permute-start | bytes 3145736 | tf_op jit(solution)/shard_map/ppermute | solution.py:358
  989.4 140.5 %collective-permute-start.34 = (bf16[256,2048]{1,0:T(8,128)(2,1)}, bf16[256,2048]{1,0:T(8,128)(2,1)}, u32[]{:S(2)}, u32[]{:S(2)}) collective-permute-start(bf16[256,2048]{1,0:T(8,128)(2,1)} %pad_maximum_fusion.18), channel_id=1, source_target_pairs={{0,16},{2,18},{4,20},{6,22},{8,24},{10,26},{12,28},{14,30},{16,0},... | collective-permute-start | bytes 3145736 | tf_op jit(solution)/shard_map/ppermute | solution.py:358
  990.5 139.4 %collective-permute-start.35 = (bf16[256,2048]{1,0:T(8,128)(2,1)}, bf16[256,2048]{1,0:T(8,128)(2,1)}, u32[]{:S(2)}, u32[]{:S(2)}) collective-permute-start(bf16[256,2048]{1,0:T(8,128)(2,1)} %pad_maximum_fusion.19), channel_id=1, source_target_pairs={{0,8},{2,10},{4,12},{6,14},{8,16},{10,18},{12,20},{14,22},{16,24},... | collective-permute-start | bytes 3145736 | tf_op jit(solution)/shard_map/ppermute | solution.py:358
  1013.3 93.3 %collective-permute-start.47 = (f32[18,128]{1,0:T(8,128)S(1)}, f32[18,128]{1,0:T(8,128)S(1)}, u32[]{:S(2)}, u32[]{:S(2)}) collective-permute-start(f32[18,128]{1,0:T(8,128)S(1)} %add.600), channel_id=1, source_target_pairs={{0,8},{2,10},{4,12},{6,14},{8,0},{10,2},{12,4},{14,6},{16,24},{18,... | collective-permute-start | bytes 27656 | tf_op jit(solution)/shard_map/ppermute | solution.py:398
  1106.6 29.6 %collective-permute-start.48 = (f32[18,128]{1,0:T(8,128)S(1)}, f32[18,128]{1,0:T(8,128)S(1)}, u32[]{:S(2)}, u32[]{:S(2)}) collective-permute-start(f32[18,128]{1,0:T(8,128)S(1)} %add.601), channel_id=1, source_target_pairs={{0,16},{2,18},{4,20},{6,22},{8,24},{10,26},{12,28},{14,30},{16,0},... | collective-permute-start | bytes 27656 | tf_op jit(solution)/shard_map/ppermute | solution.py:398
  1106.6 55.5 %collective-permute-start.38 = (bf16[128,2048]{1,0:T(8,128)(2,1)}, bf16[128,2048]{1,0:T(8,128)(2,1)}, u32[]{:S(2)}, u32[]{:S(2)}) collective-permute-start(bf16[128,2048]{1,0:T(8,128)(2,1)} %reduce-scatter.5.cloned.1.call-done), channel_id=1, source_target_pairs={{0,1},{1,0},{2,3},{3,2},{4,5},{5,4},{6,7},{7,6},{8,9},{9,8},{10,11... | collective-permute-start | bytes 1572872 | tf_op jit(solution)/shard_map/ppermute | solution.py:341
  1158.4 18.7 %collective-permute-start.37 = (bf16[128,3072]{1,0:T(8,128)(2,1)}, bf16[128,3072]{1,0:T(8,128)(2,1)S(1)}, u32[]{:S(2)}, u32[]{:S(2)}) collective-permute-start(bf16[128,3072]{1,0:T(8,128)(2,1)} %reduce-scatter.3.cloned.1.call-done), channel_id=1, source_target_pairs={{0,1},{1,0},{2,3},{3,2},{4,5},{5,4},{6,7},{7,6},{8,9},{9,8},{10,11... | collective-permute-start | bytes 2359304 | tf_op jit(solution)/shard_map/ppermute | solution.py:341
  (68 other events, 1146.7 us)
Sparse Core Ops, SparseCore 0:
  15.2 112.8 all-gather.3
  130.2 129.3 all-gather.7
  261.8 168.0 all-gather.5
  835.8 115.9 reduce-scatter.4
  955.6 202.7 reduce-scatter.2

commit v6 on v5

--- a/solution.py
+++ b/solution.py
@@ -570,40 +570,37 @@
     )(projected, projected, roped_q, roped_k, values_low, grad, cosine, sine, query_gain, key_gain)
 
 
-def expert_kernel(core_ref, order, m_ref, near_ref, far_ref, g_ref, w_ref, gu_ref, dn_ref, *refs):
-    (keep_out, send_out, keep_back, send_back, gate_back, rows_ref, dy_ref, z_ref, pair_ref) = refs[-9:]
-    core = core_ref[0]
-    far = order[5 * pl.program_id(0) + 2] == 1
-    block = m_ref.shape[3]
-    hidden = dn_ref.shape[0]
-    slots = z_ref.shape[0] // 2
+def placed(gate, slots):
+    block = gate.shape[1]
     shape = (block, block)
     earlier = (
         lax.broadcasted_iota(jnp.int32, shape, 0) < lax.broadcasted_iota(jnp.int32, shape, 1)
     ).astype(low)
-    slot_ids = lax.broadcasted_iota(jnp.int32, (slots, block), 0)
+    hit = jnp.where(gate >= 0.0, 1.0, 0.0)
+    count = mul(jnp.broadcast_to(hit, (8, block)).astype(low), earlier)[:1].astype(jnp.int32)
+    place = (lax.broadcasted_iota(jnp.int32, (slots, block), 0) == count) & (hit > 0.5)
+    weight = jnp.sum(jnp.where(place, gate, 0.0), axis=1, keepdims=True)
+    return place, place.astype(full).astype(low), weight
+
+
+def expert_kernel(core_ref, order, m_ref, g_ref, far_ref, w_ref, gu_ref, dn_ref, *refs):
+    keep_back, send_back, gate_back, rows_ref, dy_ref, z_ref, pair_ref = refs[-7:]
+    core = core_ref[0]
+    far = order[4 * pl.program_id(0) + 2] == 1
+    width = m_ref.shape[4]
+    hidden = dn_ref.shape[0]
+    slots = z_ref.shape[0] // 2
     places, picks, weights, rows, grads = [], [], [], [], []
     for part in range(2):
         at = lax.rem(core + part, 2)
-        gate = w_ref[0, at, 0]
-        hit = jnp.where(gate >= 0.0, 1.0, 0.0)
-        ones = jnp.broadcast_to(hit, (8, block)).astype(low)
-        count = mul(ones, earlier)[:1].astype(jnp.int32)
-        place = (slot_ids == count) & (hit > 0.5)
-        pick = place.astype(full).astype(low)
+        place, pick, weight = placed(w_ref[0, at, 0], slots)
         places.append(place)
         picks.append(pick)
-        weights.append(jnp.sum(jnp.where(place, gate, 0.0), axis=1, keepdims=True))
+        weights.append(weight)
         rows.append(mul(pick, m_ref[0, at, 0]).astype(low))
-        grads.append(
-            jnp.concatenate(
-                [
-                    mul(pick, jnp.where(far, far_ref[0, at, 0], near_ref[0, at, 0])),
-                    mul(pick, g_ref[0, at, 0]),
-                ],
-                axis=1,
-            )
-        )
+        near_rows = g_ref[0, at, :, :width]
+        far_rows = jnp.concatenate([far_ref[0, at], g_ref[0, at, :, width:]], axis=1)
+        grads.append(mul(pick, jnp.where(far, far_rows, near_rows)).astype(low))
     row, grad, weight = (jnp.concatenate(items, axis=0) for items in (rows, grads, weights))
     rows_ref[...] = row
     paired = mul(row, gu_ref[...])
@@ -612,18 +609,10 @@
     act = gate_in * sig
     z = (act * up).astype(low)
     z_ref[...] = z
-    y = mul(z, dn_ref[...]).astype(low).astype(full)
-    grad_gate = jnp.sum(grad * y, axis=1, keepdims=True)
-    y_scaled = (weight * y).astype(low)
-    dy = (weight * grad).astype(low)
-    dy_ref[...] = dy
-    for part, out in enumerate((keep_out, send_out)):
-        mine = slice(part * slots, (part + 1) * slots)
-        out[0] = mul(picks[part], y_scaled[mine], lhs_turned).astype(low)
-        gate_back[0, lax.rem(core + part, 2), 0] = jnp.sum(
-            jnp.where(places[part], grad_gate[mine], 0.0), axis=0, keepdims=True
-        )
-    dz = mul(dy, dn_ref[...], rhs_turned)
+    dy_ref[...] = (weight * grad.astype(full)).astype(low)
+    unweighted = mul(grad, dn_ref[...], rhs_turned)
+    grad_gate = jnp.sum(unweighted * z.astype(full), axis=1, keepdims=True)
+    dz = weight * unweighted
     grad_in = dz * up * (sig * (1.0 + gate_in * (1.0 - sig)))
     pair = jnp.concatenate([grad_in, dz * act], axis=1).astype(low)
     pair_ref[...] = pair
@@ -631,30 +620,30 @@
     for part, out in enumerate((keep_back, send_back)):
         mine = slice(part * slots, (part + 1) * slots)
         out[0] = mul(picks[part], back[mine], lhs_turned).astype(low)
+        gate_back[0, lax.rem(core + part, 2), 0] = jnp.sum(
+            jnp.where(places[part], grad_gate[mine], 0.0), axis=0, keepdims=True
+        )
 
 
 def run_expert(core, order, first, total_steps, m_all, g_all, g_far, gates_all, gate_up, down, slots, kept):
     places, _, _, block, width = m_all.shape
     paired = gate_up.shape[1]
-    steps = order.shape[0] // 5
+    steps = order.shape[0] // 4
     part_rows = steps * 2 * slots
     hidden = paired // 2
     shape = jax.ShapeDtypeStruct
 
     def gates_at(i, core, order):
-        return (order[5 * i], 0, order[5 * i + 1], 0, 0)
+        return (order[4 * i], 0, order[4 * i + 1], 0, 0)
 
     def token_at(i, core, order):
-        return (order[5 * i], 0, order[5 * i + 2], 0, 0)
-
-    def half_at(i, core, order):
-        return (order[5 * i], 0, 1 + order[5 * i + 2], 0, 0)
+        return (order[4 * i], 0, order[4 * i + 2], 0, 0)
 
     def near_at(i, core, order):
-        return (order[5 * i + 3], 0, 0, 0, 0)
+        return (order[4 * i], 0, 0, 0)
 
     def far_at(i, core, order):
-        return (order[5 * i + 4], 0, 0, 0, 0)
+        return (order[4 * i + 3], 0, 0, 0)
 
     def fixed(i, core, order):
         return (0, 0)
@@ -667,38 +656,134 @@
 
     small = pl.BlockSpec((1, 2, 1, 1, block), gates_at)
     one_block = pl.BlockSpec((1, block, width), stacked)
-    half_block = (1, 2, 1, block, width // 2)
     widths = (width, width, hidden, paired)
     grid_spec = pltpu.PrefetchScalarGridSpec(
         num_scalar_prefetch=2,
         grid=(steps,),
         in_specs=[
             pl.BlockSpec((1, 2, 1, block, width), token_at),
-            pl.BlockSpec(half_block, near_at),
-            pl.BlockSpec(half_block, far_at),
-            pl.BlockSpec(half_block, half_at),
+            pl.BlockSpec((1, 2, block, g_all.shape[3]), near_at),
+            pl.BlockSpec((1, 2, block, g_far.shape[3]), far_at),
             small,
             pl.BlockSpec(gate_up.shape, fixed, pipeline_mode=pl.Buffered(1)),
             pl.BlockSpec(down.shape, fixed, pipeline_mode=pl.Buffered(1)),
         ]
         + [pl.BlockSpec(memory_space=pl.ANY)] * (0 if kept is None else 5),
-        out_specs=[one_block] * 4 + [small] + [pl.BlockSpec((2 * slots, n), flat) for n in widths],
+        out_specs=[one_block] * 2 + [small] + [pl.BlockSpec((2 * slots, n), flat) for n in widths],
     )
     return pl.pallas_call(
         expert_kernel,
         grid_spec=grid_spec,
-        out_shape=[shape((steps, block, width), low)] * 4
+        out_shape=[shape((steps, block, width), low)] * 2
         + [shape((places, 2, 2, 1, block), full)]
         + [shape((total_steps * 2 * slots, n), low) for n in widths],
-        input_output_aliases={} if kept is None else {9 + i: 4 + i for i in range(5)},
+        input_output_aliases={} if kept is None else {8 + i: 2 + i for i in range(5)},
         compiler_params=pltpu.CompilerParams(vmem_limit_bytes=vmem_bytes),
         cost_estimate=pl.CostEstimate(
-            flops=part_rows * width * (4 * paired + 4 * hidden + 8 * block),
-            bytes_accessed=steps * block * width * 16 + part_rows * (width * 4 + paired * 3),
+            flops=part_rows * width * (4 * paired + 2 * hidden + 6 * block),
+            bytes_accessed=steps * block * width * 12 + part_rows * (width * 4 + paired * 3),
             transcendentals=part_rows * hidden,
         ),
         name="experts",
-    )(core, order, m_all, g_all, g_far, g_all, gates_all, gate_up, down, *(() if kept is None else kept))
+    )(core, order, m_all, g_all, g_far, gates_all, gate_up, down, *(() if kept is None else kept))
+
+
+def result_kernel(core_ref, order, z_ref, w_ref, dn_ref, keep_out, send_out):
+    core = core_ref[0]
+    slots = z_ref.shape[0] // 2
+    y = mul(z_ref[...], dn_ref[...]).astype(low).astype(full)
+    for part, out in enumerate((keep_out, send_out)):
+        _, pick, weight = placed(w_ref[0, lax.rem(core + part, 2), 0], slots)
+        scaled = (weight * y[part * slots : (part + 1) * slots]).astype(low)
+        out[0] = mul(pick, scaled, lhs_turned).astype(low)
+
+
+def run_result(core, order, first, hidden, gates_all, down, slots):
+    block, width, inner = gates_all.shape[4], down.shape[1], down.shape[0]
+    steps = order.shape[0] // 4
+    one_block = pl.BlockSpec((1, block, width), lambda i, core, order: (i, 0, 0))
+    return pl.pallas_call(
+        result_kernel,
+        grid_spec=pltpu.PrefetchScalarGridSpec(
+            num_scalar_prefetch=2,
+            grid=(steps,),
+            in_specs=[
+                pl.BlockSpec((2 * slots, inner), lambda i, core, order: (first + i, 0)),
+                pl.BlockSpec(
+                    (1, 2, 1, 1, block), lambda i, core, order: (order[4 * i], 0, order[4 * i + 1], 0, 0)
+                ),
+                pl.BlockSpec(down.shape, lambda i, core, order: (0, 0), pipeline_mode=pl.Buffered(1)),
+            ],
+            out_specs=[one_block] * 2,
+        ),
+        out_shape=[jax.ShapeDtypeStruct((steps, block, width), low)] * 2,
+        compiler_params=pltpu.CompilerParams(vmem_limit_bytes=vmem_bytes),
+        cost_estimate=pl.CostEstimate(
+            flops=steps * 2 * slots * width * (2 * inner + 2 * block),
+            bytes_accessed=steps * (4 * block * width + 4 * slots * inner) + 2 * inner * width,
+            transcendentals=0,
+        ),
+        name="results",
+    )(core, order, hidden, gates_all, down)
+
+
+def own_heads_kernel(rank, qkv_ref, out_ref, o_ref, *, head_dim, heads):
+    first = rank[0] == 0
+    for head in range(heads):
+        pair = [qkv_ref[:, (2 * head + i) * head_dim : (2 * head + i + 1) * head_dim] for i in range(2)]
+        o_ref[:, head * head_dim : (head + 1) * head_dim] = jnp.where(first, pair[0], pair[1])
+    kv = qkv_ref.shape[1] - 2 * heads * head_dim
+    o_ref[:, heads * head_dim : heads * head_dim + kv] = qkv_ref[:, 2 * heads * head_dim :]
+    o_ref[:, heads * head_dim + kv :] = jnp.where(first, out_ref[:head_dim], out_ref[head_dim:])
+
+
+def own_heads(rank, qkv_weight, out_weight, head_dim, heads):
+    kv = qkv_weight.shape[1] - 2 * heads * head_dim
+    return pl.pallas_call(
+        functools.partial(own_heads_kernel, head_dim=head_dim, heads=heads),
+        grid_spec=pltpu.PrefetchScalarGridSpec(
+            num_scalar_prefetch=1,
+            grid=(1,),
+            in_specs=[
+                pl.BlockSpec(qkv_weight.shape, lambda i, rank: (0, 0)),
+                pl.BlockSpec(out_weight.shape, lambda i, rank: (0, 0)),
+            ],
+            out_specs=pl.BlockSpec(
+                (qkv_weight.shape[0], heads * head_dim + kv + out_weight.shape[1]), lambda i, rank: (0, 0)
+            ),
+        ),
+        out_shape=jax.ShapeDtypeStruct(
+            (qkv_weight.shape[0], heads * head_dim + kv + out_weight.shape[1]), qkv_weight.dtype
+        ),
+        name="own_heads",
+    )(rank, qkv_weight, out_weight)
+
+
+def all_heads_kernel(rank, mine_ref, other_ref, o_ref, *, head_dim, heads):
+    first = rank[0] == 0
+    for head in range(heads):
+        cols = slice(head * head_dim, (head + 1) * head_dim)
+        mine, other = mine_ref[:, cols].astype(full), other_ref[:, cols].astype(full)
+        o_ref[:, 2 * head * head_dim : (2 * head + 1) * head_dim] = jnp.where(first, mine, other)
+        o_ref[:, (2 * head + 1) * head_dim : (2 * head + 2) * head_dim] = jnp.where(first, other, mine)
+    o_ref[:, 2 * heads * head_dim :] = mine_ref[:, heads * head_dim :].astype(full) + other_ref[
+        :, heads * head_dim :
+    ].astype(full)
+
+
+def all_heads(rank, mine, other, head_dim, heads):
+    rows, width = mine.shape
+    return pl.pallas_call(
+        functools.partial(all_heads_kernel, head_dim=head_dim, heads=heads),
+        grid_spec=pltpu.PrefetchScalarGridSpec(
+            num_scalar_prefetch=1,
+            grid=(1,),
+            in_specs=[pl.BlockSpec((rows, width), lambda i, rank: (0, 0))] * 2,
+            out_specs=pl.BlockSpec((rows, width + heads * head_dim), lambda i, rank: (0, 0)),
+        ),
+        out_shape=jax.ShapeDtypeStruct((rows, width + heads * head_dim), full),
+        name="all_heads",
+    )(rank, mine, other)
 
 
 def rms_back(values, gain, grad):
@@ -748,10 +833,8 @@
         second = jnp.where(rank == 0, other, values)
         return in_order(first, second)
 
-    by_parity = qkv_weight[:, : 2 * width_q].reshape(shard, my_heads, 2, head_dim)
-    q_local = jnp.where(rank == 0, by_parity[:, :, 0], by_parity[:, :, 1]).reshape(shard, width_q)
-    out_local = lax.dynamic_slice_in_dim(out_weight, rank * head_dim, head_dim, 0)
-    weights_local = jnp.concatenate([q_local, qkv_weight[:, 2 * width_q :], out_local], axis=1)
+    rank_at = rank[None].astype(jnp.int32)
+    weights_local = own_heads(rank_at, qkv_weight, out_weight, head_dim, my_heads)
     small_local = jnp.concatenate([router_weight, attn_gain[:, None], moe_gain[:, None]], axis=1)
     small_all = lax.all_gather(small_local, "fsdp", axis=0, tiled=True)
     weights_all = lax.all_gather(weights_local, "fsdp", axis=0, tiled=True)
@@ -760,13 +843,10 @@
     router_all = small_all[:, :experts_all]
     attn_all = small_all[:, experts_all].astype(full)
     moe_all = small_all[:, experts_all + 1].astype(full)
-    g_half = width // 2
-    g_local = jnp.stack(
-        [cotangent[:, :g_half], cotangent[:, g_half:], swap_ctx(cotangent[:, g_half:])]
-    )
+    late_cols = width * 7 // 16
     g_all = lax.all_gather(
-        g_local.reshape(3 * rows_dev, g_half), "fsdp", axis=0, tiled=True
-    ).reshape(fsdp // 2, 2, 3, rows_dev, g_half)
+        jnp.concatenate([cotangent, swap_ctx(cotangent[:, late_cols:])], axis=1), "fsdp", axis=0, tiled=True
+    ).reshape(fsdp // 2, 2, rows_dev, 2 * width - late_cols)
 
     sequence_in = sequence(tokens).astype(full)
     low_in = rms_scale(sequence_in, attn_all).astype(low)
@@ -797,7 +877,7 @@
     gates_all = lax.all_to_all(gates_sent, both, split_axis=0, concat_axis=0, tiled=True)
 
     g_all, gates_all = hold(g_all, gates_all)
-    g_far = swap_ctx(g_all[:, :, :1])
+    g_far = swap_ctx(g_all[..., :late_cols])
 
     lines = fsdp // 4
     places = list(range(1, lines)) + [0]
@@ -807,22 +887,26 @@
     gates_all = gates_all.reshape(fsdp // 2, 2, 2, 1, rows_dev)
     state = dict(kept=None, first=0, core=core[None].astype(jnp.int32))
 
+    def order_of(steps):
+        spots = [((place - p) % lines) * 2 + (side + d) % 2 for d, _, p in steps]
+        far = [i for i, step in enumerate(steps) if step[1] == 1] or [0]
+        return jnp.stack(
+            [
+                jnp.asarray(item, jnp.int32)
+                for i, step in enumerate(steps)
+                for item in (
+                    spots[i],
+                    (rank + step[1]) % 2,
+                    step[1],
+                    spots[min(far, key=lambda j, i=i: abs(j - i))],
+                )
+            ]
+        )
+
     def call(steps, raw=False):
-        spots = [((place - p) % lines) * 2 + (side + d) % 2 for d, _, p in steps]
-        near = [i for i, step in enumerate(steps) if step[1] == 0] or [0]
-        far = [i for i, step in enumerate(steps) if step[1] == 1] or [0]
-
-        def nearest(i, among):
-            return spots[min(among, key=lambda j: abs(j - i))]
-
-        order = [
-            item
-            for i, step in enumerate(steps)
-            for item in (spots[i], (rank + step[1]) % 2, step[1], nearest(i, near), nearest(i, far))
-        ]
-        keep_out, send_out, keep_back, send_back, *kept = run_expert(
+        keep_back, send_back, *kept = run_expert(
             state["core"],
-            jnp.stack([jnp.asarray(item, jnp.int32) for item in order]),
+            order_of(steps),
             state["first"],
             4 * lines,
             m_all,
@@ -836,22 +920,22 @@
         )
         state["kept"] = kept
         state["first"] += len(steps)
-        back = (keep_back, send_back)
-        return back if raw else over_core(*back), (keep_out, send_out)
+        return (keep_back, send_back) if raw else over_core(keep_back, send_back)
 
     def wait(first):
         state["core"], first = hold(state["core"], first)
         return first
 
-    back, out_far = call([(1, 1, p) for p in places])
+    steps_far, steps_own = ([(d, d, p) for p in places] for d in (1, 0))
+    steps_mixed = [[(1, 0, p) for p in part] + [(0, 1, p) for p in part] for part in parts]
+    back = call(steps_far)
     far_one, far_two = wait([pick_sum(back, 0, lines, column) for column in range(2)])
     far_one, far_two = swap_ctx(far_one), swap_side(far_two)
 
-    def mixed_call(part, raw=False):
-        return call([(1, 0, p) for p in parts[part]] + [(0, 1, p) for p in parts[part]], raw)
-
-    def mixed_sums(back):
-        return [pick_sum(back, start, start + cut, column) for start in (0, cut) for column in range(2)]
+    def mixed_sums(back, at=0):
+        return [
+            pick_sum(back, start, start + cut, column) for start in (at, at + cut) for column in range(2)
+        ]
 
     def rounds(sums, part):
         side_one, side_two, ctx_one, ctx_two = sums
@@ -863,35 +947,44 @@
             swap_ctx(add_low(ctx_two, far_two[span])),
         ]
 
-    (keep, send), out_first = mixed_call(0, raw=True)
+    keep, send = call(steps_mixed[0], raw=True)
     send, (far_one, far_two) = hold(send, (far_one, far_two))
     back = over_core(keep, send)
-    back_own, out_own = call([(0, 0, p) for p in places])
+    back_own = call(steps_own)
     sums = wait(mixed_sums(back))
     back_own = [pick_sum(back_own, 0, lines, column) for column in range(2)]
     got = rounds(sums, 0)
-    (keep, send), out_second = mixed_call(1, raw=True)
+    keep, send = call(steps_mixed[1], raw=True)
     send, got = hold(send, got)
     back = over_core(keep, send)
     entries = joined(parts[0], [item[:cut] for item in back_own], got)
     arrived = {p: line_shift(entries[p], lines - p) for p in parts[0]}
-    got = rounds(mixed_sums(back), 1)
     gate_back, rows, grad_rows, hidden, grad_pair = state["kept"]
+    hidden, sums = hold(hidden, mixed_sums(back))
+    got = rounds(sums, 1)
     grad_gates = lax.all_to_all(
         gate_back.reshape(fsdp * 2, rows_dev), both, split_axis=0, concat_axis=0, tiled=True
     ).T
-    grad_gate_up = mul(rows, grad_pair, lhs_turned)[None]
-    grad_down = mul(hidden, grad_rows, lhs_turned)[None]
+    out_far = run_result(state["core"], order_of(steps_far), 0, hidden, gates_all, expert_down[0], capacity)
+    out_rest = run_result(
+        state["core"],
+        order_of(steps_mixed[0] + steps_own + steps_mixed[1]),
+        lines,
+        hidden,
+        gates_all,
+        expert_down[0],
+        capacity,
+    )
+    got, out_far, out_rest, arrived = lax.optimization_barrier((got, out_far, out_rest, arrived))
+    entries.update(joined(parts[1], [item[cut:] for item in back_own], got))
     out_far = over_core(*out_far)
-    out_far = [pick_sum(out_far, 0, lines, column) for column in range(2)]
-    grad_gate_up, got, out_far, arrived = lax.optimization_barrier((grad_gate_up, got, out_far, arrived))
-    entries.update(joined(parts[1], [item[cut:] for item in back_own], got))
-    out_far = [swap_ctx(out_far[0]), swap_side(out_far[1])]
-    outs, entries = hold((out_first, out_own, out_second), entries)
-    out_first, out_own, out_second = (over_core(*item) for item in outs)
+    out_far = [
+        swap_ctx(pick_sum(out_far, 0, lines, 0)),
+        swap_side(pick_sum(out_far, 0, lines, 1)),
+    ]
+    out_rest = over_core(*out_rest)
     for p in parts[1][:-1]:
         arrived[p] = line_shift(entries[p], lines - p)
-    arrived, grad_down = hold(arrived, grad_down)
     grad_mid = line_total(entries[0], arrived)
 
     grad_wide = jnp.where(chosen, grad_gates, 0.0)
@@ -903,15 +996,13 @@
     grad_mixed_part, grad_moe_gain = rms_back(mixed, moe_all, grad_mid)
     grad_mixed = cotangent.astype(full) + grad_mixed_part
 
-    low_mixed, (out_far, outs) = hold(
-        grad_mixed.astype(low), (out_far, (out_first, out_own, out_second))
-    )
+    low_mixed, (out_far, out_rest) = hold(grad_mixed.astype(low), (out_far, out_rest))
     grad_branch = sequence(low_mixed)
-    out_first, out_own, out_second = outs
     out_sums = [
-        jnp.concatenate([one, two]) for one, two in zip(mixed_sums(out_first), mixed_sums(out_second))
+        jnp.concatenate([one, two])
+        for one, two in zip(mixed_sums(out_rest), mixed_sums(out_rest, 2 * cut + lines))
     ]
-    out_own = [pick_sum(out_own, 0, lines, column) for column in range(2)]
+    out_own = [pick_sum(out_rest, 2 * cut, 2 * cut + lines, column) for column in range(2)]
     (out_sums, out_own), grad_branch = hold((out_sums, out_own), grad_branch)
     side_one, side_two, ctx_one, ctx_two = out_sums
     got = [
@@ -932,6 +1023,9 @@
     grad_normed_part = mul(grad_projected, qkv_all, rhs_turned)
     grad_normed_part, got = hold(grad_normed_part, got)
     entries = joined(places, out_own, got)
+    (rows, grad_pair, hidden, grad_rows), entries = hold((rows, grad_pair, hidden, grad_rows), entries)
+    grad_gate_up = mul(rows, grad_pair, lhs_turned)[None]
+    grad_down = mul(hidden, grad_rows, lhs_turned)[None]
     output = (mixed + line_sum(entries, lines)).astype(low)
     grad_normed = of_block(grad_normed_part, rank) + swap_ctx(
         of_block(grad_normed_part, 1 - rank).astype(low)
@@ -946,18 +1040,8 @@
         jnp.concatenate([out_mine, out_other], axis=0),
         jnp.concatenate([out_other, out_mine], axis=0),
     )
-    qkv_mine = lax.psum_scatter(grad_qkv_part, "fsdp", scatter_dimension=0, tiled=True).astype(full)
-    qkv_other = swap_ctx(qkv_mine.astype(low)).astype(full)
-    q_mine = qkv_mine[:, :width_q].reshape(shard, my_heads, 1, head_dim)
-    q_other = qkv_other[:, :width_q].reshape(shard, my_heads, 1, head_dim)
-    grad_q_all = jnp.where(
-        rank == 0,
-        jnp.concatenate([q_mine, q_other], axis=2),
-        jnp.concatenate([q_other, q_mine], axis=2),
-    ).reshape(shard, 2 * width_q)
-    grad_qkv = jnp.concatenate(
-        [grad_q_all, qkv_mine[:, width_q:] + qkv_other[:, width_q:]], axis=1
-    )
+    qkv_mine = lax.psum_scatter(grad_qkv_part, "fsdp", scatter_dimension=0, tiled=True)
+    grad_qkv = all_heads(rank_at, qkv_mine, swap_ctx(qkv_mine), head_dim, my_heads)
     early = sum_owned(jnp.concatenate([grad_router.T, grad_moe_gain[None]], axis=0), fsdp, spot)
     late = sum_all(
         jnp.concatenate(

time: 1200 us -> 1190 us (level)
  waiting for transfers between devices: 630 us -> 558 us
  blocking collectives: 36 us -> 82.2 us
  Pallas kernels: 199 us -> 225 us
  local copies, waits for them, and re-layouts: 42.2 us -> 25.7 us
    ppermute x3, waiting for transfers between devices: 95.4 us -> 38.7 us  [sum_all(): lax.ppermute(values, 'fsdp', [(i, i ^ step) for i in range(fsdp)])]
    all_to_all x0 -> x1, blocking collectives: none -> 46.8 us  [body_gathered(): lax.all_to_all(gate_back.reshape(fsdp * 2, rows_dev), both, split_axis=0,...]
    pallas_call x0 -> x4, Pallas kernels: none -> 46.3 us  [the longest x2 40.2 us: run_result(): pl.pallas_call(result_kernel, grid_spec=pltpu.PrefetchScalarGridSpec(num_...]
    ppermute x6, waiting for transfers between devices: 59.2 us -> 14 us  [line_shift(): lax.ppermute(values, 'fsdp', [(i, (i + 4 * step) % fsdp) for i in range(f...]
    reduce_scatter x1, waiting for transfers between devices: 22.2 us -> 46.4 us  [body_gathered(): lax.psum_scatter(grad_qkv_part, 'fsdp', scatter_dimension=0, tiled=True)]
    pallas_call x4, Pallas kernels: 155 us -> 135 us  [run_expert(): pl.pallas_call(expert_kernel, grid_spec=grid_spec, out_shape=[shape((step...]
    ppermute x8 -> x6, waiting for transfers between devices: 12.5 us -> 24 us  [swap_core(): return lax.ppermute(values, 'fsdp', core_pairs(lax.axis_size('fsdp')))]
    convert_element_type x18 -> x19, other arithmetic: 63.8 us -> 63.8 us  [add_low(): return (one.astype(full) + two.astype(full)).astype(low)]
  transfers between devices with their start and end apart: 55 -> 52, of which waited for: 29 -> 27; matrix products, arithmetic and copies ran while one was open for 18% -> 19% of each run, Pallas kernels for 13% -> 16%
where the time goes in v6:
time: 1190 us; the launch traced here: 1180 us
  waiting for transfers between devices  558 us (47%)
  Pallas kernels  225 us (19%)
  matrix products  113 us (9%)
  other arithmetic  105 us (9%)
  blocking collectives  82.2 us (7%)
  starting transfers between devices  52.7 us (4%)
  local copies, waits for them, and re-layouts  25.7 us (2%)
  between operations  15.5 us (1%)
    ppermute x19, waiting for transfers between devices, swap_ctx(): return lax.ppermute(values, 'ctx', [(0, 1), (1, 0)])  265 us
    pallas_call x4, Pallas kernels, run_expert(): pl.pallas_call(expert_kernel, grid_spec=grid_spec, out_shape=[shape((step...  135 us
    dot_general x11, matrix products, mul(): return lax.dot_general(left, right, dims, preferred_element_type=full)  113 us
    all_gather x1, waiting for transfers between devices, body_gathered(): weights_all = lax.all_gather(weights_local, 'fsdp', axis=0, tiled=True)  65.6 us
    convert_element_type x19, other arithmetic, add_low(): return (one.astype(full) + two.astype(full)).astype(low)  63.8 us
    ppermute x8, waiting for transfers between devices, swap_side(): return lax.ppermute(values, 'fsdp', side_pairs(lax.axis_size('fsdp')))  54.5 us
    all_to_all x1, blocking collectives, body_gathered(): lax.all_to_all(gate_back.reshape(fsdp * 2, rows_dev), both, split_axis=0,...  46.8 us
    reduce_scatter x1, waiting for transfers between devices, body_gathered(): lax.psum_scatter(grad_qkv_part, 'fsdp', scatter_dimension=0, tiled=True)  46.4 us
  transfers between devices with their start and end apart: 52, of which 27 were waited for; matrix products, arithmetic and copies ran while one was open for 19% of the time, Pallas kernels for 16%

profile of v6, /device:TPU:0, one launch (start us, length us, event | category | flops | bytes accessed | tf_op | source)
XLA Modules:
  0.0 1176.1 jit_solution(15715350402939278458)
XLA Ops:
  13.4 13.3 %collective-permute-done.3 = bf16[256,1152]{1,0:T(8,128)(2,1)S(1)} collective-permute-done((bf16[256,1152]{1,0:T(8,128)(2,1)S(1)}, bf16[256,1152]{1,0:T(8,128)(2,1)S(1)}, u32[]{:S(2)}, u32[]{:S(2)}) %collective-permute-start.3) | collective-permute-done | bytes 589856 | tf_op jit(solution)/shard_map/ppermute | solution.py:341
  31.2 22.9 %all_gather.12 = bf16[2048,34]{0,1:T(8,128)(2,1)S(1)} all-gather(bf16[128,34]{0,1:T(8,128)(2,1)S(1)} %pad_maximum_fusion.21), channel_id=1, replica_groups=mesh['fsdp'=16,'ctx'=2] {'fsdp'}, dimensions={0}, use_global_device_ids=true | all-gather | bytes 147968 | tf_op jit(solution)/shard_map/all_gather | solution.py:839
  57.6 65.6 %all-gather.4.cloned.1.call-done = bf16[2048,5120]{1,0:T(8,128)(2,1)} async-done(((bf16[128,5120]{1,0:T(8,128)(2,1)}), bf16[2048,5120]{1,0:T(8,128)(2,1)}) %all-gather.4.cloned.1.call-update) | async-done | bytes 20971536 | tf_op jit(solution)/shard_map/all_gather | solution.py:840
  123.2 11.5 fusion.2.q_ref.k_ref.v_ref
  134.7 18.3 %attend.1 = (bf16[512,2048]{1,0:T(8,128)(2,1)S(1)}, bf16[512,2048]{1,0:T(8,128)(2,1)S(1)}, bf16[512,512]{1,0:T(8,128)(2,1)S(1)}, bf16[512,512]{1,0:T(8,128)(2,1)S(1)}) custom-call(f32[512,3072]{1,0:T(8,128)} %fusion.2.q_ref.k_ref.v_ref, f32[512,3072]{1,0:T(8,128)} %fusion.2.q_ref.k_ref.v_ref, f32[512,3072]{1,0:T(8,128)} %fusion.2.q_ref.k_ref.v_ref, ...), custom_call_target="tpu_custom_call" | custom-call | flops 2147483648 | bytes 9437184 | tf_op jit(solution)/shard_map/attend/pallas_call | solution.py:525
  153.0 8.5 fusion.6
  163.6 23.9 %collective-permute-done.1 = bf16[256,2048]{1,0:T(8,128)(2,1)S(1)} collective-permute-done((bf16[256,2048]{1,0:T(8,128)(2,1)S(1)}, bf16[256,2048]{1,0:T(8,128)(2,1)S(1)}, u32[]{:S(2)}, u32[]{:S(2)}) %collective-permute-start.1) | collective-permute-done | bytes 1048608 | tf_op jit(solution)/shard_map/ppermute | solution.py:341
  191.8 23.2 %collective-permute-done.2 = bf16[256,2048]{1,0:T(8,128)(2,1)S(1)} collective-permute-done((bf16[256,2048]{1,0:T(8,128)(2,1)S(1)}, bf16[256,2048]{1,0:T(8,128)(2,1)S(1)}, u32[]{:S(2)}, u32[]{:S(2)}) %collective-permute-start.2) | collective-permute-done | bytes 1048608 | tf_op jit(solution)/shard_map/ppermute | solution.py:341
  218.5 12.5 %all_to_all.24 = f32[32,1,256]{2,1,0:T(1,128)S(1)} all-to-all(f32[32,1,256]{2,1,0:T(1,128)S(1)} %copy.60), channel_id=1, replica_groups=mesh['fsdp'=16,'ctx'=2] {'fsdp','ctx'}, dimensions={0} | all-to-all | bytes 65536 | tf_op jit(solution)/shard_map/all_to_all | solution.py:877
  231.0 28.7 %all-gather.8.cloned.1.call-done = bf16[4096,3200]{1,0:T(8,128)(2,1)} async-done(((bf16[256,3200]{1,0:T(8,128)(2,1)}), bf16[4096,3200]{1,0:T(8,128)(2,1)}) %all-gather.8.cloned.1.call-update) | async-done | bytes 26214416 | tf_op jit(solution)/shard_map/all_gather | solution.py:847
  259.7 6.9 slice.403
  269.4 157.7 %collective-permute-done.4.far_ref = bf16[8,2,256,896]{3,2,1,0:T(8,128)(2,1)} collective-permute-done((bf16[8,2,256,896]{3,2,1,0:T(8,128)(2,1)}, bf16[8,2,256,896]{3,2,1,0:T(8,128)(2,1)}, u32[]{:S(2)}, u32[]{:S(2)}) %collective-permute-start.4) | collective-permute-done | bytes 7340064 | tf_op jit(solution)/shard_map/ppermute | solution.py:341
  429.9 33.0 %experts.4 = (bf16[4,256,2048]{2,1,0:T(8,128)(2,1)}, bf16[4,256,2048]{2,1,0:T(8,128)(2,1)}, f32[8,2,2,1,256]{4,3,2,1,0:T(1,128)}, bf16[4096,2048]{1,0:T(8,128)(2...) custom-call(s32[1]{0:T(128)} %bitcast.6.core_ref, s32[16]{0:T(128)} %stack.35.order, ...), custom_call_target="tpu_custom_call" | custom-call | flops 19327352832 | bytes 38273024 | tf_op jit(solution)/shard_map/experts/pallas_call | solution.py:674
  463.3 7.1 collective-permute-done.5
  470.4 4.2 add_convert_fusion.8
  477.8 34.1 %experts.5 = (bf16[4,256,2048]{2,1,0:T(8,128)(2,1)}, bf16[4,256,2048]{2,1,0:T(8,128)(2,1)}, f32[8,2,2,1,256]{4,3,2,1,0:T(1,128)}, bf16[4096,2048]{1,0:T(8,128)(2...) custom-call(s32[1]{0:T(128)} %bitcast.6.core_ref, ...), custom_call_target="tpu_custom_call", output_to_operand_aliasing={{2}: (8, {}), {3}: (9, {}), {4}: (10, {}), {5}: (11, {}), {... | custom-call | flops 19327352832 | bytes 38273024 | tf_op jit(solution)/shard_map/experts/pallas_call | solution.py:674
  512.0 10.7 collective-permute-done.6
  525.1 34.1 %experts.6 = (bf16[4,256,2048]{2,1,0:T(8,128)(2,1)}, bf16[4,256,2048]{2,1,0:T(8,128)(2,1)}, f32[8,2,2,1,256]{4,3,2,1,0:T(1,128)}, bf16[4096,2048]{1,0:T(8,128)(2...) custom-call(s32[1]{0:T(128)} %bitcast.6.core_ref, ...), custom_call_target="tpu_custom_call", output_to_operand_aliasing={{2}: (8, {}), {3}: (9, {}), {4}: (10, {}), {5}: (11, {}), {... | custom-call | flops 19327352832 | bytes 38273024 | tf_op jit(solution)/shard_map/experts/pallas_call | solution.py:674
  559.8 4.4 add_convert_fusion.27
  571.5 33.8 %experts.7 = (bf16[4,256,2048]{2,1,0:T(8,128)(2,1)}, bf16[4,256,2048]{2,1,0:T(8,128)(2,1)}, f32[8,2,2,1,256]{4,3,2,1,0:T(1,128)}, bf16[4096,2048]{1,0:T(8,128)(2...) custom-call(s32[1]{0:T(128)} %bitcast.6.core_ref, ...), custom_call_target="tpu_custom_call", output_to_operand_aliasing={{2}: (8, {}), {3}: (9, {}), {4}: (10, {}), {5}: (11, {}), {... | custom-call | flops 19327352832 | bytes 38273024 | tf_op jit(solution)/shard_map/experts/pallas_call | solution.py:674
  606.3 7.2 collective-permute-done.9
  616.1 4.4 add_convert_fusion.7
  642.8 11.9 %results.2 = (bf16[4,256,2048]{2,1,0:T(8,128)(2,1)}, bf16[4,256,2048]{2,1,0:T(8,128)(2,1)}) custom-call(s32[1]{0:T(128)} %bitcast.6.core_ref, s32[16]{0:T(128)} %stack.35.order, bf16[4096,768]{1,0:T(8,128)(2,1)} %get-tuple-element.217.z_ref, f32[8,2,2,1,256]{4,3,2,1,0:T(1,128)} %reshape.272.w_ref, bf16[768,2048]{1,0:T(8,128)(2,1)} %bitcast.157), custom_call_target="tpu_custom_call" | custom-call | flops 4294967296 | bytes 13107200 | tf_op jit(solution)/shard_map/results/pallas_call | solution.py:705
  655.3 28.3 %results.3 = (bf16[12,256,2048]{2,1,0:T(8,128)(2,1)}, bf16[12,256,2048]{2,1,0:T(8,128)(2,1)}) custom-call(s32[1]{0:T(128)} %bitcast.6.core_ref, s32[48]{0:T(128)} %stack.44.order, bf16[4096,768]{1,0:T(8,128)(2,1)} %get-tuple-element.217.z_ref, f32[8,2,2,1,256]{4,3,2,1,0:T(1,128)} %reshape.272.w_ref, bf16[768,2048]{1,0:T(8,128)(2,1)} %bitcast.158), custom_call_target="tpu_custom_call" | custom-call | flops 12884901888 | bytes 33030144 | tf_op jit(solution)/shard_map/results/pallas_call | solution.py:705
  683.6 13.9 %collective-permute-done.20 = bf16[256,2048]{1,0:T(8,128)(2,1)} collective-permute-done((bf16[256,2048]{1,0:T(8,128)(2,1)}, bf16[256,2048]{1,0:T(8,128)(2,1)}, u32[]{:S(2)}, u32[]{:S(2)}) %collective-permute-start.20) | collective-permute-done | bytes 1048608 | tf_op jit(solution)/shard_map/ppermute | solution.py:358
  706.1 16.9 %collective-permute-done.22 = bf16[4,256,2048]{2,1,0:T(8,128)(2,1)S(1)} collective-permute-done((bf16[4,256,2048]{2,1,0:T(8,128)(2,1)}, bf16[4,256,2048]{2,1,0:T(8,128)(2,1)S(1)}, u32[]{:S(2)}, u32[]{:S(2)}) %collective-permute-start.22) | collective-permute-done | bytes 4194336 | tf_op jit(solution)/shard_map/ppermute | solution.py:333
  729.1 46.8 %all_to_all.25 = f32[32,1,256]{2,1,0:T(1,128)S(1)} all-to-all(f32[32,1,256]{2,1,0:T(1,128)S(1)} %bitcast.164), channel_id=1, replica_groups=mesh['fsdp'=16,'ctx'=2] {'fsdp','ctx'}, dimensions={0} | all-to-all | bytes 65536 | tf_op jit(solution)/shard_map/all_to_all | solution.py:965
  785.3 5.2 add_convert_fusion.12
  803.1 5.8 collective-permute-done.26
  812.7 6.8 convolution_convert_fusion.1
  822.2 4.5 add_convert_fusion
  826.7 4.2 add_convert_fusion.1
  830.9 10.0 fusion.11.go_ref
  841.0 25.3 %attend_grad.1 = (bf16[512,2048]{1,0:T(8,128)(2,1)S(1)}, bf16[512,512]{1,0:T(8,128)(2,1)S(1)}, bf16[512,512]{1,0:T(8,128)(2,1)S(1)}, f32[4,1,128]{2,1,0:T(1,128)S(1)}, f32[4,1,128]{2,1,0:T(1,128)S(1)}) custom-call(f32[512,3072]{1,0:T(8,128)} %fusion.2.q_ref.k_ref.v_ref, f32[512,3072]{1,0:T(8,128)} %fusion.2.q_ref.k_ref.v_ref, bf16[512,2048]{1,0:T(8,128)(2,1)} %copy-done, ...), custom_call_target="tpu_custom_call" | custom-call | flops 5368709120 | bytes 15728640 | tf_op jit(solution)/shard_map/attend_grad/pallas_call | solution.py:549
  866.7 12.7 %collective-permute-done.28 = bf16[4,256,1024]{2,1,0:T(8,128)(2,1)} collective-permute-done((bf16[4,256,1024]{2,1,0:T(8,128)(2,1)}, bf16[4,256,1024]{2,1,0:T(8,128)(2,1)}, u32[]{:S(2)}, u32[]{:S(2)}) %collective-permute-start.28) | collective-permute-done | bytes 2097184 | tf_op jit(solution)/shard_map/ppermute | solution.py:337
  879.5 9.9 convolution_convert_fusion
  891.1 8.7 collective-permute-done.37
  899.9 4.3 collective-permute-done.38
  915.8 10.9 fusion
  926.7 38.7 %collective-permute-done.29 = bf16[4,256,1024]{2,1,0:T(8,128)(2,1)} collective-permute-done((bf16[4,256,1024]{2,1,0:T(8,128)(2,1)}, bf16[4,256,1024]{2,1,0:T(8,128)(2,1)}, u32[]{:S(2)}, u32[]{:S(2)}) %collective-permute-start.29) | collective-permute-done | bytes 2097184 | tf_op jit(solution)/shard_map/ppermute | solution.py:337
  978.2 12.3 %collective-permute-done.34 = bf16[256,2048]{1,0:T(8,128)(2,1)S(1)} collective-permute-done((bf16[256,2048]{1,0:T(8,128)(2,1)S(1)}, bf16[256,2048]{1,0:T(8,128)(2,1)S(1)}, u32[]{:S(2)}, u32[]{:S(2)}) %collective-permute-start.34) | collective-permute-done | bytes 1048608 | tf_op jit(solution)/shard_map/ppermute | solution.py:341
  998.2 33.2 %convolution_bitcast_fusion = f32[1,2048,1536]{2,1,0:T(8,128)} fusion(bf16[4096,2048]{1,0:T(8,128)(2,1)S(1)} %bitcast.146, bf16[4096,1536]{1,0:T(8,128)(2,1)} %get-tuple-element.216), kind=kOutput, calls=%fused_computation.5 | convolution fusion | flops 25769803776 | bytes 41943040 | tf_op jit(solution)/shard_map/dot_general | solution.py:321
  1031.9 19.3 %convolution_bitcast_fusion.1 = f32[1,768,2048]{2,1,0:T(8,128)} fusion(bf16[4096,768]{1,0:T(8,128)(2,1)S(1)} %bitcast.152, bf16[4096,2048]{1,0:T(8,128)(2,1)} %get-tuple-element.218), kind=kOutput, calls=%fused_computation.26 | convolution fusion | flops 12884901888 | bytes 29360128 | tf_op jit(solution)/shard_map/dot_general | solution.py:321
  1054.2 38.7 %collective-permute-done.45 = f32[18,128]{1,0:T(8,128)S(1)} collective-permute-done((f32[18,128]{1,0:T(8,128)S(1)}, f32[18,128]{1,0:T(8,128)S(1)}, u32[]{:S(2)}, u32[]{:S(2)}) %collective-permute-start.45) | collective-permute-done | bytes 9248 | tf_op jit(solution)/shard_map/ppermute | solution.py:398
  1092.9 4.6 collective-permute-start.46
  1098.9 46.4 %reduce-scatter.3.cloned.1.call-done.mine_ref = bf16[128,3072]{1,0:T(8,128)(2,1)} async-done(((bf16[2048,3072]{1,0:T(8,128)(2,1)}), bf16[128,3072]{1,0:T(8,128)(2,1)}) %reduce-scatter.3.cloned.1.call-update) | async-done | bytes 786448 | tf_op jit(solution)/shard_map/reduce_scatter | solution.py:1043
  1146.8 6.3 fusion.20
  1157.1 8.1 collective-permute-done.35.other_ref
  (351 shorter events, 160.8 us)
Async XLA Ops:
  7.2 116.1 %all-gather.4.cloned.1.call-start = ((), (), s32[]{:S(2)}) async-start(), calls=%async_computation.4 | async-start | bytes 22282240 | tf_op jit(solution)/shard_map/all_gather | solution.py:840
  10.2 249.5 %all-gather.8.cloned.1.call-start = ((), (), s32[]{:S(2)}) async-start(), calls=%async_computation.6 | async-start | bytes 27852800 | tf_op jit(solution)/shard_map/all_gather | solution.py:847
  10.4 16.3 %collective-permute-start.3 = (bf16[256,1152]{1,0:T(8,128)(2,1)S(1)}, bf16[256,1152]{1,0:T(8,128)(2,1)S(1)}, u32[]{:S(2)}, u32[]{:S(2)}) collective-permute-start(bf16[256,1152]{1,0:T(8,128)(2,1)S(1)} %slice.401), channel_id=1, source_target_pairs={{0,1},{1,0},{2,3},{3,2},{4,5},{5,4},{6,7},{7,6},{8,9},{9,8},{10,11... | collective-permute-start | bytes 1769480 | tf_op jit(solution)/shard_map/ppermute | solution.py:341
  28.1 401.9 %all-gather.6.cloned.1.call-start = ((), (), s32[]{:S(2)}) async-start(), calls=%async_computation.5 | async-start | bytes 35651584 | tf_op jit(solution)/shard_map/all_gather | solution.py:868
  28.1 26.4 %collective-permute-start = (bf16[256,2048]{1,0:T(8,128)(2,1)S(1)}, bf16[256,2048]{1,0:T(8,128)(2,1)}, u32[]{:S(2)}, u32[]{:S(2)}) collective-permute-start(bf16[256,2048]{1,0:T(8,128)(2,1)S(1)} %copy-done.6), channel_id=1, source_target_pairs={{0,1},{1,0},{2,3},{3,2},{4,5},{5,4},{6,7},{7,6},{8,9},{9,8},{10,11... | collective-permute-start | bytes 3145736 | tf_op jit(solution)/shard_map/ppermute | solution.py:341
  162.1 25.4 %collective-permute-start.1 = (bf16[256,2048]{1,0:T(8,128)(2,1)S(1)}, bf16[256,2048]{1,0:T(8,128)(2,1)S(1)}, u32[]{:S(2)}, u32[]{:S(2)}) collective-permute-start(bf16[256,2048]{1,0:T(8,128)(2,1)S(1)} %select_convert_fusion.1), channel_id=1, source_target_pairs={{0,1},{1,0},{2,3},{3,2},{4,5},{5,4},{6,7},{7,6},{8,9},{9,8},{10,11... | collective-permute-start | bytes 3145736 | tf_op jit(solution)/shard_map/ppermute | solution.py:341
  190.3 24.7 %collective-permute-start.2 = (bf16[256,2048]{1,0:T(8,128)(2,1)S(1)}, bf16[256,2048]{1,0:T(8,128)(2,1)S(1)}, u32[]{:S(2)}, u32[]{:S(2)}) collective-permute-start(bf16[256,2048]{1,0:T(8,128)(2,1)S(1)} %multiply_convert_fusion), channel_id=1, source_target_pairs={{0,1},{1,0},{2,3},{3,2},{4,5},{5,4},{6,7},{7,6},{8,9},{9,8},{10,11... | collective-permute-start | bytes 3145736 | tf_op jit(solution)/shard_map/ppermute | solution.py:341
  216.5 881.0 %reduce-scatter.5.cloned.1.call-start = ((), (), s32[]{:S(2)}) async-start(), calls=%async_computation.8 | async-start | bytes 8912896 | tf_op jit(solution)/shard_map/reduce_scatter | solution.py:1036
  266.6 160.5 %collective-permute-start.4 = (bf16[8,2,256,896]{3,2,1,0:T(8,128)(2,1)}, bf16[8,2,256,896]{3,2,1,0:T(8,128)(2,1)}, u32[]{:S(2)}, u32[]{:S(2)}) collective-permute-start(bf16[8,2,256,896]{3,2,1,0:T(8,128)(2,1)} %slice.403), channel_id=1, source_target_pairs={{0,1},{1,0},{2,3},{3,2},{4,5},{5,4},{6,7},{7,6},{8,9},{9,8},{10,11... | collective-permute-start | bytes 22020104 | tf_op jit(solution)/shard_map/ppermute | solution.py:341
  463.0 7.4 collective-permute-start.5
  474.6 48.1 %collective-permute-start.6 = (bf16[4,256,1024]{2,1,0:T(8,128)(2,1)}, bf16[4,256,1024]{2,1,0:T(8,128)(2,1)}, u32[]{:S(2)}, u32[]{:S(2)}) collective-permute-start(bf16[4,256,1024]{2,1,0:T(8,128)(2,1)} %get-tuple-element.128), channel_id=1, source_target_pairs={{0,1},{1,0},{2,3},{3,2},{4,5},{5,4},{6,7},{7,6},{8,9},{9,8},{10,11... | collective-permute-start | bytes 6291464 | tf_op jit(solution)/shard_map/ppermute | solution.py:341
  476.1 47.8 %collective-permute-start.7 = (bf16[4,256,1024]{2,1,0:T(8,128)(2,1)}, bf16[4,256,1024]{2,1,0:T(8,128)(2,1)}, u32[]{:S(2)}, u32[]{:S(2)}) collective-permute-start(bf16[4,256,1024]{2,1,0:T(8,128)(2,1)} %get-tuple-element.129), channel_id=1, source_target_pairs={{0,4},{2,6},{4,0},{6,2},{8,12},{10,14},{12,8},{14,10},{16,20},{18,... | collective-permute-start | bytes 6291464 | tf_op jit(solution)/shard_map/ppermute | solution.py:337
  523.9 35.9 %collective-permute-start.8 = (bf16[4,256,2048]{2,1,0:T(8,128)(2,1)}, bf16[4,256,2048]{2,1,0:T(8,128)(2,1)}, u32[]{:S(2)}, u32[]{:S(2)}) collective-permute-start(bf16[4,256,2048]{2,1,0:T(8,128)(2,1)} %get-tuple-element.130), channel_id=1, source_target_pairs={{0,2},{2,0},{4,6},{6,4},{8,10},{10,8},{12,14},{14,12},{16,18},{18,... | collective-permute-start | bytes 12582920 | tf_op jit(solution)/shard_map/ppermute | solution.py:333
  559.2 56.8 %collective-permute-start.14 = (bf16[4,256,2048]{2,1,0:T(8,128)(2,1)}, bf16[4,256,2048]{2,1,0:T(8,128)(2,1)}, u32[]{:S(2)}, u32[]{:S(2)}) collective-permute-start(bf16[4,256,2048]{2,1,0:T(8,128)(2,1)} %get-tuple-element.157), channel_id=1, source_target_pairs={{0,2},{2,0},{4,6},{6,4},{8,10},{10,8},{12,14},{14,12},{16,18},{18,... | collective-permute-start | bytes 12582920 | tf_op jit(solution)/shard_map/ppermute | solution.py:333
  565.8 39.5 %collective-permute-start.12 = (bf16[2,256,1024]{2,1,0:T(8,128)(2,1)S(1)}, bf16[2,256,1024]{2,1,0:T(8,128)(2,1)S(1)}, u32[]{:S(2)}, u32[]{:S(2)}) collective-permute-start(bf16[2,256,1024]{2,1,0:T(8,128)(2,1)S(1)} %add_convert_fusion.25), channel_id=1, source_target_pairs={{0,1},{1,0},{2,3},{3,2},{4,5},{5,4},{6,7},{7,6},{8,9},{9,8},{10,11... | collective-permute-start | bytes 3145736 | tf_op jit(solution)/shard_map/ppermute | solution.py:341
  567.9 37.4 %collective-permute-start.11 = (bf16[2,256,1024]{2,1,0:T(8,128)(2,1)S(1)}, bf16[2,256,1024]{2,1,0:T(8,128)(2,1)S(1)}, u32[]{:S(2)}, u32[]{:S(2)}) collective-permute-start(bf16[2,256,1024]{2,1,0:T(8,128)(2,1)S(1)} %add_convert_fusion.26), channel_id=1, source_target_pairs={{0,4},{2,6},{4,0},{6,2},{8,12},{10,14},{12,8},{14,10},{16,20},{18,... | collective-permute-start | bytes 3145736 | tf_op jit(solution)/shard_map/ppermute | solution.py:337
  569.1 44.4 %collective-permute-start.9 = (bf16[2,256,1024]{2,1,0:T(8,128)(2,1)}, bf16[2,256,1024]{2,1,0:T(8,128)(2,1)}, u32[]{:S(2)}, u32[]{:S(2)}) collective-permute-start(bf16[2,256,1024]{2,1,0:T(8,128)(2,1)} %get-tuple-element.147), channel_id=1, source_target_pairs={{0,1},{1,0},{2,3},{3,2},{4,5},{5,4},{6,7},{7,6},{8,9},{9,8},{10,11... | collective-permute-start | bytes 3145736 | tf_op jit(solution)/shard_map/ppermute | solution.py:341
  570.6 44.8 %collective-permute-start.10 = (bf16[2,256,1024]{2,1,0:T(8,128)(2,1)}, bf16[2,256,1024]{2,1,0:T(8,128)(2,1)}, u32[]{:S(2)}, u32[]{:S(2)}) collective-permute-start(bf16[2,256,1024]{2,1,0:T(8,128)(2,1)} %get-tuple-element.148), channel_id=1, source_target_pairs={{0,4},{2,6},{4,0},{6,2},{8,12},{10,14},{12,8},{14,10},{16,20},{18,... | collective-permute-start | bytes 3145736 | tf_op jit(solution)/shard_map/ppermute | solution.py:337
  615.4 14.9 %collective-permute-start.13 = (bf16[4,256,2048]{2,1,0:T(8,128)(2,1)}, bf16[4,256,2048]{2,1,0:T(8,128)(2,1)}, u32[]{:S(2)}, u32[]{:S(2)}) collective-permute-start(bf16[4,256,2048]{2,1,0:T(8,128)(2,1)} %get-tuple-element.153), channel_id=1, source_target_pairs={{0,2},{2,0},{4,6},{6,4},{8,10},{10,8},{12,14},{14,12},{16,18},{18,... | collective-permute-start | bytes 12582920 | tf_op jit(solution)/shard_map/ppermute | solution.py:333
  625.8 28.9 %collective-permute-start.19 = (bf16[256,2048]{1,0:T(8,128)(2,1)}, bf16[256,2048]{1,0:T(8,128)(2,1)S(1)}, u32[]{:S(2)}, u32[]{:S(2)}) collective-permute-start(bf16[256,2048]{1,0:T(8,128)(2,1)} %pad_maximum_fusion.11), channel_id=1, source_target_pairs={{0,24},{2,26},{4,28},{6,30},{8,0},{10,2},{12,4},{14,6},{16,8},{18,... | collective-permute-start | bytes 3145736 | tf_op jit(solution)/shard_map/ppermute | solution.py:358
  630.3 67.3 %collective-permute-start.20 = (bf16[256,2048]{1,0:T(8,128)(2,1)}, bf16[256,2048]{1,0:T(8,128)(2,1)}, u32[]{:S(2)}, u32[]{:S(2)}) collective-permute-start(bf16[256,2048]{1,0:T(8,128)(2,1)} %pad_maximum_fusion.12), channel_id=1, source_target_pairs={{0,16},{2,18},{4,20},{6,22},{8,24},{10,26},{12,28},{14,30},{16,0},... | collective-permute-start | bytes 3145736 | tf_op jit(solution)/shard_map/ppermute | solution.py:358
  634.2 63.3 %collective-permute-start.15 = (bf16[2,256,1024]{2,1,0:T(8,128)(2,1)}, bf16[2,256,1024]{2,1,0:T(8,128)(2,1)}, u32[]{:S(2)}, u32[]{:S(2)}) collective-permute-start(bf16[2,256,1024]{2,1,0:T(8,128)(2,1)} %get-tuple-element.158), channel_id=1, source_target_pairs={{0,1},{1,0},{2,3},{3,2},{4,5},{5,4},{6,7},{7,6},{8,9},{9,8},{10,11... | collective-permute-start | bytes 3145736 | tf_op jit(solution)/shard_map/ppermute | solution.py:341
  635.7 61.9 %collective-permute-start.16 = (bf16[2,256,1024]{2,1,0:T(8,128)(2,1)}, bf16[2,256,1024]{2,1,0:T(8,128)(2,1)}, u32[]{:S(2)}, u32[]{:S(2)}) collective-permute-start(bf16[2,256,1024]{2,1,0:T(8,128)(2,1)} %get-tuple-element.159), channel_id=1, source_target_pairs={{0,4},{2,6},{4,0},{6,2},{8,12},{10,14},{12,8},{14,10},{16,20},{18,... | collective-permute-start | bytes 3145736 | tf_op jit(solution)/shard_map/ppermute | solution.py:337
  639.0 58.6 %collective-permute-start.17 = (bf16[2,256,1024]{2,1,0:T(8,128)(2,1)}, bf16[2,256,1024]{2,1,0:T(8,128)(2,1)}, u32[]{:S(2)}, u32[]{:S(2)}) collective-permute-start(bf16[2,256,1024]{2,1,0:T(8,128)(2,1)} %add_convert_fusion.20), channel_id=1, source_target_pairs={{0,4},{2,6},{4,0},{6,2},{8,12},{10,14},{12,8},{14,10},{16,20},{18,... | collective-permute-start | bytes 3145736 | tf_op jit(solution)/shard_map/ppermute | solution.py:337
  654.7 42.9 %collective-permute-start.18 = (bf16[2,256,1024]{2,1,0:T(8,128)(2,1)}, bf16[2,256,1024]{2,1,0:T(8,128)(2,1)}, u32[]{:S(2)}, u32[]{:S(2)}) collective-permute-start(bf16[2,256,1024]{2,1,0:T(8,128)(2,1)} %add_convert_fusion.19), channel_id=1, source_target_pairs={{0,1},{1,0},{2,3},{3,2},{4,5},{5,4},{6,7},{7,6},{8,9},{9,8},{10,11... | collective-permute-start | bytes 3145736 | tf_op jit(solution)/shard_map/ppermute | solution.py:341
  697.6 86.2 %collective-permute-start.25 = (bf16[12,256,2048]{2,1,0:T(8,128)(2,1)}, bf16[12,256,2048]{2,1,0:T(8,128)(2,1)S(1)}, u32[]{:S(2)}, u32[]{:S(2)}) collective-permute-start(bf16[12,256,2048]{2,1,0:T(8,128)(2,1)} %get-tuple-element.180), channel_id=1, source_target_pairs={{0,2},{2,0},{4,6},{6,4},{8,10},{10,8},{12,14},{14,12},{16,18},{18,... | collective-permute-start | bytes 37748744 | tf_op jit(solution)/shard_map/ppermute | solution.py:333
  697.7 25.4 %collective-permute-start.22 = (bf16[4,256,2048]{2,1,0:T(8,128)(2,1)}, bf16[4,256,2048]{2,1,0:T(8,128)(2,1)S(1)}, u32[]{:S(2)}, u32[]{:S(2)}) collective-permute-start(bf16[4,256,2048]{2,1,0:T(8,128)(2,1)} %get-tuple-element.178), channel_id=1, source_target_pairs={{0,2},{2,0},{4,6},{6,4},{8,10},{10,8},{12,14},{14,12},{16,18},{18,... | collective-permute-start | bytes 12582920 | tf_op jit(solution)/shard_map/ppermute | solution.py:333
  704.7 73.0 %collective-permute-start.21 = (bf16[256,2048]{1,0:T(8,128)(2,1)S(1)}, bf16[256,2048]{1,0:T(8,128)(2,1)S(1)}, u32[]{:S(2)}, u32[]{:S(2)}) collective-permute-start(bf16[256,2048]{1,0:T(8,128)(2,1)S(1)} %pad_maximum_fusion.13), channel_id=1, source_target_pairs={{0,8},{2,10},{4,12},{6,14},{8,16},{10,18},{12,20},{14,22},{16,24},... | collective-permute-start | bytes 3145736 | tf_op jit(solution)/shard_map/ppermute | solution.py:358
  726.4 57.4 %collective-permute-start.24 = (bf16[4,256,1024]{2,1,0:T(8,128)(2,1)}, bf16[4,256,1024]{2,1,0:T(8,128)(2,1)}, u32[]{:S(2)}, u32[]{:S(2)}) collective-permute-start(bf16[4,256,1024]{2,1,0:T(8,128)(2,1)} %get-tuple-element.237), channel_id=1, source_target_pairs={{0,4},{2,6},{4,0},{6,2},{8,12},{10,14},{12,8},{14,10},{16,20},{18,... | collective-permute-start | bytes 6291464 | tf_op jit(solution)/shard_map/ppermute | solution.py:337
  727.6 56.2 %collective-permute-start.23 = (bf16[4,256,1024]{2,1,0:T(8,128)(2,1)}, bf16[4,256,1024]{2,1,0:T(8,128)(2,1)}, u32[]{:S(2)}, u32[]{:S(2)}) collective-permute-start(bf16[4,256,1024]{2,1,0:T(8,128)(2,1)} %get-tuple-element.238), channel_id=1, source_target_pairs={{0,1},{1,0},{2,3},{3,2},{4,5},{5,4},{6,7},{7,6},{8,9},{9,8},{10,11... | collective-permute-start | bytes 6291464 | tf_op jit(solution)/shard_map/ppermute | solution.py:341
  783.8 25.1 %collective-permute-start.26 = (bf16[256,2048]{1,0:T(8,128)(2,1)S(1)}, bf16[256,2048]{1,0:T(8,128)(2,1)}, u32[]{:S(2)}, u32[]{:S(2)}) collective-permute-start(bf16[256,2048]{1,0:T(8,128)(2,1)S(1)} %fusion.51), channel_id=1, source_target_pairs={{0,1},{1,0},{2,3},{3,2},{4,5},{5,4},{6,7},{7,6},{8,9},{9,8},{10,11... | collective-permute-start | bytes 3145736 | tf_op jit(solution)/shard_map/ppermute | solution.py:341
  819.5 325.8 %reduce-scatter.3.cloned.1.call-start = ((), (), s32[]{:S(2)}) async-start(), calls=%async_computation.7 | async-start | bytes 13369344 | tf_op jit(solution)/shard_map/reduce_scatter | solution.py:1043
  819.6 47.1 %collective-permute-start.27 = (bf16[4,256,1024]{2,1,0:T(8,128)(2,1)}, bf16[4,256,1024]{2,1,0:T(8,128)(2,1)}, u32[]{:S(2)}, u32[]{:S(2)}) collective-permute-start(bf16[4,256,1024]{2,1,0:T(8,128)(2,1)} %pad_maximum_fusion.6), channel_id=1, source_target_pairs={{0,1},{1,0},{2,3},{3,2},{4,5},{5,4},{6,7},{7,6},{8,9},{9,8},{10,11... | collective-permute-start | bytes 6291464 | tf_op jit(solution)/shard_map/ppermute | solution.py:341
  821.3 58.1 %collective-permute-start.28 = (bf16[4,256,1024]{2,1,0:T(8,128)(2,1)}, bf16[4,256,1024]{2,1,0:T(8,128)(2,1)}, u32[]{:S(2)}, u32[]{:S(2)}) collective-permute-start(bf16[4,256,1024]{2,1,0:T(8,128)(2,1)} %pad_maximum_fusion.5), channel_id=1, source_target_pairs={{0,4},{2,6},{4,0},{6,2},{8,12},{10,14},{12,8},{14,10},{16,20},{18,... | collective-permute-start | bytes 6291464 | tf_op jit(solution)/shard_map/ppermute | solution.py:337
  891.0 8.8 collective-permute-start.37
  913.4 52.0 %collective-permute-start.29 = (bf16[4,256,1024]{2,1,0:T(8,128)(2,1)}, bf16[4,256,1024]{2,1,0:T(8,128)(2,1)}, u32[]{:S(2)}, u32[]{:S(2)}) collective-permute-start(bf16[4,256,1024]{2,1,0:T(8,128)(2,1)} %add_convert_fusion.1), channel_id=1, source_target_pairs={{0,4},{2,6},{4,0},{6,2},{8,12},{10,14},{12,8},{14,10},{16,20},{18,... | collective-permute-start | bytes 6291464 | tf_op jit(solution)/shard_map/ppermute | solution.py:337
  913.7 51.8 %collective-permute-start.30 = (bf16[4,256,1024]{2,1,0:T(8,128)(2,1)}, bf16[4,256,1024]{2,1,0:T(8,128)(2,1)}, u32[]{:S(2)}, u32[]{:S(2)}) collective-permute-start(bf16[4,256,1024]{2,1,0:T(8,128)(2,1)} %add_convert_fusion), channel_id=1, source_target_pairs={{0,1},{1,0},{2,3},{3,2},{4,5},{5,4},{6,7},{7,6},{8,9},{9,8},{10,11... | collective-permute-start | bytes 6291464 | tf_op jit(solution)/shard_map/ppermute | solution.py:341
  966.0 24.5 %collective-permute-start.34 = (bf16[256,2048]{1,0:T(8,128)(2,1)S(1)}, bf16[256,2048]{1,0:T(8,128)(2,1)S(1)}, u32[]{:S(2)}, u32[]{:S(2)}) collective-permute-start(bf16[256,2048]{1,0:T(8,128)(2,1)S(1)} %select_convert_fusion), channel_id=1, source_target_pairs={{0,1},{1,0},{2,3},{3,2},{4,5},{5,4},{6,7},{7,6},{8,9},{9,8},{10,11... | collective-permute-start | bytes 3145736 | tf_op jit(solution)/shard_map/ppermute | solution.py:341
  992.8 4.5 collective-permute-start.42
  993.9 105.0 %collective-permute-start.31 = (bf16[256,2048]{1,0:T(8,128)(2,1)}, bf16[256,2048]{1,0:T(8,128)(2,1)}, u32[]{:S(2)}, u32[]{:S(2)}) collective-permute-start(bf16[256,2048]{1,0:T(8,128)(2,1)} %pad_maximum_fusion.15), channel_id=1, source_target_pairs={{0,24},{2,26},{4,28},{6,30},{8,0},{10,2},{12,4},{14,6},{16,8},{18,... | collective-permute-start | bytes 3145736 | tf_op jit(solution)/shard_map/ppermute | solution.py:358
  996.8 150.0 %collective-permute-start.32 = (bf16[256,2048]{1,0:T(8,128)(2,1)}, bf16[256,2048]{1,0:T(8,128)(2,1)}, u32[]{:S(2)}, u32[]{:S(2)}) collective-permute-start(bf16[256,2048]{1,0:T(8,128)(2,1)} %pad_maximum_fusion.16), channel_id=1, source_target_pairs={{0,16},{2,18},{4,20},{6,22},{8,24},{10,26},{12,28},{14,30},{16,0},... | collective-permute-start | bytes 3145736 | tf_op jit(solution)/shard_map/ppermute | solution.py:358
  996.8 150.0 %collective-permute-start.33 = (bf16[256,2048]{1,0:T(8,128)(2,1)}, bf16[256,2048]{1,0:T(8,128)(2,1)}, u32[]{:S(2)}, u32[]{:S(2)}) collective-permute-start(bf16[256,2048]{1,0:T(8,128)(2,1)} %pad_maximum_fusion.17), channel_id=1, source_target_pairs={{0,8},{2,10},{4,12},{6,14},{8,16},{10,18},{12,20},{14,22},{16,24},... | collective-permute-start | bytes 3145736 | tf_op jit(solution)/shard_map/ppermute | solution.py:358
  997.4 34.0 %collective-permute-start.43 = (f32[18,128]{1,0:T(8,128)S(1)}, f32[18,128]{1,0:T(8,128)S(1)}, u32[]{:S(2)}, u32[]{:S(2)}) collective-permute-start(f32[18,128]{1,0:T(8,128)S(1)} %fusion.48), channel_id=1, source_target_pairs={{0,1},{1,0},{2,3},{3,2},{4,5},{5,4},{6,7},{7,6},{8,9},{9,8},{10,11... | collective-permute-start | bytes 27656 | tf_op jit(solution)/shard_map/ppermute | solution.py:341
  1031.4 19.8 %collective-permute-start.44 = (f32[18,128]{1,0:T(8,128)S(1)}, f32[18,128]{1,0:T(8,128)S(1)}, u32[]{:S(2)}, u32[]{:S(2)}) collective-permute-start(f32[18,128]{1,0:T(8,128)S(1)} %add.671), channel_id=1, source_target_pairs={{0,4},{2,6},{4,0},{6,2},{8,12},{10,14},{12,8},{14,10},{16,20},{18,... | collective-permute-start | bytes 27656 | tf_op jit(solution)/shard_map/ppermute | solution.py:398
  1051.2 41.7 %collective-permute-start.45 = (f32[18,128]{1,0:T(8,128)S(1)}, f32[18,128]{1,0:T(8,128)S(1)}, u32[]{:S(2)}, u32[]{:S(2)}) collective-permute-start(f32[18,128]{1,0:T(8,128)S(1)} %add.672), channel_id=1, source_target_pairs={{0,8},{2,10},{4,12},{6,14},{8,0},{10,2},{12,4},{14,6},{16,24},{18,... | collective-permute-start | bytes 27656 | tf_op jit(solution)/shard_map/ppermute | solution.py:398
  1092.9 60.2 %collective-permute-start.46 = (f32[18,128]{1,0:T(8,128)S(1)}, f32[18,128]{1,0:T(8,128)S(1)}, u32[]{:S(2)}, u32[]{:S(2)}) collective-permute-start(f32[18,128]{1,0:T(8,128)S(1)} %add.673), channel_id=1, source_target_pairs={{0,16},{2,18},{4,20},{6,22},{8,24},{10,26},{12,28},{14,30},{16,0},... | collective-permute-start | bytes 27656 | tf_op jit(solution)/shard_map/ppermute | solution.py:398
  1097.5 56.9 %collective-permute-start.36 = (bf16[128,2048]{1,0:T(8,128)(2,1)}, bf16[128,2048]{1,0:T(8,128)(2,1)}, u32[]{:S(2)}, u32[]{:S(2)}) collective-permute-start(bf16[128,2048]{1,0:T(8,128)(2,1)} %reduce-scatter.5.cloned.1.call-done), channel_id=1, source_target_pairs={{0,1},{1,0},{2,3},{3,2},{4,5},{5,4},{6,7},{7,6},{8,9},{9,8},{10,11... | collective-permute-start | bytes 1572872 | tf_op jit(solution)/shard_map/ppermute | solution.py:341
  1145.3 19.8 %collective-permute-start.35 = (bf16[128,3072]{1,0:T(8,128)(2,1)}, bf16[128,3072]{1,0:T(8,128)(2,1)S(1)}, u32[]{:S(2)}, u32[]{:S(2)}) collective-permute-start(bf16[128,3072]{1,0:T(8,128)(2,1)} %reduce-scatter.3.cloned.1.call-done.mine_ref), channel_id=1, source_target_pairs={{0,1},{1,0},{2,3},{3,2},{4,5},{5,4},{6,7},{7,6},{8,9},{9,8},{10,11... | collective-permute-start | bytes 2359304 | tf_op jit(solution)/shard_map/ppermute | solution.py:341
  (81 other events, 2045.5 us)
Sparse Core Ops, SparseCore 0:
  10.4 112.8 all-gather.3
  125.4 134.2 all-gather.7
  261.9 168.0 all-gather.5
  819.7 117.9 reduce-scatter.4
  941.5 203.7 reduce-scatter.2

commit v7 on v6

--- a/solution.py
+++ b/solution.py
@@ -363,10 +363,6 @@
     for item in arrived.values():
         total = total + item.astype(full)
     return total
-
-
-def line_sum(entries, count):
-    return line_total(entries[0], {s: line_shift(entries[s], count - s) for s in range(1, count)})
 
 
 def joined(places, own, got):
@@ -965,17 +961,16 @@
     grad_gates = lax.all_to_all(
         gate_back.reshape(fsdp * 2, rows_dev), both, split_axis=0, concat_axis=0, tiled=True
     ).T
-    out_far = run_result(state["core"], order_of(steps_far), 0, hidden, gates_all, expert_down[0], capacity)
-    out_rest = run_result(
-        state["core"],
-        order_of(steps_mixed[0] + steps_own + steps_mixed[1]),
-        lines,
-        hidden,
-        gates_all,
-        expert_down[0],
-        capacity,
-    )
-    got, out_far, out_rest, arrived = lax.optimization_barrier((got, out_far, out_rest, arrived))
+    def results(first, steps, hidden):
+        return run_result(
+            state["core"], order_of(steps), first, hidden, gates_all, expert_down[0], capacity
+        )
+
+    out_far = results(0, steps_far, hidden)
+    out_rest = results(lines, steps_mixed[0] + steps_own + steps_mixed[1], hidden)
+    got, out_far, out_rest, arrived, grad_gates = lax.optimization_barrier(
+        (got, out_far, out_rest, arrived, grad_gates)
+    )
     entries.update(joined(parts[1], [item[cut:] for item in back_own], got))
     out_far = over_core(*out_far)
     out_far = [
@@ -1012,21 +1007,23 @@
         add_low(ctx_two, out_far[1]),
     ]
     grad_attended = mul(grad_branch, out_all, rhs_turned).astype(low)
+    grad_attended, got = hold(grad_attended, got)
+    got[2], got[3] = swap_side(got[2]), swap_ctx(got[3])
     grad_out_part = mul(attended, grad_branch, lhs_turned).astype(low)
     grad_q, grad_k, grad_v, gain_q_part, gain_k_part = attend_grad(
         projected, roped_q, roped_k, values_low, grad_attended, cosine, sine, gain_q, gain_k, kv_heads, group
     )
     grad_projected = jnp.concatenate([grad_q, grad_k, grad_v], axis=1)
+    grad_qkv_part = mul(low_in, grad_projected, lhs_turned).astype(low)
     grad_projected, got = hold(grad_projected, got)
-    got[2], got[3] = swap_side(got[2]), swap_ctx(got[3])
-    grad_qkv_part = mul(low_in, grad_projected, lhs_turned).astype(low)
+    entries = joined(places, out_own, got)
+    grad_projected, entries = hold(grad_projected, entries)
+    arrived = {p: line_shift(entries[p], lines - p) for p in places[:-1]}
     grad_normed_part = mul(grad_projected, qkv_all, rhs_turned)
-    grad_normed_part, got = hold(grad_normed_part, got)
-    entries = joined(places, out_own, got)
-    (rows, grad_pair, hidden, grad_rows), entries = hold((rows, grad_pair, hidden, grad_rows), entries)
+    (rows, grad_pair, hidden, grad_rows), arrived = hold((rows, grad_pair, hidden, grad_rows), arrived)
     grad_gate_up = mul(rows, grad_pair, lhs_turned)[None]
     grad_down = mul(hidden, grad_rows, lhs_turned)[None]
-    output = (mixed + line_sum(entries, lines)).astype(low)
+    output = (mixed + line_total(entries[0], arrived)).astype(low)
     grad_normed = of_block(grad_normed_part, rank) + swap_ctx(
         of_block(grad_normed_part, 1 - rank).astype(low)
     ).astype(full)

time: 1190 us -> 1240 us (1.042)
  waiting for transfers between devices: 558 us -> 660 us
  blocking collectives: 82.2 us -> 35.6 us
    ppermute x6, waiting for transfers between devices: 14 us -> 140 us  [line_shift(): lax.ppermute(values, 'fsdp', [(i, (i + 4 * step) % fsdp) for i in range(f...]
    ppermute x19, waiting for transfers between devices: 265 us -> 331 us  [swap_ctx(): return lax.ppermute(values, 'ctx', [(0, 1), (1, 0)])]
    all_to_all x1 -> x0, blocking collectives: 46.8 us -> none  [body_gathered(): lax.all_to_all(gate_back.reshape(fsdp * 2, rows_dev), both, split_axis=0,...]
    reduce_scatter x1, waiting for transfers between devices: 46.4 us -> 0.01 us  [body_gathered(): lax.psum_scatter(grad_qkv_part, 'fsdp', scatter_dimension=0, tiled=True)]
    ppermute x3, waiting for transfers between devices: 38.7 us -> 3.68 us  [sum_all(): lax.ppermute(values, 'fsdp', [(i, i ^ step) for i in range(fsdp)])]
  transfers between devices with their start and end apart: 52 -> 53, of which waited for: 27 -> 31; matrix products, arithmetic and copies ran while one was open for 19% -> 18% of each run, Pallas kernels for 16% -> 15%
where the time goes in v7:
time: 1240 us
  waiting for transfers between devices  660 us (53%)
  Pallas kernels  224 us (18%)
  matrix products  111 us (9%)
  other arithmetic  105 us (8%)
  starting transfers between devices  52.6 us (4%)
  blocking collectives  35.6 us (3%)
  local copies, waits for them, and re-layouts  31.1 us (3%)
  between operations  15.5 us (1%)
    ppermute x19, waiting for transfers between devices, swap_ctx(): return lax.ppermute(values, 'ctx', [(0, 1), (1, 0)])  331 us
    ppermute x6, waiting for transfers between devices, line_shift(): lax.ppermute(values, 'fsdp', [(i, (i + 4 * step) % fsdp) for i in range(f...  140 us
    pallas_call x4, Pallas kernels, run_expert(): pl.pallas_call(expert_kernel, grid_spec=grid_spec, out_shape=[shape((step...  135 us
    dot_general x11, matrix products, mul(): return lax.dot_general(left, right, dims, preferred_element_type=full)  111 us
    all_gather x1, waiting for transfers between devices, body_gathered(): weights_all = lax.all_gather(weights_local, 'fsdp', axis=0, tiled=True)  65.6 us
    convert_element_type x19, other arithmetic, add_low(): return (one.astype(full) + two.astype(full)).astype(low)  65.3 us
    ppermute x8, waiting for transfers between devices, swap_side(): return lax.ppermute(values, 'fsdp', side_pairs(lax.axis_size('fsdp')))  42.5 us
    pallas_call x2, Pallas kernels, run_result(): pl.pallas_call(result_kernel, grid_spec=pltpu.PrefetchScalarGridSpec(num_...  40.2 us
  transfers between devices with their start and end apart: 53, of which 31 were waited for; matrix products, arithmetic and copies ran while one was open for 18% of the time, Pallas kernels for 15%

profile of v7, /device:TPU:0, one launch (start us, length us, event | category | flops | bytes accessed | tf_op | source)
XLA Modules:
  0.0 1235.3 jit_solution(205171135555831298)
XLA Ops:
  13.4 13.3 %collective-permute-done.3 = bf16[256,1152]{1,0:T(8,128)(2,1)S(1)} collective-permute-done((bf16[256,1152]{1,0:T(8,128)(2,1)S(1)}, bf16[256,1152]{1,0:T(8,128)(2,1)S(1)}, u32[]{:S(2)}, u32[]{:S(2)}) %collective-permute-start.3) | collective-permute-done | bytes 589856 | tf_op jit(solution)/shard_map/ppermute | solution.py:341
  31.2 22.9 %all_gather.12 = bf16[2048,34]{0,1:T(8,128)(2,1)S(1)} all-gather(bf16[128,34]{0,1:T(8,128)(2,1)S(1)} %pad_maximum_fusion.20), channel_id=1, replica_groups=mesh['fsdp'=16,'ctx'=2] {'fsdp'}, dimensions={0}, use_global_device_ids=true | all-gather | bytes 147968 | tf_op jit(solution)/shard_map/all_gather | solution.py:835
  57.6 65.6 %all-gather.4.cloned.1.call-done = bf16[2048,5120]{1,0:T(8,128)(2,1)} async-done(((bf16[128,5120]{1,0:T(8,128)(2,1)}), bf16[2048,5120]{1,0:T(8,128)(2,1)}) %all-gather.4.cloned.1.call-update) | async-done | bytes 20971536 | tf_op jit(solution)/shard_map/all_gather | solution.py:836
  123.2 11.5 fusion.2.q_ref.k_ref.v_ref
  134.7 18.2 %attend.1 = (bf16[512,2048]{1,0:T(8,128)(2,1)S(1)}, bf16[512,2048]{1,0:T(8,128)(2,1)S(1)}, bf16[512,512]{1,0:T(8,128)(2,1)S(1)}, bf16[512,512]{1,0:T(8,128)(2,1)S(1)}) custom-call(f32[512,3072]{1,0:T(8,128)} %fusion.2.q_ref.k_ref.v_ref, f32[512,3072]{1,0:T(8,128)} %fusion.2.q_ref.k_ref.v_ref, f32[512,3072]{1,0:T(8,128)} %fusion.2.q_ref.k_ref.v_ref, ...), custom_call_target="tpu_custom_call" | custom-call | flops 2147483648 | bytes 9437184 | tf_op jit(solution)/shard_map/attend/pallas_call | solution.py:521
  153.0 8.4 fusion.6
  163.5 23.8 %collective-permute-done.1 = bf16[256,2048]{1,0:T(8,128)(2,1)S(1)} collective-permute-done((bf16[256,2048]{1,0:T(8,128)(2,1)S(1)}, bf16[256,2048]{1,0:T(8,128)(2,1)S(1)}, u32[]{:S(2)}, u32[]{:S(2)}) %collective-permute-start.1) | collective-permute-done | bytes 1048608 | tf_op jit(solution)/shard_map/ppermute | solution.py:341
  191.7 23.1 %collective-permute-done.2 = bf16[256,2048]{1,0:T(8,128)(2,1)S(1)} collective-permute-done((bf16[256,2048]{1,0:T(8,128)(2,1)S(1)}, bf16[256,2048]{1,0:T(8,128)(2,1)S(1)}, u32[]{:S(2)}, u32[]{:S(2)}) %collective-permute-start.2) | collective-permute-done | bytes 1048608 | tf_op jit(solution)/shard_map/ppermute | solution.py:341
  218.4 12.8 %all_to_all.24 = f32[32,1,256]{2,1,0:T(1,128)S(1)} all-to-all(f32[32,1,256]{2,1,0:T(1,128)S(1)} %copy.60), channel_id=1, replica_groups=mesh['fsdp'=16,'ctx'=2] {'fsdp','ctx'}, dimensions={0} | all-to-all | bytes 65536 | tf_op jit(solution)/shard_map/all_to_all | solution.py:873
  231.1 28.6 %all-gather.8.cloned.1.call-done = bf16[4096,3200]{1,0:T(8,128)(2,1)} async-done(((bf16[256,3200]{1,0:T(8,128)(2,1)}), bf16[4096,3200]{1,0:T(8,128)(2,1)}) %all-gather.8.cloned.1.call-update) | async-done | bytes 26214416 | tf_op jit(solution)/shard_map/all_gather | solution.py:843
  259.7 6.9 slice.403
  269.4 157.7 %collective-permute-done.4.far_ref = bf16[8,2,256,896]{3,2,1,0:T(8,128)(2,1)} collective-permute-done((bf16[8,2,256,896]{3,2,1,0:T(8,128)(2,1)}, bf16[8,2,256,896]{3,2,1,0:T(8,128)(2,1)}, u32[]{:S(2)}, u32[]{:S(2)}) %collective-permute-start.4) | collective-permute-done | bytes 7340064 | tf_op jit(solution)/shard_map/ppermute | solution.py:341
  429.9 33.1 %experts.4 = (bf16[4,256,2048]{2,1,0:T(8,128)(2,1)}, bf16[4,256,2048]{2,1,0:T(8,128)(2,1)}, f32[8,2,2,1,256]{4,3,2,1,0:T(1,128)}, bf16[4096,2048]{1,0:T(8,128)(2...) custom-call(s32[1]{0:T(128)} %bitcast.6.core_ref, s32[16]{0:T(128)} %stack.35.order, ...), custom_call_target="tpu_custom_call" | custom-call | flops 19327352832 | bytes 38273024 | tf_op jit(solution)/shard_map/experts/pallas_call | solution.py:670
  463.4 7.1 collective-permute-done.5
  470.5 4.8 add_convert_fusion.8
  478.5 34.2 %experts.5 = (bf16[4,256,2048]{2,1,0:T(8,128)(2,1)}, bf16[4,256,2048]{2,1,0:T(8,128)(2,1)}, f32[8,2,2,1,256]{4,3,2,1,0:T(1,128)}, bf16[4096,2048]{1,0:T(8,128)(2...) custom-call(s32[1]{0:T(128)} %bitcast.6.core_ref, ...), custom_call_target="tpu_custom_call", output_to_operand_aliasing={{2}: (8, {}), {3}: (9, {}), {4}: (10, {}), {5}: (11, {}), {... | custom-call | flops 19327352832 | bytes 38273024 | tf_op jit(solution)/shard_map/experts/pallas_call | solution.py:670
  512.7 10.7 collective-permute-done.7
  525.8 33.7 %experts.6 = (bf16[4,256,2048]{2,1,0:T(8,128)(2,1)}, bf16[4,256,2048]{2,1,0:T(8,128)(2,1)}, f32[8,2,2,1,256]{4,3,2,1,0:T(1,128)}, bf16[4096,2048]{1,0:T(8,128)(2...) custom-call(s32[1]{0:T(128)} %bitcast.6.core_ref, ...), custom_call_target="tpu_custom_call", output_to_operand_aliasing={{2}: (8, {}), {3}: (9, {}), {4}: (10, {}), {5}: (11, {}), {... | custom-call | flops 19327352832 | bytes 38273024 | tf_op jit(solution)/shard_map/experts/pallas_call | solution.py:670
  560.1 4.5 add_convert_fusion.27
  573.0 33.7 %experts.7 = (bf16[4,256,2048]{2,1,0:T(8,128)(2,1)}, bf16[4,256,2048]{2,1,0:T(8,128)(2,1)}, f32[8,2,2,1,256]{4,3,2,1,0:T(1,128)}, bf16[4096,2048]{1,0:T(8,128)(2...) custom-call(s32[1]{0:T(128)} %bitcast.6.core_ref, ...), custom_call_target="tpu_custom_call", output_to_operand_aliasing={{2}: (8, {}), {3}: (9, {}), {4}: (10, {}), {5}: (11, {}), {... | custom-call | flops 19327352832 | bytes 38273024 | tf_op jit(solution)/shard_map/experts/pallas_call | solution.py:670
  606.8 5.8 collective-permute-done.12
  613.3 4.7 all-to-all-start.1
  618.1 5.7 add_convert_fusion.7
  647.7 11.9 results.2
  660.1 28.3 %results.3 = (bf16[12,256,2048]{2,1,0:T(8,128)(2,1)}, bf16[12,256,2048]{2,1,0:T(8,128)(2,1)}) custom-call(s32[1]{0:T(128)} %bitcast.6.core_ref, s32[48]{0:T(128)} %stack.44.order, bf16[4096,768]{1,0:T(8,128)(2,1)} %get-tuple-element.227.z_ref, f32[8,2,2,1,256]{4,3,2,1,0:T(1,128)} %reshape.272.w_ref, bf16[768,2048]{1,0:T(8,128)(2,1)} %bitcast.155), custom_call_target="tpu_custom_call" | custom-call | flops 12884901888 | bytes 33030144 | tf_op jit(solution)/shard_map/results/pallas_call | solution.py:701
  688.4 12.8 %collective-permute-done.20 = bf16[256,2048]{1,0:T(8,128)(2,1)S(1)} collective-permute-done((bf16[256,2048]{1,0:T(8,128)(2,1)}, bf16[256,2048]{1,0:T(8,128)(2,1)S(1)}, u32[]{:S(2)}, u32[]{:S(2)}) %collective-permute-start.20) | collective-permute-done | bytes 1048608 | tf_op jit(solution)/shard_map/ppermute | solution.py:358
  710.3 17.3 %collective-permute-done.22 = bf16[4,256,2048]{2,1,0:T(8,128)(2,1)S(1)} collective-permute-done((bf16[4,256,2048]{2,1,0:T(8,128)(2,1)}, bf16[4,256,2048]{2,1,0:T(8,128)(2,1)S(1)}, u32[]{:S(2)}, u32[]{:S(2)}) %collective-permute-start.22) | collective-permute-done | bytes 4194336 | tf_op jit(solution)/shard_map/ppermute | solution.py:333
  740.8 38.5 %collective-permute-done.23 = bf16[4,256,1024]{2,1,0:T(8,128)(2,1)S(1)} collective-permute-done((bf16[4,256,1024]{2,1,0:T(8,128)(2,1)}, bf16[4,256,1024]{2,1,0:T(8,128)(2,1)S(1)}, u32[]{:S(2)}, u32[]{:S(2)}) %collective-permute-start.23) | collective-permute-done | bytes 2097184 | tf_op jit(solution)/shard_map/ppermute | solution.py:341
  782.8 5.1 add_convert_fusion.12
  799.8 6.2 collective-permute-done.26
  809.9 6.8 convolution_convert_fusion.1
  819.6 4.6 add_convert_fusion.1
  826.5 10.1 fusion.11.go_ref
  836.6 26.1 %collective-permute-done.27 = bf16[4,256,1024]{2,1,0:T(8,128)(2,1)S(1)} collective-permute-done((bf16[4,256,1024]{2,1,0:T(8,128)(2,1)}, bf16[4,256,1024]{2,1,0:T(8,128)(2,1)S(1)}, u32[]{:S(2)}, u32[]{:S(2)}) %collective-permute-start.27) | collective-permute-done | bytes 2097184 | tf_op jit(solution)/shard_map/ppermute | solution.py:341
  862.7 12.5 %collective-permute-done.28 = bf16[4,256,1024]{2,1,0:T(8,128)(2,1)S(1)} collective-permute-done((bf16[4,256,1024]{2,1,0:T(8,128)(2,1)}, bf16[4,256,1024]{2,1,0:T(8,128)(2,1)S(1)}, u32[]{:S(2)}, u32[]{:S(2)}) %collective-permute-start.28) | collective-permute-done | bytes 2097184 | tf_op jit(solution)/shard_map/ppermute | solution.py:337
  876.6 25.0 %attend_grad.1 = (bf16[512,2048]{1,0:T(8,128)(2,1)S(1)}, bf16[512,512]{1,0:T(8,128)(2,1)S(1)}, bf16[512,512]{1,0:T(8,128)(2,1)S(1)}, f32[4,1,128]{2,1,0:T(1,128)S(1)}, f32[4,1,128]{2,1,0:T(1,128)S(1)}) custom-call(f32[512,3072]{1,0:T(8,128)} %fusion.2.q_ref.k_ref.v_ref, f32[512,3072]{1,0:T(8,128)} %fusion.2.q_ref.k_ref.v_ref, bf16[512,2048]{1,0:T(8,128)(2,1)} %copy-done, ...), custom_call_target="tpu_custom_call" | custom-call | flops 5368709120 | bytes 15728640 | tf_op jit(solution)/shard_map/attend_grad/pallas_call | solution.py:545
  904.4 10.0 convolution_convert_fusion
  917.0 14.3 %collective-permute-done.37 = f32[8,33,128]{2,0,1:T(8,128)S(1)} collective-permute-done((f32[8,33,128]{2,0,1:T(8,128)S(1)}, f32[8,33,128]{2,0,1:T(8,128)S(1)}, u32[]{:S(2)}, u32[]{:S(2)}) %collective-permute-start.37) | collective-permute-done | bytes 135200 | tf_op jit(solution)/shard_map/ppermute | solution.py:406
  937.2 21.8 %collective-permute-done.29 = bf16[4,256,1024]{2,1,0:T(8,128)(2,1)} collective-permute-done((bf16[4,256,1024]{2,1,0:T(8,128)(2,1)}, bf16[4,256,1024]{2,1,0:T(8,128)(2,1)}, u32[]{:S(2)}, u32[]{:S(2)}) %collective-permute-start.29) | collective-permute-done | bytes 2097184 | tf_op jit(solution)/shard_map/ppermute | solution.py:337
  972.5 9.7 fusion
  993.9 12.9 %collective-permute-done.41 = f32[33,128]{1,0:T(8,128)S(1)} collective-permute-done((f32[33,128]{1,0:T(8,128)S(1)}, f32[33,128]{1,0:T(8,128)S(1)}, u32[]{:S(2)}, u32[]{:S(2)}) %collective-permute-start.41) | collective-permute-done | bytes 16928 | tf_op jit(solution)/shard_map/ppermute | solution.py:341
  1012.5 32.5 %collective-permute-done.31 = bf16[256,2048]{1,0:T(8,128)(2,1)} collective-permute-done((bf16[256,2048]{1,0:T(8,128)(2,1)}, bf16[256,2048]{1,0:T(8,128)(2,1)}, u32[]{:S(2)}, u32[]{:S(2)}) %collective-permute-start.31) | collective-permute-done | bytes 1048608 | tf_op jit(solution)/shard_map/ppermute | solution.py:358
  1045.0 92.0 %collective-permute-done.32 = bf16[256,2048]{1,0:T(8,128)(2,1)} collective-permute-done((bf16[256,2048]{1,0:T(8,128)(2,1)}, bf16[256,2048]{1,0:T(8,128)(2,1)}, u32[]{:S(2)}, u32[]{:S(2)}) %collective-permute-start.32) | collective-permute-done | bytes 1048608 | tf_op jit(solution)/shard_map/ppermute | solution.py:358
  1138.6 35.5 %convolution_bitcast_fusion = f32[1,2048,1536]{2,1,0:T(8,128)} fusion(bf16[4096,2048]{1,0:T(8,128)(2,1)} %get-tuple-element.225, bf16[4096,1536]{1,0:T(8,128)(2,1)} %get-tuple-element.226), kind=kOutput, calls=%fused_computation.5 | convolution fusion | flops 25769803776 | bytes 41943040 | tf_op jit(solution)/shard_map/dot_general | solution.py:321
  1175.6 15.7 %convolution_bitcast_fusion.1 = f32[1,768,2048]{2,1,0:T(8,128)} fusion(bf16[4096,768]{1,0:T(8,128)(2,1)S(1)} %bitcast.149, bf16[4096,2048]{1,0:T(8,128)(2,1)S(1)} %bitcast.143), kind=kOutput, calls=%fused_computation.26 | convolution fusion | flops 12884901888 | bytes 29360128 | tf_op jit(solution)/shard_map/dot_general | solution.py:321
  1197.1 6.5 fusion.20
  1204.8 5.3 collective-permute-done.36
  1211.7 12.6 %collective-permute-done.35.other_ref = bf16[128,3072]{1,0:T(8,128)(2,1)S(1)} collective-permute-done((bf16[128,3072]{1,0:T(8,128)(2,1)}, bf16[128,3072]{1,0:T(8,128)(2,1)S(1)}, u32[]{:S(2)}, u32[]{:S(2)}) %collective-permute-start.35) | collective-permute-done | bytes 786464 | tf_op jit(solution)/shard_map/ppermute | solution.py:341
  (350 shorter events, 174.8 us)
Async XLA Ops:
  7.2 116.1 %all-gather.4.cloned.1.call-start = ((), (), s32[]{:S(2)}) async-start(), calls=%async_computation.4 | async-start | bytes 22282240 | tf_op jit(solution)/shard_map/all_gather | solution.py:836
  10.2 249.5 %all-gather.8.cloned.1.call-start = ((), (), s32[]{:S(2)}) async-start(), calls=%async_computation.6 | async-start | bytes 27852800 | tf_op jit(solution)/shard_map/all_gather | solution.py:843
  10.4 16.3 %collective-permute-start.3 = (bf16[256,1152]{1,0:T(8,128)(2,1)S(1)}, bf16[256,1152]{1,0:T(8,128)(2,1)S(1)}, u32[]{:S(2)}, u32[]{:S(2)}) collective-permute-start(bf16[256,1152]{1,0:T(8,128)(2,1)S(1)} %slice.401), channel_id=1, source_target_pairs={{0,1},{1,0},{2,3},{3,2},{4,5},{5,4},{6,7},{7,6},{8,9},{9,8},{10,11... | collective-permute-start | bytes 1769480 | tf_op jit(solution)/shard_map/ppermute | solution.py:341
  28.1 401.9 %all-gather.6.cloned.1.call-start = ((), (), s32[]{:S(2)}) async-start(), calls=%async_computation.5 | async-start | bytes 35651584 | tf_op jit(solution)/shard_map/all_gather | solution.py:864
  28.1 26.4 %collective-permute-start = (bf16[256,2048]{1,0:T(8,128)(2,1)S(1)}, bf16[256,2048]{1,0:T(8,128)(2,1)}, u32[]{:S(2)}, u32[]{:S(2)}) collective-permute-start(bf16[256,2048]{1,0:T(8,128)(2,1)S(1)} %copy-done.6), channel_id=1, source_target_pairs={{0,1},{1,0},{2,3},{3,2},{4,5},{5,4},{6,7},{7,6},{8,9},{9,8},{10,11... | collective-permute-start | bytes 3145736 | tf_op jit(solution)/shard_map/ppermute | solution.py:341
  162.0 25.4 %collective-permute-start.1 = (bf16[256,2048]{1,0:T(8,128)(2,1)S(1)}, bf16[256,2048]{1,0:T(8,128)(2,1)S(1)}, u32[]{:S(2)}, u32[]{:S(2)}) collective-permute-start(bf16[256,2048]{1,0:T(8,128)(2,1)S(1)} %select_convert_fusion.1), channel_id=1, source_target_pairs={{0,1},{1,0},{2,3},{3,2},{4,5},{5,4},{6,7},{7,6},{8,9},{9,8},{10,11... | collective-permute-start | bytes 3145736 | tf_op jit(solution)/shard_map/ppermute | solution.py:341
  190.2 24.7 %collective-permute-start.2 = (bf16[256,2048]{1,0:T(8,128)(2,1)S(1)}, bf16[256,2048]{1,0:T(8,128)(2,1)S(1)}, u32[]{:S(2)}, u32[]{:S(2)}) collective-permute-start(bf16[256,2048]{1,0:T(8,128)(2,1)S(1)} %multiply_convert_fusion), channel_id=1, source_target_pairs={{0,1},{1,0},{2,3},{3,2},{4,5},{5,4},{6,7},{7,6},{8,9},{9,8},{10,11... | collective-permute-start | bytes 3145736 | tf_op jit(solution)/shard_map/ppermute | solution.py:341
  266.6 160.5 %collective-permute-start.4 = (bf16[8,2,256,896]{3,2,1,0:T(8,128)(2,1)}, bf16[8,2,256,896]{3,2,1,0:T(8,128)(2,1)}, u32[]{:S(2)}, u32[]{:S(2)}) collective-permute-start(bf16[8,2,256,896]{3,2,1,0:T(8,128)(2,1)} %slice.403), channel_id=1, source_target_pairs={{0,1},{1,0},{2,3},{3,2},{4,5},{5,4},{6,7},{7,6},{8,9},{9,8},{10,11... | collective-permute-start | bytes 22020104 | tf_op jit(solution)/shard_map/ppermute | solution.py:341
  475.3 48.1 %collective-permute-start.7 = (bf16[4,256,1024]{2,1,0:T(8,128)(2,1)}, bf16[4,256,1024]{2,1,0:T(8,128)(2,1)}, u32[]{:S(2)}, u32[]{:S(2)}) collective-permute-start(bf16[4,256,1024]{2,1,0:T(8,128)(2,1)} %get-tuple-element.143), channel_id=1, source_target_pairs={{0,1},{1,0},{2,3},{3,2},{4,5},{5,4},{6,7},{7,6},{8,9},{9,8},{10,11... | collective-permute-start | bytes 6291464 | tf_op jit(solution)/shard_map/ppermute | solution.py:341
  476.8 47.8 %collective-permute-start.8 = (bf16[4,256,1024]{2,1,0:T(8,128)(2,1)}, bf16[4,256,1024]{2,1,0:T(8,128)(2,1)}, u32[]{:S(2)}, u32[]{:S(2)}) collective-permute-start(bf16[4,256,1024]{2,1,0:T(8,128)(2,1)} %get-tuple-element.144), channel_id=1, source_target_pairs={{0,4},{2,6},{4,0},{6,2},{8,12},{10,14},{12,8},{14,10},{16,20},{18,... | collective-permute-start | bytes 6291464 | tf_op jit(solution)/shard_map/ppermute | solution.py:337
  524.6 35.5 %collective-permute-start.9 = (bf16[4,256,2048]{2,1,0:T(8,128)(2,1)}, bf16[4,256,2048]{2,1,0:T(8,128)(2,1)}, u32[]{:S(2)}, u32[]{:S(2)}) collective-permute-start(bf16[4,256,2048]{2,1,0:T(8,128)(2,1)} %get-tuple-element.145), channel_id=1, source_target_pairs={{0,2},{2,0},{4,6},{6,4},{8,10},{10,8},{12,14},{14,12},{16,18},{18,... | collective-permute-start | bytes 12582920 | tf_op jit(solution)/shard_map/ppermute | solution.py:333
  559.5 58.6 %collective-permute-start.6 = (bf16[4,256,2048]{2,1,0:T(8,128)(2,1)}, bf16[4,256,2048]{2,1,0:T(8,128)(2,1)}, u32[]{:S(2)}, u32[]{:S(2)}) collective-permute-start(bf16[4,256,2048]{2,1,0:T(8,128)(2,1)} %get-tuple-element.140), channel_id=1, source_target_pairs={{0,2},{2,0},{4,6},{6,4},{8,10},{10,8},{12,14},{14,12},{16,18},{18,... | collective-permute-start | bytes 12582920 | tf_op jit(solution)/shard_map/ppermute | solution.py:333
  564.6 42.1 %collective-permute-start.10 = (bf16[2,256,1024]{2,1,0:T(8,128)(2,1)S(1)}, bf16[2,256,1024]{2,1,0:T(8,128)(2,1)}, u32[]{:S(2)}, u32[]{:S(2)}) collective-permute-start(bf16[2,256,1024]{2,1,0:T(8,128)(2,1)S(1)} %get-tuple-element.155), channel_id=1, source_target_pairs={{0,1},{1,0},{2,3},{3,2},{4,5},{5,4},{6,7},{7,6},{8,9},{9,8},{10,11... | collective-permute-start | bytes 3145736 | tf_op jit(solution)/shard_map/ppermute | solution.py:341
  565.2 41.5 %collective-permute-start.11 = (bf16[2,256,1024]{2,1,0:T(8,128)(2,1)S(1)}, bf16[2,256,1024]{2,1,0:T(8,128)(2,1)}, u32[]{:S(2)}, u32[]{:S(2)}) collective-permute-start(bf16[2,256,1024]{2,1,0:T(8,128)(2,1)S(1)} %get-tuple-element.156), channel_id=1, source_target_pairs={{0,4},{2,6},{4,0},{6,2},{8,12},{10,14},{12,8},{14,10},{16,20},{18,... | collective-permute-start | bytes 3145736 | tf_op jit(solution)/shard_map/ppermute | solution.py:337
  568.1 44.5 %collective-permute-start.12 = (bf16[2,256,1024]{2,1,0:T(8,128)(2,1)S(1)}, bf16[2,256,1024]{2,1,0:T(8,128)(2,1)}, u32[]{:S(2)}, u32[]{:S(2)}) collective-permute-start(bf16[2,256,1024]{2,1,0:T(8,128)(2,1)S(1)} %add_convert_fusion.26), channel_id=1, source_target_pairs={{0,4},{2,6},{4,0},{6,2},{8,12},{10,14},{12,8},{14,10},{16,20},{18,... | collective-permute-start | bytes 3145736 | tf_op jit(solution)/shard_map/ppermute | solution.py:337
  571.6 41.1 %collective-permute-start.13 = (bf16[2,256,1024]{2,1,0:T(8,128)(2,1)}, bf16[2,256,1024]{2,1,0:T(8,128)(2,1)}, u32[]{:S(2)}, u32[]{:S(2)}) collective-permute-start(bf16[2,256,1024]{2,1,0:T(8,128)(2,1)} %add_convert_fusion.25), channel_id=1, source_target_pairs={{0,1},{1,0},{2,3},{3,2},{4,5},{5,4},{6,7},{7,6},{8,9},{9,8},{10,11... | collective-permute-start | bytes 3145736 | tf_op jit(solution)/shard_map/ppermute | solution.py:341
  612.6 21.8 %collective-permute-start.14 = (bf16[4,256,2048]{2,1,0:T(8,128)(2,1)}, bf16[4,256,2048]{2,1,0:T(8,128)(2,1)}, u32[]{:S(2)}, u32[]{:S(2)}) collective-permute-start(bf16[4,256,2048]{2,1,0:T(8,128)(2,1)} %get-tuple-element.161), channel_id=1, source_target_pairs={{0,2},{2,0},{4,6},{6,4},{8,10},{10,8},{12,14},{14,12},{16,18},{18,... | collective-permute-start | bytes 12582920 | tf_op jit(solution)/shard_map/ppermute | solution.py:333
  613.3 12.1 all-to-all-start.1
  618.0 576.9 %reduce-scatter.5.cloned.1.call-start = ((), (), s32[]{:S(2)}) async-start(), calls=%async_computation.8 | async-start | bytes 8912896 | tf_op jit(solution)/shard_map/reduce_scatter | solution.py:1033
  631.2 28.4 %collective-permute-start.19 = (bf16[256,2048]{1,0:T(8,128)(2,1)}, bf16[256,2048]{1,0:T(8,128)(2,1)S(1)}, u32[]{:S(2)}, u32[]{:S(2)}) collective-permute-start(bf16[256,2048]{1,0:T(8,128)(2,1)} %pad_maximum_fusion.10), channel_id=1, source_target_pairs={{0,24},{2,26},{4,28},{6,30},{8,0},{10,2},{12,4},{14,6},{16,8},{18,... | collective-permute-start | bytes 3145736 | tf_op jit(solution)/shard_map/ppermute | solution.py:358
  634.4 66.8 %collective-permute-start.20 = (bf16[256,2048]{1,0:T(8,128)(2,1)}, bf16[256,2048]{1,0:T(8,128)(2,1)S(1)}, u32[]{:S(2)}, u32[]{:S(2)}) collective-permute-start(bf16[256,2048]{1,0:T(8,128)(2,1)} %pad_maximum_fusion.11), channel_id=1, source_target_pairs={{0,16},{2,18},{4,20},{6,22},{8,24},{10,26},{12,28},{14,30},{16,0},... | collective-permute-start | bytes 3145736 | tf_op jit(solution)/shard_map/ppermute | solution.py:358
  638.9 62.3 %collective-permute-start.15 = (bf16[2,256,1024]{2,1,0:T(8,128)(2,1)}, bf16[2,256,1024]{2,1,0:T(8,128)(2,1)}, u32[]{:S(2)}, u32[]{:S(2)}) collective-permute-start(bf16[2,256,1024]{2,1,0:T(8,128)(2,1)} %get-tuple-element.162), channel_id=1, source_target_pairs={{0,1},{1,0},{2,3},{3,2},{4,5},{5,4},{6,7},{7,6},{8,9},{9,8},{10,11... | collective-permute-start | bytes 3145736 | tf_op jit(solution)/shard_map/ppermute | solution.py:341
  640.4 60.9 %collective-permute-start.16 = (bf16[2,256,1024]{2,1,0:T(8,128)(2,1)S(1)}, bf16[2,256,1024]{2,1,0:T(8,128)(2,1)}, u32[]{:S(2)}, u32[]{:S(2)}) collective-permute-start(bf16[2,256,1024]{2,1,0:T(8,128)(2,1)S(1)} %get-tuple-element.163), channel_id=1, source_target_pairs={{0,4},{2,6},{4,0},{6,2},{8,12},{10,14},{12,8},{14,10},{16,20},{18,... | collective-permute-start | bytes 3145736 | tf_op jit(solution)/shard_map/ppermute | solution.py:337
  644.5 56.8 %collective-permute-start.17 = (bf16[2,256,1024]{2,1,0:T(8,128)(2,1)}, bf16[2,256,1024]{2,1,0:T(8,128)(2,1)}, u32[]{:S(2)}, u32[]{:S(2)}) collective-permute-start(bf16[2,256,1024]{2,1,0:T(8,128)(2,1)} %add_convert_fusion.20), channel_id=1, source_target_pairs={{0,4},{2,6},{4,0},{6,2},{8,12},{10,14},{12,8},{14,10},{16,20},{18,... | collective-permute-start | bytes 3145736 | tf_op jit(solution)/shard_map/ppermute | solution.py:337
  659.6 41.7 %collective-permute-start.18 = (bf16[2,256,1024]{2,1,0:T(8,128)(2,1)}, bf16[2,256,1024]{2,1,0:T(8,128)(2,1)}, u32[]{:S(2)}, u32[]{:S(2)}) collective-permute-start(bf16[2,256,1024]{2,1,0:T(8,128)(2,1)} %add_convert_fusion.19), channel_id=1, source_target_pairs={{0,1},{1,0},{2,3},{3,2},{4,5},{5,4},{6,7},{7,6},{8,9},{9,8},{10,11... | collective-permute-start | bytes 3145736 | tf_op jit(solution)/shard_map/ppermute | solution.py:341
  702.3 78.2 %collective-permute-start.25 = (bf16[12,256,2048]{2,1,0:T(8,128)(2,1)}, bf16[12,256,2048]{2,1,0:T(8,128)(2,1)S(1)}, u32[]{:S(2)}, u32[]{:S(2)}) collective-permute-start(bf16[12,256,2048]{2,1,0:T(8,128)(2,1)} %get-tuple-element.186), channel_id=1, source_target_pairs={{0,2},{2,0},{4,6},{6,4},{8,10},{10,8},{12,14},{14,12},{16,18},{18,... | collective-permute-start | bytes 37748744 | tf_op jit(solution)/shard_map/ppermute | solution.py:333
  702.3 25.4 %collective-permute-start.22 = (bf16[4,256,2048]{2,1,0:T(8,128)(2,1)}, bf16[4,256,2048]{2,1,0:T(8,128)(2,1)S(1)}, u32[]{:S(2)}, u32[]{:S(2)}) collective-permute-start(bf16[4,256,2048]{2,1,0:T(8,128)(2,1)} %get-tuple-element.184), channel_id=1, source_target_pairs={{0,2},{2,0},{4,6},{6,4},{8,10},{10,8},{12,14},{14,12},{16,18},{18,... | collective-permute-start | bytes 12582920 | tf_op jit(solution)/shard_map/ppermute | solution.py:333
  708.8 27.9 %collective-permute-start.21 = (bf16[256,2048]{1,0:T(8,128)(2,1)}, bf16[256,2048]{1,0:T(8,128)(2,1)}, u32[]{:S(2)}, u32[]{:S(2)}) collective-permute-start(bf16[256,2048]{1,0:T(8,128)(2,1)} %pad_maximum_fusion.12), channel_id=1, source_target_pairs={{0,8},{2,10},{4,12},{6,14},{8,16},{10,18},{12,20},{14,22},{16,24},... | collective-permute-start | bytes 3145736 | tf_op jit(solution)/shard_map/ppermute | solution.py:358
  731.5 47.9 %collective-permute-start.23 = (bf16[4,256,1024]{2,1,0:T(8,128)(2,1)}, bf16[4,256,1024]{2,1,0:T(8,128)(2,1)S(1)}, u32[]{:S(2)}, u32[]{:S(2)}) collective-permute-start(bf16[4,256,1024]{2,1,0:T(8,128)(2,1)} %get-tuple-element.248), channel_id=1, source_target_pairs={{0,1},{1,0},{2,3},{3,2},{4,5},{5,4},{6,7},{7,6},{8,9},{9,8},{10,11... | collective-permute-start | bytes 6291464 | tf_op jit(solution)/shard_map/ppermute | solution.py:341
  732.9 47.6 %collective-permute-start.24 = (bf16[4,256,1024]{2,1,0:T(8,128)(2,1)}, bf16[4,256,1024]{2,1,0:T(8,128)(2,1)S(1)}, u32[]{:S(2)}, u32[]{:S(2)}) collective-permute-start(bf16[4,256,1024]{2,1,0:T(8,128)(2,1)} %get-tuple-element.247), channel_id=1, source_target_pairs={{0,4},{2,6},{4,0},{6,2},{8,12},{10,14},{12,8},{14,10},{16,20},{18,... | collective-permute-start | bytes 6291464 | tf_op jit(solution)/shard_map/ppermute | solution.py:337
  781.9 24.2 %collective-permute-start.26 = (bf16[256,2048]{1,0:T(8,128)(2,1)S(1)}, bf16[256,2048]{1,0:T(8,128)(2,1)}, u32[]{:S(2)}, u32[]{:S(2)}) collective-permute-start(bf16[256,2048]{1,0:T(8,128)(2,1)S(1)} %fusion.51), channel_id=1, source_target_pairs={{0,1},{1,0},{2,3},{3,2},{4,5},{5,4},{6,7},{7,6},{8,9},{9,8},{10,11... | collective-permute-start | bytes 3145736 | tf_op jit(solution)/shard_map/ppermute | solution.py:341
  816.8 378.7 %reduce-scatter.3.cloned.1.call-start = ((), (), s32[]{:S(2)}) async-start(), calls=%async_computation.7 | async-start | bytes 13369344 | tf_op jit(solution)/shard_map/reduce_scatter | solution.py:1040
  816.8 45.9 %collective-permute-start.27 = (bf16[4,256,1024]{2,1,0:T(8,128)(2,1)}, bf16[4,256,1024]{2,1,0:T(8,128)(2,1)S(1)}, u32[]{:S(2)}, u32[]{:S(2)}) collective-permute-start(bf16[4,256,1024]{2,1,0:T(8,128)(2,1)} %pad_maximum_fusion.5), channel_id=1, source_target_pairs={{0,1},{1,0},{2,3},{3,2},{4,5},{5,4},{6,7},{7,6},{8,9},{9,8},{10,11... | collective-permute-start | bytes 6291464 | tf_op jit(solution)/shard_map/ppermute | solution.py:341
  818.1 57.1 %collective-permute-start.28 = (bf16[4,256,1024]{2,1,0:T(8,128)(2,1)}, bf16[4,256,1024]{2,1,0:T(8,128)(2,1)S(1)}, u32[]{:S(2)}, u32[]{:S(2)}) collective-permute-start(bf16[4,256,1024]{2,1,0:T(8,128)(2,1)} %pad_maximum_fusion.4), channel_id=1, source_target_pairs={{0,4},{2,6},{4,0},{6,2},{8,12},{10,14},{12,8},{14,10},{16,20},{18,... | collective-permute-start | bytes 6291464 | tf_op jit(solution)/shard_map/ppermute | solution.py:337
  914.5 44.5 %collective-permute-start.29 = (bf16[4,256,1024]{2,1,0:T(8,128)(2,1)}, bf16[4,256,1024]{2,1,0:T(8,128)(2,1)}, u32[]{:S(2)}, u32[]{:S(2)}) collective-permute-start(bf16[4,256,1024]{2,1,0:T(8,128)(2,1)} %add_convert_fusion.1), channel_id=1, source_target_pairs={{0,4},{2,6},{4,0},{6,2},{8,12},{10,14},{12,8},{14,10},{16,20},{18,... | collective-permute-start | bytes 6291464 | tf_op jit(solution)/shard_map/ppermute | solution.py:337
  916.0 43.7 %collective-permute-start.30 = (bf16[4,256,1024]{2,1,0:T(8,128)(2,1)}, bf16[4,256,1024]{2,1,0:T(8,128)(2,1)}, u32[]{:S(2)}, u32[]{:S(2)}) collective-permute-start(bf16[4,256,1024]{2,1,0:T(8,128)(2,1)} %add_convert_fusion), channel_id=1, source_target_pairs={{0,1},{1,0},{2,3},{3,2},{4,5},{5,4},{6,7},{7,6},{8,9},{9,8},{10,11... | collective-permute-start | bytes 6291464 | tf_op jit(solution)/shard_map/ppermute | solution.py:341
  916.9 14.4 %collective-permute-start.37 = (f32[8,33,128]{2,0,1:T(8,128)S(1)}, f32[8,33,128]{2,0,1:T(8,128)S(1)}, u32[]{:S(2)}, u32[]{:S(2)}) collective-permute-start(f32[8,33,128]{2,0,1:T(8,128)S(1)} %dynamic-slice_bitcast_fusion), channel_id=1, source_target_pairs={{0,16},{2,18},{4,20},{6,22},{8,24},{10,26},{12,28},{14,30},{16,0},... | collective-permute-start | bytes 405512 | tf_op jit(solution)/shard_map/ppermute | solution.py:406
  935.7 50.9 %collective-permute-start.39 = (f32[2,33,128]{2,0,1:T(2,128)S(1)}, f32[2,33,128]{2,0,1:T(2,128)S(1)}, u32[]{:S(2)}, u32[]{:S(2)}) collective-permute-start(f32[2,33,128]{2,0,1:T(2,128)S(1)} %dynamic-slice_bitcast_fusion.2), channel_id=1, source_target_pairs={{0,4},{2,6},{4,0},{6,2},{8,12},{10,14},{12,8},{14,10},{16,20},{18,... | collective-permute-start | bytes 101384 | tf_op jit(solution)/shard_map/ppermute | solution.py:406
  985.5 22.0 %collective-permute-start.34 = (bf16[256,2048]{1,0:T(8,128)(2,1)}, bf16[256,2048]{1,0:T(8,128)(2,1)}, u32[]{:S(2)}, u32[]{:S(2)}) collective-permute-start(bf16[256,2048]{1,0:T(8,128)(2,1)} %select_convert_fusion), channel_id=1, source_target_pairs={{0,1},{1,0},{2,3},{3,2},{4,5},{5,4},{6,7},{7,6},{8,9},{9,8},{10,11... | collective-permute-start | bytes 3145736 | tf_op jit(solution)/shard_map/ppermute | solution.py:341
  988.0 18.8 %collective-permute-start.41 = (f32[33,128]{1,0:T(8,128)S(1)}, f32[33,128]{1,0:T(8,128)S(1)}, u32[]{:S(2)}, u32[]{:S(2)}) collective-permute-start(f32[33,128]{1,0:T(8,128)S(1)} %bitcast.178), channel_id=1, source_target_pairs={{0,1},{1,0},{2,3},{3,2},{4,5},{5,4},{6,7},{7,6},{8,9},{9,8},{10,11... | collective-permute-start | bytes 50696 | tf_op jit(solution)/shard_map/ppermute | solution.py:341
  988.9 56.1 %collective-permute-start.31 = (bf16[256,2048]{1,0:T(8,128)(2,1)}, bf16[256,2048]{1,0:T(8,128)(2,1)}, u32[]{:S(2)}, u32[]{:S(2)}) collective-permute-start(bf16[256,2048]{1,0:T(8,128)(2,1)} %pad_maximum_fusion.14), channel_id=1, source_target_pairs={{0,24},{2,26},{4,28},{6,30},{8,0},{10,2},{12,4},{14,6},{16,8},{18,... | collective-permute-start | bytes 3145736 | tf_op jit(solution)/shard_map/ppermute | solution.py:358
  993.3 143.7 %collective-permute-start.32 = (bf16[256,2048]{1,0:T(8,128)(2,1)}, bf16[256,2048]{1,0:T(8,128)(2,1)}, u32[]{:S(2)}, u32[]{:S(2)}) collective-permute-start(bf16[256,2048]{1,0:T(8,128)(2,1)} %pad_maximum_fusion.15), channel_id=1, source_target_pairs={{0,16},{2,18},{4,20},{6,22},{8,24},{10,26},{12,28},{14,30},{16,0},... | collective-permute-start | bytes 3145736 | tf_op jit(solution)/shard_map/ppermute | solution.py:358
  993.3 143.7 %collective-permute-start.33 = (bf16[256,2048]{1,0:T(8,128)(2,1)}, bf16[256,2048]{1,0:T(8,128)(2,1)}, u32[]{:S(2)}, u32[]{:S(2)}) collective-permute-start(bf16[256,2048]{1,0:T(8,128)(2,1)} %pad_maximum_fusion.16), channel_id=1, source_target_pairs={{0,8},{2,10},{4,12},{6,14},{8,16},{10,18},{12,20},{14,22},{16,24},... | collective-permute-start | bytes 3145736 | tf_op jit(solution)/shard_map/ppermute | solution.py:358
  1011.9 125.1 %collective-permute-start.42 = (f32[18,128]{1,0:T(8,128)S(1)}, f32[18,128]{1,0:T(8,128)S(1)}, u32[]{:S(2)}, u32[]{:S(2)}) collective-permute-start(f32[18,128]{1,0:T(8,128)S(1)} %pad_maximum_fusion.19), channel_id=1, source_target_pairs={{0,2},{2,0},{4,6},{6,4},{8,10},{10,8},{12,14},{14,12},{16,18},{18,... | collective-permute-start | bytes 27656 | tf_op jit(solution)/shard_map/ppermute | solution.py:390
  1137.1 37.0 %collective-permute-start.43 = (f32[18,128]{1,0:T(8,128)S(1)}, f32[18,128]{1,0:T(8,128)S(1)}, u32[]{:S(2)}, u32[]{:S(2)}) collective-permute-start(f32[18,128]{1,0:T(8,128)S(1)} %fusion.48), channel_id=1, source_target_pairs={{0,1},{1,0},{2,3},{3,2},{4,5},{5,4},{6,7},{7,6},{8,9},{9,8},{10,11... | collective-permute-start | bytes 27656 | tf_op jit(solution)/shard_map/ppermute | solution.py:341
  1174.1 17.2 %collective-permute-start.44 = (f32[18,128]{1,0:T(8,128)S(1)}, f32[18,128]{1,0:T(8,128)S(1)}, u32[]{:S(2)}, u32[]{:S(2)}) collective-permute-start(f32[18,128]{1,0:T(8,128)S(1)} %add.671), channel_id=1, source_target_pairs={{0,4},{2,6},{4,0},{6,2},{8,12},{10,14},{12,8},{14,10},{16,20},{18,... | collective-permute-start | bytes 27656 | tf_op jit(solution)/shard_map/ppermute | solution.py:394
  1195.0 15.1 %collective-permute-start.36 = (bf16[128,2048]{1,0:T(8,128)(2,1)}, bf16[128,2048]{1,0:T(8,128)(2,1)S(1)}, u32[]{:S(2)}, u32[]{:S(2)}) collective-permute-start(bf16[128,2048]{1,0:T(8,128)(2,1)} %reduce-scatter.5.cloned.1.call-done), channel_id=1, source_target_pairs={{0,1},{1,0},{2,3},{3,2},{4,5},{5,4},{6,7},{7,6},{8,9},{9,8},{10,11... | collective-permute-start | bytes 1572872 | tf_op jit(solution)/shard_map/ppermute | solution.py:341
  1195.4 28.9 %collective-permute-start.35 = (bf16[128,3072]{1,0:T(8,128)(2,1)}, bf16[128,3072]{1,0:T(8,128)(2,1)S(1)}, u32[]{:S(2)}, u32[]{:S(2)}) collective-permute-start(bf16[128,3072]{1,0:T(8,128)(2,1)} %reduce-scatter.3.cloned.1.call-done.mine_ref), channel_id=1, source_target_pairs={{0,1},{1,0},{2,3},{3,2},{4,5},{5,4},{6,7},{7,6},{8,9},{9,8},{10,11... | collective-permute-start | bytes 2359304 | tf_op jit(solution)/shard_map/ppermute | solution.py:341
  (80 other events, 1652.5 us)
Sparse Core Ops, SparseCore 0:
  10.4 112.8 all-gather.3
  125.4 134.2 all-gather.7
  261.9 168.0 all-gather.5
  816.9 115.9 reduce-scatter.4
  936.8 203.3 reduce-scatter.2

commit v8 on v7

--- a/solution.py
+++ b/solution.py
@@ -973,10 +973,7 @@
     )
     entries.update(joined(parts[1], [item[cut:] for item in back_own], got))
     out_far = over_core(*out_far)
-    out_far = [
-        swap_ctx(pick_sum(out_far, 0, lines, 0)),
-        swap_side(pick_sum(out_far, 0, lines, 1)),
-    ]
+    out_far = [pick_sum(out_far, 0, lines, 0), swap_side(pick_sum(out_far, 0, lines, 1))]
     out_rest = over_core(*out_rest)
     for p in parts[1][:-1]:
         arrived[p] = line_shift(entries[p], lines - p)
@@ -991,36 +988,38 @@
     grad_mixed_part, grad_moe_gain = rms_back(mixed, moe_all, grad_mid)
     grad_mixed = cotangent.astype(full) + grad_mixed_part
 
-    low_mixed, (out_far, out_rest) = hold(grad_mixed.astype(low), (out_far, out_rest))
+    low_mixed, (out_far[0], out_rest) = hold(grad_mixed.astype(low), (out_far[0], out_rest))
     grad_branch = sequence(low_mixed)
     out_sums = [
         jnp.concatenate([one, two])
         for one, two in zip(mixed_sums(out_rest), mixed_sums(out_rest, 2 * cut + lines))
     ]
     out_own = [pick_sum(out_rest, 2 * cut, 2 * cut + lines, column) for column in range(2)]
-    (out_sums, out_own), grad_branch = hold((out_sums, out_own), grad_branch)
+    (out_far[0], out_sums, out_own), grad_branch = hold((out_far[0], out_sums, out_own), grad_branch)
     side_one, side_two, ctx_one, ctx_two = out_sums
+    out_far[0] = swap_ctx(out_far[0])
+    grad_attended = mul(grad_branch, out_all, rhs_turned).astype(low)
+    grad_attended, out_far = hold(grad_attended, out_far)
     got = [
         swap_ctx(ctx_one),
         swap_side(side_two),
-        add_low(side_one, out_far[0]),
-        add_low(ctx_two, out_far[1]),
+        swap_side(add_low(side_one, out_far[0])),
+        swap_ctx(add_low(ctx_two, out_far[1])),
     ]
-    grad_attended = mul(grad_branch, out_all, rhs_turned).astype(low)
-    grad_attended, got = hold(grad_attended, got)
-    got[2], got[3] = swap_side(got[2]), swap_ctx(got[3])
     grad_out_part = mul(attended, grad_branch, lhs_turned).astype(low)
     grad_q, grad_k, grad_v, gain_q_part, gain_k_part = attend_grad(
         projected, roped_q, roped_k, values_low, grad_attended, cosine, sine, gain_q, gain_k, kv_heads, group
     )
     grad_projected = jnp.concatenate([grad_q, grad_k, grad_v], axis=1)
+    grad_projected, (got[0], got[1]) = hold(grad_projected, (got[0], got[1]))
     grad_qkv_part = mul(low_in, grad_projected, lhs_turned).astype(low)
     grad_projected, got = hold(grad_projected, got)
     entries = joined(places, out_own, got)
-    grad_projected, entries = hold(grad_projected, entries)
+    grad_projected, entries, rows, grad_pair, hidden, grad_rows = lax.optimization_barrier(
+        (grad_projected, entries, rows, grad_pair, hidden, grad_rows)
+    )
     arrived = {p: line_shift(entries[p], lines - p) for p in places[:-1]}
     grad_normed_part = mul(grad_projected, qkv_all, rhs_turned)
-    (rows, grad_pair, hidden, grad_rows), arrived = hold((rows, grad_pair, hidden, grad_rows), arrived)
     grad_gate_up = mul(rows, grad_pair, lhs_turned)[None]
     grad_down = mul(hidden, grad_rows, lhs_turned)[None]
     output = (mixed + line_total(entries[0], arrived)).astype(low)

time: 1240 us -> 1170 us (0.944)
  waiting for transfers between devices: 660 us -> 578 us
    ppermute x6, waiting for transfers between devices: 140 us -> 38.9 us  [line_shift(): lax.ppermute(values, 'fsdp', [(i, (i + 4 * step) % fsdp) for i in range(f...]
    ppermute x8, waiting for transfers between devices: 42.5 us -> 125 us  [swap_side(): return lax.ppermute(values, 'fsdp', side_pairs(lax.axis_size('fsdp')))]
    ppermute x19, waiting for transfers between devices: 331 us -> 259 us  [swap_ctx(): return lax.ppermute(values, 'ctx', [(0, 1), (1, 0)])]
    ppermute x3, waiting for transfers between devices: 3.68 us -> 37.1 us  [sum_all(): lax.ppermute(values, 'fsdp', [(i, i ^ step) for i in range(fsdp)])]
    ppermute x6, waiting for transfers between devices: 24.5 us -> 7.13 us  [swap_core(): return lax.ppermute(values, 'fsdp', core_pairs(lax.axis_size('fsdp')))]
  transfers between devices with their start and end apart: 53 -> 53, of which waited for: 31 -> 26; matrix products, arithmetic and copies ran while one was open for 18% -> 19% of each run, Pallas kernels for 15% -> 16%
where the time goes in v8:
time: 1170 us; the launch traced here: 1160 us
  waiting for transfers between devices  578 us (49%)
  Pallas kernels  224 us (19%)
  matrix products  110 us (9%)
  other arithmetic  108 us (9%)
  starting transfers between devices  56.5 us (5%)
  blocking collectives  35.6 us (3%)
  local copies, waits for them, and re-layouts  29.4 us (3%)
  between operations  15.5 us (1%)
    ppermute x19, waiting for transfers between devices, swap_ctx(): return lax.ppermute(values, 'ctx', [(0, 1), (1, 0)])  259 us
    pallas_call x4, Pallas kernels, run_expert(): pl.pallas_call(expert_kernel, grid_spec=grid_spec, out_shape=[shape((step...  135 us
    ppermute x8, waiting for transfers between devices, swap_side(): return lax.ppermute(values, 'fsdp', side_pairs(lax.axis_size('fsdp')))  125 us
    dot_general x11, matrix products, mul(): return lax.dot_general(left, right, dims, preferred_element_type=full)  110 us
    convert_element_type x19, other arithmetic, add_low(): return (one.astype(full) + two.astype(full)).astype(low)  68.3 us
    all_gather x1, waiting for transfers between devices, body_gathered(): weights_all = lax.all_gather(weights_local, 'fsdp', axis=0, tiled=True)  65.6 us
    pallas_call x2, Pallas kernels, run_result(): pl.pallas_call(result_kernel, grid_spec=pltpu.PrefetchScalarGridSpec(num_...  40.2 us
    ppermute x6, waiting for transfers between devices, line_shift(): lax.ppermute(values, 'fsdp', [(i, (i + 4 * step) % fsdp) for i in range(f...  38.9 us
  transfers between devices with their start and end apart: 53, of which 26 were waited for; matrix products, arithmetic and copies ran while one was open for 19% of the time, Pallas kernels for 16%

profile of v8, /device:TPU:0, one launch (start us, length us, event | category | flops | bytes accessed | tf_op | source)
XLA Modules:
  0.0 1157.1 jit_solution(9955332202167490012)
XLA Ops:
  13.4 13.3 %collective-permute-done.3 = bf16[256,1152]{1,0:T(8,128)(2,1)S(1)} collective-permute-done((bf16[256,1152]{1,0:T(8,128)(2,1)S(1)}, bf16[256,1152]{1,0:T(8,128)(2,1)S(1)}, u32[]{:S(2)}, u32[]{:S(2)}) %collective-permute-start.3) | collective-permute-done | bytes 589856 | tf_op jit(solution)/shard_map/ppermute | solution.py:341
  31.2 22.9 %all_gather.12 = bf16[2048,34]{0,1:T(8,128)(2,1)S(1)} all-gather(bf16[128,34]{0,1:T(8,128)(2,1)S(1)} %pad_maximum_fusion.21), channel_id=1, replica_groups=mesh['fsdp'=16,'ctx'=2] {'fsdp'}, dimensions={0}, use_global_device_ids=true | all-gather | bytes 147968 | tf_op jit(solution)/shard_map/all_gather | solution.py:835
  57.6 65.6 %all-gather.4.cloned.1.call-done = bf16[2048,5120]{1,0:T(8,128)(2,1)} async-done(((bf16[128,5120]{1,0:T(8,128)(2,1)}), bf16[2048,5120]{1,0:T(8,128)(2,1)}) %all-gather.4.cloned.1.call-update) | async-done | bytes 20971536 | tf_op jit(solution)/shard_map/all_gather | solution.py:836
  123.2 11.5 fusion.2.q_ref.k_ref.v_ref
  134.7 18.2 %attend.1 = (bf16[512,2048]{1,0:T(8,128)(2,1)S(1)}, bf16[512,2048]{1,0:T(8,128)(2,1)S(1)}, bf16[512,512]{1,0:T(8,128)(2,1)S(1)}, bf16[512,512]{1,0:T(8,128)(2,1)S(1)}) custom-call(f32[512,3072]{1,0:T(8,128)} %fusion.2.q_ref.k_ref.v_ref, f32[512,3072]{1,0:T(8,128)} %fusion.2.q_ref.k_ref.v_ref, f32[512,3072]{1,0:T(8,128)} %fusion.2.q_ref.k_ref.v_ref, ...), custom_call_target="tpu_custom_call" | custom-call | flops 2147483648 | bytes 9437184 | tf_op jit(solution)/shard_map/attend/pallas_call | solution.py:521
  153.0 8.4 fusion.6
  163.5 23.8 %collective-permute-done.1 = bf16[256,2048]{1,0:T(8,128)(2,1)S(1)} collective-permute-done((bf16[256,2048]{1,0:T(8,128)(2,1)S(1)}, bf16[256,2048]{1,0:T(8,128)(2,1)S(1)}, u32[]{:S(2)}, u32[]{:S(2)}) %collective-permute-start.1) | collective-permute-done | bytes 1048608 | tf_op jit(solution)/shard_map/ppermute | solution.py:341
  191.7 23.1 %collective-permute-done.2 = bf16[256,2048]{1,0:T(8,128)(2,1)S(1)} collective-permute-done((bf16[256,2048]{1,0:T(8,128)(2,1)S(1)}, bf16[256,2048]{1,0:T(8,128)(2,1)S(1)}, u32[]{:S(2)}, u32[]{:S(2)}) %collective-permute-start.2) | collective-permute-done | bytes 1048608 | tf_op jit(solution)/shard_map/ppermute | solution.py:341
  218.4 12.8 %all_to_all.24 = f32[32,1,256]{2,1,0:T(1,128)S(1)} all-to-all(f32[32,1,256]{2,1,0:T(1,128)S(1)} %copy.60), channel_id=1, replica_groups=mesh['fsdp'=16,'ctx'=2] {'fsdp','ctx'}, dimensions={0} | all-to-all | bytes 65536 | tf_op jit(solution)/shard_map/all_to_all | solution.py:873
  231.1 28.6 %all-gather.8.cloned.1.call-done = bf16[4096,3200]{1,0:T(8,128)(2,1)} async-done(((bf16[256,3200]{1,0:T(8,128)(2,1)}), bf16[4096,3200]{1,0:T(8,128)(2,1)}) %all-gather.8.cloned.1.call-update) | async-done | bytes 26214416 | tf_op jit(solution)/shard_map/all_gather | solution.py:843
  259.7 6.9 slice.403
  269.4 157.7 %collective-permute-done.4.far_ref = bf16[8,2,256,896]{3,2,1,0:T(8,128)(2,1)} collective-permute-done((bf16[8,2,256,896]{3,2,1,0:T(8,128)(2,1)}, bf16[8,2,256,896]{3,2,1,0:T(8,128)(2,1)}, u32[]{:S(2)}, u32[]{:S(2)}) %collective-permute-start.4) | collective-permute-done | bytes 7340064 | tf_op jit(solution)/shard_map/ppermute | solution.py:341
  429.9 33.1 %experts.4 = (bf16[4,256,2048]{2,1,0:T(8,128)(2,1)}, bf16[4,256,2048]{2,1,0:T(8,128)(2,1)}, f32[8,2,2,1,256]{4,3,2,1,0:T(1,128)}, bf16[4096,2048]{1,0:T(8,128)(2...) custom-call(s32[1]{0:T(128)} %bitcast.6.core_ref, s32[16]{0:T(128)} %stack.35.order, ...), custom_call_target="tpu_custom_call" | custom-call | flops 19327352832 | bytes 38273024 | tf_op jit(solution)/shard_map/experts/pallas_call | solution.py:670
  463.3 7.1 collective-permute-done.5
  470.5 4.8 add_convert_fusion.8
  478.5 34.2 %experts.5 = (bf16[4,256,2048]{2,1,0:T(8,128)(2,1)}, bf16[4,256,2048]{2,1,0:T(8,128)(2,1)}, f32[8,2,2,1,256]{4,3,2,1,0:T(1,128)}, bf16[4096,2048]{1,0:T(8,128)(2...) custom-call(s32[1]{0:T(128)} %bitcast.6.core_ref, ...), custom_call_target="tpu_custom_call", output_to_operand_aliasing={{2}: (8, {}), {3}: (9, {}), {4}: (10, {}), {5}: (11, {}), {... | custom-call | flops 19327352832 | bytes 38273024 | tf_op jit(solution)/shard_map/experts/pallas_call | solution.py:670
  512.7 10.7 collective-permute-done.7
  525.9 33.7 %experts.6 = (bf16[4,256,2048]{2,1,0:T(8,128)(2,1)}, bf16[4,256,2048]{2,1,0:T(8,128)(2,1)}, f32[8,2,2,1,256]{4,3,2,1,0:T(1,128)}, bf16[4096,2048]{1,0:T(8,128)(2...) custom-call(s32[1]{0:T(128)} %bitcast.6.core_ref, ...), custom_call_target="tpu_custom_call", output_to_operand_aliasing={{2}: (8, {}), {3}: (9, {}), {4}: (10, {}), {5}: (11, {}), {... | custom-call | flops 19327352832 | bytes 38273024 | tf_op jit(solution)/shard_map/experts/pallas_call | solution.py:670
  573.1 33.7 %experts.7 = (bf16[4,256,2048]{2,1,0:T(8,128)(2,1)}, bf16[4,256,2048]{2,1,0:T(8,128)(2,1)}, f32[8,2,2,1,256]{4,3,2,1,0:T(1,128)}, bf16[4096,2048]{1,0:T(8,128)(2...) custom-call(s32[1]{0:T(128)} %bitcast.6.core_ref, ...), custom_call_target="tpu_custom_call", output_to_operand_aliasing={{2}: (8, {}), {3}: (9, {}), {4}: (10, {}), {5}: (11, {}), {... | custom-call | flops 19327352832 | bytes 38273024 | tf_op jit(solution)/shard_map/experts/pallas_call | solution.py:670
  606.8 5.8 collective-permute-done.12
  613.4 4.7 all-to-all-start.1
  618.2 5.8 add_convert_fusion.7
  647.8 11.9 %results.2 = (bf16[4,256,2048]{2,1,0:T(8,128)(2,1)}, bf16[4,256,2048]{2,1,0:T(8,128)(2,1)}) custom-call(s32[1]{0:T(128)} %bitcast.6.core_ref, s32[16]{0:T(128)} %stack.35.order, bf16[4096,768]{1,0:T(8,128)(2,1)} %get-tuple-element.223.z_ref, f32[8,2,2,1,256]{4,3,2,1,0:T(1,128)} %reshape.272.w_ref, bf16[768,2048]{1,0:T(8,128)(2,1)} %bitcast.154), custom_call_target="tpu_custom_call" | custom-call | flops 4294967296 | bytes 13107200 | tf_op jit(solution)/shard_map/results/pallas_call | solution.py:701
  660.2 28.3 %results.3 = (bf16[12,256,2048]{2,1,0:T(8,128)(2,1)}, bf16[12,256,2048]{2,1,0:T(8,128)(2,1)}) custom-call(s32[1]{0:T(128)} %bitcast.6.core_ref, s32[48]{0:T(128)} %stack.44.order, bf16[4096,768]{1,0:T(8,128)(2,1)} %get-tuple-element.223.z_ref, f32[8,2,2,1,256]{4,3,2,1,0:T(1,128)} %reshape.272.w_ref, bf16[768,2048]{1,0:T(8,128)(2,1)} %bitcast.155), custom_call_target="tpu_custom_call" | custom-call | flops 12884901888 | bytes 33030144 | tf_op jit(solution)/shard_map/results/pallas_call | solution.py:701
  688.5 12.9 %collective-permute-done.20 = bf16[256,2048]{1,0:T(8,128)(2,1)S(1)} collective-permute-done((bf16[256,2048]{1,0:T(8,128)(2,1)}, bf16[256,2048]{1,0:T(8,128)(2,1)S(1)}, u32[]{:S(2)}, u32[]{:S(2)}) %collective-permute-start.20) | collective-permute-done | bytes 1048608 | tf_op jit(solution)/shard_map/ppermute | solution.py:358
  709.4 26.0 %collective-permute-done.21 = bf16[256,2048]{1,0:T(8,128)(2,1)S(1)} collective-permute-done((bf16[256,2048]{1,0:T(8,128)(2,1)S(1)}, bf16[256,2048]{1,0:T(8,128)(2,1)S(1)}, u32[]{:S(2)}, u32[]{:S(2)}) %collective-permute-start.21) | collective-permute-done | bytes 1048608 | tf_op jit(solution)/shard_map/ppermute | solution.py:358
  740.0 6.0 add_convert_fusion.2
  747.5 5.2 add_convert_fusion.12
  764.5 6.1 collective-permute-done.24
  774.6 6.8 convolution_convert_fusion.1
  785.5 10.6 fusion.11.go_ref
  796.2 45.4 %collective-permute-done.26 = bf16[4,256,1024]{2,1,0:T(8,128)(2,1)S(1)} collective-permute-done((bf16[4,256,1024]{2,1,0:T(8,128)(2,1)}, bf16[4,256,1024]{2,1,0:T(8,128)(2,1)S(1)}, u32[]{:S(2)}, u32[]{:S(2)}) %collective-permute-start.26) | collective-permute-done | bytes 2097184 | tf_op jit(solution)/shard_map/ppermute | solution.py:337
  843.6 25.2 %attend_grad.1 = (bf16[512,2048]{1,0:T(8,128)(2,1)S(1)}, bf16[512,512]{1,0:T(8,128)(2,1)S(1)}, bf16[512,512]{1,0:T(8,128)(2,1)S(1)}, f32[4,1,128]{2,1,0:T(1,128)S(1)}, f32[4,1,128]{2,1,0:T(1,128)S(1)}) custom-call(f32[512,3072]{1,0:T(8,128)} %fusion.2.q_ref.k_ref.v_ref, f32[512,3072]{1,0:T(8,128)} %fusion.2.q_ref.k_ref.v_ref, bf16[512,2048]{1,0:T(8,128)(2,1)} %copy-done, ...), custom_call_target="tpu_custom_call" | custom-call | flops 5368709120 | bytes 15728640 | tf_op jit(solution)/shard_map/attend_grad/pallas_call | solution.py:545
  869.1 4.9 collective-permute-done.27
  874.1 26.9 %collective-permute-done.28 = bf16[4,256,1024]{2,1,0:T(8,128)(2,1)} collective-permute-done((bf16[4,256,1024]{2,1,0:T(8,128)(2,1)}, bf16[4,256,1024]{2,1,0:T(8,128)(2,1)}, u32[]{:S(2)}, u32[]{:S(2)}) %collective-permute-start.28) | collective-permute-done | bytes 2097184 | tf_op jit(solution)/shard_map/ppermute | solution.py:337
  901.0 10.2 convolution_convert_fusion
  911.3 4.7 add_convert_fusion.1
  921.8 6.0 collective-permute-done.37
  932.8 45.8 %collective-permute-done.29 = bf16[4,256,1024]{2,1,0:T(8,128)(2,1)} collective-permute-done((bf16[4,256,1024]{2,1,0:T(8,128)(2,1)}, bf16[4,256,1024]{2,1,0:T(8,128)(2,1)}, u32[]{:S(2)}, u32[]{:S(2)}) %collective-permute-start.29) | collective-permute-done | bytes 2097184 | tf_op jit(solution)/shard_map/ppermute | solution.py:337
  978.7 4.6 fusion.39
  991.9 9.7 fusion
  1008.4 13.1 %collective-permute-done.41 = f32[33,128]{1,0:T(8,128)S(1)} collective-permute-done((f32[33,128]{1,0:T(8,128)S(1)}, f32[33,128]{1,0:T(8,128)S(1)}, u32[]{:S(2)}, u32[]{:S(2)}) %collective-permute-start.41) | collective-permute-done | bytes 16928 | tf_op jit(solution)/shard_map/ppermute | solution.py:341
  1032.3 35.5 %convolution_bitcast_fusion = f32[1,2048,1536]{2,1,0:T(8,128)} fusion(bf16[4096,2048]{1,0:T(8,128)(2,1)} %get-tuple-element.221, bf16[4096,1536]{1,0:T(8,128)(2,1)} %get-tuple-element.222), kind=kOutput, calls=%fused_computation.5 | convolution fusion | flops 25769803776 | bytes 41943040 | tf_op jit(solution)/shard_map/dot_general | solution.py:321
  1070.3 15.7 %convolution_bitcast_fusion.1 = f32[1,768,2048]{2,1,0:T(8,128)} fusion(bf16[4096,768]{1,0:T(8,128)(2,1)S(1)} %bitcast.149, bf16[4096,2048]{1,0:T(8,128)(2,1)S(1)} %bitcast.143), kind=kOutput, calls=%fused_computation.26 | convolution fusion | flops 12884901888 | bytes 29360128 | tf_op jit(solution)/shard_map/dot_general | solution.py:321
  1086.6 24.4 %collective-permute-done.45 = f32[18,128]{1,0:T(8,128)S(1)} collective-permute-done((f32[18,128]{1,0:T(8,128)S(1)}, f32[18,128]{1,0:T(8,128)S(1)}, u32[]{:S(2)}, u32[]{:S(2)}) %collective-permute-start.45) | collective-permute-done | bytes 9248 | tf_op jit(solution)/shard_map/ppermute | solution.py:394
  1117.5 6.5 fusion.20
  1124.0 12.7 %collective-permute-done.46 = f32[18,128]{1,0:T(8,128)S(1)} collective-permute-done((f32[18,128]{1,0:T(8,128)S(1)}, f32[18,128]{1,0:T(8,128)S(1)}, u32[]{:S(2)}, u32[]{:S(2)}) %collective-permute-start.46) | collective-permute-done | bytes 9248 | tf_op jit(solution)/shard_map/ppermute | solution.py:394
  1139.5 6.6 collective-permute-done.35.other_ref
  (340 shorter events, 163.6 us)
Async XLA Ops:
  7.2 116.1 %all-gather.4.cloned.1.call-start = ((), (), s32[]{:S(2)}) async-start(), calls=%async_computation.4 | async-start | bytes 22282240 | tf_op jit(solution)/shard_map/all_gather | solution.py:836
  10.2 249.5 %all-gather.8.cloned.1.call-start = ((), (), s32[]{:S(2)}) async-start(), calls=%async_computation.6 | async-start | bytes 27852800 | tf_op jit(solution)/shard_map/all_gather | solution.py:843
  10.4 16.3 %collective-permute-start.3 = (bf16[256,1152]{1,0:T(8,128)(2,1)S(1)}, bf16[256,1152]{1,0:T(8,128)(2,1)S(1)}, u32[]{:S(2)}, u32[]{:S(2)}) collective-permute-start(bf16[256,1152]{1,0:T(8,128)(2,1)S(1)} %slice.401), channel_id=1, source_target_pairs={{0,1},{1,0},{2,3},{3,2},{4,5},{5,4},{6,7},{7,6},{8,9},{9,8},{10,11... | collective-permute-start | bytes 1769480 | tf_op jit(solution)/shard_map/ppermute | solution.py:341
  28.1 401.9 %all-gather.6.cloned.1.call-start = ((), (), s32[]{:S(2)}) async-start(), calls=%async_computation.5 | async-start | bytes 35651584 | tf_op jit(solution)/shard_map/all_gather | solution.py:864
  28.1 26.4 %collective-permute-start = (bf16[256,2048]{1,0:T(8,128)(2,1)S(1)}, bf16[256,2048]{1,0:T(8,128)(2,1)}, u32[]{:S(2)}, u32[]{:S(2)}) collective-permute-start(bf16[256,2048]{1,0:T(8,128)(2,1)S(1)} %copy-done.6), channel_id=1, source_target_pairs={{0,1},{1,0},{2,3},{3,2},{4,5},{5,4},{6,7},{7,6},{8,9},{9,8},{10,11... | collective-permute-start | bytes 3145736 | tf_op jit(solution)/shard_map/ppermute | solution.py:341
  162.0 25.4 %collective-permute-start.1 = (bf16[256,2048]{1,0:T(8,128)(2,1)S(1)}, bf16[256,2048]{1,0:T(8,128)(2,1)S(1)}, u32[]{:S(2)}, u32[]{:S(2)}) collective-permute-start(bf16[256,2048]{1,0:T(8,128)(2,1)S(1)} %select_convert_fusion.1), channel_id=1, source_target_pairs={{0,1},{1,0},{2,3},{3,2},{4,5},{5,4},{6,7},{7,6},{8,9},{9,8},{10,11... | collective-permute-start | bytes 3145736 | tf_op jit(solution)/shard_map/ppermute | solution.py:341
  190.2 24.7 %collective-permute-start.2 = (bf16[256,2048]{1,0:T(8,128)(2,1)S(1)}, bf16[256,2048]{1,0:T(8,128)(2,1)S(1)}, u32[]{:S(2)}, u32[]{:S(2)}) collective-permute-start(bf16[256,2048]{1,0:T(8,128)(2,1)S(1)} %multiply_convert_fusion), channel_id=1, source_target_pairs={{0,1},{1,0},{2,3},{3,2},{4,5},{5,4},{6,7},{7,6},{8,9},{9,8},{10,11... | collective-permute-start | bytes 3145736 | tf_op jit(solution)/shard_map/ppermute | solution.py:341
  266.6 160.5 %collective-permute-start.4 = (bf16[8,2,256,896]{3,2,1,0:T(8,128)(2,1)}, bf16[8,2,256,896]{3,2,1,0:T(8,128)(2,1)}, u32[]{:S(2)}, u32[]{:S(2)}) collective-permute-start(bf16[8,2,256,896]{3,2,1,0:T(8,128)(2,1)} %slice.403), channel_id=1, source_target_pairs={{0,1},{1,0},{2,3},{3,2},{4,5},{5,4},{6,7},{7,6},{8,9},{9,8},{10,11... | collective-permute-start | bytes 22020104 | tf_op jit(solution)/shard_map/ppermute | solution.py:341
  475.3 48.1 %collective-permute-start.7 = (bf16[4,256,1024]{2,1,0:T(8,128)(2,1)}, bf16[4,256,1024]{2,1,0:T(8,128)(2,1)}, u32[]{:S(2)}, u32[]{:S(2)}) collective-permute-start(bf16[4,256,1024]{2,1,0:T(8,128)(2,1)} %get-tuple-element.141), channel_id=1, source_target_pairs={{0,1},{1,0},{2,3},{3,2},{4,5},{5,4},{6,7},{7,6},{8,9},{9,8},{10,11... | collective-permute-start | bytes 6291464 | tf_op jit(solution)/shard_map/ppermute | solution.py:341
  476.7 47.8 %collective-permute-start.8 = (bf16[4,256,1024]{2,1,0:T(8,128)(2,1)}, bf16[4,256,1024]{2,1,0:T(8,128)(2,1)}, u32[]{:S(2)}, u32[]{:S(2)}) collective-permute-start(bf16[4,256,1024]{2,1,0:T(8,128)(2,1)} %get-tuple-element.142), channel_id=1, source_target_pairs={{0,4},{2,6},{4,0},{6,2},{8,12},{10,14},{12,8},{14,10},{16,20},{18,... | collective-permute-start | bytes 6291464 | tf_op jit(solution)/shard_map/ppermute | solution.py:337
  524.6 35.6 %collective-permute-start.9 = (bf16[4,256,2048]{2,1,0:T(8,128)(2,1)}, bf16[4,256,2048]{2,1,0:T(8,128)(2,1)}, u32[]{:S(2)}, u32[]{:S(2)}) collective-permute-start(bf16[4,256,2048]{2,1,0:T(8,128)(2,1)} %get-tuple-element.143), channel_id=1, source_target_pairs={{0,2},{2,0},{4,6},{6,4},{8,10},{10,8},{12,14},{14,12},{16,18},{18,... | collective-permute-start | bytes 12582920 | tf_op jit(solution)/shard_map/ppermute | solution.py:333
  559.6 58.6 %collective-permute-start.6 = (bf16[4,256,2048]{2,1,0:T(8,128)(2,1)}, bf16[4,256,2048]{2,1,0:T(8,128)(2,1)}, u32[]{:S(2)}, u32[]{:S(2)}) collective-permute-start(bf16[4,256,2048]{2,1,0:T(8,128)(2,1)} %get-tuple-element.138), channel_id=1, source_target_pairs={{0,2},{2,0},{4,6},{6,4},{8,10},{10,8},{12,14},{14,12},{16,18},{18,... | collective-permute-start | bytes 12582920 | tf_op jit(solution)/shard_map/ppermute | solution.py:333
  564.7 42.1 %collective-permute-start.10 = (bf16[2,256,1024]{2,1,0:T(8,128)(2,1)S(1)}, bf16[2,256,1024]{2,1,0:T(8,128)(2,1)}, u32[]{:S(2)}, u32[]{:S(2)}) collective-permute-start(bf16[2,256,1024]{2,1,0:T(8,128)(2,1)S(1)} %get-tuple-element.153), channel_id=1, source_target_pairs={{0,1},{1,0},{2,3},{3,2},{4,5},{5,4},{6,7},{7,6},{8,9},{9,8},{10,11... | collective-permute-start | bytes 3145736 | tf_op jit(solution)/shard_map/ppermute | solution.py:341
  565.3 41.5 %collective-permute-start.11 = (bf16[2,256,1024]{2,1,0:T(8,128)(2,1)S(1)}, bf16[2,256,1024]{2,1,0:T(8,128)(2,1)}, u32[]{:S(2)}, u32[]{:S(2)}) collective-permute-start(bf16[2,256,1024]{2,1,0:T(8,128)(2,1)S(1)} %get-tuple-element.154), channel_id=1, source_target_pairs={{0,4},{2,6},{4,0},{6,2},{8,12},{10,14},{12,8},{14,10},{16,20},{18,... | collective-permute-start | bytes 3145736 | tf_op jit(solution)/shard_map/ppermute | solution.py:337
  568.1 44.5 %collective-permute-start.12 = (bf16[2,256,1024]{2,1,0:T(8,128)(2,1)S(1)}, bf16[2,256,1024]{2,1,0:T(8,128)(2,1)}, u32[]{:S(2)}, u32[]{:S(2)}) collective-permute-start(bf16[2,256,1024]{2,1,0:T(8,128)(2,1)S(1)} %add_convert_fusion.26), channel_id=1, source_target_pairs={{0,4},{2,6},{4,0},{6,2},{8,12},{10,14},{12,8},{14,10},{16,20},{18,... | collective-permute-start | bytes 3145736 | tf_op jit(solution)/shard_map/ppermute | solution.py:337
  571.6 41.1 %collective-permute-start.13 = (bf16[2,256,1024]{2,1,0:T(8,128)(2,1)}, bf16[2,256,1024]{2,1,0:T(8,128)(2,1)}, u32[]{:S(2)}, u32[]{:S(2)}) collective-permute-start(bf16[2,256,1024]{2,1,0:T(8,128)(2,1)} %add_convert_fusion.25), channel_id=1, source_target_pairs={{0,1},{1,0},{2,3},{3,2},{4,5},{5,4},{6,7},{7,6},{8,9},{9,8},{10,11... | collective-permute-start | bytes 3145736 | tf_op jit(solution)/shard_map/ppermute | solution.py:341
  612.7 21.9 %collective-permute-start.14 = (bf16[4,256,2048]{2,1,0:T(8,128)(2,1)}, bf16[4,256,2048]{2,1,0:T(8,128)(2,1)}, u32[]{:S(2)}, u32[]{:S(2)}) collective-permute-start(bf16[4,256,2048]{2,1,0:T(8,128)(2,1)} %get-tuple-element.159), channel_id=1, source_target_pairs={{0,2},{2,0},{4,6},{6,4},{8,10},{10,8},{12,14},{14,12},{16,18},{18,... | collective-permute-start | bytes 12582920 | tf_op jit(solution)/shard_map/ppermute | solution.py:333
  613.4 12.0 %all-to-all-start.1 = ((f32[32,1,256]{2,1,0:T(1,128)}), f32[32,1,256]{2,1,0:T(1,128)S(1)}, u32[]{:S(2)}, u32[]{:S(2)}) async-start(f32[32,1,256]{2,1,0:T(1,128)} %bitcast.161), calls=%async_computation.1 | async-start | bytes 65536 | tf_op jit(solution)/shard_map/all_to_all | solution.py:961
  618.1 497.3 %reduce-scatter.5.cloned.1.call-start = ((), (), s32[]{:S(2)}) async-start(), calls=%async_computation.8 | async-start | bytes 8912896 | tf_op jit(solution)/shard_map/reduce_scatter | solution.py:1032
  631.3 28.4 %collective-permute-start.19 = (bf16[256,2048]{1,0:T(8,128)(2,1)}, bf16[256,2048]{1,0:T(8,128)(2,1)S(1)}, u32[]{:S(2)}, u32[]{:S(2)}) collective-permute-start(bf16[256,2048]{1,0:T(8,128)(2,1)} %pad_maximum_fusion.11), channel_id=1, source_target_pairs={{0,24},{2,26},{4,28},{6,30},{8,0},{10,2},{12,4},{14,6},{16,8},{18,... | collective-permute-start | bytes 3145736 | tf_op jit(solution)/shard_map/ppermute | solution.py:358
  634.5 66.8 %collective-permute-start.20 = (bf16[256,2048]{1,0:T(8,128)(2,1)}, bf16[256,2048]{1,0:T(8,128)(2,1)S(1)}, u32[]{:S(2)}, u32[]{:S(2)}) collective-permute-start(bf16[256,2048]{1,0:T(8,128)(2,1)} %pad_maximum_fusion.12), channel_id=1, source_target_pairs={{0,16},{2,18},{4,20},{6,22},{8,24},{10,26},{12,28},{14,30},{16,0},... | collective-permute-start | bytes 3145736 | tf_op jit(solution)/shard_map/ppermute | solution.py:358
  639.0 62.3 %collective-permute-start.15 = (bf16[2,256,1024]{2,1,0:T(8,128)(2,1)}, bf16[2,256,1024]{2,1,0:T(8,128)(2,1)}, u32[]{:S(2)}, u32[]{:S(2)}) collective-permute-start(bf16[2,256,1024]{2,1,0:T(8,128)(2,1)} %get-tuple-element.160), channel_id=1, source_target_pairs={{0,1},{1,0},{2,3},{3,2},{4,5},{5,4},{6,7},{7,6},{8,9},{9,8},{10,11... | collective-permute-start | bytes 3145736 | tf_op jit(solution)/shard_map/ppermute | solution.py:341
  640.5 60.9 %collective-permute-start.16 = (bf16[2,256,1024]{2,1,0:T(8,128)(2,1)S(1)}, bf16[2,256,1024]{2,1,0:T(8,128)(2,1)}, u32[]{:S(2)}, u32[]{:S(2)}) collective-permute-start(bf16[2,256,1024]{2,1,0:T(8,128)(2,1)S(1)} %get-tuple-element.161), channel_id=1, source_target_pairs={{0,4},{2,6},{4,0},{6,2},{8,12},{10,14},{12,8},{14,10},{16,20},{18,... | collective-permute-start | bytes 3145736 | tf_op jit(solution)/shard_map/ppermute | solution.py:337
  644.6 56.8 %collective-permute-start.17 = (bf16[2,256,1024]{2,1,0:T(8,128)(2,1)}, bf16[2,256,1024]{2,1,0:T(8,128)(2,1)}, u32[]{:S(2)}, u32[]{:S(2)}) collective-permute-start(bf16[2,256,1024]{2,1,0:T(8,128)(2,1)} %add_convert_fusion.20), channel_id=1, source_target_pairs={{0,4},{2,6},{4,0},{6,2},{8,12},{10,14},{12,8},{14,10},{16,20},{18,... | collective-permute-start | bytes 3145736 | tf_op jit(solution)/shard_map/ppermute | solution.py:337
  659.7 41.7 %collective-permute-start.18 = (bf16[2,256,1024]{2,1,0:T(8,128)(2,1)}, bf16[2,256,1024]{2,1,0:T(8,128)(2,1)}, u32[]{:S(2)}, u32[]{:S(2)}) collective-permute-start(bf16[2,256,1024]{2,1,0:T(8,128)(2,1)} %add_convert_fusion.19), channel_id=1, source_target_pairs={{0,1},{1,0},{2,3},{3,2},{4,5},{5,4},{6,7},{7,6},{8,9},{9,8},{10,11... | collective-permute-start | bytes 3145736 | tf_op jit(solution)/shard_map/ppermute | solution.py:341
  702.4 43.6 %collective-permute-start.23 = (bf16[12,256,2048]{2,1,0:T(8,128)(2,1)}, bf16[12,256,2048]{2,1,0:T(8,128)(2,1)S(1)}, u32[]{:S(2)}, u32[]{:S(2)}) collective-permute-start(bf16[12,256,2048]{2,1,0:T(8,128)(2,1)} %get-tuple-element.184), channel_id=1, source_target_pairs={{0,2},{2,0},{4,6},{6,4},{8,10},{10,8},{12,14},{14,12},{16,18},{18,... | collective-permute-start | bytes 37748744 | tf_op jit(solution)/shard_map/ppermute | solution.py:333
  702.4 35.8 %collective-permute-start.22 = (bf16[4,256,2048]{2,1,0:T(8,128)(2,1)}, bf16[4,256,2048]{2,1,0:T(8,128)(2,1)}, u32[]{:S(2)}, u32[]{:S(2)}) collective-permute-start(bf16[4,256,2048]{2,1,0:T(8,128)(2,1)} %get-tuple-element.182), channel_id=1, source_target_pairs={{0,2},{2,0},{4,6},{6,4},{8,10},{10,8},{12,14},{14,12},{16,18},{18,... | collective-permute-start | bytes 12582920 | tf_op jit(solution)/shard_map/ppermute | solution.py:333
  707.8 27.6 %collective-permute-start.21 = (bf16[256,2048]{1,0:T(8,128)(2,1)S(1)}, bf16[256,2048]{1,0:T(8,128)(2,1)S(1)}, u32[]{:S(2)}, u32[]{:S(2)}) collective-permute-start(bf16[256,2048]{1,0:T(8,128)(2,1)S(1)} %pad_maximum_fusion.13), channel_id=1, source_target_pairs={{0,8},{2,10},{4,12},{6,14},{8,16},{10,18},{12,20},{14,22},{16,24},... | collective-permute-start | bytes 3145736 | tf_op jit(solution)/shard_map/ppermute | solution.py:358
  746.0 24.7 %collective-permute-start.24 = (bf16[256,2048]{1,0:T(8,128)(2,1)S(1)}, bf16[256,2048]{1,0:T(8,128)(2,1)}, u32[]{:S(2)}, u32[]{:S(2)}) collective-permute-start(bf16[256,2048]{1,0:T(8,128)(2,1)S(1)} %fusion.51), channel_id=1, source_target_pairs={{0,1},{1,0},{2,3},{3,2},{4,5},{5,4},{6,7},{7,6},{8,9},{9,8},{10,11... | collective-permute-start | bytes 3145736 | tf_op jit(solution)/shard_map/ppermute | solution.py:341
  781.4 335.5 %reduce-scatter.3.cloned.1.call-start = ((), (), s32[]{:S(2)}) async-start(), calls=%async_computation.7 | async-start | bytes 13369344 | tf_op jit(solution)/shard_map/reduce_scatter | solution.py:1039
  781.4 60.1 %collective-permute-start.26 = (bf16[4,256,1024]{2,1,0:T(8,128)(2,1)}, bf16[4,256,1024]{2,1,0:T(8,128)(2,1)S(1)}, u32[]{:S(2)}, u32[]{:S(2)}) collective-permute-start(bf16[4,256,1024]{2,1,0:T(8,128)(2,1)} %get-tuple-element.243), channel_id=1, source_target_pairs={{0,4},{2,6},{4,0},{6,2},{8,12},{10,14},{12,8},{14,10},{16,20},{18,... | collective-permute-start | bytes 6291464 | tf_op jit(solution)/shard_map/ppermute | solution.py:337
  783.0 58.5 %collective-permute-start.25 = (bf16[4,256,1024]{2,1,0:T(8,128)(2,1)}, bf16[4,256,1024]{2,1,0:T(8,128)(2,1)S(1)}, u32[]{:S(2)}, u32[]{:S(2)}) collective-permute-start(bf16[4,256,1024]{2,1,0:T(8,128)(2,1)} %get-tuple-element.190), channel_id=1, source_target_pairs={{0,1},{1,0},{2,3},{3,2},{4,5},{5,4},{6,7},{7,6},{8,9},{9,8},{10,11... | collective-permute-start | bytes 6291464 | tf_op jit(solution)/shard_map/ppermute | solution.py:341
  784.5 89.6 %collective-permute-start.27 = (bf16[4,256,1024]{2,1,0:T(8,128)(2,1)}, bf16[4,256,1024]{2,1,0:T(8,128)(2,1)}, u32[]{:S(2)}, u32[]{:S(2)}) collective-permute-start(bf16[4,256,1024]{2,1,0:T(8,128)(2,1)} %pad_maximum_fusion.6), channel_id=1, source_target_pairs={{0,1},{1,0},{2,3},{3,2},{4,5},{5,4},{6,7},{7,6},{8,9},{9,8},{10,11... | collective-permute-start | bytes 6291464 | tf_op jit(solution)/shard_map/ppermute | solution.py:341
  785.0 115.9 %collective-permute-start.28 = (bf16[4,256,1024]{2,1,0:T(8,128)(2,1)}, bf16[4,256,1024]{2,1,0:T(8,128)(2,1)}, u32[]{:S(2)}, u32[]{:S(2)}) collective-permute-start(bf16[4,256,1024]{2,1,0:T(8,128)(2,1)} %pad_maximum_fusion.5), channel_id=1, source_target_pairs={{0,4},{2,6},{4,0},{6,2},{8,12},{10,14},{12,8},{14,10},{16,20},{18,... | collective-permute-start | bytes 6291464 | tf_op jit(solution)/shard_map/ppermute | solution.py:337
  916.0 62.7 %collective-permute-start.29 = (bf16[4,256,1024]{2,1,0:T(8,128)(2,1)}, bf16[4,256,1024]{2,1,0:T(8,128)(2,1)}, u32[]{:S(2)}, u32[]{:S(2)}) collective-permute-start(bf16[4,256,1024]{2,1,0:T(8,128)(2,1)} %add_convert_fusion.1), channel_id=1, source_target_pairs={{0,4},{2,6},{4,0},{6,2},{8,12},{10,14},{12,8},{14,10},{16,20},{18,... | collective-permute-start | bytes 6291464 | tf_op jit(solution)/shard_map/ppermute | solution.py:337
  919.8 58.9 %collective-permute-start.30 = (bf16[4,256,1024]{2,1,0:T(8,128)(2,1)}, bf16[4,256,1024]{2,1,0:T(8,128)(2,1)}, u32[]{:S(2)}, u32[]{:S(2)}) collective-permute-start(bf16[4,256,1024]{2,1,0:T(8,128)(2,1)} %add_convert_fusion), channel_id=1, source_target_pairs={{0,1},{1,0},{2,3},{3,2},{4,5},{5,4},{6,7},{7,6},{8,9},{9,8},{10,11... | collective-permute-start | bytes 6291464 | tf_op jit(solution)/shard_map/ppermute | solution.py:341
  932.3 74.1 %collective-permute-start.39 = (f32[2,33,128]{2,0,1:T(2,128)S(1)}, f32[2,33,128]{2,0,1:T(2,128)S(1)}, u32[]{:S(2)}, u32[]{:S(2)}) collective-permute-start(f32[2,33,128]{2,0,1:T(2,128)S(1)} %dynamic-slice_bitcast_fusion.2), channel_id=1, source_target_pairs={{0,4},{2,6},{4,0},{6,2},{8,12},{10,14},{12,8},{14,10},{16,20},{18,... | collective-permute-start | bytes 101384 | tf_op jit(solution)/shard_map/ppermute | solution.py:406
  1004.9 17.2 %collective-permute-start.34 = (bf16[256,2048]{1,0:T(8,128)(2,1)}, bf16[256,2048]{1,0:T(8,128)(2,1)}, u32[]{:S(2)}, u32[]{:S(2)}) collective-permute-start(bf16[256,2048]{1,0:T(8,128)(2,1)} %select_convert_fusion), channel_id=1, source_target_pairs={{0,1},{1,0},{2,3},{3,2},{4,5},{5,4},{6,7},{7,6},{8,9},{9,8},{10,11... | collective-permute-start | bytes 3145736 | tf_op jit(solution)/shard_map/ppermute | solution.py:341
  1007.7 13.7 %collective-permute-start.41 = (f32[33,128]{1,0:T(8,128)S(1)}, f32[33,128]{1,0:T(8,128)S(1)}, u32[]{:S(2)}, u32[]{:S(2)}) collective-permute-start(f32[33,128]{1,0:T(8,128)S(1)} %bitcast.178), channel_id=1, source_target_pairs={{0,1},{1,0},{2,3},{3,2},{4,5},{5,4},{6,7},{7,6},{8,9},{9,8},{10,11... | collective-permute-start | bytes 50696 | tf_op jit(solution)/shard_map/ppermute | solution.py:341
  1027.1 89.9 %collective-permute-start.33 = (bf16[256,2048]{1,0:T(8,128)(2,1)}, bf16[256,2048]{1,0:T(8,128)(2,1)}, u32[]{:S(2)}, u32[]{:S(2)}) collective-permute-start(bf16[256,2048]{1,0:T(8,128)(2,1)} %pad_maximum_fusion.17), channel_id=1, source_target_pairs={{0,8},{2,10},{4,12},{6,14},{8,16},{10,18},{12,20},{14,22},{16,24},... | collective-permute-start | bytes 3145736 | tf_op jit(solution)/shard_map/ppermute | solution.py:358
  1027.1 90.4 %collective-permute-start.32 = (bf16[256,2048]{1,0:T(8,128)(2,1)}, bf16[256,2048]{1,0:T(8,128)(2,1)}, u32[]{:S(2)}, u32[]{:S(2)}) collective-permute-start(bf16[256,2048]{1,0:T(8,128)(2,1)} %pad_maximum_fusion.16), channel_id=1, source_target_pairs={{0,16},{2,18},{4,20},{6,22},{8,24},{10,26},{12,28},{14,30},{16,0},... | collective-permute-start | bytes 3145736 | tf_op jit(solution)/shard_map/ppermute | solution.py:358
  1027.1 90.4 %collective-permute-start.31 = (bf16[256,2048]{1,0:T(8,128)(2,1)}, bf16[256,2048]{1,0:T(8,128)(2,1)}, u32[]{:S(2)}, u32[]{:S(2)}) collective-permute-start(bf16[256,2048]{1,0:T(8,128)(2,1)} %pad_maximum_fusion.15), channel_id=1, source_target_pairs={{0,24},{2,26},{4,28},{6,30},{8,0},{10,2},{12,4},{14,6},{16,8},{18,... | collective-permute-start | bytes 3145736 | tf_op jit(solution)/shard_map/ppermute | solution.py:358
  1031.0 36.9 %collective-permute-start.43 = (f32[18,128]{1,0:T(8,128)S(1)}, f32[18,128]{1,0:T(8,128)S(1)}, u32[]{:S(2)}, u32[]{:S(2)}) collective-permute-start(f32[18,128]{1,0:T(8,128)S(1)} %fusion.48), channel_id=1, source_target_pairs={{0,1},{1,0},{2,3},{3,2},{4,5},{5,4},{6,7},{7,6},{8,9},{9,8},{10,11... | collective-permute-start | bytes 27656 | tf_op jit(solution)/shard_map/ppermute | solution.py:341
  1067.9 18.1 %collective-permute-start.44 = (f32[18,128]{1,0:T(8,128)S(1)}, f32[18,128]{1,0:T(8,128)S(1)}, u32[]{:S(2)}, u32[]{:S(2)}) collective-permute-start(f32[18,128]{1,0:T(8,128)S(1)} %add.671), channel_id=1, source_target_pairs={{0,4},{2,6},{4,0},{6,2},{8,12},{10,14},{12,8},{14,10},{16,20},{18,... | collective-permute-start | bytes 27656 | tf_op jit(solution)/shard_map/ppermute | solution.py:394
  1085.9 25.0 %collective-permute-start.45 = (f32[18,128]{1,0:T(8,128)S(1)}, f32[18,128]{1,0:T(8,128)S(1)}, u32[]{:S(2)}, u32[]{:S(2)}) collective-permute-start(f32[18,128]{1,0:T(8,128)S(1)} %add.672), channel_id=1, source_target_pairs={{0,8},{2,10},{4,12},{6,14},{8,0},{10,2},{12,4},{14,6},{16,24},{18,... | collective-permute-start | bytes 27656 | tf_op jit(solution)/shard_map/ppermute | solution.py:394
  1110.9 25.8 %collective-permute-start.46 = (f32[18,128]{1,0:T(8,128)S(1)}, f32[18,128]{1,0:T(8,128)S(1)}, u32[]{:S(2)}, u32[]{:S(2)}) collective-permute-start(f32[18,128]{1,0:T(8,128)S(1)} %add.673), channel_id=1, source_target_pairs={{0,16},{2,18},{4,20},{6,22},{8,24},{10,26},{12,28},{14,30},{16,0},... | collective-permute-start | bytes 27656 | tf_op jit(solution)/shard_map/ppermute | solution.py:394
  1115.5 22.5 %collective-permute-start.36 = (bf16[128,2048]{1,0:T(8,128)(2,1)}, bf16[128,2048]{1,0:T(8,128)(2,1)S(1)}, u32[]{:S(2)}, u32[]{:S(2)}) collective-permute-start(bf16[128,2048]{1,0:T(8,128)(2,1)} %reduce-scatter.5.cloned.1.call-done), channel_id=1, source_target_pairs={{0,1},{1,0},{2,3},{3,2},{4,5},{5,4},{6,7},{7,6},{8,9},{9,8},{10,11... | collective-permute-start | bytes 1572872 | tf_op jit(solution)/shard_map/ppermute | solution.py:341
  1116.9 29.2 %collective-permute-start.35 = (bf16[128,3072]{1,0:T(8,128)(2,1)}, bf16[128,3072]{1,0:T(8,128)(2,1)S(1)}, u32[]{:S(2)}, u32[]{:S(2)}) collective-permute-start(bf16[128,3072]{1,0:T(8,128)(2,1)} %reduce-scatter.3.cloned.1.call-done.mine_ref), channel_id=1, source_target_pairs={{0,1},{1,0},{2,3},{3,2},{4,5},{5,4},{6,7},{7,6},{8,9},{9,8},{10,11... | collective-permute-start | bytes 2359304 | tf_op jit(solution)/shard_map/ppermute | solution.py:341
  (76 other events, 1635.5 us)
Sparse Core Ops, SparseCore 0:
  10.4 112.8 all-gather.3
  125.4 134.2 all-gather.7
  261.9 168.0 all-gather.5
  781.5 124.6 reduce-scatter.4
  911.4 188.4 reduce-scatter.2

commit v9 on v7

--- a/solution.py
+++ b/solution.py
@@ -973,10 +973,9 @@
     )
     entries.update(joined(parts[1], [item[cut:] for item in back_own], got))
     out_far = over_core(*out_far)
-    out_far = [
-        swap_ctx(pick_sum(out_far, 0, lines, 0)),
-        swap_side(pick_sum(out_far, 0, lines, 1)),
-    ]
+    out_far = [pick_sum(out_far, 0, lines, column) for column in range(2)]
+    out_rest, out_far = hold(out_rest, out_far)
+    out_far = [swap_ctx(out_far[0]), swap_side(out_far[1])]
     out_rest = over_core(*out_rest)
     for p in parts[1][:-1]:
         arrived[p] = line_shift(entries[p], lines - p)
@@ -1000,29 +999,23 @@
     out_own = [pick_sum(out_rest, 2 * cut, 2 * cut + lines, column) for column in range(2)]
     (out_sums, out_own), grad_branch = hold((out_sums, out_own), grad_branch)
     side_one, side_two, ctx_one, ctx_two = out_sums
-    got = [
-        swap_ctx(ctx_one),
-        swap_side(side_two),
-        add_low(side_one, out_far[0]),
-        add_low(ctx_two, out_far[1]),
-    ]
     grad_attended = mul(grad_branch, out_all, rhs_turned).astype(low)
-    grad_attended, got = hold(grad_attended, got)
-    got[2], got[3] = swap_side(got[2]), swap_ctx(got[3])
+    got = [swap_ctx(ctx_one), swap_side(side_two)]
+    grad_gate_up = mul(rows, grad_pair, lhs_turned)[None]
+    grad_attended, got, grad_gate_up = lax.optimization_barrier((grad_attended, got, grad_gate_up))
+    got += [swap_side(add_low(side_one, out_far[0])), swap_ctx(add_low(ctx_two, out_far[1]))]
     grad_out_part = mul(attended, grad_branch, lhs_turned).astype(low)
     grad_q, grad_k, grad_v, gain_q_part, gain_k_part = attend_grad(
         projected, roped_q, roped_k, values_low, grad_attended, cosine, sine, gain_q, gain_k, kv_heads, group
     )
     grad_projected = jnp.concatenate([grad_q, grad_k, grad_v], axis=1)
+    grad_down = mul(hidden, grad_rows, lhs_turned)[None]
+    grad_projected, (got[3], grad_down) = hold(grad_projected, (got[3], grad_down))
     grad_qkv_part = mul(low_in, grad_projected, lhs_turned).astype(low)
-    grad_projected, got = hold(grad_projected, got)
+    grad_normed_part = mul(grad_projected, qkv_all, rhs_turned)
     entries = joined(places, out_own, got)
-    grad_projected, entries = hold(grad_projected, entries)
+    grad_normed_part, entries = hold(grad_normed_part, entries)
     arrived = {p: line_shift(entries[p], lines - p) for p in places[:-1]}
-    grad_normed_part = mul(grad_projected, qkv_all, rhs_turned)
-    (rows, grad_pair, hidden, grad_rows), arrived = hold((rows, grad_pair, hidden, grad_rows), arrived)
-    grad_gate_up = mul(rows, grad_pair, lhs_turned)[None]
-    grad_down = mul(hidden, grad_rows, lhs_turned)[None]
     output = (mixed + line_total(entries[0], arrived)).astype(low)
     grad_normed = of_block(grad_normed_part, rank) + swap_ctx(
         of_block(grad_normed_part, 1 - rank).astype(low)

time: 1240 us -> 1190 us (0.960)
  waiting for transfers between devices: 660 us -> 606 us
    ppermute x6, waiting for transfers between devices: 140 us -> 36.4 us  [line_shift(): lax.ppermute(values, 'fsdp', [(i, (i + 4 * step) % fsdp) for i in range(f...]
    ppermute x3, waiting for transfers between devices: 3.68 us -> 88.3 us  [sum_all(): lax.ppermute(values, 'fsdp', [(i, i ^ step) for i in range(fsdp)])]
    ppermute x19, waiting for transfers between devices: 331 us -> 281 us  [swap_ctx(): return lax.ppermute(values, 'ctx', [(0, 1), (1, 0)])]
    ppermute x8, waiting for transfers between devices: 42.5 us -> 75.4 us  [swap_side(): return lax.ppermute(values, 'fsdp', side_pairs(lax.axis_size('fsdp')))]
  transfers between devices with their start and end apart: 53 -> 53, of which waited for: 31 -> 31; matrix products, arithmetic and copies ran while one was open for 18% -> 18% of each run, Pallas kernels for 15% -> 16%
where the time goes in v9:
time: 1190 us; the launch traced here: 1180 us
  waiting for transfers between devices  606 us (51%)
  Pallas kernels  224 us (19%)
  other arithmetic  110 us (9%)
  matrix products  110 us (9%)
  starting transfers between devices  55.2 us (5%)
  blocking collectives  35.6 us (3%)
  local copies, waits for them, and re-layouts  26.5 us (2%)
  between operations  15.4 us (1%)
    ppermute x19, waiting for transfers between devices, swap_ctx(): return lax.ppermute(values, 'ctx', [(0, 1), (1, 0)])  281 us
    pallas_call x4, Pallas kernels, run_expert(): pl.pallas_call(expert_kernel, grid_spec=grid_spec, out_shape=[shape((step...  135 us
    dot_general x11, matrix products, mul(): return lax.dot_general(left, right, dims, preferred_element_type=full)  110 us
    ppermute x3, waiting for transfers between devices, sum_all(): lax.ppermute(values, 'fsdp', [(i, i ^ step) for i in range(fsdp)])  88.3 us
    ppermute x8, waiting for transfers between devices, swap_side(): return lax.ppermute(values, 'fsdp', side_pairs(lax.axis_size('fsdp')))  75.4 us
    convert_element_type x19, other arithmetic, add_low(): return (one.astype(full) + two.astype(full)).astype(low)  69.8 us
    all_gather x1, waiting for transfers between devices, body_gathered(): weights_all = lax.all_gather(weights_local, 'fsdp', axis=0, tiled=True)  65.6 us
    pallas_call x2, Pallas kernels, run_result(): pl.pallas_call(result_kernel, grid_spec=pltpu.PrefetchScalarGridSpec(num_...  40.2 us
  transfers between devices with their start and end apart: 53, of which 31 were waited for; matrix products, arithmetic and copies ran while one was open for 18% of the time, Pallas kernels for 16%

profile of v9, /device:TPU:0, one launch (start us, length us, event | category | flops | bytes accessed | tf_op | source)
XLA Modules:
  0.0 1182.0 jit_solution(2901189284995061058)
XLA Ops:
  13.4 13.3 %collective-permute-done.3 = bf16[256,1152]{1,0:T(8,128)(2,1)S(1)} collective-permute-done((bf16[256,1152]{1,0:T(8,128)(2,1)S(1)}, bf16[256,1152]{1,0:T(8,128)(2,1)S(1)}, u32[]{:S(2)}, u32[]{:S(2)}) %collective-permute-start.3) | collective-permute-done | bytes 589856 | tf_op jit(solution)/shard_map/ppermute | solution.py:341
  31.2 22.9 %all_gather.12 = bf16[2048,34]{0,1:T(8,128)(2,1)S(1)} all-gather(bf16[128,34]{0,1:T(8,128)(2,1)S(1)} %pad_maximum_fusion.21), channel_id=1, replica_groups=mesh['fsdp'=16,'ctx'=2] {'fsdp'}, dimensions={0}, use_global_device_ids=true | all-gather | bytes 147968 | tf_op jit(solution)/shard_map/all_gather | solution.py:835
  57.6 65.6 %all-gather.4.cloned.1.call-done = bf16[2048,5120]{1,0:T(8,128)(2,1)} async-done(((bf16[128,5120]{1,0:T(8,128)(2,1)}), bf16[2048,5120]{1,0:T(8,128)(2,1)}) %all-gather.4.cloned.1.call-update) | async-done | bytes 20971536 | tf_op jit(solution)/shard_map/all_gather | solution.py:836
  123.2 11.6 fusion.2.q_ref.k_ref.v_ref
  134.8 18.2 %attend.1 = (bf16[512,2048]{1,0:T(8,128)(2,1)S(1)}, bf16[512,2048]{1,0:T(8,128)(2,1)S(1)}, bf16[512,512]{1,0:T(8,128)(2,1)S(1)}, bf16[512,512]{1,0:T(8,128)(2,1)S(1)}) custom-call(f32[512,3072]{1,0:T(8,128)} %fusion.2.q_ref.k_ref.v_ref, f32[512,3072]{1,0:T(8,128)} %fusion.2.q_ref.k_ref.v_ref, f32[512,3072]{1,0:T(8,128)} %fusion.2.q_ref.k_ref.v_ref, ...), custom_call_target="tpu_custom_call" | custom-call | flops 2147483648 | bytes 9437184 | tf_op jit(solution)/shard_map/attend/pallas_call | solution.py:521
  153.1 8.4 fusion.6
  163.6 23.9 %collective-permute-done.1 = bf16[256,2048]{1,0:T(8,128)(2,1)S(1)} collective-permute-done((bf16[256,2048]{1,0:T(8,128)(2,1)S(1)}, bf16[256,2048]{1,0:T(8,128)(2,1)S(1)}, u32[]{:S(2)}, u32[]{:S(2)}) %collective-permute-start.1) | collective-permute-done | bytes 1048608 | tf_op jit(solution)/shard_map/ppermute | solution.py:341
  191.8 23.1 %collective-permute-done.2 = bf16[256,2048]{1,0:T(8,128)(2,1)S(1)} collective-permute-done((bf16[256,2048]{1,0:T(8,128)(2,1)S(1)}, bf16[256,2048]{1,0:T(8,128)(2,1)S(1)}, u32[]{:S(2)}, u32[]{:S(2)}) %collective-permute-start.2) | collective-permute-done | bytes 1048608 | tf_op jit(solution)/shard_map/ppermute | solution.py:341
  218.4 12.7 %all_to_all.24 = f32[32,1,256]{2,1,0:T(1,128)S(1)} all-to-all(f32[32,1,256]{2,1,0:T(1,128)S(1)} %copy.60), channel_id=1, replica_groups=mesh['fsdp'=16,'ctx'=2] {'fsdp','ctx'}, dimensions={0} | all-to-all | bytes 65536 | tf_op jit(solution)/shard_map/all_to_all | solution.py:873
  231.2 28.5 %all-gather.8.cloned.1.call-done = bf16[4096,3200]{1,0:T(8,128)(2,1)} async-done(((bf16[256,3200]{1,0:T(8,128)(2,1)}), bf16[4096,3200]{1,0:T(8,128)(2,1)}) %all-gather.8.cloned.1.call-update) | async-done | bytes 26214416 | tf_op jit(solution)/shard_map/all_gather | solution.py:843
  259.7 6.9 slice.403
  269.4 157.7 %collective-permute-done.4.far_ref = bf16[8,2,256,896]{3,2,1,0:T(8,128)(2,1)} collective-permute-done((bf16[8,2,256,896]{3,2,1,0:T(8,128)(2,1)}, bf16[8,2,256,896]{3,2,1,0:T(8,128)(2,1)}, u32[]{:S(2)}, u32[]{:S(2)}) %collective-permute-start.4) | collective-permute-done | bytes 7340064 | tf_op jit(solution)/shard_map/ppermute | solution.py:341
  429.9 33.0 %experts.4 = (bf16[4,256,2048]{2,1,0:T(8,128)(2,1)}, bf16[4,256,2048]{2,1,0:T(8,128)(2,1)}, f32[8,2,2,1,256]{4,3,2,1,0:T(1,128)}, bf16[4096,2048]{1,0:T(8,128)(2...) custom-call(s32[1]{0:T(128)} %bitcast.6.core_ref, s32[16]{0:T(128)} %stack.35.order, ...), custom_call_target="tpu_custom_call" | custom-call | flops 19327352832 | bytes 38273024 | tf_op jit(solution)/shard_map/experts/pallas_call | solution.py:670
  463.3 7.1 collective-permute-done.5
  470.4 4.8 add_convert_fusion.8
  478.5 34.2 %experts.5 = (bf16[4,256,2048]{2,1,0:T(8,128)(2,1)}, bf16[4,256,2048]{2,1,0:T(8,128)(2,1)}, f32[8,2,2,1,256]{4,3,2,1,0:T(1,128)}, bf16[4096,2048]{1,0:T(8,128)(2...) custom-call(s32[1]{0:T(128)} %bitcast.6.core_ref, ...), custom_call_target="tpu_custom_call", output_to_operand_aliasing={{2}: (8, {}), {3}: (9, {}), {4}: (10, {}), {5}: (11, {}), {... | custom-call | flops 19327352832 | bytes 38273024 | tf_op jit(solution)/shard_map/experts/pallas_call | solution.py:670
  512.7 10.7 collective-permute-done.7
  525.8 33.6 %experts.6 = (bf16[4,256,2048]{2,1,0:T(8,128)(2,1)}, bf16[4,256,2048]{2,1,0:T(8,128)(2,1)}, f32[8,2,2,1,256]{4,3,2,1,0:T(1,128)}, bf16[4096,2048]{1,0:T(8,128)(2...) custom-call(s32[1]{0:T(128)} %bitcast.6.core_ref, ...), custom_call_target="tpu_custom_call", output_to_operand_aliasing={{2}: (8, {}), {3}: (9, {}), {4}: (10, {}), {5}: (11, {}), {... | custom-call | flops 19327352832 | bytes 38273024 | tf_op jit(solution)/shard_map/experts/pallas_call | solution.py:670
  573.0 33.7 %experts.7 = (bf16[4,256,2048]{2,1,0:T(8,128)(2,1)}, bf16[4,256,2048]{2,1,0:T(8,128)(2,1)}, f32[8,2,2,1,256]{4,3,2,1,0:T(1,128)}, bf16[4096,2048]{1,0:T(8,128)(2...) custom-call(s32[1]{0:T(128)} %bitcast.6.core_ref, ...), custom_call_target="tpu_custom_call", output_to_operand_aliasing={{2}: (8, {}), {3}: (9, {}), {4}: (10, {}), {5}: (11, {}), {... | custom-call | flops 19327352832 | bytes 38273024 | tf_op jit(solution)/shard_map/experts/pallas_call | solution.py:670
  606.7 5.9 collective-permute-done.12
  613.4 4.7 all-to-all-start.1
  618.2 5.8 add_convert_fusion.7
  647.8 11.9 %results.2 = (bf16[4,256,2048]{2,1,0:T(8,128)(2,1)}, bf16[4,256,2048]{2,1,0:T(8,128)(2,1)}) custom-call(s32[1]{0:T(128)} %bitcast.6.core_ref, s32[16]{0:T(128)} %stack.35.order, bf16[4096,768]{1,0:T(8,128)(2,1)} %get-tuple-element.160.z_ref, f32[8,2,2,1,256]{4,3,2,1,0:T(1,128)} %reshape.272.w_ref, bf16[768,2048]{1,0:T(8,128)(2,1)} %bitcast.152), custom_call_target="tpu_custom_call" | custom-call | flops 4294967296 | bytes 13107200 | tf_op jit(solution)/shard_map/results/pallas_call | solution.py:701
  660.2 28.3 %results.3 = (bf16[12,256,2048]{2,1,0:T(8,128)(2,1)}, bf16[12,256,2048]{2,1,0:T(8,128)(2,1)}) custom-call(s32[1]{0:T(128)} %bitcast.6.core_ref, s32[48]{0:T(128)} %stack.44.order, bf16[4096,768]{1,0:T(8,128)(2,1)} %get-tuple-element.160.z_ref, f32[8,2,2,1,256]{4,3,2,1,0:T(1,128)} %reshape.272.w_ref, bf16[768,2048]{1,0:T(8,128)(2,1)} %bitcast.153), custom_call_target="tpu_custom_call" | custom-call | flops 12884901888 | bytes 33030144 | tf_op jit(solution)/shard_map/results/pallas_call | solution.py:701
  688.5 13.0 %collective-permute-done.20 = bf16[256,2048]{1,0:T(8,128)(2,1)S(1)} collective-permute-done((bf16[256,2048]{1,0:T(8,128)(2,1)}, bf16[256,2048]{1,0:T(8,128)(2,1)S(1)}, u32[]{:S(2)}, u32[]{:S(2)}) %collective-permute-start.20) | collective-permute-done | bytes 1048608 | tf_op jit(solution)/shard_map/ppermute | solution.py:358
  701.5 7.4 collective-permute-done.22
  708.9 5.0 add_convert_fusion.4
  723.3 23.4 %collective-permute-done.21 = bf16[256,2048]{1,0:T(8,128)(2,1)S(1)} collective-permute-done((bf16[256,2048]{1,0:T(8,128)(2,1)S(1)}, bf16[256,2048]{1,0:T(8,128)(2,1)S(1)}, u32[]{:S(2)}, u32[]{:S(2)}) %collective-permute-start.21) | collective-permute-done | bytes 1048608 | tf_op jit(solution)/shard_map/ppermute | solution.py:358
  749.4 18.7 %collective-permute-done.23 = bf16[4,256,1024]{2,1,0:T(8,128)(2,1)S(1)} collective-permute-done((bf16[4,256,1024]{2,1,0:T(8,128)(2,1)}, bf16[4,256,1024]{2,1,0:T(8,128)(2,1)S(1)}, u32[]{:S(2)}, u32[]{:S(2)}) %collective-permute-start.23) | collective-permute-done | bytes 2097184 | tf_op jit(solution)/shard_map/ppermute | solution.py:341
  771.6 5.6 add_convert_fusion.12
  789.1 5.7 collective-permute-done.26
  798.7 6.8 convolution_convert_fusion.1
  805.7 34.9 %convolution_bitcast_fusion = f32[1,2048,1536]{2,1,0:T(8,128)} fusion(bf16[4096,2048]{1,0:T(8,128)(2,1)} %get-tuple-element.191, bf16[4096,1536]{1,0:T(8,128)(2,1)} %get-tuple-element.192), kind=kOutput, calls=%fused_computation.5 | convolution fusion | flops 25769803776 | bytes 41943040 | tf_op jit(solution)/shard_map/dot_general | solution.py:321
  848.0 16.7 %convolution_bitcast_fusion.1 = f32[1,768,2048]{2,1,0:T(8,128)} fusion(bf16[4096,768]{1,0:T(8,128)(2,1)} %get-tuple-element.160.z_ref, bf16[4096,2048]{1,0:T(8,128)(2,1)S(1)} %bitcast.143), kind=kOutput, calls=%fused_computation.26 | convolution fusion | flops 12884901888 | bytes 29360128 | tf_op jit(solution)/shard_map/dot_general | solution.py:321
  864.7 9.1 fusion.11.go_ref
  873.8 15.7 %collective-permute-done.27 = bf16[4,256,1024]{2,1,0:T(8,128)(2,1)} collective-permute-done((bf16[4,256,1024]{2,1,0:T(8,128)(2,1)}, bf16[4,256,1024]{2,1,0:T(8,128)(2,1)}, u32[]{:S(2)}, u32[]{:S(2)}) %collective-permute-start.27) | collective-permute-done | bytes 2097184 | tf_op jit(solution)/shard_map/ppermute | solution.py:341
  889.5 18.5 %collective-permute-done.28 = bf16[4,256,1024]{2,1,0:T(8,128)(2,1)} collective-permute-done((bf16[4,256,1024]{2,1,0:T(8,128)(2,1)}, bf16[4,256,1024]{2,1,0:T(8,128)(2,1)}, u32[]{:S(2)}, u32[]{:S(2)}) %collective-permute-start.28) | collective-permute-done | bytes 2097184 | tf_op jit(solution)/shard_map/ppermute | solution.py:337
  908.1 25.2 %attend_grad.1 = (bf16[512,2048]{1,0:T(8,128)(2,1)S(1)}, bf16[512,512]{1,0:T(8,128)(2,1)S(1)}, bf16[512,512]{1,0:T(8,128)(2,1)S(1)}, f32[4,1,128]{2,1,0:T(1,128)S(1)}, f32[4,1,128]{2,1,0:T(1,128)S(1)}) custom-call(f32[512,3072]{1,0:T(8,128)} %fusion.2.q_ref.k_ref.v_ref, f32[512,3072]{1,0:T(8,128)} %fusion.2.q_ref.k_ref.v_ref, bf16[512,2048]{1,0:T(8,128)(2,1)} %copy-done, ...), custom_call_target="tpu_custom_call" | custom-call | flops 5368709120 | bytes 15728640 | tf_op jit(solution)/shard_map/attend_grad/pallas_call | solution.py:545
  935.4 10.3 convolution_convert_fusion
  953.8 5.1 collective-permute-done.37
  959.7 5.4 fusion.39
  965.1 48.6 %collective-permute-done.30 = bf16[4,256,1024]{2,1,0:T(8,128)(2,1)} collective-permute-done((bf16[4,256,1024]{2,1,0:T(8,128)(2,1)}, bf16[4,256,1024]{2,1,0:T(8,128)(2,1)}, u32[]{:S(2)}, u32[]{:S(2)}) %collective-permute-start.30) | collective-permute-done | bytes 2097184 | tf_op jit(solution)/shard_map/ppermute | solution.py:337
  1022.1 9.8 fusion
  1048.3 5.9 collective-permute-done.34
  1054.2 4.7 fusion.21
  1069.7 71.0 %collective-permute-done.45 = f32[18,128]{1,0:T(8,128)S(1)} collective-permute-done((f32[18,128]{1,0:T(8,128)S(1)}, f32[18,128]{1,0:T(8,128)S(1)}, u32[]{:S(2)}, u32[]{:S(2)}) %collective-permute-start.45) | collective-permute-done | bytes 9248 | tf_op jit(solution)/shard_map/ppermute | solution.py:394
  1143.4 5.9 fusion.20
  1149.3 14.2 %collective-permute-done.46 = f32[18,128]{1,0:T(8,128)S(1)} collective-permute-done((f32[18,128]{1,0:T(8,128)S(1)}, f32[18,128]{1,0:T(8,128)S(1)}, u32[]{:S(2)}, u32[]{:S(2)}) %collective-permute-start.46) | collective-permute-done | bytes 9248 | tf_op jit(solution)/shard_map/ppermute | solution.py:394
  (333 shorter events, 173.4 us)
Async XLA Ops:
  7.2 116.1 %all-gather.4.cloned.1.call-start = ((), (), s32[]{:S(2)}) async-start(), calls=%async_computation.4 | async-start | bytes 22282240 | tf_op jit(solution)/shard_map/all_gather | solution.py:836
  10.2 249.5 %all-gather.8.cloned.1.call-start = ((), (), s32[]{:S(2)}) async-start(), calls=%async_computation.6 | async-start | bytes 27852800 | tf_op jit(solution)/shard_map/all_gather | solution.py:843
  10.4 16.3 %collective-permute-start.3 = (bf16[256,1152]{1,0:T(8,128)(2,1)S(1)}, bf16[256,1152]{1,0:T(8,128)(2,1)S(1)}, u32[]{:S(2)}, u32[]{:S(2)}) collective-permute-start(bf16[256,1152]{1,0:T(8,128)(2,1)S(1)} %slice.401), channel_id=1, source_target_pairs={{0,1},{1,0},{2,3},{3,2},{4,5},{5,4},{6,7},{7,6},{8,9},{9,8},{10,11... | collective-permute-start | bytes 1769480 | tf_op jit(solution)/shard_map/ppermute | solution.py:341
  28.1 401.9 %all-gather.6.cloned.1.call-start = ((), (), s32[]{:S(2)}) async-start(), calls=%async_computation.5 | async-start | bytes 35651584 | tf_op jit(solution)/shard_map/all_gather | solution.py:864
  28.1 26.4 %collective-permute-start = (bf16[256,2048]{1,0:T(8,128)(2,1)S(1)}, bf16[256,2048]{1,0:T(8,128)(2,1)}, u32[]{:S(2)}, u32[]{:S(2)}) collective-permute-start(bf16[256,2048]{1,0:T(8,128)(2,1)S(1)} %copy-done.7), channel_id=1, source_target_pairs={{0,1},{1,0},{2,3},{3,2},{4,5},{5,4},{6,7},{7,6},{8,9},{9,8},{10,11... | collective-permute-start | bytes 3145736 | tf_op jit(solution)/shard_map/ppermute | solution.py:341
  162.1 25.4 %collective-permute-start.1 = (bf16[256,2048]{1,0:T(8,128)(2,1)S(1)}, bf16[256,2048]{1,0:T(8,128)(2,1)S(1)}, u32[]{:S(2)}, u32[]{:S(2)}) collective-permute-start(bf16[256,2048]{1,0:T(8,128)(2,1)S(1)} %select_convert_fusion.1), channel_id=1, source_target_pairs={{0,1},{1,0},{2,3},{3,2},{4,5},{5,4},{6,7},{7,6},{8,9},{9,8},{10,11... | collective-permute-start | bytes 3145736 | tf_op jit(solution)/shard_map/ppermute | solution.py:341
  190.3 24.7 %collective-permute-start.2 = (bf16[256,2048]{1,0:T(8,128)(2,1)S(1)}, bf16[256,2048]{1,0:T(8,128)(2,1)S(1)}, u32[]{:S(2)}, u32[]{:S(2)}) collective-permute-start(bf16[256,2048]{1,0:T(8,128)(2,1)S(1)} %multiply_convert_fusion), channel_id=1, source_target_pairs={{0,1},{1,0},{2,3},{3,2},{4,5},{5,4},{6,7},{7,6},{8,9},{9,8},{10,11... | collective-permute-start | bytes 3145736 | tf_op jit(solution)/shard_map/ppermute | solution.py:341
  266.6 160.5 %collective-permute-start.4 = (bf16[8,2,256,896]{3,2,1,0:T(8,128)(2,1)}, bf16[8,2,256,896]{3,2,1,0:T(8,128)(2,1)}, u32[]{:S(2)}, u32[]{:S(2)}) collective-permute-start(bf16[8,2,256,896]{3,2,1,0:T(8,128)(2,1)} %slice.403), channel_id=1, source_target_pairs={{0,1},{1,0},{2,3},{3,2},{4,5},{5,4},{6,7},{7,6},{8,9},{9,8},{10,11... | collective-permute-start | bytes 22020104 | tf_op jit(solution)/shard_map/ppermute | solution.py:341
  463.0 7.4 collective-permute-start.5
  475.3 48.1 %collective-permute-start.7 = (bf16[4,256,1024]{2,1,0:T(8,128)(2,1)}, bf16[4,256,1024]{2,1,0:T(8,128)(2,1)}, u32[]{:S(2)}, u32[]{:S(2)}) collective-permute-start(bf16[4,256,1024]{2,1,0:T(8,128)(2,1)} %get-tuple-element.137), channel_id=1, source_target_pairs={{0,1},{1,0},{2,3},{3,2},{4,5},{5,4},{6,7},{7,6},{8,9},{9,8},{10,11... | collective-permute-start | bytes 6291464 | tf_op jit(solution)/shard_map/ppermute | solution.py:341
  476.7 47.8 %collective-permute-start.8 = (bf16[4,256,1024]{2,1,0:T(8,128)(2,1)}, bf16[4,256,1024]{2,1,0:T(8,128)(2,1)}, u32[]{:S(2)}, u32[]{:S(2)}) collective-permute-start(bf16[4,256,1024]{2,1,0:T(8,128)(2,1)} %get-tuple-element.138), channel_id=1, source_target_pairs={{0,4},{2,6},{4,0},{6,2},{8,12},{10,14},{12,8},{14,10},{16,20},{18,... | collective-permute-start | bytes 6291464 | tf_op jit(solution)/shard_map/ppermute | solution.py:337
  524.6 35.5 %collective-permute-start.9 = (bf16[4,256,2048]{2,1,0:T(8,128)(2,1)}, bf16[4,256,2048]{2,1,0:T(8,128)(2,1)}, u32[]{:S(2)}, u32[]{:S(2)}) collective-permute-start(bf16[4,256,2048]{2,1,0:T(8,128)(2,1)} %get-tuple-element.139), channel_id=1, source_target_pairs={{0,2},{2,0},{4,6},{6,4},{8,10},{10,8},{12,14},{14,12},{16,18},{18,... | collective-permute-start | bytes 12582920 | tf_op jit(solution)/shard_map/ppermute | solution.py:333
  559.5 58.7 %collective-permute-start.6 = (bf16[4,256,2048]{2,1,0:T(8,128)(2,1)}, bf16[4,256,2048]{2,1,0:T(8,128)(2,1)}, u32[]{:S(2)}, u32[]{:S(2)}) collective-permute-start(bf16[4,256,2048]{2,1,0:T(8,128)(2,1)} %get-tuple-element.134), channel_id=1, source_target_pairs={{0,2},{2,0},{4,6},{6,4},{8,10},{10,8},{12,14},{14,12},{16,18},{18,... | collective-permute-start | bytes 12582920 | tf_op jit(solution)/shard_map/ppermute | solution.py:333
  564.6 42.1 %collective-permute-start.10 = (bf16[2,256,1024]{2,1,0:T(8,128)(2,1)S(1)}, bf16[2,256,1024]{2,1,0:T(8,128)(2,1)}, u32[]{:S(2)}, u32[]{:S(2)}) collective-permute-start(bf16[2,256,1024]{2,1,0:T(8,128)(2,1)S(1)} %get-tuple-element.149), channel_id=1, source_target_pairs={{0,1},{1,0},{2,3},{3,2},{4,5},{5,4},{6,7},{7,6},{8,9},{9,8},{10,11... | collective-permute-start | bytes 3145736 | tf_op jit(solution)/shard_map/ppermute | solution.py:341
  565.3 41.5 %collective-permute-start.11 = (bf16[2,256,1024]{2,1,0:T(8,128)(2,1)S(1)}, bf16[2,256,1024]{2,1,0:T(8,128)(2,1)}, u32[]{:S(2)}, u32[]{:S(2)}) collective-permute-start(bf16[2,256,1024]{2,1,0:T(8,128)(2,1)S(1)} %get-tuple-element.150), channel_id=1, source_target_pairs={{0,4},{2,6},{4,0},{6,2},{8,12},{10,14},{12,8},{14,10},{16,20},{18,... | collective-permute-start | bytes 3145736 | tf_op jit(solution)/shard_map/ppermute | solution.py:337
  568.1 44.5 %collective-permute-start.12 = (bf16[2,256,1024]{2,1,0:T(8,128)(2,1)S(1)}, bf16[2,256,1024]{2,1,0:T(8,128)(2,1)}, u32[]{:S(2)}, u32[]{:S(2)}) collective-permute-start(bf16[2,256,1024]{2,1,0:T(8,128)(2,1)S(1)} %add_convert_fusion.26), channel_id=1, source_target_pairs={{0,4},{2,6},{4,0},{6,2},{8,12},{10,14},{12,8},{14,10},{16,20},{18,... | collective-permute-start | bytes 3145736 | tf_op jit(solution)/shard_map/ppermute | solution.py:337
  571.6 41.1 %collective-permute-start.13 = (bf16[2,256,1024]{2,1,0:T(8,128)(2,1)}, bf16[2,256,1024]{2,1,0:T(8,128)(2,1)}, u32[]{:S(2)}, u32[]{:S(2)}) collective-permute-start(bf16[2,256,1024]{2,1,0:T(8,128)(2,1)} %add_convert_fusion.25), channel_id=1, source_target_pairs={{0,1},{1,0},{2,3},{3,2},{4,5},{5,4},{6,7},{7,6},{8,9},{9,8},{10,11... | collective-permute-start | bytes 3145736 | tf_op jit(solution)/shard_map/ppermute | solution.py:341
  612.7 21.9 %collective-permute-start.14 = (bf16[4,256,2048]{2,1,0:T(8,128)(2,1)}, bf16[4,256,2048]{2,1,0:T(8,128)(2,1)}, u32[]{:S(2)}, u32[]{:S(2)}) collective-permute-start(bf16[4,256,2048]{2,1,0:T(8,128)(2,1)} %get-tuple-element.155), channel_id=1, source_target_pairs={{0,2},{2,0},{4,6},{6,4},{8,10},{10,8},{12,14},{14,12},{16,18},{18,... | collective-permute-start | bytes 12582920 | tf_op jit(solution)/shard_map/ppermute | solution.py:333
  613.4 12.1 %all-to-all-start.1 = ((f32[32,1,256]{2,1,0:T(1,128)}), f32[32,1,256]{2,1,0:T(1,128)S(1)}, u32[]{:S(2)}, u32[]{:S(2)}) async-start(f32[32,1,256]{2,1,0:T(1,128)} %bitcast.159), calls=%async_computation.1 | async-start | bytes 65536 | tf_op jit(solution)/shard_map/all_to_all | solution.py:961
  618.1 523.3 %reduce-scatter.5.cloned.1.call-start = ((), (), s32[]{:S(2)}) async-start(), calls=%async_computation.8 | async-start | bytes 8912896 | tf_op jit(solution)/shard_map/reduce_scatter | solution.py:1026
  631.3 28.3 %collective-permute-start.19 = (bf16[256,2048]{1,0:T(8,128)(2,1)}, bf16[256,2048]{1,0:T(8,128)(2,1)S(1)}, u32[]{:S(2)}, u32[]{:S(2)}) collective-permute-start(bf16[256,2048]{1,0:T(8,128)(2,1)} %pad_maximum_fusion.11), channel_id=1, source_target_pairs={{0,24},{2,26},{4,28},{6,30},{8,0},{10,2},{12,4},{14,6},{16,8},{18,... | collective-permute-start | bytes 3145736 | tf_op jit(solution)/shard_map/ppermute | solution.py:358
  634.5 66.9 %collective-permute-start.20 = (bf16[256,2048]{1,0:T(8,128)(2,1)}, bf16[256,2048]{1,0:T(8,128)(2,1)S(1)}, u32[]{:S(2)}, u32[]{:S(2)}) collective-permute-start(bf16[256,2048]{1,0:T(8,128)(2,1)} %pad_maximum_fusion.12), channel_id=1, source_target_pairs={{0,16},{2,18},{4,20},{6,22},{8,24},{10,26},{12,28},{14,30},{16,0},... | collective-permute-start | bytes 3145736 | tf_op jit(solution)/shard_map/ppermute | solution.py:358
  639.0 62.4 %collective-permute-start.15 = (bf16[2,256,1024]{2,1,0:T(8,128)(2,1)}, bf16[2,256,1024]{2,1,0:T(8,128)(2,1)}, u32[]{:S(2)}, u32[]{:S(2)}) collective-permute-start(bf16[2,256,1024]{2,1,0:T(8,128)(2,1)} %get-tuple-element.156), channel_id=1, source_target_pairs={{0,1},{1,0},{2,3},{3,2},{4,5},{5,4},{6,7},{7,6},{8,9},{9,8},{10,11... | collective-permute-start | bytes 3145736 | tf_op jit(solution)/shard_map/ppermute | solution.py:341
  640.5 60.9 %collective-permute-start.16 = (bf16[2,256,1024]{2,1,0:T(8,128)(2,1)S(1)}, bf16[2,256,1024]{2,1,0:T(8,128)(2,1)}, u32[]{:S(2)}, u32[]{:S(2)}) collective-permute-start(bf16[2,256,1024]{2,1,0:T(8,128)(2,1)S(1)} %get-tuple-element.157), channel_id=1, source_target_pairs={{0,4},{2,6},{4,0},{6,2},{8,12},{10,14},{12,8},{14,10},{16,20},{18,... | collective-permute-start | bytes 3145736 | tf_op jit(solution)/shard_map/ppermute | solution.py:337
  644.6 56.8 %collective-permute-start.17 = (bf16[2,256,1024]{2,1,0:T(8,128)(2,1)}, bf16[2,256,1024]{2,1,0:T(8,128)(2,1)}, u32[]{:S(2)}, u32[]{:S(2)}) collective-permute-start(bf16[2,256,1024]{2,1,0:T(8,128)(2,1)} %add_convert_fusion.20), channel_id=1, source_target_pairs={{0,4},{2,6},{4,0},{6,2},{8,12},{10,14},{12,8},{14,10},{16,20},{18,... | collective-permute-start | bytes 3145736 | tf_op jit(solution)/shard_map/ppermute | solution.py:337
  659.6 41.8 %collective-permute-start.18 = (bf16[2,256,1024]{2,1,0:T(8,128)(2,1)}, bf16[2,256,1024]{2,1,0:T(8,128)(2,1)}, u32[]{:S(2)}, u32[]{:S(2)}) collective-permute-start(bf16[2,256,1024]{2,1,0:T(8,128)(2,1)} %add_convert_fusion.19), channel_id=1, source_target_pairs={{0,1},{1,0},{2,3},{3,2},{4,5},{5,4},{6,7},{7,6},{8,9},{9,8},{10,11... | collective-permute-start | bytes 3145736 | tf_op jit(solution)/shard_map/ppermute | solution.py:341
  701.5 7.4 collective-permute-start.22
  713.9 55.5 %collective-permute-start.25 = (bf16[12,256,2048]{2,1,0:T(8,128)(2,1)}, bf16[12,256,2048]{2,1,0:T(8,128)(2,1)S(1)}, u32[]{:S(2)}, u32[]{:S(2)}) collective-permute-start(bf16[12,256,2048]{2,1,0:T(8,128)(2,1)} %get-tuple-element.184), channel_id=1, source_target_pairs={{0,2},{2,0},{4,6},{6,4},{8,10},{10,8},{12,14},{14,12},{16,18},{18,... | collective-permute-start | bytes 37748744 | tf_op jit(solution)/shard_map/ppermute | solution.py:333
  718.7 28.0 %collective-permute-start.21 = (bf16[256,2048]{1,0:T(8,128)(2,1)S(1)}, bf16[256,2048]{1,0:T(8,128)(2,1)S(1)}, u32[]{:S(2)}, u32[]{:S(2)}) collective-permute-start(bf16[256,2048]{1,0:T(8,128)(2,1)S(1)} %pad_maximum_fusion.13), channel_id=1, source_target_pairs={{0,8},{2,10},{4,12},{6,14},{8,16},{10,18},{12,20},{14,22},{16,24},... | collective-permute-start | bytes 3145736 | tf_op jit(solution)/shard_map/ppermute | solution.py:358
  720.2 47.9 %collective-permute-start.23 = (bf16[4,256,1024]{2,1,0:T(8,128)(2,1)}, bf16[4,256,1024]{2,1,0:T(8,128)(2,1)S(1)}, u32[]{:S(2)}, u32[]{:S(2)}) collective-permute-start(bf16[4,256,1024]{2,1,0:T(8,128)(2,1)} %get-tuple-element.181), channel_id=1, source_target_pairs={{0,1},{1,0},{2,3},{3,2},{4,5},{5,4},{6,7},{7,6},{8,9},{9,8},{10,11... | collective-permute-start | bytes 6291464 | tf_op jit(solution)/shard_map/ppermute | solution.py:341
  721.7 47.6 %collective-permute-start.24 = (bf16[4,256,1024]{2,1,0:T(8,128)(2,1)}, bf16[4,256,1024]{2,1,0:T(8,128)(2,1)S(1)}, u32[]{:S(2)}, u32[]{:S(2)}) collective-permute-start(bf16[4,256,1024]{2,1,0:T(8,128)(2,1)} %get-tuple-element.182), channel_id=1, source_target_pairs={{0,4},{2,6},{4,0},{6,2},{8,12},{10,14},{12,8},{14,10},{16,20},{18,... | collective-permute-start | bytes 6291464 | tf_op jit(solution)/shard_map/ppermute | solution.py:337
  770.7 24.2 %collective-permute-start.26 = (bf16[256,2048]{1,0:T(8,128)(2,1)S(1)}, bf16[256,2048]{1,0:T(8,128)(2,1)}, u32[]{:S(2)}, u32[]{:S(2)}) collective-permute-start(bf16[256,2048]{1,0:T(8,128)(2,1)S(1)} %fusion.51), channel_id=1, source_target_pairs={{0,1},{1,0},{2,3},{3,2},{4,5},{5,4},{6,7},{7,6},{8,9},{9,8},{10,11... | collective-permute-start | bytes 3145736 | tf_op jit(solution)/shard_map/ppermute | solution.py:341
  805.6 337.1 %reduce-scatter.3.cloned.1.call-start = ((), (), s32[]{:S(2)}) async-start(), calls=%async_computation.7 | async-start | bytes 13369344 | tf_op jit(solution)/shard_map/reduce_scatter | solution.py:1033
  840.6 48.9 %collective-permute-start.27 = (bf16[4,256,1024]{2,1,0:T(8,128)(2,1)}, bf16[4,256,1024]{2,1,0:T(8,128)(2,1)}, u32[]{:S(2)}, u32[]{:S(2)}) collective-permute-start(bf16[4,256,1024]{2,1,0:T(8,128)(2,1)} %pad_maximum_fusion.6), channel_id=1, source_target_pairs={{0,1},{1,0},{2,3},{3,2},{4,5},{5,4},{6,7},{7,6},{8,9},{9,8},{10,11... | collective-permute-start | bytes 6291464 | tf_op jit(solution)/shard_map/ppermute | solution.py:341
  841.9 66.2 %collective-permute-start.28 = (bf16[4,256,1024]{2,1,0:T(8,128)(2,1)}, bf16[4,256,1024]{2,1,0:T(8,128)(2,1)}, u32[]{:S(2)}, u32[]{:S(2)}) collective-permute-start(bf16[4,256,1024]{2,1,0:T(8,128)(2,1)} %pad_maximum_fusion.5), channel_id=1, source_target_pairs={{0,4},{2,6},{4,0},{6,2},{8,12},{10,14},{12,8},{14,10},{16,20},{18,... | collective-permute-start | bytes 6291464 | tf_op jit(solution)/shard_map/ppermute | solution.py:337
  847.3 86.4 %collective-permute-start.29 = (bf16[4,256,1024]{2,1,0:T(8,128)(2,1)}, bf16[4,256,1024]{2,1,0:T(8,128)(2,1)}, u32[]{:S(2)}, u32[]{:S(2)}) collective-permute-start(bf16[4,256,1024]{2,1,0:T(8,128)(2,1)} %add_convert_fusion.1), channel_id=1, source_target_pairs={{0,1},{1,0},{2,3},{3,2},{4,5},{5,4},{6,7},{7,6},{8,9},{9,8},{10,11... | collective-permute-start | bytes 6291464 | tf_op jit(solution)/shard_map/ppermute | solution.py:341
  950.4 63.3 %collective-permute-start.30 = (bf16[4,256,1024]{2,1,0:T(8,128)(2,1)}, bf16[4,256,1024]{2,1,0:T(8,128)(2,1)}, u32[]{:S(2)}, u32[]{:S(2)}) collective-permute-start(bf16[4,256,1024]{2,1,0:T(8,128)(2,1)} %add_convert_fusion), channel_id=1, source_target_pairs={{0,4},{2,6},{4,0},{6,2},{8,12},{10,14},{12,8},{14,10},{16,20},{18,... | collective-permute-start | bytes 6291464 | tf_op jit(solution)/shard_map/ppermute | solution.py:337
  951.1 7.9 collective-permute-start.37
  959.0 77.5 %collective-permute-start.38 = (f32[4,33,128]{2,0,1:T(4,128)S(1)}, f32[4,33,128]{2,0,1:T(4,128)S(1)}, u32[]{:S(2)}, u32[]{:S(2)}) collective-permute-start(f32[4,33,128]{2,0,1:T(4,128)S(1)} %dynamic-slice_bitcast_fusion.1), channel_id=1, source_target_pairs={{0,8},{2,10},{4,12},{6,14},{8,0},{10,2},{12,4},{14,6},{16,24},{18,... | collective-permute-start | bytes 202760 | tf_op jit(solution)/shard_map/ppermute | solution.py:406
  1035.2 19.0 %collective-permute-start.34 = (bf16[256,2048]{1,0:T(8,128)(2,1)}, bf16[256,2048]{1,0:T(8,128)(2,1)}, u32[]{:S(2)}, u32[]{:S(2)}) collective-permute-start(bf16[256,2048]{1,0:T(8,128)(2,1)} %select_convert_fusion), channel_id=1, source_target_pairs={{0,1},{1,0},{2,3},{3,2},{4,5},{5,4},{6,7},{7,6},{8,9},{9,8},{10,11... | collective-permute-start | bytes 3145736 | tf_op jit(solution)/shard_map/ppermute | solution.py:341
  1042.3 16.7 %collective-permute-start.41 = (f32[33,128]{1,0:T(8,128)S(1)}, f32[33,128]{1,0:T(8,128)S(1)}, u32[]{:S(2)}, u32[]{:S(2)}) collective-permute-start(f32[33,128]{1,0:T(8,128)S(1)} %bitcast.176), channel_id=1, source_target_pairs={{0,1},{1,0},{2,3},{3,2},{4,5},{5,4},{6,7},{7,6},{8,9},{9,8},{10,11... | collective-permute-start | bytes 50696 | tf_op jit(solution)/shard_map/ppermute | solution.py:341
  1042.9 99.8 %collective-permute-start.33 = (bf16[256,2048]{1,0:T(8,128)(2,1)}, bf16[256,2048]{1,0:T(8,128)(2,1)}, u32[]{:S(2)}, u32[]{:S(2)}) collective-permute-start(bf16[256,2048]{1,0:T(8,128)(2,1)} %pad_maximum_fusion.17), channel_id=1, source_target_pairs={{0,8},{2,10},{4,12},{6,14},{8,16},{10,18},{12,20},{14,22},{16,24},... | collective-permute-start | bytes 3145736 | tf_op jit(solution)/shard_map/ppermute | solution.py:358
  1044.5 98.9 %collective-permute-start.32 = (bf16[256,2048]{1,0:T(8,128)(2,1)}, bf16[256,2048]{1,0:T(8,128)(2,1)}, u32[]{:S(2)}, u32[]{:S(2)}) collective-permute-start(bf16[256,2048]{1,0:T(8,128)(2,1)} %pad_maximum_fusion.16), channel_id=1, source_target_pairs={{0,16},{2,18},{4,20},{6,22},{8,24},{10,26},{12,28},{14,30},{16,0},... | collective-permute-start | bytes 3145736 | tf_op jit(solution)/shard_map/ppermute | solution.py:358
  1047.4 96.0 %collective-permute-start.31 = (bf16[256,2048]{1,0:T(8,128)(2,1)}, bf16[256,2048]{1,0:T(8,128)(2,1)}, u32[]{:S(2)}, u32[]{:S(2)}) collective-permute-start(bf16[256,2048]{1,0:T(8,128)(2,1)} %pad_maximum_fusion.15), channel_id=1, source_target_pairs={{0,24},{2,26},{4,28},{6,30},{8,0},{10,2},{12,4},{14,6},{16,8},{18,... | collective-permute-start | bytes 3145736 | tf_op jit(solution)/shard_map/ppermute | solution.py:358
  1067.8 72.9 %collective-permute-start.45 = (f32[18,128]{1,0:T(8,128)S(1)}, f32[18,128]{1,0:T(8,128)S(1)}, u32[]{:S(2)}, u32[]{:S(2)}) collective-permute-start(f32[18,128]{1,0:T(8,128)S(1)} %add.672), channel_id=1, source_target_pairs={{0,8},{2,10},{4,12},{6,14},{8,0},{10,2},{12,4},{14,6},{16,24},{18,... | collective-permute-start | bytes 27656 | tf_op jit(solution)/shard_map/ppermute | solution.py:394
  1140.7 22.8 %collective-permute-start.46 = (f32[18,128]{1,0:T(8,128)S(1)}, f32[18,128]{1,0:T(8,128)S(1)}, u32[]{:S(2)}, u32[]{:S(2)}) collective-permute-start(f32[18,128]{1,0:T(8,128)S(1)} %add.673), channel_id=1, source_target_pairs={{0,16},{2,18},{4,20},{6,22},{8,24},{10,26},{12,28},{14,30},{16,0},... | collective-permute-start | bytes 27656 | tf_op jit(solution)/shard_map/ppermute | solution.py:394
  1141.4 23.4 %collective-permute-start.36 = (bf16[128,2048]{1,0:T(8,128)(2,1)}, bf16[128,2048]{1,0:T(8,128)(2,1)}, u32[]{:S(2)}, u32[]{:S(2)}) collective-permute-start(bf16[128,2048]{1,0:T(8,128)(2,1)} %reduce-scatter.5.cloned.1.call-done), channel_id=1, source_target_pairs={{0,1},{1,0},{2,3},{3,2},{4,5},{5,4},{6,7},{7,6},{8,9},{9,8},{10,11... | collective-permute-start | bytes 1572872 | tf_op jit(solution)/shard_map/ppermute | solution.py:341
  1142.7 29.2 %collective-permute-start.35 = (bf16[128,3072]{1,0:T(8,128)(2,1)}, bf16[128,3072]{1,0:T(8,128)(2,1)}, u32[]{:S(2)}, u32[]{:S(2)}) collective-permute-start(bf16[128,3072]{1,0:T(8,128)(2,1)} %reduce-scatter.3.cloned.1.call-done.mine_ref), channel_id=1, source_target_pairs={{0,1},{1,0},{2,3},{3,2},{4,5},{5,4},{6,7},{7,6},{8,9},{9,8},{10,11... | collective-permute-start | bytes 2359304 | tf_op jit(solution)/shard_map/ppermute | solution.py:341
  (73 other events, 1625.3 us)
Sparse Core Ops, SparseCore 0:
  10.4 112.8 all-gather.3
  125.4 134.2 all-gather.7
  261.9 168.0 all-gather.5
  805.7 119.6 reduce-scatter.4
  945.9 186.5 reduce-scatter.2

commit v10 on v8

--- a/solution.py
+++ b/solution.py
@@ -363,6 +363,15 @@
     for item in arrived.values():
         total = total + item.astype(full)
     return total
+
+
+def line_halving(entries, place):
+    fsdp = lax.axis_size("fsdp")
+    even = place % 2 == 0
+    one, two = jnp.where(even, entries[3], entries[1]), jnp.where(even, entries[1], entries[3])
+    one, two = (lax.ppermute(item, "fsdp", [(i, i ^ 4) for i in range(fsdp)]) for item in (one, two))
+    far = lax.ppermute(add_low(entries[2], two), "fsdp", [(i, i ^ 8) for i in range(fsdp)])
+    return entries[0].astype(full) + one.astype(full) + far.astype(full)
 
 
 def joined(places, own, got):
@@ -1013,16 +1022,16 @@
     grad_projected = jnp.concatenate([grad_q, grad_k, grad_v], axis=1)
     grad_projected, (got[0], got[1]) = hold(grad_projected, (got[0], got[1]))
     grad_qkv_part = mul(low_in, grad_projected, lhs_turned).astype(low)
-    grad_projected, got = hold(grad_projected, got)
+    grad_gate_up = mul(rows, grad_pair, lhs_turned)[None]
+    got, grad_gate_up = hold(got, grad_gate_up)
     entries = joined(places, out_own, got)
-    grad_projected, entries, rows, grad_pair, hidden, grad_rows = lax.optimization_barrier(
-        (grad_projected, entries, rows, grad_pair, hidden, grad_rows)
-    )
-    arrived = {p: line_shift(entries[p], lines - p) for p in places[:-1]}
+    if lines == 4:
+        output = (mixed + line_halving(entries, place)).astype(low)
+    else:
+        output = (
+            mixed + line_total(entries[0], {p: line_shift(entries[p], lines - p) for p in places[:-1]})
+        ).astype(low)
     grad_normed_part = mul(grad_projected, qkv_all, rhs_turned)
-    grad_gate_up = mul(rows, grad_pair, lhs_turned)[None]
-    grad_down = mul(hidden, grad_rows, lhs_turned)[None]
-    output = (mixed + line_total(entries[0], arrived)).astype(low)
     grad_normed = of_block(grad_normed_part, rank) + swap_ctx(
         of_block(grad_normed_part, 1 - rank).astype(low)
     ).astype(full)
@@ -1038,7 +1047,8 @@
     )
     qkv_mine = lax.psum_scatter(grad_qkv_part, "fsdp", scatter_dimension=0, tiled=True)
     grad_qkv = all_heads(rank_at, qkv_mine, swap_ctx(qkv_mine), head_dim, my_heads)
-    early = sum_owned(jnp.concatenate([grad_router.T, grad_moe_gain[None]], axis=0), fsdp, spot)
+    early, got = hold(jnp.concatenate([grad_router.T, grad_moe_gain[None]], axis=0), got)
+    early = sum_owned(early, fsdp, spot)
     late = sum_all(
         jnp.concatenate(
             [
@@ -1050,6 +1060,8 @@
         ),
         fsdp,
     )
+    (hidden, grad_rows), late = hold((hidden, grad_rows), late)
+    grad_down = mul(hidden, grad_rows, lhs_turned)[None]
     gain_rows = width // head_dim
     return (
         output,

time: 1170 us -> 1160 us (level)
    ppermute x8, waiting for transfers between devices: 125 us -> 79.3 us  [swap_side(): return lax.ppermute(values, 'fsdp', side_pairs(lax.axis_size('fsdp')))]
    ppermute x0 -> x3, waiting for transfers between devices: none -> 39.8 us  [the longest x2 25.5 us: line_halving(): lax.ppermute(item, 'fsdp', [(i, i ^ 4) for i in range(fsdp)])]
    ppermute x3, waiting for transfers between devices: 37.1 us -> 10.1 us  [sum_all(): lax.ppermute(values, 'fsdp', [(i, i ^ step) for i in range(fsdp)])]
    ppermute x4, waiting for transfers between devices: 11.4 us -> 30.4 us  [sum_owned(): lax.ppermute(take(values, 1 - bit), 'fsdp', [(i, i ^ step) for i in range...]
    convert_element_type x19 -> x20, other arithmetic: 68.3 us -> 71.8 us  [add_low(): return (one.astype(full) + two.astype(full)).astype(low)]
    ppermute x6 -> x3, waiting for transfers between devices: 38.9 us -> 38.8 us  [line_shift(): lax.ppermute(values, 'fsdp', [(i, (i + 4 * step) % fsdp) for i in range(f...]
  transfers between devices with their start and end apart: 53 -> 53, of which waited for: 26 -> 28; matrix products, arithmetic and copies ran while one was open for 19% -> 19% of each run, Pallas kernels for 16% -> 16%
where the time goes in v10:
time: 1160 us; the launch traced here: 1150 us
  waiting for transfers between devices  571 us (49%)
  Pallas kernels  224 us (19%)
  matrix products  111 us (10%)
  other arithmetic  109 us (9%)
  starting transfers between devices  52.8 us (5%)
  blocking collectives  35.6 us (3%)
  local copies, waits for them, and re-layouts  30.4 us (3%)
  between operations  15.4 us (1%)
    ppermute x19, waiting for transfers between devices, swap_ctx(): return lax.ppermute(values, 'ctx', [(0, 1), (1, 0)])  267 us
    pallas_call x4, Pallas kernels, run_expert(): pl.pallas_call(expert_kernel, grid_spec=grid_spec, out_shape=[shape((step...  135 us
    dot_general x11, matrix products, mul(): return lax.dot_general(left, right, dims, preferred_element_type=full)  111 us
    ppermute x8, waiting for transfers between devices, swap_side(): return lax.ppermute(values, 'fsdp', side_pairs(lax.axis_size('fsdp')))  79.3 us
    convert_element_type x20, other arithmetic, add_low(): return (one.astype(full) + two.astype(full)).astype(low)  71.8 us
    all_gather x1, waiting for transfers between devices, body_gathered(): weights_all = lax.all_gather(weights_local, 'fsdp', axis=0, tiled=True)  65.6 us
    pallas_call x2, Pallas kernels, run_result(): pl.pallas_call(result_kernel, grid_spec=pltpu.PrefetchScalarGridSpec(num_...  40.2 us
    ppermute x3, waiting for transfers between devices, line_shift(): lax.ppermute(values, 'fsdp', [(i, (i + 4 * step) % fsdp) for i in range(f...  38.8 us
  transfers between devices with their start and end apart: 53, of which 28 were waited for; matrix products, arithmetic and copies ran while one was open for 19% of the time, Pallas kernels for 16%

profile of v10, /device:TPU:0, one launch (start us, length us, event | category | flops | bytes accessed | tf_op | source)
XLA Modules:
  0.0 1149.9 jit_solution(8662074012430474165)
XLA Ops:
  13.4 13.3 %collective-permute-done.3 = bf16[256,1152]{1,0:T(8,128)(2,1)S(1)} collective-permute-done((bf16[256,1152]{1,0:T(8,128)(2,1)S(1)}, bf16[256,1152]{1,0:T(8,128)(2,1)S(1)}, u32[]{:S(2)}, u32[]{:S(2)}) %collective-permute-start.3) | collective-permute-done | bytes 589856 | tf_op jit(solution)/shard_map/ppermute | solution.py:341
  31.2 22.9 %all_gather.12 = bf16[2048,34]{0,1:T(8,128)(2,1)S(1)} all-gather(bf16[128,34]{0,1:T(8,128)(2,1)S(1)} %pad_maximum_fusion.20), channel_id=1, replica_groups=mesh['fsdp'=16,'ctx'=2] {'fsdp'}, dimensions={0}, use_global_device_ids=true | all-gather | bytes 147968 | tf_op jit(solution)/shard_map/all_gather | solution.py:844
  57.6 65.6 %all-gather.4.cloned.1.call-done = bf16[2048,5120]{1,0:T(8,128)(2,1)} async-done(((bf16[128,5120]{1,0:T(8,128)(2,1)}), bf16[2048,5120]{1,0:T(8,128)(2,1)}) %all-gather.4.cloned.1.call-update) | async-done | bytes 20971536 | tf_op jit(solution)/shard_map/all_gather | solution.py:845
  123.2 11.5 fusion.2.q_ref.k_ref.v_ref
  134.7 18.2 %attend.1 = (bf16[512,2048]{1,0:T(8,128)(2,1)S(1)}, bf16[512,2048]{1,0:T(8,128)(2,1)S(1)}, bf16[512,512]{1,0:T(8,128)(2,1)S(1)}, bf16[512,512]{1,0:T(8,128)(2,1)S(1)}) custom-call(f32[512,3072]{1,0:T(8,128)} %fusion.2.q_ref.k_ref.v_ref, f32[512,3072]{1,0:T(8,128)} %fusion.2.q_ref.k_ref.v_ref, f32[512,3072]{1,0:T(8,128)} %fusion.2.q_ref.k_ref.v_ref, ...), custom_call_target="tpu_custom_call" | custom-call | flops 2147483648 | bytes 9437184 | tf_op jit(solution)/shard_map/attend/pallas_call | solution.py:530
  153.0 8.4 fusion.6
  163.5 23.8 %collective-permute-done.1 = bf16[256,2048]{1,0:T(8,128)(2,1)S(1)} collective-permute-done((bf16[256,2048]{1,0:T(8,128)(2,1)S(1)}, bf16[256,2048]{1,0:T(8,128)(2,1)S(1)}, u32[]{:S(2)}, u32[]{:S(2)}) %collective-permute-start.1) | collective-permute-done | bytes 1048608 | tf_op jit(solution)/shard_map/ppermute | solution.py:341
  191.8 23.1 %collective-permute-done.2 = bf16[256,2048]{1,0:T(8,128)(2,1)S(1)} collective-permute-done((bf16[256,2048]{1,0:T(8,128)(2,1)S(1)}, bf16[256,2048]{1,0:T(8,128)(2,1)S(1)}, u32[]{:S(2)}, u32[]{:S(2)}) %collective-permute-start.2) | collective-permute-done | bytes 1048608 | tf_op jit(solution)/shard_map/ppermute | solution.py:341
  218.4 12.8 %all_to_all.24 = f32[32,1,256]{2,1,0:T(1,128)S(1)} all-to-all(f32[32,1,256]{2,1,0:T(1,128)S(1)} %copy.60), channel_id=1, replica_groups=mesh['fsdp'=16,'ctx'=2] {'fsdp','ctx'}, dimensions={0} | all-to-all | bytes 65536 | tf_op jit(solution)/shard_map/all_to_all | solution.py:882
  231.2 28.5 %all-gather.8.cloned.1.call-done = bf16[4096,3200]{1,0:T(8,128)(2,1)} async-done(((bf16[256,3200]{1,0:T(8,128)(2,1)}), bf16[4096,3200]{1,0:T(8,128)(2,1)}) %all-gather.8.cloned.1.call-update) | async-done | bytes 26214416 | tf_op jit(solution)/shard_map/all_gather | solution.py:852
  259.7 6.9 slice.403
  269.4 157.7 %collective-permute-done.4.far_ref = bf16[8,2,256,896]{3,2,1,0:T(8,128)(2,1)} collective-permute-done((bf16[8,2,256,896]{3,2,1,0:T(8,128)(2,1)}, bf16[8,2,256,896]{3,2,1,0:T(8,128)(2,1)}, u32[]{:S(2)}, u32[]{:S(2)}) %collective-permute-start.4) | collective-permute-done | bytes 7340064 | tf_op jit(solution)/shard_map/ppermute | solution.py:341
  429.9 33.1 %experts.4 = (bf16[4,256,2048]{2,1,0:T(8,128)(2,1)}, bf16[4,256,2048]{2,1,0:T(8,128)(2,1)}, f32[8,2,2,1,256]{4,3,2,1,0:T(1,128)}, bf16[4096,2048]{1,0:T(8,128)(2...) custom-call(s32[1]{0:T(128)} %bitcast.6.core_ref, s32[16]{0:T(128)} %stack.35.order, ...), custom_call_target="tpu_custom_call" | custom-call | flops 19327352832 | bytes 38273024 | tf_op jit(solution)/shard_map/experts/pallas_call | solution.py:679
  463.3 7.1 collective-permute-done.5
  470.5 4.8 add_convert_fusion.8
  478.5 34.2 %experts.5 = (bf16[4,256,2048]{2,1,0:T(8,128)(2,1)}, bf16[4,256,2048]{2,1,0:T(8,128)(2,1)}, f32[8,2,2,1,256]{4,3,2,1,0:T(1,128)}, bf16[4096,2048]{1,0:T(8,128)(2...) custom-call(s32[1]{0:T(128)} %bitcast.6.core_ref, ...), custom_call_target="tpu_custom_call", output_to_operand_aliasing={{2}: (8, {}), {3}: (9, {}), {4}: (10, {}), {5}: (11, {}), {... | custom-call | flops 19327352832 | bytes 38273024 | tf_op jit(solution)/shard_map/experts/pallas_call | solution.py:679
  512.7 10.7 collective-permute-done.7
  525.9 33.7 %experts.6 = (bf16[4,256,2048]{2,1,0:T(8,128)(2,1)}, bf16[4,256,2048]{2,1,0:T(8,128)(2,1)}, f32[8,2,2,1,256]{4,3,2,1,0:T(1,128)}, bf16[4096,2048]{1,0:T(8,128)(2...) custom-call(s32[1]{0:T(128)} %bitcast.6.core_ref, ...), custom_call_target="tpu_custom_call", output_to_operand_aliasing={{2}: (8, {}), {3}: (9, {}), {4}: (10, {}), {5}: (11, {}), {... | custom-call | flops 19327352832 | bytes 38273024 | tf_op jit(solution)/shard_map/experts/pallas_call | solution.py:679
  573.1 33.7 %experts.7 = (bf16[4,256,2048]{2,1,0:T(8,128)(2,1)}, bf16[4,256,2048]{2,1,0:T(8,128)(2,1)}, f32[8,2,2,1,256]{4,3,2,1,0:T(1,128)}, bf16[4096,2048]{1,0:T(8,128)(2...) custom-call(s32[1]{0:T(128)} %bitcast.6.core_ref, ...), custom_call_target="tpu_custom_call", output_to_operand_aliasing={{2}: (8, {}), {3}: (9, {}), {4}: (10, {}), {5}: (11, {}), {... | custom-call | flops 19327352832 | bytes 38273024 | tf_op jit(solution)/shard_map/experts/pallas_call | solution.py:679
  606.8 5.9 collective-permute-done.12
  613.4 4.7 all-to-all-start.1
  618.2 5.7 add_convert_fusion.7
  647.8 11.9 %results.2 = (bf16[4,256,2048]{2,1,0:T(8,128)(2,1)}, bf16[4,256,2048]{2,1,0:T(8,128)(2,1)}) custom-call(s32[1]{0:T(128)} %bitcast.6.core_ref, s32[16]{0:T(128)} %stack.35.order, bf16[4096,768]{1,0:T(8,128)(2,1)} %get-tuple-element.213.z_ref, f32[8,2,2,1,256]{4,3,2,1,0:T(1,128)} %reshape.271.w_ref, bf16[768,2048]{1,0:T(8,128)(2,1)} %bitcast.154), custom_call_target="tpu_custom_call" | custom-call | flops 4294967296 | bytes 13107200 | tf_op jit(solution)/shard_map/results/pallas_call | solution.py:710
  660.2 28.3 %results.3 = (bf16[12,256,2048]{2,1,0:T(8,128)(2,1)}, bf16[12,256,2048]{2,1,0:T(8,128)(2,1)}) custom-call(s32[1]{0:T(128)} %bitcast.6.core_ref, s32[48]{0:T(128)} %stack.44.order, bf16[4096,768]{1,0:T(8,128)(2,1)} %get-tuple-element.213.z_ref, f32[8,2,2,1,256]{4,3,2,1,0:T(1,128)} %reshape.271.w_ref, bf16[768,2048]{1,0:T(8,128)(2,1)} %bitcast.155), custom_call_target="tpu_custom_call" | custom-call | flops 12884901888 | bytes 33030144 | tf_op jit(solution)/shard_map/results/pallas_call | solution.py:710
  688.5 12.8 %collective-permute-done.20 = bf16[256,2048]{1,0:T(8,128)(2,1)S(1)} collective-permute-done((bf16[256,2048]{1,0:T(8,128)(2,1)}, bf16[256,2048]{1,0:T(8,128)(2,1)S(1)}, u32[]{:S(2)}, u32[]{:S(2)}) %collective-permute-start.20) | collective-permute-done | bytes 1048608 | tf_op jit(solution)/shard_map/ppermute | solution.py:358
  709.5 26.0 %collective-permute-done.21 = bf16[256,2048]{1,0:T(8,128)(2,1)S(1)} collective-permute-done((bf16[256,2048]{1,0:T(8,128)(2,1)S(1)}, bf16[256,2048]{1,0:T(8,128)(2,1)S(1)}, u32[]{:S(2)}, u32[]{:S(2)}) %collective-permute-start.21) | collective-permute-done | bytes 1048608 | tf_op jit(solution)/shard_map/ppermute | solution.py:358
  740.0 6.1 add_convert_fusion.2
  747.6 5.1 add_convert_fusion.13
  764.6 6.1 collective-permute-done.24
  774.6 6.8 convolution_convert_fusion.1
  785.7 10.6 fusion.11.go_ref
  796.3 45.4 %collective-permute-done.26 = bf16[4,256,1024]{2,1,0:T(8,128)(2,1)S(1)} collective-permute-done((bf16[4,256,1024]{2,1,0:T(8,128)(2,1)}, bf16[4,256,1024]{2,1,0:T(8,128)(2,1)S(1)}, u32[]{:S(2)}, u32[]{:S(2)}) %collective-permute-start.26) | collective-permute-done | bytes 2097184 | tf_op jit(solution)/shard_map/ppermute | solution.py:337
  843.6 25.2 %attend_grad.1 = (bf16[512,2048]{1,0:T(8,128)(2,1)S(1)}, bf16[512,512]{1,0:T(8,128)(2,1)S(1)}, bf16[512,512]{1,0:T(8,128)(2,1)S(1)}, f32[4,1,128]{2,1,0:T(1,128)S(1)}, f32[4,1,128]{2,1,0:T(1,128)S(1)}) custom-call(f32[512,3072]{1,0:T(8,128)} %fusion.2.q_ref.k_ref.v_ref, f32[512,3072]{1,0:T(8,128)} %fusion.2.q_ref.k_ref.v_ref, bf16[512,2048]{1,0:T(8,128)(2,1)} %copy-done, ...), custom_call_target="tpu_custom_call" | custom-call | flops 5368709120 | bytes 15728640 | tf_op jit(solution)/shard_map/attend_grad/pallas_call | solution.py:554
  869.2 5.0 collective-permute-done.27
  874.2 26.9 %collective-permute-done.28 = bf16[4,256,1024]{2,1,0:T(8,128)(2,1)} collective-permute-done((bf16[4,256,1024]{2,1,0:T(8,128)(2,1)}, bf16[4,256,1024]{2,1,0:T(8,128)(2,1)}, u32[]{:S(2)}, u32[]{:S(2)}) %collective-permute-start.28) | collective-permute-done | bytes 2097184 | tf_op jit(solution)/shard_map/ppermute | solution.py:337
  901.1 10.0 convolution_convert_fusion
  911.2 10.9 fusion
  926.8 5.2 add_convert_fusion.1
  933.6 14.7 %collective-permute-done.34 = bf16[256,2048]{1,0:T(8,128)(2,1)} collective-permute-done((bf16[256,2048]{1,0:T(8,128)(2,1)}, bf16[256,2048]{1,0:T(8,128)(2,1)}, u32[]{:S(2)}, u32[]{:S(2)}) %collective-permute-start.34) | collective-permute-done | bytes 1048608 | tf_op jit(solution)/shard_map/ppermute | solution.py:341
  956.0 34.9 %convolution_bitcast_fusion = f32[1,2048,1536]{2,1,0:T(8,128)} fusion(bf16[4096,2048]{1,0:T(8,128)(2,1)} %get-tuple-element.199, bf16[4096,1536]{1,0:T(8,128)(2,1)} %get-tuple-element.200), kind=kOutput, calls=%fused_computation.5 | convolution fusion | flops 25769803776 | bytes 41943040 | tf_op jit(solution)/shard_map/dot_general | solution.py:321
  991.0 11.2 collective-permute-done.43
  1015.6 4.7 fusion.33
  1020.3 4.8 fusion.32
  1030.4 15.7 %convolution_bitcast_fusion.1 = f32[1,768,2048]{2,1,0:T(8,128)} fusion(bf16[4096,768]{1,0:T(8,128)(2,1)S(1)} %bitcast.149, bf16[4096,2048]{1,0:T(8,128)(2,1)S(1)} %bitcast.143), kind=kOutput, calls=%fused_computation.26 | convolution fusion | flops 12884901888 | bytes 29360128 | tf_op jit(solution)/shard_map/dot_general | solution.py:321
  1046.0 28.5 %collective-permute-done.38 = f32[4,33,128]{2,0,1:T(4,128)} collective-permute-done((f32[4,33,128]{2,0,1:T(4,128)}, f32[4,33,128]{2,0,1:T(4,128)}, u32[]{:S(2)}, u32[]{:S(2)}) %collective-permute-start.38) | collective-permute-done | bytes 67616 | tf_op jit(solution)/shard_map/ppermute | solution.py:415
  1091.9 25.5 %collective-permute-done.31 = bf16[256,2048]{1,0:T(8,128)(2,1)} collective-permute-done((bf16[256,2048]{1,0:T(8,128)(2,1)}, bf16[256,2048]{1,0:T(8,128)(2,1)}, u32[]{:S(2)}, u32[]{:S(2)}) %collective-permute-start.31) | collective-permute-done | bytes 1048608 | tf_op jit(solution)/shard_map/ppermute | solution.py:372
  1117.4 14.3 %collective-permute-done.33 = bf16[256,2048]{1,0:T(8,128)(2,1)} collective-permute-done((bf16[256,2048]{1,0:T(8,128)(2,1)}, bf16[256,2048]{1,0:T(8,128)(2,1)}, u32[]{:S(2)}, u32[]{:S(2)}) %collective-permute-start.33) | collective-permute-done | bytes 1048608 | tf_op jit(solution)/shard_map/ppermute | solution.py:373
  1131.8 5.3 fusion.20
  (343 shorter events, 166.2 us)
Async XLA Ops:
  7.2 116.1 %all-gather.4.cloned.1.call-start = ((), (), s32[]{:S(2)}) async-start(), calls=%async_computation.4 | async-start | bytes 22282240 | tf_op jit(solution)/shard_map/all_gather | solution.py:845
  10.2 249.5 %all-gather.8.cloned.1.call-start = ((), (), s32[]{:S(2)}) async-start(), calls=%async_computation.6 | async-start | bytes 27852800 | tf_op jit(solution)/shard_map/all_gather | solution.py:852
  10.4 16.3 %collective-permute-start.3 = (bf16[256,1152]{1,0:T(8,128)(2,1)S(1)}, bf16[256,1152]{1,0:T(8,128)(2,1)S(1)}, u32[]{:S(2)}, u32[]{:S(2)}) collective-permute-start(bf16[256,1152]{1,0:T(8,128)(2,1)S(1)} %slice.401), channel_id=1, source_target_pairs={{0,1},{1,0},{2,3},{3,2},{4,5},{5,4},{6,7},{7,6},{8,9},{9,8},{10,11... | collective-permute-start | bytes 1769480 | tf_op jit(solution)/shard_map/ppermute | solution.py:341
  28.1 401.9 %all-gather.6.cloned.1.call-start = ((), (), s32[]{:S(2)}) async-start(), calls=%async_computation.5 | async-start | bytes 35651584 | tf_op jit(solution)/shard_map/all_gather | solution.py:873
  28.1 26.4 %collective-permute-start = (bf16[256,2048]{1,0:T(8,128)(2,1)S(1)}, bf16[256,2048]{1,0:T(8,128)(2,1)}, u32[]{:S(2)}, u32[]{:S(2)}) collective-permute-start(bf16[256,2048]{1,0:T(8,128)(2,1)S(1)} %copy-done.7), channel_id=1, source_target_pairs={{0,1},{1,0},{2,3},{3,2},{4,5},{5,4},{6,7},{7,6},{8,9},{9,8},{10,11... | collective-permute-start | bytes 3145736 | tf_op jit(solution)/shard_map/ppermute | solution.py:341
  162.0 25.4 %collective-permute-start.1 = (bf16[256,2048]{1,0:T(8,128)(2,1)S(1)}, bf16[256,2048]{1,0:T(8,128)(2,1)S(1)}, u32[]{:S(2)}, u32[]{:S(2)}) collective-permute-start(bf16[256,2048]{1,0:T(8,128)(2,1)S(1)} %select_convert_fusion.1), channel_id=1, source_target_pairs={{0,1},{1,0},{2,3},{3,2},{4,5},{5,4},{6,7},{7,6},{8,9},{9,8},{10,11... | collective-permute-start | bytes 3145736 | tf_op jit(solution)/shard_map/ppermute | solution.py:341
  190.3 24.7 %collective-permute-start.2 = (bf16[256,2048]{1,0:T(8,128)(2,1)S(1)}, bf16[256,2048]{1,0:T(8,128)(2,1)S(1)}, u32[]{:S(2)}, u32[]{:S(2)}) collective-permute-start(bf16[256,2048]{1,0:T(8,128)(2,1)S(1)} %multiply_convert_fusion), channel_id=1, source_target_pairs={{0,1},{1,0},{2,3},{3,2},{4,5},{5,4},{6,7},{7,6},{8,9},{9,8},{10,11... | collective-permute-start | bytes 3145736 | tf_op jit(solution)/shard_map/ppermute | solution.py:341
  266.6 160.5 %collective-permute-start.4 = (bf16[8,2,256,896]{3,2,1,0:T(8,128)(2,1)}, bf16[8,2,256,896]{3,2,1,0:T(8,128)(2,1)}, u32[]{:S(2)}, u32[]{:S(2)}) collective-permute-start(bf16[8,2,256,896]{3,2,1,0:T(8,128)(2,1)} %slice.403), channel_id=1, source_target_pairs={{0,1},{1,0},{2,3},{3,2},{4,5},{5,4},{6,7},{7,6},{8,9},{9,8},{10,11... | collective-permute-start | bytes 22020104 | tf_op jit(solution)/shard_map/ppermute | solution.py:341
  463.0 7.4 collective-permute-start.5
  475.3 48.1 %collective-permute-start.7 = (bf16[4,256,1024]{2,1,0:T(8,128)(2,1)}, bf16[4,256,1024]{2,1,0:T(8,128)(2,1)}, u32[]{:S(2)}, u32[]{:S(2)}) collective-permute-start(bf16[4,256,1024]{2,1,0:T(8,128)(2,1)} %get-tuple-element.133), channel_id=1, source_target_pairs={{0,1},{1,0},{2,3},{3,2},{4,5},{5,4},{6,7},{7,6},{8,9},{9,8},{10,11... | collective-permute-start | bytes 6291464 | tf_op jit(solution)/shard_map/ppermute | solution.py:341
  476.7 47.8 %collective-permute-start.8 = (bf16[4,256,1024]{2,1,0:T(8,128)(2,1)}, bf16[4,256,1024]{2,1,0:T(8,128)(2,1)}, u32[]{:S(2)}, u32[]{:S(2)}) collective-permute-start(bf16[4,256,1024]{2,1,0:T(8,128)(2,1)} %get-tuple-element.134), channel_id=1, source_target_pairs={{0,4},{2,6},{4,0},{6,2},{8,12},{10,14},{12,8},{14,10},{16,20},{18,... | collective-permute-start | bytes 6291464 | tf_op jit(solution)/shard_map/ppermute | solution.py:337
  524.6 35.6 %collective-permute-start.9 = (bf16[4,256,2048]{2,1,0:T(8,128)(2,1)}, bf16[4,256,2048]{2,1,0:T(8,128)(2,1)}, u32[]{:S(2)}, u32[]{:S(2)}) collective-permute-start(bf16[4,256,2048]{2,1,0:T(8,128)(2,1)} %get-tuple-element.135), channel_id=1, source_target_pairs={{0,2},{2,0},{4,6},{6,4},{8,10},{10,8},{12,14},{14,12},{16,18},{18,... | collective-permute-start | bytes 12582920 | tf_op jit(solution)/shard_map/ppermute | solution.py:333
  559.6 58.6 %collective-permute-start.6 = (bf16[4,256,2048]{2,1,0:T(8,128)(2,1)}, bf16[4,256,2048]{2,1,0:T(8,128)(2,1)}, u32[]{:S(2)}, u32[]{:S(2)}) collective-permute-start(bf16[4,256,2048]{2,1,0:T(8,128)(2,1)} %get-tuple-element.130), channel_id=1, source_target_pairs={{0,2},{2,0},{4,6},{6,4},{8,10},{10,8},{12,14},{14,12},{16,18},{18,... | collective-permute-start | bytes 12582920 | tf_op jit(solution)/shard_map/ppermute | solution.py:333
  564.7 42.1 %collective-permute-start.10 = (bf16[2,256,1024]{2,1,0:T(8,128)(2,1)S(1)}, bf16[2,256,1024]{2,1,0:T(8,128)(2,1)}, u32[]{:S(2)}, u32[]{:S(2)}) collective-permute-start(bf16[2,256,1024]{2,1,0:T(8,128)(2,1)S(1)} %get-tuple-element.145), channel_id=1, source_target_pairs={{0,1},{1,0},{2,3},{3,2},{4,5},{5,4},{6,7},{7,6},{8,9},{9,8},{10,11... | collective-permute-start | bytes 3145736 | tf_op jit(solution)/shard_map/ppermute | solution.py:341
  565.3 41.5 %collective-permute-start.11 = (bf16[2,256,1024]{2,1,0:T(8,128)(2,1)S(1)}, bf16[2,256,1024]{2,1,0:T(8,128)(2,1)}, u32[]{:S(2)}, u32[]{:S(2)}) collective-permute-start(bf16[2,256,1024]{2,1,0:T(8,128)(2,1)S(1)} %get-tuple-element.146), channel_id=1, source_target_pairs={{0,4},{2,6},{4,0},{6,2},{8,12},{10,14},{12,8},{14,10},{16,20},{18,... | collective-permute-start | bytes 3145736 | tf_op jit(solution)/shard_map/ppermute | solution.py:337
  568.1 44.5 %collective-permute-start.12 = (bf16[2,256,1024]{2,1,0:T(8,128)(2,1)S(1)}, bf16[2,256,1024]{2,1,0:T(8,128)(2,1)}, u32[]{:S(2)}, u32[]{:S(2)}) collective-permute-start(bf16[2,256,1024]{2,1,0:T(8,128)(2,1)S(1)} %add_convert_fusion.27), channel_id=1, source_target_pairs={{0,4},{2,6},{4,0},{6,2},{8,12},{10,14},{12,8},{14,10},{16,20},{18,... | collective-permute-start | bytes 3145736 | tf_op jit(solution)/shard_map/ppermute | solution.py:337
  571.6 41.1 %collective-permute-start.13 = (bf16[2,256,1024]{2,1,0:T(8,128)(2,1)}, bf16[2,256,1024]{2,1,0:T(8,128)(2,1)}, u32[]{:S(2)}, u32[]{:S(2)}) collective-permute-start(bf16[2,256,1024]{2,1,0:T(8,128)(2,1)} %add_convert_fusion.26), channel_id=1, source_target_pairs={{0,1},{1,0},{2,3},{3,2},{4,5},{5,4},{6,7},{7,6},{8,9},{9,8},{10,11... | collective-permute-start | bytes 3145736 | tf_op jit(solution)/shard_map/ppermute | solution.py:341
  612.7 21.9 %collective-permute-start.14 = (bf16[4,256,2048]{2,1,0:T(8,128)(2,1)}, bf16[4,256,2048]{2,1,0:T(8,128)(2,1)}, u32[]{:S(2)}, u32[]{:S(2)}) collective-permute-start(bf16[4,256,2048]{2,1,0:T(8,128)(2,1)} %get-tuple-element.151), channel_id=1, source_target_pairs={{0,2},{2,0},{4,6},{6,4},{8,10},{10,8},{12,14},{14,12},{16,18},{18,... | collective-permute-start | bytes 12582920 | tf_op jit(solution)/shard_map/ppermute | solution.py:333
  613.4 12.1 %all-to-all-start.1 = ((f32[32,1,256]{2,1,0:T(1,128)}), f32[32,1,256]{2,1,0:T(1,128)S(1)}, u32[]{:S(2)}, u32[]{:S(2)}) async-start(f32[32,1,256]{2,1,0:T(1,128)} %bitcast.162), calls=%async_computation.1 | async-start | bytes 65536 | tf_op jit(solution)/shard_map/all_to_all | solution.py:970
  618.1 471.8 %reduce-scatter.5.cloned.1.call-start = ((), (), s32[]{:S(2)}) async-start(), calls=%async_computation.8 | async-start | bytes 8912896 | tf_op jit(solution)/shard_map/reduce_scatter | solution.py:1041
  631.3 28.4 %collective-permute-start.19 = (bf16[256,2048]{1,0:T(8,128)(2,1)}, bf16[256,2048]{1,0:T(8,128)(2,1)S(1)}, u32[]{:S(2)}, u32[]{:S(2)}) collective-permute-start(bf16[256,2048]{1,0:T(8,128)(2,1)} %pad_maximum_fusion.11), channel_id=1, source_target_pairs={{0,24},{2,26},{4,28},{6,30},{8,0},{10,2},{12,4},{14,6},{16,8},{18,... | collective-permute-start | bytes 3145736 | tf_op jit(solution)/shard_map/ppermute | solution.py:358
  634.5 66.8 %collective-permute-start.20 = (bf16[256,2048]{1,0:T(8,128)(2,1)}, bf16[256,2048]{1,0:T(8,128)(2,1)S(1)}, u32[]{:S(2)}, u32[]{:S(2)}) collective-permute-start(bf16[256,2048]{1,0:T(8,128)(2,1)} %pad_maximum_fusion.12), channel_id=1, source_target_pairs={{0,16},{2,18},{4,20},{6,22},{8,24},{10,26},{12,28},{14,30},{16,0},... | collective-permute-start | bytes 3145736 | tf_op jit(solution)/shard_map/ppermute | solution.py:358
  639.0 62.3 %collective-permute-start.15 = (bf16[2,256,1024]{2,1,0:T(8,128)(2,1)}, bf16[2,256,1024]{2,1,0:T(8,128)(2,1)}, u32[]{:S(2)}, u32[]{:S(2)}) collective-permute-start(bf16[2,256,1024]{2,1,0:T(8,128)(2,1)} %get-tuple-element.152), channel_id=1, source_target_pairs={{0,1},{1,0},{2,3},{3,2},{4,5},{5,4},{6,7},{7,6},{8,9},{9,8},{10,11... | collective-permute-start | bytes 3145736 | tf_op jit(solution)/shard_map/ppermute | solution.py:341
  640.5 60.9 %collective-permute-start.16 = (bf16[2,256,1024]{2,1,0:T(8,128)(2,1)S(1)}, bf16[2,256,1024]{2,1,0:T(8,128)(2,1)}, u32[]{:S(2)}, u32[]{:S(2)}) collective-permute-start(bf16[2,256,1024]{2,1,0:T(8,128)(2,1)S(1)} %get-tuple-element.153), channel_id=1, source_target_pairs={{0,4},{2,6},{4,0},{6,2},{8,12},{10,14},{12,8},{14,10},{16,20},{18,... | collective-permute-start | bytes 3145736 | tf_op jit(solution)/shard_map/ppermute | solution.py:337
  644.6 56.8 %collective-permute-start.17 = (bf16[2,256,1024]{2,1,0:T(8,128)(2,1)}, bf16[2,256,1024]{2,1,0:T(8,128)(2,1)}, u32[]{:S(2)}, u32[]{:S(2)}) collective-permute-start(bf16[2,256,1024]{2,1,0:T(8,128)(2,1)} %add_convert_fusion.21), channel_id=1, source_target_pairs={{0,4},{2,6},{4,0},{6,2},{8,12},{10,14},{12,8},{14,10},{16,20},{18,... | collective-permute-start | bytes 3145736 | tf_op jit(solution)/shard_map/ppermute | solution.py:337
  659.7 41.7 %collective-permute-start.18 = (bf16[2,256,1024]{2,1,0:T(8,128)(2,1)}, bf16[2,256,1024]{2,1,0:T(8,128)(2,1)}, u32[]{:S(2)}, u32[]{:S(2)}) collective-permute-start(bf16[2,256,1024]{2,1,0:T(8,128)(2,1)} %add_convert_fusion.20), channel_id=1, source_target_pairs={{0,1},{1,0},{2,3},{3,2},{4,5},{5,4},{6,7},{7,6},{8,9},{9,8},{10,11... | collective-permute-start | bytes 3145736 | tf_op jit(solution)/shard_map/ppermute | solution.py:341
  702.4 43.7 %collective-permute-start.23 = (bf16[12,256,2048]{2,1,0:T(8,128)(2,1)}, bf16[12,256,2048]{2,1,0:T(8,128)(2,1)S(1)}, u32[]{:S(2)}, u32[]{:S(2)}) collective-permute-start(bf16[12,256,2048]{2,1,0:T(8,128)(2,1)} %get-tuple-element.176), channel_id=1, source_target_pairs={{0,2},{2,0},{4,6},{6,4},{8,10},{10,8},{12,14},{14,12},{16,18},{18,... | collective-permute-start | bytes 37748744 | tf_op jit(solution)/shard_map/ppermute | solution.py:333
  702.4 35.8 %collective-permute-start.22 = (bf16[4,256,2048]{2,1,0:T(8,128)(2,1)}, bf16[4,256,2048]{2,1,0:T(8,128)(2,1)}, u32[]{:S(2)}, u32[]{:S(2)}) collective-permute-start(bf16[4,256,2048]{2,1,0:T(8,128)(2,1)} %get-tuple-element.174), channel_id=1, source_target_pairs={{0,2},{2,0},{4,6},{6,4},{8,10},{10,8},{12,14},{14,12},{16,18},{18,... | collective-permute-start | bytes 12582920 | tf_op jit(solution)/shard_map/ppermute | solution.py:333
  707.9 27.6 %collective-permute-start.21 = (bf16[256,2048]{1,0:T(8,128)(2,1)S(1)}, bf16[256,2048]{1,0:T(8,128)(2,1)S(1)}, u32[]{:S(2)}, u32[]{:S(2)}) collective-permute-start(bf16[256,2048]{1,0:T(8,128)(2,1)S(1)} %pad_maximum_fusion.13), channel_id=1, source_target_pairs={{0,8},{2,10},{4,12},{6,14},{8,16},{10,18},{12,20},{14,22},{16,24},... | collective-permute-start | bytes 3145736 | tf_op jit(solution)/shard_map/ppermute | solution.py:358
  746.1 24.7 %collective-permute-start.24 = (bf16[256,2048]{1,0:T(8,128)(2,1)S(1)}, bf16[256,2048]{1,0:T(8,128)(2,1)}, u32[]{:S(2)}, u32[]{:S(2)}) collective-permute-start(bf16[256,2048]{1,0:T(8,128)(2,1)S(1)} %fusion.51), channel_id=1, source_target_pairs={{0,1},{1,0},{2,3},{3,2},{4,5},{5,4},{6,7},{7,6},{8,9},{9,8},{10,11... | collective-permute-start | bytes 3145736 | tf_op jit(solution)/shard_map/ppermute | solution.py:341
  781.5 309.9 %reduce-scatter.3.cloned.1.call-start = ((), (), s32[]{:S(2)}) async-start(), calls=%async_computation.7 | async-start | bytes 13369344 | tf_op jit(solution)/shard_map/reduce_scatter | solution.py:1048
  781.5 60.1 %collective-permute-start.26 = (bf16[4,256,1024]{2,1,0:T(8,128)(2,1)}, bf16[4,256,1024]{2,1,0:T(8,128)(2,1)S(1)}, u32[]{:S(2)}, u32[]{:S(2)}) collective-permute-start(bf16[4,256,1024]{2,1,0:T(8,128)(2,1)} %get-tuple-element.233), channel_id=1, source_target_pairs={{0,4},{2,6},{4,0},{6,2},{8,12},{10,14},{12,8},{14,10},{16,20},{18,... | collective-permute-start | bytes 6291464 | tf_op jit(solution)/shard_map/ppermute | solution.py:337
  783.1 58.5 %collective-permute-start.25 = (bf16[4,256,1024]{2,1,0:T(8,128)(2,1)}, bf16[4,256,1024]{2,1,0:T(8,128)(2,1)S(1)}, u32[]{:S(2)}, u32[]{:S(2)}) collective-permute-start(bf16[4,256,1024]{2,1,0:T(8,128)(2,1)} %get-tuple-element.186), channel_id=1, source_target_pairs={{0,1},{1,0},{2,3},{3,2},{4,5},{5,4},{6,7},{7,6},{8,9},{9,8},{10,11... | collective-permute-start | bytes 6291464 | tf_op jit(solution)/shard_map/ppermute | solution.py:341
  784.6 89.6 %collective-permute-start.27 = (bf16[4,256,1024]{2,1,0:T(8,128)(2,1)}, bf16[4,256,1024]{2,1,0:T(8,128)(2,1)}, u32[]{:S(2)}, u32[]{:S(2)}) collective-permute-start(bf16[4,256,1024]{2,1,0:T(8,128)(2,1)} %pad_maximum_fusion.6), channel_id=1, source_target_pairs={{0,1},{1,0},{2,3},{3,2},{4,5},{5,4},{6,7},{7,6},{8,9},{9,8},{10,11... | collective-permute-start | bytes 6291464 | tf_op jit(solution)/shard_map/ppermute | solution.py:341
  785.1 115.9 %collective-permute-start.28 = (bf16[4,256,1024]{2,1,0:T(8,128)(2,1)}, bf16[4,256,1024]{2,1,0:T(8,128)(2,1)}, u32[]{:S(2)}, u32[]{:S(2)}) collective-permute-start(bf16[4,256,1024]{2,1,0:T(8,128)(2,1)} %pad_maximum_fusion.5), channel_id=1, source_target_pairs={{0,4},{2,6},{4,0},{6,2},{8,12},{10,14},{12,8},{14,10},{16,20},{18,... | collective-permute-start | bytes 6291464 | tf_op jit(solution)/shard_map/ppermute | solution.py:337
  925.3 23.0 %collective-permute-start.34 = (bf16[256,2048]{1,0:T(8,128)(2,1)}, bf16[256,2048]{1,0:T(8,128)(2,1)}, u32[]{:S(2)}, u32[]{:S(2)}) collective-permute-start(bf16[256,2048]{1,0:T(8,128)(2,1)} %select_convert_fusion), channel_id=1, source_target_pairs={{0,1},{1,0},{2,3},{3,2},{4,5},{5,4},{6,7},{7,6},{8,9},{9,8},{10,11... | collective-permute-start | bytes 3145736 | tf_op jit(solution)/shard_map/ppermute | solution.py:341
  932.0 82.2 %collective-permute-start.29 = (bf16[4,256,1024]{2,1,0:T(8,128)(2,1)}, bf16[4,256,1024]{2,1,0:T(8,128)(2,1)}, u32[]{:S(2)}, u32[]{:S(2)}) collective-permute-start(bf16[4,256,1024]{2,1,0:T(8,128)(2,1)} %add_convert_fusion.1), channel_id=1, source_target_pairs={{0,4},{2,6},{4,0},{6,2},{8,12},{10,14},{12,8},{14,10},{16,20},{18,... | collective-permute-start | bytes 6291464 | tf_op jit(solution)/shard_map/ppermute | solution.py:337
  953.9 60.3 %collective-permute-start.30 = (bf16[4,256,1024]{2,1,0:T(8,128)(2,1)S(1)}, bf16[4,256,1024]{2,1,0:T(8,128)(2,1)S(1)}, u32[]{:S(2)}, u32[]{:S(2)}) collective-permute-start(bf16[4,256,1024]{2,1,0:T(8,128)(2,1)S(1)} %add_convert_fusion), channel_id=1, source_target_pairs={{0,1},{1,0},{2,3},{3,2},{4,5},{5,4},{6,7},{7,6},{8,9},{9,8},{10,11... | collective-permute-start | bytes 6291464 | tf_op jit(solution)/shard_map/ppermute | solution.py:341
  955.5 46.7 %collective-permute-start.43 = (f32[18,128]{1,0:T(8,128)S(1)}, f32[18,128]{1,0:T(8,128)S(1)}, u32[]{:S(2)}, u32[]{:S(2)}) collective-permute-start(f32[18,128]{1,0:T(8,128)S(1)} %fusion.48), channel_id=1, source_target_pairs={{0,1},{1,0},{2,3},{3,2},{4,5},{5,4},{6,7},{7,6},{8,9},{9,8},{10,11... | collective-permute-start | bytes 27656 | tf_op jit(solution)/shard_map/ppermute | solution.py:341
  1009.6 4.6 collective-permute-start.46
  1015.5 13.0 %collective-permute-start.37 = (f32[8,33,128]{2,0,1:T(8,128)S(1)}, f32[8,33,128]{2,0,1:T(8,128)S(1)}, u32[]{:S(2)}, u32[]{:S(2)}) collective-permute-start(f32[8,33,128]{2,0,1:T(8,128)S(1)} %dynamic-slice_bitcast_fusion), channel_id=1, source_target_pairs={{0,16},{2,18},{4,20},{6,22},{8,24},{10,26},{12,28},{14,30},{16,0},... | collective-permute-start | bytes 405512 | tf_op jit(solution)/shard_map/ppermute | solution.py:415
  1027.0 52.6 %collective-permute-start.32 = (bf16[256,2048]{1,0:T(8,128)(2,1)}, bf16[256,2048]{1,0:T(8,128)(2,1)}, u32[]{:S(2)}, u32[]{:S(2)}) collective-permute-start(bf16[256,2048]{1,0:T(8,128)(2,1)} %get-tuple-element.270), channel_id=1, source_target_pairs={{0,8},{2,10},{4,12},{6,14},{8,0},{10,2},{12,4},{14,6},{16,24},{18,... | collective-permute-start | bytes 3145736 | tf_op jit(solution)/shard_map/ppermute | solution.py:372
  1029.9 44.6 %collective-permute-start.38 = (f32[4,33,128]{2,0,1:T(4,128)}, f32[4,33,128]{2,0,1:T(4,128)}, u32[]{:S(2)}, u32[]{:S(2)}) collective-permute-start(f32[4,33,128]{2,0,1:T(4,128)} %dynamic-slice_bitcast_fusion.1), channel_id=1, source_target_pairs={{0,8},{2,10},{4,12},{6,14},{8,0},{10,2},{12,4},{14,6},{16,24},{18,... | collective-permute-start | bytes 202760 | tf_op jit(solution)/shard_map/ppermute | solution.py:415
  1077.0 40.4 %collective-permute-start.31 = (bf16[256,2048]{1,0:T(8,128)(2,1)}, bf16[256,2048]{1,0:T(8,128)(2,1)}, u32[]{:S(2)}, u32[]{:S(2)}) collective-permute-start(bf16[256,2048]{1,0:T(8,128)(2,1)} %get-tuple-element.269), channel_id=1, source_target_pairs={{0,8},{2,10},{4,12},{6,14},{8,0},{10,2},{12,4},{14,6},{16,24},{18,... | collective-permute-start | bytes 3145736 | tf_op jit(solution)/shard_map/ppermute | solution.py:372
  1079.5 5.4 collective-permute-start.40
  1082.5 49.3 %collective-permute-start.33 = (bf16[256,2048]{1,0:T(8,128)(2,1)}, bf16[256,2048]{1,0:T(8,128)(2,1)}, u32[]{:S(2)}, u32[]{:S(2)}) collective-permute-start(bf16[256,2048]{1,0:T(8,128)(2,1)} %add_convert_fusion.11), channel_id=1, source_target_pairs={{0,16},{2,18},{4,20},{6,22},{8,24},{10,26},{12,28},{14,30},{16,0},... | collective-permute-start | bytes 3145736 | tf_op jit(solution)/shard_map/ppermute | solution.py:373
  1089.9 47.2 %collective-permute-start.36 = (bf16[128,2048]{1,0:T(8,128)(2,1)}, bf16[128,2048]{1,0:T(8,128)(2,1)}, u32[]{:S(2)}, u32[]{:S(2)}) collective-permute-start(bf16[128,2048]{1,0:T(8,128)(2,1)} %reduce-scatter.5.cloned.1.call-done), channel_id=1, source_target_pairs={{0,1},{1,0},{2,3},{3,2},{4,5},{5,4},{6,7},{7,6},{8,9},{9,8},{10,11... | collective-permute-start | bytes 1572872 | tf_op jit(solution)/shard_map/ppermute | solution.py:341
  1091.4 48.4 %collective-permute-start.35 = (bf16[128,3072]{1,0:T(8,128)(2,1)}, bf16[128,3072]{1,0:T(8,128)(2,1)}, u32[]{:S(2)}, u32[]{:S(2)}) collective-permute-start(bf16[128,3072]{1,0:T(8,128)(2,1)} %reduce-scatter.3.cloned.1.call-done.mine_ref), channel_id=1, source_target_pairs={{0,1},{1,0},{2,3},{3,2},{4,5},{5,4},{6,7},{7,6},{8,9},{9,8},{10,11... | collective-permute-start | bytes 2359304 | tf_op jit(solution)/shard_map/ppermute | solution.py:341
  (78 other events, 1836.6 us)
Sparse Core Ops, SparseCore 0:
  10.4 112.8 all-gather.3
  125.4 134.2 all-gather.7
  261.9 168.0 all-gather.5
  781.6 124.7 reduce-scatter.4
  911.3 159.4 reduce-scatter.2

commit v11 on v10

--- a/solution.py
+++ b/solution.py
@@ -365,13 +365,17 @@
     return total
 
 
-def line_halving(entries, place):
+def line_first(entries, place):
     fsdp = lax.axis_size("fsdp")
     even = place % 2 == 0
     one, two = jnp.where(even, entries[3], entries[1]), jnp.where(even, entries[1], entries[3])
-    one, two = (lax.ppermute(item, "fsdp", [(i, i ^ 4) for i in range(fsdp)]) for item in (one, two))
-    far = lax.ppermute(add_low(entries[2], two), "fsdp", [(i, i ^ 8) for i in range(fsdp)])
-    return entries[0].astype(full) + one.astype(full) + far.astype(full)
+    return [lax.ppermute(item, "fsdp", [(i, i ^ 4) for i in range(fsdp)]) for item in (one, two)]
+
+
+def line_second(entries, two):
+    return lax.ppermute(
+        add_low(entries[2], two), "fsdp", [(i, i ^ 8) for i in range(lax.axis_size("fsdp"))]
+    )
 
 
 def joined(places, own, got):
@@ -395,28 +399,19 @@
     return add_low(keep[cut], other[cut])
 
 
-def sum_all(values, fsdp):
-    values = values + lax.ppermute(values, "fsdp", core_pairs(fsdp))
-    values = values + swap_ctx(values)
-    step = 2
-    while step < fsdp:
+def sum_partners(values, fsdp, steps):
+    for step in steps:
         values = values + lax.ppermute(values, "fsdp", [(i, i ^ step) for i in range(fsdp)])
-        step *= 2
     return values
 
 
-def sum_owned(values, fsdp, spot):
-    items, shard = values.shape[0], values.shape[1] // fsdp
-    values = values.reshape(items, fsdp, shard).swapaxes(0, 1)
-    step = fsdp // 2
-    while step:
+def halve_owned(values, fsdp, spot, steps):
+    for step in steps:
         bit = (spot // step) % 2
-        values = values.reshape(2, step, items, shard)
+        values = values.reshape(2, values.shape[0] // 2, *values.shape[1:])
         other = lax.ppermute(take(values, 1 - bit), "fsdp", [(i, i ^ step) for i in range(fsdp)])
         values = take(values, bit) + other
-        step //= 2
-    values = values[0]
-    return values + swap_ctx(values)
+    return values
 
 
 def turn(values):
@@ -1008,30 +1003,27 @@
     side_one, side_two, ctx_one, ctx_two = out_sums
     out_far[0] = swap_ctx(out_far[0])
     grad_attended = mul(grad_branch, out_all, rhs_turned).astype(low)
-    grad_attended, out_far = hold(grad_attended, out_far)
+    grad_out_part = mul(attended, grad_branch, lhs_turned).astype(low)
+    grad_q, grad_k, grad_v, gain_q_part, gain_k_part = attend_grad(
+        projected, roped_q, roped_k, values_low, grad_attended, cosine, sine, gain_q, gain_k, kv_heads, group
+    )
+    grad_projected = jnp.concatenate([grad_q, grad_k, grad_v], axis=1)
+    grad_projected, out_far = hold(grad_projected, out_far)
     got = [
         swap_ctx(ctx_one),
         swap_side(side_two),
         swap_side(add_low(side_one, out_far[0])),
         swap_ctx(add_low(ctx_two, out_far[1])),
     ]
-    grad_out_part = mul(attended, grad_branch, lhs_turned).astype(low)
-    grad_q, grad_k, grad_v, gain_q_part, gain_k_part = attend_grad(
-        projected, roped_q, roped_k, values_low, grad_attended, cosine, sine, gain_q, gain_k, kv_heads, group
-    )
-    grad_projected = jnp.concatenate([grad_q, grad_k, grad_v], axis=1)
-    grad_projected, (got[0], got[1]) = hold(grad_projected, (got[0], got[1]))
     grad_qkv_part = mul(low_in, grad_projected, lhs_turned).astype(low)
+    grad_normed_part = mul(grad_projected, qkv_all, rhs_turned)
+    early = jnp.concatenate([grad_router.T, grad_moe_gain[None]], axis=0)
+    early = early.reshape(experts_all + 1, fsdp, shard).swapaxes(0, 1)
+    early = halve_owned(early, fsdp, spot, (8, 4))
     grad_gate_up = mul(rows, grad_pair, lhs_turned)[None]
-    got, grad_gate_up = hold(got, grad_gate_up)
+    got, early = hold(got, early)
     entries = joined(places, out_own, got)
-    if lines == 4:
-        output = (mixed + line_halving(entries, place)).astype(low)
-    else:
-        output = (
-            mixed + line_total(entries[0], {p: line_shift(entries[p], lines - p) for p in places[:-1]})
-        ).astype(low)
-    grad_normed_part = mul(grad_projected, qkv_all, rhs_turned)
+    one, two = line_first(entries, place)
     grad_normed = of_block(grad_normed_part, rank) + swap_ctx(
         of_block(grad_normed_part, 1 - rank).astype(low)
     ).astype(full)
@@ -1047,21 +1039,23 @@
     )
     qkv_mine = lax.psum_scatter(grad_qkv_part, "fsdp", scatter_dimension=0, tiled=True)
     grad_qkv = all_heads(rank_at, qkv_mine, swap_ctx(qkv_mine), head_dim, my_heads)
-    early, got = hold(jnp.concatenate([grad_router.T, grad_moe_gain[None]], axis=0), got)
-    early = sum_owned(early, fsdp, spot)
-    late = sum_all(
-        jnp.concatenate(
-            [
-                grad_attn_gain.reshape(-1, head_dim),
-                jnp.sum(gain_q_part, axis=0),
-                jnp.sum(gain_k_part, axis=0),
-            ],
-            axis=0,
-        ),
-        fsdp,
-    )
-    (hidden, grad_rows), late = hold((hidden, grad_rows), late)
+    early = halve_owned(early, fsdp, spot, (2, 1))[0]
+    early = early + swap_ctx(early)
+    late = jnp.concatenate(
+        [
+            grad_attn_gain.reshape(-1, head_dim),
+            jnp.sum(gain_q_part, axis=0),
+            jnp.sum(gain_k_part, axis=0),
+        ],
+        axis=0,
+    )
     grad_down = mul(hidden, grad_rows, lhs_turned)[None]
+    late, (one, two, grad_gate_up, grad_down) = hold(late, (one, two, grad_gate_up, grad_down))
+    far = line_second(entries, two)
+    late = swap_ctx(late) + late
+    late, far = hold(sum_partners(late, fsdp, (1, 2)), far)
+    output = (mixed + entries[0].astype(full) + one.astype(full) + far.astype(full)).astype(low)
+    late = sum_partners(late, fsdp, (4, 8))
     gain_rows = width // head_dim
     return (
         output,
@@ -1085,7 +1079,7 @@
     tokens, gate_up = args[0], args[8]
     fsdp, ctx = lax.axis_size("fsdp"), lax.axis_size("ctx")
     fits = tokens.size * tokens.dtype.itemsize * fsdp * ctx <= gathered_bytes
-    if fits and fsdp % 4 == 0 and ctx == 2 and fsdp >= 8 and fsdp & (fsdp - 1) == 0 and gate_up.shape[0] == 1:
+    if fits and ctx == 2 and fsdp == 16 and gate_up.shape[0] == 1:
         return body_gathered(*args)
     return body_routed(*args)
 

time: 1160 us -> 1200 us (1.034)
  waiting for transfers between devices: 571 us -> 611 us
    ppermute x8, waiting for transfers between devices: 79.3 us -> 104 us  [swap_side(): return lax.ppermute(values, 'fsdp', side_pairs(lax.axis_size('fsdp')))]
  transfers between devices with their start and end apart: 53 -> 53, of which waited for: 28 -> 30; matrix products, arithmetic and copies ran while one was open for 19% -> 19% of each run, Pallas kernels for 16% -> 16%
where the time goes in v11:
time: 1200 us; the launch traced here: 1190 us
  waiting for transfers between devices  611 us (51%)
  Pallas kernels  225 us (19%)
  other arithmetic  112 us (9%)
  matrix products  112 us (9%)
  starting transfers between devices  52.5 us (4%)
  blocking collectives  35.6 us (3%)
  local copies, waits for them, and re-layouts  27.1 us (2%)
  between operations  15.5 us (1%)
    ppermute x19, waiting for transfers between devices, swap_ctx(): return lax.ppermute(values, 'ctx', [(0, 1), (1, 0)])  275 us
    pallas_call x4, Pallas kernels, run_expert(): pl.pallas_call(expert_kernel, grid_spec=grid_spec, out_shape=[shape((step...  135 us
    dot_general x11, matrix products, mul(): return lax.dot_general(left, right, dims, preferred_element_type=full)  112 us
    ppermute x8, waiting for transfers between devices, swap_side(): return lax.ppermute(values, 'fsdp', side_pairs(lax.axis_size('fsdp')))  104 us
    convert_element_type x20, other arithmetic, add_low(): return (one.astype(full) + two.astype(full)).astype(low)  73.4 us
    all_gather x1, waiting for transfers between devices, body_gathered(): weights_all = lax.all_gather(weights_local, 'fsdp', axis=0, tiled=True)  65.6 us
    pallas_call x2, Pallas kernels, run_result(): pl.pallas_call(result_kernel, grid_spec=pltpu.PrefetchScalarGridSpec(num_...  40.2 us
    ppermute x2, waiting for transfers between devices, line_first(): lax.ppermute(item, 'fsdp', [(i, i ^ 4) for i in range(fsdp)])  39.5 us
  transfers between devices with their start and end apart: 53, of which 30 were waited for; matrix products, arithmetic and copies ran while one was open for 19% of the time, Pallas kernels for 16%

profile of v11, /device:TPU:0, one launch (start us, length us, event | category | flops | bytes accessed | tf_op | source)
XLA Modules:
  0.0 1190.7 jit_solution(3707734911487388616)
XLA Ops:
  13.4 13.3 %collective-permute-done.3 = bf16[256,1152]{1,0:T(8,128)(2,1)S(1)} collective-permute-done((bf16[256,1152]{1,0:T(8,128)(2,1)S(1)}, bf16[256,1152]{1,0:T(8,128)(2,1)S(1)}, u32[]{:S(2)}, u32[]{:S(2)}) %collective-permute-start.3) | collective-permute-done | bytes 589856 | tf_op jit(solution)/shard_map/ppermute | solution.py:341
  31.2 22.9 %all_gather.12 = bf16[2048,34]{0,1:T(8,128)(2,1)S(1)} all-gather(bf16[128,34]{0,1:T(8,128)(2,1)S(1)} %pad_maximum_fusion.19), channel_id=1, replica_groups=mesh['fsdp'=16,'ctx'=2] {'fsdp'}, dimensions={0}, use_global_device_ids=true | all-gather | bytes 147968 | tf_op jit(solution)/shard_map/all_gather | solution.py:839
  57.6 65.6 %all-gather.4.cloned.1.call-done = bf16[2048,5120]{1,0:T(8,128)(2,1)} async-done(((bf16[128,5120]{1,0:T(8,128)(2,1)}), bf16[2048,5120]{1,0:T(8,128)(2,1)}) %all-gather.4.cloned.1.call-update) | async-done | bytes 20971536 | tf_op jit(solution)/shard_map/all_gather | solution.py:840
  123.2 11.5 fusion.2.q_ref.k_ref.v_ref
  134.7 18.2 %attend.1 = (bf16[512,2048]{1,0:T(8,128)(2,1)S(1)}, bf16[512,2048]{1,0:T(8,128)(2,1)S(1)}, bf16[512,512]{1,0:T(8,128)(2,1)S(1)}, bf16[512,512]{1,0:T(8,128)(2,1)S(1)}) custom-call(f32[512,3072]{1,0:T(8,128)} %fusion.2.q_ref.k_ref.v_ref, f32[512,3072]{1,0:T(8,128)} %fusion.2.q_ref.k_ref.v_ref, f32[512,3072]{1,0:T(8,128)} %fusion.2.q_ref.k_ref.v_ref, ...), custom_call_target="tpu_custom_call" | custom-call | flops 2147483648 | bytes 9437184 | tf_op jit(solution)/shard_map/attend/pallas_call | solution.py:525
  153.0 8.4 fusion.6
  163.5 23.8 %collective-permute-done.1 = bf16[256,2048]{1,0:T(8,128)(2,1)S(1)} collective-permute-done((bf16[256,2048]{1,0:T(8,128)(2,1)S(1)}, bf16[256,2048]{1,0:T(8,128)(2,1)S(1)}, u32[]{:S(2)}, u32[]{:S(2)}) %collective-permute-start.1) | collective-permute-done | bytes 1048608 | tf_op jit(solution)/shard_map/ppermute | solution.py:341
  191.7 23.1 %collective-permute-done.2 = bf16[256,2048]{1,0:T(8,128)(2,1)S(1)} collective-permute-done((bf16[256,2048]{1,0:T(8,128)(2,1)S(1)}, bf16[256,2048]{1,0:T(8,128)(2,1)S(1)}, u32[]{:S(2)}, u32[]{:S(2)}) %collective-permute-start.2) | collective-permute-done | bytes 1048608 | tf_op jit(solution)/shard_map/ppermute | solution.py:341
  218.4 12.8 %all_to_all.24 = f32[32,1,256]{2,1,0:T(1,128)S(1)} all-to-all(f32[32,1,256]{2,1,0:T(1,128)S(1)} %copy.60), channel_id=1, replica_groups=mesh['fsdp'=16,'ctx'=2] {'fsdp','ctx'}, dimensions={0} | all-to-all | bytes 65536 | tf_op jit(solution)/shard_map/all_to_all | solution.py:877
  231.2 28.5 %all-gather.8.cloned.1.call-done = bf16[4096,3200]{1,0:T(8,128)(2,1)} async-done(((bf16[256,3200]{1,0:T(8,128)(2,1)}), bf16[4096,3200]{1,0:T(8,128)(2,1)}) %all-gather.8.cloned.1.call-update) | async-done | bytes 26214416 | tf_op jit(solution)/shard_map/all_gather | solution.py:847
  259.7 6.9 slice.403
  269.3 157.8 %collective-permute-done.4.far_ref = bf16[8,2,256,896]{3,2,1,0:T(8,128)(2,1)} collective-permute-done((bf16[8,2,256,896]{3,2,1,0:T(8,128)(2,1)}, bf16[8,2,256,896]{3,2,1,0:T(8,128)(2,1)}, u32[]{:S(2)}, u32[]{:S(2)}) %collective-permute-start.4) | collective-permute-done | bytes 7340064 | tf_op jit(solution)/shard_map/ppermute | solution.py:341
  429.9 33.1 %experts.4 = (bf16[4,256,2048]{2,1,0:T(8,128)(2,1)}, bf16[4,256,2048]{2,1,0:T(8,128)(2,1)}, f32[8,2,2,1,256]{4,3,2,1,0:T(1,128)}, bf16[4096,2048]{1,0:T(8,128)(2...) custom-call(s32[1]{0:T(128)} %bitcast.6.core_ref, s32[16]{0:T(128)} %stack.35.order, ...), custom_call_target="tpu_custom_call" | custom-call | flops 19327352832 | bytes 38273024 | tf_op jit(solution)/shard_map/experts/pallas_call | solution.py:674
  463.3 7.1 collective-permute-done.5
  470.4 4.8 add_convert_fusion.8
  478.5 34.2 %experts.5 = (bf16[4,256,2048]{2,1,0:T(8,128)(2,1)}, bf16[4,256,2048]{2,1,0:T(8,128)(2,1)}, f32[8,2,2,1,256]{4,3,2,1,0:T(1,128)}, bf16[4096,2048]{1,0:T(8,128)(2...) custom-call(s32[1]{0:T(128)} %bitcast.6.core_ref, ...), custom_call_target="tpu_custom_call", output_to_operand_aliasing={{2}: (8, {}), {3}: (9, {}), {4}: (10, {}), {5}: (11, {}), {... | custom-call | flops 19327352832 | bytes 38273024 | tf_op jit(solution)/shard_map/experts/pallas_call | solution.py:674
  512.7 10.7 collective-permute-done.7
  525.8 33.7 %experts.6 = (bf16[4,256,2048]{2,1,0:T(8,128)(2,1)}, bf16[4,256,2048]{2,1,0:T(8,128)(2,1)}, f32[8,2,2,1,256]{4,3,2,1,0:T(1,128)}, bf16[4096,2048]{1,0:T(8,128)(2...) custom-call(s32[1]{0:T(128)} %bitcast.6.core_ref, ...), custom_call_target="tpu_custom_call", output_to_operand_aliasing={{2}: (8, {}), {3}: (9, {}), {4}: (10, {}), {5}: (11, {}), {... | custom-call | flops 19327352832 | bytes 38273024 | tf_op jit(solution)/shard_map/experts/pallas_call | solution.py:674
  573.1 33.7 %experts.7 = (bf16[4,256,2048]{2,1,0:T(8,128)(2,1)}, bf16[4,256,2048]{2,1,0:T(8,128)(2,1)}, f32[8,2,2,1,256]{4,3,2,1,0:T(1,128)}, bf16[4096,2048]{1,0:T(8,128)(2...) custom-call(s32[1]{0:T(128)} %bitcast.6.core_ref, ...), custom_call_target="tpu_custom_call", output_to_operand_aliasing={{2}: (8, {}), {3}: (9, {}), {4}: (10, {}), {5}: (11, {}), {... | custom-call | flops 19327352832 | bytes 38273024 | tf_op jit(solution)/shard_map/experts/pallas_call | solution.py:674
  606.8 5.8 collective-permute-done.12
  613.3 4.7 all-to-all-start.1
  618.1 5.8 add_convert_fusion.7
  647.7 11.9 results.2
  660.1 28.3 %results.3 = (bf16[12,256,2048]{2,1,0:T(8,128)(2,1)}, bf16[12,256,2048]{2,1,0:T(8,128)(2,1)}) custom-call(s32[1]{0:T(128)} %bitcast.6.core_ref, s32[48]{0:T(128)} %stack.44.order, bf16[4096,768]{1,0:T(8,128)(2,1)} %get-tuple-element.156.z_ref, f32[8,2,2,1,256]{4,3,2,1,0:T(1,128)} %reshape.272.w_ref, bf16[768,2048]{1,0:T(8,128)(2,1)} %bitcast.153), custom_call_target="tpu_custom_call" | custom-call | flops 12884901888 | bytes 33030144 | tf_op jit(solution)/shard_map/results/pallas_call | solution.py:705
  688.4 12.9 %collective-permute-done.20 = bf16[256,2048]{1,0:T(8,128)(2,1)S(1)} collective-permute-done((bf16[256,2048]{1,0:T(8,128)(2,1)}, bf16[256,2048]{1,0:T(8,128)(2,1)S(1)}, u32[]{:S(2)}, u32[]{:S(2)}) %collective-permute-start.20) | collective-permute-done | bytes 1048608 | tf_op jit(solution)/shard_map/ppermute | solution.py:358
  709.4 26.0 %collective-permute-done.21 = bf16[256,2048]{1,0:T(8,128)(2,1)S(1)} collective-permute-done((bf16[256,2048]{1,0:T(8,128)(2,1)S(1)}, bf16[256,2048]{1,0:T(8,128)(2,1)S(1)}, u32[]{:S(2)}, u32[]{:S(2)}) %collective-permute-start.21) | collective-permute-done | bytes 1048608 | tf_op jit(solution)/shard_map/ppermute | solution.py:358
  739.9 6.0 add_convert_fusion.2
  747.4 5.1 add_convert_fusion.13
  764.5 6.1 collective-permute-done.24
  774.5 6.8 convolution_convert_fusion.1
  784.4 10.6 fusion.11.go_ref
  795.0 25.4 %attend_grad.1 = (bf16[512,2048]{1,0:T(8,128)(2,1)S(1)}, bf16[512,512]{1,0:T(8,128)(2,1)S(1)}, bf16[512,512]{1,0:T(8,128)(2,1)S(1)}, f32[4,1,128]{2,1,0:T(1,128)S(1)}, f32[4,1,128]{2,1,0:T(1,128)S(1)}) custom-call(f32[512,3072]{1,0:T(8,128)} %fusion.2.q_ref.k_ref.v_ref, f32[512,3072]{1,0:T(8,128)} %fusion.2.q_ref.k_ref.v_ref, bf16[512,2048]{1,0:T(8,128)(2,1)} %copy-done, ...), custom_call_target="tpu_custom_call" | custom-call | flops 5368709120 | bytes 15728640 | tf_op jit(solution)/shard_map/attend_grad/pallas_call | solution.py:549
  820.8 18.2 %collective-permute-done.28 = bf16[4,256,1024]{2,1,0:T(8,128)(2,1)} collective-permute-done((bf16[4,256,1024]{2,1,0:T(8,128)(2,1)}, bf16[4,256,1024]{2,1,0:T(8,128)(2,1)}, u32[]{:S(2)}, u32[]{:S(2)}) %collective-permute-start.28) | collective-permute-done | bytes 2097184 | tf_op jit(solution)/shard_map/ppermute | solution.py:337
  839.1 10.0 convolution_convert_fusion
  850.9 7.7 collective-permute-done.31
  858.8 35.0 %convolution_bitcast_fusion = f32[1,2048,1536]{2,1,0:T(8,128)} fusion(bf16[4096,2048]{1,0:T(8,128)(2,1)} %get-tuple-element.204, bf16[4096,1536]{1,0:T(8,128)(2,1)} %get-tuple-element.205), kind=kOutput, calls=%fused_computation.5 | convolution fusion | flops 25769803776 | bytes 41943040 | tf_op jit(solution)/shard_map/dot_general | solution.py:321
  905.9 11.0 fusion
  924.4 18.4 %collective-permute-done.25 = bf16[4,256,1024]{2,1,0:T(8,128)(2,1)} collective-permute-done((bf16[4,256,1024]{2,1,0:T(8,128)(2,1)}, bf16[4,256,1024]{2,1,0:T(8,128)(2,1)}, u32[]{:S(2)}, u32[]{:S(2)}) %collective-permute-start.25) | collective-permute-done | bytes 2097184 | tf_op jit(solution)/shard_map/ppermute | solution.py:341
  942.8 15.5 %collective-permute-done.26 = bf16[4,256,1024]{2,1,0:T(8,128)(2,1)} collective-permute-done((bf16[4,256,1024]{2,1,0:T(8,128)(2,1)}, bf16[4,256,1024]{2,1,0:T(8,128)(2,1)}, u32[]{:S(2)}, u32[]{:S(2)}) %collective-permute-start.26) | collective-permute-done | bytes 2097184 | tf_op jit(solution)/shard_map/ppermute | solution.py:337
  958.3 62.7 %collective-permute-done.29 = bf16[4,256,1024]{2,1,0:T(8,128)(2,1)} collective-permute-done((bf16[4,256,1024]{2,1,0:T(8,128)(2,1)}, bf16[4,256,1024]{2,1,0:T(8,128)(2,1)}, u32[]{:S(2)}, u32[]{:S(2)}) %collective-permute-start.29) | collective-permute-done | bytes 2097184 | tf_op jit(solution)/shard_map/ppermute | solution.py:337
  1021.0 4.7 fusion.33
  1034.2 16.6 %convolution_bitcast_fusion.1 = f32[1,768,2048]{2,1,0:T(8,128)} fusion(bf16[4096,768]{1,0:T(8,128)(2,1)} %get-tuple-element.156.z_ref, bf16[4096,2048]{1,0:T(8,128)(2,1)S(1)} %bitcast.143), kind=kOutput, calls=%fused_computation.26 | convolution fusion | flops 12884901888 | bytes 29360128 | tf_op jit(solution)/shard_map/dot_general | solution.py:321
  1056.1 17.4 %collective-permute-done.34 = bf16[256,2048]{1,0:T(8,128)(2,1)} collective-permute-done((bf16[256,2048]{1,0:T(8,128)(2,1)}, bf16[256,2048]{1,0:T(8,128)(2,1)}, u32[]{:S(2)}, u32[]{:S(2)}) %collective-permute-start.34) | collective-permute-done | bytes 1048608 | tf_op jit(solution)/shard_map/ppermute | solution.py:372
  1073.5 22.1 %collective-permute-done.35 = bf16[256,2048]{1,0:T(8,128)(2,1)} collective-permute-done((bf16[256,2048]{1,0:T(8,128)(2,1)}, bf16[256,2048]{1,0:T(8,128)(2,1)}, u32[]{:S(2)}, u32[]{:S(2)}) %collective-permute-start.35) | collective-permute-done | bytes 1048608 | tf_op jit(solution)/shard_map/ppermute | solution.py:372
  1112.1 34.1 %collective-permute-done.39 = bf16[256,2048]{1,0:T(8,128)(2,1)} collective-permute-done((bf16[256,2048]{1,0:T(8,128)(2,1)}, bf16[256,2048]{1,0:T(8,128)(2,1)}, u32[]{:S(2)}, u32[]{:S(2)}) %collective-permute-start.39) | collective-permute-done | bytes 1048608 | tf_op jit(solution)/shard_map/ppermute | solution.py:376
  1153.1 5.3 fusion.21
  1159.6 6.6 collective-permute-done.41
  1168.8 11.7 collective-permute-done.40.other_ref
  (335 shorter events, 172.4 us)
Async XLA Ops:
  7.2 116.1 %all-gather.4.cloned.1.call-start = ((), (), s32[]{:S(2)}) async-start(), calls=%async_computation.4 | async-start | bytes 22282240 | tf_op jit(solution)/shard_map/all_gather | solution.py:840
  10.2 249.5 %all-gather.8.cloned.1.call-start = ((), (), s32[]{:S(2)}) async-start(), calls=%async_computation.6 | async-start | bytes 27852800 | tf_op jit(solution)/shard_map/all_gather | solution.py:847
  10.4 16.3 %collective-permute-start.3 = (bf16[256,1152]{1,0:T(8,128)(2,1)S(1)}, bf16[256,1152]{1,0:T(8,128)(2,1)S(1)}, u32[]{:S(2)}, u32[]{:S(2)}) collective-permute-start(bf16[256,1152]{1,0:T(8,128)(2,1)S(1)} %slice.401), channel_id=1, source_target_pairs={{0,1},{1,0},{2,3},{3,2},{4,5},{5,4},{6,7},{7,6},{8,9},{9,8},{10,11... | collective-permute-start | bytes 1769480 | tf_op jit(solution)/shard_map/ppermute | solution.py:341
  28.1 401.9 %all-gather.6.cloned.1.call-start = ((), (), s32[]{:S(2)}) async-start(), calls=%async_computation.5 | async-start | bytes 35651584 | tf_op jit(solution)/shard_map/all_gather | solution.py:868
  28.1 26.4 %collective-permute-start = (bf16[256,2048]{1,0:T(8,128)(2,1)S(1)}, bf16[256,2048]{1,0:T(8,128)(2,1)}, u32[]{:S(2)}, u32[]{:S(2)}) collective-permute-start(bf16[256,2048]{1,0:T(8,128)(2,1)S(1)} %copy-done.7), channel_id=1, source_target_pairs={{0,1},{1,0},{2,3},{3,2},{4,5},{5,4},{6,7},{7,6},{8,9},{9,8},{10,11... | collective-permute-start | bytes 3145736 | tf_op jit(solution)/shard_map/ppermute | solution.py:341
  162.0 25.4 %collective-permute-start.1 = (bf16[256,2048]{1,0:T(8,128)(2,1)S(1)}, bf16[256,2048]{1,0:T(8,128)(2,1)S(1)}, u32[]{:S(2)}, u32[]{:S(2)}) collective-permute-start(bf16[256,2048]{1,0:T(8,128)(2,1)S(1)} %select_convert_fusion.1), channel_id=1, source_target_pairs={{0,1},{1,0},{2,3},{3,2},{4,5},{5,4},{6,7},{7,6},{8,9},{9,8},{10,11... | collective-permute-start | bytes 3145736 | tf_op jit(solution)/shard_map/ppermute | solution.py:341
  190.2 24.7 %collective-permute-start.2 = (bf16[256,2048]{1,0:T(8,128)(2,1)S(1)}, bf16[256,2048]{1,0:T(8,128)(2,1)S(1)}, u32[]{:S(2)}, u32[]{:S(2)}) collective-permute-start(bf16[256,2048]{1,0:T(8,128)(2,1)S(1)} %multiply_convert_fusion), channel_id=1, source_target_pairs={{0,1},{1,0},{2,3},{3,2},{4,5},{5,4},{6,7},{7,6},{8,9},{9,8},{10,11... | collective-permute-start | bytes 3145736 | tf_op jit(solution)/shard_map/ppermute | solution.py:341
  266.6 160.5 %collective-permute-start.4 = (bf16[8,2,256,896]{3,2,1,0:T(8,128)(2,1)}, bf16[8,2,256,896]{3,2,1,0:T(8,128)(2,1)}, u32[]{:S(2)}, u32[]{:S(2)}) collective-permute-start(bf16[8,2,256,896]{3,2,1,0:T(8,128)(2,1)} %slice.403), channel_id=1, source_target_pairs={{0,1},{1,0},{2,3},{3,2},{4,5},{5,4},{6,7},{7,6},{8,9},{9,8},{10,11... | collective-permute-start | bytes 22020104 | tf_op jit(solution)/shard_map/ppermute | solution.py:341
  463.0 7.4 collective-permute-start.5
  475.3 48.1 %collective-permute-start.7 = (bf16[4,256,1024]{2,1,0:T(8,128)(2,1)}, bf16[4,256,1024]{2,1,0:T(8,128)(2,1)}, u32[]{:S(2)}, u32[]{:S(2)}) collective-permute-start(bf16[4,256,1024]{2,1,0:T(8,128)(2,1)} %get-tuple-element.133), channel_id=1, source_target_pairs={{0,1},{1,0},{2,3},{3,2},{4,5},{5,4},{6,7},{7,6},{8,9},{9,8},{10,11... | collective-permute-start | bytes 6291464 | tf_op jit(solution)/shard_map/ppermute | solution.py:341
  476.7 47.8 %collective-permute-start.8 = (bf16[4,256,1024]{2,1,0:T(8,128)(2,1)}, bf16[4,256,1024]{2,1,0:T(8,128)(2,1)}, u32[]{:S(2)}, u32[]{:S(2)}) collective-permute-start(bf16[4,256,1024]{2,1,0:T(8,128)(2,1)} %get-tuple-element.134), channel_id=1, source_target_pairs={{0,4},{2,6},{4,0},{6,2},{8,12},{10,14},{12,8},{14,10},{16,20},{18,... | collective-permute-start | bytes 6291464 | tf_op jit(solution)/shard_map/ppermute | solution.py:337
  524.6 35.6 %collective-permute-start.9 = (bf16[4,256,2048]{2,1,0:T(8,128)(2,1)}, bf16[4,256,2048]{2,1,0:T(8,128)(2,1)}, u32[]{:S(2)}, u32[]{:S(2)}) collective-permute-start(bf16[4,256,2048]{2,1,0:T(8,128)(2,1)} %get-tuple-element.135), channel_id=1, source_target_pairs={{0,2},{2,0},{4,6},{6,4},{8,10},{10,8},{12,14},{14,12},{16,18},{18,... | collective-permute-start | bytes 12582920 | tf_op jit(solution)/shard_map/ppermute | solution.py:333
  559.5 58.5 %collective-permute-start.6 = (bf16[4,256,2048]{2,1,0:T(8,128)(2,1)}, bf16[4,256,2048]{2,1,0:T(8,128)(2,1)}, u32[]{:S(2)}, u32[]{:S(2)}) collective-permute-start(bf16[4,256,2048]{2,1,0:T(8,128)(2,1)} %get-tuple-element.130), channel_id=1, source_target_pairs={{0,2},{2,0},{4,6},{6,4},{8,10},{10,8},{12,14},{14,12},{16,18},{18,... | collective-permute-start | bytes 12582920 | tf_op jit(solution)/shard_map/ppermute | solution.py:333
  564.6 42.1 %collective-permute-start.10 = (bf16[2,256,1024]{2,1,0:T(8,128)(2,1)S(1)}, bf16[2,256,1024]{2,1,0:T(8,128)(2,1)}, u32[]{:S(2)}, u32[]{:S(2)}) collective-permute-start(bf16[2,256,1024]{2,1,0:T(8,128)(2,1)S(1)} %get-tuple-element.145), channel_id=1, source_target_pairs={{0,1},{1,0},{2,3},{3,2},{4,5},{5,4},{6,7},{7,6},{8,9},{9,8},{10,11... | collective-permute-start | bytes 3145736 | tf_op jit(solution)/shard_map/ppermute | solution.py:341
  565.3 41.5 %collective-permute-start.11 = (bf16[2,256,1024]{2,1,0:T(8,128)(2,1)S(1)}, bf16[2,256,1024]{2,1,0:T(8,128)(2,1)}, u32[]{:S(2)}, u32[]{:S(2)}) collective-permute-start(bf16[2,256,1024]{2,1,0:T(8,128)(2,1)S(1)} %get-tuple-element.146), channel_id=1, source_target_pairs={{0,4},{2,6},{4,0},{6,2},{8,12},{10,14},{12,8},{14,10},{16,20},{18,... | collective-permute-start | bytes 3145736 | tf_op jit(solution)/shard_map/ppermute | solution.py:337
  568.1 44.5 %collective-permute-start.12 = (bf16[2,256,1024]{2,1,0:T(8,128)(2,1)S(1)}, bf16[2,256,1024]{2,1,0:T(8,128)(2,1)}, u32[]{:S(2)}, u32[]{:S(2)}) collective-permute-start(bf16[2,256,1024]{2,1,0:T(8,128)(2,1)S(1)} %add_convert_fusion.27), channel_id=1, source_target_pairs={{0,4},{2,6},{4,0},{6,2},{8,12},{10,14},{12,8},{14,10},{16,20},{18,... | collective-permute-start | bytes 3145736 | tf_op jit(solution)/shard_map/ppermute | solution.py:337
  571.6 41.1 %collective-permute-start.13 = (bf16[2,256,1024]{2,1,0:T(8,128)(2,1)}, bf16[2,256,1024]{2,1,0:T(8,128)(2,1)}, u32[]{:S(2)}, u32[]{:S(2)}) collective-permute-start(bf16[2,256,1024]{2,1,0:T(8,128)(2,1)} %add_convert_fusion.26), channel_id=1, source_target_pairs={{0,1},{1,0},{2,3},{3,2},{4,5},{5,4},{6,7},{7,6},{8,9},{9,8},{10,11... | collective-permute-start | bytes 3145736 | tf_op jit(solution)/shard_map/ppermute | solution.py:341
  612.7 21.8 %collective-permute-start.14 = (bf16[4,256,2048]{2,1,0:T(8,128)(2,1)}, bf16[4,256,2048]{2,1,0:T(8,128)(2,1)}, u32[]{:S(2)}, u32[]{:S(2)}) collective-permute-start(bf16[4,256,2048]{2,1,0:T(8,128)(2,1)} %get-tuple-element.151), channel_id=1, source_target_pairs={{0,2},{2,0},{4,6},{6,4},{8,10},{10,8},{12,14},{14,12},{16,18},{18,... | collective-permute-start | bytes 12582920 | tf_op jit(solution)/shard_map/ppermute | solution.py:333
  613.3 12.1 %all-to-all-start.1 = ((f32[32,1,256]{2,1,0:T(1,128)}), f32[32,1,256]{2,1,0:T(1,128)S(1)}, u32[]{:S(2)}, u32[]{:S(2)}) async-start(f32[32,1,256]{2,1,0:T(1,128)} %bitcast.159), calls=%async_computation.1 | async-start | bytes 65536 | tf_op jit(solution)/shard_map/all_to_all | solution.py:965
  618.0 533.0 %reduce-scatter.5.cloned.1.call-start = ((), (), s32[]{:S(2)}) async-start(), calls=%async_computation.8 | async-start | bytes 8912896 | tf_op jit(solution)/shard_map/reduce_scatter | solution.py:1033
  631.2 28.3 %collective-permute-start.19 = (bf16[256,2048]{1,0:T(8,128)(2,1)}, bf16[256,2048]{1,0:T(8,128)(2,1)S(1)}, u32[]{:S(2)}, u32[]{:S(2)}) collective-permute-start(bf16[256,2048]{1,0:T(8,128)(2,1)} %pad_maximum_fusion.11), channel_id=1, source_target_pairs={{0,24},{2,26},{4,28},{6,30},{8,0},{10,2},{12,4},{14,6},{16,8},{18,... | collective-permute-start | bytes 3145736 | tf_op jit(solution)/shard_map/ppermute | solution.py:358
  634.5 66.9 %collective-permute-start.20 = (bf16[256,2048]{1,0:T(8,128)(2,1)}, bf16[256,2048]{1,0:T(8,128)(2,1)S(1)}, u32[]{:S(2)}, u32[]{:S(2)}) collective-permute-start(bf16[256,2048]{1,0:T(8,128)(2,1)} %pad_maximum_fusion.12), channel_id=1, source_target_pairs={{0,16},{2,18},{4,20},{6,22},{8,24},{10,26},{12,28},{14,30},{16,0},... | collective-permute-start | bytes 3145736 | tf_op jit(solution)/shard_map/ppermute | solution.py:358
  639.0 62.4 %collective-permute-start.15 = (bf16[2,256,1024]{2,1,0:T(8,128)(2,1)}, bf16[2,256,1024]{2,1,0:T(8,128)(2,1)}, u32[]{:S(2)}, u32[]{:S(2)}) collective-permute-start(bf16[2,256,1024]{2,1,0:T(8,128)(2,1)} %get-tuple-element.152), channel_id=1, source_target_pairs={{0,1},{1,0},{2,3},{3,2},{4,5},{5,4},{6,7},{7,6},{8,9},{9,8},{10,11... | collective-permute-start | bytes 3145736 | tf_op jit(solution)/shard_map/ppermute | solution.py:341
  640.4 60.9 %collective-permute-start.16 = (bf16[2,256,1024]{2,1,0:T(8,128)(2,1)S(1)}, bf16[2,256,1024]{2,1,0:T(8,128)(2,1)}, u32[]{:S(2)}, u32[]{:S(2)}) collective-permute-start(bf16[2,256,1024]{2,1,0:T(8,128)(2,1)S(1)} %get-tuple-element.153), channel_id=1, source_target_pairs={{0,4},{2,6},{4,0},{6,2},{8,12},{10,14},{12,8},{14,10},{16,20},{18,... | collective-permute-start | bytes 3145736 | tf_op jit(solution)/shard_map/ppermute | solution.py:337
  644.5 56.8 %collective-permute-start.17 = (bf16[2,256,1024]{2,1,0:T(8,128)(2,1)}, bf16[2,256,1024]{2,1,0:T(8,128)(2,1)}, u32[]{:S(2)}, u32[]{:S(2)}) collective-permute-start(bf16[2,256,1024]{2,1,0:T(8,128)(2,1)} %add_convert_fusion.21), channel_id=1, source_target_pairs={{0,4},{2,6},{4,0},{6,2},{8,12},{10,14},{12,8},{14,10},{16,20},{18,... | collective-permute-start | bytes 3145736 | tf_op jit(solution)/shard_map/ppermute | solution.py:337
  659.6 41.8 %collective-permute-start.18 = (bf16[2,256,1024]{2,1,0:T(8,128)(2,1)}, bf16[2,256,1024]{2,1,0:T(8,128)(2,1)}, u32[]{:S(2)}, u32[]{:S(2)}) collective-permute-start(bf16[2,256,1024]{2,1,0:T(8,128)(2,1)} %add_convert_fusion.20), channel_id=1, source_target_pairs={{0,1},{1,0},{2,3},{3,2},{4,5},{5,4},{6,7},{7,6},{8,9},{9,8},{10,11... | collective-permute-start | bytes 3145736 | tf_op jit(solution)/shard_map/ppermute | solution.py:341
  702.3 43.5 %collective-permute-start.23 = (bf16[12,256,2048]{2,1,0:T(8,128)(2,1)}, bf16[12,256,2048]{2,1,0:T(8,128)(2,1)S(1)}, u32[]{:S(2)}, u32[]{:S(2)}) collective-permute-start(bf16[12,256,2048]{2,1,0:T(8,128)(2,1)} %get-tuple-element.176), channel_id=1, source_target_pairs={{0,2},{2,0},{4,6},{6,4},{8,10},{10,8},{12,14},{14,12},{16,18},{18,... | collective-permute-start | bytes 37748744 | tf_op jit(solution)/shard_map/ppermute | solution.py:333
  702.3 35.7 %collective-permute-start.22 = (bf16[4,256,2048]{2,1,0:T(8,128)(2,1)}, bf16[4,256,2048]{2,1,0:T(8,128)(2,1)}, u32[]{:S(2)}, u32[]{:S(2)}) collective-permute-start(bf16[4,256,2048]{2,1,0:T(8,128)(2,1)} %get-tuple-element.174), channel_id=1, source_target_pairs={{0,2},{2,0},{4,6},{6,4},{8,10},{10,8},{12,14},{14,12},{16,18},{18,... | collective-permute-start | bytes 12582920 | tf_op jit(solution)/shard_map/ppermute | solution.py:333
  707.8 27.6 %collective-permute-start.21 = (bf16[256,2048]{1,0:T(8,128)(2,1)S(1)}, bf16[256,2048]{1,0:T(8,128)(2,1)S(1)}, u32[]{:S(2)}, u32[]{:S(2)}) collective-permute-start(bf16[256,2048]{1,0:T(8,128)(2,1)S(1)} %pad_maximum_fusion.13), channel_id=1, source_target_pairs={{0,8},{2,10},{4,12},{6,14},{8,16},{10,18},{12,20},{14,22},{16,24},... | collective-permute-start | bytes 3145736 | tf_op jit(solution)/shard_map/ppermute | solution.py:358
  745.9 24.7 %collective-permute-start.24 = (bf16[256,2048]{1,0:T(8,128)(2,1)S(1)}, bf16[256,2048]{1,0:T(8,128)(2,1)}, u32[]{:S(2)}, u32[]{:S(2)}) collective-permute-start(bf16[256,2048]{1,0:T(8,128)(2,1)S(1)} %fusion.50), channel_id=1, source_target_pairs={{0,1},{1,0},{2,3},{3,2},{4,5},{5,4},{6,7},{7,6},{8,9},{9,8},{10,11... | collective-permute-start | bytes 3145736 | tf_op jit(solution)/shard_map/ppermute | solution.py:341
  781.3 371.4 %reduce-scatter.3.cloned.1.call-start = ((), (), s32[]{:S(2)}) async-start(), calls=%async_computation.7 | async-start | bytes 13369344 | tf_op jit(solution)/shard_map/reduce_scatter | solution.py:1040
  781.3 57.7 %collective-permute-start.28 = (bf16[4,256,1024]{2,1,0:T(8,128)(2,1)}, bf16[4,256,1024]{2,1,0:T(8,128)(2,1)}, u32[]{:S(2)}, u32[]{:S(2)}) collective-permute-start(bf16[4,256,1024]{2,1,0:T(8,128)(2,1)} %get-tuple-element.233), channel_id=1, source_target_pairs={{0,4},{2,6},{4,0},{6,2},{8,12},{10,14},{12,8},{14,10},{16,20},{18,... | collective-permute-start | bytes 6291464 | tf_op jit(solution)/shard_map/ppermute | solution.py:337
  782.9 56.2 %collective-permute-start.27 = (bf16[4,256,1024]{2,1,0:T(8,128)(2,1)}, bf16[4,256,1024]{2,1,0:T(8,128)(2,1)}, u32[]{:S(2)}, u32[]{:S(2)}) collective-permute-start(bf16[4,256,1024]{2,1,0:T(8,128)(2,1)} %get-tuple-element.192), channel_id=1, source_target_pairs={{0,1},{1,0},{2,3},{3,2},{4,5},{5,4},{6,7},{7,6},{8,9},{9,8},{10,11... | collective-permute-start | bytes 6291464 | tf_op jit(solution)/shard_map/ppermute | solution.py:341
  850.8 7.8 collective-permute-start.31
  858.7 35.1 %collective-permute-start.32 = (f32[4,33,128]{2,0,1:T(4,128)S(1)}, f32[4,33,128]{2,0,1:T(4,128)S(1)}, u32[]{:S(2)}, u32[]{:S(2)}) collective-permute-start(f32[4,33,128]{2,0,1:T(4,128)S(1)} %dynamic-slice_bitcast_fusion.1), channel_id=1, source_target_pairs={{0,8},{2,10},{4,12},{6,14},{8,0},{10,2},{12,4},{14,6},{16,24},{18,... | collective-permute-start | bytes 202760 | tf_op jit(solution)/shard_map/ppermute | solution.py:412
  893.8 48.9 %collective-permute-start.25 = (bf16[4,256,1024]{2,1,0:T(8,128)(2,1)}, bf16[4,256,1024]{2,1,0:T(8,128)(2,1)}, u32[]{:S(2)}, u32[]{:S(2)}) collective-permute-start(bf16[4,256,1024]{2,1,0:T(8,128)(2,1)} %pad_maximum_fusion.6), channel_id=1, source_target_pairs={{0,1},{1,0},{2,3},{3,2},{4,5},{5,4},{6,7},{7,6},{8,9},{9,8},{10,11... | collective-permute-start | bytes 6291464 | tf_op jit(solution)/shard_map/ppermute | solution.py:341
  895.3 62.9 %collective-permute-start.26 = (bf16[4,256,1024]{2,1,0:T(8,128)(2,1)}, bf16[4,256,1024]{2,1,0:T(8,128)(2,1)}, u32[]{:S(2)}, u32[]{:S(2)}) collective-permute-start(bf16[4,256,1024]{2,1,0:T(8,128)(2,1)} %pad_maximum_fusion.5), channel_id=1, source_target_pairs={{0,4},{2,6},{4,0},{6,2},{8,12},{10,14},{12,8},{14,10},{16,20},{18,... | collective-permute-start | bytes 6291464 | tf_op jit(solution)/shard_map/ppermute | solution.py:337
  900.2 120.8 %collective-permute-start.29 = (bf16[4,256,1024]{2,1,0:T(8,128)(2,1)}, bf16[4,256,1024]{2,1,0:T(8,128)(2,1)}, u32[]{:S(2)}, u32[]{:S(2)}) collective-permute-start(bf16[4,256,1024]{2,1,0:T(8,128)(2,1)} %add_convert_fusion.1), channel_id=1, source_target_pairs={{0,4},{2,6},{4,0},{6,2},{8,12},{10,14},{12,8},{14,10},{16,20},{18,... | collective-permute-start | bytes 6291464 | tf_op jit(solution)/shard_map/ppermute | solution.py:337
  905.9 115.1 %collective-permute-start.30 = (bf16[4,256,1024]{2,1,0:T(8,128)(2,1)}, bf16[4,256,1024]{2,1,0:T(8,128)(2,1)}, u32[]{:S(2)}, u32[]{:S(2)}) collective-permute-start(bf16[4,256,1024]{2,1,0:T(8,128)(2,1)} %add_convert_fusion), channel_id=1, source_target_pairs={{0,1},{1,0},{2,3},{3,2},{4,5},{5,4},{6,7},{7,6},{8,9},{9,8},{10,11... | collective-permute-start | bytes 6291464 | tf_op jit(solution)/shard_map/ppermute | solution.py:341
  922.4 128.5 %collective-permute-start.33 = (bf16[256,2048]{1,0:T(8,128)(2,1)}, bf16[256,2048]{1,0:T(8,128)(2,1)}, u32[]{:S(2)}, u32[]{:S(2)}) collective-permute-start(bf16[256,2048]{1,0:T(8,128)(2,1)} %select_convert_fusion), channel_id=1, source_target_pairs={{0,1},{1,0},{2,3},{3,2},{4,5},{5,4},{6,7},{7,6},{8,9},{9,8},{10,11... | collective-permute-start | bytes 3145736 | tf_op jit(solution)/shard_map/ppermute | solution.py:341
  1032.1 41.3 %collective-permute-start.34 = (bf16[256,2048]{1,0:T(8,128)(2,1)}, bf16[256,2048]{1,0:T(8,128)(2,1)}, u32[]{:S(2)}, u32[]{:S(2)}) collective-permute-start(bf16[256,2048]{1,0:T(8,128)(2,1)} %get-tuple-element.270), channel_id=1, source_target_pairs={{0,8},{2,10},{4,12},{6,14},{8,0},{10,2},{12,4},{14,6},{16,24},{18,... | collective-permute-start | bytes 3145736 | tf_op jit(solution)/shard_map/ppermute | solution.py:372
  1033.7 61.9 %collective-permute-start.35 = (bf16[256,2048]{1,0:T(8,128)(2,1)}, bf16[256,2048]{1,0:T(8,128)(2,1)}, u32[]{:S(2)}, u32[]{:S(2)}) collective-permute-start(bf16[256,2048]{1,0:T(8,128)(2,1)} %get-tuple-element.269), channel_id=1, source_target_pairs={{0,8},{2,10},{4,12},{6,14},{8,0},{10,2},{12,4},{14,6},{16,24},{18,... | collective-permute-start | bytes 3145736 | tf_op jit(solution)/shard_map/ppermute | solution.py:372
  1055.3 45.3 %collective-permute-start.42 = (f32[2,33,128]{2,0,1:T(2,128)S(1)}, f32[2,33,128]{2,0,1:T(2,128)S(1)}, u32[]{:S(2)}, u32[]{:S(2)}) collective-permute-start(f32[2,33,128]{2,0,1:T(2,128)S(1)} %dynamic-slice_bitcast_fusion.2), channel_id=1, source_target_pairs={{0,4},{2,6},{4,0},{6,2},{8,12},{10,14},{12,8},{14,10},{16,20},{18,... | collective-permute-start | bytes 101384 | tf_op jit(solution)/shard_map/ppermute | solution.py:412
  1098.2 47.9 %collective-permute-start.39 = (bf16[256,2048]{1,0:T(8,128)(2,1)}, bf16[256,2048]{1,0:T(8,128)(2,1)}, u32[]{:S(2)}, u32[]{:S(2)}) collective-permute-start(bf16[256,2048]{1,0:T(8,128)(2,1)} %add_convert_fusion.11), channel_id=1, source_target_pairs={{0,16},{2,18},{4,20},{6,22},{8,24},{10,26},{12,28},{14,30},{16,0},... | collective-permute-start | bytes 3145736 | tf_op jit(solution)/shard_map/ppermute | solution.py:376
  1102.0 5.2 collective-permute-start.44
  1149.8 8.5 collective-permute-start.46
  1151.0 15.2 %collective-permute-start.41 = (bf16[128,2048]{1,0:T(8,128)(2,1)}, bf16[128,2048]{1,0:T(8,128)(2,1)}, u32[]{:S(2)}, u32[]{:S(2)}) collective-permute-start(bf16[128,2048]{1,0:T(8,128)(2,1)} %reduce-scatter.5.cloned.1.call-done), channel_id=1, source_target_pairs={{0,1},{1,0},{2,3},{3,2},{4,5},{5,4},{6,7},{7,6},{8,9},{9,8},{10,11... | collective-permute-start | bytes 1572872 | tf_op jit(solution)/shard_map/ppermute | solution.py:341
  1152.7 27.9 %collective-permute-start.40 = (bf16[128,3072]{1,0:T(8,128)(2,1)}, bf16[128,3072]{1,0:T(8,128)(2,1)}, u32[]{:S(2)}, u32[]{:S(2)}) collective-permute-start(bf16[128,3072]{1,0:T(8,128)(2,1)} %reduce-scatter.3.cloned.1.call-done.mine_ref), channel_id=1, source_target_pairs={{0,1},{1,0},{2,3},{3,2},{4,5},{5,4},{6,7},{7,6},{8,9},{9,8},{10,11... | collective-permute-start | bytes 2359304 | tf_op jit(solution)/shard_map/ppermute | solution.py:341
  (75 other events, 2160.4 us)
Sparse Core Ops, SparseCore 0:
  10.4 112.8 all-gather.3
  125.4 134.2 all-gather.7
  261.9 168.0 all-gather.5
  781.4 108.4 reduce-scatter.4
  893.8 171.1 reduce-scatter.2

commit v12 on v11

--- a/solution.py
+++ b/solution.py
@@ -405,13 +405,18 @@
     return values
 
 
-def halve_owned(values, fsdp, spot, steps):
-    for step in steps:
+def sum_owned(values, fsdp, spot):
+    items, shard = values.shape[0], values.shape[1] // fsdp
+    values = values.reshape(items, fsdp, shard).swapaxes(0, 1)
+    step = fsdp // 2
+    while step:
         bit = (spot // step) % 2
-        values = values.reshape(2, values.shape[0] // 2, *values.shape[1:])
+        values = values.reshape(2, step, items, shard)
         other = lax.ppermute(take(values, 1 - bit), "fsdp", [(i, i ^ step) for i in range(fsdp)])
         values = take(values, bit) + other
-    return values
+        step //= 2
+    values = values[0]
+    return values + swap_ctx(values)
 
 
 def turn(values):
@@ -1003,27 +1008,27 @@
     side_one, side_two, ctx_one, ctx_two = out_sums
     out_far[0] = swap_ctx(out_far[0])
     grad_attended = mul(grad_branch, out_all, rhs_turned).astype(low)
-    grad_out_part = mul(attended, grad_branch, lhs_turned).astype(low)
-    grad_q, grad_k, grad_v, gain_q_part, gain_k_part = attend_grad(
-        projected, roped_q, roped_k, values_low, grad_attended, cosine, sine, gain_q, gain_k, kv_heads, group
-    )
-    grad_projected = jnp.concatenate([grad_q, grad_k, grad_v], axis=1)
-    grad_projected, out_far = hold(grad_projected, out_far)
+    grad_attended, out_far = hold(grad_attended, out_far)
     got = [
         swap_ctx(ctx_one),
         swap_side(side_two),
         swap_side(add_low(side_one, out_far[0])),
         swap_ctx(add_low(ctx_two, out_far[1])),
     ]
+    grad_out_part = mul(attended, grad_branch, lhs_turned).astype(low)
+    grad_q, grad_k, grad_v, gain_q_part, gain_k_part = attend_grad(
+        projected, roped_q, roped_k, values_low, grad_attended, cosine, sine, gain_q, gain_k, kv_heads, group
+    )
+    grad_projected = jnp.concatenate([grad_q, grad_k, grad_v], axis=1)
+    grad_projected, (got[0], got[1]) = hold(grad_projected, (got[0], got[1]))
     grad_qkv_part = mul(low_in, grad_projected, lhs_turned).astype(low)
+    grad_projected, got = hold(grad_projected, got)
+    entries = joined(places, out_own, got)
     grad_normed_part = mul(grad_projected, qkv_all, rhs_turned)
-    early = jnp.concatenate([grad_router.T, grad_moe_gain[None]], axis=0)
-    early = early.reshape(experts_all + 1, fsdp, shard).swapaxes(0, 1)
-    early = halve_owned(early, fsdp, spot, (8, 4))
+    (rows, grad_pair, hidden, grad_rows), entries = hold((rows, grad_pair, hidden, grad_rows), entries)
+    one, two = line_first(entries, place)
     grad_gate_up = mul(rows, grad_pair, lhs_turned)[None]
-    got, early = hold(got, early)
-    entries = joined(places, out_own, got)
-    one, two = line_first(entries, place)
+    grad_down = mul(hidden, grad_rows, lhs_turned)[None]
     grad_normed = of_block(grad_normed_part, rank) + swap_ctx(
         of_block(grad_normed_part, 1 - rank).astype(low)
     ).astype(full)
@@ -1039,8 +1044,8 @@
     )
     qkv_mine = lax.psum_scatter(grad_qkv_part, "fsdp", scatter_dimension=0, tiled=True)
     grad_qkv = all_heads(rank_at, qkv_mine, swap_ctx(qkv_mine), head_dim, my_heads)
-    early = halve_owned(early, fsdp, spot, (2, 1))[0]
-    early = early + swap_ctx(early)
+    early, got = hold(jnp.concatenate([grad_router.T, grad_moe_gain[None]], axis=0), got)
+    early = sum_owned(early, fsdp, spot)
     late = jnp.concatenate(
         [
             grad_attn_gain.reshape(-1, head_dim),
@@ -1049,10 +1054,9 @@
         ],
         axis=0,
     )
-    grad_down = mul(hidden, grad_rows, lhs_turned)[None]
     late, (one, two, grad_gate_up, grad_down) = hold(late, (one, two, grad_gate_up, grad_down))
     far = line_second(entries, two)
-    late = swap_ctx(late) + late
+    late = late + swap_ctx(late)
     late, far = hold(sum_partners(late, fsdp, (1, 2)), far)
     output = (mixed + entries[0].astype(full) + one.astype(full) + far.astype(full)).astype(low)
     late = sum_partners(late, fsdp, (4, 8))

time: 1200 us -> 1190 us (level)
    ppermute x2, waiting for transfers between devices: 39.5 us -> 0.01 us  [line_first(): lax.ppermute(item, 'fsdp', [(i, i ^ 4) for i in range(fsdp)])]
    ppermute x8, waiting for transfers between devices: 104 us -> 137 us  [swap_side(): return lax.ppermute(values, 'fsdp', side_pairs(lax.axis_size('fsdp')))]
    ppermute x4, waiting for transfers between devices: 8.91 us -> 33.7 us  [sum_owned(): lax.ppermute(take(values, 1 - bit), 'fsdp', [(i, i ^ step) for i in range...]
    ppermute x19, waiting for transfers between devices: 275 us -> 259 us  [swap_ctx(): return lax.ppermute(values, 'ctx', [(0, 1), (1, 0)])]
  transfers between devices with their start and end apart: 53 -> 53, of which waited for: 30 -> 29; matrix products, arithmetic and copies ran while one was open for 19% -> 19% of each run, Pallas kernels for 16% -> 16%
where the time goes in v12:
time: 1190 us; the launch traced here: 1180 us
  waiting for transfers between devices  605 us (51%)
  Pallas kernels  225 us (19%)
  matrix products  114 us (10%)
  other arithmetic  106 us (9%)
  starting transfers between devices  53.6 us (5%)
  blocking collectives  35.6 us (3%)
  local copies, waits for them, and re-layouts  27.5 us (2%)
  between operations  15.5 us (1%)
    ppermute x19, waiting for transfers between devices, swap_ctx(): return lax.ppermute(values, 'ctx', [(0, 1), (1, 0)])  259 us
    ppermute x8, waiting for transfers between devices, swap_side(): return lax.ppermute(values, 'fsdp', side_pairs(lax.axis_size('fsdp')))  137 us
    pallas_call x4, Pallas kernels, run_expert(): pl.pallas_call(expert_kernel, grid_spec=grid_spec, out_shape=[shape((step...  135 us
    dot_general x11, matrix products, mul(): return lax.dot_general(left, right, dims, preferred_element_type=full)  114 us
    convert_element_type x20, other arithmetic, add_low(): return (one.astype(full) + two.astype(full)).astype(low)  66.2 us
    all_gather x1, waiting for transfers between devices, body_gathered(): weights_all = lax.all_gather(weights_local, 'fsdp', axis=0, tiled=True)  65.6 us
    pallas_call x2, Pallas kernels, run_result(): pl.pallas_call(result_kernel, grid_spec=pltpu.PrefetchScalarGridSpec(num_...  40.2 us
    ppermute x3, waiting for transfers between devices, line_shift(): lax.ppermute(values, 'fsdp', [(i, (i + 4 * step) % fsdp) for i in range(f...  39.8 us
  transfers between devices with their start and end apart: 53, of which 29 were waited for; matrix products, arithmetic and copies ran while one was open for 19% of the time, Pallas kernels for 16%

profile of v12, /device:TPU:0, one launch (start us, length us, event | category | flops | bytes accessed | tf_op | source)
XLA Modules:
  0.0 1182.3 jit_solution(15810970626795523697)
XLA Ops:
  13.4 13.3 %collective-permute-done.3 = bf16[256,1152]{1,0:T(8,128)(2,1)S(1)} collective-permute-done((bf16[256,1152]{1,0:T(8,128)(2,1)S(1)}, bf16[256,1152]{1,0:T(8,128)(2,1)S(1)}, u32[]{:S(2)}, u32[]{:S(2)}) %collective-permute-start.3) | collective-permute-done | bytes 589856 | tf_op jit(solution)/shard_map/ppermute | solution.py:341
  31.2 22.9 %all_gather.12 = bf16[2048,34]{0,1:T(8,128)(2,1)S(1)} all-gather(bf16[128,34]{0,1:T(8,128)(2,1)S(1)} %pad_maximum_fusion.22), channel_id=1, replica_groups=mesh['fsdp'=16,'ctx'=2] {'fsdp'}, dimensions={0}, use_global_device_ids=true | all-gather | bytes 147968 | tf_op jit(solution)/shard_map/all_gather | solution.py:844
  57.6 65.6 %all-gather.4.cloned.1.call-done = bf16[2048,5120]{1,0:T(8,128)(2,1)} async-done(((bf16[128,5120]{1,0:T(8,128)(2,1)}), bf16[2048,5120]{1,0:T(8,128)(2,1)}) %all-gather.4.cloned.1.call-update) | async-done | bytes 20971536 | tf_op jit(solution)/shard_map/all_gather | solution.py:845
  123.2 11.5 fusion.2.q_ref.k_ref.v_ref
  134.8 18.3 %attend.1 = (bf16[512,2048]{1,0:T(8,128)(2,1)S(1)}, bf16[512,2048]{1,0:T(8,128)(2,1)S(1)}, bf16[512,512]{1,0:T(8,128)(2,1)S(1)}, bf16[512,512]{1,0:T(8,128)(2,1)S(1)}) custom-call(f32[512,3072]{1,0:T(8,128)} %fusion.2.q_ref.k_ref.v_ref, f32[512,3072]{1,0:T(8,128)} %fusion.2.q_ref.k_ref.v_ref, f32[512,3072]{1,0:T(8,128)} %fusion.2.q_ref.k_ref.v_ref, ...), custom_call_target="tpu_custom_call" | custom-call | flops 2147483648 | bytes 9437184 | tf_op jit(solution)/shard_map/attend/pallas_call | solution.py:530
  153.1 8.5 fusion.6
  163.7 23.8 %collective-permute-done.1 = bf16[256,2048]{1,0:T(8,128)(2,1)S(1)} collective-permute-done((bf16[256,2048]{1,0:T(8,128)(2,1)S(1)}, bf16[256,2048]{1,0:T(8,128)(2,1)S(1)}, u32[]{:S(2)}, u32[]{:S(2)}) %collective-permute-start.1) | collective-permute-done | bytes 1048608 | tf_op jit(solution)/shard_map/ppermute | solution.py:341
  191.9 23.1 %collective-permute-done.2 = bf16[256,2048]{1,0:T(8,128)(2,1)S(1)} collective-permute-done((bf16[256,2048]{1,0:T(8,128)(2,1)S(1)}, bf16[256,2048]{1,0:T(8,128)(2,1)S(1)}, u32[]{:S(2)}, u32[]{:S(2)}) %collective-permute-start.2) | collective-permute-done | bytes 1048608 | tf_op jit(solution)/shard_map/ppermute | solution.py:341
  218.5 12.8 %all_to_all.24 = f32[32,1,256]{2,1,0:T(1,128)S(1)} all-to-all(f32[32,1,256]{2,1,0:T(1,128)S(1)} %copy.60), channel_id=1, replica_groups=mesh['fsdp'=16,'ctx'=2] {'fsdp','ctx'}, dimensions={0} | all-to-all | bytes 65536 | tf_op jit(solution)/shard_map/all_to_all | solution.py:882
  231.3 28.4 %all-gather.8.cloned.1.call-done = bf16[4096,3200]{1,0:T(8,128)(2,1)} async-done(((bf16[256,3200]{1,0:T(8,128)(2,1)}), bf16[4096,3200]{1,0:T(8,128)(2,1)}) %all-gather.8.cloned.1.call-update) | async-done | bytes 26214416 | tf_op jit(solution)/shard_map/all_gather | solution.py:852
  259.7 6.9 slice.403
  269.3 157.8 %collective-permute-done.4.far_ref = bf16[8,2,256,896]{3,2,1,0:T(8,128)(2,1)} collective-permute-done((bf16[8,2,256,896]{3,2,1,0:T(8,128)(2,1)}, bf16[8,2,256,896]{3,2,1,0:T(8,128)(2,1)}, u32[]{:S(2)}, u32[]{:S(2)}) %collective-permute-start.4) | collective-permute-done | bytes 7340064 | tf_op jit(solution)/shard_map/ppermute | solution.py:341
  429.9 33.0 %experts.4 = (bf16[4,256,2048]{2,1,0:T(8,128)(2,1)}, bf16[4,256,2048]{2,1,0:T(8,128)(2,1)}, f32[8,2,2,1,256]{4,3,2,1,0:T(1,128)}, bf16[4096,2048]{1,0:T(8,128)(2...) custom-call(s32[1]{0:T(128)} %bitcast.6.core_ref, s32[16]{0:T(128)} %stack.35.order, ...), custom_call_target="tpu_custom_call" | custom-call | flops 19327352832 | bytes 38273024 | tf_op jit(solution)/shard_map/experts/pallas_call | solution.py:679
  463.3 7.1 collective-permute-done.5
  470.4 4.2 add_convert_fusion.8
  477.8 34.1 %experts.5 = (bf16[4,256,2048]{2,1,0:T(8,128)(2,1)}, bf16[4,256,2048]{2,1,0:T(8,128)(2,1)}, f32[8,2,2,1,256]{4,3,2,1,0:T(1,128)}, bf16[4096,2048]{1,0:T(8,128)(2...) custom-call(s32[1]{0:T(128)} %bitcast.6.core_ref, ...), custom_call_target="tpu_custom_call", output_to_operand_aliasing={{2}: (8, {}), {3}: (9, {}), {4}: (10, {}), {5}: (11, {}), {... | custom-call | flops 19327352832 | bytes 38273024 | tf_op jit(solution)/shard_map/experts/pallas_call | solution.py:679
  512.0 10.7 collective-permute-done.6
  525.1 34.1 %experts.6 = (bf16[4,256,2048]{2,1,0:T(8,128)(2,1)}, bf16[4,256,2048]{2,1,0:T(8,128)(2,1)}, f32[8,2,2,1,256]{4,3,2,1,0:T(1,128)}, bf16[4096,2048]{1,0:T(8,128)(2...) custom-call(s32[1]{0:T(128)} %bitcast.6.core_ref, ...), custom_call_target="tpu_custom_call", output_to_operand_aliasing={{2}: (8, {}), {3}: (9, {}), {4}: (10, {}), {5}: (11, {}), {... | custom-call | flops 19327352832 | bytes 38273024 | tf_op jit(solution)/shard_map/experts/pallas_call | solution.py:679
  559.8 4.4 add_convert_fusion.28
  571.5 33.8 %experts.7 = (bf16[4,256,2048]{2,1,0:T(8,128)(2,1)}, bf16[4,256,2048]{2,1,0:T(8,128)(2,1)}, f32[8,2,2,1,256]{4,3,2,1,0:T(1,128)}, bf16[4096,2048]{1,0:T(8,128)(2...) custom-call(s32[1]{0:T(128)} %bitcast.6.core_ref, ...), custom_call_target="tpu_custom_call", output_to_operand_aliasing={{2}: (8, {}), {3}: (9, {}), {4}: (10, {}), {5}: (11, {}), {... | custom-call | flops 19327352832 | bytes 38273024 | tf_op jit(solution)/shard_map/experts/pallas_call | solution.py:679
  605.3 7.1 collective-permute-done.11
  613.1 4.7 all-to-all-start.1
  617.9 5.7 add_convert_fusion.7
  633.8 4.0 add_convert_fusion.22
  646.3 11.9 %results.2 = (bf16[4,256,2048]{2,1,0:T(8,128)(2,1)}, bf16[4,256,2048]{2,1,0:T(8,128)(2,1)}) custom-call(s32[1]{0:T(128)} %bitcast.6.core_ref, s32[16]{0:T(128)} %stack.35.order, bf16[4096,768]{1,0:T(8,128)(2,1)} %get-tuple-element.228.z_ref, f32[8,2,2,1,256]{4,3,2,1,0:T(1,128)} %reshape.271.w_ref, bf16[768,2048]{1,0:T(8,128)(2,1)} %bitcast.154), custom_call_target="tpu_custom_call" | custom-call | flops 4294967296 | bytes 13107200 | tf_op jit(solution)/shard_map/results/pallas_call | solution.py:710
  658.8 28.3 %results.3 = (bf16[12,256,2048]{2,1,0:T(8,128)(2,1)}, bf16[12,256,2048]{2,1,0:T(8,128)(2,1)}) custom-call(s32[1]{0:T(128)} %bitcast.6.core_ref, s32[48]{0:T(128)} %stack.44.order, bf16[4096,768]{1,0:T(8,128)(2,1)} %get-tuple-element.228.z_ref, f32[8,2,2,1,256]{4,3,2,1,0:T(1,128)} %reshape.271.w_ref, bf16[768,2048]{1,0:T(8,128)(2,1)} %bitcast.155), custom_call_target="tpu_custom_call" | custom-call | flops 12884901888 | bytes 33030144 | tf_op jit(solution)/shard_map/results/pallas_call | solution.py:710
  687.1 13.7 %collective-permute-done.20 = bf16[256,2048]{1,0:T(8,128)(2,1)} collective-permute-done((bf16[256,2048]{1,0:T(8,128)(2,1)}, bf16[256,2048]{1,0:T(8,128)(2,1)}, u32[]{:S(2)}, u32[]{:S(2)}) %collective-permute-start.20) | collective-permute-done | bytes 1048608 | tf_op jit(solution)/shard_map/ppermute | solution.py:358
  707.5 26.2 %collective-permute-done.21 = bf16[256,2048]{1,0:T(8,128)(2,1)S(1)} collective-permute-done((bf16[256,2048]{1,0:T(8,128)(2,1)S(1)}, bf16[256,2048]{1,0:T(8,128)(2,1)S(1)}, u32[]{:S(2)}, u32[]{:S(2)}) %collective-permute-start.21) | collective-permute-done | bytes 1048608 | tf_op jit(solution)/shard_map/ppermute | solution.py:358
  739.4 5.4 add_convert_fusion.2
  746.3 5.2 add_convert_fusion.13
  763.3 6.2 collective-permute-done.24
  773.4 6.8 convolution_convert_fusion.1
  784.4 10.6 fusion.11.go_ref
  795.1 45.4 %collective-permute-done.26 = bf16[4,256,1024]{2,1,0:T(8,128)(2,1)S(1)} collective-permute-done((bf16[4,256,1024]{2,1,0:T(8,128)(2,1)}, bf16[4,256,1024]{2,1,0:T(8,128)(2,1)S(1)}, u32[]{:S(2)}, u32[]{:S(2)}) %collective-permute-start.26) | collective-permute-done | bytes 2097184 | tf_op jit(solution)/shard_map/ppermute | solution.py:337
  842.4 25.2 %attend_grad.1 = (bf16[512,2048]{1,0:T(8,128)(2,1)S(1)}, bf16[512,512]{1,0:T(8,128)(2,1)S(1)}, bf16[512,512]{1,0:T(8,128)(2,1)S(1)}, f32[4,1,128]{2,1,0:T(1,128)S(1)}, f32[4,1,128]{2,1,0:T(1,128)S(1)}) custom-call(f32[512,3072]{1,0:T(8,128)} %fusion.2.q_ref.k_ref.v_ref, f32[512,3072]{1,0:T(8,128)} %fusion.2.q_ref.k_ref.v_ref, bf16[512,2048]{1,0:T(8,128)(2,1)} %copy-done, ...), custom_call_target="tpu_custom_call" | custom-call | flops 5368709120 | bytes 15728640 | tf_op jit(solution)/shard_map/attend_grad/pallas_call | solution.py:554
  868.0 5.0 collective-permute-done.27
  873.0 26.9 %collective-permute-done.28 = bf16[4,256,1024]{2,1,0:T(8,128)(2,1)} collective-permute-done((bf16[4,256,1024]{2,1,0:T(8,128)(2,1)}, bf16[4,256,1024]{2,1,0:T(8,128)(2,1)}, u32[]{:S(2)}, u32[]{:S(2)}) %collective-permute-start.28) | collective-permute-done | bytes 2097184 | tf_op jit(solution)/shard_map/ppermute | solution.py:337
  900.0 9.9 convolution_convert_fusion
  909.9 4.7 add_convert_fusion.1
  920.3 56.7 %collective-permute-done.29 = bf16[4,256,1024]{2,1,0:T(8,128)(2,1)} collective-permute-done((bf16[4,256,1024]{2,1,0:T(8,128)(2,1)}, bf16[4,256,1024]{2,1,0:T(8,128)(2,1)}, u32[]{:S(2)}, u32[]{:S(2)}) %collective-permute-start.29) | collective-permute-done | bytes 2097184 | tf_op jit(solution)/shard_map/ppermute | solution.py:337
  977.0 11.2 fusion
  1006.8 33.1 %convolution_bitcast_fusion = f32[1,2048,1536]{2,1,0:T(8,128)} fusion(bf16[4096,2048]{1,0:T(8,128)(2,1)S(1)} %bitcast.143, bf16[4096,1536]{1,0:T(8,128)(2,1)} %get-tuple-element.227), kind=kOutput, calls=%fused_computation.5 | convolution fusion | flops 25769803776 | bytes 41943040 | tf_op jit(solution)/shard_map/dot_general | solution.py:321
  1039.9 32.5 %collective-permute-done.40 = f32[8,33,128]{2,0,1:T(8,128)S(1)} collective-permute-done((f32[8,33,128]{2,0,1:T(8,128)S(1)}, f32[8,33,128]{2,0,1:T(8,128)S(1)}, u32[]{:S(2)}, u32[]{:S(2)}) %collective-permute-start.40) | collective-permute-done | bytes 135200 | tf_op jit(solution)/shard_map/ppermute | solution.py:415
  1075.0 19.3 %convolution_bitcast_fusion.1 = f32[1,768,2048]{2,1,0:T(8,128)} fusion(bf16[4096,768]{1,0:T(8,128)(2,1)S(1)} %bitcast.149, bf16[4096,2048]{1,0:T(8,128)(2,1)} %get-tuple-element.229), kind=kOutput, calls=%fused_computation.26 | convolution fusion | flops 12884901888 | bytes 29360128 | tf_op jit(solution)/shard_map/dot_general | solution.py:321
  1114.1 23.3 %collective-permute-done.37 = bf16[256,2048]{1,0:T(8,128)(2,1)} collective-permute-done((bf16[256,2048]{1,0:T(8,128)(2,1)}, bf16[256,2048]{1,0:T(8,128)(2,1)}, u32[]{:S(2)}, u32[]{:S(2)}) %collective-permute-start.37) | collective-permute-done | bytes 1048608 | tf_op jit(solution)/shard_map/ppermute | solution.py:376
  1144.4 6.9 fusion.21
  1152.5 4.9 collective-permute-done.39
  1160.1 11.1 collective-permute-done.38.other_ref
  (353 shorter events, 160.5 us)
Async XLA Ops:
  7.2 116.1 %all-gather.4.cloned.1.call-start = ((), (), s32[]{:S(2)}) async-start(), calls=%async_computation.4 | async-start | bytes 22282240 | tf_op jit(solution)/shard_map/all_gather | solution.py:845
  10.2 249.5 %all-gather.8.cloned.1.call-start = ((), (), s32[]{:S(2)}) async-start(), calls=%async_computation.6 | async-start | bytes 27852800 | tf_op jit(solution)/shard_map/all_gather | solution.py:852
  10.4 16.3 %collective-permute-start.3 = (bf16[256,1152]{1,0:T(8,128)(2,1)S(1)}, bf16[256,1152]{1,0:T(8,128)(2,1)S(1)}, u32[]{:S(2)}, u32[]{:S(2)}) collective-permute-start(bf16[256,1152]{1,0:T(8,128)(2,1)S(1)} %slice.401), channel_id=1, source_target_pairs={{0,1},{1,0},{2,3},{3,2},{4,5},{5,4},{6,7},{7,6},{8,9},{9,8},{10,11... | collective-permute-start | bytes 1769480 | tf_op jit(solution)/shard_map/ppermute | solution.py:341
  28.1 401.9 %all-gather.6.cloned.1.call-start = ((), (), s32[]{:S(2)}) async-start(), calls=%async_computation.5 | async-start | bytes 35651584 | tf_op jit(solution)/shard_map/all_gather | solution.py:873
  28.1 26.4 %collective-permute-start = (bf16[256,2048]{1,0:T(8,128)(2,1)S(1)}, bf16[256,2048]{1,0:T(8,128)(2,1)}, u32[]{:S(2)}, u32[]{:S(2)}) collective-permute-start(bf16[256,2048]{1,0:T(8,128)(2,1)S(1)} %copy-done.6), channel_id=1, source_target_pairs={{0,1},{1,0},{2,3},{3,2},{4,5},{5,4},{6,7},{7,6},{8,9},{9,8},{10,11... | collective-permute-start | bytes 3145736 | tf_op jit(solution)/shard_map/ppermute | solution.py:341
  162.1 25.4 %collective-permute-start.1 = (bf16[256,2048]{1,0:T(8,128)(2,1)S(1)}, bf16[256,2048]{1,0:T(8,128)(2,1)S(1)}, u32[]{:S(2)}, u32[]{:S(2)}) collective-permute-start(bf16[256,2048]{1,0:T(8,128)(2,1)S(1)} %select_convert_fusion.1), channel_id=1, source_target_pairs={{0,1},{1,0},{2,3},{3,2},{4,5},{5,4},{6,7},{7,6},{8,9},{9,8},{10,11... | collective-permute-start | bytes 3145736 | tf_op jit(solution)/shard_map/ppermute | solution.py:341
  190.3 24.6 %collective-permute-start.2 = (bf16[256,2048]{1,0:T(8,128)(2,1)S(1)}, bf16[256,2048]{1,0:T(8,128)(2,1)S(1)}, u32[]{:S(2)}, u32[]{:S(2)}) collective-permute-start(bf16[256,2048]{1,0:T(8,128)(2,1)S(1)} %multiply_convert_fusion), channel_id=1, source_target_pairs={{0,1},{1,0},{2,3},{3,2},{4,5},{5,4},{6,7},{7,6},{8,9},{9,8},{10,11... | collective-permute-start | bytes 3145736 | tf_op jit(solution)/shard_map/ppermute | solution.py:341
  266.6 160.5 %collective-permute-start.4 = (bf16[8,2,256,896]{3,2,1,0:T(8,128)(2,1)}, bf16[8,2,256,896]{3,2,1,0:T(8,128)(2,1)}, u32[]{:S(2)}, u32[]{:S(2)}) collective-permute-start(bf16[8,2,256,896]{3,2,1,0:T(8,128)(2,1)} %slice.403), channel_id=1, source_target_pairs={{0,1},{1,0},{2,3},{3,2},{4,5},{5,4},{6,7},{7,6},{8,9},{9,8},{10,11... | collective-permute-start | bytes 22020104 | tf_op jit(solution)/shard_map/ppermute | solution.py:341
  462.9 7.4 collective-permute-start.5
  474.6 48.1 %collective-permute-start.6 = (bf16[4,256,1024]{2,1,0:T(8,128)(2,1)}, bf16[4,256,1024]{2,1,0:T(8,128)(2,1)}, u32[]{:S(2)}, u32[]{:S(2)}) collective-permute-start(bf16[4,256,1024]{2,1,0:T(8,128)(2,1)} %get-tuple-element.138), channel_id=1, source_target_pairs={{0,1},{1,0},{2,3},{3,2},{4,5},{5,4},{6,7},{7,6},{8,9},{9,8},{10,11... | collective-permute-start | bytes 6291464 | tf_op jit(solution)/shard_map/ppermute | solution.py:341
  476.1 47.8 %collective-permute-start.7 = (bf16[4,256,1024]{2,1,0:T(8,128)(2,1)}, bf16[4,256,1024]{2,1,0:T(8,128)(2,1)}, u32[]{:S(2)}, u32[]{:S(2)}) collective-permute-start(bf16[4,256,1024]{2,1,0:T(8,128)(2,1)} %get-tuple-element.139), channel_id=1, source_target_pairs={{0,4},{2,6},{4,0},{6,2},{8,12},{10,14},{12,8},{14,10},{16,20},{18,... | collective-permute-start | bytes 6291464 | tf_op jit(solution)/shard_map/ppermute | solution.py:337
  523.9 35.9 %collective-permute-start.8 = (bf16[4,256,2048]{2,1,0:T(8,128)(2,1)}, bf16[4,256,2048]{2,1,0:T(8,128)(2,1)}, u32[]{:S(2)}, u32[]{:S(2)}) collective-permute-start(bf16[4,256,2048]{2,1,0:T(8,128)(2,1)} %get-tuple-element.140), channel_id=1, source_target_pairs={{0,2},{2,0},{4,6},{6,4},{8,10},{10,8},{12,14},{14,12},{16,18},{18,... | collective-permute-start | bytes 12582920 | tf_op jit(solution)/shard_map/ppermute | solution.py:333
  559.2 58.7 %collective-permute-start.14 = (bf16[4,256,2048]{2,1,0:T(8,128)(2,1)}, bf16[4,256,2048]{2,1,0:T(8,128)(2,1)}, u32[]{:S(2)}, u32[]{:S(2)}) collective-permute-start(bf16[4,256,2048]{2,1,0:T(8,128)(2,1)} %get-tuple-element.167), channel_id=1, source_target_pairs={{0,2},{2,0},{4,6},{6,4},{8,10},{10,8},{12,14},{14,12},{16,18},{18,... | collective-permute-start | bytes 12582920 | tf_op jit(solution)/shard_map/ppermute | solution.py:333
  564.2 41.1 %collective-permute-start.9 = (bf16[2,256,1024]{2,1,0:T(8,128)(2,1)}, bf16[2,256,1024]{2,1,0:T(8,128)(2,1)S(1)}, u32[]{:S(2)}, u32[]{:S(2)}) collective-permute-start(bf16[2,256,1024]{2,1,0:T(8,128)(2,1)} %get-tuple-element.157), channel_id=1, source_target_pairs={{0,1},{1,0},{2,3},{3,2},{4,5},{5,4},{6,7},{7,6},{8,9},{9,8},{10,11... | collective-permute-start | bytes 3145736 | tf_op jit(solution)/shard_map/ppermute | solution.py:341
  564.8 40.5 %collective-permute-start.10 = (bf16[2,256,1024]{2,1,0:T(8,128)(2,1)}, bf16[2,256,1024]{2,1,0:T(8,128)(2,1)}, u32[]{:S(2)}, u32[]{:S(2)}) collective-permute-start(bf16[2,256,1024]{2,1,0:T(8,128)(2,1)} %get-tuple-element.158), channel_id=1, source_target_pairs={{0,4},{2,6},{4,0},{6,2},{8,12},{10,14},{12,8},{14,10},{16,20},{18,... | collective-permute-start | bytes 3145736 | tf_op jit(solution)/shard_map/ppermute | solution.py:337
  567.4 44.9 %collective-permute-start.11 = (bf16[2,256,1024]{2,1,0:T(8,128)(2,1)S(1)}, bf16[2,256,1024]{2,1,0:T(8,128)(2,1)}, u32[]{:S(2)}, u32[]{:S(2)}) collective-permute-start(bf16[2,256,1024]{2,1,0:T(8,128)(2,1)S(1)} %add_convert_fusion.27), channel_id=1, source_target_pairs={{0,4},{2,6},{4,0},{6,2},{8,12},{10,14},{12,8},{14,10},{16,20},{18,... | collective-permute-start | bytes 3145736 | tf_op jit(solution)/shard_map/ppermute | solution.py:337
  569.9 42.5 %collective-permute-start.12 = (bf16[2,256,1024]{2,1,0:T(8,128)(2,1)S(1)}, bf16[2,256,1024]{2,1,0:T(8,128)(2,1)}, u32[]{:S(2)}, u32[]{:S(2)}) collective-permute-start(bf16[2,256,1024]{2,1,0:T(8,128)(2,1)S(1)} %add_convert_fusion.26), channel_id=1, source_target_pairs={{0,1},{1,0},{2,3},{3,2},{4,5},{5,4},{6,7},{7,6},{8,9},{9,8},{10,11... | collective-permute-start | bytes 3145736 | tf_op jit(solution)/shard_map/ppermute | solution.py:341
  612.4 21.4 %collective-permute-start.13 = (bf16[4,256,2048]{2,1,0:T(8,128)(2,1)}, bf16[4,256,2048]{2,1,0:T(8,128)(2,1)}, u32[]{:S(2)}, u32[]{:S(2)}) collective-permute-start(bf16[4,256,2048]{2,1,0:T(8,128)(2,1)} %get-tuple-element.163), channel_id=1, source_target_pairs={{0,2},{2,0},{4,6},{6,4},{8,10},{10,8},{12,14},{14,12},{16,18},{18,... | collective-permute-start | bytes 12582920 | tf_op jit(solution)/shard_map/ppermute | solution.py:333
  613.1 12.0 %all-to-all-start.1 = ((f32[32,1,256]{2,1,0:T(1,128)}), f32[32,1,256]{2,1,0:T(1,128)S(1)}, u32[]{:S(2)}, u32[]{:S(2)}) async-start(f32[32,1,256]{2,1,0:T(1,128)} %bitcast.162), calls=%async_computation.1 | async-start | bytes 65536 | tf_op jit(solution)/shard_map/all_to_all | solution.py:970
  617.8 523.3 %reduce-scatter.5.cloned.1.call-start = ((), (), s32[]{:S(2)}) async-start(), calls=%async_computation.8 | async-start | bytes 8912896 | tf_op jit(solution)/shard_map/reduce_scatter | solution.py:1038
  630.6 27.6 %collective-permute-start.19 = (bf16[256,2048]{1,0:T(8,128)(2,1)}, bf16[256,2048]{1,0:T(8,128)(2,1)S(1)}, u32[]{:S(2)}, u32[]{:S(2)}) collective-permute-start(bf16[256,2048]{1,0:T(8,128)(2,1)} %pad_maximum_fusion.11), channel_id=1, source_target_pairs={{0,24},{2,26},{4,28},{6,30},{8,0},{10,2},{12,4},{14,6},{16,8},{18,... | collective-permute-start | bytes 3145736 | tf_op jit(solution)/shard_map/ppermute | solution.py:358
  633.8 67.0 %collective-permute-start.20 = (bf16[256,2048]{1,0:T(8,128)(2,1)}, bf16[256,2048]{1,0:T(8,128)(2,1)}, u32[]{:S(2)}, u32[]{:S(2)}) collective-permute-start(bf16[256,2048]{1,0:T(8,128)(2,1)} %pad_maximum_fusion.12), channel_id=1, source_target_pairs={{0,16},{2,18},{4,20},{6,22},{8,24},{10,26},{12,28},{14,30},{16,0},... | collective-permute-start | bytes 3145736 | tf_op jit(solution)/shard_map/ppermute | solution.py:358
  637.7 63.0 %collective-permute-start.15 = (bf16[2,256,1024]{2,1,0:T(8,128)(2,1)}, bf16[2,256,1024]{2,1,0:T(8,128)(2,1)}, u32[]{:S(2)}, u32[]{:S(2)}) collective-permute-start(bf16[2,256,1024]{2,1,0:T(8,128)(2,1)} %get-tuple-element.168), channel_id=1, source_target_pairs={{0,1},{1,0},{2,3},{3,2},{4,5},{5,4},{6,7},{7,6},{8,9},{9,8},{10,11... | collective-permute-start | bytes 3145736 | tf_op jit(solution)/shard_map/ppermute | solution.py:341
  639.2 61.6 %collective-permute-start.16 = (bf16[2,256,1024]{2,1,0:T(8,128)(2,1)}, bf16[2,256,1024]{2,1,0:T(8,128)(2,1)}, u32[]{:S(2)}, u32[]{:S(2)}) collective-permute-start(bf16[2,256,1024]{2,1,0:T(8,128)(2,1)} %get-tuple-element.169), channel_id=1, source_target_pairs={{0,4},{2,6},{4,0},{6,2},{8,12},{10,14},{12,8},{14,10},{16,20},{18,... | collective-permute-start | bytes 3145736 | tf_op jit(solution)/shard_map/ppermute | solution.py:337
  643.2 57.5 %collective-permute-start.17 = (bf16[2,256,1024]{2,1,0:T(8,128)(2,1)}, bf16[2,256,1024]{2,1,0:T(8,128)(2,1)}, u32[]{:S(2)}, u32[]{:S(2)}) collective-permute-start(bf16[2,256,1024]{2,1,0:T(8,128)(2,1)} %add_convert_fusion.21), channel_id=1, source_target_pairs={{0,4},{2,6},{4,0},{6,2},{8,12},{10,14},{12,8},{14,10},{16,20},{18,... | collective-permute-start | bytes 3145736 | tf_op jit(solution)/shard_map/ppermute | solution.py:337
  658.2 42.6 %collective-permute-start.18 = (bf16[2,256,1024]{2,1,0:T(8,128)(2,1)}, bf16[2,256,1024]{2,1,0:T(8,128)(2,1)}, u32[]{:S(2)}, u32[]{:S(2)}) collective-permute-start(bf16[2,256,1024]{2,1,0:T(8,128)(2,1)} %add_convert_fusion.20), channel_id=1, source_target_pairs={{0,1},{1,0},{2,3},{3,2},{4,5},{5,4},{6,7},{7,6},{8,9},{9,8},{10,11... | collective-permute-start | bytes 3145736 | tf_op jit(solution)/shard_map/ppermute | solution.py:341
  700.8 44.0 %collective-permute-start.23 = (bf16[12,256,2048]{2,1,0:T(8,128)(2,1)}, bf16[12,256,2048]{2,1,0:T(8,128)(2,1)S(1)}, u32[]{:S(2)}, u32[]{:S(2)}) collective-permute-start(bf16[12,256,2048]{2,1,0:T(8,128)(2,1)} %get-tuple-element.191), channel_id=1, source_target_pairs={{0,2},{2,0},{4,6},{6,4},{8,10},{10,8},{12,14},{14,12},{16,18},{18,... | collective-permute-start | bytes 37748744 | tf_op jit(solution)/shard_map/ppermute | solution.py:333
  700.9 36.9 %collective-permute-start.22 = (bf16[4,256,2048]{2,1,0:T(8,128)(2,1)}, bf16[4,256,2048]{2,1,0:T(8,128)(2,1)}, u32[]{:S(2)}, u32[]{:S(2)}) collective-permute-start(bf16[4,256,2048]{2,1,0:T(8,128)(2,1)} %get-tuple-element.189), channel_id=1, source_target_pairs={{0,2},{2,0},{4,6},{6,4},{8,10},{10,8},{12,14},{14,12},{16,18},{18,... | collective-permute-start | bytes 12582920 | tf_op jit(solution)/shard_map/ppermute | solution.py:333
  706.0 27.7 %collective-permute-start.21 = (bf16[256,2048]{1,0:T(8,128)(2,1)S(1)}, bf16[256,2048]{1,0:T(8,128)(2,1)S(1)}, u32[]{:S(2)}, u32[]{:S(2)}) collective-permute-start(bf16[256,2048]{1,0:T(8,128)(2,1)S(1)} %pad_maximum_fusion.13), channel_id=1, source_target_pairs={{0,8},{2,10},{4,12},{6,14},{8,16},{10,18},{12,20},{14,22},{16,24},... | collective-permute-start | bytes 3145736 | tf_op jit(solution)/shard_map/ppermute | solution.py:358
  744.8 24.7 %collective-permute-start.24 = (bf16[256,2048]{1,0:T(8,128)(2,1)S(1)}, bf16[256,2048]{1,0:T(8,128)(2,1)}, u32[]{:S(2)}, u32[]{:S(2)}) collective-permute-start(bf16[256,2048]{1,0:T(8,128)(2,1)S(1)} %fusion.50), channel_id=1, source_target_pairs={{0,1},{1,0},{2,3},{3,2},{4,5},{5,4},{6,7},{7,6},{8,9},{9,8},{10,11... | collective-permute-start | bytes 3145736 | tf_op jit(solution)/shard_map/ppermute | solution.py:341
  780.3 364.0 %reduce-scatter.3.cloned.1.call-start = ((), (), s32[]{:S(2)}) async-start(), calls=%async_computation.7 | async-start | bytes 13369344 | tf_op jit(solution)/shard_map/reduce_scatter | solution.py:1045
  780.3 60.1 %collective-permute-start.26 = (bf16[4,256,1024]{2,1,0:T(8,128)(2,1)}, bf16[4,256,1024]{2,1,0:T(8,128)(2,1)S(1)}, u32[]{:S(2)}, u32[]{:S(2)}) collective-permute-start(bf16[4,256,1024]{2,1,0:T(8,128)(2,1)} %get-tuple-element.257), channel_id=1, source_target_pairs={{0,4},{2,6},{4,0},{6,2},{8,12},{10,14},{12,8},{14,10},{16,20},{18,... | collective-permute-start | bytes 6291464 | tf_op jit(solution)/shard_map/ppermute | solution.py:337
  781.9 58.5 %collective-permute-start.25 = (bf16[4,256,1024]{2,1,0:T(8,128)(2,1)}, bf16[4,256,1024]{2,1,0:T(8,128)(2,1)S(1)}, u32[]{:S(2)}, u32[]{:S(2)}) collective-permute-start(bf16[4,256,1024]{2,1,0:T(8,128)(2,1)} %get-tuple-element.201), channel_id=1, source_target_pairs={{0,1},{1,0},{2,3},{3,2},{4,5},{5,4},{6,7},{7,6},{8,9},{9,8},{10,11... | collective-permute-start | bytes 6291464 | tf_op jit(solution)/shard_map/ppermute | solution.py:341
  783.4 89.7 %collective-permute-start.27 = (bf16[4,256,1024]{2,1,0:T(8,128)(2,1)}, bf16[4,256,1024]{2,1,0:T(8,128)(2,1)}, u32[]{:S(2)}, u32[]{:S(2)}) collective-permute-start(bf16[4,256,1024]{2,1,0:T(8,128)(2,1)} %pad_maximum_fusion.6), channel_id=1, source_target_pairs={{0,1},{1,0},{2,3},{3,2},{4,5},{5,4},{6,7},{7,6},{8,9},{9,8},{10,11... | collective-permute-start | bytes 6291464 | tf_op jit(solution)/shard_map/ppermute | solution.py:341
  783.9 116.0 %collective-permute-start.28 = (bf16[4,256,1024]{2,1,0:T(8,128)(2,1)}, bf16[4,256,1024]{2,1,0:T(8,128)(2,1)}, u32[]{:S(2)}, u32[]{:S(2)}) collective-permute-start(bf16[4,256,1024]{2,1,0:T(8,128)(2,1)} %pad_maximum_fusion.5), channel_id=1, source_target_pairs={{0,4},{2,6},{4,0},{6,2},{8,12},{10,14},{12,8},{14,10},{16,20},{18,... | collective-permute-start | bytes 6291464 | tf_op jit(solution)/shard_map/ppermute | solution.py:337
  914.6 62.4 %collective-permute-start.29 = (bf16[4,256,1024]{2,1,0:T(8,128)(2,1)}, bf16[4,256,1024]{2,1,0:T(8,128)(2,1)}, u32[]{:S(2)}, u32[]{:S(2)}) collective-permute-start(bf16[4,256,1024]{2,1,0:T(8,128)(2,1)} %add_convert_fusion.1), channel_id=1, source_target_pairs={{0,4},{2,6},{4,0},{6,2},{8,12},{10,14},{12,8},{14,10},{16,20},{18,... | collective-permute-start | bytes 6291464 | tf_op jit(solution)/shard_map/ppermute | solution.py:337
  918.4 58.6 %collective-permute-start.30 = (bf16[4,256,1024]{2,1,0:T(8,128)(2,1)}, bf16[4,256,1024]{2,1,0:T(8,128)(2,1)}, u32[]{:S(2)}, u32[]{:S(2)}) collective-permute-start(bf16[4,256,1024]{2,1,0:T(8,128)(2,1)} %add_convert_fusion), channel_id=1, source_target_pairs={{0,1},{1,0},{2,3},{3,2},{4,5},{5,4},{6,7},{7,6},{8,9},{9,8},{10,11... | collective-permute-start | bytes 6291464 | tf_op jit(solution)/shard_map/ppermute | solution.py:341
  991.6 104.4 %collective-permute-start.31 = (bf16[256,2048]{1,0:T(8,128)(2,1)}, bf16[256,2048]{1,0:T(8,128)(2,1)}, u32[]{:S(2)}, u32[]{:S(2)}) collective-permute-start(bf16[256,2048]{1,0:T(8,128)(2,1)} %select_convert_fusion), channel_id=1, source_target_pairs={{0,1},{1,0},{2,3},{3,2},{4,5},{5,4},{6,7},{7,6},{8,9},{9,8},{10,11... | collective-permute-start | bytes 3145736 | tf_op jit(solution)/shard_map/ppermute | solution.py:341
  1004.5 94.9 %collective-permute-start.32 = (bf16[256,2048]{1,0:T(8,128)(2,1)}, bf16[256,2048]{1,0:T(8,128)(2,1)}, u32[]{:S(2)}, u32[]{:S(2)}) collective-permute-start(bf16[256,2048]{1,0:T(8,128)(2,1)} %get-tuple-element.294), channel_id=1, source_target_pairs={{0,8},{2,10},{4,12},{6,14},{8,0},{10,2},{12,4},{14,6},{16,24},{18,... | collective-permute-start | bytes 3145736 | tf_op jit(solution)/shard_map/ppermute | solution.py:372
  1004.5 94.9 %collective-permute-start.33 = (bf16[256,2048]{1,0:T(8,128)(2,1)}, bf16[256,2048]{1,0:T(8,128)(2,1)}, u32[]{:S(2)}, u32[]{:S(2)}) collective-permute-start(bf16[256,2048]{1,0:T(8,128)(2,1)} %get-tuple-element.293), channel_id=1, source_target_pairs={{0,8},{2,10},{4,12},{6,14},{8,0},{10,2},{12,4},{14,6},{16,24},{18,... | collective-permute-start | bytes 3145736 | tf_op jit(solution)/shard_map/ppermute | solution.py:372
  1006.7 65.8 %collective-permute-start.40 = (f32[8,33,128]{2,0,1:T(8,128)S(1)}, f32[8,33,128]{2,0,1:T(8,128)S(1)}, u32[]{:S(2)}, u32[]{:S(2)}) collective-permute-start(f32[8,33,128]{2,0,1:T(8,128)S(1)} %dynamic-slice_bitcast_fusion), channel_id=1, source_target_pairs={{0,16},{2,18},{4,20},{6,22},{8,24},{10,26},{12,28},{14,30},{16,0},... | collective-permute-start | bytes 405512 | tf_op jit(solution)/shard_map/ppermute | solution.py:415
  1072.6 21.8 %collective-permute-start.41 = (f32[4,33,128]{2,0,1:T(4,128)S(1)}, f32[4,33,128]{2,0,1:T(4,128)S(1)}, u32[]{:S(2)}, u32[]{:S(2)}) collective-permute-start(f32[4,33,128]{2,0,1:T(4,128)S(1)} %dynamic-slice_bitcast_fusion.1), channel_id=1, source_target_pairs={{0,8},{2,10},{4,12},{6,14},{8,0},{10,2},{12,4},{14,6},{16,24},{18,... | collective-permute-start | bytes 202760 | tf_op jit(solution)/shard_map/ppermute | solution.py:415
  1094.4 8.3 collective-permute-start.42
  1101.9 35.5 %collective-permute-start.37 = (bf16[256,2048]{1,0:T(8,128)(2,1)}, bf16[256,2048]{1,0:T(8,128)(2,1)}, u32[]{:S(2)}, u32[]{:S(2)}) collective-permute-start(bf16[256,2048]{1,0:T(8,128)(2,1)} %add_convert_fusion.11), channel_id=1, source_target_pairs={{0,16},{2,18},{4,20},{6,22},{8,24},{10,26},{12,28},{14,30},{16,0},... | collective-permute-start | bytes 3145736 | tf_op jit(solution)/shard_map/ppermute | solution.py:376
  1104.1 3.8 collective-permute-start.44
  1141.1 10.2 collective-permute-start.46
  1141.2 16.3 %collective-permute-start.39 = (bf16[128,2048]{1,0:T(8,128)(2,1)}, bf16[128,2048]{1,0:T(8,128)(2,1)}, u32[]{:S(2)}, u32[]{:S(2)}) collective-permute-start(bf16[128,2048]{1,0:T(8,128)(2,1)} %reduce-scatter.5.cloned.1.call-done), channel_id=1, source_target_pairs={{0,1},{1,0},{2,3},{3,2},{4,5},{5,4},{6,7},{7,6},{8,9},{9,8},{10,11... | collective-permute-start | bytes 1572872 | tf_op jit(solution)/shard_map/ppermute | solution.py:341
  1144.3 26.9 %collective-permute-start.38 = (bf16[128,3072]{1,0:T(8,128)(2,1)}, bf16[128,3072]{1,0:T(8,128)(2,1)S(1)}, u32[]{:S(2)}, u32[]{:S(2)}) collective-permute-start(bf16[128,3072]{1,0:T(8,128)(2,1)} %reduce-scatter.3.cloned.1.call-done.mine_ref), channel_id=1, source_target_pairs={{0,1},{1,0},{2,3},{3,2},{4,5},{5,4},{6,7},{7,6},{8,9},{9,8},{10,11... | collective-permute-start | bytes 2359304 | tf_op jit(solution)/shard_map/ppermute | solution.py:341
  (81 other events, 1654.2 us)
Sparse Core Ops, SparseCore 0:
  10.4 112.8 all-gather.3
  125.4 134.2 all-gather.7
  261.9 168.0 all-gather.5
  780.4 124.6 reduce-scatter.4
  910.0 158.7 reduce-scatter.2

commit v13 on v12

--- a/solution.py
+++ b/solution.py
@@ -403,20 +403,6 @@
     for step in steps:
         values = values + lax.ppermute(values, "fsdp", [(i, i ^ step) for i in range(fsdp)])
     return values
-
-
-def sum_owned(values, fsdp, spot):
-    items, shard = values.shape[0], values.shape[1] // fsdp
-    values = values.reshape(items, fsdp, shard).swapaxes(0, 1)
-    step = fsdp // 2
-    while step:
-        bit = (spot // step) % 2
-        values = values.reshape(2, step, items, shard)
-        other = lax.ppermute(take(values, 1 - bit), "fsdp", [(i, i ^ step) for i in range(fsdp)])
-        values = take(values, bit) + other
-        step //= 2
-    values = values[0]
-    return values + swap_ctx(values)
 
 
 def turn(values):
@@ -1008,7 +994,9 @@
     side_one, side_two, ctx_one, ctx_two = out_sums
     out_far[0] = swap_ctx(out_far[0])
     grad_attended = mul(grad_branch, out_all, rhs_turned).astype(low)
-    grad_attended, out_far = hold(grad_attended, out_far)
+    (rows, grad_pair), grad_attended = hold((rows, grad_pair), grad_attended)
+    grad_gate_up = mul(rows, grad_pair, lhs_turned)[None]
+    grad_attended, (out_far, grad_gate_up) = hold(grad_attended, (out_far, grad_gate_up))
     got = [
         swap_ctx(ctx_one),
         swap_side(side_two),
@@ -1020,23 +1008,30 @@
         projected, roped_q, roped_k, values_low, grad_attended, cosine, sine, gain_q, gain_k, kv_heads, group
     )
     grad_projected = jnp.concatenate([grad_q, grad_k, grad_v], axis=1)
-    grad_projected, (got[0], got[1]) = hold(grad_projected, (got[0], got[1]))
+    (hidden, grad_rows), grad_projected = hold((hidden, grad_rows), grad_projected)
+    grad_down = mul(hidden, grad_rows, lhs_turned)[None]
+    grad_projected, (got[0], got[1], grad_down) = hold(grad_projected, (got[0], got[1], grad_down))
     grad_qkv_part = mul(low_in, grad_projected, lhs_turned).astype(low)
-    grad_projected, got = hold(grad_projected, got)
     entries = joined(places, out_own, got)
+    grad_projected, entries = hold(grad_projected, entries)
+    one, two = line_first(entries, place)
     grad_normed_part = mul(grad_projected, qkv_all, rhs_turned)
-    (rows, grad_pair, hidden, grad_rows), entries = hold((rows, grad_pair, hidden, grad_rows), entries)
-    one, two = line_first(entries, place)
-    grad_gate_up = mul(rows, grad_pair, lhs_turned)[None]
-    grad_down = mul(hidden, grad_rows, lhs_turned)[None]
     grad_normed = of_block(grad_normed_part, rank) + swap_ctx(
         of_block(grad_normed_part, 1 - rank).astype(low)
     ).astype(full)
     grad_in_part, grad_attn_gain = rms_back(inputs, attn_all, grad_normed)
     grad_tokens = grad_mixed + grad_in_part
 
-    out_mine = lax.psum_scatter(grad_out_part, "fsdp", scatter_dimension=0, tiled=True).astype(full)
-    out_other = swap_ctx(out_mine.astype(low)).astype(full)
+    small_part = jnp.concatenate([grad_router, grad_moe_gain[:, None]], axis=1).astype(low)
+    small_cols = -(-small_part.shape[1] // head_dim) * head_dim
+    small_part = jnp.pad(small_part, ((0, 0), (0, small_cols - small_part.shape[1])))
+    out_mine = lax.psum_scatter(
+        jnp.concatenate([grad_out_part, small_part], axis=1), "fsdp", scatter_dimension=0, tiled=True
+    )
+    out_other = swap_ctx(out_mine).astype(full)
+    out_mine = out_mine.astype(full)
+    early = (out_mine + out_other)[:, width:]
+    out_mine, out_other = out_mine[:, :width], out_other[:, :width]
     grad_out = jnp.where(
         rank == 0,
         jnp.concatenate([out_mine, out_other], axis=0),
@@ -1044,8 +1039,6 @@
     )
     qkv_mine = lax.psum_scatter(grad_qkv_part, "fsdp", scatter_dimension=0, tiled=True)
     grad_qkv = all_heads(rank_at, qkv_mine, swap_ctx(qkv_mine), head_dim, my_heads)
-    early, got = hold(jnp.concatenate([grad_router.T, grad_moe_gain[None]], axis=0), got)
-    early = sum_owned(early, fsdp, spot)
     late = jnp.concatenate(
         [
             grad_attn_gain.reshape(-1, head_dim),
@@ -1054,7 +1047,7 @@
         ],
         axis=0,
     )
-    late, (one, two, grad_gate_up, grad_down) = hold(late, (one, two, grad_gate_up, grad_down))
+    late, (one, two) = hold(late, (one, two))
     far = line_second(entries, two)
     late = late + swap_ctx(late)
     late, far = hold(sum_partners(late, fsdp, (1, 2)), far)
@@ -1066,9 +1059,9 @@
         grad_tokens,
         grad_qkv,
         grad_out,
-        early[:experts_all].T,
+        early[:, :experts_all],
         lax.dynamic_slice_in_dim(late[:gain_rows].reshape(-1), spot * shard, shard, 0),
-        early[experts_all],
+        early[:, experts_all],
         late[gain_rows],
         late[gain_rows + 1],
         grad_gate_up,

time: 1190 us -> 1210 us (1.017)
  other arithmetic: 106 us -> 126 us
  waiting for transfers between devices: 605 us -> 588 us
  starting transfers between devices: 53.6 us -> 69.9 us
    ppermute x2, waiting for transfers between devices: 0.01 us -> 52.1 us  [line_first(): lax.ppermute(item, 'fsdp', [(i, i ^ 4) for i in range(fsdp)])]
    ppermute x8, waiting for transfers between devices: 137 us -> 94.8 us  [swap_side(): return lax.ppermute(values, 'fsdp', side_pairs(lax.axis_size('fsdp')))]
    ppermute x4 -> x0, waiting for transfers between devices: 33.7 us -> none  [sum_owned(): lax.ppermute(take(values, 1 - bit), 'fsdp', [(i, i ^ step) for i in range...]
    ppermute x3, starting transfers between devices: 3.58 us -> 24.7 us  [line_shift(): lax.ppermute(values, 'fsdp', [(i, (i + 4 * step) % fsdp) for i in range(f...]
    ppermute x19 -> x18, starting transfers between devices: 26.8 us -> 25.6 us  [swap_ctx(): return lax.ppermute(values, 'ctx', [(0, 1), (1, 0)])]
    ppermute x19 -> x18, waiting for transfers between devices: 259 us -> 258 us  [swap_ctx(): return lax.ppermute(values, 'ctx', [(0, 1), (1, 0)])]
  transfers between devices with their start and end apart: 53 -> 48, of which waited for: 29 -> 28; matrix products, arithmetic and copies ran while one was open for 19% -> 20% of each run, Pallas kernels for 16% -> 15%
where the time goes in v13:
time: 1210 us; the launch traced here: 1200 us
  waiting for transfers between devices  588 us (49%)
  Pallas kernels  224 us (19%)
  other arithmetic  126 us (10%)
  matrix products  115 us (10%)
  starting transfers between devices  69.9 us (6%)
  blocking collectives  35.6 us (3%)
  local copies, waits for them, and re-layouts  25.6 us (2%)
  between operations  15.4 us (1%)
    ppermute x18, waiting for transfers between devices, swap_ctx(): return lax.ppermute(values, 'ctx', [(0, 1), (1, 0)])  258 us
    pallas_call x4, Pallas kernels, run_expert(): pl.pallas_call(expert_kernel, grid_spec=grid_spec, out_shape=[shape((step...  135 us
    dot_general x11, matrix products, mul(): return lax.dot_general(left, right, dims, preferred_element_type=full)  115 us
    ppermute x8, waiting for transfers between devices, swap_side(): return lax.ppermute(values, 'fsdp', side_pairs(lax.axis_size('fsdp')))  94.8 us
    convert_element_type x20, other arithmetic, add_low(): return (one.astype(full) + two.astype(full)).astype(low)  76.8 us
    all_gather x1, waiting for transfers between devices, body_gathered(): weights_all = lax.all_gather(weights_local, 'fsdp', axis=0, tiled=True)  65.6 us
    ppermute x2, waiting for transfers between devices, line_first(): lax.ppermute(item, 'fsdp', [(i, i ^ 4) for i in range(fsdp)])  52.1 us
    ppermute x3, waiting for transfers between devices, line_shift(): lax.ppermute(values, 'fsdp', [(i, (i + 4 * step) % fsdp) for i in range(f...  45.5 us
  transfers between devices with their start and end apart: 48, of which 28 were waited for; matrix products, arithmetic and copies ran while one was open for 20% of the time, Pallas kernels for 15%

profile of v13, /device:TPU:0, one launch (start us, length us, event | category | flops | bytes accessed | tf_op | source)
XLA Modules:
  0.0 1199.9 jit_solution(6886363884793758970)
XLA Ops:
  13.4 13.3 %collective-permute-done.3 = bf16[256,1152]{1,0:T(8,128)(2,1)S(1)} collective-permute-done((bf16[256,1152]{1,0:T(8,128)(2,1)S(1)}, bf16[256,1152]{1,0:T(8,128)(2,1)S(1)}, u32[]{:S(2)}, u32[]{:S(2)}) %collective-permute-start.3) | collective-permute-done | bytes 589856 | tf_op jit(solution)/shard_map/ppermute | solution.py:341
  31.2 22.9 %all_gather.12 = bf16[2048,34]{0,1:T(8,128)(2,1)S(1)} all-gather(bf16[128,34]{0,1:T(8,128)(2,1)S(1)} %pad_maximum_fusion.22), channel_id=1, replica_groups=mesh['fsdp'=16,'ctx'=2] {'fsdp'}, dimensions={0}, use_global_device_ids=true | all-gather | bytes 147968 | tf_op jit(solution)/shard_map/all_gather | solution.py:830
  57.6 65.6 %all-gather.4.cloned.1.call-done = bf16[2048,5120]{1,0:T(8,128)(2,1)} async-done(((bf16[128,5120]{1,0:T(8,128)(2,1)}), bf16[2048,5120]{1,0:T(8,128)(2,1)}) %all-gather.4.cloned.1.call-update) | async-done | bytes 20971536 | tf_op jit(solution)/shard_map/all_gather | solution.py:831
  123.2 11.5 fusion.3.q_ref.k_ref.v_ref
  134.7 18.2 %attend.1 = (bf16[512,2048]{1,0:T(8,128)(2,1)S(1)}, bf16[512,2048]{1,0:T(8,128)(2,1)S(1)}, bf16[512,512]{1,0:T(8,128)(2,1)S(1)}, bf16[512,512]{1,0:T(8,128)(2,1)S(1)}) custom-call(f32[512,3072]{1,0:T(8,128)} %fusion.3.q_ref.k_ref.v_ref, f32[512,3072]{1,0:T(8,128)} %fusion.3.q_ref.k_ref.v_ref, f32[512,3072]{1,0:T(8,128)} %fusion.3.q_ref.k_ref.v_ref, ...), custom_call_target="tpu_custom_call" | custom-call | flops 2147483648 | bytes 9437184 | tf_op jit(solution)/shard_map/attend/pallas_call | solution.py:516
  153.0 8.4 fusion.8
  163.5 23.8 %collective-permute-done.1 = bf16[256,2048]{1,0:T(8,128)(2,1)S(1)} collective-permute-done((bf16[256,2048]{1,0:T(8,128)(2,1)S(1)}, bf16[256,2048]{1,0:T(8,128)(2,1)S(1)}, u32[]{:S(2)}, u32[]{:S(2)}) %collective-permute-start.1) | collective-permute-done | bytes 1048608 | tf_op jit(solution)/shard_map/ppermute | solution.py:341
  193.2 23.1 %collective-permute-done.2 = bf16[256,2048]{1,0:T(8,128)(2,1)S(1)} collective-permute-done((bf16[256,2048]{1,0:T(8,128)(2,1)S(1)}, bf16[256,2048]{1,0:T(8,128)(2,1)S(1)}, u32[]{:S(2)}, u32[]{:S(2)}) %collective-permute-start.2) | collective-permute-done | bytes 1048608 | tf_op jit(solution)/shard_map/ppermute | solution.py:341
  219.8 12.8 %all_to_all.24 = f32[32,1,256]{2,1,0:T(1,128)S(1)} all-to-all(f32[32,1,256]{2,1,0:T(1,128)S(1)} %copy.56), channel_id=1, replica_groups=mesh['fsdp'=16,'ctx'=2] {'fsdp','ctx'}, dimensions={0} | all-to-all | bytes 65536 | tf_op jit(solution)/shard_map/all_to_all | solution.py:868
  232.6 27.1 %all-gather.8.cloned.1.call-done = bf16[4096,3200]{1,0:T(8,128)(2,1)} async-done(((bf16[256,3200]{1,0:T(8,128)(2,1)}), bf16[4096,3200]{1,0:T(8,128)(2,1)}) %all-gather.8.cloned.1.call-update) | async-done | bytes 26214416 | tf_op jit(solution)/shard_map/all_gather | solution.py:838
  259.7 6.9 slice.412
  269.3 157.8 %collective-permute-done.4.far_ref = bf16[8,2,256,896]{3,2,1,0:T(8,128)(2,1)} collective-permute-done((bf16[8,2,256,896]{3,2,1,0:T(8,128)(2,1)}, bf16[8,2,256,896]{3,2,1,0:T(8,128)(2,1)}, u32[]{:S(2)}, u32[]{:S(2)}) %collective-permute-start.4) | collective-permute-done | bytes 7340064 | tf_op jit(solution)/shard_map/ppermute | solution.py:341
  429.9 33.1 %experts.4 = (bf16[4,256,2048]{2,1,0:T(8,128)(2,1)}, bf16[4,256,2048]{2,1,0:T(8,128)(2,1)}, f32[8,2,2,1,256]{4,3,2,1,0:T(1,128)}, bf16[4096,2048]{1,0:T(8,128)(2...) custom-call(s32[1]{0:T(128)} %bitcast.6.core_ref, s32[16]{0:T(128)} %stack.35.order, ...), custom_call_target="tpu_custom_call" | custom-call | flops 19327352832 | bytes 38273024 | tf_op jit(solution)/shard_map/experts/pallas_call | solution.py:665
  463.4 7.1 collective-permute-done.5
  470.5 4.8 add_convert_fusion.8
  478.5 34.1 %experts.5 = (bf16[4,256,2048]{2,1,0:T(8,128)(2,1)}, bf16[4,256,2048]{2,1,0:T(8,128)(2,1)}, f32[8,2,2,1,256]{4,3,2,1,0:T(1,128)}, bf16[4096,2048]{1,0:T(8,128)(2...) custom-call(s32[1]{0:T(128)} %bitcast.6.core_ref, ...), custom_call_target="tpu_custom_call", output_to_operand_aliasing={{2}: (8, {}), {3}: (9, {}), {4}: (10, {}), {5}: (11, {}), {... | custom-call | flops 19327352832 | bytes 38273024 | tf_op jit(solution)/shard_map/experts/pallas_call | solution.py:665
  512.6 10.8 collective-permute-done.6
  525.9 33.7 %experts.6 = (bf16[4,256,2048]{2,1,0:T(8,128)(2,1)}, bf16[4,256,2048]{2,1,0:T(8,128)(2,1)}, f32[8,2,2,1,256]{4,3,2,1,0:T(1,128)}, bf16[4096,2048]{1,0:T(8,128)(2...) custom-call(s32[1]{0:T(128)} %bitcast.6.core_ref, ...), custom_call_target="tpu_custom_call", output_to_operand_aliasing={{2}: (8, {}), {3}: (9, {}), {4}: (10, {}), {5}: (11, {}), {... | custom-call | flops 19327352832 | bytes 38273024 | tf_op jit(solution)/shard_map/experts/pallas_call | solution.py:665
  573.1 33.7 %experts.7 = (bf16[4,256,2048]{2,1,0:T(8,128)(2,1)}, bf16[4,256,2048]{2,1,0:T(8,128)(2,1)}, f32[8,2,2,1,256]{4,3,2,1,0:T(1,128)}, bf16[4096,2048]{1,0:T(8,128)(2...) custom-call(s32[1]{0:T(128)} %bitcast.6.core_ref, ...), custom_call_target="tpu_custom_call", output_to_operand_aliasing={{2}: (8, {}), {3}: (9, {}), {4}: (10, {}), {5}: (11, {}), {... | custom-call | flops 19327352832 | bytes 38273024 | tf_op jit(solution)/shard_map/experts/pallas_call | solution.py:665
  606.8 10.4 collective-permute-done.10
  617.8 4.7 all-to-all-start.1
  622.6 5.8 add_convert_fusion.7
  652.8 11.9 results.2
  664.6 19.7 %collective-permute-done.20 = bf16[256,2048]{1,0:T(8,128)(2,1)S(1)} collective-permute-done((bf16[256,2048]{1,0:T(8,128)(2,1)}, bf16[256,2048]{1,0:T(8,128)(2,1)S(1)}, u32[]{:S(2)}, u32[]{:S(2)}) %collective-permute-start.20) | collective-permute-done | bytes 1048608 | tf_op jit(solution)/shard_map/ppermute | solution.py:358
  685.8 28.3 %results.3 = (bf16[12,256,2048]{2,1,0:T(8,128)(2,1)}, bf16[12,256,2048]{2,1,0:T(8,128)(2,1)}) custom-call(s32[1]{0:T(128)} %bitcast.6.core_ref, s32[48]{0:T(128)} %stack.44.order, bf16[4096,768]{1,0:T(8,128)(2,1)} %get-tuple-element.208.z_ref, f32[8,2,2,1,256]{4,3,2,1,0:T(1,128)} %reshape.254.w_ref, bf16[768,2048]{1,0:T(8,128)(2,1)} %bitcast.120), custom_call_target="tpu_custom_call" | custom-call | flops 12884901888 | bytes 33030144 | tf_op jit(solution)/shard_map/results/pallas_call | solution.py:696
  719.5 22.1 %collective-permute-start.21 = (bf16[256,2048]{1,0:T(8,128)(2,1)S(1)}, bf16[256,2048]{1,0:T(8,128)(2,1)S(1)}, u32[]{:S(2)}, u32[]{:S(2)}) collective-permute-start(bf16[256,2048]{1,0:T(8,128)(2,1)S(1)} %pad_maximum_fusion.13), channel_id=1, source_target_pairs={{0,8},{2,10},{4,12},{6,14},{8,16},{10,18},{12,20},{14,22},{16,24},... | collective-permute-start | bytes 3145736 | tf_op jit(solution)/shard_map/ppermute | solution.py:358
  741.9 25.8 %collective-permute-done.21 = bf16[256,2048]{1,0:T(8,128)(2,1)S(1)} collective-permute-done((bf16[256,2048]{1,0:T(8,128)(2,1)S(1)}, bf16[256,2048]{1,0:T(8,128)(2,1)S(1)}, u32[]{:S(2)}, u32[]{:S(2)}) %collective-permute-start.21) | collective-permute-done | bytes 1048608 | tf_op jit(solution)/shard_map/ppermute | solution.py:358
  775.9 5.3 add_convert_fusion.2
  782.7 8.0 add_convert_fusion.13
  796.6 5.8 add_convert_fusion.3
  808.4 6.9 convolution_convert_fusion.1
  815.3 7.8 fusion.5
  823.9 10.6 fusion.13.go_ref
  838.4 32.4 %convolution_bitcast_fusion = f32[1,2048,1536]{2,1,0:T(8,128)} fusion(bf16[4096,2048]{1,0:T(8,128)(2,1)} %get-tuple-element.199, bf16[4096,1536]{1,0:T(8,128)(2,1)S(1)} %bitcast.108), kind=kOutput, calls=%fused_computation.8 | convolution fusion | flops 25769803776 | bytes 41943040 | tf_op jit(solution)/shard_map/dot_general | solution.py:321
  870.8 13.4 %collective-permute-done.26 = bf16[4,256,1024]{2,1,0:T(8,128)(2,1)} collective-permute-done((bf16[4,256,1024]{2,1,0:T(8,128)(2,1)}, bf16[4,256,1024]{2,1,0:T(8,128)(2,1)}, u32[]{:S(2)}, u32[]{:S(2)}) %collective-permute-start.26) | collective-permute-done | bytes 2097184 | tf_op jit(solution)/shard_map/ppermute | solution.py:337
  885.5 25.0 %attend_grad.1 = (bf16[512,2048]{1,0:T(8,128)(2,1)S(1)}, bf16[512,512]{1,0:T(8,128)(2,1)S(1)}, bf16[512,512]{1,0:T(8,128)(2,1)S(1)}, f32[4,1,128]{2,1,0:T(1,128)S(1)}, f32[4,1,128]{2,1,0:T(1,128)S(1)}) custom-call(f32[512,3072]{1,0:T(8,128)} %fusion.3.q_ref.k_ref.v_ref, f32[512,3072]{1,0:T(8,128)} %fusion.3.q_ref.k_ref.v_ref, bf16[512,2048]{1,0:T(8,128)(2,1)} %copy-done, ...), custom_call_target="tpu_custom_call" | custom-call | flops 5368709120 | bytes 15728640 | tf_op jit(solution)/shard_map/attend_grad/pallas_call | solution.py:540
  911.0 20.2 %convolution_bitcast_fusion.1 = f32[1,768,2048]{2,1,0:T(8,128)} fusion(bf16[4096,768]{1,0:T(8,128)(2,1)S(1)} %bitcast.114, bf16[4096,2048]{1,0:T(8,128)(2,1)} %get-tuple-element.209), kind=kOutput, calls=%fused_computation.29 | convolution fusion | flops 12884901888 | bytes 29360128 | tf_op jit(solution)/shard_map/dot_general | solution.py:321
  931.2 13.4 %collective-permute-done.28 = bf16[4,256,1024]{2,1,0:T(8,128)(2,1)} collective-permute-done((bf16[4,256,1024]{2,1,0:T(8,128)(2,1)}, bf16[4,256,1024]{2,1,0:T(8,128)(2,1)}, u32[]{:S(2)}, u32[]{:S(2)}) %collective-permute-start.28) | collective-permute-done | bytes 2097184 | tf_op jit(solution)/shard_map/ppermute | solution.py:337
  944.7 10.1 convolution_convert_fusion
  954.8 4.7 add_convert_fusion.1
  965.6 56.4 %collective-permute-done.29 = bf16[4,256,1024]{2,1,0:T(8,128)(2,1)} collective-permute-done((bf16[4,256,1024]{2,1,0:T(8,128)(2,1)}, bf16[4,256,1024]{2,1,0:T(8,128)(2,1)}, u32[]{:S(2)}, u32[]{:S(2)}) %collective-permute-start.29) | collective-permute-done | bytes 2097184 | tf_op jit(solution)/shard_map/ppermute | solution.py:337
  1033.5 10.1 fusion.1
  1051.9 10.7 collective-permute-done.31
  1066.9 26.0 %collective-permute-done.32 = bf16[256,2048]{1,0:T(8,128)(2,1)} collective-permute-done((bf16[256,2048]{1,0:T(8,128)(2,1)}, bf16[256,2048]{1,0:T(8,128)(2,1)}, u32[]{:S(2)}, u32[]{:S(2)}) %collective-permute-start.32) | collective-permute-done | bytes 1048608 | tf_op jit(solution)/shard_map/ppermute | solution.py:372
  1092.8 26.1 %collective-permute-done.33 = bf16[256,2048]{1,0:T(8,128)(2,1)} collective-permute-done((bf16[256,2048]{1,0:T(8,128)(2,1)}, bf16[256,2048]{1,0:T(8,128)(2,1)}, u32[]{:S(2)}, u32[]{:S(2)}) %collective-permute-start.33) | collective-permute-done | bytes 1048608 | tf_op jit(solution)/shard_map/ppermute | solution.py:372
  1130.1 24.5 %collective-permute-done.37 = bf16[256,2048]{1,0:T(8,128)(2,1)} collective-permute-done((bf16[256,2048]{1,0:T(8,128)(2,1)}, bf16[256,2048]{1,0:T(8,128)(2,1)}, u32[]{:S(2)}, u32[]{:S(2)}) %collective-permute-start.37) | collective-permute-done | bytes 1048608 | tf_op jit(solution)/shard_map/ppermute | solution.py:376
  1164.0 6.5 fusion.23
  1180.6 8.3 collective-permute-done.38.other_ref
  (301 shorter events, 174.9 us)
Async XLA Ops:
  7.2 116.1 %all-gather.4.cloned.1.call-start = ((), (), s32[]{:S(2)}) async-start(), calls=%async_computation.4 | async-start | bytes 22282240 | tf_op jit(solution)/shard_map/all_gather | solution.py:831
  10.2 249.5 %all-gather.8.cloned.1.call-start = ((), (), s32[]{:S(2)}) async-start(), calls=%async_computation.6 | async-start | bytes 27852800 | tf_op jit(solution)/shard_map/all_gather | solution.py:838
  10.4 16.3 %collective-permute-start.3 = (bf16[256,1152]{1,0:T(8,128)(2,1)S(1)}, bf16[256,1152]{1,0:T(8,128)(2,1)S(1)}, u32[]{:S(2)}, u32[]{:S(2)}) collective-permute-start(bf16[256,1152]{1,0:T(8,128)(2,1)S(1)} %slice.410), channel_id=1, source_target_pairs={{0,1},{1,0},{2,3},{3,2},{4,5},{5,4},{6,7},{7,6},{8,9},{9,8},{10,11... | collective-permute-start | bytes 1769480 | tf_op jit(solution)/shard_map/ppermute | solution.py:341
  28.1 401.9 %all-gather.6.cloned.1.call-start = ((), (), s32[]{:S(2)}) async-start(), calls=%async_computation.5 | async-start | bytes 35651584 | tf_op jit(solution)/shard_map/all_gather | solution.py:859
  28.1 26.4 %collective-permute-start = (bf16[256,2048]{1,0:T(8,128)(2,1)S(1)}, bf16[256,2048]{1,0:T(8,128)(2,1)}, u32[]{:S(2)}, u32[]{:S(2)}) collective-permute-start(bf16[256,2048]{1,0:T(8,128)(2,1)S(1)} %copy-done.4), channel_id=1, source_target_pairs={{0,1},{1,0},{2,3},{3,2},{4,5},{5,4},{6,7},{7,6},{8,9},{9,8},{10,11... | collective-permute-start | bytes 3145736 | tf_op jit(solution)/shard_map/ppermute | solution.py:341
  162.0 25.4 %collective-permute-start.1 = (bf16[256,2048]{1,0:T(8,128)(2,1)S(1)}, bf16[256,2048]{1,0:T(8,128)(2,1)S(1)}, u32[]{:S(2)}, u32[]{:S(2)}) collective-permute-start(bf16[256,2048]{1,0:T(8,128)(2,1)S(1)} %select_convert_fusion.1), channel_id=1, source_target_pairs={{0,1},{1,0},{2,3},{3,2},{4,5},{5,4},{6,7},{7,6},{8,9},{9,8},{10,11... | collective-permute-start | bytes 3145736 | tf_op jit(solution)/shard_map/ppermute | solution.py:341
  191.6 24.7 %collective-permute-start.2 = (bf16[256,2048]{1,0:T(8,128)(2,1)S(1)}, bf16[256,2048]{1,0:T(8,128)(2,1)S(1)}, u32[]{:S(2)}, u32[]{:S(2)}) collective-permute-start(bf16[256,2048]{1,0:T(8,128)(2,1)S(1)} %multiply_convert_fusion), channel_id=1, source_target_pairs={{0,1},{1,0},{2,3},{3,2},{4,5},{5,4},{6,7},{7,6},{8,9},{9,8},{10,11... | collective-permute-start | bytes 3145736 | tf_op jit(solution)/shard_map/ppermute | solution.py:341
  266.6 160.5 %collective-permute-start.4 = (bf16[8,2,256,896]{3,2,1,0:T(8,128)(2,1)}, bf16[8,2,256,896]{3,2,1,0:T(8,128)(2,1)}, u32[]{:S(2)}, u32[]{:S(2)}) collective-permute-start(bf16[8,2,256,896]{3,2,1,0:T(8,128)(2,1)} %slice.412), channel_id=1, source_target_pairs={{0,1},{1,0},{2,3},{3,2},{4,5},{5,4},{6,7},{7,6},{8,9},{9,8},{10,11... | collective-permute-start | bytes 22020104 | tf_op jit(solution)/shard_map/ppermute | solution.py:341
  463.0 7.4 collective-permute-start.5
  475.3 48.1 %collective-permute-start.6 = (bf16[4,256,1024]{2,1,0:T(8,128)(2,1)}, bf16[4,256,1024]{2,1,0:T(8,128)(2,1)}, u32[]{:S(2)}, u32[]{:S(2)}) collective-permute-start(bf16[4,256,1024]{2,1,0:T(8,128)(2,1)} %get-tuple-element.135), channel_id=1, source_target_pairs={{0,1},{1,0},{2,3},{3,2},{4,5},{5,4},{6,7},{7,6},{8,9},{9,8},{10,11... | collective-permute-start | bytes 6291464 | tf_op jit(solution)/shard_map/ppermute | solution.py:341
  476.8 47.8 %collective-permute-start.7 = (bf16[4,256,1024]{2,1,0:T(8,128)(2,1)}, bf16[4,256,1024]{2,1,0:T(8,128)(2,1)}, u32[]{:S(2)}, u32[]{:S(2)}) collective-permute-start(bf16[4,256,1024]{2,1,0:T(8,128)(2,1)} %get-tuple-element.136), channel_id=1, source_target_pairs={{0,4},{2,6},{4,0},{6,2},{8,12},{10,14},{12,8},{14,10},{16,20},{18,... | collective-permute-start | bytes 6291464 | tf_op jit(solution)/shard_map/ppermute | solution.py:337
  524.6 35.6 %collective-permute-start.8 = (bf16[4,256,2048]{2,1,0:T(8,128)(2,1)}, bf16[4,256,2048]{2,1,0:T(8,128)(2,1)}, u32[]{:S(2)}, u32[]{:S(2)}) collective-permute-start(bf16[4,256,2048]{2,1,0:T(8,128)(2,1)} %get-tuple-element.137), channel_id=1, source_target_pairs={{0,2},{2,0},{4,6},{6,4},{8,10},{10,8},{12,14},{14,12},{16,18},{18,... | collective-permute-start | bytes 12582920 | tf_op jit(solution)/shard_map/ppermute | solution.py:333
  559.6 63.0 %collective-permute-start.14 = (bf16[4,256,2048]{2,1,0:T(8,128)(2,1)}, bf16[4,256,2048]{2,1,0:T(8,128)(2,1)}, u32[]{:S(2)}, u32[]{:S(2)}) collective-permute-start(bf16[4,256,2048]{2,1,0:T(8,128)(2,1)} %get-tuple-element.167), channel_id=1, source_target_pairs={{0,2},{2,0},{4,6},{6,4},{8,10},{10,8},{12,14},{14,12},{16,18},{18,... | collective-permute-start | bytes 12582920 | tf_op jit(solution)/shard_map/ppermute | solution.py:333
  566.4 40.4 %collective-permute-start.12 = (bf16[2,256,1024]{2,1,0:T(8,128)(2,1)S(1)}, bf16[2,256,1024]{2,1,0:T(8,128)(2,1)}, u32[]{:S(2)}, u32[]{:S(2)}) collective-permute-start(bf16[2,256,1024]{2,1,0:T(8,128)(2,1)S(1)} %add_convert_fusion.26), channel_id=1, source_target_pairs={{0,1},{1,0},{2,3},{3,2},{4,5},{5,4},{6,7},{7,6},{8,9},{9,8},{10,11... | collective-permute-start | bytes 3145736 | tf_op jit(solution)/shard_map/ppermute | solution.py:341
  569.6 37.2 %collective-permute-start.11 = (bf16[2,256,1024]{2,1,0:T(8,128)(2,1)}, bf16[2,256,1024]{2,1,0:T(8,128)(2,1)}, u32[]{:S(2)}, u32[]{:S(2)}) collective-permute-start(bf16[2,256,1024]{2,1,0:T(8,128)(2,1)} %add_convert_fusion.27), channel_id=1, source_target_pairs={{0,4},{2,6},{4,0},{6,2},{8,12},{10,14},{12,8},{14,10},{16,20},{18,... | collective-permute-start | bytes 3145736 | tf_op jit(solution)/shard_map/ppermute | solution.py:337
  570.7 46.5 %collective-permute-start.10 = (bf16[2,256,1024]{2,1,0:T(8,128)(2,1)S(1)}, bf16[2,256,1024]{2,1,0:T(8,128)(2,1)}, u32[]{:S(2)}, u32[]{:S(2)}) collective-permute-start(bf16[2,256,1024]{2,1,0:T(8,128)(2,1)S(1)} %get-tuple-element.153), channel_id=1, source_target_pairs={{0,4},{2,6},{4,0},{6,2},{8,12},{10,14},{12,8},{14,10},{16,20},{18,... | collective-permute-start | bytes 3145736 | tf_op jit(solution)/shard_map/ppermute | solution.py:337
  571.6 45.6 %collective-permute-start.9 = (bf16[2,256,1024]{2,1,0:T(8,128)(2,1)S(1)}, bf16[2,256,1024]{2,1,0:T(8,128)(2,1)}, u32[]{:S(2)}, u32[]{:S(2)}) collective-permute-start(bf16[2,256,1024]{2,1,0:T(8,128)(2,1)S(1)} %get-tuple-element.152), channel_id=1, source_target_pairs={{0,1},{1,0},{2,3},{3,2},{4,5},{5,4},{6,7},{7,6},{8,9},{9,8},{10,11... | collective-permute-start | bytes 3145736 | tf_op jit(solution)/shard_map/ppermute | solution.py:341
  617.2 22.2 %collective-permute-start.13 = (bf16[4,256,2048]{2,1,0:T(8,128)(2,1)}, bf16[4,256,2048]{2,1,0:T(8,128)(2,1)}, u32[]{:S(2)}, u32[]{:S(2)}) collective-permute-start(bf16[4,256,2048]{2,1,0:T(8,128)(2,1)} %get-tuple-element.158), channel_id=1, source_target_pairs={{0,2},{2,0},{4,6},{6,4},{8,10},{10,8},{12,14},{14,12},{16,18},{18,... | collective-permute-start | bytes 12582920 | tf_op jit(solution)/shard_map/ppermute | solution.py:333
  617.8 12.1 %all-to-all-start.1 = ((f32[32,1,256]{2,1,0:T(1,128)}), f32[32,1,256]{2,1,0:T(1,128)S(1)}, u32[]{:S(2)}, u32[]{:S(2)}) async-start(f32[32,1,256]{2,1,0:T(1,128)} %bitcast.121), calls=%async_computation.1 | async-start | bytes 65536 | tf_op jit(solution)/shard_map/all_to_all | solution.py:956
  622.5 537.6 %reduce-scatter.5.cloned.1.call-start = ((), (), s32[]{:S(2)}) async-start(), calls=%async_computation.8 | async-start | bytes 9469952 | tf_op jit(solution)/shard_map/reduce_scatter | solution.py:1028
  635.7 48.6 %collective-permute-start.20 = (bf16[256,2048]{1,0:T(8,128)(2,1)}, bf16[256,2048]{1,0:T(8,128)(2,1)S(1)}, u32[]{:S(2)}, u32[]{:S(2)}) collective-permute-start(bf16[256,2048]{1,0:T(8,128)(2,1)} %pad_maximum_fusion.12), channel_id=1, source_target_pairs={{0,16},{2,18},{4,20},{6,22},{8,24},{10,26},{12,28},{14,30},{16,0},... | collective-permute-start | bytes 3145736 | tf_op jit(solution)/shard_map/ppermute | solution.py:358
  637.9 76.2 %collective-permute-start.19 = (bf16[256,2048]{1,0:T(8,128)(2,1)}, bf16[256,2048]{1,0:T(8,128)(2,1)}, u32[]{:S(2)}, u32[]{:S(2)}) collective-permute-start(bf16[256,2048]{1,0:T(8,128)(2,1)} %pad_maximum_fusion.11), channel_id=1, source_target_pairs={{0,24},{2,26},{4,28},{6,30},{8,0},{10,2},{12,4},{14,6},{16,8},{18,... | collective-permute-start | bytes 3145736 | tf_op jit(solution)/shard_map/ppermute | solution.py:358
  646.6 67.5 %collective-permute-start.18 = (bf16[2,256,1024]{2,1,0:T(8,128)(2,1)}, bf16[2,256,1024]{2,1,0:T(8,128)(2,1)}, u32[]{:S(2)}, u32[]{:S(2)}) collective-permute-start(bf16[2,256,1024]{2,1,0:T(8,128)(2,1)} %add_convert_fusion.20), channel_id=1, source_target_pairs={{0,1},{1,0},{2,3},{3,2},{4,5},{5,4},{6,7},{7,6},{8,9},{9,8},{10,11... | collective-permute-start | bytes 3145736 | tf_op jit(solution)/shard_map/ppermute | solution.py:341
  650.7 63.4 %collective-permute-start.17 = (bf16[2,256,1024]{2,1,0:T(8,128)(2,1)}, bf16[2,256,1024]{2,1,0:T(8,128)(2,1)}, u32[]{:S(2)}, u32[]{:S(2)}) collective-permute-start(bf16[2,256,1024]{2,1,0:T(8,128)(2,1)} %add_convert_fusion.21), channel_id=1, source_target_pairs={{0,4},{2,6},{4,0},{6,2},{8,12},{10,14},{12,8},{14,10},{16,20},{18,... | collective-permute-start | bytes 3145736 | tf_op jit(solution)/shard_map/ppermute | solution.py:337
  652.2 62.0 %collective-permute-start.15 = (bf16[2,256,1024]{2,1,0:T(8,128)(2,1)}, bf16[2,256,1024]{2,1,0:T(8,128)(2,1)}, u32[]{:S(2)}, u32[]{:S(2)}) collective-permute-start(bf16[2,256,1024]{2,1,0:T(8,128)(2,1)} %get-tuple-element.168), channel_id=1, source_target_pairs={{0,1},{1,0},{2,3},{3,2},{4,5},{5,4},{6,7},{7,6},{8,9},{9,8},{10,11... | collective-permute-start | bytes 3145736 | tf_op jit(solution)/shard_map/ppermute | solution.py:341
  684.4 29.8 %collective-permute-start.16 = (bf16[2,256,1024]{2,1,0:T(8,128)(2,1)}, bf16[2,256,1024]{2,1,0:T(8,128)(2,1)}, u32[]{:S(2)}, u32[]{:S(2)}) collective-permute-start(bf16[2,256,1024]{2,1,0:T(8,128)(2,1)} %get-tuple-element.169), channel_id=1, source_target_pairs={{0,4},{2,6},{4,0},{6,2},{8,12},{10,14},{12,8},{14,10},{16,20},{18,... | collective-permute-start | bytes 3145736 | tf_op jit(solution)/shard_map/ppermute | solution.py:337
  714.2 67.0 %collective-permute-start.23 = (bf16[12,256,2048]{2,1,0:T(8,128)(2,1)}, bf16[12,256,2048]{2,1,0:T(8,128)(2,1)}, u32[]{:S(2)}, u32[]{:S(2)}) collective-permute-start(bf16[12,256,2048]{2,1,0:T(8,128)(2,1)} %get-tuple-element.191), channel_id=1, source_target_pairs={{0,2},{2,0},{4,6},{6,4},{8,10},{10,8},{12,14},{14,12},{16,18},{18,... | collective-permute-start | bytes 37748744 | tf_op jit(solution)/shard_map/ppermute | solution.py:333
  714.3 61.3 %collective-permute-start.22 = (bf16[4,256,2048]{2,1,0:T(8,128)(2,1)}, bf16[4,256,2048]{2,1,0:T(8,128)(2,1)}, u32[]{:S(2)}, u32[]{:S(2)}) collective-permute-start(bf16[4,256,2048]{2,1,0:T(8,128)(2,1)} %get-tuple-element.189), channel_id=1, source_target_pairs={{0,2},{2,0},{4,6},{6,4},{8,10},{10,8},{12,14},{14,12},{16,18},{18,... | collective-permute-start | bytes 12582920 | tf_op jit(solution)/shard_map/ppermute | solution.py:333
  719.5 48.2 %collective-permute-start.21 = (bf16[256,2048]{1,0:T(8,128)(2,1)S(1)}, bf16[256,2048]{1,0:T(8,128)(2,1)S(1)}, u32[]{:S(2)}, u32[]{:S(2)}) collective-permute-start(bf16[256,2048]{1,0:T(8,128)(2,1)S(1)} %pad_maximum_fusion.13), channel_id=1, source_target_pairs={{0,8},{2,10},{4,12},{6,14},{8,16},{10,18},{12,20},{14,22},{16,24},... | collective-permute-start | bytes 3145736 | tf_op jit(solution)/shard_map/ppermute | solution.py:358
  781.2 24.6 %collective-permute-start.24 = (bf16[256,2048]{1,0:T(8,128)(2,1)S(1)}, bf16[256,2048]{1,0:T(8,128)(2,1)S(1)}, u32[]{:S(2)}, u32[]{:S(2)}) collective-permute-start(bf16[256,2048]{1,0:T(8,128)(2,1)S(1)} %fusion.51), channel_id=1, source_target_pairs={{0,1},{1,0},{2,3},{3,2},{4,5},{5,4},{6,7},{7,6},{8,9},{9,8},{10,11... | collective-permute-start | bytes 3145736 | tf_op jit(solution)/shard_map/ppermute | solution.py:341
  823.2 348.6 %reduce-scatter.3.cloned.1.call-start = ((), (), s32[]{:S(2)}) async-start(), calls=%async_computation.7 | async-start | bytes 13369344 | tf_op jit(solution)/shard_map/reduce_scatter | solution.py:1040
  823.3 60.9 %collective-permute-start.26 = (bf16[4,256,1024]{2,1,0:T(8,128)(2,1)}, bf16[4,256,1024]{2,1,0:T(8,128)(2,1)}, u32[]{:S(2)}, u32[]{:S(2)}) collective-permute-start(bf16[4,256,1024]{2,1,0:T(8,128)(2,1)} %get-tuple-element.295), channel_id=1, source_target_pairs={{0,4},{2,6},{4,0},{6,2},{8,12},{10,14},{12,8},{14,10},{16,20},{18,... | collective-permute-start | bytes 6291464 | tf_op jit(solution)/shard_map/ppermute | solution.py:337
  834.5 49.7 %collective-permute-start.25 = (bf16[4,256,1024]{2,1,0:T(8,128)(2,1)}, bf16[4,256,1024]{2,1,0:T(8,128)(2,1)S(1)}, u32[]{:S(2)}, u32[]{:S(2)}) collective-permute-start(bf16[4,256,1024]{2,1,0:T(8,128)(2,1)} %get-tuple-element.198), channel_id=1, source_target_pairs={{0,1},{1,0},{2,3},{3,2},{4,5},{5,4},{6,7},{7,6},{8,9},{9,8},{10,11... | collective-permute-start | bytes 6291464 | tf_op jit(solution)/shard_map/ppermute | solution.py:341
  835.9 95.3 %collective-permute-start.27 = (bf16[4,256,1024]{2,1,0:T(8,128)(2,1)}, bf16[4,256,1024]{2,1,0:T(8,128)(2,1)}, u32[]{:S(2)}, u32[]{:S(2)}) collective-permute-start(bf16[4,256,1024]{2,1,0:T(8,128)(2,1)} %pad_maximum_fusion.6), channel_id=1, source_target_pairs={{0,1},{1,0},{2,3},{3,2},{4,5},{5,4},{6,7},{7,6},{8,9},{9,8},{10,11... | collective-permute-start | bytes 6291464 | tf_op jit(solution)/shard_map/ppermute | solution.py:341
  836.5 108.1 %collective-permute-start.28 = (bf16[4,256,1024]{2,1,0:T(8,128)(2,1)}, bf16[4,256,1024]{2,1,0:T(8,128)(2,1)}, u32[]{:S(2)}, u32[]{:S(2)}) collective-permute-start(bf16[4,256,1024]{2,1,0:T(8,128)(2,1)} %pad_maximum_fusion.5), channel_id=1, source_target_pairs={{0,4},{2,6},{4,0},{6,2},{8,12},{10,14},{12,8},{14,10},{16,20},{18,... | collective-permute-start | bytes 6291464 | tf_op jit(solution)/shard_map/ppermute | solution.py:337
  959.5 62.4 %collective-permute-start.29 = (bf16[4,256,1024]{2,1,0:T(8,128)(2,1)}, bf16[4,256,1024]{2,1,0:T(8,128)(2,1)}, u32[]{:S(2)}, u32[]{:S(2)}) collective-permute-start(bf16[4,256,1024]{2,1,0:T(8,128)(2,1)} %add_convert_fusion.1), channel_id=1, source_target_pairs={{0,4},{2,6},{4,0},{6,2},{8,12},{10,14},{12,8},{14,10},{16,20},{18,... | collective-permute-start | bytes 6291464 | tf_op jit(solution)/shard_map/ppermute | solution.py:337
  964.0 62.4 %collective-permute-start.30 = (bf16[4,256,1024]{2,1,0:T(8,128)(2,1)}, bf16[4,256,1024]{2,1,0:T(8,128)(2,1)}, u32[]{:S(2)}, u32[]{:S(2)}) collective-permute-start(bf16[4,256,1024]{2,1,0:T(8,128)(2,1)} %add_convert_fusion), channel_id=1, source_target_pairs={{0,1},{1,0},{2,3},{3,2},{4,5},{5,4},{6,7},{7,6},{8,9},{9,8},{10,11... | collective-permute-start | bytes 6291464 | tf_op jit(solution)/shard_map/ppermute | solution.py:341
  1046.9 15.7 %collective-permute-start.31 = (bf16[256,2048]{1,0:T(8,128)(2,1)}, bf16[256,2048]{1,0:T(8,128)(2,1)}, u32[]{:S(2)}, u32[]{:S(2)}) collective-permute-start(bf16[256,2048]{1,0:T(8,128)(2,1)} %select_convert_fusion), channel_id=1, source_target_pairs={{0,1},{1,0},{2,3},{3,2},{4,5},{5,4},{6,7},{7,6},{8,9},{9,8},{10,11... | collective-permute-start | bytes 3145736 | tf_op jit(solution)/shard_map/ppermute | solution.py:341
  1049.8 43.0 %collective-permute-start.32 = (bf16[256,2048]{1,0:T(8,128)(2,1)}, bf16[256,2048]{1,0:T(8,128)(2,1)}, u32[]{:S(2)}, u32[]{:S(2)}) collective-permute-start(bf16[256,2048]{1,0:T(8,128)(2,1)} %get-tuple-element.332), channel_id=1, source_target_pairs={{0,8},{2,10},{4,12},{6,14},{8,0},{10,2},{12,4},{14,6},{16,24},{18,... | collective-permute-start | bytes 3145736 | tf_op jit(solution)/shard_map/ppermute | solution.py:372
  1049.8 69.2 %collective-permute-start.33 = (bf16[256,2048]{1,0:T(8,128)(2,1)}, bf16[256,2048]{1,0:T(8,128)(2,1)}, u32[]{:S(2)}, u32[]{:S(2)}) collective-permute-start(bf16[256,2048]{1,0:T(8,128)(2,1)} %get-tuple-element.331), channel_id=1, source_target_pairs={{0,8},{2,10},{4,12},{6,14},{8,0},{10,2},{12,4},{14,6},{16,24},{18,... | collective-permute-start | bytes 3145736 | tf_op jit(solution)/shard_map/ppermute | solution.py:372
  1121.5 33.1 %collective-permute-start.37 = (bf16[256,2048]{1,0:T(8,128)(2,1)}, bf16[256,2048]{1,0:T(8,128)(2,1)}, u32[]{:S(2)}, u32[]{:S(2)}) collective-permute-start(bf16[256,2048]{1,0:T(8,128)(2,1)} %add_convert_fusion.11), channel_id=1, source_target_pairs={{0,16},{2,18},{4,20},{6,22},{8,24},{10,26},{12,28},{14,30},{16,0},... | collective-permute-start | bytes 3145736 | tf_op jit(solution)/shard_map/ppermute | solution.py:376
  1121.6 3.7 collective-permute-start.34
  1125.3 1.2 collective-permute-start.35
  1126.4 3.7 collective-permute-start.36
  1154.6 3.8 collective-permute-start.40
  1158.5 12.1 %collective-permute-start.41 = (f32[18,128]{1,0:T(8,128)S(1)}, f32[18,128]{1,0:T(8,128)S(1)}, u32[]{:S(2)}, u32[]{:S(2)}) collective-permute-start(f32[18,128]{1,0:T(8,128)S(1)} %add.611), channel_id=1, source_target_pairs={{0,16},{2,18},{4,20},{6,22},{8,24},{10,26},{12,28},{14,30},{16,0},... | collective-permute-start | bytes 27656 | tf_op jit(solution)/shard_map/ppermute | solution.py:404
  1160.1 15.3 %collective-permute-start.39 = (bf16[128,2176]{1,0:T(8,128)(2,1)}, bf16[128,2176]{1,0:T(8,128)(2,1)}, u32[]{:S(2)}, u32[]{:S(2)}) collective-permute-start(bf16[128,2176]{1,0:T(8,128)(2,1)} %reduce-scatter.5.cloned.1.call-done), channel_id=1, source_target_pairs={{0,1},{1,0},{2,3},{3,2},{4,5},{5,4},{6,7},{7,6},{8,9},{9,8},{10,11... | collective-permute-start | bytes 1671176 | tf_op jit(solution)/shard_map/ppermute | solution.py:341
  1171.8 17.1 %collective-permute-start.38 = (bf16[128,3072]{1,0:T(8,128)(2,1)}, bf16[128,3072]{1,0:T(8,128)(2,1)S(1)}, u32[]{:S(2)}, u32[]{:S(2)}) collective-permute-start(bf16[128,3072]{1,0:T(8,128)(2,1)} %reduce-scatter.3.cloned.1.call-done.mine_ref), channel_id=1, source_target_pairs={{0,1},{1,0},{2,3},{3,2},{4,5},{5,4},{6,7},{7,6},{8,9},{9,8},{10,11... | collective-permute-start | bytes 2359304 | tf_op jit(solution)/shard_map/ppermute | solution.py:341
  (59 other events, 1843.6 us)
Sparse Core Ops, SparseCore 0:
  10.4 112.8 all-gather.3
  125.4 134.2 all-gather.7
  261.9 168.0 all-gather.5
  823.3 127.6 reduce-scatter.4
  955.5 159.5 reduce-scatter.2

commit v14 on v13

--- a/solution.py
+++ b/solution.py
@@ -931,12 +931,9 @@
     def rounds(sums, part):
         side_one, side_two, ctx_one, ctx_two = sums
         span = slice(part * cut, (part + 1) * cut)
-        return [
-            swap_ctx(ctx_one),
-            swap_side(side_two),
-            swap_side(add_low(side_one, far_one[span])),
-            swap_ctx(add_low(ctx_two, far_two[span])),
-        ]
+        to_ctx = swap_ctx(jnp.stack([ctx_one, add_low(ctx_two, far_two[span])]))
+        to_side = swap_side(jnp.stack([side_two, add_low(side_one, far_one[span])]))
+        return [to_ctx[0], to_side[0], to_side[1], to_ctx[1]]
 
     keep, send = call(steps_mixed[0], raw=True)
     send, (far_one, far_two) = hold(send, (far_one, far_two))
@@ -968,7 +965,9 @@
     )
     entries.update(joined(parts[1], [item[cut:] for item in back_own], got))
     out_far = over_core(*out_far)
-    out_far = [pick_sum(out_far, 0, lines, 0), swap_side(pick_sum(out_far, 0, lines, 1))]
+    out_far = [pick_sum(out_far, 0, lines, column) for column in range(2)]
+    out_rest, out_far = hold(out_rest, out_far)
+    out_far[1] = swap_side(out_far[1])
     out_rest = over_core(*out_rest)
     for p in parts[1][:-1]:
         arrived[p] = line_shift(entries[p], lines - p)
@@ -990,18 +989,21 @@
         for one, two in zip(mixed_sums(out_rest), mixed_sums(out_rest, 2 * cut + lines))
     ]
     out_own = [pick_sum(out_rest, 2 * cut, 2 * cut + lines, column) for column in range(2)]
-    (out_far[0], out_sums, out_own), grad_branch = hold((out_far[0], out_sums, out_own), grad_branch)
+    (out_far, out_sums, out_own), grad_branch = hold((out_far, out_sums, out_own), grad_branch)
     side_one, side_two, ctx_one, ctx_two = out_sums
-    out_far[0] = swap_ctx(out_far[0])
+    out_far[0], from_side = swap_ctx(out_far[0]), swap_side(side_two)
+    two_ctx = add_low(ctx_two, out_far[1])
     grad_attended = mul(grad_branch, out_all, rhs_turned).astype(low)
     (rows, grad_pair), grad_attended = hold((rows, grad_pair), grad_attended)
     grad_gate_up = mul(rows, grad_pair, lhs_turned)[None]
-    grad_attended, (out_far, grad_gate_up) = hold(grad_attended, (out_far, grad_gate_up))
+    grad_attended, (out_far[0], from_side, grad_gate_up) = hold(
+        grad_attended, (out_far[0], from_side, grad_gate_up)
+    )
     got = [
         swap_ctx(ctx_one),
-        swap_side(side_two),
+        from_side,
         swap_side(add_low(side_one, out_far[0])),
-        swap_ctx(add_low(ctx_two, out_far[1])),
+        swap_ctx(two_ctx),
     ]
     grad_out_part = mul(attended, grad_branch, lhs_turned).astype(low)
     grad_q, grad_k, grad_v, gain_q_part, gain_k_part = attend_grad(
@@ -1010,7 +1012,7 @@
     grad_projected = jnp.concatenate([grad_q, grad_k, grad_v], axis=1)
     (hidden, grad_rows), grad_projected = hold((hidden, grad_rows), grad_projected)
     grad_down = mul(hidden, grad_rows, lhs_turned)[None]
-    grad_projected, (got[0], got[1], grad_down) = hold(grad_projected, (got[0], got[1], grad_down))
+    grad_projected, (got[2], got[3], grad_down) = hold(grad_projected, (got[2], got[3], grad_down))
     grad_qkv_part = mul(low_in, grad_projected, lhs_turned).astype(low)
     entries = joined(places, out_own, got)
     grad_projected, entries = hold(grad_projected, entries)

time: 1210 us -> 1230 us (1.017)
  waiting for transfers between devices: 588 us -> 623 us
  starting transfers between devices: 69.9 us -> 56.2 us
    ppermute x18 -> x16, waiting for transfers between devices: 258 us -> 311 us  [swap_ctx(): return lax.ppermute(values, 'ctx', [(0, 1), (1, 0)])]
    ppermute x8 -> x6, waiting for transfers between devices: 94.8 us -> 66.7 us  [swap_side(): return lax.ppermute(values, 'fsdp', side_pairs(lax.axis_size('fsdp')))]
    convert_element_type x20 -> x16, other arithmetic: 76.8 us -> 56.5 us  [add_low(): return (one.astype(full) + two.astype(full)).astype(low)]
    ppermute x3, waiting for transfers between devices: 45.5 us -> 25.4 us  [line_shift(): lax.ppermute(values, 'fsdp', [(i, (i + 4 * step) % fsdp) for i in range(f...]
    ppermute x1, waiting for transfers between devices: 24.5 us -> 41.1 us  [line_second(): lax.ppermute(add_low(entries[2], two), 'fsdp', [(i, i ^ 8) for i in range...]
    another operation x0 -> x8, other arithmetic: none -> 12.5 us  [the longest x4 6.26 us: rounds(): to_side = swap_side(jnp.stack([side_two, add_low(side_one, far_one[span])]))]
    ppermute x18 -> x16, starting transfers between devices: 25.6 us -> 21.9 us  [swap_ctx(): return lax.ppermute(values, 'ctx', [(0, 1), (1, 0)])]
  transfers between devices with their start and end apart: 48 -> 44, of which waited for: 28 -> 32; matrix products, arithmetic and copies ran while one was open for 20% -> 19% of each run, Pallas kernels for 15% -> 15%
where the time goes in v14:
time: 1230 us; the launch traced here: 1220 us
  waiting for transfers between devices  623 us (51%)
  Pallas kernels  224 us (18%)
  other arithmetic  116 us (9%)
  matrix products  116 us (9%)
  starting transfers between devices  56.2 us (5%)
  local copies, waits for them, and re-layouts  35.7 us (3%)
  blocking collectives  35.7 us (3%)
  between operations  15.4 us (1%)
    ppermute x16, waiting for transfers between devices, swap_ctx(): return lax.ppermute(values, 'ctx', [(0, 1), (1, 0)])  311 us
    pallas_call x4, Pallas kernels, run_expert(): pl.pallas_call(expert_kernel, grid_spec=grid_spec, out_shape=[shape((step...  135 us
    dot_general x11, matrix products, mul(): return lax.dot_general(left, right, dims, preferred_element_type=full)  116 us
    ppermute x6, waiting for transfers between devices, swap_side(): return lax.ppermute(values, 'fsdp', side_pairs(lax.axis_size('fsdp')))  66.7 us
    all_gather x1, waiting for transfers between devices, body_gathered(): weights_all = lax.all_gather(weights_local, 'fsdp', axis=0, tiled=True)  65.6 us
    ppermute x2, waiting for transfers between devices, line_first(): lax.ppermute(item, 'fsdp', [(i, i ^ 4) for i in range(fsdp)])  58.3 us
    convert_element_type x16, other arithmetic, add_low(): return (one.astype(full) + two.astype(full)).astype(low)  56.5 us
    ppermute x1, waiting for transfers between devices, line_second(): lax.ppermute(add_low(entries[2], two), 'fsdp', [(i, i ^ 8) for i in range...  41.1 us
  transfers between devices with their start and end apart: 44, of which 32 were waited for; matrix products, arithmetic and copies ran while one was open for 19% of the time, Pallas kernels for 15%

profile of v14, /device:TPU:0, one launch (start us, length us, event | category | flops | bytes accessed | tf_op | source)
XLA Modules:
  0.0 1221.7 jit_solution(12326467254706004126)
XLA Ops:
  13.4 13.3 %collective-permute-done.3 = bf16[256,1152]{1,0:T(8,128)(2,1)S(1)} collective-permute-done((bf16[256,1152]{1,0:T(8,128)(2,1)S(1)}, bf16[256,1152]{1,0:T(8,128)(2,1)S(1)}, u32[]{:S(2)}, u32[]{:S(2)}) %collective-permute-start.3) | collective-permute-done | bytes 589856 | tf_op jit(solution)/shard_map/ppermute | solution.py:341
  31.2 22.9 %all_gather.12 = bf16[2048,34]{0,1:T(8,128)(2,1)S(1)} all-gather(bf16[128,34]{0,1:T(8,128)(2,1)S(1)} %pad_maximum_fusion.26), channel_id=1, replica_groups=mesh['fsdp'=16,'ctx'=2] {'fsdp'}, dimensions={0}, use_global_device_ids=true | all-gather | bytes 147968 | tf_op jit(solution)/shard_map/all_gather | solution.py:830
  57.6 65.6 %all-gather.4.cloned.1.call-done = bf16[2048,5120]{1,0:T(8,128)(2,1)} async-done(((bf16[128,5120]{1,0:T(8,128)(2,1)}), bf16[2048,5120]{1,0:T(8,128)(2,1)}) %all-gather.4.cloned.1.call-update) | async-done | bytes 20971536 | tf_op jit(solution)/shard_map/all_gather | solution.py:831
  123.2 11.5 fusion.3.q_ref.k_ref.v_ref
  134.7 18.2 %attend.1 = (bf16[512,2048]{1,0:T(8,128)(2,1)S(1)}, bf16[512,2048]{1,0:T(8,128)(2,1)S(1)}, bf16[512,512]{1,0:T(8,128)(2,1)S(1)}, bf16[512,512]{1,0:T(8,128)(2,1)S(1)}) custom-call(f32[512,3072]{1,0:T(8,128)} %fusion.3.q_ref.k_ref.v_ref, f32[512,3072]{1,0:T(8,128)} %fusion.3.q_ref.k_ref.v_ref, f32[512,3072]{1,0:T(8,128)} %fusion.3.q_ref.k_ref.v_ref, ...), custom_call_target="tpu_custom_call" | custom-call | flops 2147483648 | bytes 9437184 | tf_op jit(solution)/shard_map/attend/pallas_call | solution.py:516
  153.0 8.4 fusion.8
  163.5 23.8 %collective-permute-done.1 = bf16[256,2048]{1,0:T(8,128)(2,1)S(1)} collective-permute-done((bf16[256,2048]{1,0:T(8,128)(2,1)S(1)}, bf16[256,2048]{1,0:T(8,128)(2,1)S(1)}, u32[]{:S(2)}, u32[]{:S(2)}) %collective-permute-start.1) | collective-permute-done | bytes 1048608 | tf_op jit(solution)/shard_map/ppermute | solution.py:341
  191.8 23.1 %collective-permute-done.2 = bf16[256,2048]{1,0:T(8,128)(2,1)S(1)} collective-permute-done((bf16[256,2048]{1,0:T(8,128)(2,1)S(1)}, bf16[256,2048]{1,0:T(8,128)(2,1)S(1)}, u32[]{:S(2)}, u32[]{:S(2)}) %collective-permute-start.2) | collective-permute-done | bytes 1048608 | tf_op jit(solution)/shard_map/ppermute | solution.py:341
  218.4 12.8 %all_to_all.24 = f32[32,1,256]{2,1,0:T(1,128)S(1)} all-to-all(f32[32,1,256]{2,1,0:T(1,128)S(1)} %copy.56), channel_id=1, replica_groups=mesh['fsdp'=16,'ctx'=2] {'fsdp','ctx'}, dimensions={0} | all-to-all | bytes 65536 | tf_op jit(solution)/shard_map/all_to_all | solution.py:868
  231.2 28.5 %all-gather.8.cloned.1.call-done = bf16[4096,3200]{1,0:T(8,128)(2,1)} async-done(((bf16[256,3200]{1,0:T(8,128)(2,1)}), bf16[4096,3200]{1,0:T(8,128)(2,1)}) %all-gather.8.cloned.1.call-update) | async-done | bytes 26214416 | tf_op jit(solution)/shard_map/all_gather | solution.py:838
  259.7 6.9 slice.436
  269.4 157.7 %collective-permute-done.4.far_ref = bf16[8,2,256,896]{3,2,1,0:T(8,128)(2,1)} collective-permute-done((bf16[8,2,256,896]{3,2,1,0:T(8,128)(2,1)}, bf16[8,2,256,896]{3,2,1,0:T(8,128)(2,1)}, u32[]{:S(2)}, u32[]{:S(2)}) %collective-permute-start.4) | collective-permute-done | bytes 7340064 | tf_op jit(solution)/shard_map/ppermute | solution.py:341
  429.9 33.0 %experts.4 = (bf16[4,256,2048]{2,1,0:T(8,128)(2,1)}, bf16[4,256,2048]{2,1,0:T(8,128)(2,1)}, f32[8,2,2,1,256]{4,3,2,1,0:T(1,128)}, bf16[4096,2048]{1,0:T(8,128)(2...) custom-call(s32[1]{0:T(128)} %bitcast.6.core_ref, s32[16]{0:T(128)} %stack.59.order, ...), custom_call_target="tpu_custom_call" | custom-call | flops 19327352832 | bytes 38273024 | tf_op jit(solution)/shard_map/experts/pallas_call | solution.py:665
  463.3 7.1 collective-permute-done.5
  470.4 4.8 add_convert_fusion.8
  478.5 34.2 %experts.5 = (bf16[4,256,2048]{2,1,0:T(8,128)(2,1)}, bf16[4,256,2048]{2,1,0:T(8,128)(2,1)}, f32[8,2,2,1,256]{4,3,2,1,0:T(1,128)}, bf16[4096,2048]{1,0:T(8,128)(2...) custom-call(s32[1]{0:T(128)} %bitcast.6.core_ref, ...), custom_call_target="tpu_custom_call", output_to_operand_aliasing={{2}: (8, {}), {3}: (9, {}), {4}: (10, {}), {5}: (11, {}), {... | custom-call | flops 19327352832 | bytes 38273024 | tf_op jit(solution)/shard_map/experts/pallas_call | solution.py:665
  512.7 10.7 collective-permute-done.6
  525.9 33.7 %experts.6 = (bf16[4,256,2048]{2,1,0:T(8,128)(2,1)}, bf16[4,256,2048]{2,1,0:T(8,128)(2,1)}, f32[8,2,2,1,256]{4,3,2,1,0:T(1,128)}, bf16[4096,2048]{1,0:T(8,128)(2...) custom-call(s32[1]{0:T(128)} %bitcast.6.core_ref, ...), custom_call_target="tpu_custom_call", output_to_operand_aliasing={{2}: (8, {}), {3}: (9, {}), {4}: (10, {}), {5}: (11, {}), {... | custom-call | flops 19327352832 | bytes 38273024 | tf_op jit(solution)/shard_map/experts/pallas_call | solution.py:665
  572.8 33.7 %experts.7 = (bf16[4,256,2048]{2,1,0:T(8,128)(2,1)}, bf16[4,256,2048]{2,1,0:T(8,128)(2,1)}, f32[8,2,2,1,256]{4,3,2,1,0:T(1,128)}, bf16[4096,2048]{1,0:T(8,128)(2...) custom-call(s32[1]{0:T(128)} %bitcast.6.core_ref, ...), custom_call_target="tpu_custom_call", output_to_operand_aliasing={{2}: (8, {}), {3}: (9, {}), {4}: (10, {}), {5}: (11, {}), {... | custom-call | flops 19327352832 | bytes 38273024 | tf_op jit(solution)/shard_map/experts/pallas_call | solution.py:665
  606.5 9.1 collective-permute-done.10
  627.6 6.0 add_convert_fusion.7
  656.4 28.3 %results.3 = (bf16[12,256,2048]{2,1,0:T(8,128)(2,1)}, bf16[12,256,2048]{2,1,0:T(8,128)(2,1)}) custom-call(s32[1]{0:T(128)} %bitcast.6.core_ref, s32[48]{0:T(128)} %stack.80.order, bf16[4096,768]{1,0:T(8,128)(2,1)} %get-tuple-element.220.z_ref, f32[8,2,2,1,256]{4,3,2,1,0:T(1,128)} %reshape.254.w_ref, bf16[768,2048]{1,0:T(8,128)(2,1)} %bitcast.145), custom_call_target="tpu_custom_call" | custom-call | flops 12884901888 | bytes 33030144 | tf_op jit(solution)/shard_map/results/pallas_call | solution.py:696
  684.7 11.9 results.2
  701.5 7.1 collective-permute-done.18
  713.7 10.0 collective-permute-start.17
  724.0 25.3 %collective-permute-done.17 = bf16[256,2048]{1,0:T(8,128)(2,1)S(1)} collective-permute-done((bf16[256,2048]{1,0:T(8,128)(2,1)S(1)}, bf16[256,2048]{1,0:T(8,128)(2,1)S(1)}, u32[]{:S(2)}, u32[]{:S(2)}) %collective-permute-start.17) | collective-permute-done | bytes 1048608 | tf_op jit(solution)/shard_map/ppermute | solution.py:358
  759.7 8.0 add_convert_fusion.13
  773.9 5.7 add_convert_fusion.2
  783.2 21.0 %collective-permute-done.20 = bf16[4,256,1024]{2,1,0:T(8,128)(2,1)} collective-permute-done((bf16[4,256,1024]{2,1,0:T(8,128)(2,1)S(1)}, bf16[4,256,1024]{2,1,0:T(8,128)(2,1)}, u32[]{:S(2)}, u32[]{:S(2)}) %collective-permute-start.20) | collective-permute-done | bytes 2097184 | tf_op jit(solution)/shard_map/ppermute | solution.py:337
  804.2 6.8 convolution_convert_fusion.1
  811.0 7.9 fusion.5
  818.9 10.0 fusion.13.go_ref
  836.8 35.7 %convolution_bitcast_fusion = f32[1,2048,1536]{2,1,0:T(8,128)} fusion(bf16[4096,2048]{1,0:T(8,128)(2,1)} %get-tuple-element.209, bf16[4096,1536]{1,0:T(8,128)(2,1)} %get-tuple-element.210), kind=kOutput, calls=%fused_computation.8 | convolution fusion | flops 25769803776 | bytes 41943040 | tf_op jit(solution)/shard_map/dot_general | solution.py:321
  872.5 5.0 collective-permute-done.22
  877.5 12.1 collective-permute-done.23
  890.9 25.2 %attend_grad.1 = (bf16[512,2048]{1,0:T(8,128)(2,1)S(1)}, bf16[512,512]{1,0:T(8,128)(2,1)S(1)}, bf16[512,512]{1,0:T(8,128)(2,1)S(1)}, f32[4,1,128]{2,1,0:T(1,128)S(1)}, f32[4,1,128]{2,1,0:T(1,128)S(1)}) custom-call(f32[512,3072]{1,0:T(8,128)} %fusion.3.q_ref.k_ref.v_ref, f32[512,3072]{1,0:T(8,128)} %fusion.3.q_ref.k_ref.v_ref, bf16[512,2048]{1,0:T(8,128)(2,1)} %copy-done, ...), custom_call_target="tpu_custom_call" | custom-call | flops 5368709120 | bytes 15728640 | tf_op jit(solution)/shard_map/attend_grad/pallas_call | solution.py:540
  922.7 18.9 %convolution_bitcast_fusion.1 = f32[1,768,2048]{2,1,0:T(8,128)} fusion(bf16[4096,768]{1,0:T(8,128)(2,1)S(1)} %bitcast.140, bf16[4096,2048]{1,0:T(8,128)(2,1)} %get-tuple-element.221), kind=kOutput, calls=%fused_computation.29 | convolution fusion | flops 12884901888 | bytes 29360128 | tf_op jit(solution)/shard_map/dot_general | solution.py:321
  941.6 23.3 %collective-permute-done.24 = bf16[4,256,1024]{2,1,0:T(8,128)(2,1)} collective-permute-done((bf16[4,256,1024]{2,1,0:T(8,128)(2,1)S(1)}, bf16[4,256,1024]{2,1,0:T(8,128)(2,1)}, u32[]{:S(2)}, u32[]{:S(2)}) %collective-permute-start.24) | collective-permute-done | bytes 2097184 | tf_op jit(solution)/shard_map/ppermute | solution.py:337
  964.9 10.1 convolution_convert_fusion
  980.0 38.5 %collective-permute-done.26 = bf16[4,256,1024]{2,1,0:T(8,128)(2,1)} collective-permute-done((bf16[4,256,1024]{2,1,0:T(8,128)(2,1)}, bf16[4,256,1024]{2,1,0:T(8,128)(2,1)}, u32[]{:S(2)}, u32[]{:S(2)}) %collective-permute-start.26) | collective-permute-done | bytes 2097184 | tf_op jit(solution)/shard_map/ppermute | solution.py:341
  1025.6 9.8 fusion.1
  1045.3 14.0 %collective-permute-done.27 = bf16[256,2048]{1,0:T(8,128)(2,1)} collective-permute-done((bf16[256,2048]{1,0:T(8,128)(2,1)}, bf16[256,2048]{1,0:T(8,128)(2,1)}, u32[]{:S(2)}, u32[]{:S(2)}) %collective-permute-start.27) | collective-permute-done | bytes 1048608 | tf_op jit(solution)/shard_map/ppermute | solution.py:341
  1063.5 20.2 %collective-permute-done.28 = bf16[256,2048]{1,0:T(8,128)(2,1)} collective-permute-done((bf16[256,2048]{1,0:T(8,128)(2,1)}, bf16[256,2048]{1,0:T(8,128)(2,1)}, u32[]{:S(2)}, u32[]{:S(2)}) %collective-permute-start.28) | collective-permute-done | bytes 1048608 | tf_op jit(solution)/shard_map/ppermute | solution.py:372
  1083.7 38.1 %collective-permute-done.29 = bf16[256,2048]{1,0:T(8,128)(2,1)} collective-permute-done((bf16[256,2048]{1,0:T(8,128)(2,1)}, bf16[256,2048]{1,0:T(8,128)(2,1)}, u32[]{:S(2)}, u32[]{:S(2)}) %collective-permute-start.29) | collective-permute-done | bytes 1048608 | tf_op jit(solution)/shard_map/ppermute | solution.py:372
  1135.4 41.1 %collective-permute-done.33 = bf16[256,2048]{1,0:T(8,128)(2,1)} collective-permute-done((bf16[256,2048]{1,0:T(8,128)(2,1)}, bf16[256,2048]{1,0:T(8,128)(2,1)}, u32[]{:S(2)}, u32[]{:S(2)}) %collective-permute-start.33) | collective-permute-done | bytes 1048608 | tf_op jit(solution)/shard_map/ppermute | solution.py:376
  1181.6 6.5 fusion.23
  1190.1 6.0 collective-permute-done.35
  1201.3 9.4 collective-permute-done.34.other_ref
  (316 shorter events, 185.5 us)
Async XLA Ops:
  7.2 116.1 %all-gather.4.cloned.1.call-start = ((), (), s32[]{:S(2)}) async-start(), calls=%async_computation.4 | async-start | bytes 22282240 | tf_op jit(solution)/shard_map/all_gather | solution.py:831
  10.2 249.5 %all-gather.8.cloned.1.call-start = ((), (), s32[]{:S(2)}) async-start(), calls=%async_computation.6 | async-start | bytes 27852800 | tf_op jit(solution)/shard_map/all_gather | solution.py:838
  10.4 16.3 %collective-permute-start.3 = (bf16[256,1152]{1,0:T(8,128)(2,1)S(1)}, bf16[256,1152]{1,0:T(8,128)(2,1)S(1)}, u32[]{:S(2)}, u32[]{:S(2)}) collective-permute-start(bf16[256,1152]{1,0:T(8,128)(2,1)S(1)} %slice.434), channel_id=1, source_target_pairs={{0,1},{1,0},{2,3},{3,2},{4,5},{5,4},{6,7},{7,6},{8,9},{9,8},{10,11... | collective-permute-start | bytes 1769480 | tf_op jit(solution)/shard_map/ppermute | solution.py:341
  28.1 401.9 %all-gather.6.cloned.1.call-start = ((), (), s32[]{:S(2)}) async-start(), calls=%async_computation.5 | async-start | bytes 35651584 | tf_op jit(solution)/shard_map/all_gather | solution.py:859
  28.1 26.4 %collective-permute-start = (bf16[256,2048]{1,0:T(8,128)(2,1)S(1)}, bf16[256,2048]{1,0:T(8,128)(2,1)}, u32[]{:S(2)}, u32[]{:S(2)}) collective-permute-start(bf16[256,2048]{1,0:T(8,128)(2,1)S(1)} %copy-done.6), channel_id=1, source_target_pairs={{0,1},{1,0},{2,3},{3,2},{4,5},{5,4},{6,7},{7,6},{8,9},{9,8},{10,11... | collective-permute-start | bytes 3145736 | tf_op jit(solution)/shard_map/ppermute | solution.py:341
  54.1 163.1 %copy-start.40 = (bf16[2048,34]{0,1:T(8,128)(2,1)}, bf16[2048,34]{0,1:T(8,128)(2,1)S(1)}, u32[]{:S(2)}) copy-start(bf16[2048,34]{0,1:T(8,128)(2,1)S(1)} %all_gather.12) | copy-start | bytes 417796
  54.5 134.2 %copy-start.47 = (f32[2048,1]{0,1:T(1,128)}, f32[2048,1]{0,1:T(1,128)S(1)}, u32[]{:S(2)}) copy-start(f32[2048,1]{0,1:T(1,128)S(1)} %get-tuple-element.364) | copy-start | bytes 24580
  162.0 25.4 %collective-permute-start.1 = (bf16[256,2048]{1,0:T(8,128)(2,1)S(1)}, bf16[256,2048]{1,0:T(8,128)(2,1)S(1)}, u32[]{:S(2)}, u32[]{:S(2)}) collective-permute-start(bf16[256,2048]{1,0:T(8,128)(2,1)S(1)} %select_convert_fusion.1), channel_id=1, source_target_pairs={{0,1},{1,0},{2,3},{3,2},{4,5},{5,4},{6,7},{7,6},{8,9},{9,8},{10,11... | collective-permute-start | bytes 3145736 | tf_op jit(solution)/shard_map/ppermute | solution.py:341
  190.3 24.7 %collective-permute-start.2 = (bf16[256,2048]{1,0:T(8,128)(2,1)S(1)}, bf16[256,2048]{1,0:T(8,128)(2,1)S(1)}, u32[]{:S(2)}, u32[]{:S(2)}) collective-permute-start(bf16[256,2048]{1,0:T(8,128)(2,1)S(1)} %multiply_convert_fusion), channel_id=1, source_target_pairs={{0,1},{1,0},{2,3},{3,2},{4,5},{5,4},{6,7},{7,6},{8,9},{9,8},{10,11... | collective-permute-start | bytes 3145736 | tf_op jit(solution)/shard_map/ppermute | solution.py:341
  266.6 160.5 %collective-permute-start.4 = (bf16[8,2,256,896]{3,2,1,0:T(8,128)(2,1)}, bf16[8,2,256,896]{3,2,1,0:T(8,128)(2,1)}, u32[]{:S(2)}, u32[]{:S(2)}) collective-permute-start(bf16[8,2,256,896]{3,2,1,0:T(8,128)(2,1)} %slice.436), channel_id=1, source_target_pairs={{0,1},{1,0},{2,3},{3,2},{4,5},{5,4},{6,7},{7,6},{8,9},{9,8},{10,11... | collective-permute-start | bytes 22020104 | tf_op jit(solution)/shard_map/ppermute | solution.py:341
  463.0 7.4 collective-permute-start.5
  475.2 48.1 %collective-permute-start.6 = (bf16[4,256,1024]{2,1,0:T(8,128)(2,1)}, bf16[4,256,1024]{2,1,0:T(8,128)(2,1)}, u32[]{:S(2)}, u32[]{:S(2)}) collective-permute-start(bf16[4,256,1024]{2,1,0:T(8,128)(2,1)} %get-tuple-element.140), channel_id=1, source_target_pairs={{0,1},{1,0},{2,3},{3,2},{4,5},{5,4},{6,7},{7,6},{8,9},{9,8},{10,11... | collective-permute-start | bytes 6291464 | tf_op jit(solution)/shard_map/ppermute | solution.py:341
  476.7 47.8 %collective-permute-start.7 = (bf16[4,256,1024]{2,1,0:T(8,128)(2,1)}, bf16[4,256,1024]{2,1,0:T(8,128)(2,1)}, u32[]{:S(2)}, u32[]{:S(2)}) collective-permute-start(bf16[4,256,1024]{2,1,0:T(8,128)(2,1)} %get-tuple-element.141), channel_id=1, source_target_pairs={{0,4},{2,6},{4,0},{6,2},{8,12},{10,14},{12,8},{14,10},{16,20},{18,... | collective-permute-start | bytes 6291464 | tf_op jit(solution)/shard_map/ppermute | solution.py:337
  524.5 35.6 %collective-permute-start.8 = (bf16[4,256,2048]{2,1,0:T(8,128)(2,1)}, bf16[4,256,2048]{2,1,0:T(8,128)(2,1)}, u32[]{:S(2)}, u32[]{:S(2)}) collective-permute-start(bf16[4,256,2048]{2,1,0:T(8,128)(2,1)} %get-tuple-element.142), channel_id=1, source_target_pairs={{0,2},{2,0},{4,6},{6,4},{8,10},{10,8},{12,14},{14,12},{16,18},{18,... | collective-permute-start | bytes 12582920 | tf_op jit(solution)/shard_map/ppermute | solution.py:333
  559.6 68.0 %collective-permute-start.12 = (bf16[4,256,2048]{2,1,0:T(8,128)(2,1)}, bf16[4,256,2048]{2,1,0:T(8,128)(2,1)}, u32[]{:S(2)}, u32[]{:S(2)}) collective-permute-start(bf16[4,256,2048]{2,1,0:T(8,128)(2,1)} %get-tuple-element.172), channel_id=1, source_target_pairs={{0,2},{2,0},{4,6},{6,4},{8,10},{10,8},{12,14},{14,12},{16,18},{18,... | collective-permute-start | bytes 12582920 | tf_op jit(solution)/shard_map/ppermute | solution.py:333
  567.8 47.8 %collective-permute-start.10 = (bf16[2,2,256,1024]{3,2,1,0:T(8,128)(2,1)}, bf16[2,2,256,1024]{3,2,1,0:T(8,128)(2,1)S(1)}, u32[]{:S(2)}, u32[]{:S(2)}) collective-permute-start(bf16[2,2,256,1024]{3,2,1,0:T(8,128)(2,1)} %pad_maximum_fusion.5), channel_id=1, source_target_pairs={{0,4},{2,6},{4,0},{6,2},{8,12},{10,14},{12,8},{14,10},{16,20},{18,... | collective-permute-start | bytes 6291464 | tf_op jit(solution)/shard_map/ppermute | solution.py:337
  572.3 47.6 %collective-permute-start.9 = (bf16[2,2,256,1024]{3,2,1,0:T(8,128)(2,1)}, bf16[2,2,256,1024]{3,2,1,0:T(8,128)(2,1)}, u32[]{:S(2)}, u32[]{:S(2)}) collective-permute-start(bf16[2,2,256,1024]{3,2,1,0:T(8,128)(2,1)} %pad_maximum_fusion.4), channel_id=1, source_target_pairs={{0,1},{1,0},{2,3},{3,2},{4,5},{5,4},{6,7},{7,6},{8,9},{9,8},{10,11... | collective-permute-start | bytes 6291464 | tf_op jit(solution)/shard_map/ppermute | solution.py:341
  622.9 17.8 %collective-permute-start.11 = (bf16[4,256,2048]{2,1,0:T(8,128)(2,1)}, bf16[4,256,2048]{2,1,0:T(8,128)(2,1)}, u32[]{:S(2)}, u32[]{:S(2)}) collective-permute-start(bf16[4,256,2048]{2,1,0:T(8,128)(2,1)} %get-tuple-element.163), channel_id=1, source_target_pairs={{0,2},{2,0},{4,6},{6,4},{8,10},{10,8},{12,14},{14,12},{16,18},{18,... | collective-permute-start | bytes 12582920 | tf_op jit(solution)/shard_map/ppermute | solution.py:333
  623.6 11.3 all-to-all-start.1
  627.6 552.6 %reduce-scatter.5.cloned.1.call-start = ((), (), s32[]{:S(2)}) async-start(), calls=%async_computation.8 | async-start | bytes 9469952 | tf_op jit(solution)/shard_map/reduce_scatter | solution.py:1030
  639.4 62.0 %collective-permute-start.16 = (bf16[256,2048]{1,0:T(8,128)(2,1)}, bf16[256,2048]{1,0:T(8,128)(2,1)S(1)}, u32[]{:S(2)}, u32[]{:S(2)}) collective-permute-start(bf16[256,2048]{1,0:T(8,128)(2,1)} %pad_maximum_fusion.16), channel_id=1, source_target_pairs={{0,16},{2,18},{4,20},{6,22},{8,24},{10,26},{12,28},{14,30},{16,0},... | collective-permute-start | bytes 3145736 | tf_op jit(solution)/shard_map/ppermute | solution.py:358
  647.4 49.1 %collective-permute-start.14 = (bf16[2,2,256,1024]{3,2,1,0:T(8,128)(2,1)}, bf16[2,2,256,1024]{3,2,1,0:T(8,128)(2,1)}, u32[]{:S(2)}, u32[]{:S(2)}) collective-permute-start(bf16[2,2,256,1024]{3,2,1,0:T(8,128)(2,1)} %pad_maximum_fusion.7), channel_id=1, source_target_pairs={{0,4},{2,6},{4,0},{6,2},{8,12},{10,14},{12,8},{14,10},{16,20},{18,... | collective-permute-start | bytes 6291464 | tf_op jit(solution)/shard_map/ppermute | solution.py:337
  652.0 47.4 %collective-permute-start.13 = (bf16[2,2,256,1024]{3,2,1,0:T(8,128)(2,1)}, bf16[2,2,256,1024]{3,2,1,0:T(8,128)(2,1)}, u32[]{:S(2)}, u32[]{:S(2)}) collective-permute-start(bf16[2,2,256,1024]{3,2,1,0:T(8,128)(2,1)} %pad_maximum_fusion.6), channel_id=1, source_target_pairs={{0,1},{1,0},{2,3},{3,2},{4,5},{5,4},{6,7},{7,6},{8,9},{9,8},{10,11... | collective-permute-start | bytes 6291464 | tf_op jit(solution)/shard_map/ppermute | solution.py:341
  654.6 46.9 %collective-permute-start.15 = (bf16[256,2048]{1,0:T(8,128)(2,1)}, bf16[256,2048]{1,0:T(8,128)(2,1)}, u32[]{:S(2)}, u32[]{:S(2)}) collective-permute-start(bf16[256,2048]{1,0:T(8,128)(2,1)} %pad_maximum_fusion.15), channel_id=1, source_target_pairs={{0,24},{2,26},{4,28},{6,30},{8,0},{10,2},{12,4},{14,6},{16,8},{18,... | collective-permute-start | bytes 3145736 | tf_op jit(solution)/shard_map/ppermute | solution.py:358
  701.5 7.2 collective-permute-start.18
  712.1 46.1 %collective-permute-start.19 = (bf16[12,256,2048]{2,1,0:T(8,128)(2,1)}, bf16[12,256,2048]{2,1,0:T(8,128)(2,1)}, u32[]{:S(2)}, u32[]{:S(2)}) collective-permute-start(bf16[12,256,2048]{2,1,0:T(8,128)(2,1)} %get-tuple-element.199), channel_id=1, source_target_pairs={{0,2},{2,0},{4,6},{6,4},{8,10},{10,8},{12,14},{14,12},{16,18},{18,... | collective-permute-start | bytes 37748744 | tf_op jit(solution)/shard_map/ppermute | solution.py:333
  713.7 35.7 %collective-permute-start.17 = (bf16[256,2048]{1,0:T(8,128)(2,1)S(1)}, bf16[256,2048]{1,0:T(8,128)(2,1)S(1)}, u32[]{:S(2)}, u32[]{:S(2)}) collective-permute-start(bf16[256,2048]{1,0:T(8,128)(2,1)S(1)} %pad_maximum_fusion.17), channel_id=1, source_target_pairs={{0,8},{2,10},{4,12},{6,14},{8,16},{10,18},{12,20},{14,22},{16,24},... | collective-permute-start | bytes 3145736 | tf_op jit(solution)/shard_map/ppermute | solution.py:358
  756.7 47.5 %collective-permute-start.20 = (bf16[4,256,1024]{2,1,0:T(8,128)(2,1)S(1)}, bf16[4,256,1024]{2,1,0:T(8,128)(2,1)}, u32[]{:S(2)}, u32[]{:S(2)}) collective-permute-start(bf16[4,256,1024]{2,1,0:T(8,128)(2,1)S(1)} %copy-done.38), channel_id=1, source_target_pairs={{0,4},{2,6},{4,0},{6,2},{8,12},{10,14},{12,8},{14,10},{16,20},{18,... | collective-permute-start | bytes 6291464 | tf_op jit(solution)/shard_map/ppermute | solution.py:337
  758.2 24.6 %collective-permute-start.21 = (bf16[256,2048]{1,0:T(8,128)(2,1)S(1)}, bf16[256,2048]{1,0:T(8,128)(2,1)S(1)}, u32[]{:S(2)}, u32[]{:S(2)}) collective-permute-start(bf16[256,2048]{1,0:T(8,128)(2,1)S(1)} %fusion.55), channel_id=1, source_target_pairs={{0,1},{1,0},{2,3},{3,2},{4,5},{5,4},{6,7},{7,6},{8,9},{9,8},{10,11... | collective-permute-start | bytes 3145736 | tf_op jit(solution)/shard_map/ppermute | solution.py:341
  818.8 370.5 %reduce-scatter.3.cloned.1.call-start = ((), (), s32[]{:S(2)}) async-start(), calls=%async_computation.7 | async-start | bytes 13369344 | tf_op jit(solution)/shard_map/reduce_scatter | solution.py:1042
  828.9 48.6 %collective-permute-start.22 = (bf16[4,256,1024]{2,1,0:T(8,128)(2,1)S(1)}, bf16[4,256,1024]{2,1,0:T(8,128)(2,1)S(1)}, u32[]{:S(2)}, u32[]{:S(2)}) collective-permute-start(bf16[4,256,1024]{2,1,0:T(8,128)(2,1)S(1)} %copy-done.37), channel_id=1, source_target_pairs={{0,1},{1,0},{2,3},{3,2},{4,5},{5,4},{6,7},{7,6},{8,9},{9,8},{10,11... | collective-permute-start | bytes 6291464 | tf_op jit(solution)/shard_map/ppermute | solution.py:341
  830.4 59.2 %collective-permute-start.23 = (bf16[4,256,1024]{2,1,0:T(8,128)(2,1)S(1)}, bf16[4,256,1024]{2,1,0:T(8,128)(2,1)S(1)}, u32[]{:S(2)}, u32[]{:S(2)}) collective-permute-start(bf16[4,256,1024]{2,1,0:T(8,128)(2,1)S(1)} %copy-done.31), channel_id=1, source_target_pairs={{0,4},{2,6},{4,0},{6,2},{8,12},{10,14},{12,8},{14,10},{16,20},{18,... | collective-permute-start | bytes 6291464 | tf_op jit(solution)/shard_map/ppermute | solution.py:337
  831.9 90.8 %slice-start = ((s8[6291456]{0:T(1024)(128)(4,1)}), s8[4194304]{0:T(1024)(128)(4,1)S(1)}, s32[]{:S(2)}) async-start(s8[6291456]{0:T(1024)(128)(4,1)} %bitcast.139), calls=%async_computation.9 | async-start | bytes 8388608
  836.3 105.3 %collective-permute-start.25 = (bf16[4,256,1024]{2,1,0:T(8,128)(2,1)}, bf16[4,256,1024]{2,1,0:T(8,128)(2,1)}, u32[]{:S(2)}, u32[]{:S(2)}) collective-permute-start(bf16[4,256,1024]{2,1,0:T(8,128)(2,1)} %add_convert_fusion), channel_id=1, source_target_pairs={{0,1},{1,0},{2,3},{3,2},{4,5},{5,4},{6,7},{7,6},{8,9},{9,8},{10,11... | collective-permute-start | bytes 6291464 | tf_op jit(solution)/shard_map/ppermute | solution.py:341
  920.5 44.4 %collective-permute-start.24 = (bf16[4,256,1024]{2,1,0:T(8,128)(2,1)S(1)}, bf16[4,256,1024]{2,1,0:T(8,128)(2,1)}, u32[]{:S(2)}, u32[]{:S(2)}) collective-permute-start(bf16[4,256,1024]{2,1,0:T(8,128)(2,1)S(1)} %add_convert_fusion.1), channel_id=1, source_target_pairs={{0,4},{2,6},{4,0},{6,2},{8,12},{10,14},{12,8},{14,10},{16,20},{18,... | collective-permute-start | bytes 6291464 | tf_op jit(solution)/shard_map/ppermute | solution.py:337
  975.0 43.5 %collective-permute-start.26 = (bf16[4,256,1024]{2,1,0:T(8,128)(2,1)}, bf16[4,256,1024]{2,1,0:T(8,128)(2,1)}, u32[]{:S(2)}, u32[]{:S(2)}) collective-permute-start(bf16[4,256,1024]{2,1,0:T(8,128)(2,1)} %pad_maximum_fusion.10), channel_id=1, source_target_pairs={{0,1},{1,0},{2,3},{3,2},{4,5},{5,4},{6,7},{7,6},{8,9},{9,8},{10,11... | collective-permute-start | bytes 6291464 | tf_op jit(solution)/shard_map/ppermute | solution.py:341
  1038.7 20.6 %collective-permute-start.27 = (bf16[256,2048]{1,0:T(8,128)(2,1)}, bf16[256,2048]{1,0:T(8,128)(2,1)}, u32[]{:S(2)}, u32[]{:S(2)}) collective-permute-start(bf16[256,2048]{1,0:T(8,128)(2,1)} %select_convert_fusion), channel_id=1, source_target_pairs={{0,1},{1,0},{2,3},{3,2},{4,5},{5,4},{6,7},{7,6},{8,9},{9,8},{10,11... | collective-permute-start | bytes 3145736 | tf_op jit(solution)/shard_map/ppermute | solution.py:341
  1041.5 42.2 %collective-permute-start.28 = (bf16[256,2048]{1,0:T(8,128)(2,1)}, bf16[256,2048]{1,0:T(8,128)(2,1)}, u32[]{:S(2)}, u32[]{:S(2)}) collective-permute-start(bf16[256,2048]{1,0:T(8,128)(2,1)} %get-tuple-element.342), channel_id=1, source_target_pairs={{0,8},{2,10},{4,12},{6,14},{8,0},{10,2},{12,4},{14,6},{16,24},{18,... | collective-permute-start | bytes 3145736 | tf_op jit(solution)/shard_map/ppermute | solution.py:372
  1045.2 76.6 %collective-permute-start.29 = (bf16[256,2048]{1,0:T(8,128)(2,1)}, bf16[256,2048]{1,0:T(8,128)(2,1)}, u32[]{:S(2)}, u32[]{:S(2)}) collective-permute-start(bf16[256,2048]{1,0:T(8,128)(2,1)} %get-tuple-element.341), channel_id=1, source_target_pairs={{0,8},{2,10},{4,12},{6,14},{8,0},{10,2},{12,4},{14,6},{16,24},{18,... | collective-permute-start | bytes 3145736 | tf_op jit(solution)/shard_map/ppermute | solution.py:372
  1063.5 118.1 %copy-start.5 = (f32[256,2048]{1,0:T(8,128)S(1)}, f32[256,2048]{1,0:T(8,128)}, u32[]{:S(2)}) copy-start(f32[256,2048]{1,0:T(8,128)} %copy-done.3) | copy-start | bytes 6291460
  1124.4 52.0 %collective-permute-start.33 = (bf16[256,2048]{1,0:T(8,128)(2,1)}, bf16[256,2048]{1,0:T(8,128)(2,1)}, u32[]{:S(2)}, u32[]{:S(2)}) collective-permute-start(bf16[256,2048]{1,0:T(8,128)(2,1)} %add_convert_fusion.11), channel_id=1, source_target_pairs={{0,16},{2,18},{4,20},{6,22},{8,24},{10,26},{12,28},{14,30},{16,0},... | collective-permute-start | bytes 3145736 | tf_op jit(solution)/shard_map/ppermute | solution.py:376
  1126.8 3.7 collective-permute-start.30
  1130.5 1.2 collective-permute-start.31
  1131.7 3.7 collective-permute-start.32
  1176.4 3.7 collective-permute-start.36
  1180.1 8.0 collective-permute-start.37
  1180.2 15.9 %collective-permute-start.35 = (bf16[128,2176]{1,0:T(8,128)(2,1)}, bf16[128,2176]{1,0:T(8,128)(2,1)}, u32[]{:S(2)}, u32[]{:S(2)}) collective-permute-start(bf16[128,2176]{1,0:T(8,128)(2,1)} %reduce-scatter.5.cloned.1.call-done), channel_id=1, source_target_pairs={{0,1},{1,0},{2,3},{3,2},{4,5},{5,4},{6,7},{7,6},{8,9},{9,8},{10,11... | collective-permute-start | bytes 1671176 | tf_op jit(solution)/shard_map/ppermute | solution.py:341
  1189.4 21.3 %collective-permute-start.34 = (bf16[128,3072]{1,0:T(8,128)(2,1)}, bf16[128,3072]{1,0:T(8,128)(2,1)S(1)}, u32[]{:S(2)}, u32[]{:S(2)}) collective-permute-start(bf16[128,3072]{1,0:T(8,128)(2,1)} %reduce-scatter.3.cloned.1.call-done.mine_ref), channel_id=1, source_target_pairs={{0,1},{1,0},{2,3},{3,2},{4,5},{5,4},{6,7},{7,6},{8,9},{9,8},{10,11... | collective-permute-start | bytes 2359304 | tf_op jit(solution)/shard_map/ppermute | solution.py:341
  (63 other events, 1462.1 us)
Sparse Core Ops, SparseCore 0:
  10.4 112.8 all-gather.3
  125.4 134.2 all-gather.7
  261.9 168.0 all-gather.5
  818.9 112.8 reduce-scatter.4
  975.1 159.8 reduce-scatter.2

commit v15 on v12

--- a/solution.py
+++ b/solution.py
@@ -405,18 +405,12 @@
     return values
 
 
-def sum_owned(values, fsdp, spot):
-    items, shard = values.shape[0], values.shape[1] // fsdp
-    values = values.reshape(items, fsdp, shard).swapaxes(0, 1)
-    step = fsdp // 2
-    while step:
-        bit = (spot // step) % 2
-        values = values.reshape(2, step, items, shard)
-        other = lax.ppermute(take(values, 1 - bit), "fsdp", [(i, i ^ step) for i in range(fsdp)])
+def halve_line(values, fsdp, place):
+    for step, bit in ((2, place // 2), (1, place % 2)):
+        values = values.reshape(2, step, *values.shape[1:])
+        other = lax.ppermute(take(values, 1 - bit), "fsdp", [(i, i ^ (4 * step)) for i in range(fsdp)])
         values = take(values, bit) + other
-        step //= 2
-    values = values[0]
-    return values + swap_ctx(values)
+    return values[0]
 
 
 def turn(values):
@@ -945,6 +939,10 @@
     def rounds(sums, part):
         side_one, side_two, ctx_one, ctx_two = sums
         span = slice(part * cut, (part + 1) * cut)
+        if part == 1:
+            to_ctx = swap_ctx(jnp.stack([ctx_one, add_low(ctx_two, far_two[span])]))
+            to_side = swap_side(jnp.stack([side_two, add_low(side_one, far_one[span])]))
+            return [to_ctx[0], to_side[0], to_side[1], to_ctx[1]]
         return [
             swap_ctx(ctx_one),
             swap_side(side_two),
@@ -1024,9 +1022,11 @@
     grad_qkv_part = mul(low_in, grad_projected, lhs_turned).astype(low)
     grad_projected, got = hold(grad_projected, got)
     entries = joined(places, out_own, got)
+    (rows, grad_pair, hidden, grad_rows, grad_projected), entries = hold(
+        (rows, grad_pair, hidden, grad_rows, grad_projected), entries
+    )
+    one, two = line_first(entries, place)
     grad_normed_part = mul(grad_projected, qkv_all, rhs_turned)
-    (rows, grad_pair, hidden, grad_rows), entries = hold((rows, grad_pair, hidden, grad_rows), entries)
-    one, two = line_first(entries, place)
     grad_gate_up = mul(rows, grad_pair, lhs_turned)[None]
     grad_down = mul(hidden, grad_rows, lhs_turned)[None]
     grad_normed = of_block(grad_normed_part, rank) + swap_ctx(
@@ -1044,8 +1044,6 @@
     )
     qkv_mine = lax.psum_scatter(grad_qkv_part, "fsdp", scatter_dimension=0, tiled=True)
     grad_qkv = all_heads(rank_at, qkv_mine, swap_ctx(qkv_mine), head_dim, my_heads)
-    early, got = hold(jnp.concatenate([grad_router.T, grad_moe_gain[None]], axis=0), got)
-    early = sum_owned(early, fsdp, spot)
     late = jnp.concatenate(
         [
             grad_attn_gain.reshape(-1, head_dim),
@@ -1057,7 +1055,14 @@
     late, (one, two, grad_gate_up, grad_down) = hold(late, (one, two, grad_gate_up, grad_down))
     far = line_second(entries, two)
     late = late + swap_ctx(late)
-    late, far = hold(sum_partners(late, fsdp, (1, 2)), far)
+    early = jnp.concatenate([grad_router.T, grad_moe_gain[None]], axis=0)
+    early, late = hold(early, late)
+    early = early.reshape(-1, lines, 2, 2, shard).transpose(3, 2, 1, 0, 4)
+    early = take(early, core) + swap_core(take(early, 1 - core))
+    early = take(early, side) + swap_side(take(early, 1 - side))
+    early = early + swap_ctx(early)
+    (late, early), far = hold((sum_partners(late, fsdp, (1, 2)), early), far)
+    early = halve_line(early, fsdp, place)
     output = (mixed + entries[0].astype(full) + one.astype(full) + far.astype(full)).astype(low)
     late = sum_partners(late, fsdp, (4, 8))
     gain_rows = width // head_dim

time: 1190 us -> 1180 us (level)
  waiting for transfers between devices: 605 us -> 577 us
    ppermute x19 -> x18, waiting for transfers between devices: 259 us -> 307 us  [swap_ctx(): return lax.ppermute(values, 'ctx', [(0, 1), (1, 0)])]
    ppermute x4 -> x2, waiting for transfers between devices: 33.7 us -> 0.01 us  [halve_line(): lax.ppermute(take(values, 1 - bit), 'fsdp', [(i, i ^ 4 * step) for i in r...]
    ppermute x8, waiting for transfers between devices: 137 us -> 105 us  [swap_side(): return lax.ppermute(values, 'fsdp', side_pairs(lax.axis_size('fsdp')))]
    ppermute x3, waiting for transfers between devices: 39.8 us -> 25.4 us  [line_shift(): lax.ppermute(values, 'fsdp', [(i, (i + 4 * step) % fsdp) for i in range(f...]
    convert_element_type x20 -> x18, other arithmetic: 66.2 us -> 61.4 us  [add_low(): return (one.astype(full) + two.astype(full)).astype(low)]
    ppermute x19 -> x18, starting transfers between devices: 26.8 us -> 24.6 us  [swap_ctx(): return lax.ppermute(values, 'ctx', [(0, 1), (1, 0)])]
  transfers between devices with their start and end apart: 53 -> 51, of which waited for: 29 -> 30; matrix products, arithmetic and copies ran while one was open for 19% -> 20% of each run, Pallas kernels for 16% -> 16%
where the time goes in v15:
time: 1180 us; the launch traced here: 1170 us
  waiting for transfers between devices  577 us (49%)
  Pallas kernels  225 us (19%)
  matrix products  114 us (10%)
  other arithmetic  109 us (9%)
  starting transfers between devices  61.5 us (5%)
  blocking collectives  35.6 us (3%)
  local copies, waits for them, and re-layouts  34.9 us (3%)
  between operations  15.4 us (1%)
    ppermute x18, waiting for transfers between devices, swap_ctx(): return lax.ppermute(values, 'ctx', [(0, 1), (1, 0)])  307 us
    pallas_call x4, Pallas kernels, run_expert(): pl.pallas_call(expert_kernel, grid_spec=grid_spec, out_shape=[shape((step...  135 us
    dot_general x11, matrix products, mul(): return lax.dot_general(left, right, dims, preferred_element_type=full)  114 us
    ppermute x8, waiting for transfers between devices, swap_side(): return lax.ppermute(values, 'fsdp', side_pairs(lax.axis_size('fsdp')))  105 us
    all_gather x1, waiting for transfers between devices, body_gathered(): weights_all = lax.all_gather(weights_local, 'fsdp', axis=0, tiled=True)  65.6 us
    convert_element_type x18, other arithmetic, add_low(): return (one.astype(full) + two.astype(full)).astype(low)  61.4 us
    pallas_call x2, Pallas kernels, run_result(): pl.pallas_call(result_kernel, grid_spec=pltpu.PrefetchScalarGridSpec(num_...  40.4 us
    all_gather x1, waiting for transfers between devices, body_gathered(): lax.all_gather(jnp.concatenate([cotangent, swap_ctx(cotangent[:, late_col...  28.6 us
  transfers between devices with their start and end apart: 51, of which 30 were waited for; matrix products, arithmetic and copies ran while one was open for 20% of the time, Pallas kernels for 16%

profile of v15, /device:TPU:0, one launch (start us, length us, event | category | flops | bytes accessed | tf_op | source)
XLA Modules:
  0.0 1172.6 jit_solution(1146045142489104118)
XLA Ops:
  13.4 13.3 %collective-permute-done.3 = bf16[256,1152]{1,0:T(8,128)(2,1)S(1)} collective-permute-done((bf16[256,1152]{1,0:T(8,128)(2,1)S(1)}, bf16[256,1152]{1,0:T(8,128)(2,1)S(1)}, u32[]{:S(2)}, u32[]{:S(2)}) %collective-permute-start.3) | collective-permute-done | bytes 589856 | tf_op jit(solution)/shard_map/ppermute | solution.py:341
  31.2 22.9 %all_gather.12 = bf16[2048,34]{0,1:T(8,128)(2,1)S(1)} all-gather(bf16[128,34]{0,1:T(8,128)(2,1)S(1)} %pad_maximum_fusion.24), channel_id=1, replica_groups=mesh['fsdp'=16,'ctx'=2] {'fsdp'}, dimensions={0}, use_global_device_ids=true | all-gather | bytes 147968 | tf_op jit(solution)/shard_map/all_gather | solution.py:838
  57.6 65.6 %all-gather.4.cloned.1.call-done = bf16[2048,5120]{1,0:T(8,128)(2,1)} async-done(((bf16[128,5120]{1,0:T(8,128)(2,1)}), bf16[2048,5120]{1,0:T(8,128)(2,1)}) %all-gather.4.cloned.1.call-update) | async-done | bytes 20971536 | tf_op jit(solution)/shard_map/all_gather | solution.py:839
  123.2 11.5 fusion.2.q_ref.k_ref.v_ref
  134.7 18.2 %attend.1 = (bf16[512,2048]{1,0:T(8,128)(2,1)S(1)}, bf16[512,2048]{1,0:T(8,128)(2,1)S(1)}, bf16[512,512]{1,0:T(8,128)(2,1)S(1)}, bf16[512,512]{1,0:T(8,128)(2,1)S(1)}) custom-call(f32[512,3072]{1,0:T(8,128)} %fusion.2.q_ref.k_ref.v_ref, f32[512,3072]{1,0:T(8,128)} %fusion.2.q_ref.k_ref.v_ref, f32[512,3072]{1,0:T(8,128)} %fusion.2.q_ref.k_ref.v_ref, ...), custom_call_target="tpu_custom_call" | custom-call | flops 2147483648 | bytes 9437184 | tf_op jit(solution)/shard_map/attend/pallas_call | solution.py:524
  153.0 8.4 fusion.6
  163.5 23.8 %collective-permute-done.1 = bf16[256,2048]{1,0:T(8,128)(2,1)S(1)} collective-permute-done((bf16[256,2048]{1,0:T(8,128)(2,1)S(1)}, bf16[256,2048]{1,0:T(8,128)(2,1)S(1)}, u32[]{:S(2)}, u32[]{:S(2)}) %collective-permute-start.1) | collective-permute-done | bytes 1048608 | tf_op jit(solution)/shard_map/ppermute | solution.py:341
  191.7 23.1 %collective-permute-done.2 = bf16[256,2048]{1,0:T(8,128)(2,1)S(1)} collective-permute-done((bf16[256,2048]{1,0:T(8,128)(2,1)S(1)}, bf16[256,2048]{1,0:T(8,128)(2,1)S(1)}, u32[]{:S(2)}, u32[]{:S(2)}) %collective-permute-start.2) | collective-permute-done | bytes 1048608 | tf_op jit(solution)/shard_map/ppermute | solution.py:341
  218.4 12.7 %all_to_all.24 = f32[32,1,256]{2,1,0:T(1,128)S(1)} all-to-all(f32[32,1,256]{2,1,0:T(1,128)S(1)} %copy.55), channel_id=1, replica_groups=mesh['fsdp'=16,'ctx'=2] {'fsdp','ctx'}, dimensions={0} | all-to-all | bytes 65536 | tf_op jit(solution)/shard_map/all_to_all | solution.py:876
  231.1 28.6 %all-gather.8.cloned.1.call-done = bf16[4096,3200]{1,0:T(8,128)(2,1)} async-done(((bf16[256,3200]{1,0:T(8,128)(2,1)}), bf16[4096,3200]{1,0:T(8,128)(2,1)}) %all-gather.8.cloned.1.call-update) | async-done | bytes 26214416 | tf_op jit(solution)/shard_map/all_gather | solution.py:846
  259.7 6.9 slice.419
  269.4 157.7 %collective-permute-done.4.far_ref = bf16[8,2,256,896]{3,2,1,0:T(8,128)(2,1)} collective-permute-done((bf16[8,2,256,896]{3,2,1,0:T(8,128)(2,1)}, bf16[8,2,256,896]{3,2,1,0:T(8,128)(2,1)}, u32[]{:S(2)}, u32[]{:S(2)}) %collective-permute-start.4) | collective-permute-done | bytes 7340064 | tf_op jit(solution)/shard_map/ppermute | solution.py:341
  429.9 33.1 %experts.4 = (bf16[4,256,2048]{2,1,0:T(8,128)(2,1)}, bf16[4,256,2048]{2,1,0:T(8,128)(2,1)}, f32[8,2,2,1,256]{4,3,2,1,0:T(1,128)}, bf16[4096,2048]{1,0:T(8,128)(2...) custom-call(s32[1]{0:T(128)} %bitcast.6.core_ref, s32[16]{0:T(128)} %stack.47.order, ...), custom_call_target="tpu_custom_call" | custom-call | flops 19327352832 | bytes 38273024 | tf_op jit(solution)/shard_map/experts/pallas_call | solution.py:673
  463.3 7.1 collective-permute-done.5
  470.5 4.8 add_convert_fusion.8
  478.5 34.0 %experts.5 = (bf16[4,256,2048]{2,1,0:T(8,128)(2,1)}, bf16[4,256,2048]{2,1,0:T(8,128)(2,1)}, f32[8,2,2,1,256]{4,3,2,1,0:T(1,128)}, bf16[4096,2048]{1,0:T(8,128)(2...) custom-call(s32[1]{0:T(128)} %bitcast.6.core_ref, ...), custom_call_target="tpu_custom_call", output_to_operand_aliasing={{2}: (8, {}), {3}: (9, {}), {4}: (10, {}), {5}: (11, {}), {... | custom-call | flops 19327352832 | bytes 38273024 | tf_op jit(solution)/shard_map/experts/pallas_call | solution.py:673
  512.5 10.8 collective-permute-done.6
  525.8 33.7 %experts.6 = (bf16[4,256,2048]{2,1,0:T(8,128)(2,1)}, bf16[4,256,2048]{2,1,0:T(8,128)(2,1)}, f32[8,2,2,1,256]{4,3,2,1,0:T(1,128)}, bf16[4096,2048]{1,0:T(8,128)(2...) custom-call(s32[1]{0:T(128)} %bitcast.6.core_ref, ...), custom_call_target="tpu_custom_call", output_to_operand_aliasing={{2}: (8, {}), {3}: (9, {}), {4}: (10, {}), {5}: (11, {}), {... | custom-call | flops 19327352832 | bytes 38273024 | tf_op jit(solution)/shard_map/experts/pallas_call | solution.py:673
  560.1 4.8 add_convert_fusion.28
  573.2 33.7 %experts.7 = (bf16[4,256,2048]{2,1,0:T(8,128)(2,1)}, bf16[4,256,2048]{2,1,0:T(8,128)(2,1)}, f32[8,2,2,1,256]{4,3,2,1,0:T(1,128)}, bf16[4096,2048]{1,0:T(8,128)(2...) custom-call(s32[1]{0:T(128)} %bitcast.6.core_ref, ...), custom_call_target="tpu_custom_call", output_to_operand_aliasing={{2}: (8, {}), {3}: (9, {}), {4}: (10, {}), {5}: (11, {}), {... | custom-call | flops 19327352832 | bytes 38273024 | tf_op jit(solution)/shard_map/experts/pallas_call | solution.py:673
  607.0 10.3 collective-permute-done.10
  618.0 4.7 all-to-all-start.1
  622.7 5.7 add_convert_fusion.7
  651.2 28.5 %results.3 = (bf16[12,256,2048]{2,1,0:T(8,128)(2,1)}, bf16[12,256,2048]{2,1,0:T(8,128)(2,1)}) custom-call(s32[1]{0:T(128)} %bitcast.6.core_ref, s32[48]{0:T(128)} %stack.62.order, bf16[4096,768]{1,0:T(8,128)(2,1)} %get-tuple-element.232.z_ref, f32[8,2,2,1,256]{4,3,2,1,0:T(1,128)} %reshape.268.w_ref, bf16[768,2048]{1,0:T(8,128)(2,1)} %bitcast.161), custom_call_target="tpu_custom_call" | custom-call | flops 12884901888 | bytes 33030144 | tf_op jit(solution)/shard_map/results/pallas_call | solution.py:704
  679.7 11.9 %results.2 = (bf16[4,256,2048]{2,1,0:T(8,128)(2,1)}, bf16[4,256,2048]{2,1,0:T(8,128)(2,1)}) custom-call(s32[1]{0:T(128)} %bitcast.6.core_ref, s32[16]{0:T(128)} %stack.47.order, bf16[4096,768]{1,0:T(8,128)(2,1)} %get-tuple-element.232.z_ref, f32[8,2,2,1,256]{4,3,2,1,0:T(1,128)} %reshape.268.w_ref, bf16[768,2048]{1,0:T(8,128)(2,1)} %bitcast.162), custom_call_target="tpu_custom_call" | custom-call | flops 4294967296 | bytes 13107200 | tf_op jit(solution)/shard_map/results/pallas_call | solution.py:704
  699.1 10.9 collective-permute-start.19
  710.0 25.1 %collective-permute-done.19 = bf16[256,2048]{1,0:T(8,128)(2,1)S(1)} collective-permute-done((bf16[256,2048]{1,0:T(8,128)(2,1)S(1)}, bf16[256,2048]{1,0:T(8,128)(2,1)S(1)}, u32[]{:S(2)}, u32[]{:S(2)}) %collective-permute-start.19) | collective-permute-done | bytes 1048608 | tf_op jit(solution)/shard_map/ppermute | solution.py:358
  740.8 5.9 add_convert_fusion.2
  748.1 5.1 add_convert_fusion.13
  765.1 6.2 collective-permute-done.22
  775.3 6.8 convolution_convert_fusion.1
  786.3 10.6 fusion.11.go_ref
  796.9 45.4 %collective-permute-done.24 = bf16[4,256,1024]{2,1,0:T(8,128)(2,1)S(1)} collective-permute-done((bf16[4,256,1024]{2,1,0:T(8,128)(2,1)}, bf16[4,256,1024]{2,1,0:T(8,128)(2,1)S(1)}, u32[]{:S(2)}, u32[]{:S(2)}) %collective-permute-start.24) | collective-permute-done | bytes 2097184 | tf_op jit(solution)/shard_map/ppermute | solution.py:337
  844.3 25.4 %attend_grad.1 = (bf16[512,2048]{1,0:T(8,128)(2,1)S(1)}, bf16[512,512]{1,0:T(8,128)(2,1)S(1)}, bf16[512,512]{1,0:T(8,128)(2,1)S(1)}, f32[4,1,128]{2,1,0:T(1,128)S(1)}, f32[4,1,128]{2,1,0:T(1,128)S(1)}) custom-call(f32[512,3072]{1,0:T(8,128)} %fusion.2.q_ref.k_ref.v_ref, f32[512,3072]{1,0:T(8,128)} %fusion.2.q_ref.k_ref.v_ref, bf16[512,2048]{1,0:T(8,128)(2,1)} %copy-done, ...), custom_call_target="tpu_custom_call" | custom-call | flops 5368709120 | bytes 15728640 | tf_op jit(solution)/shard_map/attend_grad/pallas_call | solution.py:548
  870.1 4.7 collective-permute-done.25
  874.8 26.9 %collective-permute-done.26 = bf16[4,256,1024]{2,1,0:T(8,128)(2,1)} collective-permute-done((bf16[4,256,1024]{2,1,0:T(8,128)(2,1)}, bf16[4,256,1024]{2,1,0:T(8,128)(2,1)}, u32[]{:S(2)}, u32[]{:S(2)}) %collective-permute-start.26) | collective-permute-done | bytes 2097184 | tf_op jit(solution)/shard_map/ppermute | solution.py:337
  901.7 10.2 convolution_convert_fusion
  912.0 4.7 add_convert_fusion
  923.1 39.1 %collective-permute-done.28 = bf16[4,256,1024]{2,1,0:T(8,128)(2,1)} collective-permute-done((bf16[4,256,1024]{2,1,0:T(8,128)(2,1)}, bf16[4,256,1024]{2,1,0:T(8,128)(2,1)}, u32[]{:S(2)}, u32[]{:S(2)}) %collective-permute-start.28) | collective-permute-done | bytes 2097184 | tf_op jit(solution)/shard_map/ppermute | solution.py:341
  962.2 20.4 %collective-permute-done.27 = bf16[4,256,1024]{2,1,0:T(8,128)(2,1)} collective-permute-done((bf16[4,256,1024]{2,1,0:T(8,128)(2,1)}, bf16[4,256,1024]{2,1,0:T(8,128)(2,1)}, u32[]{:S(2)}, u32[]{:S(2)}) %collective-permute-start.27) | collective-permute-done | bytes 2097184 | tf_op jit(solution)/shard_map/ppermute | solution.py:337
  982.6 4.5 fusion.40
  996.7 10.6 fusion
  1013.7 33.1 %convolution_bitcast_fusion = f32[1,2048,1536]{2,1,0:T(8,128)} fusion(bf16[4096,2048]{1,0:T(8,128)(2,1)S(1)} %bitcast.150, bf16[4096,1536]{1,0:T(8,128)(2,1)} %get-tuple-element.231), kind=kOutput, calls=%fused_computation.5 | convolution fusion | flops 25769803776 | bytes 41943040 | tf_op jit(solution)/shard_map/dot_general | solution.py:321
  1046.8 19.2 %convolution_bitcast_fusion.1 = f32[1,768,2048]{2,1,0:T(8,128)} fusion(bf16[4096,768]{1,0:T(8,128)(2,1)S(1)} %bitcast.156, bf16[4096,2048]{1,0:T(8,128)(2,1)} %get-tuple-element.233), kind=kOutput, calls=%fused_computation.26 | convolution fusion | flops 12884901888 | bytes 29360128 | tf_op jit(solution)/shard_map/dot_general | solution.py:321
  1091.2 28.3 %collective-permute-done.38 = bf16[256,2048]{1,0:T(8,128)(2,1)} collective-permute-done((bf16[256,2048]{1,0:T(8,128)(2,1)}, bf16[256,2048]{1,0:T(8,128)(2,1)}, u32[]{:S(2)}, u32[]{:S(2)}) %collective-permute-start.38) | collective-permute-done | bytes 1048608 | tf_op jit(solution)/shard_map/ppermute | solution.py:376
  1123.2 6.5 fusion.21
  1137.3 10.8 collective-permute-done.40
  1149.7 12.0 %collective-permute-done.39.other_ref = bf16[128,3072]{1,0:T(8,128)(2,1)S(1)} collective-permute-done((bf16[128,3072]{1,0:T(8,128)(2,1)}, bf16[128,3072]{1,0:T(8,128)(2,1)S(1)}, u32[]{:S(2)}, u32[]{:S(2)}) %collective-permute-start.39) | collective-permute-done | bytes 786464 | tf_op jit(solution)/shard_map/ppermute | solution.py:341
  (355 shorter events, 168.9 us)
Async XLA Ops:
  7.2 116.1 %all-gather.4.cloned.1.call-start = ((), (), s32[]{:S(2)}) async-start(), calls=%async_computation.4 | async-start | bytes 22282240 | tf_op jit(solution)/shard_map/all_gather | solution.py:839
  10.2 249.5 %all-gather.8.cloned.1.call-start = ((), (), s32[]{:S(2)}) async-start(), calls=%async_computation.6 | async-start | bytes 27852800 | tf_op jit(solution)/shard_map/all_gather | solution.py:846
  10.4 16.3 %collective-permute-start.3 = (bf16[256,1152]{1,0:T(8,128)(2,1)S(1)}, bf16[256,1152]{1,0:T(8,128)(2,1)S(1)}, u32[]{:S(2)}, u32[]{:S(2)}) collective-permute-start(bf16[256,1152]{1,0:T(8,128)(2,1)S(1)} %slice.417), channel_id=1, source_target_pairs={{0,1},{1,0},{2,3},{3,2},{4,5},{5,4},{6,7},{7,6},{8,9},{9,8},{10,11... | collective-permute-start | bytes 1769480 | tf_op jit(solution)/shard_map/ppermute | solution.py:341
  28.1 401.9 %all-gather.6.cloned.1.call-start = ((), (), s32[]{:S(2)}) async-start(), calls=%async_computation.5 | async-start | bytes 35651584 | tf_op jit(solution)/shard_map/all_gather | solution.py:867
  28.1 26.4 %collective-permute-start = (bf16[256,2048]{1,0:T(8,128)(2,1)S(1)}, bf16[256,2048]{1,0:T(8,128)(2,1)}, u32[]{:S(2)}, u32[]{:S(2)}) collective-permute-start(bf16[256,2048]{1,0:T(8,128)(2,1)S(1)} %copy-done.7), channel_id=1, source_target_pairs={{0,1},{1,0},{2,3},{3,2},{4,5},{5,4},{6,7},{7,6},{8,9},{9,8},{10,11... | collective-permute-start | bytes 3145736 | tf_op jit(solution)/shard_map/ppermute | solution.py:341
  162.0 25.4 %collective-permute-start.1 = (bf16[256,2048]{1,0:T(8,128)(2,1)S(1)}, bf16[256,2048]{1,0:T(8,128)(2,1)S(1)}, u32[]{:S(2)}, u32[]{:S(2)}) collective-permute-start(bf16[256,2048]{1,0:T(8,128)(2,1)S(1)} %select_convert_fusion.1), channel_id=1, source_target_pairs={{0,1},{1,0},{2,3},{3,2},{4,5},{5,4},{6,7},{7,6},{8,9},{9,8},{10,11... | collective-permute-start | bytes 3145736 | tf_op jit(solution)/shard_map/ppermute | solution.py:341
  190.2 24.7 %collective-permute-start.2 = (bf16[256,2048]{1,0:T(8,128)(2,1)S(1)}, bf16[256,2048]{1,0:T(8,128)(2,1)S(1)}, u32[]{:S(2)}, u32[]{:S(2)}) collective-permute-start(bf16[256,2048]{1,0:T(8,128)(2,1)S(1)} %multiply_convert_fusion), channel_id=1, source_target_pairs={{0,1},{1,0},{2,3},{3,2},{4,5},{5,4},{6,7},{7,6},{8,9},{9,8},{10,11... | collective-permute-start | bytes 3145736 | tf_op jit(solution)/shard_map/ppermute | solution.py:341
  266.6 160.5 %collective-permute-start.4 = (bf16[8,2,256,896]{3,2,1,0:T(8,128)(2,1)}, bf16[8,2,256,896]{3,2,1,0:T(8,128)(2,1)}, u32[]{:S(2)}, u32[]{:S(2)}) collective-permute-start(bf16[8,2,256,896]{3,2,1,0:T(8,128)(2,1)} %slice.419), channel_id=1, source_target_pairs={{0,1},{1,0},{2,3},{3,2},{4,5},{5,4},{6,7},{7,6},{8,9},{9,8},{10,11... | collective-permute-start | bytes 22020104 | tf_op jit(solution)/shard_map/ppermute | solution.py:341
  463.0 7.4 collective-permute-start.5
  475.3 48.1 %collective-permute-start.6 = (bf16[4,256,1024]{2,1,0:T(8,128)(2,1)}, bf16[4,256,1024]{2,1,0:T(8,128)(2,1)}, u32[]{:S(2)}, u32[]{:S(2)}) collective-permute-start(bf16[4,256,1024]{2,1,0:T(8,128)(2,1)} %get-tuple-element.141), channel_id=1, source_target_pairs={{0,1},{1,0},{2,3},{3,2},{4,5},{5,4},{6,7},{7,6},{8,9},{9,8},{10,11... | collective-permute-start | bytes 6291464 | tf_op jit(solution)/shard_map/ppermute | solution.py:341
  476.7 47.8 %collective-permute-start.7 = (bf16[4,256,1024]{2,1,0:T(8,128)(2,1)}, bf16[4,256,1024]{2,1,0:T(8,128)(2,1)}, u32[]{:S(2)}, u32[]{:S(2)}) collective-permute-start(bf16[4,256,1024]{2,1,0:T(8,128)(2,1)} %get-tuple-element.142), channel_id=1, source_target_pairs={{0,4},{2,6},{4,0},{6,2},{8,12},{10,14},{12,8},{14,10},{16,20},{18,... | collective-permute-start | bytes 6291464 | tf_op jit(solution)/shard_map/ppermute | solution.py:337
  524.6 35.5 %collective-permute-start.8 = (bf16[4,256,2048]{2,1,0:T(8,128)(2,1)}, bf16[4,256,2048]{2,1,0:T(8,128)(2,1)}, u32[]{:S(2)}, u32[]{:S(2)}) collective-permute-start(bf16[4,256,2048]{2,1,0:T(8,128)(2,1)} %get-tuple-element.143), channel_id=1, source_target_pairs={{0,2},{2,0},{4,6},{6,4},{8,10},{10,8},{12,14},{14,12},{16,18},{18,... | collective-permute-start | bytes 12582920 | tf_op jit(solution)/shard_map/ppermute | solution.py:333
  559.5 63.2 %collective-permute-start.14 = (bf16[4,256,2048]{2,1,0:T(8,128)(2,1)}, bf16[4,256,2048]{2,1,0:T(8,128)(2,1)}, u32[]{:S(2)}, u32[]{:S(2)}) collective-permute-start(bf16[4,256,2048]{2,1,0:T(8,128)(2,1)} %get-tuple-element.173), channel_id=1, source_target_pairs={{0,2},{2,0},{4,6},{6,4},{8,10},{10,8},{12,14},{14,12},{16,18},{18,... | collective-permute-start | bytes 12582920 | tf_op jit(solution)/shard_map/ppermute | solution.py:333
  566.5 40.5 %collective-permute-start.12 = (bf16[2,256,1024]{2,1,0:T(8,128)(2,1)S(1)}, bf16[2,256,1024]{2,1,0:T(8,128)(2,1)}, u32[]{:S(2)}, u32[]{:S(2)}) collective-permute-start(bf16[2,256,1024]{2,1,0:T(8,128)(2,1)S(1)} %add_convert_fusion.26), channel_id=1, source_target_pairs={{0,1},{1,0},{2,3},{3,2},{4,5},{5,4},{6,7},{7,6},{8,9},{9,8},{10,11... | collective-permute-start | bytes 3145736 | tf_op jit(solution)/shard_map/ppermute | solution.py:341
  569.7 37.3 %collective-permute-start.11 = (bf16[2,256,1024]{2,1,0:T(8,128)(2,1)}, bf16[2,256,1024]{2,1,0:T(8,128)(2,1)}, u32[]{:S(2)}, u32[]{:S(2)}) collective-permute-start(bf16[2,256,1024]{2,1,0:T(8,128)(2,1)} %add_convert_fusion.27), channel_id=1, source_target_pairs={{0,4},{2,6},{4,0},{6,2},{8,12},{10,14},{12,8},{14,10},{16,20},{18,... | collective-permute-start | bytes 3145736 | tf_op jit(solution)/shard_map/ppermute | solution.py:337
  570.9 46.4 %collective-permute-start.10 = (bf16[2,256,1024]{2,1,0:T(8,128)(2,1)S(1)}, bf16[2,256,1024]{2,1,0:T(8,128)(2,1)}, u32[]{:S(2)}, u32[]{:S(2)}) collective-permute-start(bf16[2,256,1024]{2,1,0:T(8,128)(2,1)S(1)} %get-tuple-element.161), channel_id=1, source_target_pairs={{0,4},{2,6},{4,0},{6,2},{8,12},{10,14},{12,8},{14,10},{16,20},{18,... | collective-permute-start | bytes 3145736 | tf_op jit(solution)/shard_map/ppermute | solution.py:337
  571.7 45.6 %collective-permute-start.9 = (bf16[2,256,1024]{2,1,0:T(8,128)(2,1)S(1)}, bf16[2,256,1024]{2,1,0:T(8,128)(2,1)}, u32[]{:S(2)}, u32[]{:S(2)}) collective-permute-start(bf16[2,256,1024]{2,1,0:T(8,128)(2,1)S(1)} %get-tuple-element.160), channel_id=1, source_target_pairs={{0,1},{1,0},{2,3},{3,2},{4,5},{5,4},{6,7},{7,6},{8,9},{9,8},{10,11... | collective-permute-start | bytes 3145736 | tf_op jit(solution)/shard_map/ppermute | solution.py:341
  617.3 19.9 %collective-permute-start.13 = (bf16[4,256,2048]{2,1,0:T(8,128)(2,1)}, bf16[4,256,2048]{2,1,0:T(8,128)(2,1)}, u32[]{:S(2)}, u32[]{:S(2)}) collective-permute-start(bf16[4,256,2048]{2,1,0:T(8,128)(2,1)} %get-tuple-element.166), channel_id=1, source_target_pairs={{0,2},{2,0},{4,6},{6,4},{8,10},{10,8},{12,14},{14,12},{16,18},{18,... | collective-permute-start | bytes 12582920 | tf_op jit(solution)/shard_map/ppermute | solution.py:333
  618.0 12.0 %all-to-all-start.1 = ((f32[32,1,256]{2,1,0:T(1,128)}), f32[32,1,256]{2,1,0:T(1,128)S(1)}, u32[]{:S(2)}, u32[]{:S(2)}) async-start(f32[32,1,256]{2,1,0:T(1,128)} %bitcast.167), calls=%async_computation.1 | async-start | bytes 65536 | tf_op jit(solution)/shard_map/all_to_all | solution.py:968
  622.7 510.3 %reduce-scatter.5.cloned.1.call-start = ((), (), s32[]{:S(2)}) async-start(), calls=%async_computation.8 | async-start | bytes 8912896 | tf_op jit(solution)/shard_map/reduce_scatter | solution.py:1038
  636.0 60.4 %collective-permute-start.18 = (bf16[256,2048]{1,0:T(8,128)(2,1)}, bf16[256,2048]{1,0:T(8,128)(2,1)S(1)}, u32[]{:S(2)}, u32[]{:S(2)}) collective-permute-start(bf16[256,2048]{1,0:T(8,128)(2,1)} %pad_maximum_fusion.14), channel_id=1, source_target_pairs={{0,16},{2,18},{4,20},{6,22},{8,24},{10,26},{12,28},{14,30},{16,0},... | collective-permute-start | bytes 3145736 | tf_op jit(solution)/shard_map/ppermute | solution.py:358
  642.5 49.0 %collective-permute-start.16 = (bf16[2,2,256,1024]{3,2,1,0:T(8,128)(2,1)S(1)}, bf16[2,2,256,1024]{3,2,1,0:T(8,128)(2,1)}, u32[]{:S(2)}, u32[]{:S(2)}) collective-permute-start(bf16[2,2,256,1024]{3,2,1,0:T(8,128)(2,1)S(1)} %pad_maximum_fusion.5), channel_id=1, source_target_pairs={{0,4},{2,6},{4,0},{6,2},{8,12},{10,14},{12,8},{14,10},{16,20},{18,... | collective-permute-start | bytes 6291464 | tf_op jit(solution)/shard_map/ppermute | solution.py:337
  647.2 47.4 %collective-permute-start.15 = (bf16[2,2,256,1024]{3,2,1,0:T(8,128)(2,1)}, bf16[2,2,256,1024]{3,2,1,0:T(8,128)(2,1)}, u32[]{:S(2)}, u32[]{:S(2)}) collective-permute-start(bf16[2,2,256,1024]{3,2,1,0:T(8,128)(2,1)} %pad_maximum_fusion.4), channel_id=1, source_target_pairs={{0,1},{1,0},{2,3},{3,2},{4,5},{5,4},{6,7},{7,6},{8,9},{9,8},{10,11... | collective-permute-start | bytes 6291464 | tf_op jit(solution)/shard_map/ppermute | solution.py:341
  649.8 47.0 %collective-permute-start.17 = (bf16[256,2048]{1,0:T(8,128)(2,1)}, bf16[256,2048]{1,0:T(8,128)(2,1)}, u32[]{:S(2)}, u32[]{:S(2)}) collective-permute-start(bf16[256,2048]{1,0:T(8,128)(2,1)} %pad_maximum_fusion.13), channel_id=1, source_target_pairs={{0,24},{2,26},{4,28},{6,30},{8,0},{10,2},{12,4},{14,6},{16,8},{18,... | collective-permute-start | bytes 3145736 | tf_op jit(solution)/shard_map/ppermute | solution.py:358
  696.7 49.9 %collective-permute-start.21 = (bf16[12,256,2048]{2,1,0:T(8,128)(2,1)}, bf16[12,256,2048]{2,1,0:T(8,128)(2,1)S(1)}, u32[]{:S(2)}, u32[]{:S(2)}) collective-permute-start(bf16[12,256,2048]{2,1,0:T(8,128)(2,1)} %get-tuple-element.197), channel_id=1, source_target_pairs={{0,2},{2,0},{4,6},{6,4},{8,10},{10,8},{12,14},{14,12},{16,18},{18,... | collective-permute-start | bytes 37748744 | tf_op jit(solution)/shard_map/ppermute | solution.py:333
  696.7 42.4 %collective-permute-start.20 = (bf16[4,256,2048]{2,1,0:T(8,128)(2,1)}, bf16[4,256,2048]{2,1,0:T(8,128)(2,1)}, u32[]{:S(2)}, u32[]{:S(2)}) collective-permute-start(bf16[4,256,2048]{2,1,0:T(8,128)(2,1)} %get-tuple-element.195), channel_id=1, source_target_pairs={{0,2},{2,0},{4,6},{6,4},{8,10},{10,8},{12,14},{14,12},{16,18},{18,... | collective-permute-start | bytes 12582920 | tf_op jit(solution)/shard_map/ppermute | solution.py:333
  699.1 36.0 %collective-permute-start.19 = (bf16[256,2048]{1,0:T(8,128)(2,1)S(1)}, bf16[256,2048]{1,0:T(8,128)(2,1)S(1)}, u32[]{:S(2)}, u32[]{:S(2)}) collective-permute-start(bf16[256,2048]{1,0:T(8,128)(2,1)S(1)} %pad_maximum_fusion.15), channel_id=1, source_target_pairs={{0,8},{2,10},{4,12},{6,14},{8,16},{10,18},{12,20},{14,22},{16,24},... | collective-permute-start | bytes 3145736 | tf_op jit(solution)/shard_map/ppermute | solution.py:358
  746.6 24.7 %collective-permute-start.22 = (bf16[256,2048]{1,0:T(8,128)(2,1)S(1)}, bf16[256,2048]{1,0:T(8,128)(2,1)}, u32[]{:S(2)}, u32[]{:S(2)}) collective-permute-start(bf16[256,2048]{1,0:T(8,128)(2,1)S(1)} %fusion.52), channel_id=1, source_target_pairs={{0,1},{1,0},{2,3},{3,2},{4,5},{5,4},{6,7},{7,6},{8,9},{9,8},{10,11... | collective-permute-start | bytes 3145736 | tf_op jit(solution)/shard_map/ppermute | solution.py:341
  782.1 351.8 %reduce-scatter.3.cloned.1.call-start = ((), (), s32[]{:S(2)}) async-start(), calls=%async_computation.7 | async-start | bytes 13369344 | tf_op jit(solution)/shard_map/reduce_scatter | solution.py:1045
  782.2 60.1 %collective-permute-start.24 = (bf16[4,256,1024]{2,1,0:T(8,128)(2,1)}, bf16[4,256,1024]{2,1,0:T(8,128)(2,1)S(1)}, u32[]{:S(2)}, u32[]{:S(2)}) collective-permute-start(bf16[4,256,1024]{2,1,0:T(8,128)(2,1)} %get-tuple-element.263), channel_id=1, source_target_pairs={{0,4},{2,6},{4,0},{6,2},{8,12},{10,14},{12,8},{14,10},{16,20},{18,... | collective-permute-start | bytes 6291464 | tf_op jit(solution)/shard_map/ppermute | solution.py:337
  783.7 58.5 %collective-permute-start.23 = (bf16[4,256,1024]{2,1,0:T(8,128)(2,1)}, bf16[4,256,1024]{2,1,0:T(8,128)(2,1)S(1)}, u32[]{:S(2)}, u32[]{:S(2)}) collective-permute-start(bf16[4,256,1024]{2,1,0:T(8,128)(2,1)} %get-tuple-element.203), channel_id=1, source_target_pairs={{0,1},{1,0},{2,3},{3,2},{4,5},{5,4},{6,7},{7,6},{8,9},{9,8},{10,11... | collective-permute-start | bytes 6291464 | tf_op jit(solution)/shard_map/ppermute | solution.py:341
  785.2 89.6 %collective-permute-start.25 = (bf16[4,256,1024]{2,1,0:T(8,128)(2,1)}, bf16[4,256,1024]{2,1,0:T(8,128)(2,1)}, u32[]{:S(2)}, u32[]{:S(2)}) collective-permute-start(bf16[4,256,1024]{2,1,0:T(8,128)(2,1)} %pad_maximum_fusion.8), channel_id=1, source_target_pairs={{0,1},{1,0},{2,3},{3,2},{4,5},{5,4},{6,7},{7,6},{8,9},{9,8},{10,11... | collective-permute-start | bytes 6291464 | tf_op jit(solution)/shard_map/ppermute | solution.py:341
  785.7 116.0 %collective-permute-start.26 = (bf16[4,256,1024]{2,1,0:T(8,128)(2,1)}, bf16[4,256,1024]{2,1,0:T(8,128)(2,1)}, u32[]{:S(2)}, u32[]{:S(2)}) collective-permute-start(bf16[4,256,1024]{2,1,0:T(8,128)(2,1)} %pad_maximum_fusion.7), channel_id=1, source_target_pairs={{0,4},{2,6},{4,0},{6,2},{8,12},{10,14},{12,8},{14,10},{16,20},{18,... | collective-permute-start | bytes 6291464 | tf_op jit(solution)/shard_map/ppermute | solution.py:337
  916.7 45.5 %collective-permute-start.28 = (bf16[4,256,1024]{2,1,0:T(8,128)(2,1)}, bf16[4,256,1024]{2,1,0:T(8,128)(2,1)}, u32[]{:S(2)}, u32[]{:S(2)}) collective-permute-start(bf16[4,256,1024]{2,1,0:T(8,128)(2,1)} %add_convert_fusion), channel_id=1, source_target_pairs={{0,1},{1,0},{2,3},{3,2},{4,5},{5,4},{6,7},{7,6},{8,9},{9,8},{10,11... | collective-permute-start | bytes 6291464 | tf_op jit(solution)/shard_map/ppermute | solution.py:341
  920.5 62.1 %collective-permute-start.27 = (bf16[4,256,1024]{2,1,0:T(8,128)(2,1)}, bf16[4,256,1024]{2,1,0:T(8,128)(2,1)}, u32[]{:S(2)}, u32[]{:S(2)}) collective-permute-start(bf16[4,256,1024]{2,1,0:T(8,128)(2,1)} %add_convert_fusion.1), channel_id=1, source_target_pairs={{0,4},{2,6},{4,0},{6,2},{8,12},{10,14},{12,8},{14,10},{16,20},{18,... | collective-permute-start | bytes 6291464 | tf_op jit(solution)/shard_map/ppermute | solution.py:337
  994.7 74.9 %collective-permute-start.30 = (bf16[256,2048]{1,0:T(8,128)(2,1)}, bf16[256,2048]{1,0:T(8,128)(2,1)}, u32[]{:S(2)}, u32[]{:S(2)}) collective-permute-start(bf16[256,2048]{1,0:T(8,128)(2,1)} %get-tuple-element.300), channel_id=1, source_target_pairs={{0,8},{2,10},{4,12},{6,14},{8,0},{10,2},{12,4},{14,6},{16,24},{18,... | collective-permute-start | bytes 3145736 | tf_op jit(solution)/shard_map/ppermute | solution.py:372
  994.7 76.4 %collective-permute-start.31 = (bf16[256,2048]{1,0:T(8,128)(2,1)}, bf16[256,2048]{1,0:T(8,128)(2,1)}, u32[]{:S(2)}, u32[]{:S(2)}) collective-permute-start(bf16[256,2048]{1,0:T(8,128)(2,1)} %get-tuple-element.299), channel_id=1, source_target_pairs={{0,8},{2,10},{4,12},{6,14},{8,0},{10,2},{12,4},{14,6},{16,24},{18,... | collective-permute-start | bytes 3145736 | tf_op jit(solution)/shard_map/ppermute | solution.py:372
  1013.1 52.9 %collective-permute-start.29 = (bf16[256,2048]{1,0:T(8,128)(2,1)}, bf16[256,2048]{1,0:T(8,128)(2,1)}, u32[]{:S(2)}, u32[]{:S(2)}) collective-permute-start(bf16[256,2048]{1,0:T(8,128)(2,1)} %select_convert_fusion), channel_id=1, source_target_pairs={{0,1},{1,0},{2,3},{3,2},{4,5},{5,4},{6,7},{7,6},{8,9},{9,8},{10,11... | collective-permute-start | bytes 3145736 | tf_op jit(solution)/shard_map/ppermute | solution.py:341
  1071.1 5.1 collective-permute-start.32
  1075.7 43.8 %collective-permute-start.38 = (bf16[256,2048]{1,0:T(8,128)(2,1)}, bf16[256,2048]{1,0:T(8,128)(2,1)}, u32[]{:S(2)}, u32[]{:S(2)}) collective-permute-start(bf16[256,2048]{1,0:T(8,128)(2,1)} %add_convert_fusion.11), channel_id=1, source_target_pairs={{0,16},{2,18},{4,20},{6,22},{8,24},{10,26},{12,28},{14,30},{16,0},... | collective-permute-start | bytes 3145736 | tf_op jit(solution)/shard_map/ppermute | solution.py:376
  1082.4 4.5 collective-permute-start.36
  1083.7 3.8 collective-permute-start.34
  1086.8 4.4 collective-permute-start.37
  1119.5 10.2 collective-permute-start.41
  1123.2 6.5 collective-permute-start.44
  1129.8 5.2 collective-permute-start.42
  1133.0 15.1 %collective-permute-start.40 = (bf16[128,2048]{1,0:T(8,128)(2,1)}, bf16[128,2048]{1,0:T(8,128)(2,1)S(1)}, u32[]{:S(2)}, u32[]{:S(2)}) collective-permute-start(bf16[128,2048]{1,0:T(8,128)(2,1)} %reduce-scatter.5.cloned.1.call-done), channel_id=1, source_target_pairs={{0,1},{1,0},{2,3},{3,2},{4,5},{5,4},{6,7},{7,6},{8,9},{9,8},{10,11... | collective-permute-start | bytes 1572872 | tf_op jit(solution)/shard_map/ppermute | solution.py:341
  1133.9 27.7 %collective-permute-start.39 = (bf16[128,3072]{1,0:T(8,128)(2,1)}, bf16[128,3072]{1,0:T(8,128)(2,1)S(1)}, u32[]{:S(2)}, u32[]{:S(2)}) collective-permute-start(bf16[128,3072]{1,0:T(8,128)(2,1)} %reduce-scatter.3.cloned.1.call-done.mine_ref), channel_id=1, source_target_pairs={{0,1},{1,0},{2,3},{3,2},{4,5},{5,4},{6,7},{7,6},{8,9},{9,8},{10,11... | collective-permute-start | bytes 2359304 | tf_op jit(solution)/shard_map/ppermute | solution.py:341
  (80 other events, 1673.5 us)
Sparse Core Ops, SparseCore 0:
  10.4 112.8 all-gather.3
  125.4 134.2 all-gather.7
  261.9 168.0 all-gather.5
  782.2 124.5 reduce-scatter.4
  912.1 162.1 reduce-scatter.2

commit v16 on v10

--- a/solution.py
+++ b/solution.py
@@ -1008,7 +1008,9 @@
     side_one, side_two, ctx_one, ctx_two = out_sums
     out_far[0] = swap_ctx(out_far[0])
     grad_attended = mul(grad_branch, out_all, rhs_turned).astype(low)
-    grad_attended, out_far = hold(grad_attended, out_far)
+    (rows, grad_pair), grad_attended = hold((rows, grad_pair), grad_attended)
+    grad_gate_up = mul(rows, grad_pair, lhs_turned)[None]
+    grad_attended, (out_far, grad_gate_up) = hold(grad_attended, (out_far, grad_gate_up))
     got = [
         swap_ctx(ctx_one),
         swap_side(side_two),
@@ -1020,10 +1022,10 @@
         projected, roped_q, roped_k, values_low, grad_attended, cosine, sine, gain_q, gain_k, kv_heads, group
     )
     grad_projected = jnp.concatenate([grad_q, grad_k, grad_v], axis=1)
-    grad_projected, (got[0], got[1]) = hold(grad_projected, (got[0], got[1]))
+    (hidden, grad_rows), grad_projected = hold((hidden, grad_rows), grad_projected)
+    grad_down = mul(hidden, grad_rows, lhs_turned)[None]
+    grad_projected, (got[0], got[1], grad_down) = hold(grad_projected, (got[0], got[1], grad_down))
     grad_qkv_part = mul(low_in, grad_projected, lhs_turned).astype(low)
-    grad_gate_up = mul(rows, grad_pair, lhs_turned)[None]
-    got, grad_gate_up = hold(got, grad_gate_up)
     entries = joined(places, out_own, got)
     if lines == 4:
         output = (mixed + line_halving(entries, place)).astype(low)
@@ -1060,8 +1062,6 @@
         ),
         fsdp,
     )
-    (hidden, grad_rows), late = hold((hidden, grad_rows), late)
-    grad_down = mul(hidden, grad_rows, lhs_turned)[None]
     gain_rows = width // head_dim
     return (
         output,

time: 1160 us -> 1180 us (1.017)
  starting transfers between devices: 52.8 us -> 71.3 us
    ppermute x8, waiting for transfers between devices: 79.3 us -> 29.1 us  [swap_side(): return lax.ppermute(values, 'fsdp', side_pairs(lax.axis_size('fsdp')))]
    ppermute x19, waiting for transfers between devices: 267 us -> 293 us  [swap_ctx(): return lax.ppermute(values, 'ctx', [(0, 1), (1, 0)])]
    ppermute x4, waiting for transfers between devices: 30.4 us -> 53.7 us  [sum_owned(): lax.ppermute(take(values, 1 - bit), 'fsdp', [(i, i ^ step) for i in range...]
    ppermute x3, starting transfers between devices: 3.66 us -> 24.7 us  [line_shift(): lax.ppermute(values, 'fsdp', [(i, (i + 4 * step) % fsdp) for i in range(f...]
    ppermute x1, waiting for transfers between devices: 14.3 us -> 29.2 us  [line_halving(): lax.ppermute(add_low(entries[2], two), 'fsdp', [(i, i ^ 8) for i in range...]
    ppermute x2, waiting for transfers between devices: 25.5 us -> 12.6 us  [line_halving(): lax.ppermute(item, 'fsdp', [(i, i ^ 4) for i in range(fsdp)])]
where the time goes in v16:
time: 1180 us; the launch traced here: 1170 us
  waiting for transfers between devices  578 us (49%)
  Pallas kernels  224 us (19%)
  matrix products  113 us (10%)
  other arithmetic  107 us (9%)
  starting transfers between devices  71.3 us (6%)
  blocking collectives  35.6 us (3%)
  local copies, waits for them, and re-layouts  28.6 us (2%)
  between operations  15.4 us (1%)
    ppermute x19, waiting for transfers between devices, swap_ctx(): return lax.ppermute(values, 'ctx', [(0, 1), (1, 0)])  293 us
    pallas_call x4, Pallas kernels, run_expert(): pl.pallas_call(expert_kernel, grid_spec=grid_spec, out_shape=[shape((step...  135 us
    dot_general x11, matrix products, mul(): return lax.dot_general(left, right, dims, preferred_element_type=full)  113 us
    convert_element_type x20, other arithmetic, add_low(): return (one.astype(full) + two.astype(full)).astype(low)  70.3 us
    all_gather x1, waiting for transfers between devices, body_gathered(): weights_all = lax.all_gather(weights_local, 'fsdp', axis=0, tiled=True)  65.6 us
    ppermute x4, waiting for transfers between devices, sum_owned(): lax.ppermute(take(values, 1 - bit), 'fsdp', [(i, i ^ step) for i in range...  53.7 us
    ppermute x3, waiting for transfers between devices, line_shift(): lax.ppermute(values, 'fsdp', [(i, (i + 4 * step) % fsdp) for i in range(f...  45.8 us
    pallas_call x2, Pallas kernels, run_result(): pl.pallas_call(result_kernel, grid_spec=pltpu.PrefetchScalarGridSpec(num_...  40.1 us
  transfers between devices with their start and end apart: 53, of which 28 were waited for; matrix products, arithmetic and copies ran while one was open for 19% of the time, Pallas kernels for 16%

profile of v16, /device:TPU:0, one launch (start us, length us, event | category | flops | bytes accessed | tf_op | source)
XLA Modules:
  0.0 1173.0 jit_solution(8173105998523316608)
XLA Ops:
  13.4 13.3 %collective-permute-done.3 = bf16[256,1152]{1,0:T(8,128)(2,1)S(1)} collective-permute-done((bf16[256,1152]{1,0:T(8,128)(2,1)S(1)}, bf16[256,1152]{1,0:T(8,128)(2,1)S(1)}, u32[]{:S(2)}, u32[]{:S(2)}) %collective-permute-start.3) | collective-permute-done | bytes 589856 | tf_op jit(solution)/shard_map/ppermute | solution.py:341
  31.2 22.9 %all_gather.12 = bf16[2048,34]{0,1:T(8,128)(2,1)S(1)} all-gather(bf16[128,34]{0,1:T(8,128)(2,1)S(1)} %pad_maximum_fusion.20), channel_id=1, replica_groups=mesh['fsdp'=16,'ctx'=2] {'fsdp'}, dimensions={0}, use_global_device_ids=true | all-gather | bytes 147968 | tf_op jit(solution)/shard_map/all_gather | solution.py:844
  57.6 65.6 %all-gather.4.cloned.1.call-done = bf16[2048,5120]{1,0:T(8,128)(2,1)} async-done(((bf16[128,5120]{1,0:T(8,128)(2,1)}), bf16[2048,5120]{1,0:T(8,128)(2,1)}) %all-gather.4.cloned.1.call-update) | async-done | bytes 20971536 | tf_op jit(solution)/shard_map/all_gather | solution.py:845
  123.2 11.5 fusion.2.q_ref.k_ref.v_ref
  134.8 18.2 %attend.1 = (bf16[512,2048]{1,0:T(8,128)(2,1)S(1)}, bf16[512,2048]{1,0:T(8,128)(2,1)S(1)}, bf16[512,512]{1,0:T(8,128)(2,1)S(1)}, bf16[512,512]{1,0:T(8,128)(2,1)S(1)}) custom-call(f32[512,3072]{1,0:T(8,128)} %fusion.2.q_ref.k_ref.v_ref, f32[512,3072]{1,0:T(8,128)} %fusion.2.q_ref.k_ref.v_ref, f32[512,3072]{1,0:T(8,128)} %fusion.2.q_ref.k_ref.v_ref, ...), custom_call_target="tpu_custom_call" | custom-call | flops 2147483648 | bytes 9437184 | tf_op jit(solution)/shard_map/attend/pallas_call | solution.py:530
  153.0 8.4 fusion.6
  163.5 23.9 %collective-permute-done.1 = bf16[256,2048]{1,0:T(8,128)(2,1)S(1)} collective-permute-done((bf16[256,2048]{1,0:T(8,128)(2,1)S(1)}, bf16[256,2048]{1,0:T(8,128)(2,1)S(1)}, u32[]{:S(2)}, u32[]{:S(2)}) %collective-permute-start.1) | collective-permute-done | bytes 1048608 | tf_op jit(solution)/shard_map/ppermute | solution.py:341
  191.8 23.1 %collective-permute-done.2 = bf16[256,2048]{1,0:T(8,128)(2,1)S(1)} collective-permute-done((bf16[256,2048]{1,0:T(8,128)(2,1)S(1)}, bf16[256,2048]{1,0:T(8,128)(2,1)S(1)}, u32[]{:S(2)}, u32[]{:S(2)}) %collective-permute-start.2) | collective-permute-done | bytes 1048608 | tf_op jit(solution)/shard_map/ppermute | solution.py:341
  218.4 12.7 %all_to_all.24 = f32[32,1,256]{2,1,0:T(1,128)S(1)} all-to-all(f32[32,1,256]{2,1,0:T(1,128)S(1)} %copy.60), channel_id=1, replica_groups=mesh['fsdp'=16,'ctx'=2] {'fsdp','ctx'}, dimensions={0} | all-to-all | bytes 65536 | tf_op jit(solution)/shard_map/all_to_all | solution.py:882
  231.1 28.6 %all-gather.8.cloned.1.call-done = bf16[4096,3200]{1,0:T(8,128)(2,1)} async-done(((bf16[256,3200]{1,0:T(8,128)(2,1)}), bf16[4096,3200]{1,0:T(8,128)(2,1)}) %all-gather.8.cloned.1.call-update) | async-done | bytes 26214416 | tf_op jit(solution)/shard_map/all_gather | solution.py:852
  259.7 6.9 slice.403
  269.4 157.7 %collective-permute-done.4.far_ref = bf16[8,2,256,896]{3,2,1,0:T(8,128)(2,1)} collective-permute-done((bf16[8,2,256,896]{3,2,1,0:T(8,128)(2,1)}, bf16[8,2,256,896]{3,2,1,0:T(8,128)(2,1)}, u32[]{:S(2)}, u32[]{:S(2)}) %collective-permute-start.4) | collective-permute-done | bytes 7340064 | tf_op jit(solution)/shard_map/ppermute | solution.py:341
  429.9 33.0 %experts.4 = (bf16[4,256,2048]{2,1,0:T(8,128)(2,1)}, bf16[4,256,2048]{2,1,0:T(8,128)(2,1)}, f32[8,2,2,1,256]{4,3,2,1,0:T(1,128)}, bf16[4096,2048]{1,0:T(8,128)(2...) custom-call(s32[1]{0:T(128)} %bitcast.6.core_ref, s32[16]{0:T(128)} %stack.35.order, ...), custom_call_target="tpu_custom_call" | custom-call | flops 19327352832 | bytes 38273024 | tf_op jit(solution)/shard_map/experts/pallas_call | solution.py:679
  463.3 7.1 collective-permute-done.5
  470.4 4.9 add_convert_fusion.8
  478.5 34.1 %experts.5 = (bf16[4,256,2048]{2,1,0:T(8,128)(2,1)}, bf16[4,256,2048]{2,1,0:T(8,128)(2,1)}, f32[8,2,2,1,256]{4,3,2,1,0:T(1,128)}, bf16[4096,2048]{1,0:T(8,128)(2...) custom-call(s32[1]{0:T(128)} %bitcast.6.core_ref, ...), custom_call_target="tpu_custom_call", output_to_operand_aliasing={{2}: (8, {}), {3}: (9, {}), {4}: (10, {}), {5}: (11, {}), {... | custom-call | flops 19327352832 | bytes 38273024 | tf_op jit(solution)/shard_map/experts/pallas_call | solution.py:679
  512.7 10.8 collective-permute-done.7
  525.9 33.7 %experts.6 = (bf16[4,256,2048]{2,1,0:T(8,128)(2,1)}, bf16[4,256,2048]{2,1,0:T(8,128)(2,1)}, f32[8,2,2,1,256]{4,3,2,1,0:T(1,128)}, bf16[4096,2048]{1,0:T(8,128)(2...) custom-call(s32[1]{0:T(128)} %bitcast.6.core_ref, ...), custom_call_target="tpu_custom_call", output_to_operand_aliasing={{2}: (8, {}), {3}: (9, {}), {4}: (10, {}), {5}: (11, {}), {... | custom-call | flops 19327352832 | bytes 38273024 | tf_op jit(solution)/shard_map/experts/pallas_call | solution.py:679
  573.0 33.7 %experts.7 = (bf16[4,256,2048]{2,1,0:T(8,128)(2,1)}, bf16[4,256,2048]{2,1,0:T(8,128)(2,1)}, f32[8,2,2,1,256]{4,3,2,1,0:T(1,128)}, bf16[4096,2048]{1,0:T(8,128)(2...) custom-call(s32[1]{0:T(128)} %bitcast.6.core_ref, ...), custom_call_target="tpu_custom_call", output_to_operand_aliasing={{2}: (8, {}), {3}: (9, {}), {4}: (10, {}), {5}: (11, {}), {... | custom-call | flops 19327352832 | bytes 38273024 | tf_op jit(solution)/shard_map/experts/pallas_call | solution.py:679
  606.7 7.3 collective-permute-done.10
  617.8 4.7 all-to-all-start.1
  622.6 5.8 add_convert_fusion.7
  652.7 11.8 %results.2 = (bf16[4,256,2048]{2,1,0:T(8,128)(2,1)}, bf16[4,256,2048]{2,1,0:T(8,128)(2,1)}) custom-call(s32[1]{0:T(128)} %bitcast.6.core_ref, s32[16]{0:T(128)} %stack.35.order, bf16[4096,768]{1,0:T(8,128)(2,1)} %get-tuple-element.200.z_ref, f32[8,2,2,1,256]{4,3,2,1,0:T(1,128)} %reshape.271.w_ref, bf16[768,2048]{1,0:T(8,128)(2,1)} %bitcast.154), custom_call_target="tpu_custom_call" | custom-call | flops 4294967296 | bytes 13107200 | tf_op jit(solution)/shard_map/results/pallas_call | solution.py:710
  664.5 19.9 %collective-permute-done.20 = bf16[256,2048]{1,0:T(8,128)(2,1)S(1)} collective-permute-done((bf16[256,2048]{1,0:T(8,128)(2,1)}, bf16[256,2048]{1,0:T(8,128)(2,1)S(1)}, u32[]{:S(2)}, u32[]{:S(2)}) %collective-permute-start.20) | collective-permute-done | bytes 1048608 | tf_op jit(solution)/shard_map/ppermute | solution.py:358
  685.8 28.3 %results.3 = (bf16[12,256,2048]{2,1,0:T(8,128)(2,1)}, bf16[12,256,2048]{2,1,0:T(8,128)(2,1)}) custom-call(s32[1]{0:T(128)} %bitcast.6.core_ref, s32[48]{0:T(128)} %stack.44.order, bf16[4096,768]{1,0:T(8,128)(2,1)} %get-tuple-element.200.z_ref, f32[8,2,2,1,256]{4,3,2,1,0:T(1,128)} %reshape.271.w_ref, bf16[768,2048]{1,0:T(8,128)(2,1)} %bitcast.155), custom_call_target="tpu_custom_call" | custom-call | flops 12884901888 | bytes 33030144 | tf_op jit(solution)/shard_map/results/pallas_call | solution.py:710
  720.6 22.0 %collective-permute-start.21 = (bf16[256,2048]{1,0:T(8,128)(2,1)S(1)}, bf16[256,2048]{1,0:T(8,128)(2,1)S(1)}, u32[]{:S(2)}, u32[]{:S(2)}) collective-permute-start(bf16[256,2048]{1,0:T(8,128)(2,1)S(1)} %pad_maximum_fusion.13), channel_id=1, source_target_pairs={{0,8},{2,10},{4,12},{6,14},{8,16},{10,18},{12,20},{14,22},{16,24},... | collective-permute-start | bytes 3145736 | tf_op jit(solution)/shard_map/ppermute | solution.py:358
  742.7 25.9 %collective-permute-done.21 = bf16[256,2048]{1,0:T(8,128)(2,1)S(1)} collective-permute-done((bf16[256,2048]{1,0:T(8,128)(2,1)S(1)}, bf16[256,2048]{1,0:T(8,128)(2,1)S(1)}, u32[]{:S(2)}, u32[]{:S(2)}) %collective-permute-start.21) | collective-permute-done | bytes 1048608 | tf_op jit(solution)/shard_map/ppermute | solution.py:358
  773.1 6.0 add_convert_fusion.2
  780.7 5.2 add_convert_fusion.13
  797.8 5.9 collective-permute-done.24
  807.6 6.8 convolution_convert_fusion.1
  815.2 10.5 fusion.11.go_ref
  829.6 32.3 %convolution_bitcast_fusion = f32[1,2048,1536]{2,1,0:T(8,128)} fusion(bf16[4096,2048]{1,0:T(8,128)(2,1)} %get-tuple-element.191, bf16[4096,1536]{1,0:T(8,128)(2,1)S(1)} %bitcast.143), kind=kOutput, calls=%fused_computation.5 | convolution fusion | flops 25769803776 | bytes 41943040 | tf_op jit(solution)/shard_map/dot_general | solution.py:321
  861.9 12.8 %collective-permute-done.26 = bf16[4,256,1024]{2,1,0:T(8,128)(2,1)} collective-permute-done((bf16[4,256,1024]{2,1,0:T(8,128)(2,1)}, bf16[4,256,1024]{2,1,0:T(8,128)(2,1)}, u32[]{:S(2)}, u32[]{:S(2)}) %collective-permute-start.26) | collective-permute-done | bytes 2097184 | tf_op jit(solution)/shard_map/ppermute | solution.py:337
  876.1 25.0 %attend_grad.1 = (bf16[512,2048]{1,0:T(8,128)(2,1)S(1)}, bf16[512,512]{1,0:T(8,128)(2,1)S(1)}, bf16[512,512]{1,0:T(8,128)(2,1)S(1)}, f32[4,1,128]{2,1,0:T(1,128)S(1)}, f32[4,1,128]{2,1,0:T(1,128)S(1)}) custom-call(f32[512,3072]{1,0:T(8,128)} %fusion.2.q_ref.k_ref.v_ref, f32[512,3072]{1,0:T(8,128)} %fusion.2.q_ref.k_ref.v_ref, bf16[512,2048]{1,0:T(8,128)(2,1)} %copy-done, ...), custom_call_target="tpu_custom_call" | custom-call | flops 5368709120 | bytes 15728640 | tf_op jit(solution)/shard_map/attend_grad/pallas_call | solution.py:554
  901.5 20.3 %convolution_bitcast_fusion.1 = f32[1,768,2048]{2,1,0:T(8,128)} fusion(bf16[4096,768]{1,0:T(8,128)(2,1)S(1)} %bitcast.149, bf16[4096,2048]{1,0:T(8,128)(2,1)} %get-tuple-element.201), kind=kOutput, calls=%fused_computation.26 | convolution fusion | flops 12884901888 | bytes 29360128 | tf_op jit(solution)/shard_map/dot_general | solution.py:321
  921.9 12.0 %collective-permute-done.28 = bf16[4,256,1024]{2,1,0:T(8,128)(2,1)} collective-permute-done((bf16[4,256,1024]{2,1,0:T(8,128)(2,1)}, bf16[4,256,1024]{2,1,0:T(8,128)(2,1)}, u32[]{:S(2)}, u32[]{:S(2)}) %collective-permute-start.28) | collective-permute-done | bytes 2097184 | tf_op jit(solution)/shard_map/ppermute | solution.py:337
  933.9 9.9 convolution_convert_fusion
  943.9 11.2 fusion
  969.3 15.9 %collective-permute-done.34 = bf16[256,2048]{1,0:T(8,128)(2,1)} collective-permute-done((bf16[256,2048]{1,0:T(8,128)(2,1)}, bf16[256,2048]{1,0:T(8,128)(2,1)}, u32[]{:S(2)}, u32[]{:S(2)}) %collective-permute-start.34) | collective-permute-done | bytes 1048608 | tf_op jit(solution)/shard_map/ppermute | solution.py:341
  985.2 4.7 fusion.21
  992.3 34.1 %collective-permute-done.43 = f32[18,128]{1,0:T(8,128)S(1)} collective-permute-done((f32[18,128]{1,0:T(8,128)S(1)}, f32[18,128]{1,0:T(8,128)S(1)}, u32[]{:S(2)}, u32[]{:S(2)}) %collective-permute-start.43) | collective-permute-done | bytes 9248 | tf_op jit(solution)/shard_map/ppermute | solution.py:341
  1030.2 4.8 collective-permute-done.45
  1038.1 4.5 fusion.32
  1050.7 49.9 %collective-permute-done.38 = f32[4,33,128]{2,0,1:T(4,128)S(1)} collective-permute-done((f32[4,33,128]{2,0,1:T(4,128)S(1)}, f32[4,33,128]{2,0,1:T(4,128)S(1)}, u32[]{:S(2)}, u32[]{:S(2)}) %collective-permute-start.38) | collective-permute-done | bytes 67616 | tf_op jit(solution)/shard_map/ppermute | solution.py:415
  1113.2 12.6 %collective-permute-done.31 = bf16[256,2048]{1,0:T(8,128)(2,1)} collective-permute-done((bf16[256,2048]{1,0:T(8,128)(2,1)}, bf16[256,2048]{1,0:T(8,128)(2,1)}, u32[]{:S(2)}, u32[]{:S(2)}) %collective-permute-start.31) | collective-permute-done | bytes 1048608 | tf_op jit(solution)/shard_map/ppermute | solution.py:372
  1125.8 29.2 %collective-permute-done.33 = bf16[256,2048]{1,0:T(8,128)(2,1)} collective-permute-done((bf16[256,2048]{1,0:T(8,128)(2,1)}, bf16[256,2048]{1,0:T(8,128)(2,1)}, u32[]{:S(2)}, u32[]{:S(2)}) %collective-permute-start.33) | collective-permute-done | bytes 1048608 | tf_op jit(solution)/shard_map/ppermute | solution.py:373
  1155.0 5.2 fusion.20
  (339 shorter events, 163.0 us)
Async XLA Ops:
  7.2 116.1 %all-gather.4.cloned.1.call-start = ((), (), s32[]{:S(2)}) async-start(), calls=%async_computation.4 | async-start | bytes 22282240 | tf_op jit(solution)/shard_map/all_gather | solution.py:845
  10.2 249.5 %all-gather.8.cloned.1.call-start = ((), (), s32[]{:S(2)}) async-start(), calls=%async_computation.6 | async-start | bytes 27852800 | tf_op jit(solution)/shard_map/all_gather | solution.py:852
  10.4 16.3 %collective-permute-start.3 = (bf16[256,1152]{1,0:T(8,128)(2,1)S(1)}, bf16[256,1152]{1,0:T(8,128)(2,1)S(1)}, u32[]{:S(2)}, u32[]{:S(2)}) collective-permute-start(bf16[256,1152]{1,0:T(8,128)(2,1)S(1)} %slice.401), channel_id=1, source_target_pairs={{0,1},{1,0},{2,3},{3,2},{4,5},{5,4},{6,7},{7,6},{8,9},{9,8},{10,11... | collective-permute-start | bytes 1769480 | tf_op jit(solution)/shard_map/ppermute | solution.py:341
  28.1 401.9 %all-gather.6.cloned.1.call-start = ((), (), s32[]{:S(2)}) async-start(), calls=%async_computation.5 | async-start | bytes 35651584 | tf_op jit(solution)/shard_map/all_gather | solution.py:873
  28.1 26.4 %collective-permute-start = (bf16[256,2048]{1,0:T(8,128)(2,1)S(1)}, bf16[256,2048]{1,0:T(8,128)(2,1)}, u32[]{:S(2)}, u32[]{:S(2)}) collective-permute-start(bf16[256,2048]{1,0:T(8,128)(2,1)S(1)} %copy-done.7), channel_id=1, source_target_pairs={{0,1},{1,0},{2,3},{3,2},{4,5},{5,4},{6,7},{7,6},{8,9},{9,8},{10,11... | collective-permute-start | bytes 3145736 | tf_op jit(solution)/shard_map/ppermute | solution.py:341
  162.0 25.4 %collective-permute-start.1 = (bf16[256,2048]{1,0:T(8,128)(2,1)S(1)}, bf16[256,2048]{1,0:T(8,128)(2,1)S(1)}, u32[]{:S(2)}, u32[]{:S(2)}) collective-permute-start(bf16[256,2048]{1,0:T(8,128)(2,1)S(1)} %select_convert_fusion.1), channel_id=1, source_target_pairs={{0,1},{1,0},{2,3},{3,2},{4,5},{5,4},{6,7},{7,6},{8,9},{9,8},{10,11... | collective-permute-start | bytes 3145736 | tf_op jit(solution)/shard_map/ppermute | solution.py:341
  190.3 24.6 %collective-permute-start.2 = (bf16[256,2048]{1,0:T(8,128)(2,1)S(1)}, bf16[256,2048]{1,0:T(8,128)(2,1)S(1)}, u32[]{:S(2)}, u32[]{:S(2)}) collective-permute-start(bf16[256,2048]{1,0:T(8,128)(2,1)S(1)} %multiply_convert_fusion), channel_id=1, source_target_pairs={{0,1},{1,0},{2,3},{3,2},{4,5},{5,4},{6,7},{7,6},{8,9},{9,8},{10,11... | collective-permute-start | bytes 3145736 | tf_op jit(solution)/shard_map/ppermute | solution.py:341
  266.6 160.5 %collective-permute-start.4 = (bf16[8,2,256,896]{3,2,1,0:T(8,128)(2,1)}, bf16[8,2,256,896]{3,2,1,0:T(8,128)(2,1)}, u32[]{:S(2)}, u32[]{:S(2)}) collective-permute-start(bf16[8,2,256,896]{3,2,1,0:T(8,128)(2,1)} %slice.403), channel_id=1, source_target_pairs={{0,1},{1,0},{2,3},{3,2},{4,5},{5,4},{6,7},{7,6},{8,9},{9,8},{10,11... | collective-permute-start | bytes 22020104 | tf_op jit(solution)/shard_map/ppermute | solution.py:341
  463.0 7.4 collective-permute-start.5
  475.3 48.1 %collective-permute-start.7 = (bf16[4,256,1024]{2,1,0:T(8,128)(2,1)}, bf16[4,256,1024]{2,1,0:T(8,128)(2,1)}, u32[]{:S(2)}, u32[]{:S(2)}) collective-permute-start(bf16[4,256,1024]{2,1,0:T(8,128)(2,1)} %get-tuple-element.133), channel_id=1, source_target_pairs={{0,1},{1,0},{2,3},{3,2},{4,5},{5,4},{6,7},{7,6},{8,9},{9,8},{10,11... | collective-permute-start | bytes 6291464 | tf_op jit(solution)/shard_map/ppermute | solution.py:341
  476.8 47.8 %collective-permute-start.8 = (bf16[4,256,1024]{2,1,0:T(8,128)(2,1)}, bf16[4,256,1024]{2,1,0:T(8,128)(2,1)}, u32[]{:S(2)}, u32[]{:S(2)}) collective-permute-start(bf16[4,256,1024]{2,1,0:T(8,128)(2,1)} %get-tuple-element.134), channel_id=1, source_target_pairs={{0,4},{2,6},{4,0},{6,2},{8,12},{10,14},{12,8},{14,10},{16,20},{18,... | collective-permute-start | bytes 6291464 | tf_op jit(solution)/shard_map/ppermute | solution.py:337
  524.6 35.5 %collective-permute-start.9 = (bf16[4,256,2048]{2,1,0:T(8,128)(2,1)}, bf16[4,256,2048]{2,1,0:T(8,128)(2,1)}, u32[]{:S(2)}, u32[]{:S(2)}) collective-permute-start(bf16[4,256,2048]{2,1,0:T(8,128)(2,1)} %get-tuple-element.135), channel_id=1, source_target_pairs={{0,2},{2,0},{4,6},{6,4},{8,10},{10,8},{12,14},{14,12},{16,18},{18,... | collective-permute-start | bytes 12582920 | tf_op jit(solution)/shard_map/ppermute | solution.py:333
  559.6 63.1 %collective-permute-start.6 = (bf16[4,256,2048]{2,1,0:T(8,128)(2,1)}, bf16[4,256,2048]{2,1,0:T(8,128)(2,1)}, u32[]{:S(2)}, u32[]{:S(2)}) collective-permute-start(bf16[4,256,2048]{2,1,0:T(8,128)(2,1)} %get-tuple-element.130), channel_id=1, source_target_pairs={{0,2},{2,0},{4,6},{6,4},{8,10},{10,8},{12,14},{14,12},{16,18},{18,... | collective-permute-start | bytes 12582920 | tf_op jit(solution)/shard_map/ppermute | solution.py:333
  566.3 40.4 %collective-permute-start.13 = (bf16[2,256,1024]{2,1,0:T(8,128)(2,1)S(1)}, bf16[2,256,1024]{2,1,0:T(8,128)(2,1)}, u32[]{:S(2)}, u32[]{:S(2)}) collective-permute-start(bf16[2,256,1024]{2,1,0:T(8,128)(2,1)S(1)} %add_convert_fusion.26), channel_id=1, source_target_pairs={{0,1},{1,0},{2,3},{3,2},{4,5},{5,4},{6,7},{7,6},{8,9},{9,8},{10,11... | collective-permute-start | bytes 3145736 | tf_op jit(solution)/shard_map/ppermute | solution.py:341
  569.5 37.2 %collective-permute-start.12 = (bf16[2,256,1024]{2,1,0:T(8,128)(2,1)}, bf16[2,256,1024]{2,1,0:T(8,128)(2,1)}, u32[]{:S(2)}, u32[]{:S(2)}) collective-permute-start(bf16[2,256,1024]{2,1,0:T(8,128)(2,1)} %add_convert_fusion.27), channel_id=1, source_target_pairs={{0,4},{2,6},{4,0},{6,2},{8,12},{10,14},{12,8},{14,10},{16,20},{18,... | collective-permute-start | bytes 3145736 | tf_op jit(solution)/shard_map/ppermute | solution.py:337
  570.7 43.4 %collective-permute-start.10 = (bf16[2,256,1024]{2,1,0:T(8,128)(2,1)S(1)}, bf16[2,256,1024]{2,1,0:T(8,128)(2,1)}, u32[]{:S(2)}, u32[]{:S(2)}) collective-permute-start(bf16[2,256,1024]{2,1,0:T(8,128)(2,1)S(1)} %get-tuple-element.145), channel_id=1, source_target_pairs={{0,1},{1,0},{2,3},{3,2},{4,5},{5,4},{6,7},{7,6},{8,9},{9,8},{10,11... | collective-permute-start | bytes 3145736 | tf_op jit(solution)/shard_map/ppermute | solution.py:341
  572.1 45.0 %collective-permute-start.11 = (bf16[2,256,1024]{2,1,0:T(8,128)(2,1)S(1)}, bf16[2,256,1024]{2,1,0:T(8,128)(2,1)}, u32[]{:S(2)}, u32[]{:S(2)}) collective-permute-start(bf16[2,256,1024]{2,1,0:T(8,128)(2,1)S(1)} %get-tuple-element.146), channel_id=1, source_target_pairs={{0,4},{2,6},{4,0},{6,2},{8,12},{10,14},{12,8},{14,10},{16,20},{18,... | collective-permute-start | bytes 3145736 | tf_op jit(solution)/shard_map/ppermute | solution.py:337
  617.1 22.4 %collective-permute-start.14 = (bf16[4,256,2048]{2,1,0:T(8,128)(2,1)}, bf16[4,256,2048]{2,1,0:T(8,128)(2,1)}, u32[]{:S(2)}, u32[]{:S(2)}) collective-permute-start(bf16[4,256,2048]{2,1,0:T(8,128)(2,1)} %get-tuple-element.151), channel_id=1, source_target_pairs={{0,2},{2,0},{4,6},{6,4},{8,10},{10,8},{12,14},{14,12},{16,18},{18,... | collective-permute-start | bytes 12582920 | tf_op jit(solution)/shard_map/ppermute | solution.py:333
  617.8 12.1 %all-to-all-start.1 = ((f32[32,1,256]{2,1,0:T(1,128)}), f32[32,1,256]{2,1,0:T(1,128)S(1)}, u32[]{:S(2)}, u32[]{:S(2)}) async-start(f32[32,1,256]{2,1,0:T(1,128)} %bitcast.162), calls=%async_computation.1 | async-start | bytes 65536 | tf_op jit(solution)/shard_map/all_to_all | solution.py:970
  622.6 488.6 %reduce-scatter.5.cloned.1.call-start = ((), (), s32[]{:S(2)}) async-start(), calls=%async_computation.8 | async-start | bytes 8912896 | tf_op jit(solution)/shard_map/reduce_scatter | solution.py:1043
  635.7 48.7 %collective-permute-start.20 = (bf16[256,2048]{1,0:T(8,128)(2,1)}, bf16[256,2048]{1,0:T(8,128)(2,1)S(1)}, u32[]{:S(2)}, u32[]{:S(2)}) collective-permute-start(bf16[256,2048]{1,0:T(8,128)(2,1)} %pad_maximum_fusion.12), channel_id=1, source_target_pairs={{0,16},{2,18},{4,20},{6,22},{8,24},{10,26},{12,28},{14,30},{16,0},... | collective-permute-start | bytes 3145736 | tf_op jit(solution)/shard_map/ppermute | solution.py:358
  638.0 76.2 %collective-permute-start.19 = (bf16[256,2048]{1,0:T(8,128)(2,1)}, bf16[256,2048]{1,0:T(8,128)(2,1)S(1)}, u32[]{:S(2)}, u32[]{:S(2)}) collective-permute-start(bf16[256,2048]{1,0:T(8,128)(2,1)} %pad_maximum_fusion.11), channel_id=1, source_target_pairs={{0,24},{2,26},{4,28},{6,30},{8,0},{10,2},{12,4},{14,6},{16,8},{18,... | collective-permute-start | bytes 3145736 | tf_op jit(solution)/shard_map/ppermute | solution.py:358
  646.6 67.5 %collective-permute-start.18 = (bf16[2,256,1024]{2,1,0:T(8,128)(2,1)}, bf16[2,256,1024]{2,1,0:T(8,128)(2,1)}, u32[]{:S(2)}, u32[]{:S(2)}) collective-permute-start(bf16[2,256,1024]{2,1,0:T(8,128)(2,1)} %add_convert_fusion.20), channel_id=1, source_target_pairs={{0,1},{1,0},{2,3},{3,2},{4,5},{5,4},{6,7},{7,6},{8,9},{9,8},{10,11... | collective-permute-start | bytes 3145736 | tf_op jit(solution)/shard_map/ppermute | solution.py:341
  650.7 63.5 %collective-permute-start.17 = (bf16[2,256,1024]{2,1,0:T(8,128)(2,1)}, bf16[2,256,1024]{2,1,0:T(8,128)(2,1)}, u32[]{:S(2)}, u32[]{:S(2)}) collective-permute-start(bf16[2,256,1024]{2,1,0:T(8,128)(2,1)} %add_convert_fusion.21), channel_id=1, source_target_pairs={{0,4},{2,6},{4,0},{6,2},{8,12},{10,14},{12,8},{14,10},{16,20},{18,... | collective-permute-start | bytes 3145736 | tf_op jit(solution)/shard_map/ppermute | solution.py:337
  652.1 62.0 %collective-permute-start.15 = (bf16[2,256,1024]{2,1,0:T(8,128)(2,1)}, bf16[2,256,1024]{2,1,0:T(8,128)(2,1)}, u32[]{:S(2)}, u32[]{:S(2)}) collective-permute-start(bf16[2,256,1024]{2,1,0:T(8,128)(2,1)} %get-tuple-element.152), channel_id=1, source_target_pairs={{0,1},{1,0},{2,3},{3,2},{4,5},{5,4},{6,7},{7,6},{8,9},{9,8},{10,11... | collective-permute-start | bytes 3145736 | tf_op jit(solution)/shard_map/ppermute | solution.py:341
  684.4 29.8 %collective-permute-start.16 = (bf16[2,256,1024]{2,1,0:T(8,128)(2,1)S(1)}, bf16[2,256,1024]{2,1,0:T(8,128)(2,1)}, u32[]{:S(2)}, u32[]{:S(2)}) collective-permute-start(bf16[2,256,1024]{2,1,0:T(8,128)(2,1)S(1)} %get-tuple-element.153), channel_id=1, source_target_pairs={{0,4},{2,6},{4,0},{6,2},{8,12},{10,14},{12,8},{14,10},{16,20},{18,... | collective-permute-start | bytes 3145736 | tf_op jit(solution)/shard_map/ppermute | solution.py:337
  715.2 64.0 %collective-permute-start.23 = (bf16[12,256,2048]{2,1,0:T(8,128)(2,1)}, bf16[12,256,2048]{2,1,0:T(8,128)(2,1)S(1)}, u32[]{:S(2)}, u32[]{:S(2)}) collective-permute-start(bf16[12,256,2048]{2,1,0:T(8,128)(2,1)} %get-tuple-element.176), channel_id=1, source_target_pairs={{0,2},{2,0},{4,6},{6,4},{8,10},{10,8},{12,14},{14,12},{16,18},{18,... | collective-permute-start | bytes 37748744 | tf_op jit(solution)/shard_map/ppermute | solution.py:333
  715.2 55.5 %collective-permute-start.22 = (bf16[4,256,2048]{2,1,0:T(8,128)(2,1)}, bf16[4,256,2048]{2,1,0:T(8,128)(2,1)}, u32[]{:S(2)}, u32[]{:S(2)}) collective-permute-start(bf16[4,256,2048]{2,1,0:T(8,128)(2,1)} %get-tuple-element.174), channel_id=1, source_target_pairs={{0,2},{2,0},{4,6},{6,4},{8,10},{10,8},{12,14},{14,12},{16,18},{18,... | collective-permute-start | bytes 12582920 | tf_op jit(solution)/shard_map/ppermute | solution.py:333
  720.6 48.0 %collective-permute-start.21 = (bf16[256,2048]{1,0:T(8,128)(2,1)S(1)}, bf16[256,2048]{1,0:T(8,128)(2,1)S(1)}, u32[]{:S(2)}, u32[]{:S(2)}) collective-permute-start(bf16[256,2048]{1,0:T(8,128)(2,1)S(1)} %pad_maximum_fusion.13), channel_id=1, source_target_pairs={{0,8},{2,10},{4,12},{6,14},{8,16},{10,18},{12,20},{14,22},{16,24},... | collective-permute-start | bytes 3145736 | tf_op jit(solution)/shard_map/ppermute | solution.py:358
  779.1 24.6 %collective-permute-start.24 = (bf16[256,2048]{1,0:T(8,128)(2,1)S(1)}, bf16[256,2048]{1,0:T(8,128)(2,1)}, u32[]{:S(2)}, u32[]{:S(2)}) collective-permute-start(bf16[256,2048]{1,0:T(8,128)(2,1)S(1)} %fusion.51), channel_id=1, source_target_pairs={{0,1},{1,0},{2,3},{3,2},{4,5},{5,4},{6,7},{7,6},{8,9},{9,8},{10,11... | collective-permute-start | bytes 3145736 | tf_op jit(solution)/shard_map/ppermute | solution.py:341
  814.5 298.1 %reduce-scatter.3.cloned.1.call-start = ((), (), s32[]{:S(2)}) async-start(), calls=%async_computation.7 | async-start | bytes 13369344 | tf_op jit(solution)/shard_map/reduce_scatter | solution.py:1050
  814.5 60.2 %collective-permute-start.26 = (bf16[4,256,1024]{2,1,0:T(8,128)(2,1)}, bf16[4,256,1024]{2,1,0:T(8,128)(2,1)}, u32[]{:S(2)}, u32[]{:S(2)}) collective-permute-start(bf16[4,256,1024]{2,1,0:T(8,128)(2,1)} %get-tuple-element.233), channel_id=1, source_target_pairs={{0,4},{2,6},{4,0},{6,2},{8,12},{10,14},{12,8},{14,10},{16,20},{18,... | collective-permute-start | bytes 6291464 | tf_op jit(solution)/shard_map/ppermute | solution.py:337
  825.7 49.1 %collective-permute-start.25 = (bf16[4,256,1024]{2,1,0:T(8,128)(2,1)}, bf16[4,256,1024]{2,1,0:T(8,128)(2,1)S(1)}, u32[]{:S(2)}, u32[]{:S(2)}) collective-permute-start(bf16[4,256,1024]{2,1,0:T(8,128)(2,1)} %get-tuple-element.190), channel_id=1, source_target_pairs={{0,1},{1,0},{2,3},{3,2},{4,5},{5,4},{6,7},{7,6},{8,9},{9,8},{10,11... | collective-permute-start | bytes 6291464 | tf_op jit(solution)/shard_map/ppermute | solution.py:341
  827.1 94.7 %collective-permute-start.27 = (bf16[4,256,1024]{2,1,0:T(8,128)(2,1)}, bf16[4,256,1024]{2,1,0:T(8,128)(2,1)}, u32[]{:S(2)}, u32[]{:S(2)}) collective-permute-start(bf16[4,256,1024]{2,1,0:T(8,128)(2,1)} %pad_maximum_fusion.6), channel_id=1, source_target_pairs={{0,1},{1,0},{2,3},{3,2},{4,5},{5,4},{6,7},{7,6},{8,9},{9,8},{10,11... | collective-permute-start | bytes 6291464 | tf_op jit(solution)/shard_map/ppermute | solution.py:341
  827.7 106.2 %collective-permute-start.28 = (bf16[4,256,1024]{2,1,0:T(8,128)(2,1)}, bf16[4,256,1024]{2,1,0:T(8,128)(2,1)}, u32[]{:S(2)}, u32[]{:S(2)}) collective-permute-start(bf16[4,256,1024]{2,1,0:T(8,128)(2,1)} %pad_maximum_fusion.5), channel_id=1, source_target_pairs={{0,4},{2,6},{4,0},{6,2},{8,12},{10,14},{12,8},{14,10},{16,20},{18,... | collective-permute-start | bytes 6291464 | tf_op jit(solution)/shard_map/ppermute | solution.py:337
  958.7 26.4 %collective-permute-start.34 = (bf16[256,2048]{1,0:T(8,128)(2,1)}, bf16[256,2048]{1,0:T(8,128)(2,1)}, u32[]{:S(2)}, u32[]{:S(2)}) collective-permute-start(bf16[256,2048]{1,0:T(8,128)(2,1)} %select_convert_fusion), channel_id=1, source_target_pairs={{0,1},{1,0},{2,3},{3,2},{4,5},{5,4},{6,7},{7,6},{8,9},{9,8},{10,11... | collective-permute-start | bytes 3145736 | tf_op jit(solution)/shard_map/ppermute | solution.py:341
  963.3 71.7 %collective-permute-start.29 = (bf16[4,256,1024]{2,1,0:T(8,128)(2,1)}, bf16[4,256,1024]{2,1,0:T(8,128)(2,1)}, u32[]{:S(2)}, u32[]{:S(2)}) collective-permute-start(bf16[4,256,1024]{2,1,0:T(8,128)(2,1)} %add_convert_fusion.1), channel_id=1, source_target_pairs={{0,4},{2,6},{4,0},{6,2},{8,12},{10,14},{12,8},{14,10},{16,20},{18,... | collective-permute-start | bytes 6291464 | tf_op jit(solution)/shard_map/ppermute | solution.py:337
  968.0 67.0 %collective-permute-start.30 = (bf16[4,256,1024]{2,1,0:T(8,128)(2,1)}, bf16[4,256,1024]{2,1,0:T(8,128)(2,1)}, u32[]{:S(2)}, u32[]{:S(2)}) collective-permute-start(bf16[4,256,1024]{2,1,0:T(8,128)(2,1)} %add_convert_fusion), channel_id=1, source_target_pairs={{0,1},{1,0},{2,3},{3,2},{4,5},{5,4},{6,7},{7,6},{8,9},{9,8},{10,11... | collective-permute-start | bytes 6291464 | tf_op jit(solution)/shard_map/ppermute | solution.py:341
  991.1 35.3 %collective-permute-start.43 = (f32[18,128]{1,0:T(8,128)S(1)}, f32[18,128]{1,0:T(8,128)S(1)}, u32[]{:S(2)}, u32[]{:S(2)}) collective-permute-start(f32[18,128]{1,0:T(8,128)S(1)} %fusion.48), channel_id=1, source_target_pairs={{0,1},{1,0},{2,3},{3,2},{4,5},{5,4},{6,7},{7,6},{8,9},{9,8},{10,11... | collective-permute-start | bytes 27656 | tf_op jit(solution)/shard_map/ppermute | solution.py:341
  1030.2 4.8 collective-permute-start.45
  1035.0 15.7 %collective-permute-start.46 = (f32[18,128]{1,0:T(8,128)S(1)}, f32[18,128]{1,0:T(8,128)S(1)}, u32[]{:S(2)}, u32[]{:S(2)}) collective-permute-start(f32[18,128]{1,0:T(8,128)S(1)} %add.674), channel_id=1, source_target_pairs={{0,16},{2,18},{4,20},{6,22},{8,24},{10,26},{12,28},{14,30},{16,0},... | collective-permute-start | bytes 27656 | tf_op jit(solution)/shard_map/ppermute | solution.py:403
  1035.1 13.4 %collective-permute-start.37 = (f32[8,33,128]{2,0,1:T(8,128)S(1)}, f32[8,33,128]{2,0,1:T(8,128)S(1)}, u32[]{:S(2)}, u32[]{:S(2)}) collective-permute-start(f32[8,33,128]{2,0,1:T(8,128)S(1)} %dynamic-slice_bitcast_fusion), channel_id=1, source_target_pairs={{0,16},{2,18},{4,20},{6,22},{8,24},{10,26},{12,28},{14,30},{16,0},... | collective-permute-start | bytes 405512 | tf_op jit(solution)/shard_map/ppermute | solution.py:415
  1048.5 56.2 %collective-permute-start.32 = (bf16[256,2048]{1,0:T(8,128)(2,1)S(1)}, bf16[256,2048]{1,0:T(8,128)(2,1)S(1)}, u32[]{:S(2)}, u32[]{:S(2)}) collective-permute-start(bf16[256,2048]{1,0:T(8,128)(2,1)S(1)} %get-tuple-element.270), channel_id=1, source_target_pairs={{0,8},{2,10},{4,12},{6,14},{8,0},{10,2},{12,4},{14,6},{16,24},{18,... | collective-permute-start | bytes 3145736 | tf_op jit(solution)/shard_map/ppermute | solution.py:372
  1048.6 51.9 %collective-permute-start.38 = (f32[4,33,128]{2,0,1:T(4,128)S(1)}, f32[4,33,128]{2,0,1:T(4,128)S(1)}, u32[]{:S(2)}, u32[]{:S(2)}) collective-permute-start(f32[4,33,128]{2,0,1:T(4,128)S(1)} %dynamic-slice_bitcast_fusion.1), channel_id=1, source_target_pairs={{0,8},{2,10},{4,12},{6,14},{8,0},{10,2},{12,4},{14,6},{16,24},{18,... | collective-permute-start | bytes 202760 | tf_op jit(solution)/shard_map/ppermute | solution.py:415
  1100.8 25.0 %collective-permute-start.31 = (bf16[256,2048]{1,0:T(8,128)(2,1)}, bf16[256,2048]{1,0:T(8,128)(2,1)}, u32[]{:S(2)}, u32[]{:S(2)}) collective-permute-start(bf16[256,2048]{1,0:T(8,128)(2,1)} %get-tuple-element.269), channel_id=1, source_target_pairs={{0,8},{2,10},{4,12},{6,14},{8,0},{10,2},{12,4},{14,6},{16,24},{18,... | collective-permute-start | bytes 3145736 | tf_op jit(solution)/shard_map/ppermute | solution.py:372
  1106.1 48.8 %collective-permute-start.33 = (bf16[256,2048]{1,0:T(8,128)(2,1)}, bf16[256,2048]{1,0:T(8,128)(2,1)}, u32[]{:S(2)}, u32[]{:S(2)}) collective-permute-start(bf16[256,2048]{1,0:T(8,128)(2,1)} %add_convert_fusion.11), channel_id=1, source_target_pairs={{0,16},{2,18},{4,20},{6,22},{8,24},{10,26},{12,28},{14,30},{16,0},... | collective-permute-start | bytes 3145736 | tf_op jit(solution)/shard_map/ppermute | solution.py:373
  1111.1 49.2 %collective-permute-start.36 = (bf16[128,2048]{1,0:T(8,128)(2,1)}, bf16[128,2048]{1,0:T(8,128)(2,1)}, u32[]{:S(2)}, u32[]{:S(2)}) collective-permute-start(bf16[128,2048]{1,0:T(8,128)(2,1)} %reduce-scatter.5.cloned.1.call-done), channel_id=1, source_target_pairs={{0,1},{1,0},{2,3},{3,2},{4,5},{5,4},{6,7},{7,6},{8,9},{9,8},{10,11... | collective-permute-start | bytes 1572872 | tf_op jit(solution)/shard_map/ppermute | solution.py:341
  1112.6 50.4 %collective-permute-start.35 = (bf16[128,3072]{1,0:T(8,128)(2,1)}, bf16[128,3072]{1,0:T(8,128)(2,1)}, u32[]{:S(2)}, u32[]{:S(2)}) collective-permute-start(bf16[128,3072]{1,0:T(8,128)(2,1)} %reduce-scatter.3.cloned.1.call-done.mine_ref), channel_id=1, source_target_pairs={{0,1},{1,0},{2,3},{3,2},{4,5},{5,4},{6,7},{7,6},{8,9},{9,8},{10,11... | collective-permute-start | bytes 2359304 | tf_op jit(solution)/shard_map/ppermute | solution.py:341
  (76 other events, 1899.1 us)
Sparse Core Ops, SparseCore 0:
  10.4 112.8 all-gather.3
  125.4 134.2 all-gather.7
  261.9 168.0 all-gather.5
  814.6 123.6 reduce-scatter.4
  944.0 156.9 reduce-scatter.2
